TPU v7x, 32 devices: a whole 2x2x4 slice. The times are simulated.
32 devices in a mesh: section: 2 (over x), dp: 4 (over y, core), tensor: 4 (over z).
Axes of the slice: x: 2, y: 2, z: 4, core: 2. Of those that a mesh axis runs over, the one named last changes fastest.
Arguments:
- inputs: bfloat16 [8, 1024, 1024], P('dp', 'tensor'), may hold values from -6 to 6
- out_cotangent: bfloat16 [8, 1024, 1024], P('dp', 'tensor'), may hold values from -6 to 6
- group_ids: int32 [8, 1024], P('dp', 'tensor'), may hold values from 0 to 7
- group_weights: float32 [8], replicated, may hold values from 0.25 to 4
- gains: float32 [2, 4, 1024], P('section'), may hold values from 0.1 to 1.9
- qkv_weight: bfloat16 [2, 1024, 3, 1024], P('section', None, None, 'tensor'), may hold values from -0.1875 to 0.1875
- out_weight: bfloat16 [2, 1024, 1024], P('section', 'tensor'), may hold values from -0.1875 to 0.1875
- up_weight: bfloat16 [2, 1024, 4096], P('section', None, 'tensor'), may hold values from -0.1875 to 0.1875
- down_weight: bfloat16 [2, 4096, 1024], P('section', 'tensor'), may hold values from -0.09375 to 0.09375
Outputs:
- layer_outputs: bfloat16 [2, 8, 1024, 1024], P('section', 'dp', 'tensor')
- input_grads: bfloat16 [2, 8, 1024, 1024], P('section', 'dp', 'tensor')
- gains_grad: float32 [2, 4, 1024], P('section', None, ('dp', 'tensor'))
- qkv_grad: float32 [2, 1024, 3, 1024], P('section', 'dp', None, 'tensor')
- out_grad: float32 [2, 1024, 1024], P('section', 'tensor', 'dp')
- up_grad: float32 [2, 1024, 4096], P('section', 'dp', 'tensor')
- down_grad: float32 [2, 4096, 1024], P('section', 'tensor', 'dp')
All inputs are finite; a program needn't handle non-finite values.
Results may differ from a plain program's by a relative error of at most 0.02.
Values may be sent and summed in bfloat16 or wider, within the bound.
No kernel may reach another device: no remote copies, remote signals or barrier semaphores. Data moves between devices by JAX's collectives and lax.ppermute only.
A program may use at most 192 MiB of HBM per device.

v0:
```python
import jax
import jax.numpy as jnp
from jax import lax
from jax.sharding import PartitionSpec as P

HEAD_DIM = 64


NORM_EPSILON = 1e-06


def shifted(block, axis, distance):
    devices = range(lax.axis_size(axis))
    route = [(i - distance, i) for i in devices if i - distance in devices]
    return lax.ppermute(block, axis, route)


def norm_rows(vector, weight_gain):
    return (
        vector
        * lax.rsqrt(jnp.mean(vector * vector, axis=-1, keepdims=True) + NORM_EPSILON)
        * weight_gain
    )


def rotary_tables(seq_len, head_width):
    half_width = head_width // 2
    freqs = 10000.0 ** (-2.0 * jnp.arange(half_width, dtype=jnp.float32) / head_width)
    angles = jnp.arange(seq_len, dtype=jnp.float32)[:, None] * freqs[None, :]
    return (jnp.cos(angles), jnp.sin(angles))


def rotate(vector, cos_table, sin_table):
    first_half, second_half = jnp.split(vector, 2, axis=-1)
    cos_part = cos_table[:, None, :]
    sin_part = sin_table[:, None, :]
    return jnp.concatenate(
        [
            first_half * cos_part - second_half * sin_part,
            second_half * cos_part + first_half * sin_part,
        ],
        axis=-1,
    )


def contract(left_rows, right_rows):
    return lax.dot_general(
        left_rows, right_rows, (((0,), (0,)), ((), ())), preferred_element_type=jnp.float32
    )


def gather_rows(row_values, weight):

    def project(shard_rows, offset):
        return (shard_rows, jnp.dot(shard_rows, weight, preferred_element_type=jnp.float32))

    return project(lax.all_gather(row_values, "tensor", axis=0, tiled=True), jnp.int32(0))


def scatter_rows(row_values, weight, row_count):

    def partial_term(offset, span):
        return jnp.dot(row_values, weight, preferred_element_type=jnp.float32)

    return lax.psum_scatter(
        partial_term(jnp.int32(0), lax.axis_size("tensor") * row_count),
        "tensor",
        scatter_dimension=0,
        tiled=True,
    )


def gather_grads(row_values, weight):

    def project(shard_rows, offset):
        return (shard_rows, jnp.dot(shard_rows, weight.T, preferred_element_type=jnp.float32))

    return project(lax.all_gather(row_values, "tensor", axis=0, tiled=True), jnp.int32(0))


def scatter_grads(row_values, weight, row_count):

    def partial_term(offset, span):
        return jnp.dot(row_values, weight.T, preferred_element_type=jnp.float32)

    return lax.psum_scatter(
        partial_term(jnp.int32(0), lax.axis_size("tensor") * row_count),
        "tensor",
        scatter_dimension=0,
        tiled=True,
    )


def attention_probs(queries, key_rows):
    scores = jnp.einsum(
        "qhd,khd->hqk", queries, key_rows, preferred_element_type=jnp.float32
    ) * HEAD_DIM ** (-0.5)
    length = queries.shape[0]
    positions = jnp.arange(length, dtype=jnp.int32)
    causal = positions[:, None] >= positions[None, :]
    scores = jnp.where(causal[None], scores, -1e30)
    expos = jnp.exp(scores - jnp.max(scores, axis=-1, keepdims=True))
    return expos / jnp.sum(expos, axis=-1, keepdims=True)


def layer_forward(layer_input, weights):
    gains, w_qkv, w_out, w_up, w_down = weights
    row_count, model_width = layer_input.shape
    attn_in = norm_rows(layer_input, gains[0]).astype(jnp.bfloat16)
    gathered_a, qkv = gather_rows(attn_in, w_qkv.reshape(model_width, -1))
    length = qkv.shape[0]
    head_count = w_qkv.shape[2] // HEAD_DIM
    qkv = qkv.reshape(length, 3, head_count, HEAD_DIM)
    cos_table, sin_table = rotary_tables(length, HEAD_DIM)
    queries = rotate(qkv[:, 0], cos_table, sin_table).astype(jnp.bfloat16)
    key_rows = rotate(qkv[:, 1], cos_table, sin_table).astype(jnp.bfloat16)
    values = qkv[:, 2].astype(jnp.bfloat16)
    attn_probs = attention_probs(queries, key_rows).astype(jnp.bfloat16)
    mixed = jnp.einsum("hqk,khd->qhd", attn_probs, values, preferred_element_type=jnp.float32)
    mixed = mixed.reshape(length, -1).astype(jnp.bfloat16)
    attn_branch = scatter_rows(mixed, w_out, row_count)
    hidden = layer_input + norm_rows(attn_branch, gains[1])
    mlp_in = norm_rows(hidden, gains[2]).astype(jnp.bfloat16)
    gathered_c, up_act = gather_rows(mlp_in, w_up)
    gelu_out = jax.nn.gelu(up_act, approximate=True).astype(jnp.bfloat16)
    down_branch = scatter_rows(gelu_out, w_down, row_count)
    result = hidden + norm_rows(down_branch, gains[3])
    kept_values = (
        gathered_a,
        queries,
        key_rows,
        values,
        mixed,
        attn_branch,
        hidden,
        gathered_c,
        up_act,
        gelu_out,
        down_branch,
    )
    return (result, kept_values)


def layer_backward(layer_input, grad_result, kept_values, weights):
    gains, w_qkv, w_out, w_up, w_down = weights
    (
        gathered_a,
        queries,
        key_rows,
        values,
        mixed,
        attn_branch,
        hidden,
        gathered_c,
        up_act,
        gelu_out,
        down_branch,
    ) = kept_values
    row_count, model_width = layer_input.shape
    pullback = jax.vjp(norm_rows, down_branch, gains[3])[1]
    grad_down, gain_three = pullback(grad_result)
    gathered_dd, grad_gelu = gather_grads(grad_down.astype(jnp.bfloat16), w_down)
    down_total = contract(gelu_out, gathered_dd)
    pullback = jax.vjp(lambda vector: jax.nn.gelu(vector, approximate=True), up_act)[1]
    grad_up = pullback(grad_gelu)[0].astype(jnp.bfloat16)
    up_total = contract(gathered_c, grad_up)
    grad_mlp = scatter_grads(grad_up, w_up, row_count)
    pullback = jax.vjp(norm_rows, hidden, gains[2])[1]
    grad_norm_mlp, gain_two = pullback(grad_mlp)
    grad_hidden = grad_result + grad_norm_mlp
    pullback = jax.vjp(norm_rows, attn_branch, gains[1])[1]
    grad_attn, gain_one = pullback(grad_hidden)
    gathered_da, grad_mixed = gather_grads(grad_attn.astype(jnp.bfloat16), w_out)
    out_total = contract(mixed, gathered_da)
    length = grad_mixed.shape[0]
    head_count = w_qkv.shape[2] // HEAD_DIM
    grad_mixed = grad_mixed.astype(jnp.bfloat16).reshape(length, head_count, HEAD_DIM)
    attn_probs = attention_probs(queries, key_rows)
    probs_low = attn_probs.astype(jnp.bfloat16)
    grad_probs = jnp.einsum("qhd,khd->hqk", grad_mixed, values, preferred_element_type=jnp.float32)
    grad_values = jnp.einsum(
        "hqk,qhd->khd", probs_low, grad_mixed, preferred_element_type=jnp.float32
    )
    row_dots = jnp.sum(grad_probs * attn_probs, axis=-1, keepdims=True)
    grad_scores = (attn_probs * (grad_probs - row_dots)).astype(jnp.bfloat16)
    scale_value = HEAD_DIM ** (-0.5)
    grad_queries = (
        jnp.einsum("hqk,khd->qhd", grad_scores, key_rows, preferred_element_type=jnp.float32)
        * scale_value
    )
    grad_keys = (
        jnp.einsum("hqk,qhd->khd", grad_scores, queries, preferred_element_type=jnp.float32)
        * scale_value
    )
    cos_table, sin_table = rotary_tables(length, HEAD_DIM)
    pullback = jax.vjp(lambda vector: rotate(vector, cos_table, sin_table), grad_queries)[1]
    grad_q_raw = pullback(grad_queries)[0]
    grad_k_raw = pullback(grad_keys)[0]
    grad_qkv = (
        jnp.stack([grad_q_raw, grad_k_raw, grad_values], axis=1)
        .reshape(length, -1)
        .astype(jnp.bfloat16)
    )
    qkv_total = contract(gathered_a, grad_qkv).reshape(model_width, 3, -1)
    grad_attn_in = scatter_grads(grad_qkv, w_qkv.reshape(model_width, -1), row_count)
    pullback = jax.vjp(norm_rows, layer_input, gains[0])[1]
    grad_norm_in, gain_zero = pullback(grad_attn_in)
    grad_input = grad_hidden + grad_norm_in
    gain_total = jnp.stack([gain_zero, gain_one, gain_two, gain_three])
    return (grad_input, (gain_total, qkv_total, out_total, up_total, down_total))


def lagged(first_section, stacked):
    blank = jnp.zeros_like(stacked[:1])
    earlier = jnp.concatenate([blank, stacked[:-1]])
    later = jnp.concatenate([stacked[1:], blank])
    return jnp.where(first_section, earlier, later)


def per_device(
    inputs,
    out_cotangent,
    group_ids,
    group_weights,
    gains,
    qkv_weight,
    out_weight,
    up_weight,
    down_weight,
):
    weights = (gains[0], qkv_weight[0], out_weight[0], up_weight[0], down_weight[0])
    micro_count, row_count, model_width = inputs.shape
    first_section = lax.axis_index("section") == 0
    group_count = group_weights.shape[0]
    matches = group_ids[..., None] == jnp.arange(group_count, dtype=jnp.int32)
    row_scale = jnp.sum(jnp.where(matches, group_weights, 0.0), axis=-1)
    scaled = out_cotangent.astype(jnp.float32) * row_scale[..., None]
    padded = jnp.concatenate([inputs, jnp.zeros((1, row_count, model_width), jnp.bfloat16)])

    def forward_tick(received, fresh_input):
        layer_input = jnp.where(first_section, fresh_input, received)
        result, kept_values = layer_forward(layer_input.astype(jnp.float32), weights)
        result_low = result.astype(jnp.bfloat16)
        outgoing = shifted(result_low, "section", 1)
        stashed = ()
        return (outgoing, (layer_input, result_low, stashed))

    start_rows = jnp.zeros((row_count, model_width), jnp.bfloat16)
    _, (layer_inputs, layer_results, stashed) = lax.scan(forward_tick, start_rows, padded)
    layer_outputs = jnp.where(first_section, layer_results[:-1], layer_results[1:])[None]
    back_inputs = lagged(first_section, layer_inputs)
    back_stash = jax.tree.map(lambda stacked: lagged(first_section, stacked), stashed)
    grad_padded = jnp.concatenate([scaled, jnp.zeros((1, row_count, model_width), jnp.float32)])
    tick_index = jnp.arange(micro_count + 1, dtype=jnp.int32)
    tick_valid = jnp.where(first_section, tick_index >= 1, tick_index < micro_count).astype(
        jnp.float32
    )

    def backward_tick(carry, step_item):
        received, totals = carry
        layer_input, cotangent, valid_now, stash_now = step_item
        grad_now = jnp.where(first_section, received.astype(jnp.float32), cotangent)
        input_now = layer_input.astype(jnp.float32)
        kept_values = layer_forward(input_now, weights)[1]
        grad_input, layer_grads = layer_backward(input_now, grad_now, kept_values, weights)
        totals = jax.tree.map(lambda total, update: total + valid_now * update, totals, layer_grads)
        grad_low = grad_input.astype(jnp.bfloat16)
        outgoing = shifted(grad_low, "section", -1)
        return ((outgoing, totals), grad_low)

    start_totals = (
        jnp.zeros((4, model_width), jnp.float32),
        jnp.zeros(qkv_weight.shape[1:], jnp.float32),
        jnp.zeros(out_weight.shape[1:], jnp.float32),
        jnp.zeros(up_weight.shape[1:], jnp.float32),
        jnp.zeros(down_weight.shape[1:], jnp.float32),
    )
    (_, totals), grad_lows = lax.scan(
        backward_tick,
        (start_rows, start_totals),
        (back_inputs, grad_padded, tick_valid, back_stash),
    )
    input_grads = jnp.where(first_section, grad_lows[1:], grad_lows[:-1])[None]
    gain_total, qkv_total, out_total, up_total, down_total = totals
    gains_grad = lax.psum_scatter(gain_total, ("dp", "tensor"), scatter_dimension=1, tiled=True)
    qkv_grad, out_grad, up_grad, down_grad = (
        lax.psum_scatter(
            qkv_total.astype(jnp.bfloat16), "dp", scatter_dimension=0, tiled=True
        ).astype(jnp.float32),
        lax.psum_scatter(
            out_total.astype(jnp.bfloat16), "dp", scatter_dimension=1, tiled=True
        ).astype(jnp.float32),
        lax.psum_scatter(
            up_total.astype(jnp.bfloat16), "dp", scatter_dimension=0, tiled=True
        ).astype(jnp.float32),
        lax.psum_scatter(
            down_total.astype(jnp.bfloat16), "dp", scatter_dimension=1, tiled=True
        ).astype(jnp.float32),
    )
    return (
        layer_outputs,
        input_grads,
        gains_grad[None],
        qkv_grad[None],
        out_grad[None],
        up_grad[None],
        down_grad[None],
    )


def solution(mesh):
    placed = (
        P("dp", "tensor", None),
        P("dp", "tensor", None),
        P("dp", "tensor"),
        P(),
        P("section", None, None),
        P("section", None, None, "tensor"),
        P("section", "tensor", None),
        P("section", None, "tensor"),
        P("section", "tensor", None),
    )
    return jax.shard_map(
        per_device,
        mesh=mesh,
        in_specs=placed,
        out_specs=(
            P("section", "dp", "tensor", None),
            P("section", "dp", "tensor", None),
            P("section", None, ("dp", "tensor")),
            P("section", "dp", None, "tensor"),
            P("section", "tensor", "dp"),
            P("section", "dp", "tensor"),
            P("section", "tensor", "dp"),
        ),
        check_vma=False,
    )
```

profile of v0, /device:TPU:0, one launch (start us, length us, event | category | flops | bytes accessed | tf_op | source)
XLA Modules:
  0.0 2997.9 jit_solution(8786126189976020737)
XLA Ops:
  16.6 925.6 %while.41 = (s32[]{:T(128)}, bf16[256,1024]{1,0:T(8,128)(2,1)S(1)}, bf16[3,256,1024]{2,1,0:T(8,128)(2,1)}, bf16[3,256,1024]{2,1,0:T(8,128)(2,1)}, pred[]{:T(512)...) while((s32[]{:T(128)}, bf16[256,1024]{1,0:T(8,128)(2,1)S(1)}, ...), condition=%wide.region_9.10_spmd, body=%wide.region_0.9_spmd.sunk | while | flops 7564986880 | bytes 155824272 | solution.py:249
  20.9 47.9 %all-gather.7.cloned.1.call-done = bf16[1024,1024]{1,0:T(8,128)(2,1)} async-done(((bf16[256,1024]{1,0:T(8,128)(2,1)}), bf16[1024,1024]{1,0:T(8,128)(2,1)}) %all-gather.7.cloned.1.call-update) | async-done | bytes 2097168 | tf_op jit(solution)/shard_map/while/body/eval_jaxpr/all_gather | solution.py:57
  74.3 9.9 fusion.238
  95.7 75.6 %reduce-scatter.24.cloned.1.call-done = f32[256,1024]{1,0:T(8,128)} async-done(((f32[1024,1024]{1,0:T(8,128)}), f32[256,1024]{1,0:T(8,128)}) %reduce-scatter.24.cloned.1.call-update) | async-done | bytes 1048592 | tf_op jit(solution)/shard_map/while/body/eval_jaxpr/reduce_scatter | solution.py:65
  176.6 46.5 %all-gather.9.cloned.1.call-done = bf16[1024,1024]{1,0:T(8,128)(2,1)} async-done(((bf16[256,1024]{1,0:T(8,128)(2,1)}), bf16[1024,1024]{1,0:T(8,128)(2,1)}) %all-gather.9.cloned.1.call-update) | async-done | bytes 2097168 | tf_op jit(solution)/shard_map/while/body/eval_jaxpr/all_gather | solution.py:57
  223.2 8.7 fusion.241
  231.9 75.6 %reduce-scatter.26.cloned.1.call-done = f32[256,1024]{1,0:T(8,128)} async-done(((f32[1024,1024]{1,0:T(8,128)}), f32[256,1024]{1,0:T(8,128)}) %reduce-scatter.26.cloned.1.call-update) | async-done | bytes 1048592 | tf_op jit(solution)/shard_map/while/body/eval_jaxpr/reduce_scatter | solution.py:65
  314.7 11.2 collective-permute-done
  330.2 46.7 %all-gather.7.cloned.1.call-done = bf16[1024,1024]{1,0:T(8,128)(2,1)} async-done(((bf16[256,1024]{1,0:T(8,128)(2,1)}), bf16[1024,1024]{1,0:T(8,128)(2,1)}) %all-gather.7.cloned.1.call-update) | async-done | bytes 2097168 | tf_op jit(solution)/shard_map/while/body/eval_jaxpr/all_gather | solution.py:57
  382.4 9.9 fusion.238
  403.8 75.6 %reduce-scatter.24.cloned.1.call-done = f32[256,1024]{1,0:T(8,128)} async-done(((f32[1024,1024]{1,0:T(8,128)}), f32[256,1024]{1,0:T(8,128)}) %reduce-scatter.24.cloned.1.call-update) | async-done | bytes 1048592 | tf_op jit(solution)/shard_map/while/body/eval_jaxpr/reduce_scatter | solution.py:65
  484.8 46.6 %all-gather.9.cloned.1.call-done = bf16[1024,1024]{1,0:T(8,128)(2,1)} async-done(((bf16[256,1024]{1,0:T(8,128)(2,1)}), bf16[1024,1024]{1,0:T(8,128)(2,1)}) %all-gather.9.cloned.1.call-update) | async-done | bytes 2097168 | tf_op jit(solution)/shard_map/while/body/eval_jaxpr/all_gather | solution.py:57
  531.3 8.7 fusion.241
  540.1 75.6 %reduce-scatter.26.cloned.1.call-done = f32[256,1024]{1,0:T(8,128)} async-done(((f32[1024,1024]{1,0:T(8,128)}), f32[256,1024]{1,0:T(8,128)}) %reduce-scatter.26.cloned.1.call-update) | async-done | bytes 1048592 | tf_op jit(solution)/shard_map/while/body/eval_jaxpr/reduce_scatter | solution.py:65
  622.9 11.2 collective-permute-done
  638.4 46.7 %all-gather.7.cloned.1.call-done = bf16[1024,1024]{1,0:T(8,128)(2,1)} async-done(((bf16[256,1024]{1,0:T(8,128)(2,1)}), bf16[1024,1024]{1,0:T(8,128)(2,1)}) %all-gather.7.cloned.1.call-update) | async-done | bytes 2097168 | tf_op jit(solution)/shard_map/while/body/eval_jaxpr/all_gather | solution.py:57
  690.6 9.9 fusion.238
  712.0 75.6 %reduce-scatter.24.cloned.1.call-done = f32[256,1024]{1,0:T(8,128)} async-done(((f32[1024,1024]{1,0:T(8,128)}), f32[256,1024]{1,0:T(8,128)}) %reduce-scatter.24.cloned.1.call-update) | async-done | bytes 1048592 | tf_op jit(solution)/shard_map/while/body/eval_jaxpr/reduce_scatter | solution.py:65
  793.0 46.5 %all-gather.9.cloned.1.call-done = bf16[1024,1024]{1,0:T(8,128)(2,1)} async-done(((bf16[256,1024]{1,0:T(8,128)(2,1)}), bf16[1024,1024]{1,0:T(8,128)(2,1)}) %all-gather.9.cloned.1.call-update) | async-done | bytes 2097168 | tf_op jit(solution)/shard_map/while/body/eval_jaxpr/all_gather | solution.py:57
  839.5 8.7 fusion.241
  848.3 75.6 %reduce-scatter.26.cloned.1.call-done = f32[256,1024]{1,0:T(8,128)} async-done(((f32[1024,1024]{1,0:T(8,128)}), f32[256,1024]{1,0:T(8,128)}) %reduce-scatter.26.cloned.1.call-update) | async-done | bytes 1048592 | tf_op jit(solution)/shard_map/while/body/eval_jaxpr/reduce_scatter | solution.py:65
  931.1 11.1 collective-permute-done
  948.0 1858.0 %while.42 = (s32[]{:T(128)}, bf16[256,1024]{1,0:T(8,128)(2,1)S(1)}, f32[4,1024]{1,0:T(4,128)S(1)}, f32[1024,3,256]{2,0,1:T(8,128)}, f32[256,1024]{1,0:T(8,128)},...) while((s32[]{:T(128)}, bf16[256,1024]{1,0:T(8,128)(2,1)S(1)}, ...), condition=%wide.region_31.32_spmd.clone, body=%wide.region_11.31_spmd.clone.sunk | while | flops 22695434240 | bytes 623419904 | solution.py:278
  950.6 48.2 %all-gather.11.cloned.1.call-done = bf16[1024,1024]{1,0:T(8,128)(2,1)} async-done(((bf16[256,1024]{1,0:T(8,128)(2,1)}), bf16[1024,1024]{1,0:T(8,128)(2,1)}) %all-gather.11.cloned.1.call-update) | async-done | bytes 2097168 | tf_op jit(solution)/shard_map/while/body/eval_jaxpr/all_gather | solution.py:57
  1004.7 11.0 fusion.277
  1028.0 75.6 %reduce-scatter.28.cloned.1.call-done = f32[256,1024]{1,0:T(8,128)} async-done(((f32[1024,1024]{1,0:T(8,128)}), f32[256,1024]{1,0:T(8,128)}) %reduce-scatter.28.cloned.1.call-update) | async-done | bytes 1048592 | tf_op jit(solution)/shard_map/while/body/eval_jaxpr/reduce_scatter | solution.py:65
  1107.6 11.8 reduce-scatter.30.cloned.1.call-start
  1119.4 34.8 %all-gather.13.cloned.1.call-done = bf16[1024,1024]{1,0:T(8,128)(2,1)} async-done(((bf16[256,1024]{1,0:T(8,128)(2,1)}), bf16[1024,1024]{1,0:T(8,128)(2,1)}) %all-gather.13.cloned.1.call-update) | async-done | bytes 2097168 | tf_op jit(solution)/shard_map/while/body/eval_jaxpr/all_gather | solution.py:57
  1165.5 75.6 %reduce-scatter.30.cloned.1.call-done = f32[256,1024]{1,0:T(8,128)} async-done(((f32[1024,1024]{1,0:T(8,128)}), f32[256,1024]{1,0:T(8,128)}) %reduce-scatter.30.cloned.1.call-update) | async-done | bytes 1048592 | tf_op jit(solution)/shard_map/while/body/eval_jaxpr/reduce_scatter | solution.py:65
  1246.9 46.5 %all-gather.15.cloned.1.call-done = bf16[1024,1024]{1,0:T(8,128)(2,1)} async-done(((bf16[256,1024]{1,0:T(8,128)(2,1)}), bf16[1024,1024]{1,0:T(8,128)(2,1)}) %all-gather.15.cloned.1.call-update) | async-done | bytes 2097168 | tf_op jit(solution)/shard_map/while/body/eval_jaxpr/all_gather | solution.py:78
  1307.1 75.6 %reduce-scatter.32.cloned.1.call-done = f32[256,1024]{1,0:T(8,128)} async-done(((f32[1024,1024]{1,0:T(8,128)}), f32[256,1024]{1,0:T(8,128)}) %reduce-scatter.32.cloned.1.call-update) | async-done | bytes 1048592 | tf_op jit(solution)/shard_map/while/body/eval_jaxpr/reduce_scatter | solution.py:86
  1387.6 46.6 %all-gather.17.cloned.1.call-done = bf16[1024,1024]{1,0:T(8,128)(2,1)} async-done(((bf16[256,1024]{1,0:T(8,128)(2,1)}), bf16[1024,1024]{1,0:T(8,128)(2,1)}) %all-gather.17.cloned.1.call-update) | async-done | bytes 2097168 | tf_op jit(solution)/shard_map/while/body/eval_jaxpr/all_gather | solution.py:78
  1436.8 8.6 fusion.289
  1492.0 55.8 %reduce-scatter.34.cloned.1.call-done = f32[256,1024]{1,0:T(8,128)} async-done(((f32[1024,1024]{1,0:T(8,128)}), f32[256,1024]{1,0:T(8,128)}) %reduce-scatter.34.cloned.1.call-update) | async-done | bytes 1048592 | tf_op jit(solution)/shard_map/while/body/eval_jaxpr/reduce_scatter | solution.py:86
  1555.9 12.0 collective-permute-done.1
  1570.5 46.2 %all-gather.11.cloned.1.call-done = bf16[1024,1024]{1,0:T(8,128)(2,1)} async-done(((bf16[256,1024]{1,0:T(8,128)(2,1)}), bf16[1024,1024]{1,0:T(8,128)(2,1)}) %all-gather.11.cloned.1.call-update) | async-done | bytes 2097168 | tf_op jit(solution)/shard_map/while/body/eval_jaxpr/all_gather | solution.py:57
  1622.6 11.0 fusion.277
  1646.0 75.6 %reduce-scatter.28.cloned.1.call-done = f32[256,1024]{1,0:T(8,128)} async-done(((f32[1024,1024]{1,0:T(8,128)}), f32[256,1024]{1,0:T(8,128)}) %reduce-scatter.28.cloned.1.call-update) | async-done | bytes 1048592 | tf_op jit(solution)/shard_map/while/body/eval_jaxpr/reduce_scatter | solution.py:65
  1726.0 46.1 %all-gather.13.cloned.1.call-done = bf16[1024,1024]{1,0:T(8,128)(2,1)} async-done(((bf16[256,1024]{1,0:T(8,128)(2,1)}), bf16[1024,1024]{1,0:T(8,128)(2,1)}) %all-gather.13.cloned.1.call-update) | async-done | bytes 2097168 | tf_op jit(solution)/shard_map/while/body/eval_jaxpr/all_gather | solution.py:57
  1783.5 75.6 %reduce-scatter.30.cloned.1.call-done = f32[256,1024]{1,0:T(8,128)} async-done(((f32[1024,1024]{1,0:T(8,128)}), f32[256,1024]{1,0:T(8,128)}) %reduce-scatter.30.cloned.1.call-update) | async-done | bytes 1048592 | tf_op jit(solution)/shard_map/while/body/eval_jaxpr/reduce_scatter | solution.py:65
  1864.8 46.5 %all-gather.15.cloned.1.call-done = bf16[1024,1024]{1,0:T(8,128)(2,1)} async-done(((bf16[256,1024]{1,0:T(8,128)(2,1)}), bf16[1024,1024]{1,0:T(8,128)(2,1)}) %all-gather.15.cloned.1.call-update) | async-done | bytes 2097168 | tf_op jit(solution)/shard_map/while/body/eval_jaxpr/all_gather | solution.py:78
  1925.0 75.6 %reduce-scatter.32.cloned.1.call-done = f32[256,1024]{1,0:T(8,128)} async-done(((f32[1024,1024]{1,0:T(8,128)}), f32[256,1024]{1,0:T(8,128)}) %reduce-scatter.32.cloned.1.call-update) | async-done | bytes 1048592 | tf_op jit(solution)/shard_map/while/body/eval_jaxpr/reduce_scatter | solution.py:86
  2005.5 46.6 %all-gather.17.cloned.1.call-done = bf16[1024,1024]{1,0:T(8,128)(2,1)} async-done(((bf16[256,1024]{1,0:T(8,128)(2,1)}), bf16[1024,1024]{1,0:T(8,128)(2,1)}) %all-gather.17.cloned.1.call-update) | async-done | bytes 2097168 | tf_op jit(solution)/shard_map/while/body/eval_jaxpr/all_gather | solution.py:78
  2090.6 9.4 select_add_fusion.7
  2113.3 52.4 %reduce-scatter.34.cloned.1.call-done = f32[256,1024]{1,0:T(8,128)} async-done(((f32[1024,1024]{1,0:T(8,128)}), f32[256,1024]{1,0:T(8,128)}) %reduce-scatter.34.cloned.1.call-update) | async-done | bytes 1048592 | tf_op jit(solution)/shard_map/while/body/eval_jaxpr/reduce_scatter | solution.py:86
  2173.8 12.0 collective-permute-done.1
  2188.5 46.3 %all-gather.11.cloned.1.call-done = bf16[1024,1024]{1,0:T(8,128)(2,1)} async-done(((bf16[256,1024]{1,0:T(8,128)(2,1)}), bf16[1024,1024]{1,0:T(8,128)(2,1)}) %all-gather.11.cloned.1.call-update) | async-done | bytes 2097168 | tf_op jit(solution)/shard_map/while/body/eval_jaxpr/all_gather | solution.py:57
  2240.6 11.0 fusion.277
  2264.0 75.6 %reduce-scatter.28.cloned.1.call-done = f32[256,1024]{1,0:T(8,128)} async-done(((f32[1024,1024]{1,0:T(8,128)}), f32[256,1024]{1,0:T(8,128)}) %reduce-scatter.28.cloned.1.call-update) | async-done | bytes 1048592 | tf_op jit(solution)/shard_map/while/body/eval_jaxpr/reduce_scatter | solution.py:65
  2343.6 11.7 reduce-scatter.30.cloned.1.call-start
  2355.3 34.9 %all-gather.13.cloned.1.call-done = bf16[1024,1024]{1,0:T(8,128)(2,1)} async-done(((bf16[256,1024]{1,0:T(8,128)(2,1)}), bf16[1024,1024]{1,0:T(8,128)(2,1)}) %all-gather.13.cloned.1.call-update) | async-done | bytes 2097168 | tf_op jit(solution)/shard_map/while/body/eval_jaxpr/all_gather | solution.py:57
  2401.5 75.6 %reduce-scatter.30.cloned.1.call-done = f32[256,1024]{1,0:T(8,128)} async-done(((f32[1024,1024]{1,0:T(8,128)}), f32[256,1024]{1,0:T(8,128)}) %reduce-scatter.30.cloned.1.call-update) | async-done | bytes 1048592 | tf_op jit(solution)/shard_map/while/body/eval_jaxpr/reduce_scatter | solution.py:65
  2482.9 46.5 %all-gather.15.cloned.1.call-done = bf16[1024,1024]{1,0:T(8,128)(2,1)} async-done(((bf16[256,1024]{1,0:T(8,128)(2,1)}), bf16[1024,1024]{1,0:T(8,128)(2,1)}) %all-gather.15.cloned.1.call-update) | async-done | bytes 2097168 | tf_op jit(solution)/shard_map/while/body/eval_jaxpr/all_gather | solution.py:78
  2543.1 75.6 %reduce-scatter.32.cloned.1.call-done = f32[256,1024]{1,0:T(8,128)} async-done(((f32[1024,1024]{1,0:T(8,128)}), f32[256,1024]{1,0:T(8,128)}) %reduce-scatter.32.cloned.1.call-update) | async-done | bytes 1048592 | tf_op jit(solution)/shard_map/while/body/eval_jaxpr/reduce_scatter | solution.py:86
  2623.6 46.6 %all-gather.17.cloned.1.call-done = bf16[1024,1024]{1,0:T(8,128)(2,1)} async-done(((bf16[256,1024]{1,0:T(8,128)(2,1)}), bf16[1024,1024]{1,0:T(8,128)(2,1)}) %all-gather.17.cloned.1.call-update) | async-done | bytes 2097168 | tf_op jit(solution)/shard_map/while/body/eval_jaxpr/all_gather | solution.py:78
  2672.8 8.6 fusion.289
  2708.7 9.4 select_add_fusion.7
  2731.5 52.2 %reduce-scatter.34.cloned.1.call-done = f32[256,1024]{1,0:T(8,128)} async-done(((f32[1024,1024]{1,0:T(8,128)}), f32[256,1024]{1,0:T(8,128)}) %reduce-scatter.34.cloned.1.call-update) | async-done | bytes 1048592 | tf_op jit(solution)/shard_map/while/body/eval_jaxpr/reduce_scatter | solution.py:86
  2791.8 12.0 collective-permute-done.1
  2822.1 43.9 %reduce-scatter.22.cloned.1.call-done = f32[64,4]{1,0:T(8,128)} async-done(((f32[1024,4]{1,0:T(8,128)}), f32[64,4]{1,0:T(8,128)}) %reduce-scatter.22.cloned.1.call-update) | async-done | bytes 1040
  2867.4 22.3 reduce-scatter.16.cloned.1.call-done
  2891.3 28.9 reduce-scatter.14.cloned.1.call-done
  2922.2 32.1 %reduce-scatter.20.cloned.1.call-done = bf16[1024,256]{1,0:T(8,128)(2,1)} async-done(((bf16[1024,1024]{1,0:T(8,128)(2,1)}), bf16[1024,256]{1,0:T(8,128)(2,1)}) %reduce-scatter.20.cloned.1.call-update) | async-done | bytes 524304 | tf_op jit(solution)/shard_map/reduce_scatter | solution.py:296
  2956.4 31.8 %reduce-scatter.18.cloned.1.call-done = bf16[256,1024]{1,0:T(8,128)(2,1)} async-done(((bf16[1024,1024]{1,0:T(8,128)(2,1)}), bf16[256,1024]{1,0:T(8,128)(2,1)}) %reduce-scatter.18.cloned.1.call-update) | async-done | bytes 524304 | tf_op jit(solution)/shard_map/reduce_scatter | solution.py:293
  (535 shorter events, 489.2 us)
Async XLA Ops:
  16.6 52.1 %all-gather.7.cloned.1.call-start = ((), (), s32[]{:S(2)}) async-start(), calls=%async_computation.16 | async-start | bytes 2621440 | tf_op jit(solution)/shard_map/while/body/eval_jaxpr/all_gather | solution.py:57
  19.9 151.3 %reduce-scatter.24.cloned.1.call-start = ((), (), s32[]{:S(2)}) async-start(), calls=%async_computation.17 | async-start | bytes 5242880 | tf_op jit(solution)/shard_map/while/body/eval_jaxpr/reduce_scatter | solution.py:65
  95.6 127.6 %copy-start.27 = (bf16[1024,1024]{1,0:T(8,128)(2,1)S(1)}, bf16[1024,1024]{1,0:T(8,128)(2,1)}, u32[]{:S(2)}) copy-start(bf16[1024,1024]{1,0:T(8,128)(2,1)} %get-tuple-element.934) | copy-start | bytes 6291460 | tf_op jit(solution)/shard_map/while
  95.6 127.6 %all-gather.9.cloned.1.call-start = ((), (), s32[]{:S(2)}) async-start(), calls=%async_computation.18 | async-start | bytes 2621440 | tf_op jit(solution)/shard_map/while/body/eval_jaxpr/all_gather | solution.py:57
  176.6 131.0 %reduce-scatter.26.cloned.1.call-start = ((), (), s32[]{:S(2)}) async-start(), calls=%async_computation.19 | async-start | bytes 5242880 | tf_op jit(solution)/shard_map/while/body/eval_jaxpr/reduce_scatter | solution.py:65
  231.9 77.0 %copy-start.1 = (f32[256,1024]{1,0:T(8,128)S(1)}, f32[256,1024]{1,0:T(8,128)}, u32[]{:S(2)}) copy-start(f32[256,1024]{1,0:T(8,128)} %reduce-scatter.24.cloned.1.call-done) | copy-start | bytes 3145732 | tf_op jit(solution)/shard_map/while
  311.3 14.6 collective-permute-start
  325.9 51.0 %all-gather.7.cloned.1.call-start = ((), (), s32[]{:S(2)}) async-start(), calls=%async_computation.16 | async-start | bytes 2621440 | tf_op jit(solution)/shard_map/while/body/eval_jaxpr/all_gather | solution.py:57
  329.2 150.2 %reduce-scatter.24.cloned.1.call-start = ((), (), s32[]{:S(2)}) async-start(), calls=%async_computation.17 | async-start | bytes 5242880 | tf_op jit(solution)/shard_map/while/body/eval_jaxpr/reduce_scatter | solution.py:65
  403.7 127.6 %copy-start.27 = (bf16[1024,1024]{1,0:T(8,128)(2,1)S(1)}, bf16[1024,1024]{1,0:T(8,128)(2,1)}, u32[]{:S(2)}) copy-start(bf16[1024,1024]{1,0:T(8,128)(2,1)} %get-tuple-element.934) | copy-start | bytes 6291460 | tf_op jit(solution)/shard_map/while
  403.8 127.6 %all-gather.9.cloned.1.call-start = ((), (), s32[]{:S(2)}) async-start(), calls=%async_computation.18 | async-start | bytes 2621440 | tf_op jit(solution)/shard_map/while/body/eval_jaxpr/all_gather | solution.py:57
  484.7 131.0 %reduce-scatter.26.cloned.1.call-start = ((), (), s32[]{:S(2)}) async-start(), calls=%async_computation.19 | async-start | bytes 5242880 | tf_op jit(solution)/shard_map/while/body/eval_jaxpr/reduce_scatter | solution.py:65
  540.1 77.0 %copy-start.1 = (f32[256,1024]{1,0:T(8,128)S(1)}, f32[256,1024]{1,0:T(8,128)}, u32[]{:S(2)}) copy-start(f32[256,1024]{1,0:T(8,128)} %reduce-scatter.24.cloned.1.call-done) | copy-start | bytes 3145732 | tf_op jit(solution)/shard_map/while
  619.5 14.6 collective-permute-start
  634.1 51.0 %all-gather.7.cloned.1.call-start = ((), (), s32[]{:S(2)}) async-start(), calls=%async_computation.16 | async-start | bytes 2621440 | tf_op jit(solution)/shard_map/while/body/eval_jaxpr/all_gather | solution.py:57
  637.4 150.2 %reduce-scatter.24.cloned.1.call-start = ((), (), s32[]{:S(2)}) async-start(), calls=%async_computation.17 | async-start | bytes 5242880 | tf_op jit(solution)/shard_map/while/body/eval_jaxpr/reduce_scatter | solution.py:65
  711.9 127.6 %copy-start.27 = (bf16[1024,1024]{1,0:T(8,128)(2,1)S(1)}, bf16[1024,1024]{1,0:T(8,128)(2,1)}, u32[]{:S(2)}) copy-start(bf16[1024,1024]{1,0:T(8,128)(2,1)} %get-tuple-element.934) | copy-start | bytes 6291460 | tf_op jit(solution)/shard_map/while
  712.0 127.6 %all-gather.9.cloned.1.call-start = ((), (), s32[]{:S(2)}) async-start(), calls=%async_computation.18 | async-start | bytes 2621440 | tf_op jit(solution)/shard_map/while/body/eval_jaxpr/all_gather | solution.py:57
  792.9 131.0 %reduce-scatter.26.cloned.1.call-start = ((), (), s32[]{:S(2)}) async-start(), calls=%async_computation.19 | async-start | bytes 5242880 | tf_op jit(solution)/shard_map/while/body/eval_jaxpr/reduce_scatter | solution.py:65
  848.3 77.0 %copy-start.1 = (f32[256,1024]{1,0:T(8,128)S(1)}, f32[256,1024]{1,0:T(8,128)}, u32[]{:S(2)}) copy-start(f32[256,1024]{1,0:T(8,128)} %reduce-scatter.24.cloned.1.call-done) | copy-start | bytes 3145732 | tf_op jit(solution)/shard_map/while
  927.7 14.6 collective-permute-start
  948.2 156.8 %copy-start.3 = (bf16[3,256,1024]{2,1,0:T(8,128)(2,1)}, bf16[3,256,1024]{2,1,0:T(8,128)(2,1)S(1)}, u32[]{:S(2)}) copy-start(bf16[3,256,1024]{2,1,0:T(8,128)(2,1)S(1)} %get-tuple-element.986) | copy-start | bytes 4718596 | tf_op jit(solution)/shard_map/while
  948.2 296.3 %copy-start.5 = (bf16[256,1024]{1,0:T(8,128)(2,1)}, bf16[256,1024]{1,0:T(8,128)(2,1)S(1)}, u32[]{:S(2)}) copy-start(bf16[256,1024]{1,0:T(8,128)(2,1)S(1)} %get-tuple-element.957) | copy-start | bytes 1572868 | tf_op jit(solution)/shard_map/while
  948.2 50.6 %all-gather.11.cloned.1.call-start = ((), (), s32[]{:S(2)}) async-start(), calls=%async_computation.20 | async-start | bytes 2621440 | tf_op jit(solution)/shard_map/while/body/eval_jaxpr/all_gather | solution.py:57
  949.7 153.9 %reduce-scatter.28.cloned.1.call-start = ((), (), s32[]{:S(2)}) async-start(), calls=%async_computation.21 | async-start | bytes 5242880 | tf_op jit(solution)/shard_map/while/body/eval_jaxpr/reduce_scatter | solution.py:65
  1028.0 126.2 %all-gather.13.cloned.1.call-start = ((), (), s32[]{:S(2)}) async-start(), calls=%async_computation.22 | async-start | bytes 2621440 | tf_op jit(solution)/shard_map/while/body/eval_jaxpr/all_gather | solution.py:57
  1107.6 133.5 %reduce-scatter.30.cloned.1.call-start = ((), (), s32[]{:S(2)}) async-start(), calls=%async_computation.23 | async-start | bytes 5242880 | tf_op jit(solution)/shard_map/while/body/eval_jaxpr/reduce_scatter | solution.py:65
  1165.5 128.0 %all-gather.15.cloned.1.call-start = ((), (), s32[]{:S(2)}) async-start(), calls=%async_computation.24 | async-start | bytes 2621440 | tf_op jit(solution)/shard_map/while/body/eval_jaxpr/all_gather | solution.py:78
  1246.9 135.8 %reduce-scatter.32.cloned.1.call-start = ((), (), s32[]{:S(2)}) async-start(), calls=%async_computation.25 | async-start | bytes 5242880 | tf_op jit(solution)/shard_map/while/body/eval_jaxpr/reduce_scatter | solution.py:86
  1307.0 77.1 %copy-start = (f32[256,1024]{1,0:T(8,128)S(1)}, f32[256,1024]{1,0:T(8,128)}, u32[]{:S(2)}) copy-start(f32[256,1024]{1,0:T(8,128)} %reduce-scatter.28.cloned.1.call-done) | copy-start | bytes 3145732 | tf_op jit(solution)/shard_map/while
  1307.1 127.1 %all-gather.17.cloned.1.call-start = ((), (), s32[]{:S(2)}) async-start(), calls=%async_computation.26 | async-start | bytes 2621440 | tf_op jit(solution)/shard_map/while/body/eval_jaxpr/all_gather | solution.py:78
  1387.6 160.2 %reduce-scatter.34.cloned.1.call-start = ((), (), s32[]{:S(2)}) async-start(), calls=%async_computation.27 | async-start | bytes 5242880 | tf_op jit(solution)/shard_map/while/body/eval_jaxpr/reduce_scatter | solution.py:86
  1492.0 61.6 %copy-start.7 = (bf16[4,64,1024]{2,1,0:T(8,128)(2,1)S(1)}, bf16[4,64,1024]{2,1,0:T(8,128)(2,1)}, u32[]{:S(2)}) copy-start(bf16[4,64,1024]{2,1,0:T(8,128)(2,1)} %copy-done.6) | copy-start | bytes 1572868 | tf_op jit(solution)/shard_map/while
  1552.2 15.7 collective-permute-start.1
  1568.1 154.9 %copy-start.3 = (bf16[3,256,1024]{2,1,0:T(8,128)(2,1)}, bf16[3,256,1024]{2,1,0:T(8,128)(2,1)S(1)}, u32[]{:S(2)}) copy-start(bf16[3,256,1024]{2,1,0:T(8,128)(2,1)S(1)} %get-tuple-element.986) | copy-start | bytes 4718596 | tf_op jit(solution)/shard_map/while
  1568.1 294.3 %copy-start.5 = (bf16[256,1024]{1,0:T(8,128)(2,1)}, bf16[256,1024]{1,0:T(8,128)(2,1)S(1)}, u32[]{:S(2)}) copy-start(bf16[256,1024]{1,0:T(8,128)(2,1)S(1)} %get-tuple-element.957) | copy-start | bytes 1572868 | tf_op jit(solution)/shard_map/while
  1568.1 48.7 %all-gather.11.cloned.1.call-start = ((), (), s32[]{:S(2)}) async-start(), calls=%async_computation.20 | async-start | bytes 2621440 | tf_op jit(solution)/shard_map/while/body/eval_jaxpr/all_gather | solution.py:57
  1569.6 152.0 %reduce-scatter.28.cloned.1.call-start = ((), (), s32[]{:S(2)}) async-start(), calls=%async_computation.21 | async-start | bytes 5242880 | tf_op jit(solution)/shard_map/while/body/eval_jaxpr/reduce_scatter | solution.py:65
  1645.9 126.2 %all-gather.13.cloned.1.call-start = ((), (), s32[]{:S(2)}) async-start(), calls=%async_computation.22 | async-start | bytes 2621440 | tf_op jit(solution)/shard_map/while/body/eval_jaxpr/all_gather | solution.py:57
  1725.5 133.5 %reduce-scatter.30.cloned.1.call-start = ((), (), s32[]{:S(2)}) async-start(), calls=%async_computation.23 | async-start | bytes 5242880 | tf_op jit(solution)/shard_map/while/body/eval_jaxpr/reduce_scatter | solution.py:65
  1783.4 128.0 %all-gather.15.cloned.1.call-start = ((), (), s32[]{:S(2)}) async-start(), calls=%async_computation.24 | async-start | bytes 2621440 | tf_op jit(solution)/shard_map/while/body/eval_jaxpr/all_gather | solution.py:78
  1864.8 135.8 %reduce-scatter.32.cloned.1.call-start = ((), (), s32[]{:S(2)}) async-start(), calls=%async_computation.25 | async-start | bytes 5242880 | tf_op jit(solution)/shard_map/while/body/eval_jaxpr/reduce_scatter | solution.py:86
  1925.0 77.1 %copy-start = (f32[256,1024]{1,0:T(8,128)S(1)}, f32[256,1024]{1,0:T(8,128)}, u32[]{:S(2)}) copy-start(f32[256,1024]{1,0:T(8,128)} %reduce-scatter.28.cloned.1.call-done) | copy-start | bytes 3145732 | tf_op jit(solution)/shard_map/while
  1925.0 127.1 %all-gather.17.cloned.1.call-start = ((), (), s32[]{:S(2)}) async-start(), calls=%async_computation.26 | async-start | bytes 2621440 | tf_op jit(solution)/shard_map/while/body/eval_jaxpr/all_gather | solution.py:78
  2005.5 160.2 %reduce-scatter.34.cloned.1.call-start = ((), (), s32[]{:S(2)}) async-start(), calls=%async_computation.27 | async-start | bytes 5242880 | tf_op jit(solution)/shard_map/while/body/eval_jaxpr/reduce_scatter | solution.py:86
  2113.3 58.2 %copy-start.7 = (bf16[4,64,1024]{2,1,0:T(8,128)(2,1)S(1)}, bf16[4,64,1024]{2,1,0:T(8,128)(2,1)}, u32[]{:S(2)}) copy-start(bf16[4,64,1024]{2,1,0:T(8,128)(2,1)} %copy-done.6) | copy-start | bytes 1572868 | tf_op jit(solution)/shard_map/while
  2170.1 15.7 collective-permute-start.1
  2186.1 154.9 %copy-start.3 = (bf16[3,256,1024]{2,1,0:T(8,128)(2,1)}, bf16[3,256,1024]{2,1,0:T(8,128)(2,1)S(1)}, u32[]{:S(2)}) copy-start(bf16[3,256,1024]{2,1,0:T(8,128)(2,1)S(1)} %get-tuple-element.986) | copy-start | bytes 4718596 | tf_op jit(solution)/shard_map/while
  2186.1 294.3 %copy-start.5 = (bf16[256,1024]{1,0:T(8,128)(2,1)}, bf16[256,1024]{1,0:T(8,128)(2,1)S(1)}, u32[]{:S(2)}) copy-start(bf16[256,1024]{1,0:T(8,128)(2,1)S(1)} %get-tuple-element.957) | copy-start | bytes 1572868 | tf_op jit(solution)/shard_map/while
  2186.1 48.7 %all-gather.11.cloned.1.call-start = ((), (), s32[]{:S(2)}) async-start(), calls=%async_computation.20 | async-start | bytes 2621440 | tf_op jit(solution)/shard_map/while/body/eval_jaxpr/all_gather | solution.py:57
  2187.6 152.0 %reduce-scatter.28.cloned.1.call-start = ((), (), s32[]{:S(2)}) async-start(), calls=%async_computation.21 | async-start | bytes 5242880 | tf_op jit(solution)/shard_map/while/body/eval_jaxpr/reduce_scatter | solution.py:65
  2263.9 126.2 %all-gather.13.cloned.1.call-start = ((), (), s32[]{:S(2)}) async-start(), calls=%async_computation.22 | async-start | bytes 2621440 | tf_op jit(solution)/shard_map/while/body/eval_jaxpr/all_gather | solution.py:57
  2343.6 133.5 %reduce-scatter.30.cloned.1.call-start = ((), (), s32[]{:S(2)}) async-start(), calls=%async_computation.23 | async-start | bytes 5242880 | tf_op jit(solution)/shard_map/while/body/eval_jaxpr/reduce_scatter | solution.py:65
  2401.5 128.0 %all-gather.15.cloned.1.call-start = ((), (), s32[]{:S(2)}) async-start(), calls=%async_computation.24 | async-start | bytes 2621440 | tf_op jit(solution)/shard_map/while/body/eval_jaxpr/all_gather | solution.py:78
  2482.8 135.8 %reduce-scatter.32.cloned.1.call-start = ((), (), s32[]{:S(2)}) async-start(), calls=%async_computation.25 | async-start | bytes 5242880 | tf_op jit(solution)/shard_map/while/body/eval_jaxpr/reduce_scatter | solution.py:86
  2543.0 77.1 %copy-start = (f32[256,1024]{1,0:T(8,128)S(1)}, f32[256,1024]{1,0:T(8,128)}, u32[]{:S(2)}) copy-start(f32[256,1024]{1,0:T(8,128)} %reduce-scatter.28.cloned.1.call-done) | copy-start | bytes 3145732 | tf_op jit(solution)/shard_map/while
  2543.0 127.1 %all-gather.17.cloned.1.call-start = ((), (), s32[]{:S(2)}) async-start(), calls=%async_computation.26 | async-start | bytes 2621440 | tf_op jit(solution)/shard_map/while/body/eval_jaxpr/all_gather | solution.py:78
  2623.5 160.2 %reduce-scatter.34.cloned.1.call-start = ((), (), s32[]{:S(2)}) async-start(), calls=%async_computation.27 | async-start | bytes 5242880 | tf_op jit(solution)/shard_map/while/body/eval_jaxpr/reduce_scatter | solution.py:86
  2788.1 15.7 collective-permute-start.1
  2806.0 60.0 %reduce-scatter.22.cloned.1.call-start = ((), (), s32[]{:S(2)}) async-start(), calls=%async_computation.15 | async-start | bytes 557056
  2807.1 82.6 %reduce-scatter.16.cloned.1.call-start = ((), (), s32[]{:S(2)}) async-start(), calls=%async_computation.12 | async-start | bytes 655360 | tf_op jit(solution)/shard_map/reduce_scatter | solution.py:290
  2809.2 111.0 %reduce-scatter.14.cloned.1.call-start = ((), (), s32[]{:S(2)}) async-start(), calls=%async_computation.11 | async-start | bytes 1966080 | tf_op jit(solution)/shard_map/reduce_scatter | solution.py:287
  2812.6 141.7 %reduce-scatter.20.cloned.1.call-start = ((), (), s32[]{:S(2)}) async-start(), calls=%async_computation.14 | async-start | bytes 2621440 | tf_op jit(solution)/shard_map/reduce_scatter | solution.py:296
  2816.5 171.7 %reduce-scatter.18.cloned.1.call-start = ((), (), s32[]{:S(2)}) async-start(), calls=%async_computation.13 | async-start | bytes 2621440 | tf_op jit(solution)/shard_map/reduce_scatter | solution.py:293
  (87 other events, 717.3 us)
Sparse Core Ops, SparseCore 0:
  20.0 48.6 all-gather.6
  95.7 75.4 reduce-scatter.23
  176.7 46.4 all-gather.8
  232.1 75.4 reduce-scatter.25
  329.4 47.4 all-gather.6
  403.9 75.4 reduce-scatter.23
  484.9 46.4 all-gather.8
  540.2 75.4 reduce-scatter.25
  637.6 47.4 all-gather.6
  712.1 75.4 reduce-scatter.23
  793.1 46.4 all-gather.8
  848.4 75.4 reduce-scatter.25
  951.3 47.4 all-gather.10
  1028.1 75.4 reduce-scatter.27
  1107.7 46.4 all-gather.12
  1165.6 75.4 reduce-scatter.29
  1247.0 46.4 all-gather.14
  1307.2 75.4 reduce-scatter.31
  1387.7 46.4 all-gather.16
  1472.3 75.4 reduce-scatter.33
  1571.2 45.5 all-gather.10
  1646.0 75.4 reduce-scatter.27
  1725.7 46.4 all-gather.12
  1783.5 75.4 reduce-scatter.29
  1864.9 46.4 all-gather.14
  1925.1 75.4 reduce-scatter.31
  2005.6 46.4 all-gather.16
  2090.2 75.4 reduce-scatter.33
  2189.2 45.5 all-gather.10
  2264.1 75.4 reduce-scatter.27
  2343.7 46.4 all-gather.12
  2401.6 75.4 reduce-scatter.29
  2482.9 46.4 all-gather.14
  2543.1 75.4 reduce-scatter.31
  2623.6 46.4 all-gather.16
  2708.2 75.4 reduce-scatter.33
Sparse Core Ops, SparseCore 1:
  2810.6 55.4 reduce-scatter.21
  2869.1 20.5 reduce-scatter.15
  2892.1 28.1 reduce-scatter.13
  2923.0 31.3 reduce-scatter.19
  2956.8 31.3 reduce-scatter.17
where the time goes:
time: 3010 us; the launch traced here: 3000 us
  waiting for transfers between devices  2340 us (78%)
  matrix products  391 us (13%)
  other arithmetic  161 us (5%)
  local copies, waits for them, and re-layouts  45.5 us (2%)
  starting transfers between devices  39.9 us (1%)
    reduce_scatter x12, waiting for transfers between devices, scatter_rows(): lax.psum_scatter(partial_term(jnp.int32(0), lax.axis_size('tensor') * row...  907 us
    all_gather x12, waiting for transfers between devices, gather_rows(): lax.all_gather(row_values, 'tensor', axis=0, tiled=True)  537 us
    reduce_scatter x6, waiting for transfers between devices, scatter_grads(): lax.psum_scatter(partial_term(jnp.int32(0), lax.axis_size('tensor') * row...  387 us
    all_gather x6, waiting for transfers between devices, gather_grads(): lax.all_gather(row_values, 'tensor', axis=0, tiled=True)  279 us
    ppermute x6, waiting for transfers between devices, shifted(): return lax.ppermute(block, axis, route)  69.5 us
    dot_general x12, matrix products, contract(): lax.dot_general(left_rows, right_rows, (((0,), (0,)), ((), ())), preferre...  63.2 us
    sub x6, matrix products, attention_probs(): expos = jnp.exp(scores - jnp.max(scores, axis=-1, keepdims=True))  62.8 us
    dot_general x12, matrix products, partial_term(): return jnp.dot(row_values, weight, preferred_element_type=jnp.float32)  62.4 us
  transfers between devices with their start and end apart: 47, of which 47 were waited for; matrix products, arithmetic and copies ran while one was open for 3% of the time, Pallas kernels for 0%

commit v1 on v0

--- a/solution.py
+++ b/solution.py
@@ -1,12 +1,18 @@
+import math
+
 import jax
 import jax.numpy as jnp
 from jax import lax
+from jax.experimental import pallas as pl
+from jax.experimental.pallas import tpu as pltpu
 from jax.sharding import PartitionSpec as P
 
 HEAD_DIM = 64
 
 
 NORM_EPSILON = 1e-06
+TILE = 128
+KERNEL_VMEM = 32 << 20
 
 
 def shifted(block, axis, distance):
@@ -308,6 +314,451 @@
     )
 
 
+def rotated(block, cos_rows, sin_rows):
+    lane = lax.broadcasted_iota(jnp.int32, block.shape, 1)
+    ahead = pltpu.roll(block, 96, 1)
+    behind = pltpu.roll(block, 32, 1)
+    swapped = jnp.where(lane % 64 < 32, ahead, behind)
+    return block * cos_rows + swapped * sin_rows
+
+
+def dot_nt(left, right):
+    return lax.dot_general(
+        left, right, (((1,), (1,)), ((), ())), preferred_element_type=jnp.float32
+    )
+
+
+def dot_nn(left, right):
+    return jnp.dot(left, right, preferred_element_type=jnp.float32)
+
+
+def edge_masks(core, rows):
+    key = lax.broadcasted_iota(jnp.int32, (rows, 2 * rows), 0)
+    query = lax.broadcasted_iota(jnp.int32, (rows, 2 * rows), 1)
+    mine = query < rows
+    place = jnp.where(mine, query + core * rows, query - rows + (1 - core) * rows)
+    return (key + core * rows <= place, key + (1 - core) * rows <= place)
+
+
+def both_sides(value, half, start, stop, axis=0):
+    if axis == 0:
+        return jnp.concatenate([value[start:stop], value[half + start : half + stop]], axis=0)
+    return jnp.concatenate([value[:, start:stop], value[:, half + start : half + stop]], axis=1)
+
+
+def hidden_scores(scores, masks, tile, step):
+    seen = step * tile
+    pieces = []
+    for side in range(2):
+        base = side * (seen + tile)
+        if seen:
+            pieces.append(scores[base : base + seen])
+        pieces.append(jnp.where(masks[side], scores[base + seen : base + seen + tile], -1e30))
+    return jnp.concatenate(pieces, axis=0)
+
+
+def attend_kernel(core_ref, cos_ref, sin_ref, rows_ref, w_ref, q_ref, k_ref, v_ref, lse_ref, mix_ref):
+    length = rows_ref.shape[0]
+    half = length // 2
+    tile = TILE
+    proj = dot_nn(rows_ref[...], w_ref[...])
+    cos_rows, sin_rows = cos_ref[...], sin_ref[...]
+    q = (rotated(proj[:, :128], cos_rows, sin_rows) * HEAD_DIM ** (-0.5)).astype(jnp.bfloat16)
+    k = rotated(proj[:, 128:256], cos_rows, sin_rows).astype(jnp.bfloat16)
+    v32 = proj[:, 256:]
+    v = v32.astype(jnp.bfloat16)
+    q_ref[0] = q
+    k_ref[0] = k
+    v_ref[0] = v
+    v_flip = v32.T.astype(jnp.bfloat16)
+    masks = edge_masks(core_ref[0], tile)
+    lane = lax.broadcasted_iota(jnp.int32, (2 * tile, 128), 1)
+    for step in range(half // tile):
+        stop = (step + 1) * tile
+        q_rows = both_sides(q, half, step * tile, stop)
+        k_rows = both_sides(k, half, 0, stop)
+        v_cols = both_sides(v_flip, half, 0, stop, axis=1)
+        outs = []
+        for head in range(2):
+            q_head = jnp.where(lane // 64 == head, q_rows, jnp.zeros_like(q_rows))
+            scores = hidden_scores(dot_nt(k_rows, q_head), masks, tile, step)
+            top = jnp.max(scores, axis=0, keepdims=True)
+            expos = jnp.exp(scores - top)
+            total = jnp.sum(expos, axis=0, keepdims=True)
+            lse = top + jnp.log(total)
+            lse_ref[0, head : head + 1, step * tile : stop] = lse[:, :tile]
+            lse_ref[0, head : head + 1, half + step * tile : half + stop] = lse[:, tile:]
+            out = dot_nn(v_cols[64 * head : 64 * head + 64], expos.astype(jnp.bfloat16))
+            outs.append(out * (1.0 / total))
+        mixed = jnp.concatenate(outs, axis=0).T.astype(jnp.bfloat16)
+        mix_ref[step * tile : stop, :] = mixed[:tile]
+        mix_ref[half + step * tile : half + stop, :] = mixed[tile:]
+
+
+def attend_back_kernel(
+    core_ref, cos_ref, sin_ref, grad_ref, w_ref, q_ref, k_ref, v_ref, lse_ref, out_ref, dq, dk, dv
+):
+    length = grad_ref.shape[0]
+    half = length // 2
+    tile = TILE
+    d_mixed = dot_nt(grad_ref[...], w_ref[...]).astype(jnp.bfloat16)
+    q, k, v = q_ref[0], k_ref[0], v_ref[0]
+    k_flip = k.astype(jnp.float32).T.astype(jnp.bfloat16)
+    masks = edge_masks(core_ref[0], tile)
+    lane = lax.broadcasted_iota(jnp.int32, (2 * tile, 128), 1)
+    steps = half // tile
+    for step in reversed(range(steps)):
+        stop = (step + 1) * tile
+        q_rows = both_sides(q, half, step * tile, stop)
+        g_rows = both_sides(d_mixed, half, step * tile, stop)
+        k_rows = both_sides(k, half, 0, stop)
+        v_rows = both_sides(v, half, 0, stop)
+        k_cols = both_sides(k_flip, half, 0, stop, axis=1)
+        lse = both_sides(lse_ref[0], half, step * tile, stop, axis=1)
+        dq_flips = []
+        dk_sum = dv_sum = None
+        for head in range(2):
+            q_head = jnp.where(lane // 64 == head, q_rows, jnp.zeros_like(q_rows))
+            g_head = jnp.where(lane // 64 == head, g_rows, jnp.zeros_like(g_rows))
+            scores = hidden_scores(dot_nt(k_rows, q_head), masks, tile, step)
+            probs = jnp.exp(scores - lse[head : head + 1])
+            d_probs = dot_nt(v_rows, g_head)
+            dots = jnp.sum(probs * d_probs, axis=0, keepdims=True)
+            d_scores = (probs * (d_probs - dots)).astype(jnp.bfloat16)
+            dv_part = dot_nn(probs.astype(jnp.bfloat16), g_head)
+            dk_part = dot_nn(d_scores, q_head)
+            dv_sum = dv_part if dv_sum is None else dv_sum + dv_part
+            dk_sum = dk_part if dk_sum is None else dk_sum + dk_part
+            dq_flips.append(dot_nn(k_cols[64 * head : 64 * head + 64], d_scores))
+        dq_rows = jnp.concatenate(dq_flips, axis=0).T * HEAD_DIM ** (-0.5)
+        dq[step * tile : stop] = dq_rows[:tile]
+        dq[half + step * tile : half + stop] = dq_rows[tile:]
+        for base, part in ((0, slice(0, stop)), (half, slice(stop, 2 * stop))):
+            if step == steps - 1:
+                dk[base : base + stop] = dk_sum[part]
+                dv[base : base + stop] = dv_sum[part]
+            else:
+                dk[base : base + stop] += dk_sum[part]
+                dv[base : base + stop] += dv_sum[part]
+    cos_rows, sin_rows = cos_ref[...], -sin_ref[...]
+    out_ref[:, :128] = rotated(dq[...], cos_rows, sin_rows).astype(jnp.bfloat16)
+    out_ref[:, 128:256] = rotated(dk[...], cos_rows, sin_rows).astype(jnp.bfloat16)
+    out_ref[:, 256:] = dv[...].astype(jnp.bfloat16)
+
+
+def whole_block(array):
+    return pl.BlockSpec(array.shape, lambda j: (0,) * array.ndim)
+
+
+def attend(core, tables, rows, w_qkv):
+    length, width = rows.shape
+    pairs = w_qkv.shape[1] // 384
+    per_pair = pl.BlockSpec((1, length, 128), lambda j: (j, 0, 0))
+    return pl.pallas_call(
+        attend_kernel,
+        grid=(pairs,),
+        in_specs=[
+            pl.BlockSpec(memory_space=pltpu.SMEM),
+            whole_block(tables[0]),
+            whole_block(tables[1]),
+            whole_block(rows),
+            pl.BlockSpec((width, 384), lambda j: (0, j)),
+        ],
+        out_specs=[
+            per_pair,
+            per_pair,
+            per_pair,
+            pl.BlockSpec((1, 2, length), lambda j: (j, 0, 0)),
+            pl.BlockSpec((length, 128), lambda j: (0, j)),
+        ],
+        out_shape=[
+            jax.ShapeDtypeStruct((pairs, length, 128), jnp.bfloat16),
+            jax.ShapeDtypeStruct((pairs, length, 128), jnp.bfloat16),
+            jax.ShapeDtypeStruct((pairs, length, 128), jnp.bfloat16),
+            jax.ShapeDtypeStruct((pairs, 2, length), jnp.float32),
+            jax.ShapeDtypeStruct((length, pairs * 128), jnp.bfloat16),
+        ],
+        compiler_params=pltpu.CompilerParams(vmem_limit_bytes=KERNEL_VMEM),
+        name="attend",
+    )(core, *tables, rows, w_qkv)
+
+
+def attend_back(core, tables, grads, w_out, q, k, v, lse):
+    length, width = grads.shape
+    pairs = q.shape[0]
+    per_pair = pl.BlockSpec((1, length, 128), lambda j: (j, 0, 0))
+    return pl.pallas_call(
+        attend_back_kernel,
+        grid=(pairs,),
+        in_specs=[
+            pl.BlockSpec(memory_space=pltpu.SMEM),
+            whole_block(tables[0]),
+            whole_block(tables[1]),
+            whole_block(grads),
+            pl.BlockSpec((128, width), lambda j: (j, 0)),
+            per_pair,
+            per_pair,
+            per_pair,
+            pl.BlockSpec((1, 2, length), lambda j: (j, 0, 0)),
+        ],
+        out_specs=pl.BlockSpec((length, 384), lambda j: (0, j)),
+        out_shape=jax.ShapeDtypeStruct((length, pairs * 384), jnp.bfloat16),
+        scratch_shapes=[pltpu.VMEM((length, 128), jnp.float32)] * 3,
+        compiler_params=pltpu.CompilerParams(vmem_limit_bytes=KERNEL_VMEM),
+        name="attend_back",
+    )(core, *tables, grads, w_out, q, k, v, lse)
+
+
+def flip_pairs(block, distance):
+    size = lax.axis_size("dp")
+    return lax.ppermute(block, "dp", [(i, i ^ distance) for i in range(size)])
+
+
+def passed_on(block, step):
+    size = lax.axis_size("tensor")
+    return lax.ppermute(block, "tensor", [(i, (i + step) % size) for i in range(size)])
+
+
+def spread(piece):
+    pieces = [piece]
+    for _ in range(lax.axis_size("tensor") - 1):
+        pieces.append(passed_on(pieces[-1], 1))
+    return pieces
+
+
+def collected(pieces):
+    total = pieces[-1]
+    for piece in reversed(pieces[:-1]):
+        total = piece + passed_on(total.astype(jnp.bfloat16), -1).astype(jnp.float32)
+    return total
+
+
+def norm_back(vector, gain, grad):
+    scale = lax.rsqrt(jnp.mean(vector * vector, axis=-1, keepdims=True) + NORM_EPSILON)
+    weighted = grad * gain
+    inner = jnp.mean(vector * weighted, axis=-1, keepdims=True)
+    d_vector = scale * weighted - vector * (scale * scale * scale * inner)
+    return d_vector, jnp.sum(vector * scale * grad, axis=0)
+
+
+def gelu_both(up_act):
+    root = math.sqrt(2.0 / math.pi)
+    square = up_act * up_act
+    bent = jnp.tanh(root * up_act * (1.0 + 0.044715 * square))
+    value = 0.5 * up_act * (1.0 + bent)
+    slope = 0.5 * (1.0 + bent) + 0.5 * up_act * (1.0 - bent * bent) * root * (
+        1.0 + 3 * 0.044715 * square
+    )
+    return value, slope
+
+
+def per_chip(
+    inputs,
+    out_cotangent,
+    group_ids,
+    group_weights,
+    gains,
+    qkv_weight,
+    out_weight,
+    up_weight,
+    down_weight,
+):
+    micro, row_count, width = inputs.shape
+    tensor = lax.axis_size("tensor")
+    part = row_count // 2
+    wide = width // 2
+    length = tensor * row_count
+    half = length // 2
+    first = lax.axis_index("section") == 0
+    place = lax.axis_index("dp")
+    core = place % 2
+    upper = place // 2 % 2
+    core_zero = core == 0
+    low_half = upper == 0
+
+    def ordered(mine, other):
+        return jnp.where(core_zero, mine, other), jnp.where(core_zero, other, mine)
+
+    def own_first(values):
+        return jnp.where(low_half, values, jnp.roll(values, wide, axis=-1))
+
+    def full_rows(own):
+        return jnp.concatenate([own, flip_pairs(own, 1)], axis=0)
+
+    def summed_rows(partial):
+        return partial[:half] + flip_pairs(partial[half:].astype(jnp.bfloat16), 1).astype(
+            jnp.float32
+        )
+
+    def to_chip(block):
+        split = block.reshape((micro, 2, part) + block.shape[2:])
+        mine = lax.dynamic_index_in_dim(split, core, 1, keepdims=False)
+        other = lax.dynamic_index_in_dim(split, 1 - core, 1, keepdims=False)
+        return lax.all_to_all(
+            jnp.concatenate(ordered(mine, flip_pairs(other, 1))), "tensor", 0, 0, tiled=True
+        )
+
+    def from_chip(block):
+        spread_out = lax.all_to_all(block, "tensor", 0, 0, tiled=True)
+        grouped = spread_out.reshape((2, micro, part) + block.shape[2:])
+        mine = lax.dynamic_index_in_dim(grouped, core, 0, keepdims=False)
+        other = lax.dynamic_index_in_dim(grouped, 1 - core, 0, keepdims=False)
+        pair = ordered(mine, flip_pairs(other, 1))
+        return jnp.stack(pair, axis=1).reshape((micro, row_count) + block.shape[2:])
+
+    start = to_chip(own_first(jnp.where(first, inputs, out_cotangent))).reshape(half, width)
+    start = start.astype(jnp.float32)
+    group_count = group_weights.shape[0]
+    matches = group_ids[..., None] == jnp.arange(group_count, dtype=jnp.int32)
+    row_scale = jnp.sum(jnp.where(matches, group_weights, 0.0), axis=-1)
+    row_scale = to_chip(row_scale).reshape(half, 1)
+
+    def columns(local):
+        piece = lax.dynamic_slice(
+            local, (wide * upper, local.shape[1] // 2 * core), (wide, local.shape[1] // 2)
+        )
+        pieces = spread(piece)
+        others = [flip_pairs(p, 2) for p in pieces]
+        return jnp.concatenate(
+            [jnp.concatenate(pieces, axis=1), jnp.concatenate(others, axis=1)], axis=0
+        )
+
+    def rows(local):
+        piece = lax.dynamic_slice(
+            local, (local.shape[0] // 2 * core, wide * upper), (local.shape[0] // 2, wide)
+        )
+        pieces = spread(piece)
+        others = [flip_pairs(p, 2) for p in pieces]
+        return jnp.concatenate(
+            [jnp.concatenate(pieces, axis=0), jnp.concatenate(others, axis=0)], axis=1
+        )
+
+    head_cols = qkv_weight.shape[3]
+    local_qkv = jnp.concatenate(
+        [
+            qkv_weight[0, :, i, h * head_cols // 2 : (h + 1) * head_cols // 2]
+            for h in range(2)
+            for i in range(3)
+        ],
+        axis=1,
+    )
+    w_qkv = columns(local_qkv)
+    w_out = rows(out_weight[0])
+    w_up = columns(up_weight[0])
+    w_down = rows(down_weight[0])
+    gain = own_first(gains[0])
+
+    turns = jnp.arange(half, dtype=jnp.int32)
+    turns = turns // part * row_count + turns % part
+    positions = jnp.concatenate([turns + core * part, turns + (1 - core) * part])
+    freqs = 10000.0 ** (-2.0 * jnp.arange(HEAD_DIM // 2, dtype=jnp.float32) / HEAD_DIM)
+    angles = positions.astype(jnp.float32)[:, None] * freqs[None, :]
+    cos_part, sin_part = jnp.cos(angles), jnp.sin(angles)
+    tables = (
+        jnp.concatenate([cos_part] * 4, axis=1),
+        jnp.concatenate([-sin_part, sin_part] * 2, axis=1),
+    )
+    core_word = core.astype(jnp.int32).reshape(1)
+
+    def forward(layer_input):
+        attn_in = full_rows(norm_rows(layer_input, gain[0]).astype(jnp.bfloat16))
+        q, k, v, lse, mixed = attend(core_word, tables, attn_in, w_qkv)
+        attn_branch = summed_rows(dot_nn(mixed, w_out))
+        hidden = layer_input + norm_rows(attn_branch, gain[1])
+        mlp_in = full_rows(norm_rows(hidden, gain[2]).astype(jnp.bfloat16))
+        gelu_out, slope = (t.astype(jnp.bfloat16) for t in gelu_both(dot_nn(mlp_in, w_up)))
+        down_branch = summed_rows(dot_nn(gelu_out, w_down))
+        result = hidden + norm_rows(down_branch, gain[3])
+        chain = (layer_input, q, k, v, lse, attn_branch, hidden, slope, down_branch)
+        return result.astype(jnp.bfloat16), chain, (attn_in, mixed, mlp_in, gelu_out)
+
+    def backward(grad, chain):
+        layer_input, q, k, v, lse, attn_branch, hidden, slope, down_branch = chain
+        d_down, gain_three = norm_back(down_branch, gain[3], grad)
+        d_down = full_rows(d_down.astype(jnp.bfloat16))
+        d_up = (dot_nt(d_down, w_down) * slope.astype(jnp.float32)).astype(jnp.bfloat16)
+        d_mlp = summed_rows(dot_nt(d_up, w_up))
+        d_norm, gain_two = norm_back(hidden, gain[2], d_mlp)
+        d_hidden = grad + d_norm
+        d_attn, gain_one = norm_back(attn_branch, gain[1], d_hidden)
+        d_attn = full_rows(d_attn.astype(jnp.bfloat16))
+        d_qkv = attend_back(core_word, tables, d_attn, w_out, q, k, v, lse)
+        d_in = summed_rows(dot_nt(d_qkv, w_qkv))
+        d_norm, gain_zero = norm_back(layer_input, gain[0], d_in)
+        d_input = (d_hidden + d_norm).astype(jnp.bfloat16)
+        gain_rows = jnp.stack([gain_zero, gain_one, gain_two, gain_three])
+        return d_input, (d_qkv, d_attn, d_up, d_down), gain_rows
+
+    low_zero, chain_zero, lefts_zero = forward(start)
+    low_one, chain_one, lefts_one = forward(shifted(low_zero, "section", 1).astype(jnp.float32))
+    outputs = from_chip(own_first(jnp.where(first, low_zero, low_one)).reshape(tensor, part, width))
+    grad_one, rights_one, gain_one = backward(start * row_scale, chain_one)
+    grad_zero, rights_zero, gain_zero = backward(
+        shifted(grad_one, "section", -1).astype(jnp.float32), chain_zero
+    )
+    grads = from_chip(own_first(jnp.where(first, grad_zero, grad_one)).reshape(tensor, part, width))
+
+    attn_in, mixed, mlp_in, gelu_out = (
+        jnp.where(first, zero, one) for zero, one in zip(lefts_zero, lefts_one)
+    )
+    d_qkv, d_attn, d_up, d_down = (
+        jnp.where(first, zero, one) for zero, one in zip(rights_zero, rights_one)
+    )
+
+    def sum_columns(left, right, count):
+        total = contract(left, right)
+        size = total.shape[1] // tensor
+        pieces = [
+            total[:wide, j * size : (j + 1) * size]
+            + flip_pairs(
+                total[wide:, j * size : (j + 1) * size].astype(jnp.bfloat16), 2
+            ).astype(jnp.float32)
+            for j in range(tensor)
+        ]
+        kept = collected(pieces).reshape(2, wide // 2, size)
+        mine = lax.dynamic_index_in_dim(kept, core, 0, keepdims=False)
+        other = lax.dynamic_index_in_dim(kept, 1 - core, 0, keepdims=False)
+        pair = ordered(mine, flip_pairs(other, 1))
+        pair = [side.reshape(wide // 2, count, size // count) for side in pair]
+        return jnp.concatenate(pair, axis=2)
+
+    def sum_rows(left, right):
+        total = contract(left, right)
+        size = total.shape[0] // tensor
+        pieces = [
+            total[j * size : (j + 1) * size, :wide]
+            + flip_pairs(
+                total[j * size : (j + 1) * size, wide:].astype(jnp.bfloat16), 2
+            ).astype(jnp.float32)
+            for j in range(tensor)
+        ]
+        kept = collected(pieces)
+        sides = (kept[:, : wide // 2], kept[:, wide // 2 :])
+        mine = jnp.where(core_zero, sides[0], sides[1])
+        other = jnp.where(core_zero, sides[1], sides[0])
+        return jnp.concatenate(ordered(mine, flip_pairs(other, 1)), axis=0)
+
+    down_grad = sum_rows(gelu_out, d_down)
+    up_grad = sum_columns(mlp_in, d_up, 1)[:, 0]
+    out_grad = sum_rows(mixed, d_attn)
+    qkv_grad = sum_columns(attn_in, d_qkv, 3)
+    gain_total = own_first(jnp.where(first, gain_zero, gain_one))
+    gains_grad = lax.psum_scatter(gain_total, ("dp", "tensor"), scatter_dimension=1, tiled=True)
+    return (
+        outputs[None],
+        grads[None],
+        gains_grad[None],
+        qkv_grad[None],
+        out_grad[None],
+        up_grad[None],
+        down_grad[None],
+    )
+
+
+def takes_chips(sizes):
+    return sizes["section"] == 2 and sizes["dp"] == 4 and sizes["tensor"] == 4
+
+
 def solution(mesh):
     placed = (
         P("dp", "tensor", None),
@@ -320,8 +771,9 @@
         P("section", None, "tensor"),
         P("section", "tensor", None),
     )
+    body = per_chip if takes_chips(dict(mesh.shape)) else per_device
     return jax.shard_map(
-        per_device,
+        body,
         mesh=mesh,
         in_specs=placed,
         out_specs=(

time: 3010 us -> 824 us (0.27)
  waiting for transfers between devices: 2340 us -> 294 us
  matrix products: 391 us -> 137 us
  Pallas kernels: 0 us -> 97 us
  starting transfers between devices: 39.9 us -> 113 us
  other arithmetic: 161 us -> 117 us
    reduce_scatter x22 -> x0, waiting for transfers between devices: 1410 us -> none  [the longest x12 907 us: scatter_rows(): lax.psum_scatter(partial_term(jnp.int32(0), lax.axis_size('tensor') * row...]
    all_gather x18 -> x0, waiting for transfers between devices: 817 us -> none  [the longest x12 537 us: gather_rows(): lax.all_gather(row_values, 'tensor', axis=0, tiled=True)]
    ppermute x0 -> x80, waiting for transfers between devices: none -> 183 us  [the longest x24 94.6 us: passed_on(): lax.ppermute(block, 'tensor', [(i, (i + step) % size) for i in range(size)])]
    dot_general x51 -> x12, matrix products: 265 us -> 105 us  [the longest x6 52.7 us: dot_nt(): lax.dot_general(left, right, (((1,), (1,)), ((), ())), preferred_element_...]
    pallas_call x0 -> x4, Pallas kernels: none -> 97 us  [the longest x2 54 us: attend_back(): pl.pallas_call(attend_back_kernel, grid=(pairs,), in_specs=[pl.BlockSpec(...]
    ppermute x0 -> x80, starting transfers between devices: none -> 89.5 us  [the longest x24 51.1 us: passed_on(): lax.ppermute(block, 'tensor', [(i, (i + step) % size) for i in range(size)])]
    sub x6 -> x0, matrix products: 62.8 us -> none  [attention_probs(): expos = jnp.exp(scores - jnp.max(scores, axis=-1, keepdims=True))]
    convert_element_type x29 -> x23, other arithmetic: 64.9 us -> 23.2 us  [the longest x12 15.1 us: collected(): total.astype(jnp.bfloat16)]
  transfers between devices with their start and end apart: 47 -> 87, of which waited for: 47 -> 38; matrix products, arithmetic and copies ran while one was open for 3% -> 25% of each run, Pallas kernels for 0% -> 6%
where the time goes in v1:
time: 824 us; the launch traced here: 820 us
  waiting for transfers between devices  294 us (36%)
  matrix products  137 us (17%)
  other arithmetic  117 us (14%)
  starting transfers between devices  113 us (14%)
  Pallas kernels  97 us (12%)
  local copies, waits for them, and re-layouts  44.4 us (5%)
  between operations  16.7 us (2%)
    ppermute x24, waiting for transfers between devices, passed_on(): lax.ppermute(block, 'tensor', [(i, (i + step) % size) for i in range(size)])  94.6 us
    ppermute x56, waiting for transfers between devices, flip_pairs(): return lax.ppermute(block, 'dp', [(i, i ^ distance) for i in range(size)])  88.9 us
    unnamed x2, waiting for transfers between devices  58.8 us
    pallas_call x2, Pallas kernels, attend_back(): pl.pallas_call(attend_back_kernel, grid=(pairs,), in_specs=[pl.BlockSpec(...  54 us
    dot_general x6, matrix products, dot_nt(): lax.dot_general(left, right, (((1,), (1,)), ((), ())), preferred_element_...  52.7 us
    dot_general x6, matrix products, dot_nn(): return jnp.dot(left, right, preferred_element_type=jnp.float32)  52.4 us
    ppermute x24, starting transfers between devices, passed_on(): lax.ppermute(block, 'tensor', [(i, (i + step) % size) for i in range(size)])  51.1 us
    ppermute x2, waiting for transfers between devices, shifted(): return lax.ppermute(block, axis, route)  48.3 us
  transfers between devices with their start and end apart: 87, of which 38 were waited for; matrix products, arithmetic and copies ran while one was open for 25% of the time, Pallas kernels for 6%

profile of v1, /device:TPU:0, one launch (start us, length us, event | category | flops | bytes accessed | tf_op | source)
XLA Modules:
  0.0 820.1 jit_solution(10059080521125733004)
XLA Ops:
  20.9 5.9 all-to-all-start
  37.9 19.9 %collective-permute-done.2 = bf16[512,384]{1,0:T(8,128)(2,1)} collective-permute-done((bf16[512,384]{1,0:T(8,128)(2,1)S(1)}, bf16[512,384]{1,0:T(8,128)(2,1)}, u32[]{:S(2)}, u32[]{:S(2)}) %collective-permute-start.2) | collective-permute-done | bytes 393248 | tf_op jit(solution)/shard_map/ppermute | solution.py:519
  57.8 3.2 collective-permute-start.3
  62.2 3.7 fusion.87
  65.9 3.7 collective-permute-done.3
  76.9 5.1 collective-permute-done.4
  89.1 6.6 collective-permute-done.7
  97.2 6.4 collective-permute-done.8
  103.9 5.9 maximum_maximum_fusion.2.w_ref
  113.1 21.5 %attend.2 = (bf16[4,1024,128]{2,1,0:T(8,128)(2,1)S(1)}, bf16[4,1024,128]{2,1,0:T(8,128)(2,1)S(1)}, bf16[4,1024,128]{2,1,0:T(8,128)(2,1)S(1)}, f32[4,2,1024]{2,1,0:T(2,128)S(1)}, bf16[1024,512]{1,0:T(8,128)(2,1)S(1)}) custom-call(s32[1]{0:T(128)} %bitcast.4.core_ref, f32[1024,128]{1,0:T(8,128)S(1)} %get-tuple-element.138.cos_ref, ...), custom_call_target="tpu_custom_call" | custom-call | tf_op jit(solution)/shard_map/attend/pallas_call | solution.py:457
  139.2 12.4 %collective-permute-done.25 = bf16[512,512]{1,0:T(8,128)(2,1)S(1)} collective-permute-done((bf16[512,512]{1,0:T(8,128)(2,1)S(1)}, bf16[512,512]{1,0:T(8,128)(2,1)S(1)}, u32[]{:S(2)}, u32[]{:S(2)}) %collective-permute-start.25) | collective-permute-done | bytes 524320 | tf_op jit(solution)/shard_map/ppermute | solution.py:519
  151.6 11.2 %collective-permute-done.19 = bf16[512,512]{1,0:T(8,128)(2,1)S(1)} collective-permute-done((bf16[512,512]{1,0:T(8,128)(2,1)S(1)}, bf16[512,512]{1,0:T(8,128)(2,1)S(1)}, u32[]{:S(2)}, u32[]{:S(2)}) %collective-permute-start.19) | collective-permute-done | bytes 524320 | tf_op jit(solution)/shard_map/ppermute | solution.py:519
  164.8 8.3 %collective-permute-done.26 = bf16[512,512]{1,0:T(8,128)(2,1)S(1)} collective-permute-done((bf16[512,512]{1,0:T(8,128)(2,1)S(1)}, bf16[512,512]{1,0:T(8,128)(2,1)S(1)}, u32[]{:S(2)}, u32[]{:S(2)}) %collective-permute-start.26) | collective-permute-done | bytes 524320 | tf_op jit(solution)/shard_map/ppermute | solution.py:519
  174.1 6.6 collective-permute-done.20
  186.8 9.4 %collective-permute-done.23 = bf16[512,512]{1,0:T(8,128)(2,1)S(1)} collective-permute-done((bf16[512,512]{1,0:T(8,128)(2,1)S(1)}, bf16[512,512]{1,0:T(8,128)(2,1)S(1)}, u32[]{:S(2)}, u32[]{:S(2)}) %collective-permute-start.23) | collective-permute-done | bytes 524320 | tf_op jit(solution)/shard_map/ppermute | solution.py:514
  198.2 9.2 %collective-permute-done.24 = bf16[512,512]{1,0:T(8,128)(2,1)S(1)} collective-permute-done((bf16[512,512]{1,0:T(8,128)(2,1)S(1)}, bf16[512,512]{1,0:T(8,128)(2,1)S(1)}, u32[]{:S(2)}, u32[]{:S(2)}) %collective-permute-start.24) | collective-permute-done | bytes 524320 | tf_op jit(solution)/shard_map/ppermute | solution.py:514
  208.3 27.9 %maximum_maximum_fusion = bf16[1024,2048]{1,0:T(8,128)(2,1)S(1)} fusion(bf16[512,512]{1,0:T(8,128)(2,1)S(1)} %collective-permute-done.24, bf16[512,512]{1,0:T(8,128)(2,1)S(1)} %collective-permute-done.23, bf16[512,512]{1,0:T(8,128)(2,1)S(1)} %collective-permute-done.22, bf16[512,512]{1,0:T(8,128)(2,1)S(1)} %collective-permute-done.21, ...), kind=kLoop, calls=%fused_computation.8 | loop fusion | flops 33554432 | bytes 8388608 | tf_op jit(solution)/shard_map/concatenate | solution.py:622
  236.3 20.5 %fusion.52 = f32[1024,2048]{1,0:T(8,128)} fusion(bf16[1024,2048]{1,0:T(8,128)(2,1)S(1)} %maximum_maximum_fusion, bf16[512,1024]{1,0:T(8,128)(2,1)S(1)} %collective-permute-done.17, bf16[512,1024]{1,0:T(8,128)(2,1)S(1)} %multiply_convert_fusion.5), kind=kOutput, calls=%fused_computation.121 | convolution fusion | flops 4299161600 | bytes 14680064 | tf_op jit(solution)/shard_map/dot_general | solution.py:332
  258.6 8.8 %fusion.111 = f32[1024,1024]{1,0:T(8,128)S(1)} fusion(f32[1024,2048]{1,0:T(8,128)} %fusion.52, bf16[512,512]{1,0:T(8,128)(2,1)} %collective-permute-done.31, bf16[512,512]{1,0:T(8,128)(2,1)} %copy-done.141, bf16[512,512]{1,0:T(8,128)(2,1)} %copy-done.139, bf16[512,512]{1,0:T(8,128)(2,1)} %copy-done.137, bf16[512,512]{1,0:T(8,128)(2,1)S(1)} %copy-done.136, ...), kind=kOutput, calls=%fused_computation.279 | convolution fusion | flops 4347396096 | bytes 16777216 | tf_op jit(solution)/shard_map/dot_general | solution.py:332
  267.7 2.6 collective-permute-done.32
  271.3 3.4 collective-permute-start.33
  274.8 22.6 %collective-permute-done.33 = bf16[512,1024]{1,0:T(8,128)(2,1)S(1)} collective-permute-done((bf16[512,1024]{1,0:T(8,128)(2,1)S(1)}, bf16[512,1024]{1,0:T(8,128)(2,1)S(1)}, u32[]{:S(2)}, u32[]{:S(2)}) %collective-permute-start.33) | collective-permute-done | bytes 1048608 | tf_op jit(solution)/shard_map/ppermute | solution.py:21
  301.1 21.5 %attend.3 = (bf16[4,1024,128]{2,1,0:T(8,128)(2,1)S(1)}, bf16[4,1024,128]{2,1,0:T(8,128)(2,1)S(1)}, bf16[4,1024,128]{2,1,0:T(8,128)(2,1)S(1)}, f32[4,2,1024]{2,1,0:T(2,128)S(1)}, bf16[1024,512]{1,0:T(8,128)(2,1)S(1)}) custom-call(s32[1]{0:T(128)} %bitcast.4.core_ref, f32[1024,128]{1,0:T(8,128)S(1)} %get-tuple-element.138.cos_ref, ...), custom_call_target="tpu_custom_call" | custom-call | tf_op jit(solution)/shard_map/attend/pallas_call | solution.py:457
  322.7 2.7 fusion.113
  333.9 7.6 fusion.51
  341.6 10.4 %fusion.112 = f32[1024,1024]{1,0:T(8,128)} fusion(f32[1024,2048]{1,0:T(8,128)} %fusion.51, bf16[512,512]{1,0:T(8,128)(2,1)} %collective-permute-done.31, bf16[512,512]{1,0:T(8,128)(2,1)S(1)} %copy-done.142, bf16[512,512]{1,0:T(8,128)(2,1)S(1)} %copy-done.140, bf16[512,512]{1,0:T(8,128)(2,1)S(1)} %copy-done.138, bf16[512,512]{1,0:T(8,128)(2,1)S(1)} %copy-done.136, ...), kind=kOutput, calls=%fused_computation.280 | convolution fusion | flops 4347396096 | bytes 16777216 | tf_op jit(solution)/shard_map/dot_general | solution.py:332
  352.0 2.7 slice.574
  358.0 5.0 all-to-all-start.2
  365.3 3.2 all-to-all-done.2
  368.5 3.8 fusion.36
  377.7 15.3 %multiply_convert_fusion.1 = bf16[1024,2048]{1,0:T(8,128)(2,1)S(1)} fusion(f32[1024,2048]{1,0:T(8,128)} %fusion.51, bf16[512,1024]{1,0:T(8,128)(2,1)S(1)} %collective-permute-done.40, bf16[512,1024]{1,0:T(8,128)(2,1)S(1)} %fusion.32, bf16[512,512]{1,0:T(8,128)(2,1)} %collective-permute-done.31, bf16[512,512]{1,0:T(8,128)(2,1)} %copy-done.141, ...), kind=kOutput, calls=%fused_computation.2 | convolution fusion | flops 4374659072 | bytes 18874368 | tf_op jit(solution)/shard_map/dot_general | solution.py:326
  395.1 6.3 fusion.130
  405.7 2.7 multiply_reduce_fusion.1
  412.7 27.0 %attend_back.2 = bf16[1024,1536]{1,0:T(8,128)(2,1)S(1)} custom-call(s32[1]{0:T(128)} %bitcast.4.core_ref, f32[1024,128]{1,0:T(8,128)S(1)} %copy-done.3, f32[1024,128]{1,0:T(8,128)S(1)} %copy-done.6, bf16[1024,1024]{1,0:T(8,128)(2,1)S(1)} %pad_maximum_fusion.5.grad_ref, bf16[512,1024]{1,0:T(8,128)(2,1)S(1)} %maximum_maximum_fusion.3.w_ref, ...), custom_call_target="tpu_custom_call" | custom-call | tf_op jit(solution)/shard_map/attend_back/pallas_call | solution.py:490
  439.7 3.4 fusion.131
  450.0 25.7 %collective-permute-done.44 = bf16[512,1024]{1,0:T(8,128)(2,1)S(1)} collective-permute-done((bf16[512,1024]{1,0:T(8,128)(2,1)S(1)}, bf16[512,1024]{1,0:T(8,128)(2,1)S(1)}, u32[]{:S(2)}, u32[]{:S(2)}) %collective-permute-start.44) | collective-permute-done | bytes 1048608 | tf_op jit(solution)/shard_map/ppermute | solution.py:21
  482.7 4.2 all-to-all-start.1
  487.0 16.5 %multiply_convert_fusion = bf16[1024,2048]{1,0:T(8,128)(2,1)} fusion(f32[1024,2048]{1,0:T(8,128)} %fusion.52, bf16[512,1024]{1,0:T(8,128)(2,1)} %collective-permute-done.45, bf16[512,1024]{1,0:T(8,128)(2,1)} %fusion.16, bf16[512,512]{1,0:T(8,128)(2,1)} %collective-permute-done.31, bf16[512,512]{1,0:T(8,128)(2,1)} %copy-done.141, ...), kind=kOutput, calls=%fused_computation | convolution fusion | flops 4374659072 | bytes 18874368 | tf_op jit(solution)/shard_map/dot_general | solution.py:326
  503.5 8.1 fusion.128
  514.1 17.6 %fusion.129 = (bf16[2048,1024]{1,0:T(8,128)(2,1)}, f32[2048,1024]{1,0:T(8,128)}) fusion(pred[]{:T(512)S(6)} %eq.29, bf16[512,1024]{1,0:T(8,128)(2,1)} %collective-permute-done.45, bf16[512,1024]{1,0:T(8,128)(2,1)} %fusion.16, bf16[512,1024]{1,0:T(8,128)(2,1)} %copy-done.130, bf16[512,1024]{1,0:T(8,128)(2,1)} %copy-done.79, f32[1024,2048]{1,0:T(8,128)} %fusion.52, ...), kind=kOutput, calls=%fused_computation.296 | convolution fusion | flops 4346347520 | bytes 33554432 | tf_op jit(solution)/shard_map/dot_general | solution.py:53
  531.8 7.7 fusion.132
  546.3 3.8 collective-permute-start.70
  551.6 4.5 collective-permute-done.77
  558.7 8.6 %collective-permute-done.68 = bf16[512,512]{1,0:T(8,128)(2,1)} collective-permute-done((bf16[512,512]{1,0:T(8,128)(2,1)}, bf16[512,512]{1,0:T(8,128)(2,1)}, u32[]{:S(2)}, u32[]{:S(2)}) %collective-permute-start.68) | collective-permute-done | bytes 524320 | tf_op jit(solution)/shard_map/ppermute | solution.py:514
  568.4 3.8 collective-permute-start.78
  574.7 3.6 multiply_reduce_fusion.2
  578.3 3.1 multiply_reduce_fusion.3
  581.9 7.4 collective-permute-done.76
  592.9 3.5 collective-permute-start.79
  601.5 12.6 %collective-permute-done.75 = bf16[512,512]{1,0:T(8,128)(2,1)S(1)} collective-permute-done((bf16[512,512]{1,0:T(8,128)(2,1)S(1)}, bf16[512,512]{1,0:T(8,128)(2,1)S(1)}, u32[]{:S(2)}, u32[]{:S(2)}) %collective-permute-start.75) | collective-permute-done | bytes 524320 | tf_op jit(solution)/shard_map/ppermute | solution.py:514
  617.6 3.3 collective-permute-start.80
  624.3 2.7 fusion.127
  630.0 27.0 %attend_back.3 = bf16[1024,1536]{1,0:T(8,128)(2,1)S(1)} custom-call(s32[1]{0:T(128)} %bitcast.4.core_ref, f32[1024,128]{1,0:T(8,128)S(1)} %copy-done.4, f32[1024,128]{1,0:T(8,128)S(1)} %copy-done.7, bf16[1024,1024]{1,0:T(8,128)(2,1)S(1)} %pad_maximum_fusion.7.grad_ref, bf16[512,1024]{1,0:T(8,128)(2,1)S(1)} %copy-done.9, ...), custom_call_target="tpu_custom_call" | custom-call | tf_op jit(solution)/shard_map/attend_back/pallas_call | solution.py:490
  657.1 3.4 fusion.133
  660.6 3.6 fusion.126
  675.9 3.2 collective-permute-start.63
  681.7 4.3 collective-permute-start.64
  689.5 4.3 collective-permute-start.54
  699.1 2.9 collective-permute-done.54
  702.9 4.3 collective-permute-start.55
  710.4 3.5 all-to-all-start.3
  718.4 4.3 collective-permute-start.56
  724.9 17.4 %collective-permute-done.56 = bf16[512,384]{1,0:T(8,128)(2,1)S(1)} collective-permute-done((bf16[512,384]{1,0:T(8,128)(2,1)S(1)}, bf16[512,384]{1,0:T(8,128)(2,1)S(1)}, u32[]{:S(2)}, u32[]{:S(2)}) %collective-permute-start.56) | collective-permute-done | bytes 393248 | tf_op jit(solution)/shard_map/ppermute | solution.py:519
  747.0 58.7 %reduce-scatter.4.cloned.1.call-done = f32[64,4]{1,0:T(8,128)} async-done(((f32[1024,4]{1,0:T(8,128)}), f32[64,4]{1,0:T(8,128)}) %reduce-scatter.4.cloned.1.call-update) | async-done | bytes 1040
  (558 shorter events, 193.1 us)
Async XLA Ops:
  20.9 63.2 %all-to-all-start = ((bf16[4,128,1024]{2,1,0:T(8,128)(2,1)}), bf16[4,128,1024]{2,1,0:T(8,128)(2,1)S(1)}, u32[]{:S(2)}, u32[]{:S(2)}) async-start(bf16[4,128,1024]{2,1,0:T(8,128)(2,1)} %pad_maximum_fusion.16), calls=%async_computation | async-start | bytes 2097152 | tf_op jit(solution)/shard_map/all_to_all | solution.py:597
  29.5 58.0 %collective-permute-start.5 = (bf16[512,384]{1,0:T(8,128)(2,1)S(1)}, bf16[512,384]{1,0:T(8,128)(2,1)}, u32[]{:S(2)}, u32[]{:S(2)}) collective-permute-start(bf16[512,384]{1,0:T(8,128)(2,1)S(1)} %dynamic_slice.61), channel_id=1, source_target_pairs={{0,8},{4,12},{8,0},{12,4},{1,9},{5,13},{9,1},{13,5},{2,10},{6,14},... | collective-permute-start | bytes 1179656 | tf_op jit(solution)/shard_map/ppermute | solution.py:514
  31.1 26.7 %collective-permute-start.2 = (bf16[512,384]{1,0:T(8,128)(2,1)S(1)}, bf16[512,384]{1,0:T(8,128)(2,1)}, u32[]{:S(2)}, u32[]{:S(2)}) collective-permute-start(bf16[512,384]{1,0:T(8,128)(2,1)S(1)} %dynamic_slice.61), channel_id=1, source_target_pairs={{0,1},{1,2},{2,3},{3,0},{4,5},{5,6},{6,7},{7,4},{8,9},{9,10},{10,1... | collective-permute-start | bytes 1179656 | tf_op jit(solution)/shard_map/ppermute | solution.py:519
  34.7 37.6 %collective-permute-start.9 = (bf16[128,512]{1,0:T(8,128)(2,1)}, bf16[128,512]{1,0:T(8,128)(2,1)}, u32[]{:S(2)}, u32[]{:S(2)}) collective-permute-start(bf16[128,512]{1,0:T(8,128)(2,1)} %dynamic-slice_bitcast_fusion.6), channel_id=1, source_target_pairs={{0,1},{1,2},{2,3},{3,0},{4,5},{5,6},{6,7},{7,4},{8,9},{9,10},{10,1... | collective-permute-start | bytes 393224 | tf_op jit(solution)/shard_map/ppermute | solution.py:519
  74.9 14.2 %collective-permute-start.6 = (bf16[512,384]{1,0:T(8,128)(2,1)}, bf16[512,384]{1,0:T(8,128)(2,1)}, u32[]{:S(2)}, u32[]{:S(2)}) collective-permute-start(bf16[512,384]{1,0:T(8,128)(2,1)} %collective-permute-done.2), channel_id=1, source_target_pairs={{0,8},{4,12},{8,0},{12,4},{1,9},{5,13},{9,1},{13,5},{2,10},{6,14},... | collective-permute-start | bytes 1179656 | tf_op jit(solution)/shard_map/ppermute | solution.py:514
  76.4 19.3 %collective-permute-start.7 = (bf16[512,384]{1,0:T(8,128)(2,1)}, bf16[512,384]{1,0:T(8,128)(2,1)}, u32[]{:S(2)}, u32[]{:S(2)}) collective-permute-start(bf16[512,384]{1,0:T(8,128)(2,1)} %collective-permute-done.3), channel_id=1, source_target_pairs={{0,8},{4,12},{8,0},{12,4},{1,9},{5,13},{9,1},{13,5},{2,10},{6,14},... | collective-permute-start | bytes 1179656 | tf_op jit(solution)/shard_map/ppermute | solution.py:514
  82.0 21.6 %collective-permute-start.8 = (bf16[512,384]{1,0:T(8,128)(2,1)}, bf16[512,384]{1,0:T(8,128)(2,1)}, u32[]{:S(2)}, u32[]{:S(2)}) collective-permute-start(bf16[512,384]{1,0:T(8,128)(2,1)} %collective-permute-done.4), channel_id=1, source_target_pairs={{0,8},{4,12},{8,0},{12,4},{1,9},{5,13},{9,1},{13,5},{2,10},{6,14},... | collective-permute-start | bytes 1179656 | tf_op jit(solution)/shard_map/ppermute | solution.py:514
  84.7 27.4 %collective-permute-start.1 = (bf16[512,1024]{1,0:T(8,128)(2,1)S(1)}, bf16[512,1024]{1,0:T(8,128)(2,1)S(1)}, u32[]{:S(2)}, u32[]{:S(2)}) collective-permute-start(bf16[512,1024]{1,0:T(8,128)(2,1)S(1)} %fusion.34), channel_id=1, source_target_pairs={{0,4},{4,0},{8,12},{12,8},{1,5},{5,1},{9,13},{13,9},{2,6},{6,2},{1... | collective-permute-start | bytes 3145736 | tf_op jit(solution)/shard_map/ppermute | solution.py:514
  87.5 47.1 %collective-permute-start.12 = (bf16[128,512]{1,0:T(8,128)(2,1)}, bf16[128,512]{1,0:T(8,128)(2,1)S(1)}, u32[]{:S(2)}, u32[]{:S(2)}) collective-permute-start(bf16[128,512]{1,0:T(8,128)(2,1)} %dynamic-slice_bitcast_fusion.6), channel_id=1, source_target_pairs={{0,8},{4,12},{8,0},{12,4},{1,9},{5,13},{9,1},{13,5},{2,10},{6,14},... | collective-permute-start | bytes 393224 | tf_op jit(solution)/shard_map/ppermute | solution.py:514
  89.1 45.8 %collective-permute-start.18 = (bf16[512,512]{1,0:T(8,128)(2,1)S(1)}, bf16[512,512]{1,0:T(8,128)(2,1)S(1)}, u32[]{:S(2)}, u32[]{:S(2)}) collective-permute-start(bf16[512,512]{1,0:T(8,128)(2,1)S(1)} %dynamic-slice_bitcast_fusion.4), channel_id=1, source_target_pairs={{0,1},{1,2},{2,3},{3,0},{4,5},{5,6},{6,7},{7,4},{8,9},{9,10},{10,1... | collective-permute-start | bytes 1572872 | tf_op jit(solution)/shard_map/ppermute | solution.py:519
  95.7 40.7 %collective-permute-start.13 = (bf16[128,512]{1,0:T(8,128)(2,1)}, bf16[128,512]{1,0:T(8,128)(2,1)S(1)}, u32[]{:S(2)}, u32[]{:S(2)}) collective-permute-start(bf16[128,512]{1,0:T(8,128)(2,1)} %collective-permute-done.9), channel_id=1, source_target_pairs={{0,8},{4,12},{8,0},{12,4},{1,9},{5,13},{9,1},{13,5},{2,10},{6,14},... | collective-permute-start | bytes 393224 | tf_op jit(solution)/shard_map/ppermute | solution.py:514
  110.6 25.9 %collective-permute-start.14 = (bf16[128,512]{1,0:T(8,128)(2,1)}, bf16[128,512]{1,0:T(8,128)(2,1)S(1)}, u32[]{:S(2)}, u32[]{:S(2)}) collective-permute-start(bf16[128,512]{1,0:T(8,128)(2,1)} %collective-permute-done.10), channel_id=1, source_target_pairs={{0,8},{4,12},{8,0},{12,4},{1,9},{5,13},{9,1},{13,5},{2,10},{6,14},... | collective-permute-start | bytes 393224 | tf_op jit(solution)/shard_map/ppermute | solution.py:514
  112.1 24.3 %collective-permute-start.15 = (bf16[128,512]{1,0:T(8,128)(2,1)S(1)}, bf16[128,512]{1,0:T(8,128)(2,1)S(1)}, u32[]{:S(2)}, u32[]{:S(2)}) collective-permute-start(bf16[128,512]{1,0:T(8,128)(2,1)S(1)} %collective-permute-done.11), channel_id=1, source_target_pairs={{0,8},{4,12},{8,0},{12,4},{1,9},{5,13},{9,1},{13,5},{2,10},{6,14},... | collective-permute-start | bytes 393224 | tf_op jit(solution)/shard_map/ppermute | solution.py:514
  134.6 17.0 %collective-permute-start.25 = (bf16[512,512]{1,0:T(8,128)(2,1)S(1)}, bf16[512,512]{1,0:T(8,128)(2,1)S(1)}, u32[]{:S(2)}, u32[]{:S(2)}) collective-permute-start(bf16[512,512]{1,0:T(8,128)(2,1)S(1)} %dynamic-slice_bitcast_fusion.3), channel_id=1, source_target_pairs={{0,1},{1,2},{2,3},{3,0},{4,5},{5,6},{6,7},{7,4},{8,9},{9,10},{10,1... | collective-permute-start | bytes 1572872 | tf_op jit(solution)/shard_map/ppermute | solution.py:519
  134.9 27.9 %collective-permute-start.19 = (bf16[512,512]{1,0:T(8,128)(2,1)S(1)}, bf16[512,512]{1,0:T(8,128)(2,1)S(1)}, u32[]{:S(2)}, u32[]{:S(2)}) collective-permute-start(bf16[512,512]{1,0:T(8,128)(2,1)S(1)} %collective-permute-done.18), channel_id=1, source_target_pairs={{0,1},{1,2},{2,3},{3,0},{4,5},{5,6},{6,7},{7,4},{8,9},{9,10},{10,1... | collective-permute-start | bytes 1572872 | tf_op jit(solution)/shard_map/ppermute | solution.py:519
  139.1 41.6 %collective-permute-start.16 = (bf16[512,1024]{1,0:T(8,128)(2,1)S(1)}, bf16[512,1024]{1,0:T(8,128)(2,1)S(1)}, u32[]{:S(2)}, u32[]{:S(2)}) collective-permute-start(bf16[512,1024]{1,0:T(8,128)(2,1)S(1)} %slice.577), channel_id=1, source_target_pairs={{0,4},{4,0},{8,12},{12,8},{1,5},{5,1},{9,13},{13,9},{2,6},{6,2},{1... | collective-permute-start | bytes 3145736 | tf_op jit(solution)/shard_map/ppermute | solution.py:514
  151.5 21.5 %collective-permute-start.26 = (bf16[512,512]{1,0:T(8,128)(2,1)S(1)}, bf16[512,512]{1,0:T(8,128)(2,1)S(1)}, u32[]{:S(2)}, u32[]{:S(2)}) collective-permute-start(bf16[512,512]{1,0:T(8,128)(2,1)S(1)} %collective-permute-done.25), channel_id=1, source_target_pairs={{0,1},{1,2},{2,3},{3,0},{4,5},{5,6},{6,7},{7,4},{8,9},{9,10},{10,1... | collective-permute-start | bytes 1572872 | tf_op jit(solution)/shard_map/ppermute | solution.py:519
  162.8 17.9 %collective-permute-start.20 = (bf16[512,512]{1,0:T(8,128)(2,1)S(1)}, bf16[512,512]{1,0:T(8,128)(2,1)S(1)}, u32[]{:S(2)}, u32[]{:S(2)}) collective-permute-start(bf16[512,512]{1,0:T(8,128)(2,1)S(1)} %collective-permute-done.19), channel_id=1, source_target_pairs={{0,1},{1,2},{2,3},{3,0},{4,5},{5,6},{6,7},{7,4},{8,9},{9,10},{10,1... | collective-permute-start | bytes 1572872 | tf_op jit(solution)/shard_map/ppermute | solution.py:519
  162.8 21.2 %collective-permute-start.21 = (bf16[512,512]{1,0:T(8,128)(2,1)S(1)}, bf16[512,512]{1,0:T(8,128)(2,1)S(1)}, u32[]{:S(2)}, u32[]{:S(2)}) collective-permute-start(bf16[512,512]{1,0:T(8,128)(2,1)S(1)} %dynamic-slice_bitcast_fusion.4), channel_id=1, source_target_pairs={{0,8},{4,12},{8,0},{12,4},{1,9},{5,13},{9,1},{13,5},{2,10},{6,14},... | collective-permute-start | bytes 1572872 | tf_op jit(solution)/shard_map/ppermute | solution.py:514
  164.1 21.9 %collective-permute-start.22 = (bf16[512,512]{1,0:T(8,128)(2,1)S(1)}, bf16[512,512]{1,0:T(8,128)(2,1)S(1)}, u32[]{:S(2)}, u32[]{:S(2)}) collective-permute-start(bf16[512,512]{1,0:T(8,128)(2,1)S(1)} %collective-permute-done.18), channel_id=1, source_target_pairs={{0,8},{4,12},{8,0},{12,4},{1,9},{5,13},{9,1},{13,5},{2,10},{6,14},... | collective-permute-start | bytes 1572872 | tf_op jit(solution)/shard_map/ppermute | solution.py:514
  173.1 23.0 %collective-permute-start.23 = (bf16[512,512]{1,0:T(8,128)(2,1)S(1)}, bf16[512,512]{1,0:T(8,128)(2,1)S(1)}, u32[]{:S(2)}, u32[]{:S(2)}) collective-permute-start(bf16[512,512]{1,0:T(8,128)(2,1)S(1)} %collective-permute-done.19), channel_id=1, source_target_pairs={{0,8},{4,12},{8,0},{12,4},{1,9},{5,13},{9,1},{13,5},{2,10},{6,14},... | collective-permute-start | bytes 1572872 | tf_op jit(solution)/shard_map/ppermute | solution.py:514
  180.7 16.4 %collective-permute-start.27 = (bf16[512,512]{1,0:T(8,128)(2,1)S(1)}, bf16[512,512]{1,0:T(8,128)(2,1)S(1)}, u32[]{:S(2)}, u32[]{:S(2)}) collective-permute-start(bf16[512,512]{1,0:T(8,128)(2,1)S(1)} %collective-permute-done.26), channel_id=1, source_target_pairs={{0,1},{1,2},{2,3},{3,0},{4,5},{5,6},{6,7},{7,4},{8,9},{9,10},{10,1... | collective-permute-start | bytes 1572872 | tf_op jit(solution)/shard_map/ppermute | solution.py:519
  180.7 26.7 %collective-permute-start.24 = (bf16[512,512]{1,0:T(8,128)(2,1)S(1)}, bf16[512,512]{1,0:T(8,128)(2,1)S(1)}, u32[]{:S(2)}, u32[]{:S(2)}) collective-permute-start(bf16[512,512]{1,0:T(8,128)(2,1)S(1)} %collective-permute-done.20), channel_id=1, source_target_pairs={{0,8},{4,12},{8,0},{12,4},{1,9},{5,13},{9,1},{13,5},{2,10},{6,14},... | collective-permute-start | bytes 1572872 | tf_op jit(solution)/shard_map/ppermute | solution.py:514
  184.0 52.3 %collective-permute-start.17 = (bf16[512,1024]{1,0:T(8,128)(2,1)S(1)}, bf16[512,1024]{1,0:T(8,128)(2,1)S(1)}, u32[]{:S(2)}, u32[]{:S(2)}) collective-permute-start(bf16[512,1024]{1,0:T(8,128)(2,1)S(1)} %multiply_convert_fusion.5), channel_id=1, source_target_pairs={{0,4},{4,0},{8,12},{12,8},{1,5},{5,1},{9,13},{13,9},{2,6},{6,2},{1... | collective-permute-start | bytes 3145736 | tf_op jit(solution)/shard_map/ppermute | solution.py:514
  185.9 70.9 %collective-permute-start.28 = (bf16[512,512]{1,0:T(8,128)(2,1)S(1)}, bf16[512,512]{1,0:T(8,128)(2,1)S(1)}, u32[]{:S(2)}, u32[]{:S(2)}) collective-permute-start(bf16[512,512]{1,0:T(8,128)(2,1)S(1)} %dynamic-slice_bitcast_fusion.3), channel_id=1, source_target_pairs={{0,8},{4,12},{8,0},{12,4},{1,9},{5,13},{9,1},{13,5},{2,10},{6,14},... | collective-permute-start | bytes 1572872 | tf_op jit(solution)/shard_map/ppermute | solution.py:514
  196.1 60.7 %collective-permute-start.29 = (bf16[512,512]{1,0:T(8,128)(2,1)S(1)}, bf16[512,512]{1,0:T(8,128)(2,1)S(1)}, u32[]{:S(2)}, u32[]{:S(2)}) collective-permute-start(bf16[512,512]{1,0:T(8,128)(2,1)S(1)} %collective-permute-done.25), channel_id=1, source_target_pairs={{0,8},{4,12},{8,0},{12,4},{1,9},{5,13},{9,1},{13,5},{2,10},{6,14},... | collective-permute-start | bytes 1572872 | tf_op jit(solution)/shard_map/ppermute | solution.py:514
  197.0 59.8 %collective-permute-start.30 = (bf16[512,512]{1,0:T(8,128)(2,1)S(1)}, bf16[512,512]{1,0:T(8,128)(2,1)S(1)}, u32[]{:S(2)}, u32[]{:S(2)}) collective-permute-start(bf16[512,512]{1,0:T(8,128)(2,1)S(1)} %collective-permute-done.26), channel_id=1, source_target_pairs={{0,8},{4,12},{8,0},{12,4},{1,9},{5,13},{9,1},{13,5},{2,10},{6,14},... | collective-permute-start | bytes 1572872 | tf_op jit(solution)/shard_map/ppermute | solution.py:514
  207.4 51.2 %collective-permute-start.31 = (bf16[512,512]{1,0:T(8,128)(2,1)S(1)}, bf16[512,512]{1,0:T(8,128)(2,1)}, u32[]{:S(2)}, u32[]{:S(2)}) collective-permute-start(bf16[512,512]{1,0:T(8,128)(2,1)S(1)} %collective-permute-done.27), channel_id=1, source_target_pairs={{0,8},{4,12},{8,0},{12,4},{1,9},{5,13},{9,1},{13,5},{2,10},{6,14},... | collective-permute-start | bytes 1572872 | tf_op jit(solution)/shard_map/ppermute | solution.py:514
  271.3 26.1 %collective-permute-start.33 = (bf16[512,1024]{1,0:T(8,128)(2,1)S(1)}, bf16[512,1024]{1,0:T(8,128)(2,1)S(1)}, u32[]{:S(2)}, u32[]{:S(2)}) collective-permute-start(bf16[512,1024]{1,0:T(8,128)(2,1)S(1)} %add_convert_fusion.3), channel_id=1, source_target_pairs={{0,16},{1,17},{2,18},{3,19},{4,20},{5,21},{6,22},{7,23},{8,24},{9,... | collective-permute-start | bytes 3145736 | tf_op jit(solution)/shard_map/ppermute | solution.py:21
  448.2 27.5 %collective-permute-start.44 = (bf16[512,1024]{1,0:T(8,128)(2,1)S(1)}, bf16[512,1024]{1,0:T(8,128)(2,1)S(1)}, u32[]{:S(2)}, u32[]{:S(2)}) collective-permute-start(bf16[512,1024]{1,0:T(8,128)(2,1)S(1)} %fusion.23), channel_id=1, source_target_pairs={{16,0},{17,1},{18,2},{19,3},{20,4},{21,5},{22,6},{23,7},{24,8},{25... | collective-permute-start | bytes 3145736 | tf_op jit(solution)/shard_map/ppermute | solution.py:21
  482.7 67.3 %all-to-all-start.1 = ((bf16[4,128,1024]{2,1,0:T(8,128)(2,1)}), bf16[4,128,1024]{2,1,0:T(8,128)(2,1)}, u32[]{:S(2)}, u32[]{:S(2)}) async-start(bf16[4,128,1024]{2,1,0:T(8,128)(2,1)} %bitcast.169), calls=%async_computation.1 | async-start | bytes 2097152 | tf_op jit(solution)/shard_map/all_to_all | solution.py:602
  513.0 31.2 %collective-permute-start.69 = (bf16[512,512]{1,0:T(8,128)(2,1)}, bf16[512,512]{1,0:T(8,128)(2,1)}, u32[]{:S(2)}, u32[]{:S(2)}) collective-permute-start(bf16[512,512]{1,0:T(8,128)(2,1)} %get-tuple-element.82), channel_id=1, source_target_pairs={{0,8},{4,12},{8,0},{12,4},{1,9},{5,13},{9,1},{13,5},{2,10},{6,14},... | collective-permute-start | bytes 1572872 | tf_op jit(solution)/shard_map/ppermute | solution.py:514
  541.1 15.0 %collective-permute-start.77 = (bf16[512,512]{1,0:T(8,128)(2,1)}, bf16[512,512]{1,0:T(8,128)(2,1)}, u32[]{:S(2)}, u32[]{:S(2)}) collective-permute-start(bf16[512,512]{1,0:T(8,128)(2,1)} %get-tuple-element.78), channel_id=1, source_target_pairs={{0,8},{4,12},{8,0},{12,4},{1,9},{5,13},{9,1},{13,5},{2,10},{6,14},... | collective-permute-start | bytes 1572872 | tf_op jit(solution)/shard_map/ppermute | solution.py:514
  542.1 25.2 %collective-permute-start.68 = (bf16[512,512]{1,0:T(8,128)(2,1)}, bf16[512,512]{1,0:T(8,128)(2,1)}, u32[]{:S(2)}, u32[]{:S(2)}) collective-permute-start(bf16[512,512]{1,0:T(8,128)(2,1)} %get-tuple-element.83), channel_id=1, source_target_pairs={{0,8},{4,12},{8,0},{12,4},{1,9},{5,13},{9,1},{13,5},{2,10},{6,14},... | collective-permute-start | bytes 1572872 | tf_op jit(solution)/shard_map/ppermute | solution.py:514
  544.2 29.9 %collective-permute-start.46 = (bf16[512,1024]{1,0:T(8,128)(2,1)}, bf16[512,1024]{1,0:T(8,128)(2,1)}, u32[]{:S(2)}, u32[]{:S(2)}) collective-permute-start(bf16[512,1024]{1,0:T(8,128)(2,1)} %slice.571), channel_id=1, source_target_pairs={{0,4},{4,0},{8,12},{12,8},{1,5},{5,1},{9,13},{13,9},{2,6},{6,2},{1... | collective-permute-start | bytes 3145736 | tf_op jit(solution)/shard_map/ppermute | solution.py:514
  546.3 22.1 %collective-permute-start.70 = (bf16[512,512]{1,0:T(8,128)(2,1)}, bf16[512,512]{1,0:T(8,128)(2,1)}, u32[]{:S(2)}, u32[]{:S(2)}) collective-permute-start(bf16[512,512]{1,0:T(8,128)(2,1)} %fusion.61), channel_id=1, source_target_pairs={{0,3},{1,0},{2,1},{3,2},{4,7},{5,4},{6,5},{7,6},{8,11},{9,8},{10,9... | collective-permute-start | bytes 1572872 | tf_op jit(solution)/shard_map/ppermute | solution.py:519
  551.3 46.6 %collective-permute-start.38 = (bf16[2,128,1024]{2,1,0:T(8,128)(2,1)S(1)}, bf16[2,128,1024]{2,1,0:T(8,128)(2,1)S(1)}, u32[]{:S(2)}, u32[]{:S(2)}) collective-permute-start(bf16[2,128,1024]{2,1,0:T(8,128)(2,1)S(1)} %dynamic-slice_bitcast_fusion.2), channel_id=1, source_target_pairs={{0,4},{4,0},{8,12},{12,8},{1,5},{5,1},{9,13},{13,9},{2,6},{6,2},{1... | collective-permute-start | bytes 1572872 | tf_op jit(solution)/shard_map/ppermute | solution.py:514
  556.1 36.8 %collective-permute-start.67 = (bf16[512,512]{1,0:T(8,128)(2,1)}, bf16[512,512]{1,0:T(8,128)(2,1)S(1)}, u32[]{:S(2)}, u32[]{:S(2)}) collective-permute-start(bf16[512,512]{1,0:T(8,128)(2,1)} %get-tuple-element.84), channel_id=1, source_target_pairs={{0,8},{4,12},{8,0},{12,4},{1,9},{5,13},{9,1},{13,5},{2,10},{6,14},... | collective-permute-start | bytes 1572872 | tf_op jit(solution)/shard_map/ppermute | solution.py:514
  567.3 22.0 %collective-permute-start.76 = (bf16[512,512]{1,0:T(8,128)(2,1)S(1)}, bf16[512,512]{1,0:T(8,128)(2,1)S(1)}, u32[]{:S(2)}, u32[]{:S(2)}) collective-permute-start(bf16[512,512]{1,0:T(8,128)(2,1)S(1)} %copy-done.93), channel_id=1, source_target_pairs={{0,8},{4,12},{8,0},{12,4},{1,9},{5,13},{9,1},{13,5},{2,10},{6,14},... | collective-permute-start | bytes 1572872 | tf_op jit(solution)/shard_map/ppermute | solution.py:514
  568.4 22.0 %collective-permute-start.78 = (bf16[512,512]{1,0:T(8,128)(2,1)S(1)}, bf16[512,512]{1,0:T(8,128)(2,1)S(1)}, u32[]{:S(2)}, u32[]{:S(2)}) collective-permute-start(bf16[512,512]{1,0:T(8,128)(2,1)S(1)} %fusion.55), channel_id=1, source_target_pairs={{0,3},{1,0},{2,1},{3,2},{4,7},{5,4},{6,5},{7,6},{8,11},{9,8},{10,9... | collective-permute-start | bytes 1572872 | tf_op jit(solution)/shard_map/ppermute | solution.py:519
  574.1 22.3 %collective-permute-start.71 = (bf16[512,512]{1,0:T(8,128)(2,1)S(1)}, bf16[512,512]{1,0:T(8,128)(2,1)S(1)}, u32[]{:S(2)}, u32[]{:S(2)}) collective-permute-start(bf16[512,512]{1,0:T(8,128)(2,1)S(1)} %fusion.63), channel_id=1, source_target_pairs={{0,3},{1,0},{2,1},{3,2},{4,7},{5,4},{6,5},{7,6},{8,11},{9,8},{10,9... | collective-permute-start | bytes 1572872 | tf_op jit(solution)/shard_map/ppermute | solution.py:519
  589.3 31.6 %collective-permute-start.66 = (bf16[512,512]{1,0:T(8,128)(2,1)S(1)}, bf16[512,512]{1,0:T(8,128)(2,1)S(1)}, u32[]{:S(2)}, u32[]{:S(2)}) collective-permute-start(bf16[512,512]{1,0:T(8,128)(2,1)S(1)} %copy-done.91), channel_id=1, source_target_pairs={{0,8},{4,12},{8,0},{12,4},{1,9},{5,13},{9,1},{13,5},{2,10},{6,14},... | collective-permute-start | bytes 1572872 | tf_op jit(solution)/shard_map/ppermute | solution.py:514
  590.5 23.7 %collective-permute-start.75 = (bf16[512,512]{1,0:T(8,128)(2,1)S(1)}, bf16[512,512]{1,0:T(8,128)(2,1)S(1)}, u32[]{:S(2)}, u32[]{:S(2)}) collective-permute-start(bf16[512,512]{1,0:T(8,128)(2,1)S(1)} %copy-done.92), channel_id=1, source_target_pairs={{0,8},{4,12},{8,0},{12,4},{1,9},{5,13},{9,1},{13,5},{2,10},{6,14},... | collective-permute-start | bytes 1572872 | tf_op jit(solution)/shard_map/ppermute | solution.py:514
  592.9 22.4 %collective-permute-start.79 = (bf16[512,512]{1,0:T(8,128)(2,1)S(1)}, bf16[512,512]{1,0:T(8,128)(2,1)S(1)}, u32[]{:S(2)}, u32[]{:S(2)}) collective-permute-start(bf16[512,512]{1,0:T(8,128)(2,1)S(1)} %fusion.57), channel_id=1, source_target_pairs={{0,3},{1,0},{2,1},{3,2},{4,7},{5,4},{6,5},{7,6},{8,11},{9,8},{10,9... | collective-permute-start | bytes 1572872 | tf_op jit(solution)/shard_map/ppermute | solution.py:519
  596.4 27.8 %collective-permute-start.47 = (bf16[512,1024]{1,0:T(8,128)(2,1)S(1)}, bf16[512,1024]{1,0:T(8,128)(2,1)S(1)}, u32[]{:S(2)}, u32[]{:S(2)}) collective-permute-start(bf16[512,1024]{1,0:T(8,128)(2,1)S(1)} %subtract_convert_fusion), channel_id=1, source_target_pairs={{0,4},{4,0},{8,12},{12,8},{1,5},{5,1},{9,13},{13,9},{2,6},{6,2},{1... | collective-permute-start | bytes 3145736 | tf_op jit(solution)/shard_map/ppermute | solution.py:514
  597.9 23.0 %collective-permute-start.72 = (bf16[512,512]{1,0:T(8,128)(2,1)S(1)}, bf16[512,512]{1,0:T(8,128)(2,1)S(1)}, u32[]{:S(2)}, u32[]{:S(2)}) collective-permute-start(bf16[512,512]{1,0:T(8,128)(2,1)S(1)} %fusion.65), channel_id=1, source_target_pairs={{0,3},{1,0},{2,1},{3,2},{4,7},{5,4},{6,5},{7,6},{8,11},{9,8},{10,9... | collective-permute-start | bytes 1572872 | tf_op jit(solution)/shard_map/ppermute | solution.py:519
  614.1 54.4 %collective-permute-start.74 = (bf16[512,512]{1,0:T(8,128)(2,1)}, bf16[512,512]{1,0:T(8,128)(2,1)}, u32[]{:S(2)}, u32[]{:S(2)}) collective-permute-start(bf16[512,512]{1,0:T(8,128)(2,1)} %get-tuple-element.77), channel_id=1, source_target_pairs={{0,8},{4,12},{8,0},{12,4},{1,9},{5,13},{9,1},{13,5},{2,10},{6,14},... | collective-permute-start | bytes 1572872 | tf_op jit(solution)/shard_map/ppermute | solution.py:514
  617.6 52.1 %collective-permute-start.80 = (bf16[512,512]{1,0:T(8,128)(2,1)}, bf16[512,512]{1,0:T(8,128)(2,1)}, u32[]{:S(2)}, u32[]{:S(2)}) collective-permute-start(bf16[512,512]{1,0:T(8,128)(2,1)} %fusion.59), channel_id=1, source_target_pairs={{0,3},{1,0},{2,1},{3,2},{4,7},{5,4},{6,5},{7,6},{8,11},{9,8},{10,9... | collective-permute-start | bytes 1572872 | tf_op jit(solution)/shard_map/ppermute | solution.py:519
  624.2 89.8 %collective-permute-start.73 = (f32[256,512]{1,0:T(8,128)}, f32[256,512]{1,0:T(8,128)}, u32[]{:S(2)}, u32[]{:S(2)}) collective-permute-start(f32[256,512]{1,0:T(8,128)} %dynamic-slice_bitcast_fusion), channel_id=1, source_target_pairs={{0,4},{4,0},{8,12},{12,8},{1,5},{5,1},{9,13},{13,9},{2,6},{6,2},{1... | collective-permute-start | bytes 1572872 | tf_op jit(solution)/shard_map/ppermute | solution.py:514
  627.8 37.4 %collective-permute-start.61 = (bf16[128,512]{1,0:T(8,128)(2,1)}, bf16[128,512]{1,0:T(8,128)(2,1)}, u32[]{:S(2)}, u32[]{:S(2)}) collective-permute-start(bf16[128,512]{1,0:T(8,128)(2,1)} %get-tuple-element.100), channel_id=1, source_target_pairs={{0,8},{4,12},{8,0},{12,4},{1,9},{5,13},{9,1},{13,5},{2,10},{6,14},... | collective-permute-start | bytes 393224 | tf_op jit(solution)/shard_map/ppermute | solution.py:514
  628.9 43.8 %collective-permute-start.60 = (bf16[128,512]{1,0:T(8,128)(2,1)}, bf16[128,512]{1,0:T(8,128)(2,1)}, u32[]{:S(2)}, u32[]{:S(2)}) collective-permute-start(bf16[128,512]{1,0:T(8,128)(2,1)} %get-tuple-element.101), channel_id=1, source_target_pairs={{0,8},{4,12},{8,0},{12,4},{1,9},{5,13},{9,1},{13,5},{2,10},{6,14},... | collective-permute-start | bytes 393224 | tf_op jit(solution)/shard_map/ppermute | solution.py:514
  665.3 14.2 %collective-permute-start.59 = (bf16[128,512]{1,0:T(8,128)(2,1)S(1)}, bf16[128,512]{1,0:T(8,128)(2,1)S(1)}, u32[]{:S(2)}, u32[]{:S(2)}) collective-permute-start(bf16[128,512]{1,0:T(8,128)(2,1)S(1)} %copy-done.108), channel_id=1, source_target_pairs={{0,8},{4,12},{8,0},{12,4},{1,9},{5,13},{9,1},{13,5},{2,10},{6,14},... | collective-permute-start | bytes 393224 | tf_op jit(solution)/shard_map/ppermute | solution.py:514
  668.6 13.2 %collective-permute-start.53 = (bf16[512,384]{1,0:T(8,128)(2,1)S(1)}, bf16[512,384]{1,0:T(8,128)(2,1)S(1)}, u32[]{:S(2)}, u32[]{:S(2)}) collective-permute-start(bf16[512,384]{1,0:T(8,128)(2,1)S(1)} %get-tuple-element.86), channel_id=1, source_target_pairs={{0,8},{4,12},{8,0},{12,4},{1,9},{5,13},{9,1},{13,5},{2,10},{6,14},... | collective-permute-start | bytes 1179656 | tf_op jit(solution)/shard_map/ppermute | solution.py:514
  679.2 15.2 %collective-permute-start.81 = (f32[512,256]{1,0:T(8,128)S(1)}, f32[512,256]{1,0:T(8,128)S(1)}, u32[]{:S(2)}, u32[]{:S(2)}) collective-permute-start(f32[512,256]{1,0:T(8,128)S(1)} %slice_select_fusion), channel_id=1, source_target_pairs={{0,4},{4,0},{8,12},{12,8},{1,5},{5,1},{9,13},{13,9},{2,6},{6,2},{1... | collective-permute-start | bytes 1572872 | tf_op jit(solution)/shard_map/ppermute | solution.py:514
  681.7 21.2 %collective-permute-start.48 = (bf16[512,1024]{1,0:T(8,128)(2,1)S(1)}, bf16[512,1024]{1,0:T(8,128)(2,1)S(1)}, u32[]{:S(2)}, u32[]{:S(2)}) collective-permute-start(bf16[512,1024]{1,0:T(8,128)(2,1)S(1)} %slice.570), channel_id=1, source_target_pairs={{0,4},{4,0},{8,12},{12,8},{1,5},{5,1},{9,13},{13,9},{2,6},{6,2},{1... | collective-permute-start | bytes 3145736 | tf_op jit(solution)/shard_map/ppermute | solution.py:514
  694.5 30.4 %collective-permute-start.50 = (bf16[512,384]{1,0:T(8,128)(2,1)S(1)}, bf16[512,384]{1,0:T(8,128)(2,1)}, u32[]{:S(2)}, u32[]{:S(2)}) collective-permute-start(bf16[512,384]{1,0:T(8,128)(2,1)S(1)} %get-tuple-element.85), channel_id=1, source_target_pairs={{0,8},{4,12},{8,0},{12,4},{1,9},{5,13},{9,1},{13,5},{2,10},{6,14},... | collective-permute-start | bytes 1179656 | tf_op jit(solution)/shard_map/ppermute | solution.py:514
  698.2 18.1 %collective-permute-start.51 = (bf16[512,384]{1,0:T(8,128)(2,1)}, bf16[512,384]{1,0:T(8,128)(2,1)}, u32[]{:S(2)}, u32[]{:S(2)}) collective-permute-start(bf16[512,384]{1,0:T(8,128)(2,1)} %get-tuple-element.88), channel_id=1, source_target_pairs={{0,8},{4,12},{8,0},{12,4},{1,9},{5,13},{9,1},{13,5},{2,10},{6,14},... | collective-permute-start | bytes 1179656 | tf_op jit(solution)/shard_map/ppermute | solution.py:514
  702.0 21.8 %collective-permute-start.65 = (f32[128,256]{1,0:T(8,128)}, f32[128,256]{1,0:T(8,128)}, u32[]{:S(2)}, u32[]{:S(2)}) collective-permute-start(f32[128,256]{1,0:T(8,128)} %slice_select_fusion.2), channel_id=1, source_target_pairs={{0,4},{4,0},{8,12},{12,8},{1,5},{5,1},{9,13},{13,9},{2,6},{6,2},{1... | collective-permute-start | bytes 393224 | tf_op jit(solution)/shard_map/ppermute | solution.py:514
  702.9 14.0 %collective-permute-start.55 = (bf16[512,384]{1,0:T(8,128)(2,1)}, bf16[512,384]{1,0:T(8,128)(2,1)}, u32[]{:S(2)}, u32[]{:S(2)}) collective-permute-start(bf16[512,384]{1,0:T(8,128)(2,1)} %fusion.71), channel_id=1, source_target_pairs={{0,3},{1,0},{2,1},{3,2},{4,7},{5,4},{6,5},{7,6},{8,11},{9,8},{10,9... | collective-permute-start | bytes 1179656 | tf_op jit(solution)/shard_map/ppermute | solution.py:519
  710.4 33.5 %all-to-all-start.3 = ((bf16[4,128,1024]{2,1,0:T(8,128)(2,1)}), bf16[4,128,1024]{2,1,0:T(8,128)(2,1)S(1)}, u32[]{:S(2)}, u32[]{:S(2)}) async-start(bf16[4,128,1024]{2,1,0:T(8,128)(2,1)} %bitcast.31), calls=%async_computation.3 | async-start | bytes 2097152 | tf_op jit(solution)/shard_map/all_to_all | solution.py:602
  713.9 91.8 %reduce-scatter.4.cloned.1.call-start = ((), (), s32[]{:S(2)}) async-start(), calls=%async_computation.5 | async-start | bytes 557056
  718.4 23.8 %collective-permute-start.56 = (bf16[512,384]{1,0:T(8,128)(2,1)S(1)}, bf16[512,384]{1,0:T(8,128)(2,1)S(1)}, u32[]{:S(2)}, u32[]{:S(2)}) collective-permute-start(bf16[512,384]{1,0:T(8,128)(2,1)S(1)} %fusion.73), channel_id=1, source_target_pairs={{0,3},{1,0},{2,1},{3,2},{4,7},{5,4},{6,5},{7,6},{8,11},{9,8},{10,9... | collective-permute-start | bytes 1179656 | tf_op jit(solution)/shard_map/ppermute | solution.py:519
  743.8 63.5 %collective-permute-start.57 = (f32[256,384]{0,1:T(8,128)S(1)}, f32[256,384]{0,1:T(8,128)S(1)}, u32[]{:S(2)}, u32[]{:S(2)}) collective-permute-start(f32[256,384]{0,1:T(8,128)S(1)} %bitcast.180), channel_id=1, source_target_pairs={{0,4},{4,0},{8,12},{12,8},{1,5},{5,1},{9,13},{13,9},{2,6},{6,2},{1... | collective-permute-start | bytes 1179656 | tf_op jit(solution)/shard_map/ppermute | solution.py:514
  744.7 66.0 %collective-permute-start.49 = (bf16[2,128,1024]{2,1,0:T(8,128)(2,1)}, bf16[2,128,1024]{2,1,0:T(8,128)(2,1)}, u32[]{:S(2)}, u32[]{:S(2)}) collective-permute-start(bf16[2,128,1024]{2,1,0:T(8,128)(2,1)} %dynamic-slice_bitcast_fusion.1), channel_id=1, source_target_pairs={{0,4},{4,0},{8,12},{12,8},{1,5},{5,1},{9,13},{13,9},{2,6},{6,2},{1... | collective-permute-start | bytes 1572872 | tf_op jit(solution)/shard_map/ppermute | solution.py:514
  (166 other events, 2792.6 us)
Sparse Core Ops, SparseCore 0:
  746.4 59.2 reduce-scatter.3

commit v2 on v0

--- a/solution.py
+++ b/solution.py
@@ -1,12 +1,20 @@
+import functools
+import math
+
 import jax
 import jax.numpy as jnp
 from jax import lax
+from jax.experimental import pallas as pl
+from jax.experimental.pallas import tpu as pltpu
 from jax.sharding import PartitionSpec as P
 
 HEAD_DIM = 64
 
 
 NORM_EPSILON = 1e-06
+TILE = 128
+CHUNK = 32
+KERNEL_VMEM = 40 << 20
 
 
 def shifted(block, axis, distance):
@@ -308,6 +316,669 @@
     )
 
 
+def rotated(block, cos_rows, sin_rows):
+    lane = lax.broadcasted_iota(jnp.int32, block.shape, 1)
+    ahead = pltpu.roll(block, 96, 1)
+    behind = pltpu.roll(block, 32, 1)
+    swapped = jnp.where(lane % 64 < 32, ahead, behind)
+    return block * cos_rows + swapped * sin_rows
+
+
+def dot_nt(left, right):
+    return lax.dot_general(
+        left, right, (((1,), (1,)), ((), ())), preferred_element_type=jnp.float32
+    )
+
+
+def dot_nn(left, right):
+    return jnp.dot(left, right, preferred_element_type=jnp.float32)
+
+
+def side_by_side(refs):
+    return jnp.concatenate([ref[...] for ref in refs], axis=1)
+
+
+def stacked_up(refs):
+    return jnp.concatenate([ref[...] for ref in refs], axis=0)
+
+
+def edge_masks(core, rows):
+    key = lax.broadcasted_iota(jnp.int32, (rows, 2 * rows), 0)
+    query = lax.broadcasted_iota(jnp.int32, (rows, 2 * rows), 1)
+    mine = query < rows
+    place = jnp.where(mine, query + core * rows, query - rows + (1 - core) * rows)
+    return (key + core * rows <= place, key + (1 - core) * rows <= place)
+
+
+def both_sides(value, half, start, stop, axis=0):
+    if axis == 0:
+        return jnp.concatenate([value[start:stop], value[half + start : half + stop]], axis=0)
+    return jnp.concatenate([value[:, start:stop], value[:, half + start : half + stop]], axis=1)
+
+
+def hidden_scores(scores, masks, tile, step):
+    seen = step * tile
+    pieces = []
+    for side in range(2):
+        base = side * (seen + tile)
+        if seen:
+            pieces.append(scores[base : base + seen])
+        pieces.append(jnp.where(masks[side], scores[base + seen : base + seen + tile], -1e30))
+    return jnp.concatenate(pieces, axis=0)
+
+
+def one_head(rows, head):
+    lane = lax.broadcasted_iota(jnp.int32, rows.shape, 1)
+    return jnp.where(lane // 64 == head, rows, jnp.zeros_like(rows))
+
+
+def pick_piece(weight, owns, others, axis):
+    for j, (own, other) in enumerate(zip(owns, others)):
+
+        @pl.when(pl.program_id(0) == j)
+        def _():
+            size = own.shape[axis]
+            if axis == 0:
+                weight[:size] = own[...]
+                weight[size:] = other[...]
+            else:
+                weight[:, :size] = own[...]
+                weight[:, size:] = other[...]
+
+
+def attend_kernel(pieces, core_ref, cos_ref, sin_ref, own_rows, other_rows, *refs):
+    owns, others = refs[:pieces], refs[pieces : 2 * pieces]
+    q_ref, k_ref, v_ref, lse_ref, mix_ref, weight = refs[2 * pieces :]
+    half = own_rows.shape[0]
+    tile = TILE
+    pick_piece(weight, owns, others, 0)
+    proj = dot_nn(stacked_up([own_rows, other_rows]), weight[...])
+    cos_rows, sin_rows = cos_ref[...], sin_ref[...]
+    q = (rotated(proj[:, :128], cos_rows, sin_rows) * HEAD_DIM ** (-0.5)).astype(jnp.bfloat16)
+    k = rotated(proj[:, 128:256], cos_rows, sin_rows).astype(jnp.bfloat16)
+    v32 = proj[:, 256:]
+    q_ref[0] = q
+    k_ref[0] = k
+    v_ref[0] = v32.astype(jnp.bfloat16)
+    v_flip = v32.T.astype(jnp.bfloat16)
+    masks = edge_masks(core_ref[0], tile)
+
+    def scored(step, head):
+        stop = (step + 1) * tile
+        q_head = one_head(both_sides(q, half, step * tile, stop), head)
+        return hidden_scores(dot_nt(both_sides(k, half, 0, stop), q_head), masks, tile, step)
+
+    units = [(step, head) for step in range(half // tile) for head in range(2)]
+    ahead = scored(*units[0])
+    outs = []
+    for spot, (step, head) in enumerate(units):
+        scores = ahead
+        if spot + 1 < len(units):
+            ahead = scored(*units[spot + 1])
+        stop = (step + 1) * tile
+        top = jnp.max(scores, axis=0, keepdims=True)
+        expos = jnp.exp(scores - top)
+        total = jnp.sum(expos, axis=0, keepdims=True)
+        lse = top + jnp.log(total)
+        lse_ref[0, head : head + 1, step * tile : stop] = lse[:, :tile]
+        lse_ref[0, head : head + 1, half + step * tile : half + stop] = lse[:, tile:]
+        v_cols = both_sides(v_flip, half, 0, stop, axis=1)
+        out = dot_nn(v_cols[64 * head : 64 * head + 64], expos.astype(jnp.bfloat16))
+        outs.append(out * (1.0 / total))
+        if head == 1:
+            mixed = jnp.concatenate(outs, axis=0).T.astype(jnp.bfloat16)
+            outs = []
+            mix_ref[step * tile : stop, :] = mixed[:tile]
+            mix_ref[half + step * tile : half + stop, :] = mixed[tile:]
+
+
+def attend_back_kernel(pieces, core_ref, cos_ref, sin_ref, own_rows, other_rows, *refs):
+    owns, others = refs[:pieces], refs[pieces : 2 * pieces]
+    q_ref, k_ref, v_ref, lse_ref, out_ref, weight, dq, dk, dv = refs[2 * pieces :]
+    half = own_rows.shape[0]
+    tile = TILE
+    pick_piece(weight, owns, others, 1)
+    d_mixed = dot_nt(stacked_up([own_rows, other_rows]), weight[...]).astype(jnp.bfloat16)
+    q, k, v = q_ref[0], k_ref[0], v_ref[0]
+    k_flip = k.astype(jnp.float32).T.astype(jnp.bfloat16)
+    masks = edge_masks(core_ref[0], tile)
+    steps = half // tile
+
+    def scored(step, head):
+        stop = (step + 1) * tile
+        q_head = one_head(both_sides(q, half, step * tile, stop), head)
+        g_head = one_head(both_sides(d_mixed, half, step * tile, stop), head)
+        scores = hidden_scores(dot_nt(both_sides(k, half, 0, stop), q_head), masks, tile, step)
+        return q_head, g_head, scores, dot_nt(both_sides(v, half, 0, stop), g_head)
+
+    units = [(step, head) for step in reversed(range(steps)) for head in range(2)]
+    ahead = scored(*units[0])
+    dq_flips = []
+    dk_sum = dv_sum = None
+    for spot, (step, head) in enumerate(units):
+        q_head, g_head, scores, d_probs = ahead
+        if spot + 1 < len(units):
+            ahead = scored(*units[spot + 1])
+        stop = (step + 1) * tile
+        lse = both_sides(lse_ref[0], half, step * tile, stop, axis=1)
+        probs = jnp.exp(scores - lse[head : head + 1])
+        dots = jnp.sum(probs * d_probs, axis=0, keepdims=True)
+        d_scores = (probs * (d_probs - dots)).astype(jnp.bfloat16)
+        dv_part = dot_nn(probs.astype(jnp.bfloat16), g_head)
+        dk_part = dot_nn(d_scores, q_head)
+        k_cols = both_sides(k_flip, half, 0, stop, axis=1)
+        dq_flips.append(dot_nn(k_cols[64 * head : 64 * head + 64], d_scores))
+        if head == 0:
+            dv_sum, dk_sum = dv_part, dk_part
+            continue
+        dv_sum, dk_sum = dv_sum + dv_part, dk_sum + dk_part
+        dq_rows = jnp.concatenate(dq_flips, axis=0).T * HEAD_DIM ** (-0.5)
+        dq_flips = []
+        dq[step * tile : stop] = dq_rows[:tile]
+        dq[half + step * tile : half + stop] = dq_rows[tile:]
+        for base, part in ((0, slice(0, stop)), (half, slice(stop, 2 * stop))):
+            if step == steps - 1:
+                dk[base : base + stop] = dk_sum[part]
+                dv[base : base + stop] = dv_sum[part]
+            else:
+                dk[base : base + stop] += dk_sum[part]
+                dv[base : base + stop] += dv_sum[part]
+    cos_rows, sin_rows = cos_ref[...], -sin_ref[...]
+    out_ref[:, :128] = rotated(dq[...], cos_rows, sin_rows).astype(jnp.bfloat16)
+    out_ref[:, 128:256] = rotated(dk[...], cos_rows, sin_rows).astype(jnp.bfloat16)
+    out_ref[:, 256:] = dv[...].astype(jnp.bfloat16)
+
+
+def split_rows(total, own_ref, other_ref):
+    half = own_ref.shape[0]
+    own_ref[...] = total[:half]
+    other_ref[...] = total[half:].astype(jnp.bfloat16)
+
+
+def into_model_kernel(pieces, left_ref, *refs):
+    owns, others = refs[:pieces], refs[pieces : 2 * pieces]
+    weight = jnp.concatenate([stacked_up(owns), stacked_up(others)], axis=1)
+    split_rows(dot_nn(left_ref[...], weight), *refs[2 * pieces :])
+
+
+def back_to_model_kernel(pieces, left_ref, *refs):
+    owns, others = refs[:pieces], refs[pieces : 2 * pieces]
+    weight = jnp.concatenate([side_by_side(owns), side_by_side(others)], axis=0)
+    split_rows(dot_nt(left_ref[...], weight), *refs[2 * pieces :])
+
+
+def gelu_both(up_act):
+    root = math.sqrt(2.0 / math.pi)
+    square = up_act * up_act
+    rise = 0.5 + 0.5 * jnp.tanh(up_act * (root + root * 0.044715 * square))
+    value = up_act * rise
+    slope = rise + value * (1.0 - rise) * (2.0 * root + 6.0 * root * 0.044715 * square)
+    return value, slope
+
+
+def mlp_up_kernel(pieces, own_rows, other_rows, *refs):
+    owns, others = refs[:pieces], refs[pieces : 2 * pieces]
+    gelu_ref, slope_ref = refs[2 * pieces :]
+    half = own_rows.shape[0]
+    size = owns[0].shape[1]
+    step = half // 2
+    units = [(j, i) for j in range(pieces) for i in range(4)]
+
+    def product(j, i):
+        rows = (own_rows, other_rows)[i // 2][i % 2 * step : (i % 2 + 1) * step]
+        return dot_nn(rows, stacked_up([owns[j], others[j]]))
+
+    ahead = product(*units[0])
+    for spot, (j, i) in enumerate(units):
+        up_act = ahead
+        if spot + 1 < len(units):
+            ahead = product(*units[spot + 1])
+        value, slope = gelu_both(up_act)
+        gelu_ref[i * step : (i + 1) * step, j * size : (j + 1) * size] = value.astype(jnp.bfloat16)
+        slope_ref[i * step : (i + 1) * step, j * size : (j + 1) * size] = slope.astype(
+            jnp.bfloat16
+        )
+
+
+def mlp_up_back_kernel(pieces, own_rows, other_rows, slope_ref, *refs):
+    owns, others = refs[:pieces], refs[pieces : 2 * pieces]
+    out_ref = refs[-1]
+    size = owns[0].shape[0]
+    rows = stacked_up([own_rows, other_rows])
+    for j in range(pieces):
+        cols = slice(j * size, (j + 1) * size)
+        d_gelu = dot_nt(rows, side_by_side([owns[j], others[j]]))
+        out_ref[:, cols] = (d_gelu * slope_ref[:, cols].astype(jnp.float32)).astype(jnp.bfloat16)
+
+
+def inverse_size(rows):
+    return lax.rsqrt(jnp.mean(rows * rows, axis=-1, keepdims=True) + NORM_EPSILON)
+
+
+def norm_back(rows, gain, grad):
+    scale = inverse_size(rows)
+    weighted = grad * gain
+    inner = jnp.mean(rows * weighted, axis=-1, keepdims=True)
+    return scale * weighted - rows * (scale * scale * scale * inner), rows * scale * grad
+
+
+def folded(rows):
+    return jnp.sum(rows.reshape(rows.shape[0] // 8, 8, rows.shape[1]), axis=0)
+
+
+def wide(ref, spot):
+    return ref[spot, :].astype(jnp.float32)
+
+
+def by_chunks(count, body, sums=0, width=0):
+    def one(i, carry):
+        more = body(pl.ds(pl.multiple_of(i * CHUNK, CHUNK), CHUNK))
+        return tuple(old + folded(new) for old, new in zip(carry, more))
+
+    start = tuple(jnp.zeros((8, width), jnp.float32) for _ in range(sums))
+    totals = lax.fori_loop(0, count // CHUNK, one, start)
+    return [jnp.sum(total, axis=0, keepdims=True) for total in totals]
+
+
+def norm_in_kernel(gain_ref, rows_ref, out_ref):
+    def body(spot):
+        rows = wide(rows_ref, spot)
+        out_ref[spot, :] = (rows * inverse_size(rows) * gain_ref[0:1]).astype(jnp.bfloat16)
+        return ()
+
+    by_chunks(rows_ref.shape[0], body)
+
+
+def after_attention_kernel(
+    gain_ref, rows_ref, own_ref, other_ref, branch_ref, hidden_ref, out_ref
+):
+    def body(spot):
+        branch = own_ref[spot, :] + wide(other_ref, spot)
+        hidden = wide(rows_ref, spot) + branch * inverse_size(branch) * gain_ref[1:2]
+        branch_ref[spot, :] = branch
+        hidden_ref[spot, :] = hidden
+        out_ref[spot, :] = (hidden * inverse_size(hidden) * gain_ref[2:3]).astype(jnp.bfloat16)
+        return ()
+
+    by_chunks(rows_ref.shape[0], body)
+
+
+def after_mlp_kernel(gain_ref, hidden_ref, own_ref, other_ref, branch_ref, out_ref):
+    def body(spot):
+        branch = own_ref[spot, :] + wide(other_ref, spot)
+        branch_ref[spot, :] = branch
+        result = hidden_ref[spot, :] + branch * inverse_size(branch) * gain_ref[3:4]
+        out_ref[spot, :] = result.astype(jnp.bfloat16)
+        return ()
+
+    by_chunks(hidden_ref.shape[0], body)
+
+
+def into_mlp_back_kernel(gain_ref, grad_ref, branch_ref, out_ref, sum_ref):
+    def body(spot):
+        d_rows, d_gain = norm_back(branch_ref[spot, :], gain_ref[3:4], wide(grad_ref, spot))
+        out_ref[spot, :] = d_rows.astype(jnp.bfloat16)
+        return (d_gain,)
+
+    (sum_ref[...],) = by_chunks(grad_ref.shape[0], body, 1, grad_ref.shape[1])
+
+
+def into_attention_back_kernel(
+    gain_ref, grad_ref, own_ref, other_ref, hidden_ref, branch_ref, d_hidden_ref, out_ref, *sums
+):
+    def body(spot):
+        d_rows = own_ref[spot, :] + wide(other_ref, spot)
+        d_rows, d_gain = norm_back(hidden_ref[spot, :], gain_ref[2:3], d_rows)
+        d_hidden = wide(grad_ref, spot) + d_rows
+        d_hidden_ref[spot, :] = d_hidden
+        d_rows, d_first = norm_back(branch_ref[spot, :], gain_ref[1:2], d_hidden)
+        out_ref[spot, :] = d_rows.astype(jnp.bfloat16)
+        return (d_first, d_gain)
+
+    totals = by_chunks(grad_ref.shape[0], body, 2, grad_ref.shape[1])
+    sums[0][...], sums[1][...] = totals
+
+
+def out_of_layer_kernel(gain_ref, rows_ref, own_ref, other_ref, d_hidden_ref, out_ref, sum_ref):
+    def body(spot):
+        d_rows = own_ref[spot, :] + wide(other_ref, spot)
+        d_rows, d_gain = norm_back(wide(rows_ref, spot), gain_ref[0:1], d_rows)
+        out_ref[spot, :] = (d_hidden_ref[spot, :] + d_rows).astype(jnp.bfloat16)
+        return (d_gain,)
+
+    (sum_ref[...],) = by_chunks(rows_ref.shape[0], body, 1, rows_ref.shape[1])
+
+
+def on_chip(kernel, name, outs, *operands):
+    space = pl.BlockSpec(memory_space=pltpu.VMEM)
+    return pl.pallas_call(
+        kernel,
+        in_specs=[space] * len(operands),
+        out_specs=[space] * len(outs),
+        out_shape=[jax.ShapeDtypeStruct(shape, dtype) for shape, dtype in outs],
+        compiler_params=pltpu.CompilerParams(vmem_limit_bytes=KERNEL_VMEM),
+        name=name,
+    )(*operands)
+
+
+def whole_block(array):
+    return pl.BlockSpec(array.shape, lambda j: (0,) * array.ndim)
+
+
+def by_pairs(kernel, name, core, operands, pieces, blocks, outs, scratch):
+    return pl.pallas_call(
+        functools.partial(kernel, len(pieces[0])),
+        grid=(len(pieces[0]),),
+        in_specs=[pl.BlockSpec(memory_space=pltpu.SMEM)]
+        + [whole_block(array) for array in (*operands, *pieces[0], *pieces[1])]
+        + [spec for _, spec in blocks],
+        out_specs=[spec for _, _, spec in outs],
+        out_shape=[jax.ShapeDtypeStruct(shape, dtype) for shape, dtype, _ in outs],
+        scratch_shapes=scratch,
+        compiler_params=pltpu.CompilerParams(vmem_limit_bytes=KERNEL_VMEM),
+        name=name,
+    )(core, *operands, *pieces[0], *pieces[1], *[array for array, _ in blocks])
+
+
+def attend(core, tables, rows, pieces):
+    half, features = rows[0].shape
+    length, count = 2 * half, len(pieces[0])
+    lanes = ((count, length, 128), jnp.bfloat16, pl.BlockSpec((1, length, 128), lambda j: (j, 0, 0)))
+    lse = ((count, 2, length), jnp.float32, pl.BlockSpec((1, 2, length), lambda j: (j, 0, 0)))
+    mixed = ((length, count * 128), jnp.bfloat16, pl.BlockSpec((length, 128), lambda j: (0, j)))
+    return by_pairs(
+        attend_kernel,
+        "attend",
+        core,
+        (*tables, *rows),
+        pieces,
+        (),
+        (lanes, lanes, lanes, lse, mixed),
+        [pltpu.VMEM((features, 384), jnp.bfloat16)],
+    )
+
+
+def attend_back(core, tables, rows, pieces, q, k, v, lse):
+    half, features = rows[0].shape
+    length, count = 2 * half, len(pieces[0])
+    lanes = pl.BlockSpec((1, length, 128), lambda j: (j, 0, 0))
+    lse_spec = pl.BlockSpec((1, 2, length), lambda j: (j, 0, 0))
+    out = ((length, count * 384), jnp.bfloat16, pl.BlockSpec((length, 384), lambda j: (0, j)))
+    return by_pairs(
+        attend_back_kernel,
+        "attend_back",
+        core,
+        (*tables, *rows),
+        pieces,
+        ((q, lanes), (k, lanes), (v, lanes), (lse, lse_spec)),
+        (out,),
+        [pltpu.VMEM((128, features), jnp.bfloat16)] + [pltpu.VMEM((length, 128), jnp.float32)] * 3,
+    )[0]
+
+
+def model_rows(kernel, name, left, pieces):
+    owns, others = pieces
+    length, width = left.shape[0], 2 * owns[0].shape[kernel is into_model_kernel]
+    outs = (((length // 2, width), jnp.float32), ((length // 2, width), jnp.bfloat16))
+    kernel = functools.partial(kernel, len(owns))
+    own, other = on_chip(kernel, name, outs, left, *owns, *others)
+    return own, flip_pairs(other, 1)
+
+
+def flip_pairs(block, distance):
+    size = lax.axis_size("dp")
+    return lax.ppermute(block, "dp", [(i, i ^ distance) for i in range(size)])
+
+
+def passed_on(block, step):
+    size = lax.axis_size("tensor")
+    return lax.ppermute(block, "tensor", [(i, (i + step) % size) for i in range(size)])
+
+
+def spread(piece):
+    pieces = [piece]
+    for _ in range(lax.axis_size("tensor") - 1):
+        pieces.append(passed_on(pieces[-1], 1))
+    return pieces
+
+
+def collected(pieces):
+    total = pieces[-1]
+    for piece in reversed(pieces[:-1]):
+        total = piece + passed_on(total.astype(jnp.bfloat16), -1).astype(jnp.float32)
+    return total
+
+
+def summed_everywhere(value):
+    for distance in (1, 2):
+        value = value + flip_pairs(value, distance)
+    size = lax.axis_size("tensor")
+    for distance in (1, 2):
+        value = value + lax.ppermute(value, "tensor", [(i, i ^ distance) for i in range(size)])
+    return value
+
+
+def after(values, token):
+    return lax.optimization_barrier((values, token))[0]
+
+
+def per_chip(
+    inputs,
+    out_cotangent,
+    group_ids,
+    group_weights,
+    gains,
+    qkv_weight,
+    out_weight,
+    up_weight,
+    down_weight,
+):
+    micro, row_count, width = inputs.shape
+    tensor = lax.axis_size("tensor")
+    part = row_count // 2
+    wide_half = width // 2
+    length = tensor * row_count
+    half = length // 2
+    first = lax.axis_index("section") == 0
+    place = lax.axis_index("dp")
+    core = place % 2
+    upper = place // 2 % 2
+    core_zero = core == 0
+    low_half = upper == 0
+
+    def ordered(mine, other):
+        return jnp.where(core_zero, mine, other), jnp.where(core_zero, other, mine)
+
+    def own_first(values):
+        return jnp.where(low_half, values, jnp.roll(values, wide_half, axis=-1))
+
+    def both_rows(own):
+        return own, flip_pairs(own, 1)
+
+    def to_chip(block):
+        split = block.reshape((micro, 2, part) + block.shape[2:])
+        mine = lax.dynamic_index_in_dim(split, core, 1, keepdims=False)
+        other = lax.dynamic_index_in_dim(split, 1 - core, 1, keepdims=False)
+        return lax.all_to_all(
+            jnp.concatenate(ordered(mine, flip_pairs(other, 1))), "tensor", 0, 0, tiled=True
+        )
+
+    def from_chip(block):
+        spread_out = lax.all_to_all(block, "tensor", 0, 0, tiled=True)
+        grouped = spread_out.reshape((2, micro, part) + block.shape[2:])
+        mine = lax.dynamic_index_in_dim(grouped, core, 0, keepdims=False)
+        other = lax.dynamic_index_in_dim(grouped, 1 - core, 0, keepdims=False)
+        pair = ordered(mine, flip_pairs(other, 1))
+        return jnp.stack(pair, axis=1).reshape((micro, row_count) + block.shape[2:])
+
+    group_count = group_weights.shape[0]
+    matches = group_ids[..., None] == jnp.arange(group_count, dtype=jnp.int32)
+    row_scale = jnp.sum(jnp.where(matches, group_weights, 0.0), axis=-1)
+    weighted = (out_cotangent.astype(jnp.float32) * row_scale[..., None]).astype(jnp.bfloat16)
+    start = to_chip(own_first(jnp.where(first, inputs, weighted))).reshape(half, width)
+
+    def columns(local):
+        size = local.shape[-1] // 2
+        mid = (0,) * (local.ndim - 2)
+        piece = lax.dynamic_slice(
+            local, (wide_half * upper, *mid, size * core), (wide_half, *local.shape[1:-1], size)
+        )
+        pieces = spread(piece.reshape(wide_half, -1))
+        return pieces, [flip_pairs(piece, 2) for piece in pieces]
+
+    def rows(local):
+        size = local.shape[0] // 2
+        pieces = spread(
+            lax.dynamic_slice(local, (size * core, wide_half * upper), (size, wide_half))
+        )
+        return pieces, [flip_pairs(piece, 2) for piece in pieces]
+
+    w_qkv = columns(qkv_weight[0])
+    w_out = rows(out_weight[0])
+    w_up = columns(up_weight[0])
+    w_down = rows(down_weight[0])
+    gain = own_first(gains[0])
+
+    turns = jnp.arange(half, dtype=jnp.int32)
+    turns = turns // part * row_count + turns % part
+    positions = jnp.concatenate([turns + core * part, turns + (1 - core) * part])
+    freqs = 10000.0 ** (-2.0 * jnp.arange(HEAD_DIM // 2, dtype=jnp.float32) / HEAD_DIM)
+    angles = positions.astype(jnp.float32)[:, None] * freqs[None, :]
+    cos_part, sin_part = jnp.cos(angles), jnp.sin(angles)
+    tables = (
+        jnp.concatenate([cos_part] * 4, axis=1),
+        jnp.concatenate([-sin_part, sin_part] * 2, axis=1),
+    )
+    core_word = core.astype(jnp.int32).reshape(1)
+    units = tensor * w_up[0][0].shape[1]
+    row32, row16 = ((half, width), jnp.float32), ((half, width), jnp.bfloat16)
+    unit16 = ((length, units), jnp.bfloat16)
+    sum32 = ((1, width), jnp.float32)
+
+    def forward(layer_input):
+        attn_in = both_rows(on_chip(norm_in_kernel, "norm_in", (row16,), gain, layer_input)[0])
+        *heads, mixed = attend(core_word, tables, attn_in, w_qkv)
+        parts = model_rows(into_model_kernel, "attn_out", mixed, w_out)
+        branch, hidden, mlp_in = on_chip(
+            after_attention_kernel, "after_attn", (row32, row32, row16), gain, layer_input, *parts
+        )
+        mlp_in = both_rows(mlp_in)
+        kernel = functools.partial(mlp_up_kernel, tensor)
+        gelu_out, slope = on_chip(
+            kernel, "mlp_up", (unit16, unit16), *mlp_in, *w_up[0], *w_up[1]
+        )
+        parts = model_rows(into_model_kernel, "mlp_down", gelu_out, w_down)
+        mlp_branch, result = on_chip(
+            after_mlp_kernel, "after_mlp", (row32, row16), gain, hidden, *parts
+        )
+        saved = (layer_input, heads, branch, hidden, slope, mlp_branch)
+        return result, saved, (attn_in, mixed, mlp_in, gelu_out)
+
+    def backward(grad, saved):
+        layer_input, heads, branch, hidden, slope, mlp_branch = saved
+        d_down, sum_three = on_chip(
+            into_mlp_back_kernel, "into_mlp_back", (row16, sum32), gain, grad, mlp_branch
+        )
+        d_down = both_rows(d_down)
+        kernel = functools.partial(mlp_up_back_kernel, tensor)
+        d_up = on_chip(kernel, "mlp_up_back", (unit16,), *d_down, slope, *w_down[0], *w_down[1])[0]
+        parts = model_rows(back_to_model_kernel, "mlp_back", d_up, w_up)
+        d_hidden, d_attn, sum_one, sum_two = on_chip(
+            into_attention_back_kernel,
+            "into_attn_back",
+            (row32, row16, sum32, sum32),
+            gain,
+            grad,
+            *parts,
+            hidden,
+            branch,
+        )
+        d_attn = both_rows(d_attn)
+        d_qkv = attend_back(core_word, tables, d_attn, w_out, *heads)
+        parts = model_rows(back_to_model_kernel, "attn_back", d_qkv, w_qkv)
+        d_input, sum_zero = on_chip(
+            out_of_layer_kernel, "out_of_layer", (row16, sum32), gain, layer_input, *parts, d_hidden
+        )
+        sums = jnp.concatenate([sum_zero, sum_one, sum_two, sum_three])
+        return d_input, (d_qkv, d_attn, d_up, d_down), sums
+
+    low_zero, saved_zero, lefts_zero = forward(start)
+    low_one, saved_one, lefts_one = forward(shifted(low_zero, "section", 1))
+    grad_one, rights_one, gain_one = backward(start, saved_one)
+    lows = after((low_zero, low_one), grad_one)
+    outputs = from_chip(own_first(jnp.where(first, *lows)).reshape(tensor, part, width))
+    grad_zero, rights_zero, gain_zero = backward(shifted(grad_one, "section", -1), saved_zero)
+    grads = from_chip(own_first(jnp.where(first, grad_zero, grad_one)).reshape(tensor, part, width))
+
+    def joined(pair):
+        return lax.optimization_barrier(jnp.concatenate(pair, axis=0))
+
+    def own_layer(zero, one):
+        if isinstance(zero, tuple):
+            zero, one = joined(zero), joined(one)
+        return jnp.where(first, zero, one)
+
+    attn_in, mixed, mlp_in, gelu_out = map(own_layer, lefts_zero, lefts_one)
+    d_qkv, d_attn, d_up, d_down = map(own_layer, rights_zero, rights_one)
+
+    def halves(total, axis):
+        own = lax.slice_in_dim(total, 0, wide_half, axis=axis)
+        other = lax.slice_in_dim(total, wide_half, width, axis=axis).astype(jnp.bfloat16)
+        return own + flip_pairs(other, 2).astype(jnp.float32)
+
+    def sum_columns(left, right):
+        size = right.shape[1] // tensor
+        pieces = [None] * tensor
+        for j in reversed(range(tensor)):
+            pieces[j] = halves(contract(left, right[:, j * size : (j + 1) * size]), 0)
+        return collected(pieces)
+
+    def sum_rows(left, right):
+        size = left.shape[1] // tensor
+        pieces = [None] * tensor
+        for j in reversed(range(tensor)):
+            pieces[j] = halves(contract(left[:, j * size : (j + 1) * size], right), 1)
+        return collected(pieces)
+
+    down_sum = sum_rows(gelu_out, d_down)
+    up_sum = sum_columns(mlp_in, d_up)
+    out_sum = sum_rows(mixed, d_attn)
+    qkv_sum = sum_columns(attn_in, d_qkv)
+
+    def by_columns(kept, count):
+        size = kept.shape[1]
+        kept = kept.reshape(2, wide_half // 2, size)
+        mine = lax.dynamic_index_in_dim(kept, core, 0, keepdims=False)
+        other = lax.dynamic_index_in_dim(kept, 1 - core, 0, keepdims=False)
+        pair = ordered(mine, flip_pairs(other, 1))
+        pair = [side.reshape(wide_half // 2, count, size // count) for side in pair]
+        return jnp.concatenate(pair, axis=2)
+
+    def by_rows(kept):
+        sides = (kept[:, : wide_half // 2], kept[:, wide_half // 2 :])
+        mine = jnp.where(core_zero, sides[0], sides[1])
+        other = jnp.where(core_zero, sides[1], sides[0])
+        return jnp.concatenate(ordered(mine, flip_pairs(other, 1)), axis=0)
+
+    gain_total = summed_everywhere(own_first(jnp.where(first, gain_zero, gain_one)))
+    size = width // (tensor * lax.axis_size("dp"))
+    spot = (place * tensor + lax.axis_index("tensor")) * size
+    gains_grad = lax.dynamic_slice_in_dim(gain_total, spot, size, axis=1)
+    return (
+        outputs[None],
+        grads[None],
+        gains_grad[None],
+        by_columns(qkv_sum, 3)[None],
+        by_rows(out_sum)[None],
+        by_columns(up_sum, 1)[:, 0][None],
+        by_rows(down_sum)[None],
+    )
+
+
+def takes_chips(sizes):
+    return sizes["section"] == 2 and sizes["dp"] == 4 and sizes["tensor"] == 4
+
+
 def solution(mesh):
     placed = (
         P("dp", "tensor", None),
@@ -320,8 +991,9 @@
         P("section", None, "tensor"),
         P("section", "tensor", None),
     )
+    body = per_chip if takes_chips(dict(mesh.shape)) else per_device
     return jax.shard_map(
-        per_device,
+        body,
         mesh=mesh,
         in_specs=placed,
         out_specs=(

time: 3010 us -> 722 us (0.24)
  waiting for transfers between devices: 2340 us -> 261 us
  matrix products: 391 us -> 25 us
  Pallas kernels: 0 us -> 188 us
  other arithmetic: 161 us -> 61.4 us
  starting transfers between devices: 39.9 us -> 112 us
    reduce_scatter x22 -> x0, waiting for transfers between devices: 1410 us -> none  [the longest x12 907 us: scatter_rows(): lax.psum_scatter(partial_term(jnp.int32(0), lax.axis_size('tensor') * row...]
    all_gather x18 -> x0, waiting for transfers between devices: 817 us -> none  [the longest x12 537 us: gather_rows(): lax.all_gather(row_values, 'tensor', axis=0, tiled=True)]
    dot_general x51 -> x0, matrix products: 265 us -> none  [the longest x12 62.4 us: partial_term(): return jnp.dot(row_values, weight, preferred_element_type=jnp.float32)]
    ppermute x0 -> x83, waiting for transfers between devices: none -> 214 us  [the longest x24 120 us: passed_on(): lax.ppermute(block, 'tensor', [(i, (i + step) % size) for i in range(size)])]
    pallas_call x0 -> x28, Pallas kernels: none -> 188 us  [the longest x24 106 us: on_chip(): pl.pallas_call(kernel, in_specs=[space] * len(operands), out_specs=[space...]
    ppermute x0 -> x83, starting transfers between devices: none -> 92 us  [the longest x24 45.3 us: passed_on(): lax.ppermute(block, 'tensor', [(i, (i + step) % size) for i in range(size)])]
    sub x6 -> x0, matrix products: 62.8 us -> none  [attention_probs(): expos = jnp.exp(scores - jnp.max(scores, axis=-1, keepdims=True))]
    convert_element_type x29 -> x13, other arithmetic: 64.9 us -> 10.7 us  [the longest x12 10.1 us: collected(): total.astype(jnp.bfloat16)]
  transfers between devices with their start and end apart: 47 -> 88, of which waited for: 47 -> 41; matrix products, arithmetic and copies ran while one was open for 3% -> 14% of each run, Pallas kernels for 0% -> 13%
where the time goes in v2:
time: 722 us; the launch traced here: 711 us
  waiting for transfers between devices  261 us (36%)
  Pallas kernels  188 us (26%)
  starting transfers between devices  112 us (16%)
  other arithmetic  61.4 us (9%)
  local copies, waits for them, and re-layouts  59.7 us (8%)
  matrix products  25 us (3%)
    ppermute x24, waiting for transfers between devices, passed_on(): lax.ppermute(block, 'tensor', [(i, (i + step) % size) for i in range(size)])  120 us
    pallas_call x24, Pallas kernels, on_chip(): pl.pallas_call(kernel, in_specs=[space] * len(operands), out_specs=[space...  106 us
    ppermute x57, waiting for transfers between devices, flip_pairs(): return lax.ppermute(block, 'dp', [(i, i ^ distance) for i in range(size)])  93.7 us
    pallas_call x4, Pallas kernels, by_pairs(): pl.pallas_call(functools.partial(kernel, len(pieces[0])), grid=(len(piece...  82.1 us
    ppermute x24, starting transfers between devices, passed_on(): lax.ppermute(block, 'tensor', [(i, (i + step) % size) for i in range(size)])  45.3 us
    ppermute x57, starting transfers between devices, flip_pairs(): return lax.ppermute(block, 'dp', [(i, i ^ distance) for i in range(size)])  40.7 us
    unnamed x308, local copies, waits for them, and re-layouts  38.7 us
    ppermute x2, waiting for transfers between devices, shifted(): return lax.ppermute(block, axis, route)  38.2 us
  transfers between devices with their start and end apart: 88, of which 41 were waited for; matrix products, arithmetic and copies ran while one was open for 14% of the time, Pallas kernels for 13%

profile of v2, /device:TPU:0, one launch (start us, length us, event | category | flops | bytes accessed | tf_op | source)
XLA Modules:
  0.0 710.8 jit_solution(3834912331770529531)
XLA Ops:
  11.4 6.2 all-to-all-start
  23.6 24.0 %collective-permute-done.2.refs_1_ = bf16[512,384]{1,0:T(8,128)(2,1)} collective-permute-done((bf16[512,384]{1,0:T(8,128)(2,1)S(1)}, bf16[512,384]{1,0:T(8,128)(2,1)}, u32[]{:S(2)}, u32[]{:S(2)}) %collective-permute-start.2) | collective-permute-done | bytes 393248 | tf_op jit(solution)/shard_map/ppermute | solution.py:735
  47.6 3.2 collective-permute-start.3
  51.5 9.0 %all-to-all-done = bf16[4,128,1024]{2,1,0:T(8,128)(2,1)S(1)} async-done(((bf16[4,128,1024]{2,1,0:T(8,128)(2,1)}), bf16[4,128,1024]{2,1,0:T(8,128)(2,1)S(1)}, u32[]{:S(2)}, u32[]{:S(2)}) %all-to-all-start) | async-done | bytes 1048608 | tf_op jit(solution)/shard_map/all_to_all | solution.py:802
  60.5 2.7 norm_in.2.own_rows
  64.5 8.0 %collective-permute-done.9.refs_1_ = bf16[128,512]{1,0:T(8,128)(2,1)} collective-permute-done((bf16[128,512]{1,0:T(8,128)(2,1)S(1)}, bf16[128,512]{1,0:T(8,128)(2,1)}, u32[]{:S(2)}, u32[]{:S(2)}) %collective-permute-start.9) | collective-permute-done | bytes 131104 | tf_op jit(solution)/shard_map/ppermute | solution.py:735
  74.0 9.3 %collective-permute-done.10.refs_2_ = bf16[128,512]{1,0:T(8,128)(2,1)} collective-permute-done((bf16[128,512]{1,0:T(8,128)(2,1)}, bf16[128,512]{1,0:T(8,128)(2,1)}, u32[]{:S(2)}, u32[]{:S(2)}) %collective-permute-start.10) | collective-permute-done | bytes 131104 | tf_op jit(solution)/shard_map/ppermute | solution.py:735
  85.4 5.1 collective-permute-done.11.refs_3_
  93.3 2.7 fusion.63
  97.8 6.9 collective-permute-done.7.refs_6_
  106.2 6.9 collective-permute-done.8.refs_7_
  117.1 17.2 %attend.2 = (bf16[4,1024,128]{2,1,0:T(8,128)(2,1)S(1)}, bf16[4,1024,128]{2,1,0:T(8,128)(2,1)S(1)}, bf16[4,1024,128]{2,1,0:T(8,128)(2,1)S(1)}, f32[4,2,1024]{2,1,0:T(2,128)S(1)}, bf16[1024,512]{1,0:T(8,128)(2,1)S(1)}) custom-call(s32[1]{0:T(128)} %bitcast.5.core_ref, f32[1024,128]{1,0:T(8,128)S(1)} %get-tuple-element.173.cos_ref, ...), custom_call_target="tpu_custom_call" | custom-call | tf_op jit(solution)/shard_map/attend/pallas_call | solution.py:669
  136.1 2.7 attn_out.2
  139.4 13.4 %collective-permute-done.25.refs_1_ = bf16[512,512]{1,0:T(8,128)(2,1)S(1)} collective-permute-done((bf16[512,512]{1,0:T(8,128)(2,1)S(1)}, bf16[512,512]{1,0:T(8,128)(2,1)S(1)}, u32[]{:S(2)}, u32[]{:S(2)}) %collective-permute-start.25) | collective-permute-done | bytes 524320 | tf_op jit(solution)/shard_map/ppermute | solution.py:735
  154.4 9.6 %collective-permute-done.19.refs_2_ = bf16[512,512]{1,0:T(8,128)(2,1)S(1)} collective-permute-done((bf16[512,512]{1,0:T(8,128)(2,1)S(1)}, bf16[512,512]{1,0:T(8,128)(2,1)S(1)}, u32[]{:S(2)}, u32[]{:S(2)}) %collective-permute-start.19) | collective-permute-done | bytes 524320 | tf_op jit(solution)/shard_map/ppermute | solution.py:735
  165.5 9.7 %collective-permute-done.26.refs_2_ = bf16[512,512]{1,0:T(8,128)(2,1)S(1)} collective-permute-done((bf16[512,512]{1,0:T(8,128)(2,1)S(1)}, bf16[512,512]{1,0:T(8,128)(2,1)S(1)}, u32[]{:S(2)}, u32[]{:S(2)}) %collective-permute-start.26) | collective-permute-done | bytes 524320 | tf_op jit(solution)/shard_map/ppermute | solution.py:735
  175.5 3.4 after_attn.2
  181.9 4.6 collective-permute-done.20.refs_3_
  188.5 5.2 collective-permute-done.27.refs_3_
  196.6 9.7 %collective-permute-done.24.refs_7_ = bf16[512,512]{1,0:T(8,128)(2,1)S(1)} collective-permute-done((bf16[512,512]{1,0:T(8,128)(2,1)S(1)}, bf16[512,512]{1,0:T(8,128)(2,1)S(1)}, u32[]{:S(2)}, u32[]{:S(2)}) %collective-permute-start.24) | collective-permute-done | bytes 524320 | tf_op jit(solution)/shard_map/ppermute | solution.py:730
  207.8 9.8 %mlp_up.2 = (bf16[1024,2048]{1,0:T(8,128)(2,1)S(1)}, bf16[1024,2048]{1,0:T(8,128)(2,1)}) custom-call(bf16[512,1024]{1,0:T(8,128)(2,1)S(1)} %get-tuple-element.69.own_rows, bf16[512,1024]{1,0:T(8,128)(2,1)S(1)} %collective-permute-done.17.other_rows, bf16[512,512]{1,0:T(8,128)(2,1)S(1)} %dynamic-slice_bitcast_fusion.4.refs_0_, ...), custom_call_target="tpu_custom_call" | custom-call | tf_op jit(solution)/shard_map/mlp_up/pallas_call | solution.py:654
  218.6 10.2 %collective-permute-done.29.refs_5_ = bf16[512,512]{1,0:T(8,128)(2,1)S(1)} collective-permute-done((bf16[512,512]{1,0:T(8,128)(2,1)S(1)}, bf16[512,512]{1,0:T(8,128)(2,1)S(1)}, u32[]{:S(2)}, u32[]{:S(2)}) %collective-permute-start.29) | collective-permute-done | bytes 524320 | tf_op jit(solution)/shard_map/ppermute | solution.py:730
  228.8 11.2 %collective-permute-done.30.refs_6_ = bf16[512,512]{1,0:T(8,128)(2,1)S(1)} collective-permute-done((bf16[512,512]{1,0:T(8,128)(2,1)S(1)}, bf16[512,512]{1,0:T(8,128)(2,1)S(1)}, u32[]{:S(2)}, u32[]{:S(2)}) %collective-permute-start.30) | collective-permute-done | bytes 524320 | tf_op jit(solution)/shard_map/ppermute | solution.py:730
  240.0 10.8 %collective-permute-done.31.refs_7_ = bf16[512,512]{1,0:T(8,128)(2,1)S(1)} collective-permute-done((bf16[512,512]{1,0:T(8,128)(2,1)S(1)}, bf16[512,512]{1,0:T(8,128)(2,1)S(1)}, u32[]{:S(2)}, u32[]{:S(2)}) %collective-permute-start.31) | collective-permute-done | bytes 524320 | tf_op jit(solution)/shard_map/ppermute | solution.py:730
  250.8 4.5 mlp_down.2
  262.9 3.6 collective-permute-start.33
  266.5 22.2 %collective-permute-done.33.rows_ref = bf16[512,1024]{1,0:T(8,128)(2,1)S(1)} collective-permute-done((bf16[512,1024]{1,0:T(8,128)(2,1)S(1)}, bf16[512,1024]{1,0:T(8,128)(2,1)S(1)}, u32[]{:S(2)}, u32[]{:S(2)}) %collective-permute-start.33) | collective-permute-done | bytes 1048608 | tf_op jit(solution)/shard_map/ppermute | solution.py:23
  293.1 16.9 %attend.3 = (bf16[4,1024,128]{2,1,0:T(8,128)(2,1)S(1)}, bf16[4,1024,128]{2,1,0:T(8,128)(2,1)S(1)}, bf16[4,1024,128]{2,1,0:T(8,128)(2,1)S(1)}, f32[4,2,1024]{2,1,0:T(2,128)S(1)}, bf16[1024,512]{1,0:T(8,128)(2,1)S(1)}) custom-call(s32[1]{0:T(128)} %bitcast.5.core_ref, f32[1024,128]{1,0:T(8,128)S(1)} %get-tuple-element.173.cos_ref, ...), custom_call_target="tpu_custom_call" | custom-call | tf_op jit(solution)/shard_map/attend/pallas_call | solution.py:669
  312.1 2.8 attn_out.3
  317.6 3.4 after_attn.3
  325.1 9.7 %mlp_up.3 = (bf16[1024,2048]{1,0:T(8,128)(2,1)S(1)}, bf16[1024,2048]{1,0:T(8,128)(2,1)}) custom-call(bf16[512,1024]{1,0:T(8,128)(2,1)S(1)} %get-tuple-element.78.own_rows, bf16[512,1024]{1,0:T(8,128)(2,1)S(1)} %collective-permute-done.36.other_rows, bf16[512,512]{1,0:T(8,128)(2,1)S(1)} %dynamic-slice_bitcast_fusion.4.refs_0_, ...), custom_call_target="tpu_custom_call" | custom-call | tf_op jit(solution)/shard_map/mlp_up/pallas_call | solution.py:654
  334.8 4.5 mlp_down.3
  349.6 6.7 mlp_up_back.2.left_ref
  357.4 4.5 mlp_back.2
  364.7 4.9 into_attn_back.2
  372.2 2.9 collective-permute-done.40.other_rows
  384.0 24.1 %attend_back.2.left_ref = bf16[1024,1536]{1,0:T(8,128)(2,1)S(1)} custom-call(s32[1]{0:T(128)} %bitcast.5.core_ref, f32[1024,128]{1,0:T(8,128)S(1)} %get-tuple-element.173.cos_ref, f32[1024,128]{1,0:T(8,128)S(1)} %get-tuple-element.174.sin_ref, bf16[512,1024]{1,0:T(8,128)(2,1)} %get-tuple-element.89.own_rows, ...), custom_call_target="tpu_custom_call" | custom-call | tf_op jit(solution)/shard_map/attend_back/pallas_call | solution.py:669
  408.1 6.3 attn_back.2
  424.2 3.1 out_of_layer.2
  430.2 5.1 all-to-all-start.1
  439.0 16.0 %collective-permute-done.43.grad_ref = bf16[512,1024]{1,0:T(8,128)(2,1)} collective-permute-done((bf16[512,1024]{1,0:T(8,128)(2,1)}, bf16[512,1024]{1,0:T(8,128)(2,1)}, u32[]{:S(2)}, u32[]{:S(2)}) %collective-permute-start.43) | collective-permute-done | bytes 1048608 | tf_op jit(solution)/shard_map/ppermute | solution.py:23
  455.1 4.7 into_mlp_back.3
  464.2 3.0 pad_maximum_fusion.3
  480.9 7.5 %mlp_up_back.3.left_ref = bf16[1024,2048]{1,0:T(8,128)(2,1)S(1)} custom-call(bf16[512,1024]{1,0:T(8,128)(2,1)} %get-tuple-element.101.own_rows, bf16[512,1024]{1,0:T(8,128)(2,1)} %collective-permute-done.44.other_rows, bf16[1024,2048]{1,0:T(8,128)(2,1)} %get-tuple-element.102.slope_ref, bf16[512,512]{1,0:T(8,128)(2,1)S(1)} %dynamic-slice_bitcast_fusion.3.refs_0_, ...), custom_call_target="tpu_custom_call" | custom-call | tf_op jit(solution)/shard_map/mlp_up_back/pallas_call | solution.py:654
  493.2 3.8 fusion.16
  499.8 4.7 mlp_back.3
  517.5 3.8 collective-permute-start.81
  527.3 5.2 into_attn_back.3
  535.6 6.5 collective-permute-done.71
  542.1 3.8 collective-permute-start.82
  554.0 4.3 collective-permute-done.82
  560.3 4.2 collective-permute-done.70
  564.5 3.8 collective-permute-start.83
  568.6 3.8 collective-permute-start.75
  576.0 23.9 %attend_back.3.left_ref = bf16[1024,1536]{1,0:T(8,128)(2,1)S(1)} custom-call(s32[1]{0:T(128)} %bitcast.5.core_ref, f32[1024,128]{1,0:T(8,128)S(1)} %get-tuple-element.173.cos_ref, f32[1024,128]{1,0:T(8,128)S(1)} %get-tuple-element.174.sin_ref, bf16[512,1024]{1,0:T(8,128)(2,1)S(1)} %get-tuple-element.106.own_rows, ...), custom_call_target="tpu_custom_call" | custom-call | tf_op jit(solution)/shard_map/attend_back/pallas_call | solution.py:669
  615.3 5.2 attn_back.3
  627.9 3.2 collective-permute-start.66
  641.5 4.3 collective-permute-start.57
  649.5 5.4 collective-permute-done.57
  655.8 4.3 collective-permute-start.58
  663.8 3.6 all-to-all-start.2
  671.1 4.3 collective-permute-start.59
  680.5 14.6 %collective-permute-done.59 = bf16[512,384]{1,0:T(8,128)(2,1)S(1)} collective-permute-done((bf16[512,384]{1,0:T(8,128)(2,1)S(1)}, bf16[512,384]{1,0:T(8,128)(2,1)S(1)}, u32[]{:S(2)}, u32[]{:S(2)}) %collective-permute-start.59) | collective-permute-done | bytes 393248 | tf_op jit(solution)/shard_map/ppermute | solution.py:735
  697.5 6.0 collective-permute-start.52
  (567 shorter events, 230.9 us)
Async XLA Ops:
  11.4 49.1 %all-to-all-start = ((bf16[4,128,1024]{2,1,0:T(8,128)(2,1)}), bf16[4,128,1024]{2,1,0:T(8,128)(2,1)S(1)}, u32[]{:S(2)}, u32[]{:S(2)}) async-start(bf16[4,128,1024]{2,1,0:T(8,128)(2,1)} %pad_maximum_fusion.8), calls=%async_computation | async-start | bytes 2097152 | tf_op jit(solution)/shard_map/all_to_all | solution.py:802
  20.8 26.8 %collective-permute-start.2 = (bf16[512,384]{1,0:T(8,128)(2,1)S(1)}, bf16[512,384]{1,0:T(8,128)(2,1)}, u32[]{:S(2)}, u32[]{:S(2)}) collective-permute-start(bf16[512,384]{1,0:T(8,128)(2,1)S(1)} %copy.47.refs_0_), channel_id=1, source_target_pairs={{0,1},{1,2},{2,3},{3,0},{4,5},{5,6},{6,7},{7,4},{8,9},{9,10},{10,1... | collective-permute-start | bytes 1179656 | tf_op jit(solution)/shard_map/ppermute | solution.py:735
  47.6 16.6 %collective-permute-start.3 = (bf16[512,384]{1,0:T(8,128)(2,1)}, bf16[512,384]{1,0:T(8,128)(2,1)}, u32[]{:S(2)}, u32[]{:S(2)}) collective-permute-start(bf16[512,384]{1,0:T(8,128)(2,1)} %collective-permute-done.2.refs_1_), channel_id=1, source_target_pairs={{0,1},{1,2},{2,3},{3,0},{4,5},{5,6},{6,7},{7,4},{8,9},{9,10},{10,1... | collective-permute-start | bytes 1179656 | tf_op jit(solution)/shard_map/ppermute | solution.py:735
  63.3 51.4 %collective-permute-start.1 = (bf16[512,1024]{1,0:T(8,128)(2,1)}, bf16[512,1024]{1,0:T(8,128)(2,1)}, u32[]{:S(2)}, u32[]{:S(2)}) collective-permute-start(bf16[512,1024]{1,0:T(8,128)(2,1)} %norm_in.2.own_rows), channel_id=1, source_target_pairs={{0,4},{4,0},{8,12},{12,8},{1,5},{5,1},{9,13},{13,9},{2,6},{6,2},{1... | collective-permute-start | bytes 3145736 | tf_op jit(solution)/shard_map/ppermute | solution.py:730
  64.3 27.8 %collective-permute-start.4 = (bf16[512,384]{1,0:T(8,128)(2,1)}, bf16[512,384]{1,0:T(8,128)(2,1)}, u32[]{:S(2)}, u32[]{:S(2)}) collective-permute-start(bf16[512,384]{1,0:T(8,128)(2,1)} %collective-permute-done.3.refs_2_), channel_id=1, source_target_pairs={{0,1},{1,2},{2,3},{3,0},{4,5},{5,6},{6,7},{7,4},{8,9},{9,10},{10,1... | collective-permute-start | bytes 1179656 | tf_op jit(solution)/shard_map/ppermute | solution.py:735
  72.4 20.7 %collective-permute-start.5 = (bf16[512,384]{1,0:T(8,128)(2,1)S(1)}, bf16[512,384]{1,0:T(8,128)(2,1)}, u32[]{:S(2)}, u32[]{:S(2)}) collective-permute-start(bf16[512,384]{1,0:T(8,128)(2,1)S(1)} %copy.47.refs_0_), channel_id=1, source_target_pairs={{0,8},{4,12},{8,0},{12,4},{1,9},{5,13},{9,1},{13,5},{2,10},{6,14},... | collective-permute-start | bytes 1179656 | tf_op jit(solution)/shard_map/ppermute | solution.py:730
  83.9 12.3 %collective-permute-start.6 = (bf16[512,384]{1,0:T(8,128)(2,1)}, bf16[512,384]{1,0:T(8,128)(2,1)}, u32[]{:S(2)}, u32[]{:S(2)}) collective-permute-start(bf16[512,384]{1,0:T(8,128)(2,1)} %collective-permute-done.2.refs_1_), channel_id=1, source_target_pairs={{0,8},{4,12},{8,0},{12,4},{1,9},{5,13},{9,1},{13,5},{2,10},{6,14},... | collective-permute-start | bytes 1179656 | tf_op jit(solution)/shard_map/ppermute | solution.py:730
  90.6 14.1 %collective-permute-start.7 = (bf16[512,384]{1,0:T(8,128)(2,1)}, bf16[512,384]{1,0:T(8,128)(2,1)}, u32[]{:S(2)}, u32[]{:S(2)}) collective-permute-start(bf16[512,384]{1,0:T(8,128)(2,1)} %collective-permute-done.3.refs_2_), channel_id=1, source_target_pairs={{0,8},{4,12},{8,0},{12,4},{1,9},{5,13},{9,1},{13,5},{2,10},{6,14},... | collective-permute-start | bytes 1179656 | tf_op jit(solution)/shard_map/ppermute | solution.py:730
  92.1 21.0 %collective-permute-start.8 = (bf16[512,384]{1,0:T(8,128)(2,1)}, bf16[512,384]{1,0:T(8,128)(2,1)}, u32[]{:S(2)}, u32[]{:S(2)}) collective-permute-start(bf16[512,384]{1,0:T(8,128)(2,1)} %collective-permute-done.4.refs_3_), channel_id=1, source_target_pairs={{0,8},{4,12},{8,0},{12,4},{1,9},{5,13},{9,1},{13,5},{2,10},{6,14},... | collective-permute-start | bytes 1179656 | tf_op jit(solution)/shard_map/ppermute | solution.py:730
  93.2 45.8 %collective-permute-start.18 = (bf16[512,512]{1,0:T(8,128)(2,1)S(1)}, bf16[512,512]{1,0:T(8,128)(2,1)S(1)}, u32[]{:S(2)}, u32[]{:S(2)}) collective-permute-start(bf16[512,512]{1,0:T(8,128)(2,1)S(1)} %dynamic-slice_bitcast_fusion.4.refs_0_), channel_id=1, source_target_pairs={{0,1},{1,2},{2,3},{3,0},{4,5},{5,6},{6,7},{7,4},{8,9},{9,10},{10,1... | collective-permute-start | bytes 1572872 | tf_op jit(solution)/shard_map/ppermute | solution.py:735
  96.3 39.7 %collective-permute-start.12 = (bf16[128,512]{1,0:T(8,128)(2,1)S(1)}, bf16[128,512]{1,0:T(8,128)(2,1)S(1)}, u32[]{:S(2)}, u32[]{:S(2)}) collective-permute-start(bf16[128,512]{1,0:T(8,128)(2,1)S(1)} %copy-done.71), channel_id=1, source_target_pairs={{0,8},{4,12},{8,0},{12,4},{1,9},{5,13},{9,1},{13,5},{2,10},{6,14},... | collective-permute-start | bytes 393224 | tf_op jit(solution)/shard_map/ppermute | solution.py:730
  104.7 31.4 %collective-permute-start.13 = (bf16[128,512]{1,0:T(8,128)(2,1)}, bf16[128,512]{1,0:T(8,128)(2,1)S(1)}, u32[]{:S(2)}, u32[]{:S(2)}) collective-permute-start(bf16[128,512]{1,0:T(8,128)(2,1)} %collective-permute-done.9.refs_1_), channel_id=1, source_target_pairs={{0,8},{4,12},{8,0},{12,4},{1,9},{5,13},{9,1},{13,5},{2,10},{6,14},... | collective-permute-start | bytes 393224 | tf_op jit(solution)/shard_map/ppermute | solution.py:730
  113.1 23.0 %collective-permute-start.14 = (bf16[128,512]{1,0:T(8,128)(2,1)}, bf16[128,512]{1,0:T(8,128)(2,1)S(1)}, u32[]{:S(2)}, u32[]{:S(2)}) collective-permute-start(bf16[128,512]{1,0:T(8,128)(2,1)} %collective-permute-done.10.refs_2_), channel_id=1, source_target_pairs={{0,8},{4,12},{8,0},{12,4},{1,9},{5,13},{9,1},{13,5},{2,10},{6,14},... | collective-permute-start | bytes 393224 | tf_op jit(solution)/shard_map/ppermute | solution.py:730
  114.6 21.5 %collective-permute-start.15 = (bf16[128,512]{1,0:T(8,128)(2,1)}, bf16[128,512]{1,0:T(8,128)(2,1)S(1)}, u32[]{:S(2)}, u32[]{:S(2)}) collective-permute-start(bf16[128,512]{1,0:T(8,128)(2,1)} %collective-permute-done.11.refs_3_), channel_id=1, source_target_pairs={{0,8},{4,12},{8,0},{12,4},{1,9},{5,13},{9,1},{13,5},{2,10},{6,14},... | collective-permute-start | bytes 393224 | tf_op jit(solution)/shard_map/ppermute | solution.py:730
  136.0 16.8 %collective-permute-start.25 = (bf16[512,512]{1,0:T(8,128)(2,1)S(1)}, bf16[512,512]{1,0:T(8,128)(2,1)S(1)}, u32[]{:S(2)}, u32[]{:S(2)}) collective-permute-start(bf16[512,512]{1,0:T(8,128)(2,1)S(1)} %dynamic-slice_bitcast_fusion.3.refs_0_), channel_id=1, source_target_pairs={{0,1},{1,2},{2,3},{3,0},{4,5},{5,6},{6,7},{7,4},{8,9},{9,10},{10,1... | collective-permute-start | bytes 1572872 | tf_op jit(solution)/shard_map/ppermute | solution.py:735
  138.9 36.6 %collective-permute-start.16 = (bf16[512,1024]{1,0:T(8,128)(2,1)S(1)}, bf16[512,1024]{1,0:T(8,128)(2,1)S(1)}, u32[]{:S(2)}, u32[]{:S(2)}) collective-permute-start(bf16[512,1024]{1,0:T(8,128)(2,1)S(1)} %get-tuple-element.67), channel_id=1, source_target_pairs={{0,4},{4,0},{8,12},{12,8},{1,5},{5,1},{9,13},{13,9},{2,6},{6,2},{1... | collective-permute-start | bytes 3145736 | tf_op jit(solution)/shard_map/ppermute | solution.py:730
  139.0 25.0 %collective-permute-start.19 = (bf16[512,512]{1,0:T(8,128)(2,1)S(1)}, bf16[512,512]{1,0:T(8,128)(2,1)S(1)}, u32[]{:S(2)}, u32[]{:S(2)}) collective-permute-start(bf16[512,512]{1,0:T(8,128)(2,1)S(1)} %collective-permute-done.18.refs_1_), channel_id=1, source_target_pairs={{0,1},{1,2},{2,3},{3,0},{4,5},{5,6},{6,7},{7,4},{8,9},{9,10},{10,1... | collective-permute-start | bytes 1572872 | tf_op jit(solution)/shard_map/ppermute | solution.py:735
  152.8 22.5 %collective-permute-start.26 = (bf16[512,512]{1,0:T(8,128)(2,1)S(1)}, bf16[512,512]{1,0:T(8,128)(2,1)S(1)}, u32[]{:S(2)}, u32[]{:S(2)}) collective-permute-start(bf16[512,512]{1,0:T(8,128)(2,1)S(1)} %collective-permute-done.25.refs_1_), channel_id=1, source_target_pairs={{0,1},{1,2},{2,3},{3,0},{4,5},{5,6},{6,7},{7,4},{8,9},{9,10},{10,1... | collective-permute-start | bytes 1572872 | tf_op jit(solution)/shard_map/ppermute | solution.py:735
  152.8 27.5 %collective-permute-start.21 = (bf16[512,512]{1,0:T(8,128)(2,1)S(1)}, bf16[512,512]{1,0:T(8,128)(2,1)S(1)}, u32[]{:S(2)}, u32[]{:S(2)}) collective-permute-start(bf16[512,512]{1,0:T(8,128)(2,1)S(1)} %dynamic-slice_bitcast_fusion.4.refs_0_), channel_id=1, source_target_pairs={{0,8},{4,12},{8,0},{12,4},{1,9},{5,13},{9,1},{13,5},{2,10},{6,14},... | collective-permute-start | bytes 1572872 | tf_op jit(solution)/shard_map/ppermute | solution.py:730
  164.0 22.5 %collective-permute-start.20 = (bf16[512,512]{1,0:T(8,128)(2,1)S(1)}, bf16[512,512]{1,0:T(8,128)(2,1)S(1)}, u32[]{:S(2)}, u32[]{:S(2)}) collective-permute-start(bf16[512,512]{1,0:T(8,128)(2,1)S(1)} %collective-permute-done.19.refs_2_), channel_id=1, source_target_pairs={{0,1},{1,2},{2,3},{3,0},{4,5},{5,6},{6,7},{7,4},{8,9},{9,10},{10,1... | collective-permute-start | bytes 1572872 | tf_op jit(solution)/shard_map/ppermute | solution.py:735
  164.0 24.0 %collective-permute-start.22 = (bf16[512,512]{1,0:T(8,128)(2,1)S(1)}, bf16[512,512]{1,0:T(8,128)(2,1)S(1)}, u32[]{:S(2)}, u32[]{:S(2)}) collective-permute-start(bf16[512,512]{1,0:T(8,128)(2,1)S(1)} %collective-permute-done.18.refs_1_), channel_id=1, source_target_pairs={{0,8},{4,12},{8,0},{12,4},{1,9},{5,13},{9,1},{13,5},{2,10},{6,14},... | collective-permute-start | bytes 1572872 | tf_op jit(solution)/shard_map/ppermute | solution.py:730
  175.2 18.4 %collective-permute-start.27 = (bf16[512,512]{1,0:T(8,128)(2,1)S(1)}, bf16[512,512]{1,0:T(8,128)(2,1)S(1)}, u32[]{:S(2)}, u32[]{:S(2)}) collective-permute-start(bf16[512,512]{1,0:T(8,128)(2,1)S(1)} %collective-permute-done.26.refs_2_), channel_id=1, source_target_pairs={{0,1},{1,2},{2,3},{3,0},{4,5},{5,6},{6,7},{7,4},{8,9},{9,10},{10,1... | collective-permute-start | bytes 1572872 | tf_op jit(solution)/shard_map/ppermute | solution.py:735
  180.3 27.6 %collective-permute-start.17 = (bf16[512,1024]{1,0:T(8,128)(2,1)S(1)}, bf16[512,1024]{1,0:T(8,128)(2,1)S(1)}, u32[]{:S(2)}, u32[]{:S(2)}) collective-permute-start(bf16[512,1024]{1,0:T(8,128)(2,1)S(1)} %get-tuple-element.69.own_rows), channel_id=1, source_target_pairs={{0,4},{4,0},{8,12},{12,8},{1,5},{5,1},{9,13},{13,9},{2,6},{6,2},{1... | collective-permute-start | bytes 3145736 | tf_op jit(solution)/shard_map/ppermute | solution.py:730
  180.3 14.9 %collective-permute-start.23 = (bf16[512,512]{1,0:T(8,128)(2,1)S(1)}, bf16[512,512]{1,0:T(8,128)(2,1)S(1)}, u32[]{:S(2)}, u32[]{:S(2)}) collective-permute-start(bf16[512,512]{1,0:T(8,128)(2,1)S(1)} %collective-permute-done.19.refs_2_), channel_id=1, source_target_pairs={{0,8},{4,12},{8,0},{12,4},{1,9},{5,13},{9,1},{13,5},{2,10},{6,14},... | collective-permute-start | bytes 1572872 | tf_op jit(solution)/shard_map/ppermute | solution.py:730
  186.5 19.8 %collective-permute-start.24 = (bf16[512,512]{1,0:T(8,128)(2,1)S(1)}, bf16[512,512]{1,0:T(8,128)(2,1)S(1)}, u32[]{:S(2)}, u32[]{:S(2)}) collective-permute-start(bf16[512,512]{1,0:T(8,128)(2,1)S(1)} %collective-permute-done.20.refs_3_), channel_id=1, source_target_pairs={{0,8},{4,12},{8,0},{12,4},{1,9},{5,13},{9,1},{13,5},{2,10},{6,14},... | collective-permute-start | bytes 1572872 | tf_op jit(solution)/shard_map/ppermute | solution.py:730
  188.0 30.6 %collective-permute-start.28 = (bf16[512,512]{1,0:T(8,128)(2,1)S(1)}, bf16[512,512]{1,0:T(8,128)(2,1)S(1)}, u32[]{:S(2)}, u32[]{:S(2)}) collective-permute-start(bf16[512,512]{1,0:T(8,128)(2,1)S(1)} %dynamic-slice_bitcast_fusion.3.refs_0_), channel_id=1, source_target_pairs={{0,8},{4,12},{8,0},{12,4},{1,9},{5,13},{9,1},{13,5},{2,10},{6,14},... | collective-permute-start | bytes 1572872 | tf_op jit(solution)/shard_map/ppermute | solution.py:730
  193.7 35.1 %collective-permute-start.29 = (bf16[512,512]{1,0:T(8,128)(2,1)S(1)}, bf16[512,512]{1,0:T(8,128)(2,1)S(1)}, u32[]{:S(2)}, u32[]{:S(2)}) collective-permute-start(bf16[512,512]{1,0:T(8,128)(2,1)S(1)} %collective-permute-done.25.refs_1_), channel_id=1, source_target_pairs={{0,8},{4,12},{8,0},{12,4},{1,9},{5,13},{9,1},{13,5},{2,10},{6,14},... | collective-permute-start | bytes 1572872 | tf_op jit(solution)/shard_map/ppermute | solution.py:730
  195.2 44.8 %collective-permute-start.30 = (bf16[512,512]{1,0:T(8,128)(2,1)S(1)}, bf16[512,512]{1,0:T(8,128)(2,1)S(1)}, u32[]{:S(2)}, u32[]{:S(2)}) collective-permute-start(bf16[512,512]{1,0:T(8,128)(2,1)S(1)} %collective-permute-done.26.refs_2_), channel_id=1, source_target_pairs={{0,8},{4,12},{8,0},{12,4},{1,9},{5,13},{9,1},{13,5},{2,10},{6,14},... | collective-permute-start | bytes 1572872 | tf_op jit(solution)/shard_map/ppermute | solution.py:730
  206.3 44.5 %collective-permute-start.31 = (bf16[512,512]{1,0:T(8,128)(2,1)S(1)}, bf16[512,512]{1,0:T(8,128)(2,1)S(1)}, u32[]{:S(2)}, u32[]{:S(2)}) collective-permute-start(bf16[512,512]{1,0:T(8,128)(2,1)S(1)} %collective-permute-done.27.refs_3_), channel_id=1, source_target_pairs={{0,8},{4,12},{8,0},{12,4},{1,9},{5,13},{9,1},{13,5},{2,10},{6,14},... | collective-permute-start | bytes 1572872 | tf_op jit(solution)/shard_map/ppermute | solution.py:730
  262.9 25.8 %collective-permute-start.33 = (bf16[512,1024]{1,0:T(8,128)(2,1)S(1)}, bf16[512,1024]{1,0:T(8,128)(2,1)S(1)}, u32[]{:S(2)}, u32[]{:S(2)}) collective-permute-start(bf16[512,1024]{1,0:T(8,128)(2,1)S(1)} %get-tuple-element.98), channel_id=1, source_target_pairs={{0,16},{1,17},{2,18},{3,19},{4,20},{5,21},{6,22},{7,23},{8,24},{9,... | collective-permute-start | bytes 3145736 | tf_op jit(solution)/shard_map/ppermute | solution.py:23
  427.4 27.7 %collective-permute-start.43 = (bf16[512,1024]{1,0:T(8,128)(2,1)}, bf16[512,1024]{1,0:T(8,128)(2,1)}, u32[]{:S(2)}, u32[]{:S(2)}) collective-permute-start(bf16[512,1024]{1,0:T(8,128)(2,1)} %get-tuple-element.97), channel_id=1, source_target_pairs={{16,0},{17,1},{18,2},{19,3},{20,4},{21,5},{22,6},{23,7},{24,8},{25... | collective-permute-start | bytes 3145736 | tf_op jit(solution)/shard_map/ppermute | solution.py:23
  430.2 37.1 %all-to-all-start.1 = ((bf16[4,128,1024]{2,1,0:T(8,128)(2,1)}), bf16[4,128,1024]{2,1,0:T(8,128)(2,1)}, u32[]{:S(2)}, u32[]{:S(2)}) async-start(bf16[4,128,1024]{2,1,0:T(8,128)(2,1)} %bitcast.103), calls=%async_computation.1 | async-start | bytes 2097152 | tf_op jit(solution)/shard_map/all_to_all | solution.py:807
  469.2 36.4 %collective-permute-start.42 = (bf16[2,128,1024]{2,1,0:T(8,128)(2,1)}, bf16[2,128,1024]{2,1,0:T(8,128)(2,1)}, u32[]{:S(2)}, u32[]{:S(2)}) collective-permute-start(bf16[2,128,1024]{2,1,0:T(8,128)(2,1)} %dynamic-slice_bitcast_fusion.2), channel_id=1, source_target_pairs={{0,4},{4,0},{8,12},{12,8},{1,5},{5,1},{9,13},{13,9},{2,6},{6,2},{1... | collective-permute-start | bytes 1572872 | tf_op jit(solution)/shard_map/ppermute | solution.py:730
  491.7 23.8 %collective-permute-start.80 = (bf16[512,512]{1,0:T(8,128)(2,1)}, bf16[512,512]{1,0:T(8,128)(2,1)}, u32[]{:S(2)}, u32[]{:S(2)}) collective-permute-start(bf16[512,512]{1,0:T(8,128)(2,1)} %slice.468), channel_id=1, source_target_pairs={{0,8},{4,12},{8,0},{12,4},{1,9},{5,13},{9,1},{13,5},{2,10},{6,14},... | collective-permute-start | bytes 1572872 | tf_op jit(solution)/shard_map/ppermute | solution.py:730
  504.5 22.1 %collective-permute-start.45 = (bf16[512,1024]{1,0:T(8,128)(2,1)S(1)}, bf16[512,1024]{1,0:T(8,128)(2,1)S(1)}, u32[]{:S(2)}, u32[]{:S(2)}) collective-permute-start(bf16[512,1024]{1,0:T(8,128)(2,1)S(1)} %get-tuple-element.104), channel_id=1, source_target_pairs={{0,4},{4,0},{8,12},{12,8},{1,5},{5,1},{9,13},{13,9},{2,6},{6,2},{1... | collective-permute-start | bytes 3145736 | tf_op jit(solution)/shard_map/ppermute | solution.py:730
  504.8 16.6 %collective-permute-start.72 = (bf16[512,512]{1,0:T(8,128)(2,1)S(1)}, bf16[512,512]{1,0:T(8,128)(2,1)S(1)}, u32[]{:S(2)}, u32[]{:S(2)}) collective-permute-start(bf16[512,512]{1,0:T(8,128)(2,1)S(1)} %slice.472), channel_id=1, source_target_pairs={{0,8},{4,12},{8,0},{12,4},{1,9},{5,13},{9,1},{13,5},{2,10},{6,14},... | collective-permute-start | bytes 1572872 | tf_op jit(solution)/shard_map/ppermute | solution.py:730
  509.6 22.9 %collective-permute-start.79 = (bf16[512,512]{1,0:T(8,128)(2,1)}, bf16[512,512]{1,0:T(8,128)(2,1)}, u32[]{:S(2)}, u32[]{:S(2)}) collective-permute-start(bf16[512,512]{1,0:T(8,128)(2,1)} %slice.469), channel_id=1, source_target_pairs={{0,8},{4,12},{8,0},{12,4},{1,9},{5,13},{9,1},{13,5},{2,10},{6,14},... | collective-permute-start | bytes 1572872 | tf_op jit(solution)/shard_map/ppermute | solution.py:730
  514.8 27.3 %collective-permute-start.71 = (bf16[512,512]{1,0:T(8,128)(2,1)}, bf16[512,512]{1,0:T(8,128)(2,1)}, u32[]{:S(2)}, u32[]{:S(2)}) collective-permute-start(bf16[512,512]{1,0:T(8,128)(2,1)} %slice.473), channel_id=1, source_target_pairs={{0,8},{4,12},{8,0},{12,4},{1,9},{5,13},{9,1},{13,5},{2,10},{6,14},... | collective-permute-start | bytes 1572872 | tf_op jit(solution)/shard_map/ppermute | solution.py:730
  517.5 16.4 %collective-permute-start.81 = (bf16[512,512]{1,0:T(8,128)(2,1)}, bf16[512,512]{1,0:T(8,128)(2,1)}, u32[]{:S(2)}, u32[]{:S(2)}) collective-permute-start(bf16[512,512]{1,0:T(8,128)(2,1)} %fusion.1), channel_id=1, source_target_pairs={{0,3},{1,0},{2,1},{3,2},{4,7},{5,4},{6,5},{7,6},{8,11},{9,8},{10,9... | collective-permute-start | bytes 1572872 | tf_op jit(solution)/shard_map/ppermute | solution.py:735
  522.3 23.7 %collective-permute-start.73 = (bf16[512,512]{1,0:T(8,128)(2,1)}, bf16[512,512]{1,0:T(8,128)(2,1)}, u32[]{:S(2)}, u32[]{:S(2)}) collective-permute-start(bf16[512,512]{1,0:T(8,128)(2,1)} %fusion.15), channel_id=1, source_target_pairs={{0,3},{1,0},{2,1},{3,2},{4,7},{5,4},{6,5},{7,6},{8,11},{9,8},{10,9... | collective-permute-start | bytes 1572872 | tf_op jit(solution)/shard_map/ppermute | solution.py:735
  526.6 26.8 %collective-permute-start.78 = (bf16[512,512]{1,0:T(8,128)(2,1)}, bf16[512,512]{1,0:T(8,128)(2,1)}, u32[]{:S(2)}, u32[]{:S(2)}) collective-permute-start(bf16[512,512]{1,0:T(8,128)(2,1)} %slice.470), channel_id=1, source_target_pairs={{0,8},{4,12},{8,0},{12,4},{1,9},{5,13},{9,1},{13,5},{2,10},{6,14},... | collective-permute-start | bytes 1572872 | tf_op jit(solution)/shard_map/ppermute | solution.py:730
  532.5 32.0 %collective-permute-start.70 = (bf16[512,512]{1,0:T(8,128)(2,1)}, bf16[512,512]{1,0:T(8,128)(2,1)S(1)}, u32[]{:S(2)}, u32[]{:S(2)}) collective-permute-start(bf16[512,512]{1,0:T(8,128)(2,1)} %slice.474), channel_id=1, source_target_pairs={{0,8},{4,12},{8,0},{12,4},{1,9},{5,13},{9,1},{13,5},{2,10},{6,14},... | collective-permute-start | bytes 1572872 | tf_op jit(solution)/shard_map/ppermute | solution.py:730
  534.0 38.3 %collective-permute-start.46 = (bf16[512,1024]{1,0:T(8,128)(2,1)S(1)}, bf16[512,1024]{1,0:T(8,128)(2,1)S(1)}, u32[]{:S(2)}, u32[]{:S(2)}) collective-permute-start(bf16[512,1024]{1,0:T(8,128)(2,1)S(1)} %get-tuple-element.106.own_rows), channel_id=1, source_target_pairs={{0,4},{4,0},{8,12},{12,8},{1,5},{5,1},{9,13},{13,9},{2,6},{6,2},{1... | collective-permute-start | bytes 3145736 | tf_op jit(solution)/shard_map/ppermute | solution.py:730
  542.1 16.2 %collective-permute-start.82 = (bf16[512,512]{1,0:T(8,128)(2,1)S(1)}, bf16[512,512]{1,0:T(8,128)(2,1)S(1)}, u32[]{:S(2)}, u32[]{:S(2)}) collective-permute-start(bf16[512,512]{1,0:T(8,128)(2,1)S(1)} %fusion.5), channel_id=1, source_target_pairs={{0,3},{1,0},{2,1},{3,2},{4,7},{5,4},{6,5},{7,6},{8,11},{9,8},{10,9... | collective-permute-start | bytes 1572872 | tf_op jit(solution)/shard_map/ppermute | solution.py:735
  547.5 20.9 %collective-permute-start.74 = (bf16[512,512]{1,0:T(8,128)(2,1)S(1)}, bf16[512,512]{1,0:T(8,128)(2,1)S(1)}, u32[]{:S(2)}, u32[]{:S(2)}) collective-permute-start(bf16[512,512]{1,0:T(8,128)(2,1)S(1)} %fusion.19), channel_id=1, source_target_pairs={{0,3},{1,0},{2,1},{3,2},{4,7},{5,4},{6,5},{7,6},{8,11},{9,8},{10,9... | collective-permute-start | bytes 1572872 | tf_op jit(solution)/shard_map/ppermute | solution.py:735
  553.4 57.2 %collective-permute-start.77 = (bf16[512,512]{1,0:T(8,128)(2,1)}, bf16[512,512]{1,0:T(8,128)(2,1)}, u32[]{:S(2)}, u32[]{:S(2)}) collective-permute-start(bf16[512,512]{1,0:T(8,128)(2,1)} %slice.471), channel_id=1, source_target_pairs={{0,8},{4,12},{8,0},{12,4},{1,9},{5,13},{9,1},{13,5},{2,10},{6,14},... | collective-permute-start | bytes 1572872 | tf_op jit(solution)/shard_map/ppermute | solution.py:730
  558.3 63.5 %collective-permute-start.69 = (bf16[512,512]{1,0:T(8,128)(2,1)}, bf16[512,512]{1,0:T(8,128)(2,1)}, u32[]{:S(2)}, u32[]{:S(2)}) collective-permute-start(bf16[512,512]{1,0:T(8,128)(2,1)} %slice.475), channel_id=1, source_target_pairs={{0,8},{4,12},{8,0},{12,4},{1,9},{5,13},{9,1},{13,5},{2,10},{6,14},... | collective-permute-start | bytes 1572872 | tf_op jit(solution)/shard_map/ppermute | solution.py:730
  564.5 46.1 %collective-permute-start.83 = (bf16[512,512]{1,0:T(8,128)(2,1)S(1)}, bf16[512,512]{1,0:T(8,128)(2,1)}, u32[]{:S(2)}, u32[]{:S(2)}) collective-permute-start(bf16[512,512]{1,0:T(8,128)(2,1)S(1)} %fusion.9), channel_id=1, source_target_pairs={{0,3},{1,0},{2,1},{3,2},{4,7},{5,4},{6,5},{7,6},{8,11},{9,8},{10,9... | collective-permute-start | bytes 1572872 | tf_op jit(solution)/shard_map/ppermute | solution.py:735
  568.6 53.4 %collective-permute-start.75 = (bf16[512,512]{1,0:T(8,128)(2,1)S(1)}, bf16[512,512]{1,0:T(8,128)(2,1)}, u32[]{:S(2)}, u32[]{:S(2)}) collective-permute-start(bf16[512,512]{1,0:T(8,128)(2,1)S(1)} %fusion.23), channel_id=1, source_target_pairs={{0,3},{1,0},{2,1},{3,2},{4,7},{5,4},{6,5},{7,6},{8,11},{9,8},{10,9... | collective-permute-start | bytes 1572872 | tf_op jit(solution)/shard_map/ppermute | solution.py:735
  607.9 12.6 %collective-permute-start.64 = (bf16[128,512]{1,0:T(8,128)(2,1)S(1)}, bf16[128,512]{1,0:T(8,128)(2,1)S(1)}, u32[]{:S(2)}, u32[]{:S(2)}) collective-permute-start(bf16[128,512]{1,0:T(8,128)(2,1)S(1)} %slice.480), channel_id=1, source_target_pairs={{0,8},{4,12},{8,0},{12,4},{1,9},{5,13},{9,1},{13,5},{2,10},{6,14},... | collective-permute-start | bytes 393224 | tf_op jit(solution)/shard_map/ppermute | solution.py:730
  613.1 11.8 %collective-permute-start.63 = (bf16[128,512]{1,0:T(8,128)(2,1)S(1)}, bf16[128,512]{1,0:T(8,128)(2,1)S(1)}, u32[]{:S(2)}, u32[]{:S(2)}) collective-permute-start(bf16[128,512]{1,0:T(8,128)(2,1)S(1)} %slice.481), channel_id=1, source_target_pairs={{0,8},{4,12},{8,0},{12,4},{1,9},{5,13},{9,1},{13,5},{2,10},{6,14},... | collective-permute-start | bytes 393224 | tf_op jit(solution)/shard_map/ppermute | solution.py:730
  614.5 19.5 %collective-permute-start.62 = (bf16[128,512]{1,0:T(8,128)(2,1)S(1)}, bf16[128,512]{1,0:T(8,128)(2,1)S(1)}, u32[]{:S(2)}, u32[]{:S(2)}) collective-permute-start(bf16[128,512]{1,0:T(8,128)(2,1)S(1)} %slice.482), channel_id=1, source_target_pairs={{0,8},{4,12},{8,0},{12,4},{1,9},{5,13},{9,1},{13,5},{2,10},{6,14},... | collective-permute-start | bytes 393224 | tf_op jit(solution)/shard_map/ppermute | solution.py:730
  620.5 17.6 %collective-permute-start.61 = (bf16[128,512]{1,0:T(8,128)(2,1)S(1)}, bf16[128,512]{1,0:T(8,128)(2,1)S(1)}, u32[]{:S(2)}, u32[]{:S(2)}) collective-permute-start(bf16[128,512]{1,0:T(8,128)(2,1)S(1)} %slice.483), channel_id=1, source_target_pairs={{0,8},{4,12},{8,0},{12,4},{1,9},{5,13},{9,1},{13,5},{2,10},{6,14},... | collective-permute-start | bytes 393224 | tf_op jit(solution)/shard_map/ppermute | solution.py:730
  621.8 38.2 %collective-permute-start.47 = (bf16[512,1024]{1,0:T(8,128)(2,1)S(1)}, bf16[512,1024]{1,0:T(8,128)(2,1)S(1)}, u32[]{:S(2)}, u32[]{:S(2)}) collective-permute-start(bf16[512,1024]{1,0:T(8,128)(2,1)S(1)} %get-tuple-element.112), channel_id=1, source_target_pairs={{0,4},{4,0},{8,12},{12,8},{1,5},{5,1},{9,13},{13,9},{2,6},{6,2},{1... | collective-permute-start | bytes 3145736 | tf_op jit(solution)/shard_map/ppermute | solution.py:730
  624.9 11.2 %collective-permute-start.56 = (bf16[512,384]{1,0:T(8,128)(2,1)S(1)}, bf16[512,384]{1,0:T(8,128)(2,1)S(1)}, u32[]{:S(2)}, u32[]{:S(2)}) collective-permute-start(bf16[512,384]{1,0:T(8,128)(2,1)S(1)} %slice.476), channel_id=1, source_target_pairs={{0,8},{4,12},{8,0},{12,4},{1,9},{5,13},{9,1},{13,5},{2,10},{6,14},... | collective-permute-start | bytes 1179656 | tf_op jit(solution)/shard_map/ppermute | solution.py:730
  634.0 15.5 %collective-permute-start.55 = (bf16[512,384]{1,0:T(8,128)(2,1)S(1)}, bf16[512,384]{1,0:T(8,128)(2,1)S(1)}, u32[]{:S(2)}, u32[]{:S(2)}) collective-permute-start(bf16[512,384]{1,0:T(8,128)(2,1)S(1)} %slice.477), channel_id=1, source_target_pairs={{0,8},{4,12},{8,0},{12,4},{1,9},{5,13},{9,1},{13,5},{2,10},{6,14},... | collective-permute-start | bytes 1179656 | tf_op jit(solution)/shard_map/ppermute | solution.py:730
  638.1 29.5 %collective-permute-start.54 = (bf16[512,384]{1,0:T(8,128)(2,1)}, bf16[512,384]{1,0:T(8,128)(2,1)}, u32[]{:S(2)}, u32[]{:S(2)}) collective-permute-start(bf16[512,384]{1,0:T(8,128)(2,1)} %slice.478), channel_id=1, source_target_pairs={{0,8},{4,12},{8,0},{12,4},{1,9},{5,13},{9,1},{13,5},{2,10},{6,14},... | collective-permute-start | bytes 1179656 | tf_op jit(solution)/shard_map/ppermute | solution.py:730
  641.5 13.4 %collective-permute-start.57 = (bf16[512,384]{1,0:T(8,128)(2,1)S(1)}, bf16[512,384]{1,0:T(8,128)(2,1)S(1)}, u32[]{:S(2)}, u32[]{:S(2)}) collective-permute-start(bf16[512,384]{1,0:T(8,128)(2,1)S(1)} %fusion.29), channel_id=1, source_target_pairs={{0,3},{1,0},{2,1},{3,2},{4,7},{5,4},{6,5},{7,6},{8,11},{9,8},{10,9... | collective-permute-start | bytes 1179656 | tf_op jit(solution)/shard_map/ppermute | solution.py:735
  647.6 32.9 %collective-permute-start.53 = (bf16[512,384]{1,0:T(8,128)(2,1)}, bf16[512,384]{1,0:T(8,128)(2,1)}, u32[]{:S(2)}, u32[]{:S(2)}) collective-permute-start(bf16[512,384]{1,0:T(8,128)(2,1)} %slice.479), channel_id=1, source_target_pairs={{0,8},{4,12},{8,0},{12,4},{1,9},{5,13},{9,1},{13,5},{2,10},{6,14},... | collective-permute-start | bytes 1179656 | tf_op jit(solution)/shard_map/ppermute | solution.py:730
  649.5 47.1 %collective-permute-start.68 = (f32[128,256]{1,0:T(8,128)}, f32[128,256]{1,0:T(8,128)}, u32[]{:S(2)}, u32[]{:S(2)}) collective-permute-start(f32[128,256]{1,0:T(8,128)} %slice_select_fusion.2), channel_id=1, source_target_pairs={{0,4},{4,0},{8,12},{12,8},{1,5},{5,1},{9,13},{13,9},{2,6},{6,2},{1... | collective-permute-start | bytes 393224 | tf_op jit(solution)/shard_map/ppermute | solution.py:730
  655.8 13.8 %collective-permute-start.58 = (bf16[512,384]{1,0:T(8,128)(2,1)}, bf16[512,384]{1,0:T(8,128)(2,1)}, u32[]{:S(2)}, u32[]{:S(2)}) collective-permute-start(bf16[512,384]{1,0:T(8,128)(2,1)} %fusion.33), channel_id=1, source_target_pairs={{0,3},{1,0},{2,1},{3,2},{4,7},{5,4},{6,5},{7,6},{8,11},{9,8},{10,9... | collective-permute-start | bytes 1179656 | tf_op jit(solution)/shard_map/ppermute | solution.py:735
  663.8 39.8 %all-to-all-start.2 = ((bf16[4,128,1024]{2,1,0:T(8,128)(2,1)}), bf16[4,128,1024]{2,1,0:T(8,128)(2,1)S(1)}, u32[]{:S(2)}, u32[]{:S(2)}) async-start(bf16[4,128,1024]{2,1,0:T(8,128)(2,1)} %bitcast.17), calls=%async_computation.2 | async-start | bytes 2097152 | tf_op jit(solution)/shard_map/all_to_all | solution.py:807
  671.1 24.0 %collective-permute-start.59 = (bf16[512,384]{1,0:T(8,128)(2,1)S(1)}, bf16[512,384]{1,0:T(8,128)(2,1)S(1)}, u32[]{:S(2)}, u32[]{:S(2)}) collective-permute-start(bf16[512,384]{1,0:T(8,128)(2,1)S(1)} %fusion.37), channel_id=1, source_target_pairs={{0,3},{1,0},{2,1},{3,2},{4,7},{5,4},{6,5},{7,6},{8,11},{9,8},{10,9... | collective-permute-start | bytes 1179656 | tf_op jit(solution)/shard_map/ppermute | solution.py:735
  680.5 17.1 %collective-permute-start.51 = (f32[4,1024]{1,0:T(4,128)S(1)}, f32[4,1024]{1,0:T(4,128)S(1)}, u32[]{:S(2)}, u32[]{:S(2)}) collective-permute-start(f32[4,1024]{1,0:T(4,128)S(1)} %add.199), channel_id=1, source_target_pairs={{0,1},{1,0},{2,3},{3,2},{4,5},{5,4},{6,7},{7,6},{8,9},{9,8},{10,11... | collective-permute-start | bytes 49160 | tf_op jit(solution)/shard_map/ppermute | solution.py:757
  (177 other events, 3841.6 us)

commit v3 on v2

--- a/solution.py
+++ b/solution.py
@@ -495,16 +495,18 @@
     other_ref[...] = total[half:].astype(jnp.bfloat16)
 
 
-def into_model_kernel(pieces, left_ref, *refs):
+def into_model_kernel(lefts, pieces, *refs):
+    left, refs = side_by_side(refs[:lefts]), refs[lefts:]
     owns, others = refs[:pieces], refs[pieces : 2 * pieces]
     weight = jnp.concatenate([stacked_up(owns), stacked_up(others)], axis=1)
-    split_rows(dot_nn(left_ref[...], weight), *refs[2 * pieces :])
-
-
-def back_to_model_kernel(pieces, left_ref, *refs):
+    split_rows(dot_nn(left, weight), *refs[2 * pieces :])
+
+
+def back_to_model_kernel(lefts, pieces, *refs):
+    left, refs = side_by_side(refs[:lefts]), refs[lefts:]
     owns, others = refs[:pieces], refs[pieces : 2 * pieces]
     weight = jnp.concatenate([side_by_side(owns), side_by_side(others)], axis=0)
-    split_rows(dot_nt(left_ref[...], weight), *refs[2 * pieces :])
+    split_rows(dot_nt(left, weight), *refs[2 * pieces :])
 
 
 def gelu_both(up_act):
@@ -698,11 +700,11 @@
     )
 
 
-def attend_back(core, tables, rows, pieces, q, k, v, lse):
+def attend_back(core, tables, rows, pieces, base, q, k, v, lse):
     half, features = rows[0].shape
     length, count = 2 * half, len(pieces[0])
-    lanes = pl.BlockSpec((1, length, 128), lambda j: (j, 0, 0))
-    lse_spec = pl.BlockSpec((1, 2, length), lambda j: (j, 0, 0))
+    lanes = pl.BlockSpec((1, length, 128), lambda j: (base + j, 0, 0))
+    lse_spec = pl.BlockSpec((1, 2, length), lambda j: (base + j, 0, 0))
     out = ((length, count * 384), jnp.bfloat16, pl.BlockSpec((length, 384), lambda j: (0, j)))
     return by_pairs(
         attend_back_kernel,
@@ -716,12 +718,12 @@
     )[0]
 
 
-def model_rows(kernel, name, left, pieces):
+def model_rows(kernel, name, lefts, pieces):
     owns, others = pieces
-    length, width = left.shape[0], 2 * owns[0].shape[kernel is into_model_kernel]
+    length, width = lefts[0].shape[0], 2 * owns[0].shape[kernel is into_model_kernel]
     outs = (((length // 2, width), jnp.float32), ((length // 2, width), jnp.bfloat16))
-    kernel = functools.partial(kernel, len(owns))
-    own, other = on_chip(kernel, name, outs, left, *owns, *others)
+    kernel = functools.partial(kernel, len(lefts), len(owns))
+    own, other = on_chip(kernel, name, outs, *lefts, *owns, *others)
     return own, flip_pairs(other, 1)
 
 
@@ -733,20 +735,6 @@
 def passed_on(block, step):
     size = lax.axis_size("tensor")
     return lax.ppermute(block, "tensor", [(i, (i + step) % size) for i in range(size)])
-
-
-def spread(piece):
-    pieces = [piece]
-    for _ in range(lax.axis_size("tensor") - 1):
-        pieces.append(passed_on(pieces[-1], 1))
-    return pieces
-
-
-def collected(pieces):
-    total = pieces[-1]
-    for piece in reversed(pieces[:-1]):
-        total = piece + passed_on(total.astype(jnp.bfloat16), -1).astype(jnp.float32)
-    return total
 
 
 def summed_everywhere(value):
@@ -758,8 +746,13 @@
     return value
 
 
-def after(values, token):
-    return lax.optimization_barrier((values, token))[0]
+class Sequence:
+    def __init__(self, token):
+        self.token = token
+
+    def step(self, *values):
+        values, self.token = lax.optimization_barrier((values, self.token))
+        return values[0] if len(values) == 1 else values
 
 
 def per_chip(
@@ -811,32 +804,67 @@
         pair = ordered(mine, flip_pairs(other, 1))
         return jnp.stack(pair, axis=1).reshape((micro, row_count) + block.shape[2:])
 
-    group_count = group_weights.shape[0]
-    matches = group_ids[..., None] == jnp.arange(group_count, dtype=jnp.int32)
-    row_scale = jnp.sum(jnp.where(matches, group_weights, 0.0), axis=-1)
-    weighted = (out_cotangent.astype(jnp.float32) * row_scale[..., None]).astype(jnp.bfloat16)
-    start = to_chip(own_first(jnp.where(first, inputs, weighted))).reshape(half, width)
-
     def columns(local):
         size = local.shape[-1] // 2
         mid = (0,) * (local.ndim - 2)
         piece = lax.dynamic_slice(
             local, (wide_half * upper, *mid, size * core), (wide_half, *local.shape[1:-1], size)
         )
-        pieces = spread(piece.reshape(wide_half, -1))
-        return pieces, [flip_pairs(piece, 2) for piece in pieces]
+        return piece.reshape(wide_half, -1)
 
     def rows(local):
         size = local.shape[0] // 2
-        pieces = spread(
-            lax.dynamic_slice(local, (size * core, wide_half * upper), (size, wide_half))
-        )
-        return pieces, [flip_pairs(piece, 2) for piece in pieces]
-
-    w_qkv = columns(qkv_weight[0])
-    w_out = rows(out_weight[0])
-    w_up = columns(up_weight[0])
-    w_down = rows(down_weight[0])
+        return lax.dynamic_slice(local, (size * core, wide_half * upper), (size, wide_half))
+
+    core_word = core.astype(jnp.int32).reshape(1)
+    order = Sequence(core_word)
+    pieces = {
+        "qkv": [columns(qkv_weight[0])],
+        "out": [rows(out_weight[0])],
+        "up": [columns(up_weight[0])],
+        "down": [rows(down_weight[0])],
+    }
+    flown = {name: [] for name in pieces}
+    ringing = {}
+
+    def flip(name):
+        flown[name].append(flip_pairs(order.step(pieces[name][-1]), 2))
+
+    def ring(name):
+        ringing[name] = passed_on(order.step(pieces[name][-1]), 1)
+
+    def caught(name):
+        pieces[name].append(order.step(ringing.pop(name)))
+        flip(name)
+
+    def whole(name):
+        flown[name] = list(order.step(*flown[name]))
+        return pieces[name], flown[name]
+
+    group_count = group_weights.shape[0]
+    matches = group_ids[..., None] == jnp.arange(group_count, dtype=jnp.int32)
+    row_scale = jnp.sum(jnp.where(matches, group_weights, 0.0), axis=-1)
+    weighted = (out_cotangent.astype(jnp.float32) * row_scale[..., None]).astype(jnp.bfloat16)
+    ring("qkv")
+    flip("qkv")
+    ring("out")
+    flip("out")
+    start = to_chip(own_first(jnp.where(first, inputs, weighted))).reshape(half, width)
+    flip("up")
+    caught("qkv")
+    ring("qkv")
+    caught("out")
+    ring("out")
+    flip("down")
+    caught("out")
+    ring("out")
+    caught("qkv")
+    ring("qkv")
+    ring("up")
+    caught("out")
+    ring("down")
+    start = order.step(start)
+    caught("qkv")
     gain = own_first(gains[0])
 
     turns = jnp.arange(half, dtype=jnp.int32)
@@ -849,40 +877,52 @@
         jnp.concatenate([cos_part] * 4, axis=1),
         jnp.concatenate([-sin_part, sin_part] * 2, axis=1),
     )
-    core_word = core.astype(jnp.int32).reshape(1)
-    units = tensor * w_up[0][0].shape[1]
+    units = tensor * pieces["up"][0].shape[1]
     row32, row16 = ((half, width), jnp.float32), ((half, width), jnp.bfloat16)
     unit16 = ((length, units), jnp.bfloat16)
     sum32 = ((1, width), jnp.float32)
 
-    def forward(layer_input):
+    def forward(layer_input, between=None):
+        pause = between or (lambda: None)
         attn_in = both_rows(on_chip(norm_in_kernel, "norm_in", (row16,), gain, layer_input)[0])
-        *heads, mixed = attend(core_word, tables, attn_in, w_qkv)
-        parts = model_rows(into_model_kernel, "attn_out", mixed, w_out)
+        pause()
+        *heads, mixed = attend(core_word, tables, order.step(*attn_in), weights["qkv"])
+        mixed = order.step(mixed)
+        pause()
+        parts = model_rows(into_model_kernel, "attn_out", [mixed], weights["out"])
         branch, hidden, mlp_in = on_chip(
             after_attention_kernel, "after_attn", (row32, row32, row16), gain, layer_input, *parts
         )
-        mlp_in = both_rows(mlp_in)
+        mlp_in = both_rows(order.step(mlp_in))
+        pause()
         kernel = functools.partial(mlp_up_kernel, tensor)
         gelu_out, slope = on_chip(
-            kernel, "mlp_up", (unit16, unit16), *mlp_in, *w_up[0], *w_up[1]
+            kernel, "mlp_up", (unit16, unit16), *mlp_in, *weights["up"][0], *weights["up"][1]
         )
-        parts = model_rows(into_model_kernel, "mlp_down", gelu_out, w_down)
+        gelu_out = order.step(gelu_out)
+        pause()
+        parts = model_rows(into_model_kernel, "mlp_down", [gelu_out], weights["down"])
         mlp_branch, result = on_chip(
             after_mlp_kernel, "after_mlp", (row32, row16), gain, hidden, *parts
         )
         saved = (layer_input, heads, branch, hidden, slope, mlp_branch)
         return result, saved, (attn_in, mixed, mlp_in, gelu_out)
 
-    def backward(grad, saved):
+    def backward(grad, saved, between=None):
+        pause = between or (lambda **new: None)
         layer_input, heads, branch, hidden, slope, mlp_branch = saved
         d_down, sum_three = on_chip(
             into_mlp_back_kernel, "into_mlp_back", (row16, sum32), gain, grad, mlp_branch
         )
         d_down = both_rows(d_down)
         kernel = functools.partial(mlp_up_back_kernel, tensor)
-        d_up = on_chip(kernel, "mlp_up_back", (unit16,), *d_down, slope, *w_down[0], *w_down[1])[0]
-        parts = model_rows(back_to_model_kernel, "mlp_back", d_up, w_up)
+        d_up = on_chip(
+            kernel, "mlp_up_back", (unit16,), *d_down, slope, *weights["down"][0], *weights["down"][1]
+        )[0]
+        pause(d_down=d_down)
+        d_up = order.step(d_up)
+        parts = model_rows(back_to_model_kernel, "mlp_back", [d_up], weights["up"])
+        pause(d_up=d_up)
         d_hidden, d_attn, sum_one, sum_two = on_chip(
             into_attention_back_kernel,
             "into_attn_back",
@@ -893,22 +933,50 @@
             hidden,
             branch,
         )
-        d_attn = both_rows(d_attn)
-        d_qkv = attend_back(core_word, tables, d_attn, w_out, *heads)
-        parts = model_rows(back_to_model_kernel, "attn_back", d_qkv, w_qkv)
+        d_attn = both_rows(order.step(d_attn))
+        pause(d_attn=d_attn)
+        d_qkv = []
+        for base in range(0, tensor, 2):
+            some = [side[base : base + 2] for side in weights["out"]]
+            rows_now = order.step(*d_attn)
+            d_qkv.append(attend_back(core_word, tables, rows_now, some, base, *heads))
+            d_qkv[-1] = order.step(d_qkv[-1])
+            pause(d_qkv=d_qkv[-1])
+        parts = model_rows(back_to_model_kernel, "attn_back", d_qkv, weights["qkv"])
         d_input, sum_zero = on_chip(
             out_of_layer_kernel, "out_of_layer", (row16, sum32), gain, layer_input, *parts, d_hidden
         )
         sums = jnp.concatenate([sum_zero, sum_one, sum_two, sum_three])
-        return d_input, (d_qkv, d_attn, d_up, d_down), sums
-
-    low_zero, saved_zero, lefts_zero = forward(start)
+        return order.step(d_input), (d_qkv, d_attn, d_up, d_down), sums
+
+    weights = {}
+
+    def arrivals():
+        caught("up")
+        ring("up")
+        caught("down")
+        ring("down")
+        weights["qkv"] = whole("qkv")
+        yield
+        caught("up")
+        ring("up")
+        caught("down")
+        ring("down")
+        weights["out"] = whole("out")
+        yield
+        caught("up")
+        caught("down")
+        weights["up"] = whole("up")
+        yield
+        weights["down"] = whole("down")
+        yield
+
+    steps = arrivals()
+    low_zero, saved_zero, lefts_zero = forward(start, lambda: next(steps))
+    low_zero = order.step(low_zero)
     low_one, saved_one, lefts_one = forward(shifted(low_zero, "section", 1))
     grad_one, rights_one, gain_one = backward(start, saved_one)
-    lows = after((low_zero, low_one), grad_one)
-    outputs = from_chip(own_first(jnp.where(first, *lows)).reshape(tensor, part, width))
-    grad_zero, rights_zero, gain_zero = backward(shifted(grad_one, "section", -1), saved_zero)
-    grads = from_chip(own_first(jnp.where(first, grad_zero, grad_one)).reshape(tensor, part, width))
+    received = shifted(grad_one, "section", -1)
 
     def joined(pair):
         return lax.optimization_barrier(jnp.concatenate(pair, axis=0))
@@ -918,32 +986,93 @@
             zero, one = joined(zero), joined(one)
         return jnp.where(first, zero, one)
 
+    lows = order.step(low_zero, low_one)
+    outputs = from_chip(own_first(jnp.where(first, *lows)).reshape(tensor, part, width))
+    lefts_zero, lefts_one = order.step(lefts_zero, lefts_one)
     attn_in, mixed, mlp_in, gelu_out = map(own_layer, lefts_zero, lefts_one)
-    d_qkv, d_attn, d_up, d_down = map(own_layer, rights_zero, rights_one)
-
-    def halves(total, axis):
+    attn_in, mixed, mlp_in, gelu_out = order.step(attn_in, mixed, mlp_in, gelu_out)
+    received = order.step(received)
+
+    sums = {name: [None] * tensor for name in pieces}
+    moving = {}
+
+    def halves(name, j, total, axis):
         own = lax.slice_in_dim(total, 0, wide_half, axis=axis)
         other = lax.slice_in_dim(total, wide_half, width, axis=axis).astype(jnp.bfloat16)
-        return own + flip_pairs(other, 2).astype(jnp.float32)
-
-    def sum_columns(left, right):
-        size = right.shape[1] // tensor
-        pieces = [None] * tensor
-        for j in reversed(range(tensor)):
-            pieces[j] = halves(contract(left, right[:, j * size : (j + 1) * size]), 0)
-        return collected(pieces)
-
-    def sum_rows(left, right):
-        size = left.shape[1] // tensor
-        pieces = [None] * tensor
-        for j in reversed(range(tensor)):
-            pieces[j] = halves(contract(left[:, j * size : (j + 1) * size], right), 1)
-        return collected(pieces)
-
-    down_sum = sum_rows(gelu_out, d_down)
-    up_sum = sum_columns(mlp_in, d_up)
-    out_sum = sum_rows(mixed, d_attn)
-    qkv_sum = sum_columns(attn_in, d_qkv)
+        own, other = order.step(own, other)
+        sums[name][j] = (own, flip_pairs(other, 2))
+
+    def column_piece(name, j, left, right):
+        halves(name, j, contract(*order.step(left, right)), 0)
+
+    def row_piece(name, j, left, right):
+        halves(name, j, contract(*order.step(left, right)), 1)
+
+    def gathered(name, j):
+        own, other = sums[name][j]
+        total = own + order.step(other).astype(jnp.float32)
+        if name in moving:
+            total = total + order.step(moving.pop(name)).astype(jnp.float32)
+        if j == 0:
+            sums[name] = total
+        else:
+            moving[name] = passed_on(order.step(total.astype(jnp.bfloat16)), -1)
+
+    def block(array, j, count=tensor):
+        size = array.shape[1] // count
+        return array[:, j * size : (j + 1) * size]
+
+    new_one = {"d_qkv": list(rights_one[0]), "d_attn": rights_one[1], "d_up": rights_one[2]}
+    new_one["d_down"] = rights_one[3]
+    order_back = list(reversed(range(tensor)))
+
+    def departures():
+        new = yield
+        d_down = own_layer(new["d_down"], new_one["d_down"])
+        for j in order_back:
+            row_piece("down", j, block(gelu_out, j), d_down)
+        new = yield
+        d_up = own_layer(new["d_up"], new_one["d_up"])
+        for j in order_back:
+            column_piece("up", j, mlp_in, block(d_up, j))
+        new = yield
+        d_attn = own_layer(new["d_attn"], new_one["d_attn"])
+        gathered("down", 3)
+        new = yield
+        upper_pairs = []
+        for half_pairs in range(2):
+            d_qkv = own_layer(new["d_qkv"], new_one["d_qkv"][half_pairs])
+            upper_pairs.append(d_qkv)
+            if half_pairs == 0:
+                gathered("down", 2)
+                gathered("up", 3)
+                new = yield
+        gathered("down", 1)
+        gathered("up", 2)
+        for j in order_back:
+            column_piece("qkv", j, attn_in, block(upper_pairs[j // 2], j % 2, 2))
+        for j in order_back:
+            row_piece("out", j, block(mixed, j), d_attn)
+        yield
+
+    leaving = departures()
+    next(leaving)
+    grad_zero, rights_zero, gain_zero = backward(
+        received, saved_zero, lambda **new: leaving.send(new)
+    )
+    gathered("down", 0)
+    gathered("up", 1)
+    gathered("qkv", 3)
+    gathered("up", 0)
+    gathered("qkv", 2)
+    gathered("out", 3)
+    gathered("qkv", 1)
+    gathered("out", 2)
+    gathered("qkv", 0)
+    gathered("out", 1)
+    gathered("out", 0)
+    down_sum, up_sum, out_sum, qkv_sum = (sums[name] for name in ("down", "up", "out", "qkv"))
+    grads = from_chip(own_first(jnp.where(first, grad_zero, grad_one)).reshape(tensor, part, width))
 
     def by_columns(kept, count):
         size = kept.shape[1]

time: 722 us -> 770 us (1.066)
  waiting for transfers between devices: 261 us -> 311 us
  local copies, waits for them, and re-layouts: 59.7 us -> 77.7 us
  starting transfers between devices: 112 us -> 101 us
  Pallas kernels: 188 us -> 196 us
    ppermute x57, waiting for transfers between devices: 93.7 us -> 127 us  [flip_pairs(): return lax.ppermute(block, 'dp', [(i, i ^ distance) for i in range(size)])]
    ppermute x24, waiting for transfers between devices: 120 us -> 140 us  [passed_on(): lax.ppermute(block, 'tensor', [(i, (i + step) % size) for i in range(size)])]
    unnamed x308 -> x386, local copies, waits for them, and re-layouts: 38.7 us -> 52 us
    all_to_all x1, waiting for transfers between devices: 9.01 us -> 0.01 us  [to_chip(): lax.all_to_all(jnp.concatenate(ordered(mine, flip_pairs(other, 1))), 'ten...]
    pallas_call x4 -> x6, Pallas kernels: 82.1 us -> 85 us  [by_pairs(): pl.pallas_call(functools.partial(kernel, len(pieces[0])), grid=(len(piece...]
  transfers between devices with their start and end apart: 88 -> 88, of which waited for: 41 -> 41; matrix products, arithmetic and copies ran while one was open for 14% -> 11% of each run, Pallas kernels for 13% -> 12%
where the time goes in v3:
time: 770 us; the launch traced here: 761 us
  waiting for transfers between devices  311 us (40%)
  Pallas kernels  196 us (25%)
  starting transfers between devices  101 us (13%)
  local copies, waits for them, and re-layouts  77.7 us (10%)
  other arithmetic  54.4 us (7%)
  matrix products  17.4 us (2%)
    ppermute x24, waiting for transfers between devices, passed_on(): lax.ppermute(block, 'tensor', [(i, (i + step) % size) for i in range(size)])  140 us
    ppermute x57, waiting for transfers between devices, flip_pairs(): return lax.ppermute(block, 'dp', [(i, i ^ distance) for i in range(size)])  127 us
    pallas_call x24, Pallas kernels, on_chip(): pl.pallas_call(kernel, in_specs=[space] * len(operands), out_specs=[space...  111 us
    pallas_call x6, Pallas kernels, by_pairs(): pl.pallas_call(functools.partial(kernel, len(pieces[0])), grid=(len(piece...  85 us
    unnamed x386, local copies, waits for them, and re-layouts  52 us
    ppermute x24, starting transfers between devices, passed_on(): lax.ppermute(block, 'tensor', [(i, (i + step) % size) for i in range(size)])  45.6 us
    ppermute x2, waiting for transfers between devices, shifted(): return lax.ppermute(block, axis, route)  36.5 us
    ppermute x57, starting transfers between devices, flip_pairs(): return lax.ppermute(block, 'dp', [(i, i ^ distance) for i in range(size)])  34.5 us
  transfers between devices with their start and end apart: 88, of which 41 were waited for; matrix products, arithmetic and copies ran while one was open for 11% of the time, Pallas kernels for 12%

profile of v3, /device:TPU:0, one launch (start us, length us, event | category | flops | bytes accessed | tf_op | source)
XLA Modules:
  0.0 760.6 jit_solution(14122791513090264565)
XLA Ops:
  11.1 6.2 all-to-all-start
  22.1 25.0 %collective-permute-done.2.refs_1_.refs_3_ = bf16[512,384]{1,0:T(8,128)(2,1)S(1)} collective-permute-done((bf16[512,384]{1,0:T(8,128)(2,1)S(1)}, bf16[512,384]{1,0:T(8,128)(2,1)S(1)}, u32[]{:S(2)}, u32[]{:S(2)}) %collective-permute-start.2) | collective-permute-done | bytes 393248 | tf_op jit(solution)/shard_map/ppermute | solution.py:737
  47.2 3.3 collective-permute-start.5
  52.9 9.0 %collective-permute-done.1.refs_2_.refs_1_ = bf16[128,512]{1,0:T(8,128)(2,1)S(1)} collective-permute-done((bf16[128,512]{1,0:T(8,128)(2,1)S(1)}, bf16[128,512]{1,0:T(8,128)(2,1)S(1)}, u32[]{:S(2)}, u32[]{:S(2)}) %collective-permute-start.1) | collective-permute-done | bytes 131104 | tf_op jit(solution)/shard_map/ppermute | solution.py:737
  63.3 5.4 collective-permute-done.3.refs_3_.refs_0_
  71.2 5.7 collective-permute-done.4.refs_4_.refs_1_
  86.9 9.7 %collective-permute-done.13.refs_1_.refs_2_ = bf16[512,512]{1,0:T(8,128)(2,1)} collective-permute-done((bf16[512,512]{1,0:T(8,128)(2,1)S(1)}, bf16[512,512]{1,0:T(8,128)(2,1)}, u32[]{:S(2)}, u32[]{:S(2)}) %collective-permute-start.13) | collective-permute-done | bytes 524320 | tf_op jit(solution)/shard_map/ppermute | solution.py:737
  98.3 9.6 %collective-permute-done.12.refs_2_.refs_1_ = bf16[512,512]{1,0:T(8,128)(2,1)} collective-permute-done((bf16[512,512]{1,0:T(8,128)(2,1)S(1)}, bf16[512,512]{1,0:T(8,128)(2,1)}, u32[]{:S(2)}, u32[]{:S(2)}) %collective-permute-start.12) | collective-permute-done | bytes 524320 | tf_op jit(solution)/shard_map/ppermute | solution.py:737
  109.5 3.1 fusion.7
  113.8 5.9 collective-permute-done.11.refs_7_.refs_9_
  130.9 16.7 %attend.2 = (bf16[4,1024,128]{2,1,0:T(8,128)(2,1)S(1)}, bf16[4,1024,128]{2,1,0:T(8,128)(2,1)S(1)}, bf16[4,1024,128]{2,1,0:T(8,128)(2,1)S(1)}, f32[4,2,1024]{2,1,0:T(2,128)S(1)}, bf16[1024,512]{1,0:T(8,128)(2,1)S(1)}) custom-call(s32[1]{0:T(128)} %bitcast.8.core_ref, f32[1024,128]{1,0:T(8,128)S(1)} %pad_maximum_fusion.11.cos_ref, ...), custom_call_target="tpu_custom_call" | custom-call | tf_op jit(solution)/shard_map/attend/pallas_call | solution.py:671
  150.2 3.2 attn_out.2
  156.1 3.4 after_attn.2
  162.7 7.3 collective-permute-done.22.refs_3_.refs_4_
  170.5 10.3 %collective-permute-done.27.refs_4_.refs_3_ = bf16[512,512]{1,0:T(8,128)(2,1)S(1)} collective-permute-done((bf16[512,512]{1,0:T(8,128)(2,1)}, bf16[512,512]{1,0:T(8,128)(2,1)S(1)}, u32[]{:S(2)}, u32[]{:S(2)}) %collective-permute-start.27) | collective-permute-done | bytes 524320 | tf_op jit(solution)/shard_map/ppermute | solution.py:737
  183.3 8.3 %collective-permute-done.25.refs_6_.refs_7_ = bf16[512,512]{1,0:T(8,128)(2,1)S(1)} collective-permute-done((bf16[512,512]{1,0:T(8,128)(2,1)S(1)}, bf16[512,512]{1,0:T(8,128)(2,1)S(1)}, u32[]{:S(2)}, u32[]{:S(2)}) %collective-permute-start.25) | collective-permute-done | bytes 524320 | tf_op jit(solution)/shard_map/ppermute | solution.py:732
  192.1 10.7 %collective-permute-done.26.refs_7_.refs_8_ = bf16[512,512]{1,0:T(8,128)(2,1)S(1)} collective-permute-done((bf16[512,512]{1,0:T(8,128)(2,1)S(1)}, bf16[512,512]{1,0:T(8,128)(2,1)S(1)}, u32[]{:S(2)}, u32[]{:S(2)}) %collective-permute-start.26) | collective-permute-done | bytes 524320 | tf_op jit(solution)/shard_map/ppermute | solution.py:732
  203.4 11.2 %mlp_up.2 = (bf16[1024,2048]{1,0:T(8,128)(2,1)S(1)}, bf16[1024,2048]{1,0:T(8,128)(2,1)}) custom-call(bf16[512,1024]{1,0:T(8,128)(2,1)S(1)} %get-tuple-element.543.own_rows, bf16[512,1024]{1,0:T(8,128)(2,1)S(1)} %collective-permute-done.21.other_rows, bf16[512,512]{1,0:T(8,128)(2,1)S(1)} %get-tuple-element.455.refs_0_.refs_1_, ...), custom_call_target="tpu_custom_call" | custom-call | tf_op jit(solution)/shard_map/mlp_up/pallas_call | solution.py:656
  214.6 10.7 %collective-permute-done.29.refs_6_.refs_5_ = bf16[512,512]{1,0:T(8,128)(2,1)S(1)} collective-permute-done((bf16[512,512]{1,0:T(8,128)(2,1)}, bf16[512,512]{1,0:T(8,128)(2,1)S(1)}, u32[]{:S(2)}, u32[]{:S(2)}) %collective-permute-start.29) | collective-permute-done | bytes 524320 | tf_op jit(solution)/shard_map/ppermute | solution.py:732
  225.3 11.2 %collective-permute-done.30.refs_7_.refs_6_ = bf16[512,512]{1,0:T(8,128)(2,1)S(1)} collective-permute-done((bf16[512,512]{1,0:T(8,128)(2,1)}, bf16[512,512]{1,0:T(8,128)(2,1)S(1)}, u32[]{:S(2)}, u32[]{:S(2)}) %collective-permute-start.30) | collective-permute-done | bytes 524320 | tf_op jit(solution)/shard_map/ppermute | solution.py:732
  236.6 10.1 %collective-permute-done.31.refs_8_.refs_7_ = bf16[512,512]{1,0:T(8,128)(2,1)S(1)} collective-permute-done((bf16[512,512]{1,0:T(8,128)(2,1)S(1)}, bf16[512,512]{1,0:T(8,128)(2,1)S(1)}, u32[]{:S(2)}, u32[]{:S(2)}) %collective-permute-start.31) | collective-permute-done | bytes 524320 | tf_op jit(solution)/shard_map/ppermute | solution.py:732
  246.7 5.9 mlp_down.2
  257.3 3.8 collective-permute-start.33
  261.1 22.2 %collective-permute-done.33.rows_ref = bf16[512,1024]{1,0:T(8,128)(2,1)S(1)} collective-permute-done((bf16[512,1024]{1,0:T(8,128)(2,1)S(1)}, bf16[512,1024]{1,0:T(8,128)(2,1)S(1)}, u32[]{:S(2)}, u32[]{:S(2)}) %collective-permute-start.33) | collective-permute-done | bytes 1048608 | tf_op jit(solution)/shard_map/ppermute | solution.py:23
  287.9 16.7 %attend.3 = (bf16[4,1024,128]{2,1,0:T(8,128)(2,1)S(1)}, bf16[4,1024,128]{2,1,0:T(8,128)(2,1)S(1)}, bf16[4,1024,128]{2,1,0:T(8,128)(2,1)S(1)}, f32[4,2,1024]{2,1,0:T(2,128)S(1)}, bf16[1024,512]{1,0:T(8,128)(2,1)S(1)}) custom-call(s32[1]{0:T(128)} %bitcast.8.core_ref, f32[1024,128]{1,0:T(8,128)S(1)} %pad_maximum_fusion.11.cos_ref, ...), custom_call_target="tpu_custom_call" | custom-call | tf_op jit(solution)/shard_map/attend/pallas_call | solution.py:671
  305.7 3.0 attn_out.3
  312.3 3.4 after_attn.3
  321.1 11.1 %mlp_up.3 = (bf16[1024,2048]{1,0:T(8,128)(2,1)S(1)}, bf16[1024,2048]{1,0:T(8,128)(2,1)}) custom-call(bf16[512,1024]{1,0:T(8,128)(2,1)S(1)} %get-tuple-element.545.own_rows, bf16[512,1024]{1,0:T(8,128)(2,1)S(1)} %collective-permute-done.36.other_rows, bf16[512,512]{1,0:T(8,128)(2,1)S(1)} %get-tuple-element.455.refs_0_.refs_1_, ...), custom_call_target="tpu_custom_call" | custom-call | tf_op jit(solution)/shard_map/mlp_up/pallas_call | solution.py:656
  332.3 6.5 mlp_down.3
  351.5 7.4 mlp_up_back.2.refs_0_
  359.0 6.1 mlp_back.2
  372.3 3.9 into_attn_back.2
  380.3 12.6 %attend_back.4.refs_0_ = bf16[1024,768]{1,0:T(8,128)(2,1)S(1)} custom-call(s32[1]{0:T(128)} %bitcast.8.core_ref, f32[1024,128]{1,0:T(8,128)S(1)} %pad_maximum_fusion.11.cos_ref, f32[1024,128]{1,0:T(8,128)S(1)} %pad_maximum_fusion.12.sin_ref, bf16[512,1024]{1,0:T(8,128)(2,1)S(1)} %get-tuple-element.523.own_rows, ...), custom_call_target="tpu_custom_call" | custom-call | tf_op jit(solution)/shard_map/attend_back/pallas_call | solution.py:671
  393.0 13.0 %attend_back.5.refs_1_ = bf16[1024,768]{1,0:T(8,128)(2,1)S(1)} custom-call(s32[1]{0:T(128)} %bitcast.8.core_ref, f32[1024,128]{1,0:T(8,128)S(1)} %pad_maximum_fusion.11.cos_ref, f32[1024,128]{1,0:T(8,128)S(1)} %pad_maximum_fusion.12.sin_ref, bf16[512,1024]{1,0:T(8,128)(2,1)S(1)} %get-tuple-element.523.own_rows, ...), custom_call_target="tpu_custom_call" | custom-call | tf_op jit(solution)/shard_map/attend_back/pallas_call | solution.py:671
  406.1 5.4 attn_back.2
  416.5 3.2 pad_maximum_fusion
  421.2 5.0 all-to-all-start.1
  439.2 14.3 %collective-permute-done.43.grad_ref = bf16[512,1024]{1,0:T(8,128)(2,1)S(1)} collective-permute-done((bf16[512,1024]{1,0:T(8,128)(2,1)}, bf16[512,1024]{1,0:T(8,128)(2,1)S(1)}, u32[]{:S(2)}, u32[]{:S(2)}) %collective-permute-start.43) | collective-permute-done | bytes 1048608 | tf_op jit(solution)/shard_map/ppermute | solution.py:23
  453.5 3.5 into_mlp_back.3
  479.8 7.7 %mlp_up_back.3.refs_0_ = bf16[1024,2048]{1,0:T(8,128)(2,1)S(1)} custom-call(bf16[512,1024]{1,0:T(8,128)(2,1)} %get-tuple-element.553.own_rows, bf16[512,1024]{1,0:T(8,128)(2,1)} %collective-permute-done.44.other_rows, bf16[1024,2048]{1,0:T(8,128)(2,1)} %get-tuple-element.554.slope_ref, bf16[512,512]{1,0:T(8,128)(2,1)S(1)} %get-tuple-element.470.refs_1_.refs_0_, ...), custom_call_target="tpu_custom_call" | custom-call | tf_op jit(solution)/shard_map/mlp_up_back/pallas_call | solution.py:656
  487.6 5.7 mlp_back.3
  509.4 4.9 into_attn_back.3
  523.9 6.8 collective-permute-done.47
  531.4 3.6 collective-permute-start.50
  539.8 13.1 %attend_back.6.refs_0_ = bf16[1024,768]{1,0:T(8,128)(2,1)S(1)} custom-call(s32[1]{0:T(128)} %bitcast.8.core_ref, f32[1024,128]{1,0:T(8,128)S(1)} %pad_maximum_fusion.11.cos_ref, f32[1024,128]{1,0:T(8,128)S(1)} %pad_maximum_fusion.12.sin_ref, bf16[512,1024]{1,0:T(8,128)(2,1)} %get-tuple-element.625.own_rows, ...), custom_call_target="tpu_custom_call" | custom-call | tf_op jit(solution)/shard_map/attend_back/pallas_call | solution.py:671
  555.2 20.5 %collective-permute-done.48 = bf16[512,512]{1,0:T(8,128)(2,1)S(1)} collective-permute-done((bf16[512,512]{1,0:T(8,128)(2,1)S(1)}, bf16[512,512]{1,0:T(8,128)(2,1)S(1)}, u32[]{:S(2)}, u32[]{:S(2)}) %collective-permute-start.48) | collective-permute-done | bytes 524320 | tf_op jit(solution)/shard_map/ppermute | solution.py:732
  575.9 12.9 %attend_back.7.refs_1_ = bf16[1024,768]{1,0:T(8,128)(2,1)S(1)} custom-call(s32[1]{0:T(128)} %bitcast.8.core_ref, f32[1024,128]{1,0:T(8,128)S(1)} %pad_maximum_fusion.11.cos_ref, f32[1024,128]{1,0:T(8,128)S(1)} %pad_maximum_fusion.12.sin_ref, bf16[512,1024]{1,0:T(8,128)(2,1)} %get-tuple-element.625.own_rows, ...), custom_call_target="tpu_custom_call" | custom-call | tf_op jit(solution)/shard_map/attend_back/pallas_call | solution.py:671
  590.5 3.6 collective-permute-start.55
  595.9 19.9 %collective-permute-done.54 = bf16[512,512]{1,0:T(8,128)(2,1)S(1)} collective-permute-done((bf16[512,512]{1,0:T(8,128)(2,1)S(1)}, bf16[512,512]{1,0:T(8,128)(2,1)S(1)}, u32[]{:S(2)}, u32[]{:S(2)}) %collective-permute-start.54) | collective-permute-done | bytes 524320 | tf_op jit(solution)/shard_map/ppermute | solution.py:737
  628.8 4.8 collective-permute-done.78
  636.2 3.9 collective-permute-start.79
  641.7 4.9 attn_back.3
  647.3 5.0 collective-permute-start.67
  658.1 6.2 collective-permute-done.63
  666.1 2.8 collective-permute-done.61
  668.9 3.8 collective-permute-start.71
  673.1 3.8 collective-permute-start.81
  685.7 5.4 collective-permute-done.81
  691.8 3.2 collective-permute-done.58
  695.1 6.5 collective-permute-done.59
  702.9 4.3 all-to-all-start.2
  711.5 3.9 collective-permute-start.72
  717.7 17.6 %collective-permute-done.72 = bf16[512,384]{1,0:T(8,128)(2,1)S(1)} collective-permute-done((bf16[512,384]{1,0:T(8,128)(2,1)S(1)}, bf16[512,384]{1,0:T(8,128)(2,1)S(1)}, u32[]{:S(2)}, u32[]{:S(2)}) %collective-permute-start.72) | collective-permute-done | bytes 393248 | tf_op jit(solution)/shard_map/ppermute | solution.py:737
  739.1 11.1 %collective-permute-done.73 = bf16[512,384]{1,0:T(8,128)(2,1)S(1)} collective-permute-done((bf16[512,384]{1,0:T(8,128)(2,1)S(1)}, bf16[512,384]{1,0:T(8,128)(2,1)S(1)}, u32[]{:S(2)}, u32[]{:S(2)}) %collective-permute-start.73) | collective-permute-done | bytes 393248 | tf_op jit(solution)/shard_map/ppermute | solution.py:737
  (684 shorter events, 238.2 us)
Async XLA Ops:
  11.1 65.8 %all-to-all-start = ((bf16[4,128,1024]{2,1,0:T(8,128)(2,1)}), bf16[4,128,1024]{2,1,0:T(8,128)(2,1)S(1)}, u32[]{:S(2)}, u32[]{:S(2)}) async-start(bf16[4,128,1024]{2,1,0:T(8,128)(2,1)} %pad_maximum_fusion.8), calls=%async_computation | async-start | bytes 2097152 | tf_op jit(solution)/shard_map/all_to_all | solution.py:795
  17.8 29.4 %collective-permute-start.2 = (bf16[512,384]{1,0:T(8,128)(2,1)S(1)}, bf16[512,384]{1,0:T(8,128)(2,1)S(1)}, u32[]{:S(2)}, u32[]{:S(2)}) collective-permute-start(bf16[512,384]{1,0:T(8,128)(2,1)S(1)} %copy.44), channel_id=1, source_target_pairs={{0,1},{1,2},{2,3},{3,0},{4,5},{5,6},{6,7},{7,4},{8,9},{9,10},{10,1... | collective-permute-start | bytes 1179656 | tf_op jit(solution)/shard_map/ppermute | solution.py:737
  47.2 21.5 %collective-permute-start.5 = (bf16[512,384]{1,0:T(8,128)(2,1)S(1)}, bf16[512,384]{1,0:T(8,128)(2,1)}, u32[]{:S(2)}, u32[]{:S(2)}) collective-permute-start(bf16[512,384]{1,0:T(8,128)(2,1)S(1)} %collective-permute-done.2.refs_1_.refs_3_), channel_id=1, source_target_pairs={{0,1},{1,2},{2,3},{3,0},{4,5},{5,6},{6,7},{7,4},{8,9},{9,10},{10,1... | collective-permute-start | bytes 1179656 | tf_op jit(solution)/shard_map/ppermute | solution.py:737
  68.7 16.8 %collective-permute-start.10 = (bf16[512,384]{1,0:T(8,128)(2,1)}, bf16[512,384]{1,0:T(8,128)(2,1)}, u32[]{:S(2)}, u32[]{:S(2)}) collective-permute-start(bf16[512,384]{1,0:T(8,128)(2,1)} %collective-permute-done.5.refs_2_.refs_4_), channel_id=1, source_target_pairs={{0,1},{1,2},{2,3},{3,0},{4,5},{5,6},{6,7},{7,4},{8,9},{9,10},{10,1... | collective-permute-start | bytes 1179656 | tf_op jit(solution)/shard_map/ppermute | solution.py:737
  71.1 25.6 %collective-permute-start.13 = (bf16[512,512]{1,0:T(8,128)(2,1)S(1)}, bf16[512,512]{1,0:T(8,128)(2,1)}, u32[]{:S(2)}, u32[]{:S(2)}) collective-permute-start(bf16[512,512]{1,0:T(8,128)(2,1)S(1)} %get-tuple-element.455.refs_0_.refs_1_), channel_id=1, source_target_pairs={{0,1},{1,2},{2,3},{3,0},{4,5},{5,6},{6,7},{7,4},{8,9},{9,10},{10,1... | collective-permute-start | bytes 1572872 | tf_op jit(solution)/shard_map/ppermute | solution.py:737
  79.3 43.2 %collective-permute-start.6 = (bf16[512,1024]{1,0:T(8,128)(2,1)S(1)}, bf16[512,1024]{1,0:T(8,128)(2,1)}, u32[]{:S(2)}, u32[]{:S(2)}) collective-permute-start(bf16[512,1024]{1,0:T(8,128)(2,1)S(1)} %norm_in.2.own_rows), channel_id=1, source_target_pairs={{0,4},{4,0},{8,12},{12,8},{1,5},{5,1},{9,13},{13,9},{2,6},{6,2},{1... | collective-permute-start | bytes 3145736 | tf_op jit(solution)/shard_map/ppermute | solution.py:732
  79.4 28.5 %collective-permute-start.12 = (bf16[512,512]{1,0:T(8,128)(2,1)S(1)}, bf16[512,512]{1,0:T(8,128)(2,1)}, u32[]{:S(2)}, u32[]{:S(2)}) collective-permute-start(bf16[512,512]{1,0:T(8,128)(2,1)S(1)} %get-tuple-element.470.refs_1_.refs_0_), channel_id=1, source_target_pairs={{0,1},{1,2},{2,3},{3,0},{4,5},{5,6},{6,7},{7,4},{8,9},{9,10},{10,1... | collective-permute-start | bytes 1572872 | tf_op jit(solution)/shard_map/ppermute | solution.py:737
  81.6 15.1 %collective-permute-start.7 = (bf16[512,384]{1,0:T(8,128)(2,1)}, bf16[512,384]{1,0:T(8,128)(2,1)}, u32[]{:S(2)}, u32[]{:S(2)}) collective-permute-start(bf16[512,384]{1,0:T(8,128)(2,1)} %copy.46), channel_id=1, source_target_pairs={{0,8},{4,12},{8,0},{12,4},{1,9},{5,13},{9,1},{13,5},{2,10},{6,14},... | collective-permute-start | bytes 1179656 | tf_op jit(solution)/shard_map/ppermute | solution.py:732
  85.4 24.0 %collective-permute-start.8 = (bf16[512,384]{1,0:T(8,128)(2,1)S(1)}, bf16[512,384]{1,0:T(8,128)(2,1)}, u32[]{:S(2)}, u32[]{:S(2)}) collective-permute-start(bf16[512,384]{1,0:T(8,128)(2,1)S(1)} %collective-permute-done.2.refs_1_.refs_3_), channel_id=1, source_target_pairs={{0,8},{4,12},{8,0},{12,4},{1,9},{5,13},{9,1},{13,5},{2,10},{6,14},... | collective-permute-start | bytes 1179656 | tf_op jit(solution)/shard_map/ppermute | solution.py:732
  96.6 25.4 %collective-permute-start.19 = (bf16[512,512]{1,0:T(8,128)(2,1)}, bf16[512,512]{1,0:T(8,128)(2,1)S(1)}, u32[]{:S(2)}, u32[]{:S(2)}) collective-permute-start(bf16[512,512]{1,0:T(8,128)(2,1)} %collective-permute-done.13.refs_1_.refs_2_), channel_id=1, source_target_pairs={{0,1},{1,2},{2,3},{3,0},{4,5},{5,6},{6,7},{7,4},{8,9},{9,10},{10,1... | collective-permute-start | bytes 1572872 | tf_op jit(solution)/shard_map/ppermute | solution.py:737
  96.7 15.9 %collective-permute-start.9 = (bf16[512,384]{1,0:T(8,128)(2,1)}, bf16[512,384]{1,0:T(8,128)(2,1)S(1)}, u32[]{:S(2)}, u32[]{:S(2)}) collective-permute-start(bf16[512,384]{1,0:T(8,128)(2,1)} %collective-permute-done.5.refs_2_.refs_4_), channel_id=1, source_target_pairs={{0,8},{4,12},{8,0},{12,4},{1,9},{5,13},{9,1},{13,5},{2,10},{6,14},... | collective-permute-start | bytes 1179656 | tf_op jit(solution)/shard_map/ppermute | solution.py:732
  107.9 11.8 %collective-permute-start.11 = (bf16[512,384]{1,0:T(8,128)(2,1)}, bf16[512,384]{1,0:T(8,128)(2,1)S(1)}, u32[]{:S(2)}, u32[]{:S(2)}) collective-permute-start(bf16[512,384]{1,0:T(8,128)(2,1)} %collective-permute-done.10.refs_3_.refs_5_), channel_id=1, source_target_pairs={{0,8},{4,12},{8,0},{12,4},{1,9},{5,13},{9,1},{13,5},{2,10},{6,14},... | collective-permute-start | bytes 1179656 | tf_op jit(solution)/shard_map/ppermute | solution.py:732
  109.4 40.7 %collective-permute-start.18 = (bf16[512,512]{1,0:T(8,128)(2,1)}, bf16[512,512]{1,0:T(8,128)(2,1)}, u32[]{:S(2)}, u32[]{:S(2)}) collective-permute-start(bf16[512,512]{1,0:T(8,128)(2,1)} %collective-permute-done.12.refs_2_.refs_1_), channel_id=1, source_target_pairs={{0,1},{1,2},{2,3},{3,0},{4,5},{5,6},{6,7},{7,4},{8,9},{9,10},{10,1... | collective-permute-start | bytes 1572872 | tf_op jit(solution)/shard_map/ppermute | solution.py:737
  113.3 36.8 %collective-permute-start.14 = (bf16[128,512]{1,0:T(8,128)(2,1)}, bf16[128,512]{1,0:T(8,128)(2,1)}, u32[]{:S(2)}, u32[]{:S(2)}) collective-permute-start(bf16[128,512]{1,0:T(8,128)(2,1)} %copy-done.102), channel_id=1, source_target_pairs={{0,8},{4,12},{8,0},{12,4},{1,9},{5,13},{9,1},{13,5},{2,10},{6,14},... | collective-permute-start | bytes 393224 | tf_op jit(solution)/shard_map/ppermute | solution.py:732
  120.5 29.6 %collective-permute-start.15 = (bf16[128,512]{1,0:T(8,128)(2,1)}, bf16[128,512]{1,0:T(8,128)(2,1)}, u32[]{:S(2)}, u32[]{:S(2)}) collective-permute-start(bf16[128,512]{1,0:T(8,128)(2,1)} %copy-done.117), channel_id=1, source_target_pairs={{0,8},{4,12},{8,0},{12,4},{1,9},{5,13},{9,1},{13,5},{2,10},{6,14},... | collective-permute-start | bytes 393224 | tf_op jit(solution)/shard_map/ppermute | solution.py:732
  122.0 28.1 %collective-permute-start.16 = (bf16[128,512]{1,0:T(8,128)(2,1)}, bf16[128,512]{1,0:T(8,128)(2,1)}, u32[]{:S(2)}, u32[]{:S(2)}) collective-permute-start(bf16[128,512]{1,0:T(8,128)(2,1)} %copy-done.107), channel_id=1, source_target_pairs={{0,8},{4,12},{8,0},{12,4},{1,9},{5,13},{9,1},{13,5},{2,10},{6,14},... | collective-permute-start | bytes 393224 | tf_op jit(solution)/shard_map/ppermute | solution.py:732
  122.5 27.6 %collective-permute-start.17 = (bf16[128,512]{1,0:T(8,128)(2,1)}, bf16[128,512]{1,0:T(8,128)(2,1)}, u32[]{:S(2)}, u32[]{:S(2)}) collective-permute-start(bf16[128,512]{1,0:T(8,128)(2,1)} %copy-done.112), channel_id=1, source_target_pairs={{0,8},{4,12},{8,0},{12,4},{1,9},{5,13},{9,1},{13,5},{2,10},{6,14},... | collective-permute-start | bytes 393224 | tf_op jit(solution)/shard_map/ppermute | solution.py:732
  153.4 16.6 %collective-permute-start.22 = (bf16[512,512]{1,0:T(8,128)(2,1)S(1)}, bf16[512,512]{1,0:T(8,128)(2,1)S(1)}, u32[]{:S(2)}, u32[]{:S(2)}) collective-permute-start(bf16[512,512]{1,0:T(8,128)(2,1)S(1)} %copy-done.18), channel_id=1, source_target_pairs={{0,1},{1,2},{2,3},{3,0},{4,5},{5,6},{6,7},{7,4},{8,9},{9,10},{10,1... | collective-permute-start | bytes 1572872 | tf_op jit(solution)/shard_map/ppermute | solution.py:737
  153.5 27.3 %collective-permute-start.27 = (bf16[512,512]{1,0:T(8,128)(2,1)}, bf16[512,512]{1,0:T(8,128)(2,1)S(1)}, u32[]{:S(2)}, u32[]{:S(2)}) collective-permute-start(bf16[512,512]{1,0:T(8,128)(2,1)} %collective-permute-done.18.refs_3_.refs_2_), channel_id=1, source_target_pairs={{0,1},{1,2},{2,3},{3,0},{4,5},{5,6},{6,7},{7,4},{8,9},{9,10},{10,1... | collective-permute-start | bytes 1572872 | tf_op jit(solution)/shard_map/ppermute | solution.py:737
  154.3 27.0 %collective-permute-start.23 = (bf16[512,512]{1,0:T(8,128)(2,1)S(1)}, bf16[512,512]{1,0:T(8,128)(2,1)S(1)}, u32[]{:S(2)}, u32[]{:S(2)}) collective-permute-start(bf16[512,512]{1,0:T(8,128)(2,1)S(1)} %get-tuple-element.455.refs_0_.refs_1_), channel_id=1, source_target_pairs={{0,8},{4,12},{8,0},{12,4},{1,9},{5,13},{9,1},{13,5},{2,10},{6,14},... | collective-permute-start | bytes 1572872 | tf_op jit(solution)/shard_map/ppermute | solution.py:732
  162.1 41.3 %collective-permute-start.21 = (bf16[512,1024]{1,0:T(8,128)(2,1)S(1)}, bf16[512,1024]{1,0:T(8,128)(2,1)S(1)}, u32[]{:S(2)}, u32[]{:S(2)}) collective-permute-start(bf16[512,1024]{1,0:T(8,128)(2,1)S(1)} %get-tuple-element.543.own_rows), channel_id=1, source_target_pairs={{0,4},{4,0},{8,12},{12,8},{1,5},{5,1},{9,13},{13,9},{2,6},{6,2},{1... | collective-permute-start | bytes 3145736 | tf_op jit(solution)/shard_map/ppermute | solution.py:732
  162.2 20.6 %collective-permute-start.24 = (bf16[512,512]{1,0:T(8,128)(2,1)}, bf16[512,512]{1,0:T(8,128)(2,1)S(1)}, u32[]{:S(2)}, u32[]{:S(2)}) collective-permute-start(bf16[512,512]{1,0:T(8,128)(2,1)} %collective-permute-done.13.refs_1_.refs_2_), channel_id=1, source_target_pairs={{0,8},{4,12},{8,0},{12,4},{1,9},{5,13},{9,1},{13,5},{2,10},{6,14},... | collective-permute-start | bytes 1572872 | tf_op jit(solution)/shard_map/ppermute | solution.py:732
  170.0 21.6 %collective-permute-start.25 = (bf16[512,512]{1,0:T(8,128)(2,1)S(1)}, bf16[512,512]{1,0:T(8,128)(2,1)S(1)}, u32[]{:S(2)}, u32[]{:S(2)}) collective-permute-start(bf16[512,512]{1,0:T(8,128)(2,1)S(1)} %copy-done.18), channel_id=1, source_target_pairs={{0,8},{4,12},{8,0},{12,4},{1,9},{5,13},{9,1},{13,5},{2,10},{6,14},... | collective-permute-start | bytes 1572872 | tf_op jit(solution)/shard_map/ppermute | solution.py:732
  180.8 22.0 %collective-permute-start.26 = (bf16[512,512]{1,0:T(8,128)(2,1)S(1)}, bf16[512,512]{1,0:T(8,128)(2,1)S(1)}, u32[]{:S(2)}, u32[]{:S(2)}) collective-permute-start(bf16[512,512]{1,0:T(8,128)(2,1)S(1)} %collective-permute-done.22.refs_3_.refs_4_), channel_id=1, source_target_pairs={{0,8},{4,12},{8,0},{12,4},{1,9},{5,13},{9,1},{13,5},{2,10},{6,14},... | collective-permute-start | bytes 1572872 | tf_op jit(solution)/shard_map/ppermute | solution.py:732
  181.3 33.3 %collective-permute-start.28 = (bf16[512,512]{1,0:T(8,128)(2,1)S(1)}, bf16[512,512]{1,0:T(8,128)(2,1)S(1)}, u32[]{:S(2)}, u32[]{:S(2)}) collective-permute-start(bf16[512,512]{1,0:T(8,128)(2,1)S(1)} %get-tuple-element.470.refs_1_.refs_0_), channel_id=1, source_target_pairs={{0,8},{4,12},{8,0},{12,4},{1,9},{5,13},{9,1},{13,5},{2,10},{6,14},... | collective-permute-start | bytes 1572872 | tf_op jit(solution)/shard_map/ppermute | solution.py:732
  182.8 42.5 %collective-permute-start.29 = (bf16[512,512]{1,0:T(8,128)(2,1)}, bf16[512,512]{1,0:T(8,128)(2,1)S(1)}, u32[]{:S(2)}, u32[]{:S(2)}) collective-permute-start(bf16[512,512]{1,0:T(8,128)(2,1)} %collective-permute-done.12.refs_2_.refs_1_), channel_id=1, source_target_pairs={{0,8},{4,12},{8,0},{12,4},{1,9},{5,13},{9,1},{13,5},{2,10},{6,14},... | collective-permute-start | bytes 1572872 | tf_op jit(solution)/shard_map/ppermute | solution.py:732
  191.6 44.9 %collective-permute-start.30 = (bf16[512,512]{1,0:T(8,128)(2,1)}, bf16[512,512]{1,0:T(8,128)(2,1)S(1)}, u32[]{:S(2)}, u32[]{:S(2)}) collective-permute-start(bf16[512,512]{1,0:T(8,128)(2,1)} %collective-permute-done.18.refs_3_.refs_2_), channel_id=1, source_target_pairs={{0,8},{4,12},{8,0},{12,4},{1,9},{5,13},{9,1},{13,5},{2,10},{6,14},... | collective-permute-start | bytes 1572872 | tf_op jit(solution)/shard_map/ppermute | solution.py:732
  202.9 43.8 %collective-permute-start.31 = (bf16[512,512]{1,0:T(8,128)(2,1)S(1)}, bf16[512,512]{1,0:T(8,128)(2,1)S(1)}, u32[]{:S(2)}, u32[]{:S(2)}) collective-permute-start(bf16[512,512]{1,0:T(8,128)(2,1)S(1)} %collective-permute-done.27.refs_4_.refs_3_), channel_id=1, source_target_pairs={{0,8},{4,12},{8,0},{12,4},{1,9},{5,13},{9,1},{13,5},{2,10},{6,14},... | collective-permute-start | bytes 1572872 | tf_op jit(solution)/shard_map/ppermute | solution.py:732
  257.3 26.1 %collective-permute-start.33 = (bf16[512,1024]{1,0:T(8,128)(2,1)S(1)}, bf16[512,1024]{1,0:T(8,128)(2,1)S(1)}, u32[]{:S(2)}, u32[]{:S(2)}) collective-permute-start(bf16[512,1024]{1,0:T(8,128)(2,1)S(1)} %get-tuple-element.533), channel_id=1, source_target_pairs={{0,16},{1,17},{2,18},{3,19},{4,20},{5,21},{6,22},{7,23},{8,24},{9,... | collective-permute-start | bytes 3145736 | tf_op jit(solution)/shard_map/ppermute | solution.py:23
  421.2 39.3 %all-to-all-start.1 = ((bf16[4,128,1024]{2,1,0:T(8,128)(2,1)}), bf16[4,128,1024]{2,1,0:T(8,128)(2,1)}, u32[]{:S(2)}, u32[]{:S(2)}) async-start(bf16[4,128,1024]{2,1,0:T(8,128)(2,1)} %bitcast.122), calls=%async_computation.1 | async-start | bytes 2097152 | tf_op jit(solution)/shard_map/all_to_all | solution.py:800
  426.2 27.3 %collective-permute-start.43 = (bf16[512,1024]{1,0:T(8,128)(2,1)}, bf16[512,1024]{1,0:T(8,128)(2,1)S(1)}, u32[]{:S(2)}, u32[]{:S(2)}) collective-permute-start(bf16[512,1024]{1,0:T(8,128)(2,1)} %copy-done.136), channel_id=1, source_target_pairs={{16,0},{17,1},{18,2},{19,3},{20,4},{21,5},{22,6},{23,7},{24,8},{25... | collective-permute-start | bytes 3145736 | tf_op jit(solution)/shard_map/ppermute | solution.py:23
  462.4 58.7 %collective-permute-start.42 = (bf16[2,128,1024]{2,1,0:T(8,128)(2,1)}, bf16[2,128,1024]{2,1,0:T(8,128)(2,1)}, u32[]{:S(2)}, u32[]{:S(2)}) collective-permute-start(bf16[2,128,1024]{2,1,0:T(8,128)(2,1)} %dynamic-slice_bitcast_fusion.2), channel_id=1, source_target_pairs={{0,4},{4,0},{8,12},{12,8},{1,5},{5,1},{9,13},{13,9},{2,6},{6,2},{1... | collective-permute-start | bytes 1572872 | tf_op jit(solution)/shard_map/ppermute | solution.py:732
  515.6 15.8 %collective-permute-start.46 = (bf16[512,1024]{1,0:T(8,128)(2,1)}, bf16[512,1024]{1,0:T(8,128)(2,1)}, u32[]{:S(2)}, u32[]{:S(2)}) collective-permute-start(bf16[512,1024]{1,0:T(8,128)(2,1)} %get-tuple-element.625.own_rows), channel_id=1, source_target_pairs={{0,4},{4,0},{8,12},{12,8},{1,5},{5,1},{9,13},{13,9},{2,6},{6,2},{1... | collective-permute-start | bytes 3145736 | tf_op jit(solution)/shard_map/ppermute | solution.py:732
  515.8 15.0 %collective-permute-start.47 = (bf16[512,512]{1,0:T(8,128)(2,1)}, bf16[512,512]{1,0:T(8,128)(2,1)S(1)}, u32[]{:S(2)}, u32[]{:S(2)}) collective-permute-start(bf16[512,512]{1,0:T(8,128)(2,1)} %slice.371), channel_id=1, source_target_pairs={{0,8},{4,12},{8,0},{12,4},{1,9},{5,13},{9,1},{13,5},{2,10},{6,14},... | collective-permute-start | bytes 1572872 | tf_op jit(solution)/shard_map/ppermute | solution.py:732
  519.1 33.8 %collective-permute-start.49 = (bf16[512,512]{1,0:T(8,128)(2,1)S(1)}, bf16[512,512]{1,0:T(8,128)(2,1)S(1)}, u32[]{:S(2)}, u32[]{:S(2)}) collective-permute-start(bf16[512,512]{1,0:T(8,128)(2,1)S(1)} %copy-done.183), channel_id=1, source_target_pairs={{0,8},{4,12},{8,0},{12,4},{1,9},{5,13},{9,1},{13,5},{2,10},{6,14},... | collective-permute-start | bytes 1572872 | tf_op jit(solution)/shard_map/ppermute | solution.py:732
  520.6 113.5 %collective-permute-start.66 = (bf16[512,512]{1,0:T(8,128)(2,1)}, bf16[512,512]{1,0:T(8,128)(2,1)}, u32[]{:S(2)}, u32[]{:S(2)}) collective-permute-start(bf16[512,512]{1,0:T(8,128)(2,1)} %slice.368), channel_id=1, source_target_pairs={{0,8},{4,12},{8,0},{12,4},{1,9},{5,13},{9,1},{13,5},{2,10},{6,14},... | collective-permute-start | bytes 1572872 | tf_op jit(solution)/shard_map/ppermute | solution.py:732
  521.1 69.3 %collective-permute-start.53 = (bf16[512,512]{1,0:T(8,128)(2,1)}, bf16[512,512]{1,0:T(8,128)(2,1)S(1)}, u32[]{:S(2)}, u32[]{:S(2)}) collective-permute-start(bf16[512,512]{1,0:T(8,128)(2,1)} %slice.369), channel_id=1, source_target_pairs={{0,8},{4,12},{8,0},{12,4},{1,9},{5,13},{9,1},{13,5},{2,10},{6,14},... | collective-permute-start | bytes 1572872 | tf_op jit(solution)/shard_map/ppermute | solution.py:732
  530.8 44.9 %collective-permute-start.48 = (bf16[512,512]{1,0:T(8,128)(2,1)S(1)}, bf16[512,512]{1,0:T(8,128)(2,1)S(1)}, u32[]{:S(2)}, u32[]{:S(2)}) collective-permute-start(bf16[512,512]{1,0:T(8,128)(2,1)S(1)} %copy-done.184), channel_id=1, source_target_pairs={{0,8},{4,12},{8,0},{12,4},{1,9},{5,13},{9,1},{13,5},{2,10},{6,14},... | collective-permute-start | bytes 1572872 | tf_op jit(solution)/shard_map/ppermute | solution.py:732
  531.4 23.1 %collective-permute-start.50 = (bf16[512,512]{1,0:T(8,128)(2,1)S(1)}, bf16[512,512]{1,0:T(8,128)(2,1)S(1)}, u32[]{:S(2)}, u32[]{:S(2)}) collective-permute-start(bf16[512,512]{1,0:T(8,128)(2,1)S(1)} %add_convert_fusion.5), channel_id=1, source_target_pairs={{0,3},{1,0},{2,1},{3,2},{4,7},{5,4},{6,5},{7,6},{8,11},{9,8},{10,9... | collective-permute-start | bytes 1572872 | tf_op jit(solution)/shard_map/ppermute | solution.py:737
  552.9 64.4 %collective-permute-start.52 = (bf16[512,512]{1,0:T(8,128)(2,1)}, bf16[512,512]{1,0:T(8,128)(2,1)S(1)}, u32[]{:S(2)}, u32[]{:S(2)}) collective-permute-start(bf16[512,512]{1,0:T(8,128)(2,1)} %slice.366), channel_id=1, source_target_pairs={{0,8},{4,12},{8,0},{12,4},{1,9},{5,13},{9,1},{13,5},{2,10},{6,14},... | collective-permute-start | bytes 1572872 | tf_op jit(solution)/shard_map/ppermute | solution.py:732
  554.5 81.2 %collective-permute-start.69 = (bf16[512,512]{1,0:T(8,128)(2,1)}, bf16[512,512]{1,0:T(8,128)(2,1)}, u32[]{:S(2)}, u32[]{:S(2)}) collective-permute-start(bf16[512,512]{1,0:T(8,128)(2,1)} %slice.364), channel_id=1, source_target_pairs={{0,8},{4,12},{8,0},{12,4},{1,9},{5,13},{9,1},{13,5},{2,10},{6,14},... | collective-permute-start | bytes 1572872 | tf_op jit(solution)/shard_map/ppermute | solution.py:732
  590.5 28.4 %collective-permute-start.55 = (bf16[512,512]{1,0:T(8,128)(2,1)S(1)}, bf16[512,512]{1,0:T(8,128)(2,1)S(1)}, u32[]{:S(2)}, u32[]{:S(2)}) collective-permute-start(bf16[512,512]{1,0:T(8,128)(2,1)S(1)} %add_convert_fusion.3), channel_id=1, source_target_pairs={{0,3},{1,0},{2,1},{3,2},{4,7},{5,4},{6,5},{7,6},{8,11},{9,8},{10,9... | collective-permute-start | bytes 1572872 | tf_op jit(solution)/shard_map/ppermute | solution.py:737
  594.0 21.8 %collective-permute-start.54 = (bf16[512,512]{1,0:T(8,128)(2,1)S(1)}, bf16[512,512]{1,0:T(8,128)(2,1)S(1)}, u32[]{:S(2)}, u32[]{:S(2)}) collective-permute-start(bf16[512,512]{1,0:T(8,128)(2,1)S(1)} %add_convert_fusion.4), channel_id=1, source_target_pairs={{0,3},{1,0},{2,1},{3,2},{4,7},{5,4},{6,5},{7,6},{8,11},{9,8},{10,9... | collective-permute-start | bytes 1572872 | tf_op jit(solution)/shard_map/ppermute | solution.py:737
  615.8 20.4 %collective-permute-start.64 = (bf16[512,512]{1,0:T(8,128)(2,1)S(1)}, bf16[512,512]{1,0:T(8,128)(2,1)S(1)}, u32[]{:S(2)}, u32[]{:S(2)}) collective-permute-start(bf16[512,512]{1,0:T(8,128)(2,1)S(1)} %copy-done.182), channel_id=1, source_target_pairs={{0,8},{4,12},{8,0},{12,4},{1,9},{5,13},{9,1},{13,5},{2,10},{6,14},... | collective-permute-start | bytes 1572872 | tf_op jit(solution)/shard_map/ppermute | solution.py:732
  617.3 29.3 %collective-permute-start.76 = (bf16[128,512]{1,0:T(8,128)(2,1)S(1)}, bf16[128,512]{1,0:T(8,128)(2,1)S(1)}, u32[]{:S(2)}, u32[]{:S(2)}) collective-permute-start(bf16[128,512]{1,0:T(8,128)(2,1)S(1)} %slice.376), channel_id=1, source_target_pairs={{0,8},{4,12},{8,0},{12,4},{1,9},{5,13},{9,1},{13,5},{2,10},{6,14},... | collective-permute-start | bytes 393224 | tf_op jit(solution)/shard_map/ppermute | solution.py:732
  633.6 21.3 %collective-permute-start.70 = (bf16[512,384]{1,0:T(8,128)(2,1)S(1)}, bf16[512,384]{1,0:T(8,128)(2,1)S(1)}, u32[]{:S(2)}, u32[]{:S(2)}) collective-permute-start(bf16[512,384]{1,0:T(8,128)(2,1)S(1)} %slice.375), channel_id=1, source_target_pairs={{0,8},{4,12},{8,0},{12,4},{1,9},{5,13},{9,1},{13,5},{2,10},{6,14},... | collective-permute-start | bytes 1179656 | tf_op jit(solution)/shard_map/ppermute | solution.py:732
  634.1 12.5 %collective-permute-start.75 = (bf16[128,512]{1,0:T(8,128)(2,1)}, bf16[128,512]{1,0:T(8,128)(2,1)S(1)}, u32[]{:S(2)}, u32[]{:S(2)}) collective-permute-start(bf16[128,512]{1,0:T(8,128)(2,1)} %slice.377), channel_id=1, source_target_pairs={{0,8},{4,12},{8,0},{12,4},{1,9},{5,13},{9,1},{13,5},{2,10},{6,14},... | collective-permute-start | bytes 393224 | tf_op jit(solution)/shard_map/ppermute | solution.py:732
  635.7 17.1 %collective-permute-start.77 = (bf16[128,512]{1,0:T(8,128)(2,1)S(1)}, bf16[128,512]{1,0:T(8,128)(2,1)S(1)}, u32[]{:S(2)}, u32[]{:S(2)}) collective-permute-start(bf16[128,512]{1,0:T(8,128)(2,1)S(1)} %slice.378), channel_id=1, source_target_pairs={{0,8},{4,12},{8,0},{12,4},{1,9},{5,13},{9,1},{13,5},{2,10},{6,14},... | collective-permute-start | bytes 393224 | tf_op jit(solution)/shard_map/ppermute | solution.py:732
  636.2 18.1 %collective-permute-start.79 = (bf16[128,512]{1,0:T(8,128)(2,1)S(1)}, bf16[128,512]{1,0:T(8,128)(2,1)S(1)}, u32[]{:S(2)}, u32[]{:S(2)}) collective-permute-start(bf16[128,512]{1,0:T(8,128)(2,1)S(1)} %add_convert_fusion.11), channel_id=1, source_target_pairs={{0,3},{1,0},{2,1},{3,2},{4,7},{5,4},{6,5},{7,6},{8,11},{9,8},{10,9... | collective-permute-start | bytes 393224 | tf_op jit(solution)/shard_map/ppermute | solution.py:737
  647.3 29.7 %collective-permute-start.67 = (bf16[512,512]{1,0:T(8,128)(2,1)}, bf16[512,512]{1,0:T(8,128)(2,1)S(1)}, u32[]{:S(2)}, u32[]{:S(2)}) collective-permute-start(bf16[512,512]{1,0:T(8,128)(2,1)} %add_convert_fusion.1), channel_id=1, source_target_pairs={{0,3},{1,0},{2,1},{3,2},{4,7},{5,4},{6,5},{7,6},{8,11},{9,8},{10,9... | collective-permute-start | bytes 1572872 | tf_op jit(solution)/shard_map/ppermute | solution.py:737
  652.3 12.1 %collective-permute-start.63 = (bf16[512,384]{1,0:T(8,128)(2,1)S(1)}, bf16[512,384]{1,0:T(8,128)(2,1)S(1)}, u32[]{:S(2)}, u32[]{:S(2)}) collective-permute-start(bf16[512,384]{1,0:T(8,128)(2,1)S(1)} %slice.374), channel_id=1, source_target_pairs={{0,8},{4,12},{8,0},{12,4},{1,9},{5,13},{9,1},{13,5},{2,10},{6,14},... | collective-permute-start | bytes 1179656 | tf_op jit(solution)/shard_map/ppermute | solution.py:732
  652.8 16.1 %collective-permute-start.61 = (bf16[512,384]{1,0:T(8,128)(2,1)S(1)}, bf16[512,384]{1,0:T(8,128)(2,1)S(1)}, u32[]{:S(2)}, u32[]{:S(2)}) collective-permute-start(bf16[512,384]{1,0:T(8,128)(2,1)S(1)} %slice.372), channel_id=1, source_target_pairs={{0,8},{4,12},{8,0},{12,4},{1,9},{5,13},{9,1},{13,5},{2,10},{6,14},... | collective-permute-start | bytes 1179656 | tf_op jit(solution)/shard_map/ppermute | solution.py:732
  654.3 18.8 %collective-permute-start.62 = (bf16[512,384]{1,0:T(8,128)(2,1)}, bf16[512,384]{1,0:T(8,128)(2,1)S(1)}, u32[]{:S(2)}, u32[]{:S(2)}) collective-permute-start(bf16[512,384]{1,0:T(8,128)(2,1)} %slice.373), channel_id=1, source_target_pairs={{0,8},{4,12},{8,0},{12,4},{1,9},{5,13},{9,1},{13,5},{2,10},{6,14},... | collective-permute-start | bytes 1179656 | tf_op jit(solution)/shard_map/ppermute | solution.py:732
  664.4 17.7 %collective-permute-start.51 = (bf16[512,1024]{1,0:T(8,128)(2,1)S(1)}, bf16[512,1024]{1,0:T(8,128)(2,1)S(1)}, u32[]{:S(2)}, u32[]{:S(2)}) collective-permute-start(bf16[512,1024]{1,0:T(8,128)(2,1)S(1)} %get-tuple-element.630), channel_id=1, source_target_pairs={{0,4},{4,0},{8,12},{12,8},{1,5},{5,1},{9,13},{13,9},{2,6},{6,2},{1... | collective-permute-start | bytes 3145736 | tf_op jit(solution)/shard_map/ppermute | solution.py:732
  665.1 14.8 %collective-permute-start.65 = (bf16[512,512]{1,0:T(8,128)(2,1)S(1)}, bf16[512,512]{1,0:T(8,128)(2,1)S(1)}, u32[]{:S(2)}, u32[]{:S(2)}) collective-permute-start(bf16[512,512]{1,0:T(8,128)(2,1)S(1)} %copy-done.179), channel_id=1, source_target_pairs={{0,3},{1,0},{2,1},{3,2},{4,7},{5,4},{6,5},{7,6},{8,11},{9,8},{10,9... | collective-permute-start | bytes 1572872 | tf_op jit(solution)/shard_map/ppermute | solution.py:737
  668.9 41.3 %collective-permute-start.71 = (bf16[512,384]{1,0:T(8,128)(2,1)}, bf16[512,384]{1,0:T(8,128)(2,1)}, u32[]{:S(2)}, u32[]{:S(2)}) collective-permute-start(bf16[512,384]{1,0:T(8,128)(2,1)} %add_convert_fusion.8), channel_id=1, source_target_pairs={{0,3},{1,0},{2,1},{3,2},{4,7},{5,4},{6,5},{7,6},{8,11},{9,8},{10,9... | collective-permute-start | bytes 1179656 | tf_op jit(solution)/shard_map/ppermute | solution.py:737
  673.1 18.0 %collective-permute-start.81 = (bf16[128,512]{1,0:T(8,128)(2,1)S(1)}, bf16[128,512]{1,0:T(8,128)(2,1)S(1)}, u32[]{:S(2)}, u32[]{:S(2)}) collective-permute-start(bf16[128,512]{1,0:T(8,128)(2,1)S(1)} %add_convert_fusion.9), channel_id=1, source_target_pairs={{0,3},{1,0},{2,1},{3,2},{4,7},{5,4},{6,5},{7,6},{8,11},{9,8},{10,9... | collective-permute-start | bytes 393224 | tf_op jit(solution)/shard_map/ppermute | solution.py:737
  678.0 37.5 %collective-permute-start.68 = (bf16[512,512]{1,0:T(8,128)(2,1)}, bf16[512,512]{1,0:T(8,128)(2,1)}, u32[]{:S(2)}, u32[]{:S(2)}) collective-permute-start(bf16[512,512]{1,0:T(8,128)(2,1)} %add_convert_fusion), channel_id=1, source_target_pairs={{0,3},{1,0},{2,1},{3,2},{4,7},{5,4},{6,5},{7,6},{8,11},{9,8},{10,9... | collective-permute-start | bytes 1572872 | tf_op jit(solution)/shard_map/ppermute | solution.py:737
  682.1 54.9 %collective-permute-start.84 = (f32[512,256]{1,0:T(8,128)}, f32[512,256]{1,0:T(8,128)}, u32[]{:S(2)}, u32[]{:S(2)}) collective-permute-start(f32[512,256]{1,0:T(8,128)} %slice_select_fusion), channel_id=1, source_target_pairs={{0,4},{4,0},{8,12},{12,8},{1,5},{5,1},{9,13},{13,9},{2,6},{6,2},{1... | collective-permute-start | bytes 1572872 | tf_op jit(solution)/shard_map/ppermute | solution.py:732
  695.0 13.6 %collective-permute-start.82 = (f32[128,256]{1,0:T(8,128)S(1)}, f32[128,256]{1,0:T(8,128)}, u32[]{:S(2)}, u32[]{:S(2)}) collective-permute-start(f32[128,256]{1,0:T(8,128)S(1)} %slice_select_fusion.2), channel_id=1, source_target_pairs={{0,4},{4,0},{8,12},{12,8},{1,5},{5,1},{9,13},{13,9},{2,6},{6,2},{1... | collective-permute-start | bytes 393224 | tf_op jit(solution)/shard_map/ppermute | solution.py:732
  702.9 49.7 %all-to-all-start.2 = ((bf16[4,128,1024]{2,1,0:T(8,128)(2,1)}), bf16[4,128,1024]{2,1,0:T(8,128)(2,1)S(1)}, u32[]{:S(2)}, u32[]{:S(2)}) async-start(bf16[4,128,1024]{2,1,0:T(8,128)(2,1)} %bitcast.17), calls=%async_computation.2 | async-start | bytes 2097152 | tf_op jit(solution)/shard_map/all_to_all | solution.py:800
  711.5 23.8 %collective-permute-start.72 = (bf16[512,384]{1,0:T(8,128)(2,1)S(1)}, bf16[512,384]{1,0:T(8,128)(2,1)S(1)}, u32[]{:S(2)}, u32[]{:S(2)}) collective-permute-start(bf16[512,384]{1,0:T(8,128)(2,1)S(1)} %add_convert_fusion.7), channel_id=1, source_target_pairs={{0,3},{1,0},{2,1},{3,2},{4,7},{5,4},{6,5},{7,6},{8,11},{9,8},{10,9... | collective-permute-start | bytes 1179656 | tf_op jit(solution)/shard_map/ppermute | solution.py:737
  717.7 33.6 %collective-permute-start.83 = (f32[256,512]{1,0:T(8,128)}, f32[256,512]{1,0:T(8,128)}, u32[]{:S(2)}, u32[]{:S(2)}) collective-permute-start(f32[256,512]{1,0:T(8,128)} %dynamic-slice_bitcast_fusion), channel_id=1, source_target_pairs={{0,4},{4,0},{8,12},{12,8},{1,5},{5,1},{9,13},{13,9},{2,6},{6,2},{1... | collective-permute-start | bytes 1572872 | tf_op jit(solution)/shard_map/ppermute | solution.py:732
  735.4 14.7 %collective-permute-start.73 = (bf16[512,384]{1,0:T(8,128)(2,1)S(1)}, bf16[512,384]{1,0:T(8,128)(2,1)S(1)}, u32[]{:S(2)}, u32[]{:S(2)}) collective-permute-start(bf16[512,384]{1,0:T(8,128)(2,1)S(1)} %add_convert_fusion.6), channel_id=1, source_target_pairs={{0,3},{1,0},{2,1},{3,2},{4,7},{5,4},{6,5},{7,6},{8,11},{9,8},{10,9... | collective-permute-start | bytes 1179656 | tf_op jit(solution)/shard_map/ppermute | solution.py:737
  (230 other events, 2834.9 us)

commit v4 on v3

--- a/solution.py
+++ b/solution.py
@@ -13,8 +13,12 @@
 
 NORM_EPSILON = 1e-06
 TILE = 128
+PAIR_WORK = 1024
+QKV = slice(0, 384)
+OUT = slice(384, 512)
 CHUNK = 32
-KERNEL_VMEM = 40 << 20
+KERNEL_VMEM = 24 << 20
+ROWS_VMEM = 8 << 20
 
 
 def shifted(block, axis, distance):
@@ -334,12 +338,13 @@
     return jnp.dot(left, right, preferred_element_type=jnp.float32)
 
 
-def side_by_side(refs):
-    return jnp.concatenate([ref[...] for ref in refs], axis=1)
-
-
-def stacked_up(refs):
-    return jnp.concatenate([ref[...] for ref in refs], axis=0)
+def model_weight(owns, others, cols):
+    sides = [jnp.concatenate([ref[:, cols] for ref in refs], axis=1) for refs in (owns, others)]
+    return jnp.concatenate(sides, axis=0)
+
+
+def stacked_up(values):
+    return jnp.concatenate(values, axis=0)
 
 
 def edge_masks(core, rows):
@@ -372,18 +377,14 @@
     return jnp.where(lane // 64 == head, rows, jnp.zeros_like(rows))
 
 
-def pick_piece(weight, owns, others, axis):
+def pick_piece(weight, owns, others, cols):
     for j, (own, other) in enumerate(zip(owns, others)):
 
         @pl.when(pl.program_id(0) == j)
         def _():
-            size = own.shape[axis]
-            if axis == 0:
-                weight[:size] = own[...]
-                weight[size:] = other[...]
-            else:
-                weight[:, :size] = own[...]
-                weight[:, size:] = other[...]
+            size = own.shape[0]
+            weight[:size] = own[:, cols]
+            weight[size:] = other[:, cols]
 
 
 def attend_kernel(pieces, core_ref, cos_ref, sin_ref, own_rows, other_rows, *refs):
@@ -391,8 +392,8 @@
     q_ref, k_ref, v_ref, lse_ref, mix_ref, weight = refs[2 * pieces :]
     half = own_rows.shape[0]
     tile = TILE
-    pick_piece(weight, owns, others, 0)
-    proj = dot_nn(stacked_up([own_rows, other_rows]), weight[...])
+    pick_piece(weight, owns, others, QKV)
+    proj = dot_nn(stacked_up([own_rows[...], other_rows[...]]), weight[...])
     cos_rows, sin_rows = cos_ref[...], sin_ref[...]
     q = (rotated(proj[:, :128], cos_rows, sin_rows) * HEAD_DIM ** (-0.5)).astype(jnp.bfloat16)
     k = rotated(proj[:, 128:256], cos_rows, sin_rows).astype(jnp.bfloat16)
@@ -437,8 +438,9 @@
     q_ref, k_ref, v_ref, lse_ref, out_ref, weight, dq, dk, dv = refs[2 * pieces :]
     half = own_rows.shape[0]
     tile = TILE
-    pick_piece(weight, owns, others, 1)
-    d_mixed = dot_nt(stacked_up([own_rows, other_rows]), weight[...]).astype(jnp.bfloat16)
+    pick_piece(weight, owns, others, OUT)
+    rows = stacked_up([own_rows[...], other_rows[...]])
+    d_mixed = dot_nn(rows, weight[...]).astype(jnp.bfloat16)
     q, k, v = q_ref[0], k_ref[0], v_ref[0]
     k_flip = k.astype(jnp.float32).T.astype(jnp.bfloat16)
     masks = edge_masks(core_ref[0], tile)
@@ -495,17 +497,9 @@
     other_ref[...] = total[half:].astype(jnp.bfloat16)
 
 
-def into_model_kernel(lefts, pieces, *refs):
-    left, refs = side_by_side(refs[:lefts]), refs[lefts:]
-    owns, others = refs[:pieces], refs[pieces : 2 * pieces]
-    weight = jnp.concatenate([stacked_up(owns), stacked_up(others)], axis=1)
-    split_rows(dot_nn(left, weight), *refs[2 * pieces :])
-
-
-def back_to_model_kernel(lefts, pieces, *refs):
-    left, refs = side_by_side(refs[:lefts]), refs[lefts:]
-    owns, others = refs[:pieces], refs[pieces : 2 * pieces]
-    weight = jnp.concatenate([side_by_side(owns), side_by_side(others)], axis=0)
+def to_model_kernel(lefts, pieces, cols, *refs):
+    left, refs = jnp.concatenate([ref[...] for ref in refs[:lefts]], axis=1), refs[lefts:]
+    weight = model_weight(refs[:pieces], refs[pieces : 2 * pieces], cols)
     split_rows(dot_nt(left, weight), *refs[2 * pieces :])
 
 
@@ -522,13 +516,13 @@
     owns, others = refs[:pieces], refs[pieces : 2 * pieces]
     gelu_ref, slope_ref = refs[2 * pieces :]
     half = own_rows.shape[0]
-    size = owns[0].shape[1]
+    size = owns[0].shape[1] // 2
     step = half // 2
     units = [(j, i) for j in range(pieces) for i in range(4)]
 
     def product(j, i):
         rows = (own_rows, other_rows)[i // 2][i % 2 * step : (i % 2 + 1) * step]
-        return dot_nn(rows, stacked_up([owns[j], others[j]]))
+        return dot_nn(rows, stacked_up([owns[j][:, :size], others[j][:, :size]]))
 
     ahead = product(*units[0])
     for spot, (j, i) in enumerate(units):
@@ -545,11 +539,11 @@
 def mlp_up_back_kernel(pieces, own_rows, other_rows, slope_ref, *refs):
     owns, others = refs[:pieces], refs[pieces : 2 * pieces]
     out_ref = refs[-1]
-    size = owns[0].shape[0]
-    rows = stacked_up([own_rows, other_rows])
+    size = owns[0].shape[1] // 2
+    rows = stacked_up([own_rows[...], other_rows[...]])
     for j in range(pieces):
         cols = slice(j * size, (j + 1) * size)
-        d_gelu = dot_nt(rows, side_by_side([owns[j], others[j]]))
+        d_gelu = dot_nn(rows, stacked_up([owns[j][:, size:], others[j][:, size:]]))
         out_ref[:, cols] = (d_gelu * slope_ref[:, cols].astype(jnp.float32)).astype(jnp.bfloat16)
 
 
@@ -651,14 +645,21 @@
     (sum_ref[...],) = by_chunks(rows_ref.shape[0], body, 1, rows_ref.shape[1])
 
 
-def on_chip(kernel, name, outs, *operands):
+def work(flops, arrays):
+    size = sum(math.prod(array.shape) * jnp.dtype(array.dtype).itemsize for array in arrays)
+    return pl.CostEstimate(flops=flops, bytes_accessed=size, transcendentals=0)
+
+
+def on_chip(kernel, name, outs, *operands, limit=ROWS_VMEM, flops=0):
+    shapes = [jax.ShapeDtypeStruct(shape, dtype) for shape, dtype in outs]
     space = pl.BlockSpec(memory_space=pltpu.VMEM)
     return pl.pallas_call(
         kernel,
         in_specs=[space] * len(operands),
         out_specs=[space] * len(outs),
-        out_shape=[jax.ShapeDtypeStruct(shape, dtype) for shape, dtype in outs],
-        compiler_params=pltpu.CompilerParams(vmem_limit_bytes=KERNEL_VMEM),
+        out_shape=shapes,
+        compiler_params=pltpu.CompilerParams(vmem_limit_bytes=limit),
+        cost_estimate=work(flops, (*operands, *shapes)),
         name=name,
     )(*operands)
 
@@ -667,7 +668,8 @@
     return pl.BlockSpec(array.shape, lambda j: (0,) * array.ndim)
 
 
-def by_pairs(kernel, name, core, operands, pieces, blocks, outs, scratch):
+def by_pairs(kernel, name, core, operands, pieces, blocks, outs, scratch, flops):
+    shapes = [jax.ShapeDtypeStruct(shape, dtype) for shape, dtype, _ in outs]
     return pl.pallas_call(
         functools.partial(kernel, len(pieces[0])),
         grid=(len(pieces[0]),),
@@ -675,9 +677,10 @@
         + [whole_block(array) for array in (*operands, *pieces[0], *pieces[1])]
         + [spec for _, spec in blocks],
         out_specs=[spec for _, _, spec in outs],
-        out_shape=[jax.ShapeDtypeStruct(shape, dtype) for shape, dtype, _ in outs],
+        out_shape=shapes,
         scratch_shapes=scratch,
         compiler_params=pltpu.CompilerParams(vmem_limit_bytes=KERNEL_VMEM),
+        cost_estimate=work(flops, (*operands, *pieces[0], *pieces[1], *shapes)),
         name=name,
     )(core, *operands, *pieces[0], *pieces[1], *[array for array, _ in blocks])
 
@@ -697,6 +700,7 @@
         (),
         (lanes, lanes, lanes, lse, mixed),
         [pltpu.VMEM((features, 384), jnp.bfloat16)],
+        count * length * (2 * features * 384 + 2 * PAIR_WORK * length),
     )
 
 
@@ -714,16 +718,20 @@
         pieces,
         ((q, lanes), (k, lanes), (v, lanes), (lse, lse_spec)),
         (out,),
-        [pltpu.VMEM((128, features), jnp.bfloat16)] + [pltpu.VMEM((length, 128), jnp.float32)] * 3,
+        [pltpu.VMEM((features, 128), jnp.bfloat16)] + [pltpu.VMEM((length, 128), jnp.float32)] * 3,
+        count * length * (2 * features * 128 + 5 * PAIR_WORK * length),
     )[0]
 
 
-def model_rows(kernel, name, lefts, pieces):
+def model_rows(name, lefts, pieces, cols):
     owns, others = pieces
-    length, width = lefts[0].shape[0], 2 * owns[0].shape[kernel is into_model_kernel]
+    length, width = lefts[0].shape[0], 2 * owns[0].shape[0]
     outs = (((length // 2, width), jnp.float32), ((length // 2, width), jnp.bfloat16))
-    kernel = functools.partial(kernel, len(lefts), len(owns))
-    own, other = on_chip(kernel, name, outs, *lefts, *owns, *others)
+    kernel = functools.partial(to_model_kernel, len(lefts), len(owns), cols)
+    hidden = sum(left.shape[1] for left in lefts)
+    flops = 2 * length * width * hidden
+    operands = (*lefts, *owns, *others)
+    own, other = on_chip(kernel, name, outs, *operands, limit=KERNEL_VMEM, flops=flops)
     return own, flip_pairs(other, 1)
 
 
@@ -808,21 +816,21 @@
         size = local.shape[-1] // 2
         mid = (0,) * (local.ndim - 2)
         piece = lax.dynamic_slice(
-            local, (wide_half * upper, *mid, size * core), (wide_half, *local.shape[1:-1], size)
+            local,
+            (wide_half * upper, *mid, size * core),
+            (wide_half, *local.shape[1:-1], size),
         )
         return piece.reshape(wide_half, -1)
 
     def rows(local):
         size = local.shape[0] // 2
-        return lax.dynamic_slice(local, (size * core, wide_half * upper), (size, wide_half))
+        return lax.dynamic_slice(local, (size * core, wide_half * upper), (size, wide_half)).T
 
     core_word = core.astype(jnp.int32).reshape(1)
     order = Sequence(core_word)
     pieces = {
-        "qkv": [columns(qkv_weight[0])],
-        "out": [rows(out_weight[0])],
-        "up": [columns(up_weight[0])],
-        "down": [rows(down_weight[0])],
+        "attn": [jnp.concatenate([columns(qkv_weight[0]), rows(out_weight[0])], axis=1)],
+        "mlp": [jnp.concatenate([columns(up_weight[0]), rows(down_weight[0])], axis=1)],
     }
     flown = {name: [] for name in pieces}
     ringing = {}
@@ -830,41 +838,36 @@
     def flip(name):
         flown[name].append(flip_pairs(order.step(pieces[name][-1]), 2))
 
+    def flipped(name, j):
+        flown[name][j] = order.step(flown[name][j])
+
     def ring(name):
         ringing[name] = passed_on(order.step(pieces[name][-1]), 1)
 
     def caught(name):
         pieces[name].append(order.step(ringing.pop(name)))
-        flip(name)
-
-    def whole(name):
-        flown[name] = list(order.step(*flown[name]))
-        return pieces[name], flown[name]
 
     group_count = group_weights.shape[0]
     matches = group_ids[..., None] == jnp.arange(group_count, dtype=jnp.int32)
     row_scale = jnp.sum(jnp.where(matches, group_weights, 0.0), axis=-1)
     weighted = (out_cotangent.astype(jnp.float32) * row_scale[..., None]).astype(jnp.bfloat16)
-    ring("qkv")
-    flip("qkv")
-    ring("out")
-    flip("out")
     start = to_chip(own_first(jnp.where(first, inputs, weighted))).reshape(half, width)
-    flip("up")
-    caught("qkv")
-    ring("qkv")
-    caught("out")
-    ring("out")
-    flip("down")
-    caught("out")
-    ring("out")
-    caught("qkv")
-    ring("qkv")
-    ring("up")
-    caught("out")
-    ring("down")
+    flip("attn")
+    ring("attn")
+    caught("attn")
+    flipped("attn", 0)
+    ring("attn")
+    flip("attn")
+    flip("mlp")
+    caught("attn")
+    flipped("attn", 1)
+    ring("attn")
+    flip("attn")
+    caught("attn")
+    ring("mlp")
+    flip("attn")
+    flipped("mlp", 0)
     start = order.step(start)
-    caught("qkv")
     gain = own_first(gains[0])
 
     turns = jnp.arange(half, dtype=jnp.int32)
@@ -877,31 +880,36 @@
         jnp.concatenate([cos_part] * 4, axis=1),
         jnp.concatenate([-sin_part, sin_part] * 2, axis=1),
     )
-    units = tensor * pieces["up"][0].shape[1]
+    units = tensor * pieces["mlp"][0].shape[1] // 2
     row32, row16 = ((half, width), jnp.float32), ((half, width), jnp.bfloat16)
     unit16 = ((length, units), jnp.bfloat16)
     sum32 = ((1, width), jnp.float32)
+    mlp_cost = {"limit": KERNEL_VMEM, "flops": 2 * length * width * units}
+    ups, downs = slice(0, units // tensor), slice(units // tensor, None)
+    weights = {name: (pieces[name], flown[name]) for name in pieces}
+
+    def mlp_pieces():
+        return (*weights["mlp"][0], *weights["mlp"][1])
 
     def forward(layer_input, between=None):
         pause = between or (lambda: None)
         attn_in = both_rows(on_chip(norm_in_kernel, "norm_in", (row16,), gain, layer_input)[0])
         pause()
-        *heads, mixed = attend(core_word, tables, order.step(*attn_in), weights["qkv"])
+        *heads, mixed = attend(core_word, tables, order.step(*attn_in), weights["attn"])
         mixed = order.step(mixed)
         pause()
-        parts = model_rows(into_model_kernel, "attn_out", [mixed], weights["out"])
+        parts = model_rows("attn_out", [mixed], weights["attn"], OUT)
         branch, hidden, mlp_in = on_chip(
             after_attention_kernel, "after_attn", (row32, row32, row16), gain, layer_input, *parts
         )
         mlp_in = both_rows(order.step(mlp_in))
         pause()
         kernel = functools.partial(mlp_up_kernel, tensor)
-        gelu_out, slope = on_chip(
-            kernel, "mlp_up", (unit16, unit16), *mlp_in, *weights["up"][0], *weights["up"][1]
-        )
+        outs = (unit16, unit16)
+        gelu_out, slope = on_chip(kernel, "mlp_up", outs, *mlp_in, *mlp_pieces(), **mlp_cost)
         gelu_out = order.step(gelu_out)
         pause()
-        parts = model_rows(into_model_kernel, "mlp_down", [gelu_out], weights["down"])
+        parts = model_rows("mlp_down", [gelu_out], weights["mlp"], downs)
         mlp_branch, result = on_chip(
             after_mlp_kernel, "after_mlp", (row32, row16), gain, hidden, *parts
         )
@@ -916,12 +924,11 @@
         )
         d_down = both_rows(d_down)
         kernel = functools.partial(mlp_up_back_kernel, tensor)
-        d_up = on_chip(
-            kernel, "mlp_up_back", (unit16,), *d_down, slope, *weights["down"][0], *weights["down"][1]
-        )[0]
+        operands = (*d_down, slope, *mlp_pieces())
+        (d_up,) = on_chip(kernel, "mlp_up_back", (unit16,), *operands, **mlp_cost)
         pause(d_down=d_down)
         d_up = order.step(d_up)
-        parts = model_rows(back_to_model_kernel, "mlp_back", [d_up], weights["up"])
+        parts = model_rows("mlp_back", [d_up], weights["mlp"], ups)
         pause(d_up=d_up)
         d_hidden, d_attn, sum_one, sum_two = on_chip(
             into_attention_back_kernel,
@@ -936,39 +943,36 @@
         d_attn = both_rows(order.step(d_attn))
         pause(d_attn=d_attn)
         d_qkv = []
-        for base in range(0, tensor, 2):
-            some = [side[base : base + 2] for side in weights["out"]]
+        for base in reversed(range(0, tensor, 2)):
+            some = [side[base : base + 2] for side in weights["attn"]]
             rows_now = order.step(*d_attn)
-            d_qkv.append(attend_back(core_word, tables, rows_now, some, base, *heads))
-            d_qkv[-1] = order.step(d_qkv[-1])
-            pause(d_qkv=d_qkv[-1])
-        parts = model_rows(back_to_model_kernel, "attn_back", d_qkv, weights["qkv"])
+            now = attend_back(core_word, tables, rows_now, some, base, *heads)
+            d_qkv.insert(0, order.step(now))
+            pause(d_qkv=d_qkv[0])
+        parts = model_rows("attn_back", d_qkv, weights["attn"], QKV)
         d_input, sum_zero = on_chip(
             out_of_layer_kernel, "out_of_layer", (row16, sum32), gain, layer_input, *parts, d_hidden
         )
         sums = jnp.concatenate([sum_zero, sum_one, sum_two, sum_three])
         return order.step(d_input), (d_qkv, d_attn, d_up, d_down), sums
 
-    weights = {}
-
     def arrivals():
-        caught("up")
-        ring("up")
-        caught("down")
-        ring("down")
-        weights["qkv"] = whole("qkv")
+        flipped("attn", 2)
+        caught("mlp")
+        ring("mlp")
+        flip("mlp")
+        flipped("attn", 3)
         yield
-        caught("up")
-        ring("up")
-        caught("down")
-        ring("down")
-        weights["out"] = whole("out")
+        caught("mlp")
+        ring("mlp")
+        flip("mlp")
         yield
-        caught("up")
-        caught("down")
-        weights["up"] = whole("up")
+        flipped("mlp", 1)
+        caught("mlp")
+        flip("mlp")
+        flipped("mlp", 2)
+        flipped("mlp", 3)
         yield
-        weights["down"] = whole("down")
         yield
 
     steps = arrivals()
@@ -996,17 +1000,14 @@
     sums = {name: [None] * tensor for name in pieces}
     moving = {}
 
-    def halves(name, j, total, axis):
-        own = lax.slice_in_dim(total, 0, wide_half, axis=axis)
-        other = lax.slice_in_dim(total, wide_half, width, axis=axis).astype(jnp.bfloat16)
+    def leave(name, j, *pairs):
+        totals = [contract(*pair) for pair in order.step(*pairs)]
+        own = jnp.concatenate([total[:wide_half] for total in totals], axis=1)
+        other = jnp.concatenate(
+            [total[wide_half:].astype(jnp.bfloat16) for total in totals], axis=1
+        )
         own, other = order.step(own, other)
         sums[name][j] = (own, flip_pairs(other, 2))
-
-    def column_piece(name, j, left, right):
-        halves(name, j, contract(*order.step(left, right)), 0)
-
-    def row_piece(name, j, left, right):
-        halves(name, j, contract(*order.step(left, right)), 1)
 
     def gathered(name, j):
         own, other = sums[name][j]
@@ -1022,37 +1023,33 @@
         size = array.shape[1] // count
         return array[:, j * size : (j + 1) * size]
 
-    new_one = {"d_qkv": list(rights_one[0]), "d_attn": rights_one[1], "d_up": rights_one[2]}
-    new_one["d_down"] = rights_one[3]
-    order_back = list(reversed(range(tensor)))
+    d_qkv_one, d_attn_one, d_up_one, d_down_one = rights_one
 
     def departures():
         new = yield
-        d_down = own_layer(new["d_down"], new_one["d_down"])
-        for j in order_back:
-            row_piece("down", j, block(gelu_out, j), d_down)
+        d_down = own_layer(new["d_down"], d_down_one)
         new = yield
-        d_up = own_layer(new["d_up"], new_one["d_up"])
-        for j in order_back:
-            column_piece("up", j, mlp_in, block(d_up, j))
+        d_up = own_layer(new["d_up"], d_up_one)
+
+        def mlp_piece(j):
+            leave("mlp", j, (mlp_in, block(d_up, j)), (d_down, block(gelu_out, j)))
+
+        mlp_piece(3)
+        mlp_piece(2)
         new = yield
-        d_attn = own_layer(new["d_attn"], new_one["d_attn"])
-        gathered("down", 3)
+        d_attn = own_layer(new["d_attn"], d_attn_one)
+        gathered("mlp", 3)
+        mlp_piece(1)
         new = yield
-        upper_pairs = []
-        for half_pairs in range(2):
-            d_qkv = own_layer(new["d_qkv"], new_one["d_qkv"][half_pairs])
-            upper_pairs.append(d_qkv)
-            if half_pairs == 0:
-                gathered("down", 2)
-                gathered("up", 3)
-                new = yield
-        gathered("down", 1)
-        gathered("up", 2)
-        for j in order_back:
-            column_piece("qkv", j, attn_in, block(upper_pairs[j // 2], j % 2, 2))
-        for j in order_back:
-            row_piece("out", j, block(mixed, j), d_attn)
+        high = own_layer(new["d_qkv"], d_qkv_one[1])
+        gathered("mlp", 2)
+        mlp_piece(0)
+        new = yield
+        low = own_layer(new["d_qkv"], d_qkv_one[0])
+        gathered("mlp", 1)
+        for j in reversed(range(tensor)):
+            d_qkv = block((low, high)[j // 2], j % 2, 2)
+            leave("attn", j, (attn_in, d_qkv), (d_attn, block(mixed, j)))
         yield
 
     leaving = departures()
@@ -1060,34 +1057,26 @@
     grad_zero, rights_zero, gain_zero = backward(
         received, saved_zero, lambda **new: leaving.send(new)
     )
-    gathered("down", 0)
-    gathered("up", 1)
-    gathered("qkv", 3)
-    gathered("up", 0)
-    gathered("qkv", 2)
-    gathered("out", 3)
-    gathered("qkv", 1)
-    gathered("out", 2)
-    gathered("qkv", 0)
-    gathered("out", 1)
-    gathered("out", 0)
-    down_sum, up_sum, out_sum, qkv_sum = (sums[name] for name in ("down", "up", "out", "qkv"))
+    gathered("mlp", 0)
+    gathered("attn", 3)
+    gathered("attn", 2)
+    gathered("attn", 1)
+    gathered("attn", 0)
     grads = from_chip(own_first(jnp.where(first, grad_zero, grad_one)).reshape(tensor, part, width))
 
-    def by_columns(kept, count):
-        size = kept.shape[1]
-        kept = kept.reshape(2, wide_half // 2, size)
+    def both_cores(kept):
+        kept = kept.reshape(2, wide_half // 2, kept.shape[1])
         mine = lax.dynamic_index_in_dim(kept, core, 0, keepdims=False)
         other = lax.dynamic_index_in_dim(kept, 1 - core, 0, keepdims=False)
-        pair = ordered(mine, flip_pairs(other, 1))
-        pair = [side.reshape(wide_half // 2, count, size // count) for side in pair]
-        return jnp.concatenate(pair, axis=2)
-
-    def by_rows(kept):
-        sides = (kept[:, : wide_half // 2], kept[:, wide_half // 2 :])
-        mine = jnp.where(core_zero, sides[0], sides[1])
-        other = jnp.where(core_zero, sides[1], sides[0])
-        return jnp.concatenate(ordered(mine, flip_pairs(other, 1)), axis=0)
+        return ordered(mine, flip_pairs(other, 1))
+
+    pair = both_cores(sums["mlp"])
+    up_grad = jnp.concatenate([side[:, ups] for side in pair], axis=1)
+    down_grad = jnp.concatenate([side[:, downs].T for side in pair], axis=0)
+    pair = both_cores(sums["attn"])
+    qkv_grad = [side[:, QKV].reshape(wide_half // 2, 3, -1) for side in pair]
+    qkv_grad = jnp.concatenate(qkv_grad, axis=2)
+    out_grad = jnp.concatenate([side[:, OUT].T for side in pair], axis=0)
 
     gain_total = summed_everywhere(own_first(jnp.where(first, gain_zero, gain_one)))
     size = width // (tensor * lax.axis_size("dp"))
@@ -1097,10 +1086,10 @@
         outputs[None],
         grads[None],
         gains_grad[None],
-        by_columns(qkv_sum, 3)[None],
-        by_rows(out_sum)[None],
-        by_columns(up_sum, 1)[:, 0][None],
-        by_rows(down_sum)[None],
+        qkv_grad[None],
+        out_grad[None],
+        up_grad[None],
+        down_grad[None],
     )
 
 

time: 770 us -> 725 us (0.942)
  waiting for transfers between devices: 311 us -> 276 us
  starting transfers between devices: 101 us -> 80.9 us
  local copies, waits for them, and re-layouts: 77.7 us -> 85.4 us
    ppermute x24 -> x12, waiting for transfers between devices: 140 us -> 64.9 us  [passed_on(): lax.ppermute(block, 'tensor', [(i, (i + step) % size) for i in range(size)])]
    ppermute x2, waiting for transfers between devices: 6.49 us -> 37.6 us  [summed_everywhere(): lax.ppermute(value, 'tensor', [(i, i ^ distance) for i in range(size)])]
    ppermute x57 -> x39, waiting for transfers between devices: 127 us -> 146 us  [flip_pairs(): return lax.ppermute(block, 'dp', [(i, i ^ distance) for i in range(size)])]
    ppermute x24 -> x12, starting transfers between devices: 45.6 us -> 26.6 us  [passed_on(): lax.ppermute(block, 'tensor', [(i, (i + step) % size) for i in range(size)])]
    ppermute x57 -> x39, starting transfers between devices: 34.5 us -> 23.2 us  [flip_pairs(): return lax.ppermute(block, 'dp', [(i, i ^ distance) for i in range(size)])]
    ppermute x2, starting transfers between devices: 5.23 us -> 15.3 us  [shifted(): return lax.ppermute(block, axis, route)]
    dynamic_slice x3 -> x4, local copies, waits for them, and re-layouts: 1.14 us -> 11 us  [the longest x3 8.64 us: both_cores(): mine = lax.dynamic_index_in_dim(kept, core, 0, keepdims=False)]
    ppermute x2, waiting for transfers between devices: 36.5 us -> 27.2 us  [shifted(): return lax.ppermute(block, axis, route)]
  transfers between devices with their start and end apart: 88 -> 58, of which waited for: 41 -> 31; matrix products, arithmetic and copies ran while one was open for 11% -> 13% of each run, Pallas kernels for 12% -> 9%
where the time goes in v4:
time: 725 us; the launch traced here: 714 us
  waiting for transfers between devices  276 us (38%)
  Pallas kernels  194 us (27%)
  local copies, waits for them, and re-layouts  85.4 us (12%)
  starting transfers between devices  80.9 us (11%)
  other arithmetic  57.2 us (8%)
  matrix products  17 us (2%)
    ppermute x39, waiting for transfers between devices, flip_pairs(): return lax.ppermute(block, 'dp', [(i, i ^ distance) for i in range(size)])  146 us
    pallas_call x24, Pallas kernels, on_chip(): pl.pallas_call(kernel, in_specs=[space] * len(operands), out_specs=[space...  108 us
    pallas_call x6, Pallas kernels, by_pairs(): pl.pallas_call(functools.partial(kernel, len(pieces[0])), grid=(len(piece...  85.7 us
    ppermute x12, waiting for transfers between devices, passed_on(): lax.ppermute(block, 'tensor', [(i, (i + step) % size) for i in range(size)])  64.9 us
    unnamed x245, local copies, waits for them, and re-layouts  46.6 us
    ppermute x2, waiting for transfers between devices, summed_everywhere(): lax.ppermute(value, 'tensor', [(i, i ^ distance) for i in range(size)])  37.6 us
    ppermute x2, waiting for transfers between devices, shifted(): return lax.ppermute(block, axis, route)  27.2 us
    ppermute x12, starting transfers between devices, passed_on(): lax.ppermute(block, 'tensor', [(i, (i + step) % size) for i in range(size)])  26.6 us
  transfers between devices with their start and end apart: 58, of which 31 were waited for; matrix products, arithmetic and copies ran while one was open for 13% of the time, Pallas kernels for 9%

profile of v4, /device:TPU:0, one launch (start us, length us, event | category | flops | bytes accessed | tf_op | source)
XLA Modules:
  0.0 713.9 jit_solution(15041721391331505881)
XLA Ops:
  15.0 2.7 collective-permute-start.1
  21.4 3.9 all-to-all-start
  28.5 4.5 collective-permute-done.1.refs_1_.refs_2_.refs_3_
  35.8 25.0 %collective-permute-done.4.refs_2_.refs_3_.refs_0_.refs_4_ = bf16[512,512]{1,0:T(8,128)(2,1)} collective-permute-done((bf16[512,512]{1,0:T(8,128)(2,1)}, bf16[512,512]{1,0:T(8,128)(2,1)}, u32[]{:S(2)}, u32[]{:S(2)}) %collective-permute-start.4) | collective-permute-done | bytes 524320 | tf_op jit(solution)/shard_map/ppermute | solution.py:745
  61.6 4.3 collective-permute-start.6
  65.9 11.5 %collective-permute-done.6.refs_3_.refs_4_.refs_1_.refs_5_ = bf16[512,512]{1,0:T(8,128)(2,1)} collective-permute-done((bf16[512,512]{1,0:T(8,128)(2,1)}, bf16[512,512]{1,0:T(8,128)(2,1)}, u32[]{:S(2)}, u32[]{:S(2)}) %collective-permute-start.6) | collective-permute-done | bytes 524320 | tf_op jit(solution)/shard_map/ppermute | solution.py:745
  79.7 2.7 norm_in.2.own_rows
  87.5 10.0 %collective-permute-done.10.refs_6_.refs_7_.refs_2_.refs_8_ = bf16[512,512]{1,0:T(8,128)(2,1)S(1)} collective-permute-done((bf16[512,512]{1,0:T(8,128)(2,1)}, bf16[512,512]{1,0:T(8,128)(2,1)S(1)}, u32[]{:S(2)}, u32[]{:S(2)}) %collective-permute-start.10) | collective-permute-done | bytes 524320 | tf_op jit(solution)/shard_map/ppermute | solution.py:740
  97.5 6.4 collective-permute-done.9.refs_1_.refs_2_
  103.8 4.5 collective-permute-done.8.refs_7_.refs_8_.refs_3_.refs_9_
  110.8 17.2 %attend.2 = (bf16[4,1024,128]{2,1,0:T(8,128)(2,1)S(1)}, bf16[4,1024,128]{2,1,0:T(8,128)(2,1)S(1)}, bf16[4,1024,128]{2,1,0:T(8,128)(2,1)S(1)}, f32[4,2,1024]{2,1,0:T(2,128)S(1)}, bf16[1024,512]{1,0:T(8,128)(2,1)S(1)}) custom-call(s32[1]{0:T(128)} %bitcast.11.core_ref, f32[1024,128]{1,0:T(8,128)S(1)} %pad_maximum_fusion.25.cos_ref, ...), custom_call_target="tpu_custom_call" | custom-call | flops 11811160064 | bytes 11567104 | tf_op jit(solution)/shard_map/attend/pallas_call | solution.py:673
  130.0 3.7 attn_out.2
  137.6 3.4 after_attn.2
  142.3 17.7 %collective-permute-done.15.refs_5_.refs_6_ = bf16[512,1024]{1,0:T(8,128)(2,1)S(1)} collective-permute-done((bf16[512,1024]{1,0:T(8,128)(2,1)}, bf16[512,1024]{1,0:T(8,128)(2,1)S(1)}, u32[]{:S(2)}, u32[]{:S(2)}) %collective-permute-start.15) | collective-permute-done | bytes 1048608 | tf_op jit(solution)/shard_map/ppermute | solution.py:740
  160.1 2.6 collective-permute-done.14.refs_3_.refs_4_
  163.2 19.3 %collective-permute-done.16.refs_6_.refs_7_ = bf16[512,1024]{1,0:T(8,128)(2,1)S(1)} collective-permute-done((bf16[512,1024]{1,0:T(8,128)(2,1)S(1)}, bf16[512,1024]{1,0:T(8,128)(2,1)S(1)}, u32[]{:S(2)}, u32[]{:S(2)}) %collective-permute-start.16) | collective-permute-done | bytes 1048608 | tf_op jit(solution)/shard_map/ppermute | solution.py:740
  182.5 22.0 %collective-permute-done.17.refs_7_.refs_8_ = bf16[512,1024]{1,0:T(8,128)(2,1)S(1)} collective-permute-done((bf16[512,1024]{1,0:T(8,128)(2,1)S(1)}, bf16[512,1024]{1,0:T(8,128)(2,1)S(1)}, u32[]{:S(2)}, u32[]{:S(2)}) %collective-permute-start.17) | collective-permute-done | bytes 1048608 | tf_op jit(solution)/shard_map/ppermute | solution.py:740
  204.6 9.9 %mlp_up.2 = (bf16[1024,2048]{1,0:T(8,128)(2,1)S(1)}, bf16[1024,2048]{1,0:T(8,128)(2,1)S(1)}) custom-call(bf16[512,1024]{1,0:T(8,128)(2,1)S(1)} %get-tuple-element.402.own_rows, bf16[512,1024]{1,0:T(8,128)(2,1)S(1)} %collective-permute-done.13.other_rows, bf16[512,1024]{1,0:T(8,128)(2,1)S(1)} %pad_maximum_fusion.13.refs_0_.refs_1_, ...), custom_call_target="tpu_custom_call" | custom-call | flops 4294967296 | bytes 18874368 | tf_op jit(solution)/shard_map/mlp_up/pallas_call | solution.py:656
  214.5 6.5 mlp_down.2
  221.2 2.6 collective-permute-done.18.other_ref
  225.7 13.8 %collective-permute-start.19 = (bf16[512,1024]{1,0:T(8,128)(2,1)S(1)}, bf16[512,1024]{1,0:T(8,128)(2,1)S(1)}, u32[]{:S(2)}, u32[]{:S(2)}) collective-permute-start(bf16[512,1024]{1,0:T(8,128)(2,1)S(1)} %get-tuple-element.392), channel_id=1, source_target_pairs={{0,16},{1,17},{2,18},{3,19},{4,20},{5,21},{6,22},{7,23},{8,24},{9,... | collective-permute-start | bytes 3145736 | tf_op jit(solution)/shard_map/ppermute | solution.py:27
  239.6 11.9 %collective-permute-done.19.rows_ref = bf16[512,1024]{1,0:T(8,128)(2,1)S(1)} collective-permute-done((bf16[512,1024]{1,0:T(8,128)(2,1)S(1)}, bf16[512,1024]{1,0:T(8,128)(2,1)S(1)}, u32[]{:S(2)}, u32[]{:S(2)}) %collective-permute-start.19) | collective-permute-done | bytes 1048608 | tf_op jit(solution)/shard_map/ppermute | solution.py:27
  253.4 2.6 collective-permute-done.20.other_rows
  256.0 16.9 %attend.3 = (bf16[4,1024,128]{2,1,0:T(8,128)(2,1)S(1)}, bf16[4,1024,128]{2,1,0:T(8,128)(2,1)S(1)}, bf16[4,1024,128]{2,1,0:T(8,128)(2,1)S(1)}, f32[4,2,1024]{2,1,0:T(2,128)S(1)}, bf16[1024,512]{1,0:T(8,128)(2,1)S(1)}) custom-call(s32[1]{0:T(128)} %bitcast.11.core_ref, f32[1024,128]{1,0:T(8,128)S(1)} %pad_maximum_fusion.25.cos_ref, ...), custom_call_target="tpu_custom_call" | custom-call | flops 11811160064 | bytes 11567104 | tf_op jit(solution)/shard_map/attend/pallas_call | solution.py:673
  274.9 3.7 attn_out.3
  278.8 2.5 collective-permute-done.21.other_ref
  281.3 3.4 after_attn.3
  287.5 9.5 %mlp_up.3 = (bf16[1024,2048]{1,0:T(8,128)(2,1)S(1)}, bf16[1024,2048]{1,0:T(8,128)(2,1)S(1)}) custom-call(bf16[512,1024]{1,0:T(8,128)(2,1)S(1)} %get-tuple-element.404.own_rows, bf16[512,1024]{1,0:T(8,128)(2,1)S(1)} %collective-permute-done.22.other_rows, bf16[512,1024]{1,0:T(8,128)(2,1)S(1)} %pad_maximum_fusion.13.refs_0_.refs_1_, ...), custom_call_target="tpu_custom_call" | custom-call | flops 4294967296 | bytes 18874368 | tf_op jit(solution)/shard_map/mlp_up/pallas_call | solution.py:656
  297.0 6.5 mlp_down.3
  313.4 5.7 mlp_up_back.2.refs_0_
  321.2 6.5 mlp_back.2
  327.9 2.5 collective-permute-done.25.other_ref
  330.4 3.9 into_attn_back.2
  337.1 12.8 %attend_back.4.refs_1_ = bf16[1024,768]{1,0:T(8,128)(2,1)S(1)} custom-call(s32[1]{0:T(128)} %bitcast.11.core_ref, f32[1024,128]{1,0:T(8,128)S(1)} %pad_maximum_fusion.25.cos_ref, f32[1024,128]{1,0:T(8,128)S(1)} %pad_maximum_fusion.26.sin_ref, bf16[512,1024]{1,0:T(8,128)(2,1)S(1)} %get-tuple-element.381.own_rows, ...), custom_call_target="tpu_custom_call" | custom-call | flops 11274289152 | bytes 6815744 | tf_op jit(solution)/shard_map/attend_back/pallas_call | solution.py:673
  352.0 13.2 %attend_back.5.refs_0_ = bf16[1024,768]{1,0:T(8,128)(2,1)S(1)} custom-call(s32[1]{0:T(128)} %bitcast.11.core_ref, f32[1024,128]{1,0:T(8,128)S(1)} %copy-done.71, f32[1024,128]{1,0:T(8,128)S(1)} %copy-done.68, bf16[512,1024]{1,0:T(8,128)(2,1)S(1)} %get-tuple-element.381.own_rows, bf16[512,1024]{1,0:T(8,128)(2,1)S(1)} %collective-permute-done.26.other_rows, ...), custom_call_target="tpu_custom_call" | custom-call | flops 11274289152 | bytes 6815744 | tf_op jit(solution)/shard_map/attend_back/pallas_call | solution.py:673
  365.3 5.7 attn_back.2
  371.2 2.5 collective-permute-done.27.other_ref
  376.8 3.1 pad_maximum_fusion
  381.5 4.3 all-to-all-start.1
  398.0 15.3 %collective-permute-done.29.grad_ref = bf16[512,1024]{1,0:T(8,128)(2,1)S(1)} collective-permute-done((bf16[512,1024]{1,0:T(8,128)(2,1)}, bf16[512,1024]{1,0:T(8,128)(2,1)S(1)}, u32[]{:S(2)}, u32[]{:S(2)}) %collective-permute-start.29) | collective-permute-done | bytes 1048608 | tf_op jit(solution)/shard_map/ppermute | solution.py:27
  413.3 3.3 into_mlp_back.3
  433.7 6.3 mlp_up_back.3.refs_0_
  440.0 5.9 mlp_back.3
  472.8 4.0 into_attn_back.3
  476.8 6.8 collective-permute-done.34
  488.9 3.5 collective-permute-start.35
  492.4 12.5 %collective-permute-done.33 = bf16[512,1024]{0,1:T(8,128)(2,1)S(1)} collective-permute-done((bf16[512,1024]{0,1:T(8,128)(2,1)S(1)}, bf16[512,1024]{0,1:T(8,128)(2,1)S(1)}, u32[]{:S(2)}, u32[]{:S(2)}) %collective-permute-start.33) | collective-permute-done | bytes 1048608 | tf_op jit(solution)/shard_map/ppermute | solution.py:740
  508.2 12.6 %attend_back.6.refs_1_ = bf16[1024,768]{1,0:T(8,128)(2,1)S(1)} custom-call(s32[1]{0:T(128)} %bitcast.11.core_ref, f32[1024,128]{1,0:T(8,128)S(1)} %copy-done.72, f32[1024,128]{1,0:T(8,128)S(1)} %copy-done.69, bf16[512,1024]{1,0:T(8,128)(2,1)S(1)} %get-tuple-element.470.own_rows, bf16[512,1024]{1,0:T(8,128)(2,1)S(1)} %collective-permute-done.32.other_rows, ...), custom_call_target="tpu_custom_call" | custom-call | flops 11274289152 | bytes 6815744 | tf_op jit(solution)/shard_map/attend_back/pallas_call | solution.py:673
  520.9 13.0 %attend_back.7.refs_0_ = bf16[1024,768]{1,0:T(8,128)(2,1)S(1)} custom-call(s32[1]{0:T(128)} %bitcast.11.core_ref, f32[1024,128]{1,0:T(8,128)S(1)} %copy-done.72, f32[1024,128]{1,0:T(8,128)S(1)} %copy-done.69, bf16[512,1024]{1,0:T(8,128)(2,1)S(1)} %get-tuple-element.470.own_rows, bf16[512,1024]{1,0:T(8,128)(2,1)S(1)} %collective-permute-done.32.other_rows, ...), custom_call_target="tpu_custom_call" | custom-call | flops 11274289152 | bytes 6815744 | tf_op jit(solution)/shard_map/attend_back/pallas_call | solution.py:673
  548.5 3.5 collective-permute-start.43
  552.0 5.1 attn_back.3
  564.3 7.9 %collective-permute-done.47 = bf16[512,512]{0,1:T(8,128)(2,1)S(1)} collective-permute-done((bf16[512,512]{0,1:T(8,128)(2,1)S(1)}, bf16[512,512]{0,1:T(8,128)(2,1)S(1)}, u32[]{:S(2)}, u32[]{:S(2)}) %collective-permute-start.47) | collective-permute-done | bytes 524320 | tf_op jit(solution)/shard_map/ppermute | solution.py:740
  572.4 11.1 %collective-permute-done.46 = bf16[512,512]{0,1:T(8,128)(2,1)S(1)} collective-permute-done((bf16[512,512]{0,1:T(8,128)(2,1)S(1)}, bf16[512,512]{0,1:T(8,128)(2,1)S(1)}, u32[]{:S(2)}, u32[]{:S(2)}) %collective-permute-start.46) | collective-permute-done | bytes 524320 | tf_op jit(solution)/shard_map/ppermute | solution.py:740
  584.9 9.7 %collective-permute-done.45 = bf16[512,512]{0,1:T(8,128)(2,1)S(1)} collective-permute-done((bf16[512,512]{0,1:T(8,128)(2,1)S(1)}, bf16[512,512]{0,1:T(8,128)(2,1)S(1)}, u32[]{:S(2)}, u32[]{:S(2)}) %collective-permute-start.45) | collective-permute-done | bytes 524320 | tf_op jit(solution)/shard_map/ppermute | solution.py:740
  599.3 9.7 %collective-permute-done.48 = bf16[512,512]{0,1:T(8,128)(2,1)S(1)} collective-permute-done((bf16[512,512]{0,1:T(8,128)(2,1)S(1)}, bf16[512,512]{0,1:T(8,128)(2,1)S(1)}, u32[]{:S(2)}, u32[]{:S(2)}) %collective-permute-start.48) | collective-permute-done | bytes 524320 | tf_op jit(solution)/shard_map/ppermute | solution.py:745
  613.7 4.5 all-to-all-start.2
  618.3 3.4 add_convert_fusion
  621.7 3.8 collective-permute-start.53
  625.5 5.3 collective-permute-done.49
  638.0 35.2 %collective-permute-done.40 = f32[4,1024]{1,0:T(4,128)S(1)} collective-permute-done((f32[4,1024]{1,0:T(4,128)S(1)}, f32[4,1024]{1,0:T(4,128)S(1)}, u32[]{:S(2)}, u32[]{:S(2)}) %collective-permute-start.40) | collective-permute-done | bytes 16416 | tf_op jit(solution)/shard_map/ppermute | solution.py:753
  681.5 3.5 constant_dynamic-slice_fusion.4
  685.9 3.3 convert_add_fusion
  689.2 2.6 reshape.86
  691.8 2.8 constant_dynamic-slice_fusion.2
  (499 shorter events, 204.4 us)
Async XLA Ops:
  8.0 11.3 %collective-permute-start = (bf16[2,128,1024]{2,1,0:T(8,128)(2,1)}, bf16[2,128,1024]{2,1,0:T(8,128)(2,1)}, u32[]{:S(2)}, u32[]{:S(2)}) collective-permute-start(bf16[2,128,1024]{2,1,0:T(8,128)(2,1)} %dynamic-slice_bitcast_fusion.3), channel_id=1, source_target_pairs={{0,4},{4,0},{8,12},{12,8},{1,5},{5,1},{9,13},{13,9},{2,6},{6,2},{1... | collective-permute-start | bytes 1572872 | tf_op jit(solution)/shard_map/ppermute | solution.py:740
  15.0 17.9 %collective-permute-start.1 = (bf16[512,512]{1,0:T(8,128)(2,1)}, bf16[512,512]{1,0:T(8,128)(2,1)}, u32[]{:S(2)}, u32[]{:S(2)}) collective-permute-start(bf16[512,512]{1,0:T(8,128)(2,1)} %pad_maximum_fusion.24.refs_0_.refs_1_.refs_2_), channel_id=1, source_target_pairs={{0,1},{1,2},{2,3},{3,0},{4,5},{5,6},{6,7},{7,4},{8,9},{9,10},{10,1... | collective-permute-start | bytes 1572872 | tf_op jit(solution)/shard_map/ppermute | solution.py:745
  17.7 15.3 %collective-permute-start.2 = (bf16[512,512]{1,0:T(8,128)(2,1)}, bf16[512,512]{1,0:T(8,128)(2,1)}, u32[]{:S(2)}, u32[]{:S(2)}) collective-permute-start(bf16[512,512]{1,0:T(8,128)(2,1)} %pad_maximum_fusion.24.refs_0_.refs_1_.refs_2_), channel_id=1, source_target_pairs={{0,8},{4,12},{8,0},{12,4},{1,9},{5,13},{9,1},{13,5},{2,10},{6,14},... | collective-permute-start | bytes 1572872 | tf_op jit(solution)/shard_map/ppermute | solution.py:740
  21.4 58.3 %all-to-all-start = ((bf16[4,128,1024]{2,1,0:T(8,128)(2,1)}), bf16[4,128,1024]{2,1,0:T(8,128)(2,1)S(1)}, u32[]{:S(2)}, u32[]{:S(2)}) async-start(bf16[4,128,1024]{2,1,0:T(8,128)(2,1)} %pad_maximum_fusion.12), calls=%async_computation | async-start | bytes 2097152 | tf_op jit(solution)/shard_map/all_to_all | solution.py:803
  33.0 27.8 %collective-permute-start.5 = (bf16[512,512]{1,0:T(8,128)(2,1)}, bf16[512,512]{1,0:T(8,128)(2,1)S(1)}, u32[]{:S(2)}, u32[]{:S(2)}) collective-permute-start(bf16[512,512]{1,0:T(8,128)(2,1)} %collective-permute-done.1.refs_1_.refs_2_.refs_3_), channel_id=1, source_target_pairs={{0,8},{4,12},{8,0},{12,4},{1,9},{5,13},{9,1},{13,5},{2,10},{6,14},... | collective-permute-start | bytes 1572872 | tf_op jit(solution)/shard_map/ppermute | solution.py:740
  34.6 26.1 %collective-permute-start.4 = (bf16[512,512]{1,0:T(8,128)(2,1)}, bf16[512,512]{1,0:T(8,128)(2,1)}, u32[]{:S(2)}, u32[]{:S(2)}) collective-permute-start(bf16[512,512]{1,0:T(8,128)(2,1)} %collective-permute-done.1.refs_1_.refs_2_.refs_3_), channel_id=1, source_target_pairs={{0,1},{1,2},{2,3},{3,0},{4,5},{5,6},{6,7},{7,4},{8,9},{9,10},{10,1... | collective-permute-start | bytes 1572872 | tf_op jit(solution)/shard_map/ppermute | solution.py:745
  35.2 44.5 %collective-permute-start.3 = (bf16[512,1024]{1,0:T(8,128)(2,1)S(1)}, bf16[512,1024]{1,0:T(8,128)(2,1)S(1)}, u32[]{:S(2)}, u32[]{:S(2)}) collective-permute-start(bf16[512,1024]{1,0:T(8,128)(2,1)S(1)} %pad_maximum_fusion.13.refs_0_.refs_1_), channel_id=1, source_target_pairs={{0,8},{4,12},{8,0},{12,4},{1,9},{5,13},{9,1},{13,5},{2,10},{6,14},... | collective-permute-start | bytes 3145736 | tf_op jit(solution)/shard_map/ppermute | solution.py:740
  61.6 15.8 %collective-permute-start.6 = (bf16[512,512]{1,0:T(8,128)(2,1)}, bf16[512,512]{1,0:T(8,128)(2,1)}, u32[]{:S(2)}, u32[]{:S(2)}) collective-permute-start(bf16[512,512]{1,0:T(8,128)(2,1)} %collective-permute-done.4.refs_2_.refs_3_.refs_0_.refs_4_), channel_id=1, source_target_pairs={{0,1},{1,2},{2,3},{3,0},{4,5},{5,6},{6,7},{7,4},{8,9},{9,10},{10,1... | collective-permute-start | bytes 1572872 | tf_op jit(solution)/shard_map/ppermute | solution.py:745
  77.4 26.4 %collective-permute-start.9 = (bf16[512,1024]{1,0:T(8,128)(2,1)S(1)}, bf16[512,1024]{1,0:T(8,128)(2,1)}, u32[]{:S(2)}, u32[]{:S(2)}) collective-permute-start(bf16[512,1024]{1,0:T(8,128)(2,1)S(1)} %pad_maximum_fusion.13.refs_0_.refs_1_), channel_id=1, source_target_pairs={{0,1},{1,2},{2,3},{3,0},{4,5},{5,6},{6,7},{7,4},{8,9},{9,10},{10,1... | collective-permute-start | bytes 3145736 | tf_op jit(solution)/shard_map/ppermute | solution.py:745
  82.5 28.4 %collective-permute-start.7 = (bf16[512,1024]{1,0:T(8,128)(2,1)}, bf16[512,1024]{1,0:T(8,128)(2,1)}, u32[]{:S(2)}, u32[]{:S(2)}) collective-permute-start(bf16[512,1024]{1,0:T(8,128)(2,1)} %norm_in.2.own_rows), channel_id=1, source_target_pairs={{0,4},{4,0},{8,12},{12,8},{1,5},{5,1},{9,13},{13,9},{2,6},{6,2},{1... | collective-permute-start | bytes 3145736 | tf_op jit(solution)/shard_map/ppermute | solution.py:740
  82.5 15.0 %collective-permute-start.10 = (bf16[512,512]{1,0:T(8,128)(2,1)}, bf16[512,512]{1,0:T(8,128)(2,1)S(1)}, u32[]{:S(2)}, u32[]{:S(2)}) collective-permute-start(bf16[512,512]{1,0:T(8,128)(2,1)} %collective-permute-done.4.refs_2_.refs_3_.refs_0_.refs_4_), channel_id=1, source_target_pairs={{0,8},{4,12},{8,0},{12,4},{1,9},{5,13},{9,1},{13,5},{2,10},{6,14},... | collective-permute-start | bytes 1572872 | tf_op jit(solution)/shard_map/ppermute | solution.py:740
  84.1 24.3 %collective-permute-start.8 = (bf16[512,512]{1,0:T(8,128)(2,1)}, bf16[512,512]{1,0:T(8,128)(2,1)S(1)}, u32[]{:S(2)}, u32[]{:S(2)}) collective-permute-start(bf16[512,512]{1,0:T(8,128)(2,1)} %collective-permute-done.6.refs_3_.refs_4_.refs_1_.refs_5_), channel_id=1, source_target_pairs={{0,8},{4,12},{8,0},{12,4},{1,9},{5,13},{9,1},{13,5},{2,10},{6,14},... | collective-permute-start | bytes 1572872 | tf_op jit(solution)/shard_map/ppermute | solution.py:740
  87.0 250.1 %copy-start.70 = (f32[1024,128]{1,0:T(8,128)}, f32[1024,128]{1,0:T(8,128)S(1)}, u32[]{:S(2)}) copy-start(f32[1024,128]{1,0:T(8,128)S(1)} %pad_maximum_fusion.25.cos_ref) | copy-start | bytes 1572868
  87.5 249.7 %copy-start.67 = (f32[1024,128]{1,0:T(8,128)}, f32[1024,128]{1,0:T(8,128)S(1)}, u32[]{:S(2)}) copy-start(f32[1024,128]{1,0:T(8,128)S(1)} %pad_maximum_fusion.26.sin_ref) | copy-start | bytes 1572868
  97.5 267.8 %copy-start.40 = (bf16[512,512]{1,0:T(8,128)(2,1)}, bf16[512,512]{1,0:T(8,128)(2,1)S(1)}, u32[]{:S(2)}) copy-start(bf16[512,512]{1,0:T(8,128)(2,1)S(1)} %collective-permute-done.10.refs_6_.refs_7_.refs_2_.refs_8_) | copy-start | bytes 1572868
  108.3 257.0 %copy-start.42 = (bf16[512,512]{1,0:T(8,128)(2,1)}, bf16[512,512]{1,0:T(8,128)(2,1)S(1)}, u32[]{:S(2)}) copy-start(bf16[512,512]{1,0:T(8,128)(2,1)S(1)} %collective-permute-done.8.refs_7_.refs_8_.refs_3_.refs_9_) | copy-start | bytes 1572868
  108.3 27.1 %collective-permute-start.12 = (bf16[512,1024]{1,0:T(8,128)(2,1)}, bf16[512,1024]{1,0:T(8,128)(2,1)S(1)}, u32[]{:S(2)}, u32[]{:S(2)}) collective-permute-start(bf16[512,1024]{1,0:T(8,128)(2,1)} %collective-permute-done.9.refs_1_.refs_2_), channel_id=1, source_target_pairs={{0,1},{1,2},{2,3},{3,0},{4,5},{5,6},{6,7},{7,4},{8,9},{9,10},{10,1... | collective-permute-start | bytes 3145736 | tf_op jit(solution)/shard_map/ppermute | solution.py:745
  133.7 3.8 collective-permute-start.11
  133.8 26.2 %collective-permute-start.15 = (bf16[512,1024]{1,0:T(8,128)(2,1)}, bf16[512,1024]{1,0:T(8,128)(2,1)S(1)}, u32[]{:S(2)}, u32[]{:S(2)}) collective-permute-start(bf16[512,1024]{1,0:T(8,128)(2,1)} %collective-permute-done.9.refs_1_.refs_2_), channel_id=1, source_target_pairs={{0,8},{4,12},{8,0},{12,4},{1,9},{5,13},{9,1},{13,5},{2,10},{6,14},... | collective-permute-start | bytes 3145736 | tf_op jit(solution)/shard_map/ppermute | solution.py:740
  135.4 183.8 %copy-start.9 = (bf16[512,1024]{1,0:T(8,128)(2,1)}, bf16[512,1024]{1,0:T(8,128)(2,1)S(1)}, u32[]{:S(2)}) copy-start(bf16[512,1024]{1,0:T(8,128)(2,1)S(1)} %collective-permute-done.12.refs_2_.refs_3_) | copy-start | bytes 3145732
  135.4 27.3 %collective-permute-start.14 = (bf16[512,1024]{1,0:T(8,128)(2,1)S(1)}, bf16[512,1024]{1,0:T(8,128)(2,1)S(1)}, u32[]{:S(2)}, u32[]{:S(2)}) collective-permute-start(bf16[512,1024]{1,0:T(8,128)(2,1)S(1)} %collective-permute-done.12.refs_2_.refs_3_), channel_id=1, source_target_pairs={{0,1},{1,2},{2,3},{3,0},{4,5},{5,6},{6,7},{7,4},{8,9},{9,10},{10,1... | collective-permute-start | bytes 3145736 | tf_op jit(solution)/shard_map/ppermute | solution.py:745
  136.0 46.5 %collective-permute-start.16 = (bf16[512,1024]{1,0:T(8,128)(2,1)S(1)}, bf16[512,1024]{1,0:T(8,128)(2,1)S(1)}, u32[]{:S(2)}, u32[]{:S(2)}) collective-permute-start(bf16[512,1024]{1,0:T(8,128)(2,1)S(1)} %collective-permute-done.12.refs_2_.refs_3_), channel_id=1, source_target_pairs={{0,8},{4,12},{8,0},{12,4},{1,9},{5,13},{9,1},{13,5},{2,10},{6,14},... | collective-permute-start | bytes 3145736 | tf_op jit(solution)/shard_map/ppermute | solution.py:740
  160.1 159.1 %copy-start.11 = (bf16[512,1024]{1,0:T(8,128)(2,1)}, bf16[512,1024]{1,0:T(8,128)(2,1)S(1)}, u32[]{:S(2)}) copy-start(bf16[512,1024]{1,0:T(8,128)(2,1)S(1)} %collective-permute-done.15.refs_5_.refs_6_) | copy-start | bytes 3145732
  162.7 41.9 %collective-permute-start.17 = (bf16[512,1024]{1,0:T(8,128)(2,1)S(1)}, bf16[512,1024]{1,0:T(8,128)(2,1)S(1)}, u32[]{:S(2)}, u32[]{:S(2)}) collective-permute-start(bf16[512,1024]{1,0:T(8,128)(2,1)S(1)} %collective-permute-done.14.refs_3_.refs_4_), channel_id=1, source_target_pairs={{0,8},{4,12},{8,0},{12,4},{1,9},{5,13},{9,1},{13,5},{2,10},{6,14},... | collective-permute-start | bytes 3145736 | tf_op jit(solution)/shard_map/ppermute | solution.py:740
  163.2 41.4 %collective-permute-start.13 = (bf16[512,1024]{1,0:T(8,128)(2,1)S(1)}, bf16[512,1024]{1,0:T(8,128)(2,1)S(1)}, u32[]{:S(2)}, u32[]{:S(2)}) collective-permute-start(bf16[512,1024]{1,0:T(8,128)(2,1)S(1)} %get-tuple-element.402.own_rows), channel_id=1, source_target_pairs={{0,4},{4,0},{8,12},{12,8},{1,5},{5,1},{9,13},{13,9},{2,6},{6,2},{1... | collective-permute-start | bytes 3145736 | tf_op jit(solution)/shard_map/ppermute | solution.py:740
  221.1 2.7 collective-permute-start.18
  225.7 25.8 %collective-permute-start.19 = (bf16[512,1024]{1,0:T(8,128)(2,1)S(1)}, bf16[512,1024]{1,0:T(8,128)(2,1)S(1)}, u32[]{:S(2)}, u32[]{:S(2)}) collective-permute-start(bf16[512,1024]{1,0:T(8,128)(2,1)S(1)} %get-tuple-element.392), channel_id=1, source_target_pairs={{0,16},{1,17},{2,18},{3,19},{4,20},{5,21},{6,22},{7,23},{8,24},{9,... | collective-permute-start | bytes 3145736 | tf_op jit(solution)/shard_map/ppermute | solution.py:27
  253.3 2.7 collective-permute-start.20
  278.6 2.7 collective-permute-start.21
  284.7 2.7 collective-permute-start.22
  303.6 2.7 collective-permute-start.23
  310.7 2.7 collective-permute-start.24
  327.7 2.7 collective-permute-start.25
  334.4 2.7 collective-permute-start.26
  371.0 2.7 collective-permute-start.27
  381.5 42.0 %all-to-all-start.1 = ((bf16[4,128,1024]{2,1,0:T(8,128)(2,1)}), bf16[4,128,1024]{2,1,0:T(8,128)(2,1)}, u32[]{:S(2)}, u32[]{:S(2)}) async-start(bf16[4,128,1024]{2,1,0:T(8,128)(2,1)} %bitcast.122), calls=%async_computation.1 | async-start | bytes 2097152 | tf_op jit(solution)/shard_map/all_to_all | solution.py:808
  385.8 27.6 %collective-permute-start.29 = (bf16[512,1024]{1,0:T(8,128)(2,1)}, bf16[512,1024]{1,0:T(8,128)(2,1)S(1)}, u32[]{:S(2)}, u32[]{:S(2)}) collective-permute-start(bf16[512,1024]{1,0:T(8,128)(2,1)} %copy-done.52), channel_id=1, source_target_pairs={{16,0},{17,1},{18,2},{19,3},{20,4},{21,5},{22,6},{23,7},{24,8},{25... | collective-permute-start | bytes 3145736 | tf_op jit(solution)/shard_map/ppermute | solution.py:27
  416.6 8.8 %collective-permute-start.30 = (bf16[512,1024]{1,0:T(8,128)(2,1)}, bf16[512,1024]{1,0:T(8,128)(2,1)}, u32[]{:S(2)}, u32[]{:S(2)}) collective-permute-start(bf16[512,1024]{1,0:T(8,128)(2,1)} %get-tuple-element.412.own_rows), channel_id=1, source_target_pairs={{0,4},{4,0},{8,12},{12,8},{1,5},{5,1},{9,13},{13,9},{2,6},{6,2},{1... | collective-permute-start | bytes 3145736 | tf_op jit(solution)/shard_map/ppermute | solution.py:740
  456.1 14.9 %collective-permute-start.31 = (bf16[512,1024]{1,0:T(8,128)(2,1)S(1)}, bf16[512,1024]{1,0:T(8,128)(2,1)S(1)}, u32[]{:S(2)}, u32[]{:S(2)}) collective-permute-start(bf16[512,1024]{1,0:T(8,128)(2,1)S(1)} %get-tuple-element.417), channel_id=1, source_target_pairs={{0,4},{4,0},{8,12},{12,8},{1,5},{5,1},{9,13},{13,9},{2,6},{6,2},{1... | collective-permute-start | bytes 3145736 | tf_op jit(solution)/shard_map/ppermute | solution.py:740
  457.5 26.1 %collective-permute-start.34 = (bf16[512,1024]{0,1:T(8,128)(2,1)S(1)}, bf16[512,1024]{0,1:T(8,128)(2,1)S(1)}, u32[]{:S(2)}, u32[]{:S(2)}) collective-permute-start(bf16[512,1024]{0,1:T(8,128)(2,1)S(1)} %pad_maximum_fusion.15), channel_id=1, source_target_pairs={{0,8},{4,12},{8,0},{12,4},{1,9},{5,13},{9,1},{13,5},{2,10},{6,14},... | collective-permute-start | bytes 3145736 | tf_op jit(solution)/shard_map/ppermute | solution.py:740
  469.2 35.7 %collective-permute-start.33 = (bf16[512,1024]{0,1:T(8,128)(2,1)S(1)}, bf16[512,1024]{0,1:T(8,128)(2,1)S(1)}, u32[]{:S(2)}, u32[]{:S(2)}) collective-permute-start(bf16[512,1024]{0,1:T(8,128)(2,1)S(1)} %pad_maximum_fusion.16), channel_id=1, source_target_pairs={{0,8},{4,12},{8,0},{12,4},{1,9},{5,13},{9,1},{13,5},{2,10},{6,14},... | collective-permute-start | bytes 3145736 | tf_op jit(solution)/shard_map/ppermute | solution.py:740
  483.6 24.5 %collective-permute-start.32 = (bf16[512,1024]{1,0:T(8,128)(2,1)S(1)}, bf16[512,1024]{1,0:T(8,128)(2,1)S(1)}, u32[]{:S(2)}, u32[]{:S(2)}) collective-permute-start(bf16[512,1024]{1,0:T(8,128)(2,1)S(1)} %get-tuple-element.470.own_rows), channel_id=1, source_target_pairs={{0,4},{4,0},{8,12},{12,8},{1,5},{5,1},{9,13},{13,9},{2,6},{6,2},{1... | collective-permute-start | bytes 3145736 | tf_op jit(solution)/shard_map/ppermute | solution.py:740
  488.9 58.5 %collective-permute-start.35 = (bf16[512,1024]{0,1:T(8,128)(2,1)S(1)}, bf16[512,1024]{0,1:T(8,128)(2,1)S(1)}, u32[]{:S(2)}, u32[]{:S(2)}) collective-permute-start(bf16[512,1024]{0,1:T(8,128)(2,1)S(1)} %add_convert_fusion.2), channel_id=1, source_target_pairs={{0,3},{1,0},{2,1},{3,2},{4,7},{5,4},{6,5},{7,6},{8,11},{9,8},{10,9... | collective-permute-start | bytes 3145736 | tf_op jit(solution)/shard_map/ppermute | solution.py:745
  506.6 50.7 %collective-permute-start.42 = (bf16[512,1024]{0,1:T(8,128)(2,1)S(1)}, bf16[512,1024]{0,1:T(8,128)(2,1)S(1)}, u32[]{:S(2)}, u32[]{:S(2)}) collective-permute-start(bf16[512,1024]{0,1:T(8,128)(2,1)S(1)} %pad_maximum_fusion.17), channel_id=1, source_target_pairs={{0,8},{4,12},{8,0},{12,4},{1,9},{5,13},{9,1},{13,5},{2,10},{6,14},... | collective-permute-start | bytes 3145736 | tf_op jit(solution)/shard_map/ppermute | solution.py:740
  548.5 47.7 %collective-permute-start.43 = (bf16[512,1024]{0,1:T(8,128)(2,1)S(1)}, bf16[512,1024]{0,1:T(8,128)(2,1)S(1)}, u32[]{:S(2)}, u32[]{:S(2)}) collective-permute-start(bf16[512,1024]{0,1:T(8,128)(2,1)S(1)} %add_convert_fusion.1), channel_id=1, source_target_pairs={{0,3},{1,0},{2,1},{3,2},{4,7},{5,4},{6,5},{7,6},{8,11},{9,8},{10,9... | collective-permute-start | bytes 3145736 | tf_op jit(solution)/shard_map/ppermute | solution.py:745
  557.1 39.6 %collective-permute-start.36 = (bf16[512,1024]{1,0:T(8,128)(2,1)S(1)}, bf16[512,1024]{1,0:T(8,128)(2,1)S(1)}, u32[]{:S(2)}, u32[]{:S(2)}) collective-permute-start(bf16[512,1024]{1,0:T(8,128)(2,1)S(1)} %get-tuple-element.476), channel_id=1, source_target_pairs={{0,4},{4,0},{8,12},{12,8},{1,5},{5,1},{9,13},{13,9},{2,6},{6,2},{1... | collective-permute-start | bytes 3145736 | tf_op jit(solution)/shard_map/ppermute | solution.py:740
  557.4 14.8 %collective-permute-start.47 = (bf16[512,512]{0,1:T(8,128)(2,1)S(1)}, bf16[512,512]{0,1:T(8,128)(2,1)S(1)}, u32[]{:S(2)}, u32[]{:S(2)}) collective-permute-start(bf16[512,512]{0,1:T(8,128)(2,1)S(1)} %pad_maximum_fusion.30), channel_id=1, source_target_pairs={{0,8},{4,12},{8,0},{12,4},{1,9},{5,13},{9,1},{13,5},{2,10},{6,14},... | collective-permute-start | bytes 1572872 | tf_op jit(solution)/shard_map/ppermute | solution.py:740
  559.1 24.3 %collective-permute-start.46 = (bf16[512,512]{0,1:T(8,128)(2,1)S(1)}, bf16[512,512]{0,1:T(8,128)(2,1)S(1)}, u32[]{:S(2)}, u32[]{:S(2)}) collective-permute-start(bf16[512,512]{0,1:T(8,128)(2,1)S(1)} %pad_maximum_fusion.29), channel_id=1, source_target_pairs={{0,8},{4,12},{8,0},{12,4},{1,9},{5,13},{9,1},{13,5},{2,10},{6,14},... | collective-permute-start | bytes 1572872 | tf_op jit(solution)/shard_map/ppermute | solution.py:740
  561.5 33.2 %collective-permute-start.45 = (bf16[512,512]{0,1:T(8,128)(2,1)S(1)}, bf16[512,512]{0,1:T(8,128)(2,1)S(1)}, u32[]{:S(2)}, u32[]{:S(2)}) collective-permute-start(bf16[512,512]{0,1:T(8,128)(2,1)S(1)} %pad_maximum_fusion.28), channel_id=1, source_target_pairs={{0,8},{4,12},{8,0},{12,4},{1,9},{5,13},{9,1},{13,5},{2,10},{6,14},... | collective-permute-start | bytes 1572872 | tf_op jit(solution)/shard_map/ppermute | solution.py:740
  572.2 62.4 %collective-permute-start.28 = (bf16[2,128,1024]{2,1,0:T(8,128)(2,1)}, bf16[2,128,1024]{2,1,0:T(8,128)(2,1)}, u32[]{:S(2)}, u32[]{:S(2)}) collective-permute-start(bf16[2,128,1024]{2,1,0:T(8,128)(2,1)} %dynamic-slice_bitcast_fusion.1), channel_id=1, source_target_pairs={{0,4},{4,0},{8,12},{12,8},{1,5},{5,1},{9,13},{13,9},{2,6},{6,2},{1... | collective-permute-start | bytes 1572872 | tf_op jit(solution)/shard_map/ppermute | solution.py:740
  583.4 92.1 %collective-permute-start.52 = (bf16[512,1024]{0,1:T(8,128)(2,1)}, bf16[512,1024]{0,1:T(8,128)(2,1)}, u32[]{:S(2)}, u32[]{:S(2)}) collective-permute-start(bf16[512,1024]{0,1:T(8,128)(2,1)} %pad_maximum_fusion.23), channel_id=1, source_target_pairs={{0,8},{4,12},{8,0},{12,4},{1,9},{5,13},{9,1},{13,5},{2,10},{6,14},... | collective-permute-start | bytes 3145736 | tf_op jit(solution)/shard_map/ppermute | solution.py:740
  594.7 80.8 %collective-permute-start.44 = (bf16[512,512]{0,1:T(8,128)(2,1)}, bf16[512,512]{0,1:T(8,128)(2,1)}, u32[]{:S(2)}, u32[]{:S(2)}) collective-permute-start(bf16[512,512]{0,1:T(8,128)(2,1)} %pad_maximum_fusion.27), channel_id=1, source_target_pairs={{0,8},{4,12},{8,0},{12,4},{1,9},{5,13},{9,1},{13,5},{2,10},{6,14},... | collective-permute-start | bytes 1572872 | tf_op jit(solution)/shard_map/ppermute | solution.py:740
  596.2 12.8 %collective-permute-start.48 = (bf16[512,512]{0,1:T(8,128)(2,1)S(1)}, bf16[512,512]{0,1:T(8,128)(2,1)S(1)}, u32[]{:S(2)}, u32[]{:S(2)}) collective-permute-start(bf16[512,512]{0,1:T(8,128)(2,1)S(1)} %add_convert_fusion.5), channel_id=1, source_target_pairs={{0,3},{1,0},{2,1},{3,2},{4,7},{5,4},{6,5},{7,6},{8,11},{9,8},{10,9... | collective-permute-start | bytes 1572872 | tf_op jit(solution)/shard_map/ppermute | solution.py:745
  599.0 22.7 %collective-permute-start.38 = (f32[4,1024]{1,0:T(4,128)S(1)}, f32[4,1024]{1,0:T(4,128)S(1)}, u32[]{:S(2)}, u32[]{:S(2)}) collective-permute-start(f32[4,1024]{1,0:T(4,128)S(1)} %maximum_select_fusion.5), channel_id=1, source_target_pairs={{0,4},{4,0},{8,12},{12,8},{1,5},{5,1},{9,13},{13,9},{2,6},{6,2},{1... | collective-permute-start | bytes 49160 | tf_op jit(solution)/shard_map/ppermute | solution.py:740
  610.0 20.8 %collective-permute-start.49 = (bf16[512,512]{0,1:T(8,128)(2,1)}, bf16[512,512]{0,1:T(8,128)(2,1)}, u32[]{:S(2)}, u32[]{:S(2)}) collective-permute-start(bf16[512,512]{0,1:T(8,128)(2,1)} %add_convert_fusion.4), channel_id=1, source_target_pairs={{0,3},{1,0},{2,1},{3,2},{4,7},{5,4},{6,5},{7,6},{8,11},{9,8},{10,9... | collective-permute-start | bytes 1572872 | tf_op jit(solution)/shard_map/ppermute | solution.py:745
  613.7 86.1 %all-to-all-start.2 = ((bf16[4,128,1024]{2,1,0:T(8,128)(2,1)}), bf16[4,128,1024]{2,1,0:T(8,128)(2,1)}, u32[]{:S(2)}, u32[]{:S(2)}) async-start(bf16[4,128,1024]{2,1,0:T(8,128)(2,1)} %bitcast.19), calls=%async_computation.2 | async-start | bytes 2097152 | tf_op jit(solution)/shard_map/all_to_all | solution.py:808
  621.7 64.2 %collective-permute-start.53 = (bf16[512,1024]{0,1:T(8,128)(2,1)}, bf16[512,1024]{0,1:T(8,128)(2,1)}, u32[]{:S(2)}, u32[]{:S(2)}) collective-permute-start(bf16[512,1024]{0,1:T(8,128)(2,1)} %add_convert_fusion), channel_id=1, source_target_pairs={{0,3},{1,0},{2,1},{3,2},{4,7},{5,4},{6,5},{7,6},{8,11},{9,8},{10,9... | collective-permute-start | bytes 3145736 | tf_op jit(solution)/shard_map/ppermute | solution.py:745
  630.8 3.7 collective-permute-start.39
  634.6 43.9 %collective-permute-start.50 = (bf16[512,512]{0,1:T(8,128)(2,1)S(1)}, bf16[512,512]{0,1:T(8,128)(2,1)}, u32[]{:S(2)}, u32[]{:S(2)}) collective-permute-start(bf16[512,512]{0,1:T(8,128)(2,1)S(1)} %add_convert_fusion.3), channel_id=1, source_target_pairs={{0,3},{1,0},{2,1},{3,2},{4,7},{5,4},{6,5},{7,6},{8,11},{9,8},{10,9... | collective-permute-start | bytes 1572872 | tf_op jit(solution)/shard_map/ppermute | solution.py:745
  634.6 38.6 %collective-permute-start.40 = (f32[4,1024]{1,0:T(4,128)S(1)}, f32[4,1024]{1,0:T(4,128)S(1)}, u32[]{:S(2)}, u32[]{:S(2)}) collective-permute-start(f32[4,1024]{1,0:T(4,128)S(1)} %add.160), channel_id=1, source_target_pairs={{0,1},{1,0},{2,3},{3,2},{4,5},{5,4},{6,7},{7,6},{8,9},{9,8},{10,11... | collective-permute-start | bytes 49160 | tf_op jit(solution)/shard_map/ppermute | solution.py:753
  673.2 4.7 collective-permute-start.41
  685.9 15.1 %collective-permute-start.51 = (f32[256,512]{0,1:T(8,128)}, f32[256,512]{0,1:T(8,128)}, u32[]{:S(2)}, u32[]{:S(2)}) collective-permute-start(f32[256,512]{0,1:T(8,128)} %bitcast.116), channel_id=1, source_target_pairs={{0,4},{4,0},{8,12},{12,8},{1,5},{5,1},{9,13},{13,9},{2,6},{6,2},{1... | collective-permute-start | bytes 1572872 | tf_op jit(solution)/shard_map/ppermute | solution.py:740
  699.3 7.3 %collective-permute-start.54 = (f32[256,1024]{1,0:T(8,128)}, f32[256,1024]{1,0:T(8,128)}, u32[]{:S(2)}, u32[]{:S(2)}) collective-permute-start(f32[256,1024]{1,0:T(8,128)} %bitcast.130), channel_id=1, source_target_pairs={{0,4},{4,0},{8,12},{12,8},{1,5},{5,1},{9,13},{13,9},{2,6},{6,2},{1... | collective-permute-start | bytes 3145736 | tf_op jit(solution)/shard_map/ppermute | solution.py:740
  700.9 3.3 collective-permute-start.37
  (128 other events, 1350.9 us)

commit v5 on v4

--- a/solution.py
+++ b/solution.py
@@ -338,8 +338,14 @@
     return jnp.dot(left, right, preferred_element_type=jnp.float32)
 
 
+def columns_of(ref, cols):
+    return ref[...] if ref.shape[1] == cols.stop - cols.start else ref[:, cols]
+
+
 def model_weight(owns, others, cols):
-    sides = [jnp.concatenate([ref[:, cols] for ref in refs], axis=1) for refs in (owns, others)]
+    sides = [
+        jnp.concatenate([columns_of(ref, cols) for ref in refs], axis=1) for refs in (owns, others)
+    ]
     return jnp.concatenate(sides, axis=0)
 
 
@@ -517,12 +523,13 @@
     gelu_ref, slope_ref = refs[2 * pieces :]
     half = own_rows.shape[0]
     size = owns[0].shape[1] // 2
+    cols = slice(0, size)
     step = half // 2
     units = [(j, i) for j in range(pieces) for i in range(4)]
 
     def product(j, i):
         rows = (own_rows, other_rows)[i // 2][i % 2 * step : (i % 2 + 1) * step]
-        return dot_nn(rows, stacked_up([owns[j][:, :size], others[j][:, :size]]))
+        return dot_nn(rows, stacked_up([columns_of(owns[j], cols), columns_of(others[j], cols)]))
 
     ahead = product(*units[0])
     for spot, (j, i) in enumerate(units):
@@ -541,9 +548,11 @@
     out_ref = refs[-1]
     size = owns[0].shape[1] // 2
     rows = stacked_up([own_rows[...], other_rows[...]])
+    taken = slice(size, 2 * size)
     for j in range(pieces):
         cols = slice(j * size, (j + 1) * size)
-        d_gelu = dot_nn(rows, stacked_up([owns[j][:, size:], others[j][:, size:]]))
+        weight = stacked_up([columns_of(owns[j], taken), columns_of(others[j], taken)])
+        d_gelu = dot_nn(rows, weight)
         out_ref[:, cols] = (d_gelu * slope_ref[:, cols].astype(jnp.float32)).astype(jnp.bfloat16)
 
 
@@ -650,42 +659,48 @@
     return pl.CostEstimate(flops=flops, bytes_accessed=size, transcendentals=0)
 
 
-def on_chip(kernel, name, outs, *operands, limit=ROWS_VMEM, flops=0):
+def without(kernel, first, count):
+    return lambda *refs: kernel(*refs[:first], *refs[first + count :])
+
+
+def on_chip(kernel, name, outs, *operands, limit=ROWS_VMEM, flops=0, waits=()):
     shapes = [jax.ShapeDtypeStruct(shape, dtype) for shape, dtype in outs]
     space = pl.BlockSpec(memory_space=pltpu.VMEM)
     return pl.pallas_call(
-        kernel,
-        in_specs=[space] * len(operands),
+        without(kernel, len(operands), len(waits)),
+        in_specs=[space] * len(operands) + [pl.BlockSpec(memory_space=pl.ANY)] * len(waits),
         out_specs=[space] * len(outs),
         out_shape=shapes,
         compiler_params=pltpu.CompilerParams(vmem_limit_bytes=limit),
         cost_estimate=work(flops, (*operands, *shapes)),
         name=name,
-    )(*operands)
+    )(*operands, *waits)
 
 
 def whole_block(array):
     return pl.BlockSpec(array.shape, lambda j: (0,) * array.ndim)
 
 
-def by_pairs(kernel, name, core, operands, pieces, blocks, outs, scratch, flops):
+def by_pairs(kernel, name, core, operands, pieces, blocks, outs, scratch, flops, waits):
     shapes = [jax.ShapeDtypeStruct(shape, dtype) for shape, dtype, _ in outs]
+    taken = 1 + len(operands) + 2 * len(pieces[0]) + len(blocks)
     return pl.pallas_call(
-        functools.partial(kernel, len(pieces[0])),
+        without(functools.partial(kernel, len(pieces[0])), taken, len(waits)),
         grid=(len(pieces[0]),),
         in_specs=[pl.BlockSpec(memory_space=pltpu.SMEM)]
         + [whole_block(array) for array in (*operands, *pieces[0], *pieces[1])]
-        + [spec for _, spec in blocks],
+        + [spec for _, spec in blocks]
+        + [pl.BlockSpec(memory_space=pl.ANY)] * len(waits),
         out_specs=[spec for _, _, spec in outs],
         out_shape=shapes,
         scratch_shapes=scratch,
         compiler_params=pltpu.CompilerParams(vmem_limit_bytes=KERNEL_VMEM),
         cost_estimate=work(flops, (*operands, *pieces[0], *pieces[1], *shapes)),
         name=name,
-    )(core, *operands, *pieces[0], *pieces[1], *[array for array, _ in blocks])
-
-
-def attend(core, tables, rows, pieces):
+    )(core, *operands, *pieces[0], *pieces[1], *[array for array, _ in blocks], *waits)
+
+
+def attend(core, tables, rows, pieces, waits):
     half, features = rows[0].shape
     length, count = 2 * half, len(pieces[0])
     lanes = ((count, length, 128), jnp.bfloat16, pl.BlockSpec((1, length, 128), lambda j: (j, 0, 0)))
@@ -701,10 +716,11 @@
         (lanes, lanes, lanes, lse, mixed),
         [pltpu.VMEM((features, 384), jnp.bfloat16)],
         count * length * (2 * features * 384 + 2 * PAIR_WORK * length),
-    )
-
-
-def attend_back(core, tables, rows, pieces, base, q, k, v, lse):
+        waits,
+    )
+
+
+def attend_back(core, tables, rows, pieces, base, waits, q, k, v, lse):
     half, features = rows[0].shape
     length, count = 2 * half, len(pieces[0])
     lanes = pl.BlockSpec((1, length, 128), lambda j: (base + j, 0, 0))
@@ -720,10 +736,11 @@
         (out,),
         [pltpu.VMEM((features, 128), jnp.bfloat16)] + [pltpu.VMEM((length, 128), jnp.float32)] * 3,
         count * length * (2 * features * 128 + 5 * PAIR_WORK * length),
+        waits,
     )[0]
 
 
-def model_rows(name, lefts, pieces, cols):
+def model_rows(name, lefts, pieces, cols, waits=()):
     owns, others = pieces
     length, width = lefts[0].shape[0], 2 * owns[0].shape[0]
     outs = (((length // 2, width), jnp.float32), ((length // 2, width), jnp.bfloat16))
@@ -731,7 +748,8 @@
     hidden = sum(left.shape[1] for left in lefts)
     flops = 2 * length * width * hidden
     operands = (*lefts, *owns, *others)
-    own, other = on_chip(kernel, name, outs, *operands, limit=KERNEL_VMEM, flops=flops)
+    more = {"limit": KERNEL_VMEM, "flops": flops, "waits": waits}
+    own, other = on_chip(kernel, name, outs, *operands, **more)
     return own, flip_pairs(other, 1)
 
 
@@ -745,22 +763,36 @@
     return lax.ppermute(block, "tensor", [(i, (i + step) % size) for i in range(size)])
 
 
-def summed_everywhere(value):
-    for distance in (1, 2):
-        value = value + flip_pairs(value, distance)
-    size = lax.axis_size("tensor")
-    for distance in (1, 2):
-        value = value + lax.ppermute(value, "tensor", [(i, i ^ distance) for i in range(size)])
-    return value
-
-
-class Sequence:
-    def __init__(self, token):
-        self.token = token
-
-    def step(self, *values):
-        values, self.token = lax.optimization_barrier((values, self.token))
-        return values[0] if len(values) == 1 else values
+def pack_kernel(first_ref, second_ref, own_ref, other_ref):
+    half, width = own_ref.shape[0], first_ref.shape[1]
+    own_ref[:, :width] = first_ref[:half]
+    own_ref[:, width:] = second_ref[:half]
+    other_ref[:, :width] = first_ref[half:].astype(jnp.bfloat16)
+    other_ref[:, width:] = second_ref[half:].astype(jnp.bfloat16)
+
+
+def last_sum_kernel(core_ref, own_ref, other_ref, moved_ref, keep_ref, send_ref):
+    rows = keep_ref.shape[0]
+
+    def total(block):
+        spot = pl.ds(pl.multiple_of(block * rows, rows), rows)
+        return own_ref[spot, :] + wide(other_ref, spot) + wide(moved_ref, spot)
+
+    keep_ref[...] = total(core_ref[0])
+    send_ref[...] = total(1 - core_ref[0])
+
+
+def joined_kernel(spots, core_ref, keep_ref, sent_ref, column_ref, row_ref):
+    size = row_ref.shape[0] // 2
+    for core in range(2):
+
+        @pl.when(core_ref[0] == core)
+        def _():
+            for place, source in ((core, keep_ref), (1 - core, sent_ref)):
+                for start, stop, to in spots:
+                    step = stop - start
+                    column_ref[:, to + place * step : to + (place + 1) * step] = source[:, start:stop]
+                row_ref[place * size : (place + 1) * size] = source[:, spots[-1][1] :].T
 
 
 def per_chip(
@@ -827,47 +859,30 @@
         return lax.dynamic_slice(local, (size * core, wide_half * upper), (size, wide_half)).T
 
     core_word = core.astype(jnp.int32).reshape(1)
-    order = Sequence(core_word)
-    pieces = {
-        "attn": [jnp.concatenate([columns(qkv_weight[0]), rows(out_weight[0])], axis=1)],
-        "mlp": [jnp.concatenate([columns(up_weight[0]), rows(down_weight[0])], axis=1)],
-    }
-    flown = {name: [] for name in pieces}
-    ringing = {}
-
-    def flip(name):
-        flown[name].append(flip_pairs(order.step(pieces[name][-1]), 2))
-
-    def flipped(name, j):
-        flown[name][j] = order.step(flown[name][j])
-
-    def ring(name):
-        ringing[name] = passed_on(order.step(pieces[name][-1]), 1)
-
-    def caught(name):
-        pieces[name].append(order.step(ringing.pop(name)))
+    attn_piece = jnp.concatenate([columns(qkv_weight[0]), rows(out_weight[0])], axis=1)
+    mlp_piece = jnp.concatenate([columns(up_weight[0]), rows(down_weight[0])], axis=1)
+    units = tensor * mlp_piece.shape[1] // 2
+    ups, downs = slice(0, units // tensor), slice(units // tensor, 2 * units // tensor)
+
+    def spread(piece):
+        pieces = [piece]
+        for _ in range(tensor - 1):
+            pieces.append(passed_on(pieces[-1], 1))
+        return pieces
+
+    attn_own, mlp_own = spread(attn_piece), spread(mlp_piece)
+    attn_other = [flip_pairs(piece, 2) for piece in attn_own]
+    mlp_other = [flip_pairs(piece, 2) for piece in mlp_own[:-1]]
+    up_last, down_last = (flip_pairs(mlp_own[-1][:, cols], 2) for cols in (ups, downs))
+    w_attn = (attn_own, attn_other)
+    w_up = (mlp_own, mlp_other + [up_last])
+    w_down = (mlp_own, mlp_other + [down_last])
 
     group_count = group_weights.shape[0]
     matches = group_ids[..., None] == jnp.arange(group_count, dtype=jnp.int32)
     row_scale = jnp.sum(jnp.where(matches, group_weights, 0.0), axis=-1)
     weighted = (out_cotangent.astype(jnp.float32) * row_scale[..., None]).astype(jnp.bfloat16)
     start = to_chip(own_first(jnp.where(first, inputs, weighted))).reshape(half, width)
-    flip("attn")
-    ring("attn")
-    caught("attn")
-    flipped("attn", 0)
-    ring("attn")
-    flip("attn")
-    flip("mlp")
-    caught("attn")
-    flipped("attn", 1)
-    ring("attn")
-    flip("attn")
-    caught("attn")
-    ring("mlp")
-    flip("attn")
-    flipped("mlp", 0)
-    start = order.step(start)
     gain = own_first(gains[0])
 
     turns = jnp.arange(half, dtype=jnp.int32)
@@ -880,106 +895,76 @@
         jnp.concatenate([cos_part] * 4, axis=1),
         jnp.concatenate([-sin_part, sin_part] * 2, axis=1),
     )
-    units = tensor * pieces["mlp"][0].shape[1] // 2
     row32, row16 = ((half, width), jnp.float32), ((half, width), jnp.bfloat16)
     unit16 = ((length, units), jnp.bfloat16)
     sum32 = ((1, width), jnp.float32)
     mlp_cost = {"limit": KERNEL_VMEM, "flops": 2 * length * width * units}
-    ups, downs = slice(0, units // tensor), slice(units // tensor, None)
-    weights = {name: (pieces[name], flown[name]) for name in pieces}
-
-    def mlp_pieces():
-        return (*weights["mlp"][0], *weights["mlp"][1])
-
-    def forward(layer_input, between=None):
-        pause = between or (lambda: None)
-        attn_in = both_rows(on_chip(norm_in_kernel, "norm_in", (row16,), gain, layer_input)[0])
-        pause()
-        *heads, mixed = attend(core_word, tables, order.step(*attn_in), weights["attn"])
-        mixed = order.step(mixed)
-        pause()
-        parts = model_rows("attn_out", [mixed], weights["attn"], OUT)
+
+    def forward(layer_input, waits):
+        attn_in = both_rows(
+            on_chip(norm_in_kernel, "norm_in", (row16,), gain, layer_input, waits=waits[0])[0]
+        )
+        *heads, mixed = attend(core_word, tables, attn_in, w_attn, waits[1])
+        parts = model_rows("attn_out", [mixed], w_attn, OUT, waits[2])
+        operands = (gain, layer_input, *parts)
         branch, hidden, mlp_in = on_chip(
-            after_attention_kernel, "after_attn", (row32, row32, row16), gain, layer_input, *parts
+            after_attention_kernel, "after_attn", (row32, row32, row16), *operands, waits=waits[3]
         )
-        mlp_in = both_rows(order.step(mlp_in))
-        pause()
+        mlp_in = both_rows(mlp_in)
         kernel = functools.partial(mlp_up_kernel, tensor)
-        outs = (unit16, unit16)
-        gelu_out, slope = on_chip(kernel, "mlp_up", outs, *mlp_in, *mlp_pieces(), **mlp_cost)
-        gelu_out = order.step(gelu_out)
-        pause()
-        parts = model_rows("mlp_down", [gelu_out], weights["mlp"], downs)
+        operands = (*mlp_in, *w_up[0], *w_up[1])
+        gelu_out, slope = on_chip(kernel, "mlp_up", (unit16, unit16), *operands, **mlp_cost)
+        parts = model_rows("mlp_down", [gelu_out], w_down, downs)
         mlp_branch, result = on_chip(
             after_mlp_kernel, "after_mlp", (row32, row16), gain, hidden, *parts
         )
         saved = (layer_input, heads, branch, hidden, slope, mlp_branch)
         return result, saved, (attn_in, mixed, mlp_in, gelu_out)
 
-    def backward(grad, saved, between=None):
-        pause = between or (lambda **new: None)
+    def backward(grad, saved, hook, waits=()):
         layer_input, heads, branch, hidden, slope, mlp_branch = saved
+        operands = (gain, grad, mlp_branch)
         d_down, sum_three = on_chip(
-            into_mlp_back_kernel, "into_mlp_back", (row16, sum32), gain, grad, mlp_branch
+            into_mlp_back_kernel, "into_mlp_back", (row16, sum32), *operands, waits=waits
         )
         d_down = both_rows(d_down)
         kernel = functools.partial(mlp_up_back_kernel, tensor)
-        operands = (*d_down, slope, *mlp_pieces())
+        operands = (*d_down, slope, *w_down[0], *w_down[1])
         (d_up,) = on_chip(kernel, "mlp_up_back", (unit16,), *operands, **mlp_cost)
-        pause(d_down=d_down)
-        d_up = order.step(d_up)
-        parts = model_rows("mlp_back", [d_up], weights["mlp"], ups)
-        pause(d_up=d_up)
+        waits = hook(d_down, d_up)
+        parts = model_rows("mlp_back", [d_up], w_up, ups)
+        operands = (gain, grad, *parts, hidden, branch)
+        outs = (row32, row16, sum32, sum32)
         d_hidden, d_attn, sum_one, sum_two = on_chip(
-            into_attention_back_kernel,
-            "into_attn_back",
-            (row32, row16, sum32, sum32),
-            gain,
-            grad,
-            *parts,
-            hidden,
-            branch,
+            into_attention_back_kernel, "into_attn_back", outs, *operands, waits=waits
         )
-        d_attn = both_rows(order.step(d_attn))
-        pause(d_attn=d_attn)
+        d_attn = both_rows(d_attn)
+        waits = hook(d_attn)
         d_qkv = []
         for base in reversed(range(0, tensor, 2)):
-            some = [side[base : base + 2] for side in weights["attn"]]
-            rows_now = order.step(*d_attn)
-            now = attend_back(core_word, tables, rows_now, some, base, *heads)
-            d_qkv.insert(0, order.step(now))
-            pause(d_qkv=d_qkv[0])
-        parts = model_rows("attn_back", d_qkv, weights["attn"], QKV)
+            some = [side[base : base + 2] for side in w_attn]
+            now = attend_back(core_word, tables, d_attn, some, base, waits, *heads)
+            d_qkv.insert(0, now)
+            waits = hook(now)
+        parts = model_rows("attn_back", d_qkv, w_attn, QKV, waits)
+        operands = (gain, layer_input, *parts, d_hidden)
         d_input, sum_zero = on_chip(
-            out_of_layer_kernel, "out_of_layer", (row16, sum32), gain, layer_input, *parts, d_hidden
+            out_of_layer_kernel, "out_of_layer", (row16, sum32), *operands
         )
         sums = jnp.concatenate([sum_zero, sum_one, sum_two, sum_three])
-        return order.step(d_input), (d_qkv, d_attn, d_up, d_down), sums
-
-    def arrivals():
-        flipped("attn", 2)
-        caught("mlp")
-        ring("mlp")
-        flip("mlp")
-        flipped("attn", 3)
-        yield
-        caught("mlp")
-        ring("mlp")
-        flip("mlp")
-        yield
-        flipped("mlp", 1)
-        caught("mlp")
-        flip("mlp")
-        flipped("mlp", 2)
-        flipped("mlp", 3)
-        yield
-        yield
-
-    steps = arrivals()
-    low_zero, saved_zero, lefts_zero = forward(start, lambda: next(steps))
-    low_zero = order.step(low_zero)
-    low_one, saved_one, lefts_one = forward(shifted(low_zero, "section", 1))
-    grad_one, rights_one, gain_one = backward(start, saved_one)
+        return d_input, (d_qkv, d_attn, d_up, d_down), sums
+
+    low_zero, saved_zero, lefts_zero = forward(
+        start,
+        (
+            (attn_own[3], mlp_other[0], attn_other[1]),
+            (mlp_own[1],),
+            (mlp_own[2], mlp_other[1]),
+            (mlp_own[3], mlp_other[2]),
+        ),
+    )
+    low_one, saved_one, lefts_one = forward(shifted(low_zero, "section", 1), ((),) * 4)
+    grad_one, rights_one, gain_one = backward(start, saved_one, lambda *new: ())
     received = shifted(grad_one, "section", -1)
 
     def joined(pair):
@@ -988,100 +973,108 @@
     def own_layer(zero, one):
         if isinstance(zero, tuple):
             zero, one = joined(zero), joined(one)
-        return jnp.where(first, zero, one)
-
-    lows = order.step(low_zero, low_one)
+        return lax.optimization_barrier(jnp.where(first, zero, one))
+
+    lefts_zero, lefts_one = lax.optimization_barrier((lefts_zero, lefts_one, grad_one))[:2]
+    attn_in, mixed, mlp_in, gelu_out = lefts = list(map(own_layer, lefts_zero, lefts_one))
+    lows = lax.optimization_barrier((low_zero, low_one, grad_one))[:2]
     outputs = from_chip(own_first(jnp.where(first, *lows)).reshape(tensor, part, width))
-    lefts_zero, lefts_one = order.step(lefts_zero, lefts_one)
-    attn_in, mixed, mlp_in, gelu_out = map(own_layer, lefts_zero, lefts_one)
-    attn_in, mixed, mlp_in, gelu_out = order.step(attn_in, mixed, mlp_in, gelu_out)
-    received = order.step(received)
-
-    sums = {name: [None] * tensor for name in pieces}
-    moving = {}
-
-    def leave(name, j, *pairs):
-        totals = [contract(*pair) for pair in order.step(*pairs)]
-        own = jnp.concatenate([total[:wide_half] for total in totals], axis=1)
-        other = jnp.concatenate(
-            [total[wide_half:].astype(jnp.bfloat16) for total in totals], axis=1
-        )
-        own, other = order.step(own, other)
-        sums[name][j] = (own, flip_pairs(other, 2))
-
-    def gathered(name, j):
-        own, other = sums[name][j]
-        total = own + order.step(other).astype(jnp.float32)
-        if name in moving:
-            total = total + order.step(moving.pop(name)).astype(jnp.float32)
-        if j == 0:
-            sums[name] = total
-        else:
-            moving[name] = passed_on(order.step(total.astype(jnp.bfloat16)), -1)
 
     def block(array, j, count=tensor):
         size = array.shape[1] // count
         return array[:, j * size : (j + 1) * size]
 
+    def leave(*pairs):
+        totals = [contract(*pair) for pair in pairs]
+        size = sum(total.shape[1] for total in totals)
+        outs = (((wide_half, size), jnp.float32), ((wide_half, size), jnp.bfloat16))
+        own, other = on_chip(pack_kernel, "pack", outs, *totals)
+        return own, flip_pairs(other, 2)
+
+    def mlp_leaves(j):
+        return leave((mlp_in, block(d_up, j)), (d_down, block(gelu_out, j)))
+
+    def attn_leaves(j, d_qkv):
+        return leave((attn_in, block(d_qkv, j % 2, 2)), (d_attn, block(mixed, j)))
+
+    def moves_on(piece, moved=None):
+        own, other = piece
+        total = own + other.astype(jnp.float32)
+        if moved is not None:
+            total = total + moved.astype(jnp.float32)
+        return passed_on(total.astype(jnp.bfloat16), -1)
+
     d_qkv_one, d_attn_one, d_up_one, d_down_one = rights_one
-
-    def departures():
-        new = yield
-        d_down = own_layer(new["d_down"], d_down_one)
-        new = yield
-        d_up = own_layer(new["d_up"], d_up_one)
-
-        def mlp_piece(j):
-            leave("mlp", j, (mlp_in, block(d_up, j)), (d_down, block(gelu_out, j)))
-
-        mlp_piece(3)
-        mlp_piece(2)
-        new = yield
-        d_attn = own_layer(new["d_attn"], d_attn_one)
-        gathered("mlp", 3)
-        mlp_piece(1)
-        new = yield
-        high = own_layer(new["d_qkv"], d_qkv_one[1])
-        gathered("mlp", 2)
-        mlp_piece(0)
-        new = yield
-        low = own_layer(new["d_qkv"], d_qkv_one[0])
-        gathered("mlp", 1)
-        for j in reversed(range(tensor)):
-            d_qkv = block((low, high)[j // 2], j % 2, 2)
-            leave("attn", j, (attn_in, d_qkv), (d_attn, block(mixed, j)))
-        yield
-
-    leaving = departures()
-    next(leaving)
-    grad_zero, rights_zero, gain_zero = backward(
-        received, saved_zero, lambda **new: leaving.send(new)
-    )
-    gathered("mlp", 0)
-    gathered("attn", 3)
-    gathered("attn", 2)
-    gathered("attn", 1)
-    gathered("attn", 0)
+    mlp_sums, attn_sums = [None] * tensor, [None] * tensor
+    mlp_moves, attn_moves = [None] * tensor, [None] * tensor
+    hooks = iter(range(4))
+
+    def hook(*new):
+        nonlocal d_down, d_up, d_attn
+        turn = next(hooks)
+        if turn == 0:
+            d_down, d_up = own_layer(new[0], d_down_one), own_layer(new[1], d_up_one)
+            mlp_sums[3] = mlp_leaves(3)
+            mlp_sums[2] = mlp_leaves(2)
+            return (mlp_sums[3][1],)
+        if turn == 1:
+            d_attn = own_layer(new[0], d_attn_one)
+            mlp_moves[3] = moves_on(mlp_sums[3])
+            mlp_sums[1] = mlp_leaves(1)
+            return (mlp_sums[2][1], mlp_moves[3])
+        if turn == 2:
+            mlp_moves[2] = moves_on(mlp_sums[2], mlp_moves[3])
+            mlp_sums[0] = mlp_leaves(0)
+            d_qkv = own_layer(new[0], d_qkv_one[1])
+            attn_sums[3] = attn_leaves(3, d_qkv)
+            attn_sums[2] = attn_leaves(2, d_qkv)
+            return (mlp_sums[1][1], mlp_moves[2])
+        mlp_moves[1] = moves_on(mlp_sums[1], mlp_moves[2])
+        d_qkv = own_layer(new[0], d_qkv_one[0])
+        attn_sums[1] = attn_leaves(1, d_qkv)
+        attn_sums[0] = attn_leaves(0, d_qkv)
+        return (mlp_sums[0][1], mlp_moves[1])
+
+    d_down = d_up = d_attn = None
+    grad_zero, rights_zero, gain_zero = backward(received, saved_zero, hook, tuple(lefts))
+    attn_moves[3] = moves_on(attn_sums[3])
+    attn_moves[2] = moves_on(attn_sums[2], attn_moves[3])
+    attn_moves[1] = moves_on(attn_sums[1], attn_moves[2])
     grads = from_chip(own_first(jnp.where(first, grad_zero, grad_one)).reshape(tensor, part, width))
 
-    def both_cores(kept):
-        kept = kept.reshape(2, wide_half // 2, kept.shape[1])
-        mine = lax.dynamic_index_in_dim(kept, core, 0, keepdims=False)
-        other = lax.dynamic_index_in_dim(kept, 1 - core, 0, keepdims=False)
-        return ordered(mine, flip_pairs(other, 1))
-
-    pair = both_cores(sums["mlp"])
-    up_grad = jnp.concatenate([side[:, ups] for side in pair], axis=1)
-    down_grad = jnp.concatenate([side[:, downs].T for side in pair], axis=0)
-    pair = both_cores(sums["attn"])
-    qkv_grad = [side[:, QKV].reshape(wide_half // 2, 3, -1) for side in pair]
-    qkv_grad = jnp.concatenate(qkv_grad, axis=2)
-    out_grad = jnp.concatenate([side[:, OUT].T for side in pair], axis=0)
-
-    gain_total = summed_everywhere(own_first(jnp.where(first, gain_zero, gain_one)))
-    size = width // (tensor * lax.axis_size("dp"))
-    spot = (place * tensor + lax.axis_index("tensor")) * size
-    gains_grad = lax.dynamic_slice_in_dim(gain_total, spot, size, axis=1)
+    def finished(name, piece, moved, spots, columns_out, rows_out):
+        size = piece[0].shape[1]
+        outs = (((wide_half // 2, size), jnp.float32),) * 2
+        space = pl.BlockSpec(memory_space=pltpu.VMEM)
+
+        def call(kernel, label, outs, *operands):
+            return pl.pallas_call(
+                kernel,
+                in_specs=[pl.BlockSpec(memory_space=pltpu.SMEM)] + [space] * len(operands),
+                out_specs=[space] * len(outs),
+                out_shape=[jax.ShapeDtypeStruct(shape, dtype) for shape, dtype in outs],
+                compiler_params=pltpu.CompilerParams(vmem_limit_bytes=ROWS_VMEM),
+                name=label,
+            )(core_word, *operands)
+
+        keep, send = call(last_sum_kernel, name + "_sum", outs, *piece, moved)
+        outs = (
+            ((wide_half // 2, columns_out), jnp.float32),
+            ((rows_out, wide_half // 2), jnp.float32),
+        )
+        kernel = functools.partial(joined_kernel, spots)
+        return call(kernel, name + "_join", outs, keep, flip_pairs(send, 1))
+
+    unit = units // tensor
+    up_grad, down_grad = finished(
+        "mlp", mlp_sums[0], mlp_moves[1], ((0, unit, 0),), 2 * unit, 2 * unit
+    )
+    spots = tuple((i * 128, (i + 1) * 128, i * 256) for i in range(3))
+    qkv_grad, out_grad = finished("attn", attn_sums[0], attn_moves[1], spots, 768, 256)
+    qkv_grad = qkv_grad.reshape(wide_half // 2, 3, -1)
+
+    gain_total = own_first(jnp.where(first, gain_zero, gain_one))
+    gains_grad = lax.psum_scatter(gain_total, ("dp", "tensor"), scatter_dimension=1, tiled=True)
     return (
         outputs[None],
         grads[None],

time: 725 us -> 763 us (1.052)
  waiting for transfers between devices: 276 us -> 334 us
  local copies, waits for them, and re-layouts: 85.4 us -> 63.9 us
  Pallas kernels: 194 us -> 214 us
  other arithmetic: 57.2 us -> 38.1 us
  between operations: 3.26 us -> 15.9 us
  starting transfers between devices: 80.9 us -> 72.9 us
    unnamed x0 -> x2, waiting for transfers between devices: none -> 49.1 us
    ppermute x12, waiting for transfers between devices: 64.9 us -> 112 us  [passed_on(): lax.ppermute(block, 'tensor', [(i, (i + step) % size) for i in range(size)])]
    ppermute x2 -> x0, waiting for transfers between devices: 37.6 us -> none  [summed_everywhere(): lax.ppermute(value, 'tensor', [(i, i ^ distance) for i in range(size)])]
    ppermute x39 -> x38, waiting for transfers between devices: 146 us -> 123 us  [flip_pairs(): return lax.ppermute(block, 'dp', [(i, i ^ distance) for i in range(size)])]
    all_to_all x1, waiting for transfers between devices: 0.01 us -> 21.3 us  [to_chip(): lax.all_to_all(jnp.concatenate(ordered(mine, flip_pairs(other, 1))), 'ten...]
    pallas_call x30 -> x42, Pallas kernels: 194 us -> 214 us  [the longest x32 125 us: on_chip(): pl.pallas_call(without(kernel, len(operands), len(waits)), in_specs=[spac...]
    dynamic_slice x4 -> x0, local copies, waits for them, and re-layouts: 11 us -> none  [the longest x3 8.64 us: both_cores(): mine = lax.dynamic_index_in_dim(kept, core, 0, keepdims=False)]
    ppermute x2, starting transfers between devices: 15.3 us -> 4.56 us  [shifted(): return lax.ppermute(block, axis, route)]
  transfers between devices with their start and end apart: 58 -> 56, of which waited for: 31 -> 30; matrix products, arithmetic and copies ran while one was open for 13% -> 9% of each run, Pallas kernels for 9% -> 13%
where the time goes in v5:
time: 763 us; the launch traced here: 758 us
  waiting for transfers between devices  334 us (44%)
  Pallas kernels  214 us (28%)
  starting transfers between devices  72.9 us (10%)
  local copies, waits for them, and re-layouts  63.9 us (8%)
  other arithmetic  38.1 us (5%)
  matrix products  19 us (2%)
  between operations  15.9 us (2%)
    pallas_call x32, Pallas kernels, on_chip(): pl.pallas_call(without(kernel, len(operands), len(waits)), in_specs=[spac...  125 us
    ppermute x38, waiting for transfers between devices, flip_pairs(): return lax.ppermute(block, 'dp', [(i, i ^ distance) for i in range(size)])  123 us
    ppermute x12, waiting for transfers between devices, passed_on(): lax.ppermute(block, 'tensor', [(i, (i + step) % size) for i in range(size)])  112 us
    pallas_call x6, Pallas kernels, by_pairs(): pl.pallas_call(without(functools.partial(kernel, len(pieces[0])), taken,...  83.9 us
    unnamed x2, waiting for transfers between devices  49.1 us
    unnamed x250, local copies, waits for them, and re-layouts  48.6 us
    ppermute x12, starting transfers between devices, passed_on(): lax.ppermute(block, 'tensor', [(i, (i + step) % size) for i in range(size)])  31.8 us
    ppermute x2, waiting for transfers between devices, shifted(): return lax.ppermute(block, axis, route)  28.9 us
  transfers between devices with their start and end apart: 56, of which 30 were waited for; matrix products, arithmetic and copies ran while one was open for 9% of the time, Pallas kernels for 13%

profile of v5, /device:TPU:0, one launch (start us, length us, event | category | flops | bytes accessed | tf_op | source)
XLA Modules:
  0.0 758.0 jit_solution(13673930477491730037)
XLA Ops:
  21.5 2.7 collective-permute-start.1
  26.4 3.9 all-to-all-start
  41.1 48.6 %collective-permute-done.2.refs_7_.refs_3_.refs_5_.refs_4_ = bf16[512,512]{1,0:T(8,128)(2,1)} collective-permute-done((bf16[512,512]{1,0:T(8,128)(2,1)}, bf16[512,512]{1,0:T(8,128)(2,1)}, u32[]{:S(2)}, u32[]{:S(2)}) %collective-permute-start.2) | collective-permute-done | bytes 524320 | tf_op jit(solution)/shard_map/ppermute | solution.py:763
  89.8 4.3 collective-permute-start.3
  94.1 2.5 collective-permute-start.11
  97.5 9.3 %collective-permute-done.3.refs_2_.refs_8_.refs_4_.refs_6_.refs_5_ = bf16[512,512]{1,0:T(8,128)(2,1)S(1)} collective-permute-done((bf16[512,512]{1,0:T(8,128)(2,1)}, bf16[512,512]{1,0:T(8,128)(2,1)S(1)}, u32[]{:S(2)}, u32[]{:S(2)}) %collective-permute-start.3) | collective-permute-done | bytes 524320 | tf_op jit(solution)/shard_map/ppermute | solution.py:763
  107.6 21.3 %all-to-all-done = bf16[4,128,1024]{2,1,0:T(8,128)(2,1)S(1)} async-done(((bf16[4,128,1024]{2,1,0:T(8,128)(2,1)}), bf16[4,128,1024]{2,1,0:T(8,128)(2,1)S(1)}, u32[]{:S(2)}, u32[]{:S(2)}) %all-to-all-start) | async-done | bytes 1048608 | tf_op jit(solution)/shard_map/all_to_all | solution.py:835
  130.9 2.7 norm_in.2.refs_3_
  140.2 8.4 %collective-permute-done.7.refs_9_.refs_5_.refs_7_.refs_6_ = bf16[512,512]{1,0:T(8,128)(2,1)S(1)} collective-permute-done((bf16[512,512]{1,0:T(8,128)(2,1)}, bf16[512,512]{1,0:T(8,128)(2,1)S(1)}, u32[]{:S(2)}, u32[]{:S(2)}) %collective-permute-start.7) | collective-permute-done | bytes 524320 | tf_op jit(solution)/shard_map/ppermute | solution.py:758
  151.4 8.4 %collective-permute-done.8.refs_11_.refs_7_.refs_8_ = bf16[512,512]{1,0:T(8,128)(2,1)S(1)} collective-permute-done((bf16[512,512]{1,0:T(8,128)(2,1)}, bf16[512,512]{1,0:T(8,128)(2,1)S(1)}, u32[]{:S(2)}, u32[]{:S(2)}) %collective-permute-start.8) | collective-permute-done | bytes 524320 | tf_op jit(solution)/shard_map/ppermute | solution.py:758
  159.8 11.2 %collective-permute-done.9.refs_12_.refs_8_.refs_9_ = bf16[512,512]{1,0:T(8,128)(2,1)S(1)} collective-permute-done((bf16[512,512]{1,0:T(8,128)(2,1)}, bf16[512,512]{1,0:T(8,128)(2,1)S(1)}, u32[]{:S(2)}, u32[]{:S(2)}) %collective-permute-start.9) | collective-permute-done | bytes 524320 | tf_op jit(solution)/shard_map/ppermute | solution.py:758
  172.3 16.8 %attend.2 = (bf16[4,1024,128]{2,1,0:T(8,128)(2,1)S(1)}, bf16[4,1024,128]{2,1,0:T(8,128)(2,1)S(1)}, bf16[4,1024,128]{2,1,0:T(8,128)(2,1)S(1)}, f32[4,2,1024]{2,1,0:T(2,128)S(1)}, bf16[1024,512]{1,0:T(8,128)(2,1)S(1)}) custom-call(s32[1]{0:T(128)} %bitcast.5.refs_0_.core_ref, f32[1024,128]{1,0:T(8,128)S(1)} %pad_maximum_fusion.12.refs_1_, ...), custom_call_target="tpu_custom_call" | custom-call | flops 11811160064 | bytes 11567104 | tf_op jit(solution)/shard_map/attend/pallas_call | solution.py:687
  193.5 3.0 attn_out.2
  196.6 19.0 %collective-permute-done.15.refs_5_.refs_8_.refs_7_.refs_9_ = bf16[512,1024]{1,0:T(8,128)(2,1)S(1)} collective-permute-done((bf16[512,1024]{1,0:T(8,128)(2,1)S(1)}, bf16[512,1024]{1,0:T(8,128)(2,1)S(1)}, u32[]{:S(2)}, u32[]{:S(2)}) %collective-permute-start.15) | collective-permute-done | bytes 1048608 | tf_op jit(solution)/shard_map/ppermute | solution.py:758
  215.6 3.7 after_attn.2
  222.9 12.7 %collective-permute-done.17.refs_9_.refs_8_ = bf16[512,512]{1,0:T(8,128)(2,1)S(1)} collective-permute-done((bf16[512,512]{1,0:T(8,128)(2,1)S(1)}, bf16[512,512]{1,0:T(8,128)(2,1)S(1)}, u32[]{:S(2)}, u32[]{:S(2)}) %collective-permute-start.17) | collective-permute-done | bytes 524320 | tf_op jit(solution)/shard_map/ppermute | solution.py:758
  235.6 9.7 %mlp_up.2 = (bf16[1024,2048]{1,0:T(8,128)(2,1)S(1)}, bf16[1024,2048]{1,0:T(8,128)(2,1)S(1)}) custom-call(bf16[512,1024]{1,0:T(8,128)(2,1)S(1)} %get-tuple-element.143.refs_0_, bf16[512,1024]{1,0:T(8,128)(2,1)S(1)} %collective-permute-done.16.refs_1_, bf16[512,1024]{1,0:T(8,128)(2,1)S(1)} %copy-done.10, ...), custom_call_target="tpu_custom_call" | custom-call | flops 4294967296 | bytes 18350080 | tf_op jit(solution)/shard_map/mlp_up/pallas_call | solution.py:669
  247.3 6.5 mlp_down.2
  253.9 2.6 collective-permute-done.19.refs_3_
  258.5 3.3 collective-permute-start.20
  261.7 22.6 %collective-permute-done.20.refs_1_ = bf16[512,1024]{1,0:T(8,128)(2,1)S(1)} collective-permute-done((bf16[512,1024]{1,0:T(8,128)(2,1)S(1)}, bf16[512,1024]{1,0:T(8,128)(2,1)S(1)}, u32[]{:S(2)}, u32[]{:S(2)}) %collective-permute-start.20) | collective-permute-done | bytes 1048608 | tf_op jit(solution)/shard_map/ppermute | solution.py:27
  284.4 12.1 %norm_in.3.refs_3_ = bf16[512,1024]{1,0:T(8,128)(2,1)S(1)} custom-call(f32[4,1024]{1,0:T(4,128)S(1)} %maximum_select_fusion.3.refs_0_, bf16[512,1024]{1,0:T(8,128)(2,1)S(1)} %collective-permute-done.20.refs_1_), custom_call_target="tpu_custom_call" | custom-call | bytes 2113536 | tf_op jit(solution)/shard_map/norm_in/pallas_call | solution.py:669
  296.6 2.6 collective-permute-done.21.refs_4_
  299.3 16.6 %attend.3 = (bf16[4,1024,128]{2,1,0:T(8,128)(2,1)S(1)}, bf16[4,1024,128]{2,1,0:T(8,128)(2,1)S(1)}, bf16[4,1024,128]{2,1,0:T(8,128)(2,1)S(1)}, f32[4,2,1024]{2,1,0:T(2,128)S(1)}, bf16[1024,512]{1,0:T(8,128)(2,1)S(1)}) custom-call(s32[1]{0:T(128)} %bitcast.5.refs_0_.core_ref, f32[1024,128]{1,0:T(8,128)S(1)} %pad_maximum_fusion.12.refs_1_, ...), custom_call_target="tpu_custom_call" | custom-call | flops 11811160064 | bytes 11567104 | tf_op jit(solution)/shard_map/attend/pallas_call | solution.py:687
  317.8 3.0 attn_out.3
  321.0 2.5 collective-permute-done.22.refs_3_
  323.6 3.4 after_attn.3
  327.2 2.5 collective-permute-done.23.refs_1_
  329.7 9.5 %mlp_up.3 = (bf16[1024,2048]{1,0:T(8,128)(2,1)S(1)}, bf16[1024,2048]{1,0:T(8,128)(2,1)S(1)}) custom-call(bf16[512,1024]{1,0:T(8,128)(2,1)S(1)} %get-tuple-element.145.refs_0_, bf16[512,1024]{1,0:T(8,128)(2,1)S(1)} %collective-permute-done.23.refs_1_, bf16[512,1024]{1,0:T(8,128)(2,1)S(1)} %copy-done.10, ...), custom_call_target="tpu_custom_call" | custom-call | flops 4294967296 | bytes 18350080 | tf_op jit(solution)/shard_map/mlp_up/pallas_call | solution.py:669
  339.2 6.5 mlp_down.3
  346.0 2.5 collective-permute-done.24.refs_3_
  353.1 2.5 collective-permute-done.25.refs_1_
  355.6 6.1 mlp_up_back.2.refs_0_
  361.8 6.5 mlp_back.2
  371.1 3.9 into_attn_back.2
  377.8 12.6 %attend_back.5.refs_1_ = bf16[1024,768]{1,0:T(8,128)(2,1)S(1)} custom-call(s32[1]{0:T(128)} %bitcast.5.refs_0_.core_ref, f32[1024,128]{1,0:T(8,128)S(1)} %pad_maximum_fusion.12.refs_1_, f32[1024,128]{1,0:T(8,128)S(1)} %pad_maximum_fusion.13.refs_2_, bf16[512,1024]{1,0:T(8,128)(2,1)S(1)} %get-tuple-element.125.refs_3_, ...), custom_call_target="tpu_custom_call" | custom-call | flops 11274289152 | bytes 6815744 | tf_op jit(solution)/shard_map/attend_back/pallas_call | solution.py:687
  390.4 12.9 %attend_back.4.refs_0_ = bf16[1024,768]{1,0:T(8,128)(2,1)S(1)} custom-call(s32[1]{0:T(128)} %bitcast.5.refs_0_.core_ref, f32[1024,128]{1,0:T(8,128)S(1)} %pad_maximum_fusion.12.refs_1_, f32[1024,128]{1,0:T(8,128)S(1)} %pad_maximum_fusion.13.refs_2_, bf16[512,1024]{1,0:T(8,128)(2,1)S(1)} %get-tuple-element.125.refs_3_, ...), custom_call_target="tpu_custom_call" | custom-call | flops 11274289152 | bytes 6815744 | tf_op jit(solution)/shard_map/attend_back/pallas_call | solution.py:687
  404.2 5.4 attn_back.2
  412.3 3.1 out_of_layer.2
  416.7 3.0 pad_maximum_fusion
  422.4 4.3 all-to-all-start.1
  436.7 6.3 collective-permute-done.30.refs_1_
  444.6 4.8 into_mlp_back.3
  463.1 6.5 mlp_up_back.3.refs_0_
  474.7 6.6 mlp_back.3
  491.5 19.2 %collective-permute-done.33.refs_6_ = bf16[512,1024]{1,0:T(8,128)(2,1)S(1)} collective-permute-done((bf16[512,1024]{1,0:T(8,128)(2,1)S(1)}, bf16[512,1024]{1,0:T(8,128)(2,1)S(1)}, u32[]{:S(2)}, u32[]{:S(2)}) %collective-permute-start.33) | collective-permute-done | bytes 1048608 | tf_op jit(solution)/shard_map/ppermute | solution.py:758
  510.7 5.2 into_attn_back.3
  525.2 8.0 %collective-permute-done.36.refs_13_ = bf16[512,1024]{1,0:T(8,128)(2,1)S(1)} collective-permute-done((bf16[512,1024]{1,0:T(8,128)(2,1)S(1)}, bf16[512,1024]{1,0:T(8,128)(2,1)S(1)}, u32[]{:S(2)}, u32[]{:S(2)}) %collective-permute-start.36) | collective-permute-done | bytes 1048608 | tf_op jit(solution)/shard_map/ppermute | solution.py:758
  534.7 7.4 collective-permute-done.37.refs_14_
  542.2 12.5 %attend_back.7.refs_1_ = bf16[1024,768]{1,0:T(8,128)(2,1)S(1)} custom-call(s32[1]{0:T(128)} %bitcast.5.refs_0_.core_ref, f32[1024,128]{1,0:T(8,128)S(1)} %copy-done.92, f32[1024,128]{1,0:T(8,128)S(1)} %copy-done.90, bf16[512,1024]{1,0:T(8,128)(2,1)S(1)} %get-tuple-element.155.refs_3_, bf16[512,1024]{1,0:T(8,128)(2,1)S(1)} %collective-permute-done.34.refs_4_, ...), custom_call_target="tpu_custom_call" | custom-call | flops 11274289152 | bytes 6815744 | tf_op jit(solution)/shard_map/attend_back/pallas_call | solution.py:687
  555.4 3.4 collective-permute-start.38
  567.7 10.4 %collective-permute-done.35.refs_13_ = bf16[512,1024]{1,0:T(8,128)(2,1)S(1)} collective-permute-done((bf16[512,1024]{1,0:T(8,128)(2,1)S(1)}, bf16[512,1024]{1,0:T(8,128)(2,1)S(1)}, u32[]{:S(2)}, u32[]{:S(2)}) %collective-permute-start.35) | collective-permute-done | bytes 1048608 | tf_op jit(solution)/shard_map/ppermute | solution.py:758
  578.1 2.9 collective-permute-done.38.refs_14_
  581.6 4.3 collective-permute-start.40
  586.0 12.5 %attend_back.6.refs_0_ = bf16[1024,768]{1,0:T(8,128)(2,1)S(1)} custom-call(s32[1]{0:T(128)} %bitcast.5.refs_0_.core_ref, f32[1024,128]{1,0:T(8,128)S(1)} %copy-done.92, f32[1024,128]{1,0:T(8,128)S(1)} %copy-done.90, bf16[512,1024]{1,0:T(8,128)(2,1)S(1)} %get-tuple-element.155.refs_3_, bf16[512,1024]{1,0:T(8,128)(2,1)S(1)} %collective-permute-done.34.refs_4_, ...), custom_call_target="tpu_custom_call" | custom-call | flops 11274289152 | bytes 6815744 | tf_op jit(solution)/shard_map/attend_back/pallas_call | solution.py:687
  598.5 8.9 %collective-permute-done.40.refs_11_.moved_ref = bf16[512,1024]{1,0:T(8,128)(2,1)S(1)} collective-permute-done((bf16[512,1024]{1,0:T(8,128)(2,1)S(1)}, bf16[512,1024]{1,0:T(8,128)(2,1)S(1)}, u32[]{:S(2)}, u32[]{:S(2)}) %collective-permute-start.40) | collective-permute-done | bytes 1048608 | tf_op jit(solution)/shard_map/ppermute | solution.py:763
  607.4 5.2 attn_back.3
  616.9 4.3 collective-permute-start.47
  628.9 4.2 all-to-all-start.2
  634.9 4.4 collective-permute-start.48
  642.7 21.0 %collective-permute-done.48 = bf16[512,512]{1,0:T(8,128)(2,1)S(1)} collective-permute-done((bf16[512,512]{1,0:T(8,128)(2,1)S(1)}, bf16[512,512]{1,0:T(8,128)(2,1)S(1)}, u32[]{:S(2)}, u32[]{:S(2)}) %collective-permute-start.48) | collective-permute-done | bytes 524320 | tf_op jit(solution)/shard_map/ppermute | solution.py:763
  670.6 12.7 %collective-permute-done.49.moved_ref = bf16[512,512]{1,0:T(8,128)(2,1)S(1)} collective-permute-done((bf16[512,512]{1,0:T(8,128)(2,1)S(1)}, bf16[512,512]{1,0:T(8,128)(2,1)S(1)}, u32[]{:S(2)}, u32[]{:S(2)}) %collective-permute-start.49) | collective-permute-done | bytes 524320 | tf_op jit(solution)/shard_map/ppermute | solution.py:763
  694.3 2.9 mlp_join.1
  697.2 49.1 %reduce-scatter.4.cloned.1.call-done = f32[64,4]{1,0:T(8,128)} async-done(((f32[1024,4]{1,0:T(8,128)}), f32[64,4]{1,0:T(8,128)}) %reduce-scatter.4.cloned.1.call-update) | async-done | bytes 1040
  (423 shorter events, 174.7 us)
Async XLA Ops:
  14.5 9.7 %collective-permute-start = (bf16[2,128,1024]{2,1,0:T(8,128)(2,1)}, bf16[2,128,1024]{2,1,0:T(8,128)(2,1)}, u32[]{:S(2)}, u32[]{:S(2)}) collective-permute-start(bf16[2,128,1024]{2,1,0:T(8,128)(2,1)} %dynamic-slice_bitcast_fusion.3), channel_id=1, source_target_pairs={{0,4},{4,0},{8,12},{12,8},{1,5},{5,1},{9,13},{13,9},{2,6},{6,2},{1... | collective-permute-start | bytes 1572872 | tf_op jit(solution)/shard_map/ppermute | solution.py:758
  21.5 17.9 %collective-permute-start.1 = (bf16[512,512]{1,0:T(8,128)(2,1)}, bf16[512,512]{1,0:T(8,128)(2,1)}, u32[]{:S(2)}, u32[]{:S(2)}) collective-permute-start(bf16[512,512]{1,0:T(8,128)(2,1)} %pad_maximum_fusion.14.refs_5_.refs_1_.refs_2_), channel_id=1, source_target_pairs={{0,1},{1,2},{2,3},{3,0},{4,5},{5,6},{6,7},{7,4},{8,9},{9,10},{10,1... | collective-permute-start | bytes 1572872 | tf_op jit(solution)/shard_map/ppermute | solution.py:763
  26.4 102.4 %all-to-all-start = ((bf16[4,128,1024]{2,1,0:T(8,128)(2,1)}), bf16[4,128,1024]{2,1,0:T(8,128)(2,1)S(1)}, u32[]{:S(2)}, u32[]{:S(2)}) async-start(bf16[4,128,1024]{2,1,0:T(8,128)(2,1)} %pad_maximum_fusion.8), calls=%async_computation | async-start | bytes 2097152 | tf_op jit(solution)/shard_map/all_to_all | solution.py:835
  31.1 63.0 %copy-start.122 = (f32[1,4,1024]{2,1,0:T(4,128)S(1)}, f32[1,4,1024]{2,1,0:T(4,128)}, u32[]{:S(2)}) copy-start(f32[1,4,1024]{2,1,0:T(4,128)} %param.13) | copy-start | bytes 49156
  33.6 60.6 %collective-permute-start.10 = (bf16[512,1024]{1,0:T(8,128)(2,1)S(1)}, bf16[512,1024]{1,0:T(8,128)(2,1)}, u32[]{:S(2)}, u32[]{:S(2)}) collective-permute-start(bf16[512,1024]{1,0:T(8,128)(2,1)S(1)} %pad_maximum_fusion.9.refs_2_.refs_1_.refs_3_), channel_id=1, source_target_pairs={{0,1},{1,2},{2,3},{3,0},{4,5},{5,6},{6,7},{7,4},{8,9},{9,10},{10,1... | collective-permute-start | bytes 3145736 | tf_op jit(solution)/shard_map/ppermute | solution.py:763
  35.6 61.8 %collective-permute-start.4 = (bf16[512,1024]{1,0:T(8,128)(2,1)S(1)}, bf16[512,1024]{1,0:T(8,128)(2,1)S(1)}, u32[]{:S(2)}, u32[]{:S(2)}) collective-permute-start(bf16[512,1024]{1,0:T(8,128)(2,1)S(1)} %pad_maximum_fusion.9.refs_2_.refs_1_.refs_3_), channel_id=1, source_target_pairs={{0,8},{4,12},{8,0},{12,4},{1,9},{5,13},{9,1},{13,5},{2,10},{6,14},... | collective-permute-start | bytes 3145736 | tf_op jit(solution)/shard_map/ppermute | solution.py:758
  39.5 50.3 %collective-permute-start.2 = (bf16[512,512]{1,0:T(8,128)(2,1)}, bf16[512,512]{1,0:T(8,128)(2,1)}, u32[]{:S(2)}, u32[]{:S(2)}) collective-permute-start(bf16[512,512]{1,0:T(8,128)(2,1)} %collective-permute-done.1.refs_6_.refs_2_.refs_3_), channel_id=1, source_target_pairs={{0,1},{1,2},{2,3},{3,0},{4,5},{5,6},{6,7},{7,4},{8,9},{9,10},{10,1... | collective-permute-start | bytes 1572872 | tf_op jit(solution)/shard_map/ppermute | solution.py:763
  39.6 57.1 %collective-permute-start.5 = (bf16[512,512]{1,0:T(8,128)(2,1)}, bf16[512,512]{1,0:T(8,128)(2,1)S(1)}, u32[]{:S(2)}, u32[]{:S(2)}) collective-permute-start(bf16[512,512]{1,0:T(8,128)(2,1)} %collective-permute-done.1.refs_6_.refs_2_.refs_3_), channel_id=1, source_target_pairs={{0,8},{4,12},{8,0},{12,4},{1,9},{5,13},{9,1},{13,5},{2,10},{6,14},... | collective-permute-start | bytes 1572872 | tf_op jit(solution)/shard_map/ppermute | solution.py:758
  89.8 17.0 %collective-permute-start.3 = (bf16[512,512]{1,0:T(8,128)(2,1)}, bf16[512,512]{1,0:T(8,128)(2,1)S(1)}, u32[]{:S(2)}, u32[]{:S(2)}) collective-permute-start(bf16[512,512]{1,0:T(8,128)(2,1)} %collective-permute-done.2.refs_7_.refs_3_.refs_5_.refs_4_), channel_id=1, source_target_pairs={{0,1},{1,2},{2,3},{3,0},{4,5},{5,6},{6,7},{7,4},{8,9},{9,10},{10,1... | collective-permute-start | bytes 1572872 | tf_op jit(solution)/shard_map/ppermute | solution.py:763
  94.1 56.8 %collective-permute-start.11 = (bf16[512,1024]{1,0:T(8,128)(2,1)}, bf16[512,1024]{1,0:T(8,128)(2,1)S(1)}, u32[]{:S(2)}, u32[]{:S(2)}) collective-permute-start(bf16[512,1024]{1,0:T(8,128)(2,1)} %collective-permute-done.10.refs_13_.refs_3_.refs_2_.refs_4_), channel_id=1, source_target_pairs={{0,1},{1,2},{2,3},{3,0},{4,5},{5,6},{6,7},{7,4},{8,9},{9,10},{10,1... | collective-permute-start | bytes 3145736 | tf_op jit(solution)/shard_map/ppermute | solution.py:763
  133.6 37.4 %collective-permute-start.6 = (bf16[512,1024]{1,0:T(8,128)(2,1)}, bf16[512,1024]{1,0:T(8,128)(2,1)}, u32[]{:S(2)}, u32[]{:S(2)}) collective-permute-start(bf16[512,1024]{1,0:T(8,128)(2,1)} %norm_in.2.refs_3_), channel_id=1, source_target_pairs={{0,4},{4,0},{8,12},{12,8},{1,5},{5,1},{9,13},{13,9},{2,6},{6,2},{1... | collective-permute-start | bytes 3145736 | tf_op jit(solution)/shard_map/ppermute | solution.py:758
  133.7 14.9 %collective-permute-start.7 = (bf16[512,512]{1,0:T(8,128)(2,1)}, bf16[512,512]{1,0:T(8,128)(2,1)S(1)}, u32[]{:S(2)}, u32[]{:S(2)}) collective-permute-start(bf16[512,512]{1,0:T(8,128)(2,1)} %pad_maximum_fusion.14.refs_5_.refs_1_.refs_2_), channel_id=1, source_target_pairs={{0,8},{4,12},{8,0},{12,4},{1,9},{5,13},{9,1},{13,5},{2,10},{6,14},... | collective-permute-start | bytes 1572872 | tf_op jit(solution)/shard_map/ppermute | solution.py:758
  135.2 24.6 %collective-permute-start.8 = (bf16[512,512]{1,0:T(8,128)(2,1)}, bf16[512,512]{1,0:T(8,128)(2,1)S(1)}, u32[]{:S(2)}, u32[]{:S(2)}) collective-permute-start(bf16[512,512]{1,0:T(8,128)(2,1)} %collective-permute-done.2.refs_7_.refs_3_.refs_5_.refs_4_), channel_id=1, source_target_pairs={{0,8},{4,12},{8,0},{12,4},{1,9},{5,13},{9,1},{13,5},{2,10},{6,14},... | collective-permute-start | bytes 1572872 | tf_op jit(solution)/shard_map/ppermute | solution.py:758
  135.8 35.3 %collective-permute-start.9 = (bf16[512,512]{1,0:T(8,128)(2,1)}, bf16[512,512]{1,0:T(8,128)(2,1)S(1)}, u32[]{:S(2)}, u32[]{:S(2)}) collective-permute-start(bf16[512,512]{1,0:T(8,128)(2,1)} %copy-done.33), channel_id=1, source_target_pairs={{0,8},{4,12},{8,0},{12,4},{1,9},{5,13},{9,1},{13,5},{2,10},{6,14},... | collective-permute-start | bytes 1572872 | tf_op jit(solution)/shard_map/ppermute | solution.py:758
  139.7 250.7 %copy-start.91 = (f32[1024,128]{1,0:T(8,128)}, f32[1024,128]{1,0:T(8,128)S(1)}, u32[]{:S(2)}) copy-start(f32[1024,128]{1,0:T(8,128)S(1)} %pad_maximum_fusion.12.refs_1_) | copy-start | bytes 1572868
  149.4 44.1 %collective-permute-start.12 = (bf16[512,1024]{1,0:T(8,128)(2,1)}, bf16[512,1024]{1,0:T(8,128)(2,1)S(1)}, u32[]{:S(2)}, u32[]{:S(2)}) collective-permute-start(bf16[512,1024]{1,0:T(8,128)(2,1)} %collective-permute-done.10.refs_13_.refs_3_.refs_2_.refs_4_), channel_id=1, source_target_pairs={{0,8},{4,12},{8,0},{12,4},{1,9},{5,13},{9,1},{13,5},{2,10},{6,14},... | collective-permute-start | bytes 3145736 | tf_op jit(solution)/shard_map/ppermute | solution.py:758
  150.9 64.7 %collective-permute-start.15 = (bf16[512,1024]{1,0:T(8,128)(2,1)S(1)}, bf16[512,1024]{1,0:T(8,128)(2,1)S(1)}, u32[]{:S(2)}, u32[]{:S(2)}) collective-permute-start(bf16[512,1024]{1,0:T(8,128)(2,1)S(1)} %collective-permute-done.11.refs_9_.refs_4_.refs_3_.refs_5_), channel_id=1, source_target_pairs={{0,8},{4,12},{8,0},{12,4},{1,9},{5,13},{9,1},{13,5},{2,10},{6,14},... | collective-permute-start | bytes 3145736 | tf_op jit(solution)/shard_map/ppermute | solution.py:758
  159.8 243.5 %copy-start.52 = (bf16[512,512]{1,0:T(8,128)(2,1)}, bf16[512,512]{1,0:T(8,128)(2,1)S(1)}, u32[]{:S(2)}) copy-start(bf16[512,512]{1,0:T(8,128)(2,1)S(1)} %collective-permute-done.8.refs_11_.refs_7_.refs_8_) | copy-start | bytes 1572868
  159.8 55.8 %collective-permute-start.14 = (bf16[512,1024]{1,0:T(8,128)(2,1)S(1)}, bf16[512,1024]{1,0:T(8,128)(2,1)S(1)}, u32[]{:S(2)}, u32[]{:S(2)}) collective-permute-start(bf16[512,1024]{1,0:T(8,128)(2,1)S(1)} %collective-permute-done.11.refs_9_.refs_4_.refs_3_.refs_5_), channel_id=1, source_target_pairs={{0,1},{1,2},{2,3},{3,0},{4,5},{5,6},{6,7},{7,4},{8,9},{9,10},{10,1... | collective-permute-start | bytes 3145736 | tf_op jit(solution)/shard_map/ppermute | solution.py:763
  171.1 232.3 %copy-start.54 = (bf16[512,512]{1,0:T(8,128)(2,1)}, bf16[512,512]{1,0:T(8,128)(2,1)S(1)}, u32[]{:S(2)}) copy-start(bf16[512,512]{1,0:T(8,128)(2,1)S(1)} %collective-permute-done.9.refs_12_.refs_8_.refs_9_) | copy-start | bytes 1572868
  193.5 168.2 %copy-start.6 = (bf16[512,1024]{1,0:T(8,128)(2,1)}, bf16[512,1024]{1,0:T(8,128)(2,1)S(1)}, u32[]{:S(2)}) copy-start(bf16[512,1024]{1,0:T(8,128)(2,1)S(1)} %collective-permute-done.12.refs_10_.refs_7_.refs_6_.refs_8_) | copy-start | bytes 3145732
  196.6 19.0 %collective-permute-start.13 = (bf16[512,1024]{1,0:T(8,128)(2,1)S(1)}, bf16[512,1024]{1,0:T(8,128)(2,1)S(1)}, u32[]{:S(2)}, u32[]{:S(2)}) collective-permute-start(bf16[512,1024]{1,0:T(8,128)(2,1)S(1)} %get-tuple-element.103), channel_id=1, source_target_pairs={{0,4},{4,0},{8,12},{12,8},{1,5},{5,1},{9,13},{13,9},{2,6},{6,2},{1... | collective-permute-start | bytes 3145736 | tf_op jit(solution)/shard_map/ppermute | solution.py:758
  215.6 146.1 %copy-start.19 = (bf16[512,1024]{1,0:T(8,128)(2,1)}, bf16[512,1024]{1,0:T(8,128)(2,1)S(1)}, u32[]{:S(2)}) copy-start(bf16[512,1024]{1,0:T(8,128)(2,1)S(1)} %collective-permute-done.15.refs_5_.refs_8_.refs_7_.refs_9_) | copy-start | bytes 3145732
  220.6 15.0 %collective-permute-start.16 = (bf16[512,1024]{1,0:T(8,128)(2,1)S(1)}, bf16[512,1024]{1,0:T(8,128)(2,1)S(1)}, u32[]{:S(2)}, u32[]{:S(2)}) collective-permute-start(bf16[512,1024]{1,0:T(8,128)(2,1)S(1)} %get-tuple-element.143.refs_0_), channel_id=1, source_target_pairs={{0,4},{4,0},{8,12},{12,8},{1,5},{5,1},{9,13},{13,9},{2,6},{6,2},{1... | collective-permute-start | bytes 3145736 | tf_op jit(solution)/shard_map/ppermute | solution.py:758
  220.8 14.8 %collective-permute-start.17 = (bf16[512,512]{1,0:T(8,128)(2,1)S(1)}, bf16[512,512]{1,0:T(8,128)(2,1)S(1)}, u32[]{:S(2)}, u32[]{:S(2)}) collective-permute-start(bf16[512,512]{1,0:T(8,128)(2,1)S(1)} %get-tuple-element.241), channel_id=1, source_target_pairs={{0,8},{4,12},{8,0},{12,4},{1,9},{5,13},{9,1},{13,5},{2,10},{6,14},... | collective-permute-start | bytes 1572872 | tf_op jit(solution)/shard_map/ppermute | solution.py:758
  222.4 24.9 %collective-permute-start.18 = (bf16[512,512]{1,0:T(8,128)(2,1)S(1)}, bf16[512,512]{1,0:T(8,128)(2,1)S(1)}, u32[]{:S(2)}, u32[]{:S(2)}) collective-permute-start(bf16[512,512]{1,0:T(8,128)(2,1)S(1)} %get-tuple-element.240), channel_id=1, source_target_pairs={{0,8},{4,12},{8,0},{12,4},{1,9},{5,13},{9,1},{13,5},{2,10},{6,14},... | collective-permute-start | bytes 1572872 | tf_op jit(solution)/shard_map/ppermute | solution.py:758
  235.6 126.2 %copy-start.97 = (bf16[512,512]{1,0:T(8,128)(2,1)}, bf16[512,512]{1,0:T(8,128)(2,1)S(1)}, u32[]{:S(2)}) copy-start(bf16[512,512]{1,0:T(8,128)(2,1)S(1)} %collective-permute-done.17.refs_9_.refs_8_) | copy-start | bytes 1572868
  247.3 108.3 %copy-start.56 = (bf16[512,512]{1,0:T(8,128)(2,1)}, bf16[512,512]{1,0:T(8,128)(2,1)S(1)}, u32[]{:S(2)}) copy-start(bf16[512,512]{1,0:T(8,128)(2,1)S(1)} %collective-permute-done.18.refs_8_.refs_10_) | copy-start | bytes 1572868
  253.8 2.7 collective-permute-start.19
  258.5 25.9 %collective-permute-start.20 = (bf16[512,1024]{1,0:T(8,128)(2,1)S(1)}, bf16[512,1024]{1,0:T(8,128)(2,1)S(1)}, u32[]{:S(2)}, u32[]{:S(2)}) collective-permute-start(bf16[512,1024]{1,0:T(8,128)(2,1)S(1)} %get-tuple-element.134), channel_id=1, source_target_pairs={{0,16},{1,17},{2,18},{3,19},{4,20},{5,21},{6,22},{7,23},{8,24},{9,... | collective-permute-start | bytes 3145736 | tf_op jit(solution)/shard_map/ppermute | solution.py:27
  296.5 2.7 collective-permute-start.21
  320.8 2.7 collective-permute-start.22
  327.0 2.7 collective-permute-start.23
  345.8 2.7 collective-permute-start.24
  352.9 2.7 collective-permute-start.25
  368.4 2.7 collective-permute-start.26
  375.0 2.7 collective-permute-start.27
  409.6 2.7 collective-permute-start.28
  415.4 27.5 %collective-permute-start.30 = (bf16[512,1024]{1,0:T(8,128)(2,1)}, bf16[512,1024]{1,0:T(8,128)(2,1)}, u32[]{:S(2)}, u32[]{:S(2)}) collective-permute-start(bf16[512,1024]{1,0:T(8,128)(2,1)} %get-tuple-element.133), channel_id=1, source_target_pairs={{16,0},{17,1},{18,2},{19,3},{20,4},{21,5},{22,6},{23,7},{24,8},{25... | collective-permute-start | bytes 3145736 | tf_op jit(solution)/shard_map/ppermute | solution.py:27
  422.4 30.8 %all-to-all-start.1 = ((bf16[4,128,1024]{2,1,0:T(8,128)(2,1)}), bf16[4,128,1024]{2,1,0:T(8,128)(2,1)}, u32[]{:S(2)}, u32[]{:S(2)}) async-start(bf16[4,128,1024]{2,1,0:T(8,128)(2,1)} %bitcast.79), calls=%async_computation.1 | async-start | bytes 2097152 | tf_op jit(solution)/shard_map/all_to_all | solution.py:840
  449.3 5.7 collective-permute-start.31
  455.0 213.4 %collective-permute-start.29 = (bf16[2,128,1024]{2,1,0:T(8,128)(2,1)}, bf16[2,128,1024]{2,1,0:T(8,128)(2,1)}, u32[]{:S(2)}, u32[]{:S(2)}) collective-permute-start(bf16[2,128,1024]{2,1,0:T(8,128)(2,1)} %dynamic-slice_bitcast_fusion.1), channel_id=1, source_target_pairs={{0,4},{4,0},{8,12},{12,8},{1,5},{5,1},{9,13},{13,9},{2,6},{6,2},{1... | collective-permute-start | bytes 1572872 | tf_op jit(solution)/shard_map/ppermute | solution.py:758
  481.2 10.3 %collective-permute-start.32 = (bf16[512,1024]{1,0:T(8,128)(2,1)S(1)}, bf16[512,1024]{1,0:T(8,128)(2,1)S(1)}, u32[]{:S(2)}, u32[]{:S(2)}) collective-permute-start(bf16[512,1024]{1,0:T(8,128)(2,1)S(1)} %get-tuple-element.152), channel_id=1, source_target_pairs={{0,4},{4,0},{8,12},{12,8},{1,5},{5,1},{9,13},{13,9},{2,6},{6,2},{1... | collective-permute-start | bytes 3145736 | tf_op jit(solution)/shard_map/ppermute | solution.py:758
  484.7 26.1 %collective-permute-start.33 = (bf16[512,1024]{1,0:T(8,128)(2,1)S(1)}, bf16[512,1024]{1,0:T(8,128)(2,1)S(1)}, u32[]{:S(2)}, u32[]{:S(2)}) collective-permute-start(bf16[512,1024]{1,0:T(8,128)(2,1)S(1)} %get-tuple-element.154), channel_id=1, source_target_pairs={{0,8},{4,12},{8,0},{12,4},{1,9},{5,13},{9,1},{13,5},{2,10},{6,14},... | collective-permute-start | bytes 3145736 | tf_op jit(solution)/shard_map/ppermute | solution.py:758
  489.6 43.6 %collective-permute-start.36 = (bf16[512,1024]{1,0:T(8,128)(2,1)S(1)}, bf16[512,1024]{1,0:T(8,128)(2,1)S(1)}, u32[]{:S(2)}, u32[]{:S(2)}) collective-permute-start(bf16[512,1024]{1,0:T(8,128)(2,1)S(1)} %get-tuple-element.162), channel_id=1, source_target_pairs={{0,8},{4,12},{8,0},{12,4},{1,9},{5,13},{9,1},{13,5},{2,10},{6,14},... | collective-permute-start | bytes 3145736 | tf_op jit(solution)/shard_map/ppermute | solution.py:758
  516.0 18.7 %collective-permute-start.34 = (bf16[512,1024]{1,0:T(8,128)(2,1)S(1)}, bf16[512,1024]{1,0:T(8,128)(2,1)S(1)}, u32[]{:S(2)}, u32[]{:S(2)}) collective-permute-start(bf16[512,1024]{1,0:T(8,128)(2,1)S(1)} %get-tuple-element.155.refs_3_), channel_id=1, source_target_pairs={{0,4},{4,0},{8,12},{12,8},{1,5},{5,1},{9,13},{13,9},{2,6},{6,2},{1... | collective-permute-start | bytes 3145736 | tf_op jit(solution)/shard_map/ppermute | solution.py:758
  516.5 25.6 %collective-permute-start.37 = (bf16[512,1024]{1,0:T(8,128)(2,1)S(1)}, bf16[512,1024]{1,0:T(8,128)(2,1)S(1)}, u32[]{:S(2)}, u32[]{:S(2)}) collective-permute-start(bf16[512,1024]{1,0:T(8,128)(2,1)S(1)} %add_convert_fusion.2), channel_id=1, source_target_pairs={{0,3},{1,0},{2,1},{3,2},{4,7},{5,4},{6,5},{7,6},{8,11},{9,8},{10,9... | collective-permute-start | bytes 3145736 | tf_op jit(solution)/shard_map/ppermute | solution.py:763
  520.8 77.7 %collective-permute-start.39 = (bf16[512,1024]{1,0:T(8,128)(2,1)S(1)}, bf16[512,1024]{1,0:T(8,128)(2,1)S(1)}, u32[]{:S(2)}, u32[]{:S(2)}) collective-permute-start(bf16[512,1024]{1,0:T(8,128)(2,1)S(1)} %get-tuple-element.164), channel_id=1, source_target_pairs={{0,8},{4,12},{8,0},{12,4},{1,9},{5,13},{9,1},{13,5},{2,10},{6,14},... | collective-permute-start | bytes 3145736 | tf_op jit(solution)/shard_map/ppermute | solution.py:758
  533.2 44.9 %collective-permute-start.35 = (bf16[512,1024]{1,0:T(8,128)(2,1)S(1)}, bf16[512,1024]{1,0:T(8,128)(2,1)S(1)}, u32[]{:S(2)}, u32[]{:S(2)}) collective-permute-start(bf16[512,1024]{1,0:T(8,128)(2,1)S(1)} %get-tuple-element.160), channel_id=1, source_target_pairs={{0,8},{4,12},{8,0},{12,4},{1,9},{5,13},{9,1},{13,5},{2,10},{6,14},... | collective-permute-start | bytes 3145736 | tf_op jit(solution)/shard_map/ppermute | solution.py:758
  555.4 25.7 %collective-permute-start.38 = (bf16[512,1024]{1,0:T(8,128)(2,1)S(1)}, bf16[512,1024]{1,0:T(8,128)(2,1)S(1)}, u32[]{:S(2)}, u32[]{:S(2)}) collective-permute-start(bf16[512,1024]{1,0:T(8,128)(2,1)S(1)} %add_convert_fusion.1), channel_id=1, source_target_pairs={{0,3},{1,0},{2,1},{3,2},{4,7},{5,4},{6,5},{7,6},{8,11},{9,8},{10,9... | collective-permute-start | bytes 3145736 | tf_op jit(solution)/shard_map/ppermute | solution.py:763
  564.1 51.9 %collective-permute-start.46 = (bf16[512,512]{1,0:T(8,128)(2,1)S(1)}, bf16[512,512]{1,0:T(8,128)(2,1)S(1)}, u32[]{:S(2)}, u32[]{:S(2)}) collective-permute-start(bf16[512,512]{1,0:T(8,128)(2,1)S(1)} %get-tuple-element.185), channel_id=1, source_target_pairs={{0,8},{4,12},{8,0},{12,4},{1,9},{5,13},{9,1},{13,5},{2,10},{6,14},... | collective-permute-start | bytes 1572872 | tf_op jit(solution)/shard_map/ppermute | solution.py:758
  581.6 25.7 %collective-permute-start.40 = (bf16[512,1024]{1,0:T(8,128)(2,1)S(1)}, bf16[512,1024]{1,0:T(8,128)(2,1)S(1)}, u32[]{:S(2)}, u32[]{:S(2)}) collective-permute-start(bf16[512,1024]{1,0:T(8,128)(2,1)S(1)} %add_convert_fusion), channel_id=1, source_target_pairs={{0,3},{1,0},{2,1},{3,2},{4,7},{5,4},{6,5},{7,6},{8,11},{9,8},{10,9... | collective-permute-start | bytes 3145736 | tf_op jit(solution)/shard_map/ppermute | solution.py:763
  612.6 12.6 %collective-permute-start.41 = (bf16[512,1024]{1,0:T(8,128)(2,1)S(1)}, bf16[512,1024]{1,0:T(8,128)(2,1)S(1)}, u32[]{:S(2)}, u32[]{:S(2)}) collective-permute-start(bf16[512,1024]{1,0:T(8,128)(2,1)S(1)} %get-tuple-element.167), channel_id=1, source_target_pairs={{0,4},{4,0},{8,12},{12,8},{1,5},{5,1},{9,13},{13,9},{2,6},{6,2},{1... | collective-permute-start | bytes 3145736 | tf_op jit(solution)/shard_map/ppermute | solution.py:758
  614.4 18.9 %collective-permute-start.45 = (bf16[512,512]{1,0:T(8,128)(2,1)}, bf16[512,512]{1,0:T(8,128)(2,1)}, u32[]{:S(2)}, u32[]{:S(2)}) collective-permute-start(bf16[512,512]{1,0:T(8,128)(2,1)} %get-tuple-element.183), channel_id=1, source_target_pairs={{0,8},{4,12},{8,0},{12,4},{1,9},{5,13},{9,1},{13,5},{2,10},{6,14},... | collective-permute-start | bytes 1572872 | tf_op jit(solution)/shard_map/ppermute | solution.py:758
  616.9 16.4 %collective-permute-start.47 = (bf16[512,512]{1,0:T(8,128)(2,1)}, bf16[512,512]{1,0:T(8,128)(2,1)}, u32[]{:S(2)}, u32[]{:S(2)}) collective-permute-start(bf16[512,512]{1,0:T(8,128)(2,1)} %add_convert_fusion.5), channel_id=1, source_target_pairs={{0,3},{1,0},{2,1},{3,2},{4,7},{5,4},{6,5},{7,6},{8,11},{9,8},{10,9... | collective-permute-start | bytes 1572872 | tf_op jit(solution)/shard_map/ppermute | solution.py:763
  624.6 18.1 %collective-permute-start.44 = (bf16[512,512]{1,0:T(8,128)(2,1)}, bf16[512,512]{1,0:T(8,128)(2,1)}, u32[]{:S(2)}, u32[]{:S(2)}) collective-permute-start(bf16[512,512]{1,0:T(8,128)(2,1)} %get-tuple-element.181), channel_id=1, source_target_pairs={{0,8},{4,12},{8,0},{12,4},{1,9},{5,13},{9,1},{13,5},{2,10},{6,14},... | collective-permute-start | bytes 1572872 | tf_op jit(solution)/shard_map/ppermute | solution.py:758
  628.9 55.3 %all-to-all-start.2 = ((bf16[4,128,1024]{2,1,0:T(8,128)(2,1)}), bf16[4,128,1024]{2,1,0:T(8,128)(2,1)}, u32[]{:S(2)}, u32[]{:S(2)}) async-start(bf16[4,128,1024]{2,1,0:T(8,128)(2,1)} %bitcast.19), calls=%async_computation.2 | async-start | bytes 2097152 | tf_op jit(solution)/shard_map/all_to_all | solution.py:840
  633.2 113.1 %reduce-scatter.4.cloned.1.call-start = ((), (), s32[]{:S(2)}) async-start(), calls=%async_computation.4 | async-start | bytes 557056
  634.9 28.8 %collective-permute-start.48 = (bf16[512,512]{1,0:T(8,128)(2,1)S(1)}, bf16[512,512]{1,0:T(8,128)(2,1)S(1)}, u32[]{:S(2)}, u32[]{:S(2)}) collective-permute-start(bf16[512,512]{1,0:T(8,128)(2,1)S(1)} %add_convert_fusion.4), channel_id=1, source_target_pairs={{0,3},{1,0},{2,1},{3,2},{4,7},{5,4},{6,5},{7,6},{8,11},{9,8},{10,9... | collective-permute-start | bytes 1572872 | tf_op jit(solution)/shard_map/ppermute | solution.py:763
  641.5 29.1 %collective-permute-start.43 = (bf16[512,512]{1,0:T(8,128)(2,1)S(1)}, bf16[512,512]{1,0:T(8,128)(2,1)S(1)}, u32[]{:S(2)}, u32[]{:S(2)}) collective-permute-start(bf16[512,512]{1,0:T(8,128)(2,1)S(1)} %get-tuple-element.179), channel_id=1, source_target_pairs={{0,8},{4,12},{8,0},{12,4},{1,9},{5,13},{9,1},{13,5},{2,10},{6,14},... | collective-permute-start | bytes 1572872 | tf_op jit(solution)/shard_map/ppermute | solution.py:758
  665.0 18.3 %collective-permute-start.49 = (bf16[512,512]{1,0:T(8,128)(2,1)S(1)}, bf16[512,512]{1,0:T(8,128)(2,1)S(1)}, u32[]{:S(2)}, u32[]{:S(2)}) collective-permute-start(bf16[512,512]{1,0:T(8,128)(2,1)S(1)} %add_convert_fusion.3), channel_id=1, source_target_pairs={{0,3},{1,0},{2,1},{3,2},{4,7},{5,4},{6,5},{7,6},{8,11},{9,8},{10,9... | collective-permute-start | bytes 1572872 | tf_op jit(solution)/shard_map/ppermute | solution.py:763
  668.4 25.9 %collective-permute-start.51 = (f32[256,1024]{1,0:T(8,128)}, f32[256,1024]{1,0:T(8,128)}, u32[]{:S(2)}, u32[]{:S(2)}) collective-permute-start(f32[256,1024]{1,0:T(8,128)} %get-tuple-element.192), channel_id=1, source_target_pairs={{0,4},{4,0},{8,12},{12,8},{1,5},{5,1},{9,13},{13,9},{2,6},{6,2},{1... | collective-permute-start | bytes 3145736 | tf_op jit(solution)/shard_map/ppermute | solution.py:758
  684.3 6.0 collective-permute-start.50
  686.1 61.6 %collective-permute-start.42 = (bf16[2,128,1024]{2,1,0:T(8,128)(2,1)}, bf16[2,128,1024]{2,1,0:T(8,128)(2,1)}, u32[]{:S(2)}, u32[]{:S(2)}) collective-permute-start(bf16[2,128,1024]{2,1,0:T(8,128)(2,1)} %dynamic-slice_bitcast_fusion), channel_id=1, source_target_pairs={{0,4},{4,0},{8,12},{12,8},{1,5},{5,1},{9,13},{13,9},{2,6},{6,2},{1... | collective-permute-start | bytes 1572872 | tf_op jit(solution)/shard_map/ppermute | solution.py:758
  (115 other events, 1053.8 us)
Sparse Core Ops, SparseCore 0:
  687.9 58.3 reduce-scatter.3

commit v6 on v5

--- a/solution.py
+++ b/solution.py
@@ -14,11 +14,12 @@
 NORM_EPSILON = 1e-06
 TILE = 128
 PAIR_WORK = 1024
+MODEL_HALF = 512
 QKV = slice(0, 384)
 OUT = slice(384, 512)
 CHUNK = 32
-KERNEL_VMEM = 24 << 20
-ROWS_VMEM = 8 << 20
+KERNEL_VMEM = 20 << 20
+ROWS_VMEM = 3 << 20
 
 
 def shifted(block, axis, distance):
@@ -338,14 +339,8 @@
     return jnp.dot(left, right, preferred_element_type=jnp.float32)
 
 
-def columns_of(ref, cols):
-    return ref[...] if ref.shape[1] == cols.stop - cols.start else ref[:, cols]
-
-
 def model_weight(owns, others, cols):
-    sides = [
-        jnp.concatenate([columns_of(ref, cols) for ref in refs], axis=1) for refs in (owns, others)
-    ]
+    sides = [jnp.concatenate([ref[:, cols] for ref in refs], axis=1) for refs in (owns, others)]
     return jnp.concatenate(sides, axis=0)
 
 
@@ -509,6 +504,11 @@
     split_rows(dot_nt(left, weight), *refs[2 * pieces :])
 
 
+def mlp_down_kernel(pieces, left_ref, *refs):
+    sides = [stacked_up([ref[...] for ref in side]) for side in (refs[:pieces], refs[pieces:-2])]
+    split_rows(dot_nn(left_ref[...], jnp.concatenate(sides, axis=1)), *refs[-2:])
+
+
 def gelu_both(up_act):
     root = math.sqrt(2.0 / math.pi)
     square = up_act * up_act
@@ -522,14 +522,13 @@
     owns, others = refs[:pieces], refs[pieces : 2 * pieces]
     gelu_ref, slope_ref = refs[2 * pieces :]
     half = own_rows.shape[0]
-    size = owns[0].shape[1] // 2
-    cols = slice(0, size)
+    size = owns[0].shape[1]
     step = half // 2
     units = [(j, i) for j in range(pieces) for i in range(4)]
 
     def product(j, i):
         rows = (own_rows, other_rows)[i // 2][i % 2 * step : (i % 2 + 1) * step]
-        return dot_nn(rows, stacked_up([columns_of(owns[j], cols), columns_of(others[j], cols)]))
+        return dot_nn(rows, stacked_up([owns[j][...], others[j][...]]))
 
     ahead = product(*units[0])
     for spot, (j, i) in enumerate(units):
@@ -546,13 +545,12 @@
 def mlp_up_back_kernel(pieces, own_rows, other_rows, slope_ref, *refs):
     owns, others = refs[:pieces], refs[pieces : 2 * pieces]
     out_ref = refs[-1]
-    size = owns[0].shape[1] // 2
+    size = owns[0].shape[0]
     rows = stacked_up([own_rows[...], other_rows[...]])
-    taken = slice(size, 2 * size)
     for j in range(pieces):
         cols = slice(j * size, (j + 1) * size)
-        weight = stacked_up([columns_of(owns[j], taken), columns_of(others[j], taken)])
-        d_gelu = dot_nn(rows, weight)
+        weight = jnp.concatenate([owns[j][...], others[j][...]], axis=1)
+        d_gelu = dot_nt(rows, weight)
         out_ref[:, cols] = (d_gelu * slope_ref[:, cols].astype(jnp.float32)).astype(jnp.bfloat16)
 
 
@@ -740,17 +738,16 @@
     )[0]
 
 
-def model_rows(name, lefts, pieces, cols, waits=()):
-    owns, others = pieces
-    length, width = lefts[0].shape[0], 2 * owns[0].shape[0]
+def exchanged(parts):
+    return parts[0], flip_pairs(parts[1], 1)
+
+
+def model_rows(kernel, name, lefts, pieces, waits=()):
+    length, width = lefts[0].shape[0], 2 * MODEL_HALF
     outs = (((length // 2, width), jnp.float32), ((length // 2, width), jnp.bfloat16))
-    kernel = functools.partial(to_model_kernel, len(lefts), len(owns), cols)
     hidden = sum(left.shape[1] for left in lefts)
-    flops = 2 * length * width * hidden
-    operands = (*lefts, *owns, *others)
-    more = {"limit": KERNEL_VMEM, "flops": flops, "waits": waits}
-    own, other = on_chip(kernel, name, outs, *operands, **more)
-    return own, flip_pairs(other, 1)
+    more = {"limit": KERNEL_VMEM, "flops": 2 * length * width * hidden, "waits": waits}
+    return exchanged(on_chip(kernel, name, outs, *lefts, *pieces[0], *pieces[1], **more))
 
 
 def flip_pairs(block, distance):
@@ -764,11 +761,80 @@
 
 
 def pack_kernel(first_ref, second_ref, own_ref, other_ref):
+    half = first_ref.shape[0] // 2
+    own_ref[:half] = first_ref[:half]
+    own_ref[half:] = second_ref[:, :half]
+    other_ref[:half] = first_ref[half:].astype(jnp.bfloat16)
+    other_ref[half:] = second_ref[:, half:].astype(jnp.bfloat16)
+
+
+def pack_wide_kernel(first_ref, second_ref, own_ref, other_ref):
     half, width = own_ref.shape[0], first_ref.shape[1]
     own_ref[:, :width] = first_ref[:half]
     own_ref[:, width:] = second_ref[:half]
     other_ref[:, :width] = first_ref[half:].astype(jnp.bfloat16)
     other_ref[:, width:] = second_ref[half:].astype(jnp.bfloat16)
+
+
+def gate_kernel(up_ref, down_ref, up_out, down_out):
+    up_out[...] = up_ref[...]
+    down_out[...] = down_ref[...]
+
+
+def mlp_sum_kernel(core_ref, own_ref, other_ref, moved_ref, up_keep, down_keep, up_send, down_send):
+    half = own_ref.shape[0] // 2
+    size = up_keep.shape[0]
+
+    def total(rows, cols):
+        more = other_ref[rows, cols].astype(jnp.float32) + moved_ref[rows, cols].astype(jnp.float32)
+        return own_ref[rows, cols] + more
+
+    for core in range(2):
+
+        @pl.when(core_ref[0] == core)
+        def _():
+            for place, up, down in ((core, up_keep, down_keep), (1 - core, up_send, down_send)):
+                spot = slice(place * size, (place + 1) * size)
+                up[...] = total(spot, slice(None))
+                down[...] = total(slice(half, None), spot)
+
+
+def mlp_join_kernel(core_ref, up_keep, down_keep, up_sent, down_sent, up_out, down_out):
+    size = up_keep.shape[1]
+    for core in range(2):
+
+        @pl.when(core_ref[0] == core)
+        def _():
+            places = ((core, up_keep, down_keep), (1 - core, up_sent, down_sent))
+            for place, up, down in places:
+                spot = slice(place * size, (place + 1) * size)
+                up_out[:, spot] = up[...]
+                down_out[spot] = down[...]
+
+
+def pick_kernel(core_ref, rows_ref, keep_ref, send_ref):
+    count = keep_ref.shape[0]
+    keep_ref[...] = rows_ref[pl.ds(core_ref[0] * count, count)]
+    send_ref[...] = rows_ref[pl.ds((1 - core_ref[0]) * count, count)]
+
+
+def in_order_kernel(core_ref, keep_ref, sent_ref, out_ref):
+    out_ref[:, pl.ds(core_ref[0], 1)] = keep_ref[...][:, None]
+    out_ref[:, pl.ds(1 - core_ref[0], 1)] = sent_ref[...][:, None]
+
+
+def with_core(kernel, name, core, outs, *operands, waits=()):
+    space = pl.BlockSpec(memory_space=pltpu.VMEM)
+    return pl.pallas_call(
+        without(kernel, 1 + len(operands), len(waits)),
+        in_specs=[pl.BlockSpec(memory_space=pltpu.SMEM)]
+        + [space] * len(operands)
+        + [pl.BlockSpec(memory_space=pl.ANY)] * len(waits),
+        out_specs=[space] * len(outs),
+        out_shape=[jax.ShapeDtypeStruct(shape, dtype) for shape, dtype in outs],
+        compiler_params=pltpu.CompilerParams(vmem_limit_bytes=ROWS_VMEM),
+        name=name,
+    )(core, *operands, *waits)
 
 
 def last_sum_kernel(core_ref, own_ref, other_ref, moved_ref, keep_ref, send_ref):
@@ -836,13 +902,17 @@
             jnp.concatenate(ordered(mine, flip_pairs(other, 1))), "tensor", 0, 0, tiled=True
         )
 
-    def from_chip(block):
+    def from_chip(block, waits=()):
         spread_out = lax.all_to_all(block, "tensor", 0, 0, tiled=True)
-        grouped = spread_out.reshape((2, micro, part) + block.shape[2:])
-        mine = lax.dynamic_index_in_dim(grouped, core, 0, keepdims=False)
-        other = lax.dynamic_index_in_dim(grouped, 1 - core, 0, keepdims=False)
-        pair = ordered(mine, flip_pairs(other, 1))
-        return jnp.stack(pair, axis=1).reshape((micro, row_count) + block.shape[2:])
+        piece = ((micro, part, width), jnp.bfloat16)
+        keep, send = with_core(
+            pick_kernel, "pick", core_word, (piece, piece), spread_out, waits=waits
+        )
+        outs = (((micro, 2, part, width), jnp.bfloat16),)
+        (rows,) = with_core(
+            in_order_kernel, "in_order", core_word, outs, keep, flip_pairs(send, 1)
+        )
+        return rows.reshape(micro, row_count, width)
 
     def columns(local):
         size = local.shape[-1] // 2
@@ -856,13 +926,10 @@
 
     def rows(local):
         size = local.shape[0] // 2
-        return lax.dynamic_slice(local, (size * core, wide_half * upper), (size, wide_half)).T
+        return lax.dynamic_slice(local, (size * core, wide_half * upper), (size, wide_half))
 
     core_word = core.astype(jnp.int32).reshape(1)
-    attn_piece = jnp.concatenate([columns(qkv_weight[0]), rows(out_weight[0])], axis=1)
-    mlp_piece = jnp.concatenate([columns(up_weight[0]), rows(down_weight[0])], axis=1)
-    units = tensor * mlp_piece.shape[1] // 2
-    ups, downs = slice(0, units // tensor), slice(units // tensor, 2 * units // tensor)
+    attn_piece = jnp.concatenate([columns(qkv_weight[0]), rows(out_weight[0]).T], axis=1)
 
     def spread(piece):
         pieces = [piece]
@@ -870,13 +937,19 @@
             pieces.append(passed_on(pieces[-1], 1))
         return pieces
 
-    attn_own, mlp_own = spread(attn_piece), spread(mlp_piece)
+    attn_own = spread(attn_piece)
     attn_other = [flip_pairs(piece, 2) for piece in attn_own]
-    mlp_other = [flip_pairs(piece, 2) for piece in mlp_own[:-1]]
-    up_last, down_last = (flip_pairs(mlp_own[-1][:, cols], 2) for cols in (ups, downs))
-    w_attn = (attn_own, attn_other)
-    w_up = (mlp_own, mlp_other + [up_last])
-    w_down = (mlp_own, mlp_other + [down_last])
+    up_piece, down_piece = columns(up_weight[0]), rows(down_weight[0])
+    outs = tuple((piece.shape, piece.dtype) for piece in (up_piece, down_piece))
+    up_piece, down_piece = on_chip(
+        gate_kernel, "gate", outs, up_piece, down_piece, waits=(attn_own[2],)
+    )
+    up_own, down_own = spread(up_piece), spread(down_piece)
+    up_other = [flip_pairs(piece, 2) for piece in up_own]
+    down_other = [flip_pairs(piece, 2) for piece in down_own]
+    w_attn, w_up, w_down = (attn_own, attn_other), (up_own, up_other), (down_own, down_other)
+    unit = up_piece.shape[1]
+    units = tensor * unit
 
     group_count = group_weights.shape[0]
     matches = group_ids[..., None] == jnp.arange(group_count, dtype=jnp.int32)
@@ -899,13 +972,19 @@
     unit16 = ((length, units), jnp.bfloat16)
     sum32 = ((1, width), jnp.float32)
     mlp_cost = {"limit": KERNEL_VMEM, "flops": 2 * length * width * units}
+    every = slice(None)
+
+    def model_kernel(cols, lefts=1):
+        return functools.partial(to_model_kernel, lefts, tensor, cols)
+
+    down_kernel = functools.partial(mlp_down_kernel, tensor)
 
     def forward(layer_input, waits):
         attn_in = both_rows(
             on_chip(norm_in_kernel, "norm_in", (row16,), gain, layer_input, waits=waits[0])[0]
         )
         *heads, mixed = attend(core_word, tables, attn_in, w_attn, waits[1])
-        parts = model_rows("attn_out", [mixed], w_attn, OUT, waits[2])
+        parts = model_rows(model_kernel(OUT), "attn_out", [mixed], w_attn, waits[2])
         operands = (gain, layer_input, *parts)
         branch, hidden, mlp_in = on_chip(
             after_attention_kernel, "after_attn", (row32, row32, row16), *operands, waits=waits[3]
@@ -914,7 +993,7 @@
         kernel = functools.partial(mlp_up_kernel, tensor)
         operands = (*mlp_in, *w_up[0], *w_up[1])
         gelu_out, slope = on_chip(kernel, "mlp_up", (unit16, unit16), *operands, **mlp_cost)
-        parts = model_rows("mlp_down", [gelu_out], w_down, downs)
+        parts = model_rows(down_kernel, "mlp_down", [gelu_out], w_down)
         mlp_branch, result = on_chip(
             after_mlp_kernel, "after_mlp", (row32, row16), gain, hidden, *parts
         )
@@ -932,7 +1011,8 @@
         operands = (*d_down, slope, *w_down[0], *w_down[1])
         (d_up,) = on_chip(kernel, "mlp_up_back", (unit16,), *operands, **mlp_cost)
         waits = hook(d_down, d_up)
-        parts = model_rows("mlp_back", [d_up], w_up, ups)
+        parts = model_rows(model_kernel(every), "mlp_back", [d_up], w_up, waits)
+        waits = hook()
         operands = (gain, grad, *parts, hidden, branch)
         outs = (row32, row16, sum32, sum32)
         d_hidden, d_attn, sum_one, sum_two = on_chip(
@@ -946,7 +1026,7 @@
             now = attend_back(core_word, tables, d_attn, some, base, waits, *heads)
             d_qkv.insert(0, now)
             waits = hook(now)
-        parts = model_rows("attn_back", d_qkv, w_attn, QKV, waits)
+        parts = model_rows(model_kernel(QKV, 2), "attn_back", d_qkv, w_attn, waits)
         operands = (gain, layer_input, *parts, d_hidden)
         d_input, sum_zero = on_chip(
             out_of_layer_kernel, "out_of_layer", (row16, sum32), *operands
@@ -957,10 +1037,10 @@
     low_zero, saved_zero, lefts_zero = forward(
         start,
         (
-            (attn_own[3], mlp_other[0], attn_other[1]),
-            (mlp_own[1],),
-            (mlp_own[2], mlp_other[1]),
-            (mlp_own[3], mlp_other[2]),
+            (attn_other[1],),
+            (up_own[1], down_own[1], up_other[0]),
+            (up_own[2], down_other[0]),
+            (down_own[2], up_other[1], down_other[1], up_own[3]),
         ),
     )
     low_one, saved_one, lefts_one = forward(shifted(low_zero, "section", 1), ((),) * 4)
@@ -973,29 +1053,30 @@
     def own_layer(zero, one):
         if isinstance(zero, tuple):
             zero, one = joined(zero), joined(one)
-        return lax.optimization_barrier(jnp.where(first, zero, one))
+        return jnp.where(first, zero, one)
 
     lefts_zero, lefts_one = lax.optimization_barrier((lefts_zero, lefts_one, grad_one))[:2]
     attn_in, mixed, mlp_in, gelu_out = lefts = list(map(own_layer, lefts_zero, lefts_one))
     lows = lax.optimization_barrier((low_zero, low_one, grad_one))[:2]
-    outputs = from_chip(own_first(jnp.where(first, *lows)).reshape(tensor, part, width))
+    lows = own_first(jnp.where(first, *lows)).reshape(tensor, part, width)
 
     def block(array, j, count=tensor):
         size = array.shape[1] // count
         return array[:, j * size : (j + 1) * size]
 
-    def leave(*pairs):
+    def leave(kernel, shape, *pairs):
         totals = [contract(*pair) for pair in pairs]
-        size = sum(total.shape[1] for total in totals)
-        outs = (((wide_half, size), jnp.float32), ((wide_half, size), jnp.bfloat16))
-        own, other = on_chip(pack_kernel, "pack", outs, *totals)
+        own, other = on_chip(kernel, "pack", ((shape, jnp.float32), (shape, jnp.bfloat16)), *totals)
         return own, flip_pairs(other, 2)
 
     def mlp_leaves(j):
-        return leave((mlp_in, block(d_up, j)), (d_down, block(gelu_out, j)))
+        shape = (wide_half + unit, unit)
+        return leave(pack_kernel, shape, (mlp_in, block(d_up, j)), (block(gelu_out, j), d_down))
 
     def attn_leaves(j, d_qkv):
-        return leave((attn_in, block(d_qkv, j % 2, 2)), (d_attn, block(mixed, j)))
+        shape = (wide_half, 512)
+        pairs = ((attn_in, block(d_qkv, j % 2, 2)), (d_attn, block(mixed, j)))
+        return leave(pack_wide_kernel, shape, *pairs)
 
     def moves_on(piece, moved=None):
         own, other = piece
@@ -1007,7 +1088,7 @@
     d_qkv_one, d_attn_one, d_up_one, d_down_one = rights_one
     mlp_sums, attn_sums = [None] * tensor, [None] * tensor
     mlp_moves, attn_moves = [None] * tensor, [None] * tensor
-    hooks = iter(range(4))
+    hooks = iter(range(5))
 
     def hook(*new):
         nonlocal d_down, d_up, d_attn
@@ -1016,13 +1097,15 @@
             d_down, d_up = own_layer(new[0], d_down_one), own_layer(new[1], d_up_one)
             mlp_sums[3] = mlp_leaves(3)
             mlp_sums[2] = mlp_leaves(2)
+            return (mlp_sums[3][0], mlp_sums[2][0])
+        if turn == 1:
             return (mlp_sums[3][1],)
-        if turn == 1:
+        if turn == 2:
             d_attn = own_layer(new[0], d_attn_one)
             mlp_moves[3] = moves_on(mlp_sums[3])
             mlp_sums[1] = mlp_leaves(1)
             return (mlp_sums[2][1], mlp_moves[3])
-        if turn == 2:
+        if turn == 3:
             mlp_moves[2] = moves_on(mlp_sums[2], mlp_moves[3])
             mlp_sums[0] = mlp_leaves(0)
             d_qkv = own_layer(new[0], d_qkv_one[1])
@@ -1040,41 +1123,44 @@
     attn_moves[3] = moves_on(attn_sums[3])
     attn_moves[2] = moves_on(attn_sums[2], attn_moves[3])
     attn_moves[1] = moves_on(attn_sums[1], attn_moves[2])
+    outputs = from_chip(lows, (attn_sums[3][0],))
     grads = from_chip(own_first(jnp.where(first, grad_zero, grad_one)).reshape(tensor, part, width))
 
-    def finished(name, piece, moved, spots, columns_out, rows_out):
-        size = piece[0].shape[1]
-        outs = (((wide_half // 2, size), jnp.float32),) * 2
-        space = pl.BlockSpec(memory_space=pltpu.VMEM)
-
-        def call(kernel, label, outs, *operands):
-            return pl.pallas_call(
-                kernel,
-                in_specs=[pl.BlockSpec(memory_space=pltpu.SMEM)] + [space] * len(operands),
-                out_specs=[space] * len(outs),
-                out_shape=[jax.ShapeDtypeStruct(shape, dtype) for shape, dtype in outs],
-                compiler_params=pltpu.CompilerParams(vmem_limit_bytes=ROWS_VMEM),
-                name=label,
-            )(core_word, *operands)
-
-        keep, send = call(last_sum_kernel, name + "_sum", outs, *piece, moved)
-        outs = (
-            ((wide_half // 2, columns_out), jnp.float32),
-            ((rows_out, wide_half // 2), jnp.float32),
-        )
-        kernel = functools.partial(joined_kernel, spots)
-        return call(kernel, name + "_join", outs, keep, flip_pairs(send, 1))
-
-    unit = units // tensor
-    up_grad, down_grad = finished(
-        "mlp", mlp_sums[0], mlp_moves[1], ((0, unit, 0),), 2 * unit, 2 * unit
+    block32 = ((wide_half // 2, unit), jnp.float32)
+    down32 = ((unit, wide_half // 2), jnp.float32)
+    up_keep, down_keep, up_send, down_send = with_core(
+        mlp_sum_kernel,
+        "mlp_sum",
+        core_word,
+        (block32, down32, block32, down32),
+        *mlp_sums[0],
+        mlp_moves[1],
+    )
+    outs = (
+        ((wide_half // 2, 2 * unit), jnp.float32),
+        ((2 * unit, wide_half // 2), jnp.float32),
+    )
+    sent = flip_pairs(up_send, 1), flip_pairs(down_send, 1)
+    up_grad, down_grad = with_core(
+        mlp_join_kernel, "mlp_join", core_word, outs, up_keep, down_keep, *sent
+    )
+    outs = (((wide_half // 2, 512), jnp.float32),) * 2
+    keep, send = with_core(
+        last_sum_kernel, "attn_sum", core_word, outs, *attn_sums[0], attn_moves[1]
     )
     spots = tuple((i * 128, (i + 1) * 128, i * 256) for i in range(3))
-    qkv_grad, out_grad = finished("attn", attn_sums[0], attn_moves[1], spots, 768, 256)
+    outs = (((wide_half // 2, 768), jnp.float32), ((256, wide_half // 2), jnp.float32))
+    kernel = functools.partial(joined_kernel, spots)
+    qkv_grad, out_grad = with_core(
+        kernel, "attn_join", core_word, outs, keep, flip_pairs(send, 1)
+    )
     qkv_grad = qkv_grad.reshape(wide_half // 2, 3, -1)
 
     gain_total = own_first(jnp.where(first, gain_zero, gain_one))
-    gains_grad = lax.psum_scatter(gain_total, ("dp", "tensor"), scatter_dimension=1, tiled=True)
+    count = tensor * lax.axis_size("dp")
+    gain_parts = gain_total.reshape(4, count, width // count).swapaxes(0, 1)
+    gain_parts = lax.all_to_all(gain_parts, ("dp", "tensor"), 0, 0, tiled=True)
+    gains_grad = jnp.sum(gain_parts, axis=0)
     return (
         outputs[None],
         grads[None],

time: 763 us -> 702 us (0.920)
  waiting for transfers between devices: 334 us -> 298 us
  local copies, waits for them, and re-layouts: 63.9 us -> 35.1 us
  starting transfers between devices: 72.9 us -> 97.1 us
  Pallas kernels: 214 us -> 194 us
  between operations: 15.9 us -> 3.2 us
  matrix products: 19 us -> 27.5 us
    unnamed x2 -> x0, waiting for transfers between devices: 49.1 us -> none
    pallas_call x32 -> x33, Pallas kernels: 125 us -> 97 us  [on_chip(): pl.pallas_call(without(kernel, len(operands), len(waits)), in_specs=[spac...]
    all_to_all x1, waiting for transfers between devices: 21.3 us -> 0.01 us  [to_chip(): lax.all_to_all(jnp.concatenate(ordered(mine, flip_pairs(other, 1))), 'ten...]
    unnamed x250 -> x288, local copies, waits for them, and re-layouts: 48.6 us -> 27.5 us
    ppermute x2, waiting for transfers between devices: 28.9 us -> 44.9 us  [shifted(): return lax.ppermute(block, axis, route)]
    ppermute x38 -> x42, waiting for transfers between devices: 123 us -> 139 us  [flip_pairs(): return lax.ppermute(block, 'dp', [(i, i ^ distance) for i in range(size)])]
    all_to_all x2, waiting for transfers between devices: 0.01 us -> 11.4 us  [from_chip(): spread_out = lax.all_to_all(block, 'tensor', 0, 0, tiled=True)]
    all_to_all x2, starting transfers between devices: 8.5 us -> 19 us  [from_chip(): spread_out = lax.all_to_all(block, 'tensor', 0, 0, tiled=True)]
  transfers between devices with their start and end apart: 56 -> 63, of which waited for: 30 -> 37; matrix products, arithmetic and copies ran while one was open for 9% -> 8% of each run, Pallas kernels for 13% -> 12%
where the time goes in v6:
time: 702 us; the launch traced here: 692 us
  waiting for transfers between devices  298 us (42%)
  Pallas kernels  194 us (28%)
  starting transfers between devices  97.1 us (14%)
  other arithmetic  38.4 us (5%)
  local copies, waits for them, and re-layouts  35.1 us (5%)
  matrix products  27.5 us (4%)
    ppermute x42, waiting for transfers between devices, flip_pairs(): return lax.ppermute(block, 'dp', [(i, i ^ distance) for i in range(size)])  139 us
    ppermute x15, waiting for transfers between devices, passed_on(): lax.ppermute(block, 'tensor', [(i, (i + step) % size) for i in range(size)])  103 us
    pallas_call x33, Pallas kernels, on_chip(): pl.pallas_call(without(kernel, len(operands), len(waits)), in_specs=[spac...  97 us
    pallas_call x6, Pallas kernels, by_pairs(): pl.pallas_call(without(functools.partial(kernel, len(pieces[0])), taken,...  83.8 us
    ppermute x2, waiting for transfers between devices, shifted(): return lax.ppermute(block, axis, route)  44.9 us
    ppermute x15, starting transfers between devices, passed_on(): lax.ppermute(block, 'tensor', [(i, (i + step) % size) for i in range(size)])  34.2 us
    unnamed x288, local copies, waits for them, and re-layouts  27.5 us
    dot_general x16, matrix products, contract(): lax.dot_general(left_rows, right_rows, (((0,), (0,)), ((), ())), preferre...  27.5 us
  transfers between devices with their start and end apart: 63, of which 37 were waited for; matrix products, arithmetic and copies ran while one was open for 8% of the time, Pallas kernels for 12%

profile of v6, /device:TPU:0, one launch (start us, length us, event | category | flops | bytes accessed | tf_op | source)
XLA Modules:
  0.0 692.5 jit_solution(11323363031665869054)
XLA Ops:
  11.0 6.2 all-to-all-start
  21.0 29.0 %collective-permute-done.1.refs_6_.refs_2_.refs_3_ = bf16[512,512]{1,0:T(8,128)(2,1)S(1)} collective-permute-done((bf16[512,512]{1,0:T(8,128)(2,1)S(1)}, bf16[512,512]{1,0:T(8,128)(2,1)S(1)}, u32[]{:S(2)}, u32[]{:S(2)}) %collective-permute-start.1) | collective-permute-done | bytes 524320 | tf_op jit(solution)/shard_map/ppermute | solution.py:760
  50.0 3.3 collective-permute-start.4
  55.3 9.4 %collective-permute-done.4.refs_2_.refs_7_.refs_3_.refs_5_.refs_4_ = bf16[512,512]{1,0:T(8,128)(2,1)S(1)} collective-permute-done((bf16[512,512]{1,0:T(8,128)(2,1)S(1)}, bf16[512,512]{1,0:T(8,128)(2,1)S(1)}, u32[]{:S(2)}, u32[]{:S(2)}) %collective-permute-start.4) | collective-permute-done | bytes 524320 | tf_op jit(solution)/shard_map/ppermute | solution.py:760
  68.1 2.7 norm_in.2.refs_3_
  74.8 4.7 collective-permute-done.6.refs_9_.refs_5_.refs_7_.refs_6_
  83.4 7.2 %collective-permute-done.7.refs_11_.refs_7_.refs_8_ = bf16[512,512]{1,0:T(8,128)(2,1)} collective-permute-done((bf16[512,512]{1,0:T(8,128)(2,1)S(1)}, bf16[512,512]{1,0:T(8,128)(2,1)}, u32[]{:S(2)}, u32[]{:S(2)}) %collective-permute-start.7) | collective-permute-done | bytes 524320 | tf_op jit(solution)/shard_map/ppermute | solution.py:755
  95.7 5.1 collective-permute-done.10.refs_14_.refs_2_.refs_4_
  101.8 11.2 %collective-permute-done.8.refs_12_.refs_8_.refs_9_ = bf16[512,512]{1,0:T(8,128)(2,1)S(1)} collective-permute-done((bf16[512,512]{1,0:T(8,128)(2,1)}, bf16[512,512]{1,0:T(8,128)(2,1)S(1)}, u32[]{:S(2)}, u32[]{:S(2)}) %collective-permute-start.8) | collective-permute-done | bytes 524320 | tf_op jit(solution)/shard_map/ppermute | solution.py:755
  113.1 17.1 %attend.2 = (bf16[4,1024,128]{2,1,0:T(8,128)(2,1)S(1)}, bf16[4,1024,128]{2,1,0:T(8,128)(2,1)S(1)}, bf16[4,1024,128]{2,1,0:T(8,128)(2,1)S(1)}, f32[4,2,1024]{2,1,0:T(2,128)S(1)}, bf16[1024,512]{1,0:T(8,128)(2,1)S(1)}) custom-call(s32[1]{0:T(128)} %bitcast.refs_0_, f32[1024,128]{1,0:T(8,128)S(1)} %pad_maximum_fusion.9.refs_1_, ...), custom_call_target="tpu_custom_call" | custom-call | flops 11811160064 | bytes 11567104 | tf_op jit(solution)/shard_map/attend/pallas_call | solution.py:685
  133.2 3.0 attn_out.2
  136.3 2.5 collective-permute-start.15
  140.9 11.9 %collective-permute-done.15.refs_4_.refs_3_.refs_5_ = bf16[512,512]{1,0:T(8,128)(2,1)S(1)} collective-permute-done((bf16[512,512]{1,0:T(8,128)(2,1)S(1)}, bf16[512,512]{1,0:T(8,128)(2,1)S(1)}, u32[]{:S(2)}, u32[]{:S(2)}) %collective-permute-start.15) | collective-permute-done | bytes 524320 | tf_op jit(solution)/shard_map/ppermute | solution.py:760
  153.6 10.5 %collective-permute-done.17.refs_6_.refs_8_ = bf16[512,512]{1,0:T(8,128)(2,1)S(1)} collective-permute-done((bf16[512,512]{1,0:T(8,128)(2,1)S(1)}, bf16[512,512]{1,0:T(8,128)(2,1)S(1)}, u32[]{:S(2)}, u32[]{:S(2)}) %collective-permute-start.17) | collective-permute-done | bytes 524320 | tf_op jit(solution)/shard_map/ppermute | solution.py:755
  164.1 3.4 after_attn.2
  171.7 12.2 %collective-permute-done.22.refs_4_.refs_6_ = bf16[512,512]{1,0:T(8,128)(2,1)S(1)} collective-permute-done((bf16[512,512]{1,0:T(8,128)(2,1)S(1)}, bf16[512,512]{1,0:T(8,128)(2,1)S(1)}, u32[]{:S(2)}, u32[]{:S(2)}) %collective-permute-start.22) | collective-permute-done | bytes 524320 | tf_op jit(solution)/shard_map/ppermute | solution.py:760
  185.4 8.7 %collective-permute-done.21.refs_9_.refs_8_ = bf16[512,512]{1,0:T(8,128)(2,1)S(1)} collective-permute-done((bf16[512,512]{1,0:T(8,128)(2,1)S(1)}, bf16[512,512]{1,0:T(8,128)(2,1)S(1)}, u32[]{:S(2)}, u32[]{:S(2)}) %collective-permute-start.21) | collective-permute-done | bytes 524320 | tf_op jit(solution)/shard_map/ppermute | solution.py:755
  194.1 7.8 %mlp_up.2 = (bf16[1024,2048]{1,0:T(8,128)(2,1)S(1)}, bf16[1024,2048]{1,0:T(8,128)(2,1)S(1)}) custom-call(bf16[512,1024]{1,0:T(8,128)(2,1)S(1)} %get-tuple-element.153.refs_0_, bf16[512,1024]{1,0:T(8,128)(2,1)S(1)} %collective-permute-done.19.refs_1_, bf16[512,512]{1,0:T(8,128)(2,1)S(1)} %get-tuple-element.109.refs_2_.refs_1_, ...), custom_call_target="tpu_custom_call" | custom-call | flops 4294967296 | bytes 14680064 | tf_op jit(solution)/shard_map/mlp_up/pallas_call | solution.py:667
  205.4 10.5 %collective-permute-done.24.refs_8_.refs_10_ = bf16[512,512]{1,0:T(8,128)(2,1)S(1)} collective-permute-done((bf16[512,512]{1,0:T(8,128)(2,1)S(1)}, bf16[512,512]{1,0:T(8,128)(2,1)S(1)}, u32[]{:S(2)}, u32[]{:S(2)}) %collective-permute-start.24) | collective-permute-done | bytes 524320 | tf_op jit(solution)/shard_map/ppermute | solution.py:755
  215.9 4.5 mlp_down.2
  220.5 2.6 collective-permute-done.25.refs_3_
  225.1 3.5 collective-permute-start.26
  228.6 22.2 %collective-permute-done.26.refs_1_ = bf16[512,1024]{1,0:T(8,128)(2,1)S(1)} collective-permute-done((bf16[512,1024]{1,0:T(8,128)(2,1)S(1)}, bf16[512,1024]{1,0:T(8,128)(2,1)S(1)}, u32[]{:S(2)}, u32[]{:S(2)}) %collective-permute-start.26) | collective-permute-done | bytes 1048608 | tf_op jit(solution)/shard_map/ppermute | solution.py:28
  252.7 2.6 collective-permute-done.27.refs_4_
  255.3 16.2 %attend.3 = (bf16[4,1024,128]{2,1,0:T(8,128)(2,1)S(1)}, bf16[4,1024,128]{2,1,0:T(8,128)(2,1)S(1)}, bf16[4,1024,128]{2,1,0:T(8,128)(2,1)S(1)}, f32[4,2,1024]{2,1,0:T(2,128)S(1)}, bf16[1024,512]{1,0:T(8,128)(2,1)S(1)}) custom-call(s32[1]{0:T(128)} %bitcast.refs_0_, f32[1024,128]{1,0:T(8,128)S(1)} %pad_maximum_fusion.9.refs_1_, ...), custom_call_target="tpu_custom_call" | custom-call | flops 11811160064 | bytes 11567104 | tf_op jit(solution)/shard_map/attend/pallas_call | solution.py:685
  273.6 3.0 attn_out.3
  279.3 3.4 after_attn.3
  285.6 7.7 %mlp_up.3 = (bf16[1024,2048]{1,0:T(8,128)(2,1)S(1)}, bf16[1024,2048]{1,0:T(8,128)(2,1)S(1)}) custom-call(bf16[512,1024]{1,0:T(8,128)(2,1)S(1)} %get-tuple-element.155.refs_0_, bf16[512,1024]{1,0:T(8,128)(2,1)S(1)} %collective-permute-done.29.refs_1_, bf16[512,512]{1,0:T(8,128)(2,1)S(1)} %copy-done.84, bf16[512,512]{1,0:T(8,128)(2,1)S(1)} %copy-done.88, ...), custom_call_target="tpu_custom_call" | custom-call | flops 4294967296 | bytes 14680064 | tf_op jit(solution)/shard_map/mlp_up/pallas_call | solution.py:667
  293.4 4.5 mlp_down.3
  307.7 4.5 mlp_up_back.2.refs_0_
  312.3 4.5 mlp_back.2
  319.6 4.0 into_attn_back.2
  326.4 12.7 %attend_back.4.refs_0_ = bf16[1024,768]{1,0:T(8,128)(2,1)S(1)} custom-call(s32[1]{0:T(128)} %bitcast.refs_0_, f32[1024,128]{1,0:T(8,128)S(1)} %copy-done.79, f32[1024,128]{1,0:T(8,128)S(1)} %pad_maximum_fusion.10.refs_2_, bf16[512,1024]{1,0:T(8,128)(2,1)S(1)} %get-tuple-element.135.refs_3_, bf16[512,1024]{1,0:T(8,128)(2,1)S(1)} %collective-permute-done.33.refs_4_, ...), custom_call_target="tpu_custom_call" | custom-call | flops 11274289152 | bytes 6815744 | tf_op jit(solution)/shard_map/attend_back/pallas_call | solution.py:685
  339.1 13.0 %attend_back.5.refs_1_ = bf16[1024,768]{1,0:T(8,128)(2,1)S(1)} custom-call(s32[1]{0:T(128)} %bitcast.refs_0_, f32[1024,128]{1,0:T(8,128)S(1)} %copy-done.79, f32[1024,128]{1,0:T(8,128)S(1)} %pad_maximum_fusion.10.refs_2_, bf16[512,1024]{1,0:T(8,128)(2,1)S(1)} %get-tuple-element.135.refs_3_, bf16[512,1024]{1,0:T(8,128)(2,1)S(1)} %collective-permute-done.33.refs_4_, ...), custom_call_target="tpu_custom_call" | custom-call | flops 11274289152 | bytes 6815744 | tf_op jit(solution)/shard_map/attend_back/pallas_call | solution.py:685
  352.1 5.4 attn_back.2
  360.2 3.1 out_of_layer.2
  368.1 22.7 %collective-permute-done.35.refs_1_ = bf16[512,1024]{1,0:T(8,128)(2,1)S(1)} collective-permute-done((bf16[512,1024]{1,0:T(8,128)(2,1)}, bf16[512,1024]{1,0:T(8,128)(2,1)S(1)}, u32[]{:S(2)}, u32[]{:S(2)}) %collective-permute-start.35) | collective-permute-done | bytes 1048608 | tf_op jit(solution)/shard_map/ppermute | solution.py:28
  396.6 4.5 mlp_up_back.3.refs_0_
  404.1 4.6 broadcast_select_fusion
  411.3 2.7 fusion.11.refs_0_
  422.0 4.5 mlp_back.3
  431.6 2.6 fusion.7.refs_0_
  434.2 18.5 %collective-permute-done.38.refs_6_ = bf16[1024,512]{1,0:T(8,128)(2,1)S(1)} collective-permute-done((bf16[1024,512]{1,0:T(8,128)(2,1)S(1)}, bf16[1024,512]{1,0:T(8,128)(2,1)S(1)}, u32[]{:S(2)}, u32[]{:S(2)}) %collective-permute-start.38) | collective-permute-done | bytes 1048608 | tf_op jit(solution)/shard_map/ppermute | solution.py:755
  452.7 4.0 into_attn_back.3
  458.1 3.5 collective-permute-start.41
  470.7 4.5 collective-permute-done.40.refs_13_
  475.2 8.7 %collective-permute-done.41.refs_14_ = bf16[1024,512]{1,0:T(8,128)(2,1)S(1)} collective-permute-done((bf16[1024,512]{1,0:T(8,128)(2,1)S(1)}, bf16[1024,512]{1,0:T(8,128)(2,1)S(1)}, u32[]{:S(2)}, u32[]{:S(2)}) %collective-permute-start.41) | collective-permute-done | bytes 1048608 | tf_op jit(solution)/shard_map/ppermute | solution.py:760
  483.9 12.6 %attend_back.6.refs_1_ = bf16[1024,768]{1,0:T(8,128)(2,1)S(1)} custom-call(s32[1]{0:T(128)} %bitcast.refs_0_, f32[1024,128]{1,0:T(8,128)S(1)} %copy-done.80, f32[1024,128]{1,0:T(8,128)S(1)} %copy-done.57, bf16[512,1024]{1,0:T(8,128)(2,1)S(1)} %get-tuple-element.167.refs_3_, bf16[512,1024]{1,0:T(8,128)(2,1)S(1)} %collective-permute-done.39.refs_4_, ...), custom_call_target="tpu_custom_call" | custom-call | flops 11274289152 | bytes 6815744 | tf_op jit(solution)/shard_map/attend_back/pallas_call | solution.py:685
  498.8 4.6 collective-permute-start.44
  509.6 21.7 %collective-permute-done.52 = bf16[512,512]{1,0:T(8,128)(2,1)S(1)} collective-permute-done((bf16[512,512]{1,0:T(8,128)(2,1)S(1)}, bf16[512,512]{1,0:T(8,128)(2,1)S(1)}, u32[]{:S(2)}, u32[]{:S(2)}) %collective-permute-start.52) | collective-permute-done | bytes 524320 | tf_op jit(solution)/shard_map/ppermute | solution.py:755
  532.3 3.5 collective-permute-start.53
  537.0 12.3 %attend_back.7.refs_0_ = bf16[1024,768]{1,0:T(8,128)(2,1)S(1)} custom-call(s32[1]{0:T(128)} %bitcast.refs_0_, f32[1024,128]{1,0:T(8,128)S(1)} %copy-done.80, f32[1024,128]{1,0:T(8,128)S(1)} %copy-done.57, bf16[512,1024]{1,0:T(8,128)(2,1)S(1)} %get-tuple-element.167.refs_3_, bf16[512,1024]{1,0:T(8,128)(2,1)S(1)} %collective-permute-done.39.refs_4_, ...), custom_call_target="tpu_custom_call" | custom-call | flops 11274289152 | bytes 6815744 | tf_op jit(solution)/shard_map/attend_back/pallas_call | solution.py:685
  549.3 19.7 %collective-permute-done.46.refs_11_.refs_3_ = bf16[1024,512]{1,0:T(8,128)(2,1)S(1)} collective-permute-done((bf16[1024,512]{1,0:T(8,128)(2,1)S(1)}, bf16[1024,512]{1,0:T(8,128)(2,1)S(1)}, u32[]{:S(2)}, u32[]{:S(2)}) %collective-permute-start.46) | collective-permute-done | bytes 1048608 | tf_op jit(solution)/shard_map/ppermute | solution.py:760
  569.0 6.1 attn_back.3
  577.8 5.8 all-to-all-start.1
  583.7 3.3 fusion.27.refs_1_
  589.3 3.8 collective-permute-start.54
  594.5 3.4 out_of_layer.3
  599.5 11.4 %all-to-all-done.1.refs_1_ = bf16[4,128,1024]{2,1,0:T(8,128)(2,1)} async-done(((bf16[4,128,1024]{2,1,0:T(8,128)(2,1)}), bf16[4,128,1024]{2,1,0:T(8,128)(2,1)}, u32[]{:S(2)}, u32[]{:S(2)}) %all-to-all-start.1) | async-done | bytes 1048608 | tf_op jit(solution)/shard_map/all_to_all | solution.py:906
  610.9 13.2 %all-to-all-start.2 = ((bf16[4,128,1024]{2,1,0:T(8,128)(2,1)}), bf16[4,128,1024]{2,1,0:T(8,128)(2,1)}, u32[]{:S(2)}, u32[]{:S(2)}) async-start(bf16[4,128,1024]{2,1,0:T(8,128)(2,1)} %bitcast.58), calls=%async_computation.2 | async-start | bytes 2097152 | tf_op jit(solution)/shard_map/all_to_all | solution.py:906
  632.0 9.7 %collective-permute-done.50 = bf16[512,512]{1,0:T(8,128)(2,1)S(1)} collective-permute-done((bf16[512,512]{1,0:T(8,128)(2,1)S(1)}, bf16[512,512]{1,0:T(8,128)(2,1)S(1)}, u32[]{:S(2)}, u32[]{:S(2)}) %collective-permute-start.50) | collective-permute-done | bytes 524320 | tf_op jit(solution)/shard_map/ppermute | solution.py:755
  643.0 3.9 collective-permute-start.55
  651.0 6.7 collective-permute-done.55.refs_3_
  671.2 5.9 all-to-all-start.3
  (491 shorter events, 176.8 us)
Async XLA Ops:
  6.8 2.1 collective-permute-start
  11.0 57.1 %all-to-all-start = ((bf16[4,128,1024]{2,1,0:T(8,128)(2,1)}), bf16[4,128,1024]{2,1,0:T(8,128)(2,1)S(1)}, u32[]{:S(2)}, u32[]{:S(2)}) async-start(bf16[4,128,1024]{2,1,0:T(8,128)(2,1)} %pad_maximum_fusion.8), calls=%async_computation | async-start | bytes 2097152 | tf_op jit(solution)/shard_map/all_to_all | solution.py:901
  18.9 333.2 %copy-start.4 = (bf16[512,512]{1,0:T(8,128)(2,1)}, bf16[512,512]{1,0:T(8,128)(2,1)S(1)}, u32[]{:S(2)}) copy-start(bf16[512,512]{1,0:T(8,128)(2,1)S(1)} %pad_maximum_fusion.11.refs_5_.refs_1_.refs_2_) | copy-start | bytes 1572868
  18.9 31.1 %collective-permute-start.1 = (bf16[512,512]{1,0:T(8,128)(2,1)S(1)}, bf16[512,512]{1,0:T(8,128)(2,1)S(1)}, u32[]{:S(2)}, u32[]{:S(2)}) collective-permute-start(bf16[512,512]{1,0:T(8,128)(2,1)S(1)} %pad_maximum_fusion.11.refs_5_.refs_1_.refs_2_), channel_id=1, source_target_pairs={{0,1},{1,2},{2,3},{3,0},{4,5},{5,6},{6,7},{7,4},{8,9},{9,10},{10,1... | collective-permute-start | bytes 1572872 | tf_op jit(solution)/shard_map/ppermute | solution.py:760
  50.0 14.7 %collective-permute-start.4 = (bf16[512,512]{1,0:T(8,128)(2,1)S(1)}, bf16[512,512]{1,0:T(8,128)(2,1)S(1)}, u32[]{:S(2)}, u32[]{:S(2)}) collective-permute-start(bf16[512,512]{1,0:T(8,128)(2,1)S(1)} %collective-permute-done.1.refs_6_.refs_2_.refs_3_), channel_id=1, source_target_pairs={{0,1},{1,2},{2,3},{3,0},{4,5},{5,6},{6,7},{7,4},{8,9},{9,10},{10,1... | collective-permute-start | bytes 1572872 | tf_op jit(solution)/shard_map/ppermute | solution.py:760
  53.2 14.9 %collective-permute-start.2 = (bf16[512,512]{1,0:T(8,128)(2,1)S(1)}, bf16[512,512]{1,0:T(8,128)(2,1)S(1)}, u32[]{:S(2)}, u32[]{:S(2)}) collective-permute-start(bf16[512,512]{1,0:T(8,128)(2,1)S(1)} %collective-permute-done.1.refs_6_.refs_2_.refs_3_), channel_id=1, source_target_pairs={{0,8},{4,12},{8,0},{12,4},{1,9},{5,13},{9,1},{13,5},{2,10},{6,14},... | collective-permute-start | bytes 1572872 | tf_op jit(solution)/shard_map/ppermute | solution.py:755
  54.8 24.7 %collective-permute-start.6 = (bf16[512,512]{1,0:T(8,128)(2,1)S(1)}, bf16[512,512]{1,0:T(8,128)(2,1)}, u32[]{:S(2)}, u32[]{:S(2)}) collective-permute-start(bf16[512,512]{1,0:T(8,128)(2,1)S(1)} %pad_maximum_fusion.11.refs_5_.refs_1_.refs_2_), channel_id=1, source_target_pairs={{0,8},{4,12},{8,0},{12,4},{1,9},{5,13},{9,1},{13,5},{2,10},{6,14},... | collective-permute-start | bytes 1572872 | tf_op jit(solution)/shard_map/ppermute | solution.py:755
  64.7 16.3 %collective-permute-start.5 = (bf16[512,512]{1,0:T(8,128)(2,1)S(1)}, bf16[512,512]{1,0:T(8,128)(2,1)}, u32[]{:S(2)}, u32[]{:S(2)}) collective-permute-start(bf16[512,512]{1,0:T(8,128)(2,1)S(1)} %collective-permute-done.4.refs_2_.refs_7_.refs_3_.refs_5_.refs_4_), channel_id=1, source_target_pairs={{0,1},{1,2},{2,3},{3,0},{4,5},{5,6},{6,7},{7,4},{8,9},{9,10},{10,1... | collective-permute-start | bytes 1572872 | tf_op jit(solution)/shard_map/ppermute | solution.py:760
  66.1 24.6 %collective-permute-start.7 = (bf16[512,512]{1,0:T(8,128)(2,1)S(1)}, bf16[512,512]{1,0:T(8,128)(2,1)}, u32[]{:S(2)}, u32[]{:S(2)}) collective-permute-start(bf16[512,512]{1,0:T(8,128)(2,1)S(1)} %collective-permute-done.4.refs_2_.refs_7_.refs_3_.refs_5_.refs_4_), channel_id=1, source_target_pairs={{0,8},{4,12},{8,0},{12,4},{1,9},{5,13},{9,1},{13,5},{2,10},{6,14},... | collective-permute-start | bytes 1572872 | tf_op jit(solution)/shard_map/ppermute | solution.py:755
  70.8 42.2 %collective-permute-start.3 = (bf16[512,1024]{1,0:T(8,128)(2,1)}, bf16[512,1024]{1,0:T(8,128)(2,1)}, u32[]{:S(2)}, u32[]{:S(2)}) collective-permute-start(bf16[512,1024]{1,0:T(8,128)(2,1)} %norm_in.2.refs_3_), channel_id=1, source_target_pairs={{0,4},{4,0},{8,12},{12,8},{1,5},{5,1},{9,13},{13,9},{2,6},{6,2},{1... | collective-permute-start | bytes 3145736 | tf_op jit(solution)/shard_map/ppermute | solution.py:755
  72.2 22.9 %collective-permute-start.9 = (bf16[512,512]{1,0:T(8,128)(2,1)S(1)}, bf16[512,512]{1,0:T(8,128)(2,1)S(1)}, u32[]{:S(2)}, u32[]{:S(2)}) collective-permute-start(bf16[512,512]{1,0:T(8,128)(2,1)S(1)} %get-tuple-element.109.refs_2_.refs_1_), channel_id=1, source_target_pairs={{0,1},{1,2},{2,3},{3,0},{4,5},{5,6},{6,7},{7,4},{8,9},{9,10},{10,1... | collective-permute-start | bytes 1572872 | tf_op jit(solution)/shard_map/ppermute | solution.py:760
  79.4 22.4 %collective-permute-start.11 = (bf16[512,512]{1,0:T(8,128)(2,1)S(1)}, bf16[512,512]{1,0:T(8,128)(2,1)S(1)}, u32[]{:S(2)}, u32[]{:S(2)}) collective-permute-start(bf16[512,512]{1,0:T(8,128)(2,1)S(1)} %get-tuple-element.109.refs_2_.refs_1_), channel_id=1, source_target_pairs={{0,8},{4,12},{8,0},{12,4},{1,9},{5,13},{9,1},{13,5},{2,10},{6,14},... | collective-permute-start | bytes 1572872 | tf_op jit(solution)/shard_map/ppermute | solution.py:755
  81.0 19.8 %collective-permute-start.10 = (bf16[512,512]{1,0:T(8,128)(2,1)S(1)}, bf16[512,512]{1,0:T(8,128)(2,1)S(1)}, u32[]{:S(2)}, u32[]{:S(2)}) collective-permute-start(bf16[512,512]{1,0:T(8,128)(2,1)S(1)} %get-tuple-element.110.refs_1_.refs_3_), channel_id=1, source_target_pairs={{0,1},{1,2},{2,3},{3,0},{4,5},{5,6},{6,7},{7,4},{8,9},{9,10},{10,1... | collective-permute-start | bytes 1572872 | tf_op jit(solution)/shard_map/ppermute | solution.py:760
  90.7 22.4 %collective-permute-start.8 = (bf16[512,512]{1,0:T(8,128)(2,1)}, bf16[512,512]{1,0:T(8,128)(2,1)S(1)}, u32[]{:S(2)}, u32[]{:S(2)}) collective-permute-start(bf16[512,512]{1,0:T(8,128)(2,1)} %collective-permute-done.5.refs_8_.refs_4_.refs_6_.refs_5_), channel_id=1, source_target_pairs={{0,8},{4,12},{8,0},{12,4},{1,9},{5,13},{9,1},{13,5},{2,10},{6,14},... | collective-permute-start | bytes 1572872 | tf_op jit(solution)/shard_map/ppermute | solution.py:755
  95.1 38.0 %collective-permute-start.13 = (bf16[512,512]{1,0:T(8,128)(2,1)S(1)}, bf16[512,512]{1,0:T(8,128)(2,1)S(1)}, u32[]{:S(2)}, u32[]{:S(2)}) collective-permute-start(bf16[512,512]{1,0:T(8,128)(2,1)S(1)} %get-tuple-element.110.refs_1_.refs_3_), channel_id=1, source_target_pairs={{0,8},{4,12},{8,0},{12,4},{1,9},{5,13},{9,1},{13,5},{2,10},{6,14},... | collective-permute-start | bytes 1572872 | tf_op jit(solution)/shard_map/ppermute | solution.py:755
  100.8 32.3 %collective-permute-start.12 = (bf16[512,512]{1,0:T(8,128)(2,1)S(1)}, bf16[512,512]{1,0:T(8,128)(2,1)S(1)}, u32[]{:S(2)}, u32[]{:S(2)}) collective-permute-start(bf16[512,512]{1,0:T(8,128)(2,1)S(1)} %collective-permute-done.9.refs_13_.refs_3_.refs_2_), channel_id=1, source_target_pairs={{0,1},{1,2},{2,3},{3,0},{4,5},{5,6},{6,7},{7,4},{8,9},{9,10},{10,1... | collective-permute-start | bytes 1572872 | tf_op jit(solution)/shard_map/ppermute | solution.py:760
  136.2 27.9 %collective-permute-start.14 = (bf16[512,1024]{1,0:T(8,128)(2,1)S(1)}, bf16[512,1024]{1,0:T(8,128)(2,1)S(1)}, u32[]{:S(2)}, u32[]{:S(2)}) collective-permute-start(bf16[512,1024]{1,0:T(8,128)(2,1)S(1)} %get-tuple-element.113), channel_id=1, source_target_pairs={{0,4},{4,0},{8,12},{12,8},{1,5},{5,1},{9,13},{13,9},{2,6},{6,2},{1... | collective-permute-start | bytes 3145736 | tf_op jit(solution)/shard_map/ppermute | solution.py:755
  136.3 16.6 %collective-permute-start.15 = (bf16[512,512]{1,0:T(8,128)(2,1)S(1)}, bf16[512,512]{1,0:T(8,128)(2,1)S(1)}, u32[]{:S(2)}, u32[]{:S(2)}) collective-permute-start(bf16[512,512]{1,0:T(8,128)(2,1)S(1)} %collective-permute-done.10.refs_14_.refs_2_.refs_4_), channel_id=1, source_target_pairs={{0,1},{1,2},{2,3},{3,0},{4,5},{5,6},{6,7},{7,4},{8,9},{9,10},{10,1... | collective-permute-start | bytes 1572872 | tf_op jit(solution)/shard_map/ppermute | solution.py:760
  138.8 14.8 %collective-permute-start.16 = (bf16[512,512]{1,0:T(8,128)(2,1)S(1)}, bf16[512,512]{1,0:T(8,128)(2,1)S(1)}, u32[]{:S(2)}, u32[]{:S(2)}) collective-permute-start(bf16[512,512]{1,0:T(8,128)(2,1)S(1)} %collective-permute-done.9.refs_13_.refs_3_.refs_2_), channel_id=1, source_target_pairs={{0,8},{4,12},{8,0},{12,4},{1,9},{5,13},{9,1},{13,5},{2,10},{6,14},... | collective-permute-start | bytes 1572872 | tf_op jit(solution)/shard_map/ppermute | solution.py:755
  140.4 23.7 %collective-permute-start.17 = (bf16[512,512]{1,0:T(8,128)(2,1)S(1)}, bf16[512,512]{1,0:T(8,128)(2,1)S(1)}, u32[]{:S(2)}, u32[]{:S(2)}) collective-permute-start(bf16[512,512]{1,0:T(8,128)(2,1)S(1)} %collective-permute-done.10.refs_14_.refs_2_.refs_4_), channel_id=1, source_target_pairs={{0,8},{4,12},{8,0},{12,4},{1,9},{5,13},{9,1},{13,5},{2,10},{6,14},... | collective-permute-start | bytes 1572872 | tf_op jit(solution)/shard_map/ppermute | solution.py:755
  140.8 23.2 %collective-permute-start.18 = (bf16[512,512]{1,0:T(8,128)(2,1)S(1)}, bf16[512,512]{1,0:T(8,128)(2,1)S(1)}, u32[]{:S(2)}, u32[]{:S(2)}) collective-permute-start(bf16[512,512]{1,0:T(8,128)(2,1)S(1)} %collective-permute-done.12.refs_9_.refs_4_.refs_3_), channel_id=1, source_target_pairs={{0,1},{1,2},{2,3},{3,0},{4,5},{5,6},{6,7},{7,4},{8,9},{9,10},{10,1... | collective-permute-start | bytes 1572872 | tf_op jit(solution)/shard_map/ppermute | solution.py:760
  167.5 26.6 %collective-permute-start.19 = (bf16[512,1024]{1,0:T(8,128)(2,1)S(1)}, bf16[512,1024]{1,0:T(8,128)(2,1)S(1)}, u32[]{:S(2)}, u32[]{:S(2)}) collective-permute-start(bf16[512,1024]{1,0:T(8,128)(2,1)S(1)} %get-tuple-element.153.refs_0_), channel_id=1, source_target_pairs={{0,4},{4,0},{8,12},{12,8},{1,5},{5,1},{9,13},{13,9},{2,6},{6,2},{1... | collective-permute-start | bytes 3145736 | tf_op jit(solution)/shard_map/ppermute | solution.py:755
  167.6 16.3 %collective-permute-start.22 = (bf16[512,512]{1,0:T(8,128)(2,1)S(1)}, bf16[512,512]{1,0:T(8,128)(2,1)S(1)}, u32[]{:S(2)}, u32[]{:S(2)}) collective-permute-start(bf16[512,512]{1,0:T(8,128)(2,1)S(1)} %collective-permute-done.15.refs_4_.refs_3_.refs_5_), channel_id=1, source_target_pairs={{0,1},{1,2},{2,3},{3,0},{4,5},{5,6},{6,7},{7,4},{8,9},{9,10},{10,1... | collective-permute-start | bytes 1572872 | tf_op jit(solution)/shard_map/ppermute | solution.py:760
  168.1 17.3 %collective-permute-start.20 = (bf16[512,512]{1,0:T(8,128)(2,1)S(1)}, bf16[512,512]{1,0:T(8,128)(2,1)S(1)}, u32[]{:S(2)}, u32[]{:S(2)}) collective-permute-start(bf16[512,512]{1,0:T(8,128)(2,1)S(1)} %collective-permute-done.12.refs_9_.refs_4_.refs_3_), channel_id=1, source_target_pairs={{0,8},{4,12},{8,0},{12,4},{1,9},{5,13},{9,1},{13,5},{2,10},{6,14},... | collective-permute-start | bytes 1572872 | tf_op jit(solution)/shard_map/ppermute | solution.py:755
  169.6 24.5 %collective-permute-start.21 = (bf16[512,512]{1,0:T(8,128)(2,1)S(1)}, bf16[512,512]{1,0:T(8,128)(2,1)S(1)}, u32[]{:S(2)}, u32[]{:S(2)}) collective-permute-start(bf16[512,512]{1,0:T(8,128)(2,1)S(1)} %collective-permute-done.18.refs_7_.refs_5_.refs_4_), channel_id=1, source_target_pairs={{0,8},{4,12},{8,0},{12,4},{1,9},{5,13},{9,1},{13,5},{2,10},{6,14},... | collective-permute-start | bytes 1572872 | tf_op jit(solution)/shard_map/ppermute | solution.py:755
  170.1 35.2 %collective-permute-start.23 = (bf16[512,512]{1,0:T(8,128)(2,1)S(1)}, bf16[512,512]{1,0:T(8,128)(2,1)S(1)}, u32[]{:S(2)}, u32[]{:S(2)}) collective-permute-start(bf16[512,512]{1,0:T(8,128)(2,1)S(1)} %collective-permute-done.15.refs_4_.refs_3_.refs_5_), channel_id=1, source_target_pairs={{0,8},{4,12},{8,0},{12,4},{1,9},{5,13},{9,1},{13,5},{2,10},{6,14},... | collective-permute-start | bytes 1572872 | tf_op jit(solution)/shard_map/ppermute | solution.py:755
  183.9 32.0 %collective-permute-start.24 = (bf16[512,512]{1,0:T(8,128)(2,1)S(1)}, bf16[512,512]{1,0:T(8,128)(2,1)S(1)}, u32[]{:S(2)}, u32[]{:S(2)}) collective-permute-start(bf16[512,512]{1,0:T(8,128)(2,1)S(1)} %collective-permute-done.22.refs_4_.refs_6_), channel_id=1, source_target_pairs={{0,8},{4,12},{8,0},{12,4},{1,9},{5,13},{9,1},{13,5},{2,10},{6,14},... | collective-permute-start | bytes 1572872 | tf_op jit(solution)/shard_map/ppermute | solution.py:755
  220.4 2.7 collective-permute-start.25
  225.1 25.8 %collective-permute-start.26 = (bf16[512,1024]{1,0:T(8,128)(2,1)S(1)}, bf16[512,1024]{1,0:T(8,128)(2,1)S(1)}, u32[]{:S(2)}, u32[]{:S(2)}) collective-permute-start(bf16[512,1024]{1,0:T(8,128)(2,1)S(1)} %get-tuple-element.144), channel_id=1, source_target_pairs={{0,16},{1,17},{2,18},{3,19},{4,20},{5,21},{6,22},{7,23},{8,24},{9,... | collective-permute-start | bytes 3145736 | tf_op jit(solution)/shard_map/ppermute | solution.py:28
  252.6 2.7 collective-permute-start.27
  276.6 2.7 collective-permute-start.28
  282.8 2.7 collective-permute-start.29
  297.9 2.7 collective-permute-start.30
  304.9 2.7 collective-permute-start.31
  316.9 2.7 collective-permute-start.32
  323.6 2.7 collective-permute-start.33
  357.5 2.7 collective-permute-start.34
  363.4 27.4 %collective-permute-start.35 = (bf16[512,1024]{1,0:T(8,128)(2,1)}, bf16[512,1024]{1,0:T(8,128)(2,1)S(1)}, u32[]{:S(2)}, u32[]{:S(2)}) collective-permute-start(bf16[512,1024]{1,0:T(8,128)(2,1)} %get-tuple-element.143), channel_id=1, source_target_pairs={{16,0},{17,1},{18,2},{19,3},{20,4},{21,5},{22,6},{23,7},{24,8},{25... | collective-permute-start | bytes 3145736 | tf_op jit(solution)/shard_map/ppermute | solution.py:28
  393.4 2.7 collective-permute-start.36
  426.5 7.7 %collective-permute-start.37 = (bf16[512,1024]{1,0:T(8,128)(2,1)S(1)}, bf16[512,1024]{1,0:T(8,128)(2,1)S(1)}, u32[]{:S(2)}, u32[]{:S(2)}) collective-permute-start(bf16[512,1024]{1,0:T(8,128)(2,1)S(1)} %get-tuple-element.164), channel_id=1, source_target_pairs={{0,4},{4,0},{8,12},{12,8},{1,5},{5,1},{9,13},{13,9},{2,6},{6,2},{1... | collective-permute-start | bytes 3145736 | tf_op jit(solution)/shard_map/ppermute | solution.py:755
  426.6 26.0 %collective-permute-start.38 = (bf16[1024,512]{1,0:T(8,128)(2,1)S(1)}, bf16[1024,512]{1,0:T(8,128)(2,1)S(1)}, u32[]{:S(2)}, u32[]{:S(2)}) collective-permute-start(bf16[1024,512]{1,0:T(8,128)(2,1)S(1)} %get-tuple-element.166), channel_id=1, source_target_pairs={{0,8},{4,12},{8,0},{12,4},{1,9},{5,13},{9,1},{13,5},{2,10},{6,14},... | collective-permute-start | bytes 3145736 | tf_op jit(solution)/shard_map/ppermute | solution.py:755
  431.0 44.1 %collective-permute-start.40 = (bf16[1024,512]{1,0:T(8,128)(2,1)S(1)}, bf16[1024,512]{1,0:T(8,128)(2,1)S(1)}, u32[]{:S(2)}, u32[]{:S(2)}) collective-permute-start(bf16[1024,512]{1,0:T(8,128)(2,1)S(1)} %get-tuple-element.172), channel_id=1, source_target_pairs={{0,8},{4,12},{8,0},{12,4},{1,9},{5,13},{9,1},{13,5},{2,10},{6,14},... | collective-permute-start | bytes 3145736 | tf_op jit(solution)/shard_map/ppermute | solution.py:755
  456.7 18.4 %collective-permute-start.39 = (bf16[512,1024]{1,0:T(8,128)(2,1)S(1)}, bf16[512,1024]{1,0:T(8,128)(2,1)S(1)}, u32[]{:S(2)}, u32[]{:S(2)}) collective-permute-start(bf16[512,1024]{1,0:T(8,128)(2,1)S(1)} %get-tuple-element.167.refs_3_), channel_id=1, source_target_pairs={{0,4},{4,0},{8,12},{12,8},{1,5},{5,1},{9,13},{13,9},{2,6},{6,2},{1... | collective-permute-start | bytes 3145736 | tf_op jit(solution)/shard_map/ppermute | solution.py:755
  458.1 25.8 %collective-permute-start.41 = (bf16[1024,512]{1,0:T(8,128)(2,1)S(1)}, bf16[1024,512]{1,0:T(8,128)(2,1)S(1)}, u32[]{:S(2)}, u32[]{:S(2)}) collective-permute-start(bf16[1024,512]{1,0:T(8,128)(2,1)S(1)} %add_convert_fusion.2), channel_id=1, source_target_pairs={{0,3},{1,0},{2,1},{3,2},{4,7},{5,4},{6,5},{7,6},{8,11},{9,8},{10,9... | collective-permute-start | bytes 3145736 | tf_op jit(solution)/shard_map/ppermute | solution.py:760
  463.1 72.7 %collective-permute-start.43 = (bf16[1024,512]{1,0:T(8,128)(2,1)S(1)}, bf16[1024,512]{1,0:T(8,128)(2,1)S(1)}, u32[]{:S(2)}, u32[]{:S(2)}) collective-permute-start(bf16[1024,512]{1,0:T(8,128)(2,1)S(1)} %get-tuple-element.176), channel_id=1, source_target_pairs={{0,8},{4,12},{8,0},{12,4},{1,9},{5,13},{9,1},{13,5},{2,10},{6,14},... | collective-permute-start | bytes 3145736 | tf_op jit(solution)/shard_map/ppermute | solution.py:755
  470.2 79.2 %collective-permute-start.45 = (bf16[1024,512]{1,0:T(8,128)(2,1)S(1)}, bf16[1024,512]{1,0:T(8,128)(2,1)S(1)}, u32[]{:S(2)}, u32[]{:S(2)}) collective-permute-start(bf16[1024,512]{1,0:T(8,128)(2,1)S(1)} %get-tuple-element.177), channel_id=1, source_target_pairs={{0,8},{4,12},{8,0},{12,4},{1,9},{5,13},{9,1},{13,5},{2,10},{6,14},... | collective-permute-start | bytes 3145736 | tf_op jit(solution)/shard_map/ppermute | solution.py:755
  498.8 37.1 %collective-permute-start.44 = (bf16[1024,512]{1,0:T(8,128)(2,1)S(1)}, bf16[1024,512]{1,0:T(8,128)(2,1)S(1)}, u32[]{:S(2)}, u32[]{:S(2)}) collective-permute-start(bf16[1024,512]{1,0:T(8,128)(2,1)S(1)} %add_convert_fusion.1), channel_id=1, source_target_pairs={{0,3},{1,0},{2,1},{3,2},{4,7},{5,4},{6,5},{7,6},{8,11},{9,8},{10,9... | collective-permute-start | bytes 3145736 | tf_op jit(solution)/shard_map/ppermute | solution.py:760
  504.5 26.9 %collective-permute-start.52 = (bf16[512,512]{1,0:T(8,128)(2,1)S(1)}, bf16[512,512]{1,0:T(8,128)(2,1)S(1)}, u32[]{:S(2)}, u32[]{:S(2)}) collective-permute-start(bf16[512,512]{1,0:T(8,128)(2,1)S(1)} %get-tuple-element.199), channel_id=1, source_target_pairs={{0,8},{4,12},{8,0},{12,4},{1,9},{5,13},{9,1},{13,5},{2,10},{6,14},... | collective-permute-start | bytes 1572872 | tf_op jit(solution)/shard_map/ppermute | solution.py:755
  509.1 77.9 %collective-permute-start.51 = (bf16[512,512]{1,0:T(8,128)(2,1)}, bf16[512,512]{1,0:T(8,128)(2,1)}, u32[]{:S(2)}, u32[]{:S(2)}) collective-permute-start(bf16[512,512]{1,0:T(8,128)(2,1)} %get-tuple-element.198), channel_id=1, source_target_pairs={{0,8},{4,12},{8,0},{12,4},{1,9},{5,13},{9,1},{13,5},{2,10},{6,14},... | collective-permute-start | bytes 1572872 | tf_op jit(solution)/shard_map/ppermute | solution.py:755
  532.3 54.7 %collective-permute-start.53 = (bf16[512,512]{1,0:T(8,128)(2,1)}, bf16[512,512]{1,0:T(8,128)(2,1)}, u32[]{:S(2)}, u32[]{:S(2)}) collective-permute-start(bf16[512,512]{1,0:T(8,128)(2,1)} %add_convert_fusion.5), channel_id=1, source_target_pairs={{0,3},{1,0},{2,1},{3,2},{4,7},{5,4},{6,5},{7,6},{8,11},{9,8},{10,9... | collective-permute-start | bytes 1572872 | tf_op jit(solution)/shard_map/ppermute | solution.py:760
  536.3 32.7 %collective-permute-start.46 = (bf16[1024,512]{1,0:T(8,128)(2,1)S(1)}, bf16[1024,512]{1,0:T(8,128)(2,1)S(1)}, u32[]{:S(2)}, u32[]{:S(2)}) collective-permute-start(bf16[1024,512]{1,0:T(8,128)(2,1)S(1)} %add_convert_fusion), channel_id=1, source_target_pairs={{0,3},{1,0},{2,1},{3,2},{4,7},{5,4},{6,5},{7,6},{8,11},{9,8},{10,9... | collective-permute-start | bytes 3145736 | tf_op jit(solution)/shard_map/ppermute | solution.py:760
  576.5 18.0 %collective-permute-start.47 = (bf16[512,1024]{1,0:T(8,128)(2,1)}, bf16[512,1024]{1,0:T(8,128)(2,1)}, u32[]{:S(2)}, u32[]{:S(2)}) collective-permute-start(bf16[512,1024]{1,0:T(8,128)(2,1)} %get-tuple-element.180), channel_id=1, source_target_pairs={{0,4},{4,0},{8,12},{12,8},{1,5},{5,1},{9,13},{13,9},{2,6},{6,2},{1... | collective-permute-start | bytes 3145736 | tf_op jit(solution)/shard_map/ppermute | solution.py:755
  577.8 33.0 %all-to-all-start.1 = ((bf16[4,128,1024]{2,1,0:T(8,128)(2,1)}), bf16[4,128,1024]{2,1,0:T(8,128)(2,1)}, u32[]{:S(2)}, u32[]{:S(2)}) async-start(bf16[4,128,1024]{2,1,0:T(8,128)(2,1)} %bitcast.59), calls=%async_computation.1 | async-start | bytes 2097152 | tf_op jit(solution)/shard_map/all_to_all | solution.py:906
  589.3 42.6 %collective-permute-start.54 = (bf16[512,512]{1,0:T(8,128)(2,1)}, bf16[512,512]{1,0:T(8,128)(2,1)}, u32[]{:S(2)}, u32[]{:S(2)}) collective-permute-start(bf16[512,512]{1,0:T(8,128)(2,1)} %add_convert_fusion.4), channel_id=1, source_target_pairs={{0,3},{1,0},{2,1},{3,2},{4,7},{5,4},{6,5},{7,6},{8,11},{9,8},{10,9... | collective-permute-start | bytes 1572872 | tf_op jit(solution)/shard_map/ppermute | solution.py:760
  610.9 50.4 %all-to-all-start.2 = ((bf16[4,128,1024]{2,1,0:T(8,128)(2,1)}), bf16[4,128,1024]{2,1,0:T(8,128)(2,1)}, u32[]{:S(2)}, u32[]{:S(2)}) async-start(bf16[4,128,1024]{2,1,0:T(8,128)(2,1)} %bitcast.58), calls=%async_computation.2 | async-start | bytes 2097152 | tf_op jit(solution)/shard_map/all_to_all | solution.py:906
  626.8 14.9 %collective-permute-start.50 = (bf16[512,512]{1,0:T(8,128)(2,1)S(1)}, bf16[512,512]{1,0:T(8,128)(2,1)S(1)}, u32[]{:S(2)}, u32[]{:S(2)}) collective-permute-start(bf16[512,512]{1,0:T(8,128)(2,1)S(1)} %get-tuple-element.196), channel_id=1, source_target_pairs={{0,8},{4,12},{8,0},{12,4},{1,9},{5,13},{9,1},{13,5},{2,10},{6,14},... | collective-permute-start | bytes 1572872 | tf_op jit(solution)/shard_map/ppermute | solution.py:755
  630.5 20.5 %collective-permute-start.49 = (bf16[512,512]{1,0:T(8,128)(2,1)S(1)}, bf16[512,512]{1,0:T(8,128)(2,1)S(1)}, u32[]{:S(2)}, u32[]{:S(2)}) collective-permute-start(bf16[512,512]{1,0:T(8,128)(2,1)S(1)} %get-tuple-element.194), channel_id=1, source_target_pairs={{0,8},{4,12},{8,0},{12,4},{1,9},{5,13},{9,1},{13,5},{2,10},{6,14},... | collective-permute-start | bytes 1572872 | tf_op jit(solution)/shard_map/ppermute | solution.py:755
  643.0 14.7 %collective-permute-start.55 = (bf16[512,512]{1,0:T(8,128)(2,1)S(1)}, bf16[512,512]{1,0:T(8,128)(2,1)S(1)}, u32[]{:S(2)}, u32[]{:S(2)}) collective-permute-start(bf16[512,512]{1,0:T(8,128)(2,1)S(1)} %add_convert_fusion.3), channel_id=1, source_target_pairs={{0,3},{1,0},{2,1},{3,2},{4,7},{5,4},{6,5},{7,6},{8,11},{9,8},{10,9... | collective-permute-start | bytes 1572872 | tf_op jit(solution)/shard_map/ppermute | solution.py:760
  648.9 28.2 %collective-permute-start.42 = (bf16[2,128,1024]{2,1,0:T(8,128)(2,1)}, bf16[2,128,1024]{2,1,0:T(8,128)(2,1)S(1)}, u32[]{:S(2)}, u32[]{:S(2)}) collective-permute-start(bf16[2,128,1024]{2,1,0:T(8,128)(2,1)} %get-tuple-element.175), channel_id=1, source_target_pairs={{0,4},{4,0},{8,12},{12,8},{1,5},{5,1},{9,13},{13,9},{2,6},{6,2},{1... | collective-permute-start | bytes 1572872 | tf_op jit(solution)/shard_map/ppermute | solution.py:755
  658.6 19.6 %collective-permute-start.56 = (f32[256,512]{1,0:T(8,128)}, f32[256,512]{1,0:T(8,128)}, u32[]{:S(2)}, u32[]{:S(2)}) collective-permute-start(f32[256,512]{1,0:T(8,128)} %get-tuple-element.201), channel_id=1, source_target_pairs={{0,4},{4,0},{8,12},{12,8},{1,5},{5,1},{9,13},{13,9},{2,6},{6,2},{1... | collective-permute-start | bytes 1572872 | tf_op jit(solution)/shard_map/ppermute | solution.py:755
  660.7 22.9 %collective-permute-start.57 = (f32[256,512]{1,0:T(8,128)}, f32[256,512]{1,0:T(8,128)S(1)}, u32[]{:S(2)}, u32[]{:S(2)}) collective-permute-start(f32[256,512]{1,0:T(8,128)} %get-tuple-element.207), channel_id=1, source_target_pairs={{0,4},{4,0},{8,12},{12,8},{1,5},{5,1},{9,13},{13,9},{2,6},{6,2},{1... | collective-permute-start | bytes 1572872 | tf_op jit(solution)/shard_map/ppermute | solution.py:755
  661.2 23.2 %collective-permute-start.58 = (f32[512,256]{1,0:T(8,128)}, f32[512,256]{1,0:T(8,128)}, u32[]{:S(2)}, u32[]{:S(2)}) collective-permute-start(f32[512,256]{1,0:T(8,128)} %get-tuple-element.208), channel_id=1, source_target_pairs={{0,4},{4,0},{8,12},{12,8},{1,5},{5,1},{9,13},{13,9},{2,6},{6,2},{1... | collective-permute-start | bytes 1572872 | tf_op jit(solution)/shard_map/ppermute | solution.py:755
  663.3 27.7 %collective-permute-start.48 = (bf16[2,128,1024]{2,1,0:T(8,128)(2,1)}, bf16[2,128,1024]{2,1,0:T(8,128)(2,1)S(1)}, u32[]{:S(2)}, u32[]{:S(2)}) collective-permute-start(bf16[2,128,1024]{2,1,0:T(8,128)(2,1)} %get-tuple-element.184), channel_id=1, source_target_pairs={{0,4},{4,0},{8,12},{12,8},{1,5},{5,1},{9,13},{13,9},{2,6},{6,2},{1... | collective-permute-start | bytes 1572872 | tf_op jit(solution)/shard_map/ppermute | solution.py:755
  671.2 17.9 %all-to-all-start.3 = ((f32[16,1,256]{2,1,0:T(1,128)}), f32[16,1,256]{2,1,0:T(1,128)S(1)}, u32[]{:S(2)}, u32[]{:S(2)}) async-start(f32[16,1,256]{2,1,0:T(1,128)} %reshape.132), calls=%async_computation.3 | async-start | bytes 32768 | tf_op jit(solution)/shard_map/all_to_all | solution.py:1162
  (141 other events, 3739.8 us)

commit v7 on v6

--- a/solution.py
+++ b/solution.py
@@ -760,20 +760,109 @@
     return lax.ppermute(block, "tensor", [(i, (i + step) % size) for i in range(size)])
 
 
-def pack_kernel(first_ref, second_ref, own_ref, other_ref):
-    half = first_ref.shape[0] // 2
-    own_ref[:half] = first_ref[:half]
-    own_ref[half:] = second_ref[:, :half]
-    other_ref[:half] = first_ref[half:].astype(jnp.bfloat16)
-    other_ref[half:] = second_ref[:, half:].astype(jnp.bfloat16)
-
-
-def pack_wide_kernel(first_ref, second_ref, own_ref, other_ref):
-    half, width = own_ref.shape[0], first_ref.shape[1]
-    own_ref[:, :width] = first_ref[:half]
-    own_ref[:, width:] = second_ref[:half]
-    other_ref[:, :width] = first_ref[half:].astype(jnp.bfloat16)
-    other_ref[:, width:] = second_ref[half:].astype(jnp.bfloat16)
+def dot_tn(left, right):
+    return lax.dot_general(
+        left, right, (((0,), (0,)), ((), ())), preferred_element_type=jnp.float32
+    )
+
+
+def fetch(first_ref, zeros, ones, buffers, sems):
+    for section, sources in enumerate((zeros, ones)):
+
+        @pl.when(first_ref[0] == section)
+        def _():
+            copies = [
+                pltpu.make_async_copy(source, buffer, sems.at[i])
+                for i, (source, buffer) in enumerate(zip(sources, buffers))
+            ]
+            for copy in copies:
+                copy.start()
+            for copy in copies:
+                copy.wait()
+
+
+def mlp_grads_kernel(base, section_ref, *refs):
+    (own_one, other_one, own_two, other_two), (rows, d_up, gelu, d_down, sems) = refs[12:16], refs[16:]
+    half, size = own_one.shape[0] // 2, own_one.shape[1]
+    cols = pl.ds(base * size, 2 * size)
+
+    def parts(own_rows, other_rows, d_up_ref, gelu_ref, own_grad, other_grad):
+        whole = (d_up_ref.at[:, cols], gelu_ref.at[:, cols])
+        return (own_rows, other_rows, *whole, own_grad, other_grad)
+
+    count = refs[0].shape[0]
+    buffers = (
+        rows.at[pl.ds(0, count)],
+        rows.at[pl.ds(count, count)],
+        d_up,
+        gelu,
+        d_down.at[pl.ds(0, count)],
+        d_down.at[pl.ds(count, count)],
+    )
+    fetch(section_ref, parts(*refs[:6]), parts(*refs[6:12]), buffers, sems)
+    for j, own, other in ((1, own_two, other_two), (0, own_one, other_one)):
+        cols = slice(j * size, (j + 1) * size)
+        up = dot_tn(rows[...], d_up[:, cols])
+        own[:half] = up[:half]
+        other[:half] = up[half:].astype(jnp.bfloat16)
+        down = dot_tn(gelu[:, cols], d_down[...])
+        own[half:] = down[:, :half]
+        other[half:] = down[:, half:].astype(jnp.bfloat16)
+
+
+def attn_grads_kernel(base, section_ref, *refs):
+    (own_one, other_one, own_two, other_two), (rows, d_qkv, mixed, d_attn, sems) = refs[12:16], refs[16:]
+    half, size = own_one.shape[0], d_qkv.shape[1] // 2
+    count = refs[0].shape[0]
+    cols = pl.ds(base * 128, 256)
+
+    def parts(own_rows, other_rows, d_qkv_ref, mixed_ref, own_grad, other_grad):
+        return (own_rows, other_rows, d_qkv_ref, mixed_ref.at[:, cols], own_grad, other_grad)
+
+    buffers = (
+        rows.at[pl.ds(0, count)],
+        rows.at[pl.ds(count, count)],
+        d_qkv,
+        mixed,
+        d_attn.at[pl.ds(0, count)],
+        d_attn.at[pl.ds(count, count)],
+    )
+    fetch(section_ref, parts(*refs[:6]), parts(*refs[6:12]), buffers, sems)
+    for j, own, other in ((1, own_two, other_two), (0, own_one, other_one)):
+        qkv = dot_tn(rows[...], d_qkv[:, j * size : (j + 1) * size])
+        out = dot_tn(d_attn[...], mixed[:, j * 128 : (j + 1) * 128])
+        own[:, :size] = qkv[:half]
+        own[:, size:] = out[:half]
+        other[:, :size] = qkv[half:].astype(jnp.bfloat16)
+        other[:, size:] = out[half:].astype(jnp.bfloat16)
+
+
+def weight_grads(kernel, name, base, section, zeros, ones, shape, columns, waits=()):
+    length = 2 * zeros[0].shape[0]
+    width = zeros[0].shape[1]
+    every = pl.BlockSpec(memory_space=pl.ANY)
+    space = pl.BlockSpec(memory_space=pltpu.VMEM)
+    arrays = (*zeros, *ones)
+    first, second, third, fourth = pl.pallas_call(
+        without(functools.partial(kernel, base), 1 + len(arrays), len(waits)),
+        in_specs=[pl.BlockSpec(memory_space=pltpu.SMEM)] + [every] * (len(arrays) + len(waits)),
+        out_specs=[space] * 4,
+        out_shape=[
+            jax.ShapeDtypeStruct(shape, jnp.float32),
+            jax.ShapeDtypeStruct(shape, jnp.bfloat16),
+        ]
+        * 2,
+        scratch_shapes=[
+            pltpu.VMEM((length, width), jnp.bfloat16),
+            pltpu.VMEM((length, columns[0]), jnp.bfloat16),
+            pltpu.VMEM((length, columns[1]), jnp.bfloat16),
+            pltpu.VMEM((length, width), jnp.bfloat16),
+            pltpu.SemaphoreType.DMA((6,)),
+        ],
+        compiler_params=pltpu.CompilerParams(vmem_limit_bytes=KERNEL_VMEM),
+        name=name,
+    )(section, *arrays, *waits)
+    return [(first, flip_pairs(second, 2)), (third, flip_pairs(fourth, 2))]
 
 
 def gate_kernel(up_ref, down_ref, up_out, down_out):
@@ -902,8 +991,7 @@
             jnp.concatenate(ordered(mine, flip_pairs(other, 1))), "tensor", 0, 0, tiled=True
         )
 
-    def from_chip(block, waits=()):
-        spread_out = lax.all_to_all(block, "tensor", 0, 0, tiled=True)
+    def from_chip(spread_out, waits=()):
         piece = ((micro, part, width), jnp.bfloat16)
         keep, send = with_core(
             pick_kernel, "pick", core_word, (piece, piece), spread_out, waits=waits
@@ -1000,16 +1088,16 @@
         saved = (layer_input, heads, branch, hidden, slope, mlp_branch)
         return result, saved, (attn_in, mixed, mlp_in, gelu_out)
 
-    def backward(grad, saved, hook, waits=()):
+    def backward(grad, saved, hook, late=()):
         layer_input, heads, branch, hidden, slope, mlp_branch = saved
         operands = (gain, grad, mlp_branch)
         d_down, sum_three = on_chip(
-            into_mlp_back_kernel, "into_mlp_back", (row16, sum32), *operands, waits=waits
+            into_mlp_back_kernel, "into_mlp_back", (row16, sum32), *operands
         )
         d_down = both_rows(d_down)
         kernel = functools.partial(mlp_up_back_kernel, tensor)
         operands = (*d_down, slope, *w_down[0], *w_down[1])
-        (d_up,) = on_chip(kernel, "mlp_up_back", (unit16,), *operands, **mlp_cost)
+        (d_up,) = on_chip(kernel, "mlp_up_back", (unit16,), *operands, **mlp_cost, waits=late)
         waits = hook(d_down, d_up)
         parts = model_rows(model_kernel(every), "mlp_back", [d_up], w_up, waits)
         waits = hook()
@@ -1029,7 +1117,7 @@
         parts = model_rows(model_kernel(QKV, 2), "attn_back", d_qkv, w_attn, waits)
         operands = (gain, layer_input, *parts, d_hidden)
         d_input, sum_zero = on_chip(
-            out_of_layer_kernel, "out_of_layer", (row16, sum32), *operands
+            out_of_layer_kernel, "out_of_layer", (row16, sum32), *operands, waits=hook()
         )
         sums = jnp.concatenate([sum_zero, sum_one, sum_two, sum_three])
         return d_input, (d_qkv, d_attn, d_up, d_down), sums
@@ -1037,46 +1125,49 @@
     low_zero, saved_zero, lefts_zero = forward(
         start,
         (
-            (attn_other[1],),
-            (up_own[1], down_own[1], up_other[0]),
-            (up_own[2], down_other[0]),
-            (down_own[2], up_other[1], down_other[1], up_own[3]),
+            (up_piece,),
+            (up_own[1], down_own[1]),
+            (up_own[2], down_own[2], up_other[0], down_other[0]),
+            (up_own[3], down_own[3], up_other[1], down_other[1]),
         ),
     )
     low_one, saved_one, lefts_one = forward(shifted(low_zero, "section", 1), ((),) * 4)
     grad_one, rights_one, gain_one = backward(start, saved_one, lambda *new: ())
     received = shifted(grad_one, "section", -1)
 
-    def joined(pair):
-        return lax.optimization_barrier(jnp.concatenate(pair, axis=0))
-
-    def own_layer(zero, one):
-        if isinstance(zero, tuple):
-            zero, one = joined(zero), joined(one)
-        return jnp.where(first, zero, one)
-
-    lefts_zero, lefts_one = lax.optimization_barrier((lefts_zero, lefts_one, grad_one))[:2]
-    attn_in, mixed, mlp_in, gelu_out = lefts = list(map(own_layer, lefts_zero, lefts_one))
     lows = lax.optimization_barrier((low_zero, low_one, grad_one))[:2]
     lows = own_first(jnp.where(first, *lows)).reshape(tensor, part, width)
-
-    def block(array, j, count=tensor):
-        size = array.shape[1] // count
-        return array[:, j * size : (j + 1) * size]
-
-    def leave(kernel, shape, *pairs):
-        totals = [contract(*pair) for pair in pairs]
-        own, other = on_chip(kernel, "pack", ((shape, jnp.float32), (shape, jnp.bfloat16)), *totals)
-        return own, flip_pairs(other, 2)
-
-    def mlp_leaves(j):
-        shape = (wide_half + unit, unit)
-        return leave(pack_kernel, shape, (mlp_in, block(d_up, j)), (block(gelu_out, j), d_down))
-
-    def attn_leaves(j, d_qkv):
-        shape = (wide_half, 512)
-        pairs = ((attn_in, block(d_qkv, j % 2, 2)), (d_attn, block(mixed, j)))
-        return leave(pack_wide_kernel, shape, *pairs)
+    lows = lax.all_to_all(lows, "tensor", 0, 0, tiled=True)
+
+    section_word = lax.axis_index("section").astype(jnp.int32).reshape(1)
+
+    def mlp_leaves(base):
+        zeros = (*lefts_zero[2], d_up, lefts_zero[3], *d_down)
+        ones = (*lefts_one[2], rights_one[2], lefts_one[3], *rights_one[3])
+        mlp_sums[base : base + 2] = weight_grads(
+            mlp_grads_kernel,
+            "mlp_grads",
+            base,
+            section_word,
+            zeros,
+            ones,
+            (wide_half + unit, unit),
+            (2 * unit, 2 * unit),
+        )
+
+    def attn_leaves(base, d_qkv):
+        zeros = (*lefts_zero[0], d_qkv, lefts_zero[1], *d_attn)
+        ones = (*lefts_one[0], rights_one[0][base // 2], lefts_one[1], *rights_one[1])
+        attn_sums[base : base + 2] = weight_grads(
+            attn_grads_kernel,
+            "attn_grads",
+            base,
+            section_word,
+            zeros,
+            ones,
+            (wide_half, 512),
+            (768, 256),
+        )
 
     def moves_on(piece, moved=None):
         own, other = piece
@@ -1085,46 +1176,42 @@
             total = total + moved.astype(jnp.float32)
         return passed_on(total.astype(jnp.bfloat16), -1)
 
-    d_qkv_one, d_attn_one, d_up_one, d_down_one = rights_one
     mlp_sums, attn_sums = [None] * tensor, [None] * tensor
     mlp_moves, attn_moves = [None] * tensor, [None] * tensor
-    hooks = iter(range(5))
+    hooks = iter(range(6))
 
     def hook(*new):
         nonlocal d_down, d_up, d_attn
         turn = next(hooks)
         if turn == 0:
-            d_down, d_up = own_layer(new[0], d_down_one), own_layer(new[1], d_up_one)
-            mlp_sums[3] = mlp_leaves(3)
-            mlp_sums[2] = mlp_leaves(2)
-            return (mlp_sums[3][0], mlp_sums[2][0])
+            d_down, d_up = new
+            mlp_leaves(2)
+            return (mlp_sums[3][0],)
         if turn == 1:
+            mlp_leaves(0)
+            return (mlp_sums[1][0],)
+        if turn == 2:
+            (d_attn,) = new
             return (mlp_sums[3][1],)
-        if turn == 2:
-            d_attn = own_layer(new[0], d_attn_one)
+        if turn == 3:
             mlp_moves[3] = moves_on(mlp_sums[3])
-            mlp_sums[1] = mlp_leaves(1)
-            return (mlp_sums[2][1], mlp_moves[3])
-        if turn == 3:
+            attn_leaves(2, new[0])
+            return (mlp_sums[2][1], mlp_moves[3], attn_sums[3][0])
+        if turn == 4:
             mlp_moves[2] = moves_on(mlp_sums[2], mlp_moves[3])
-            mlp_sums[0] = mlp_leaves(0)
-            d_qkv = own_layer(new[0], d_qkv_one[1])
-            attn_sums[3] = attn_leaves(3, d_qkv)
-            attn_sums[2] = attn_leaves(2, d_qkv)
-            return (mlp_sums[1][1], mlp_moves[2])
+            attn_leaves(0, new[0])
+            return (mlp_sums[1][1], mlp_moves[2], attn_sums[1][0])
         mlp_moves[1] = moves_on(mlp_sums[1], mlp_moves[2])
-        d_qkv = own_layer(new[0], d_qkv_one[0])
-        attn_sums[1] = attn_leaves(1, d_qkv)
-        attn_sums[0] = attn_leaves(0, d_qkv)
         return (mlp_sums[0][1], mlp_moves[1])
 
     d_down = d_up = d_attn = None
-    grad_zero, rights_zero, gain_zero = backward(received, saved_zero, hook, tuple(lefts))
+    grad_zero, rights_zero, gain_zero = backward(received, saved_zero, hook, (lows,))
     attn_moves[3] = moves_on(attn_sums[3])
     attn_moves[2] = moves_on(attn_sums[2], attn_moves[3])
     attn_moves[1] = moves_on(attn_sums[1], attn_moves[2])
-    outputs = from_chip(lows, (attn_sums[3][0],))
-    grads = from_chip(own_first(jnp.where(first, grad_zero, grad_one)).reshape(tensor, part, width))
+    outputs = from_chip(lows, (grad_zero,))
+    grads = own_first(jnp.where(first, grad_zero, grad_one)).reshape(tensor, part, width)
+    grads = from_chip(lax.all_to_all(grads, "tensor", 0, 0, tiled=True))
 
     block32 = ((wide_half // 2, unit), jnp.float32)
     down32 = ((unit, wide_half // 2), jnp.float32)

time: 702 us -> 656 us (0.934)
  starting transfers between devices: 97.1 us -> 65 us
  matrix products: 27.5 us -> 0 us
  Pallas kernels: 194 us -> 219 us
  waiting for transfers between devices: 298 us -> 279 us
  other arithmetic: 38.4 us -> 27.1 us
  blocking collectives: 0 us -> 10.4 us
  local copies, waits for them, and re-layouts: 35.1 us -> 43.2 us
    dot_general x16 -> x0, matrix products: 27.5 us -> none  [contract(): lax.dot_general(left_rows, right_rows, (((0,), (0,)), ((), ())), preferre...]
    pallas_call x0 -> x4, Pallas kernels: none -> 26.8 us  [weight_grads(): pl.pallas_call(without(functools.partial(kernel, base), 1 + len(arrays),...]
    all_to_all x3 -> x2, starting transfers between devices: 24.9 us -> 7.93 us  [the longest x1 4.26 us: per_chip(): lows = lax.all_to_all(lows, 'tensor', 0, 0, tiled=True)]
    ppermute x15, starting transfers between devices: 34.2 us -> 19.9 us  [passed_on(): lax.ppermute(block, 'tensor', [(i, (i + step) % size) for i in range(size)])]
    all_to_all x0 -> x1, blocking collectives: none -> 10.4 us  [per_chip(): gain_parts = lax.all_to_all(gain_parts, ('dp', 'tensor'), 0, 0, tiled=True)]
    all_to_all x3 -> x2, waiting for transfers between devices: 11.4 us -> 0.98 us  [the longest x1 0.98 us: per_chip(): lows = lax.all_to_all(lows, 'tensor', 0, 0, tiled=True)]
    unnamed x288 -> x268, local copies, waits for them, and re-layouts: 27.5 us -> 36.6 us
    ppermute x42, waiting for transfers between devices: 139 us -> 131 us  [flip_pairs(): return lax.ppermute(block, 'dp', [(i, i ^ distance) for i in range(size)])]
  transfers between devices with their start and end apart: 63 -> 62, of which waited for: 37 -> 37; matrix products, arithmetic and copies ran while one was open for 8% -> 4% of each run, Pallas kernels for 12% -> 16%
where the time goes in v7:
time: 656 us; the launch traced here: 646 us
  waiting for transfers between devices  279 us (43%)
  Pallas kernels  219 us (33%)
  starting transfers between devices  65 us (10%)
  local copies, waits for them, and re-layouts  43.2 us (7%)
  other arithmetic  27.1 us (4%)
  blocking collectives  10.4 us (2%)
    ppermute x42, waiting for transfers between devices, flip_pairs(): return lax.ppermute(block, 'dp', [(i, i ^ distance) for i in range(size)])  131 us
    ppermute x15, waiting for transfers between devices, passed_on(): lax.ppermute(block, 'tensor', [(i, (i + step) % size) for i in range(size)])  104 us
    pallas_call x25, Pallas kernels, on_chip(): pl.pallas_call(without(kernel, len(operands), len(waits)), in_specs=[spac...  94.9 us
    pallas_call x6, Pallas kernels, by_pairs(): pl.pallas_call(without(functools.partial(kernel, len(pieces[0])), taken,...  84.4 us
    ppermute x2, waiting for transfers between devices, shifted(): return lax.ppermute(block, axis, route)  42.8 us
    unnamed x268, local copies, waits for them, and re-layouts  36.6 us
    pallas_call x4, Pallas kernels, weight_grads(): pl.pallas_call(without(functools.partial(kernel, base), 1 + len(arrays),...  26.8 us
    ppermute x42, starting transfers between devices, flip_pairs(): return lax.ppermute(block, 'dp', [(i, i ^ distance) for i in range(size)])  26.4 us
  transfers between devices with their start and end apart: 62, of which 37 were waited for; matrix products, arithmetic and copies ran while one was open for 4% of the time, Pallas kernels for 16%

profile of v7, /device:TPU:0, one launch (start us, length us, event | category | flops | bytes accessed | tf_op | source)
XLA Modules:
  0.0 646.4 jit_solution(12111633221104197573)
XLA Ops:
  11.1 6.2 all-to-all-start
  21.0 29.1 %collective-permute-done.1.refs_6_.refs_2_.refs_3_ = bf16[512,512]{1,0:T(8,128)(2,1)} collective-permute-done((bf16[512,512]{1,0:T(8,128)(2,1)S(1)}, bf16[512,512]{1,0:T(8,128)(2,1)}, u32[]{:S(2)}, u32[]{:S(2)}) %collective-permute-start.1) | collective-permute-done | bytes 524320 | tf_op jit(solution)/shard_map/ppermute | solution.py:760
  50.1 3.2 collective-permute-start.2
  55.4 9.6 %collective-permute-done.2.refs_2_.refs_7_.refs_3_.refs_5_.refs_4_ = bf16[512,512]{1,0:T(8,128)(2,1)S(1)} collective-permute-done((bf16[512,512]{1,0:T(8,128)(2,1)}, bf16[512,512]{1,0:T(8,128)(2,1)S(1)}, u32[]{:S(2)}, u32[]{:S(2)}) %collective-permute-start.2) | collective-permute-done | bytes 524320 | tf_op jit(solution)/shard_map/ppermute | solution.py:760
  84.3 7.7 %collective-permute-done.7.refs_11_.refs_7_.refs_8_ = bf16[512,512]{1,0:T(8,128)(2,1)S(1)} collective-permute-done((bf16[512,512]{1,0:T(8,128)(2,1)S(1)}, bf16[512,512]{1,0:T(8,128)(2,1)S(1)}, u32[]{:S(2)}, u32[]{:S(2)}) %collective-permute-start.7) | collective-permute-done | bytes 524320 | tf_op jit(solution)/shard_map/ppermute | solution.py:755
  94.1 7.1 %collective-permute-done.10.refs_14_.refs_2_.refs_4_ = bf16[512,512]{1,0:T(8,128)(2,1)S(1)} collective-permute-done((bf16[512,512]{1,0:T(8,128)(2,1)}, bf16[512,512]{1,0:T(8,128)(2,1)S(1)}, u32[]{:S(2)}, u32[]{:S(2)}) %collective-permute-start.10) | collective-permute-done | bytes 524320 | tf_op jit(solution)/shard_map/ppermute | solution.py:760
  103.2 2.6 collective-permute-start.12
  105.8 16.7 %attend.2 = (bf16[4,1024,128]{2,1,0:T(8,128)(2,1)S(1)}, bf16[4,1024,128]{2,1,0:T(8,128)(2,1)S(1)}, bf16[4,1024,128]{2,1,0:T(8,128)(2,1)S(1)}, f32[4,2,1024]{2,1,0:T(2,128)S(1)}, bf16[1024,512]{1,0:T(8,128)(2,1)S(1)}) custom-call(s32[1]{0:T(128)} %bitcast.refs_0_, f32[1024,128]{1,0:T(8,128)S(1)} %pad_maximum_fusion.1.refs_1_, ...), custom_call_target="tpu_custom_call" | custom-call | flops 11811160064 | bytes 11567104 | tf_op jit(solution)/shard_map/attend/pallas_call | solution.py:685
  127.0 3.0 attn_out.2
  132.4 12.5 %collective-permute-done.18.refs_6_.refs_7_ = bf16[512,512]{1,0:T(8,128)(2,1)S(1)} collective-permute-done((bf16[512,512]{1,0:T(8,128)(2,1)S(1)}, bf16[512,512]{1,0:T(8,128)(2,1)S(1)}, u32[]{:S(2)}, u32[]{:S(2)}) %collective-permute-start.18) | collective-permute-done | bytes 524320 | tf_op jit(solution)/shard_map/ppermute | solution.py:755
  144.9 10.8 %collective-permute-done.19.refs_7_.refs_6_.refs_8_ = bf16[512,512]{1,0:T(8,128)(2,1)S(1)} collective-permute-done((bf16[512,512]{1,0:T(8,128)(2,1)S(1)}, bf16[512,512]{1,0:T(8,128)(2,1)S(1)}, u32[]{:S(2)}, u32[]{:S(2)}) %collective-permute-start.19) | collective-permute-done | bytes 524320 | tf_op jit(solution)/shard_map/ppermute | solution.py:755
  155.7 3.3 collective-permute-done.17.refs_5_.refs_4_.refs_6_
  159.0 3.4 after_attn.2
  166.6 10.7 %collective-permute-done.21.refs_8_.refs_7_ = bf16[512,512]{1,0:T(8,128)(2,1)S(1)} collective-permute-done((bf16[512,512]{1,0:T(8,128)(2,1)S(1)}, bf16[512,512]{1,0:T(8,128)(2,1)S(1)}, u32[]{:S(2)}, u32[]{:S(2)}) %collective-permute-start.21) | collective-permute-done | bytes 524320 | tf_op jit(solution)/shard_map/ppermute | solution.py:755
  177.3 11.2 %collective-permute-done.22.refs_9_.refs_8_ = bf16[512,512]{1,0:T(8,128)(2,1)S(1)} collective-permute-done((bf16[512,512]{1,0:T(8,128)(2,1)S(1)}, bf16[512,512]{1,0:T(8,128)(2,1)S(1)}, u32[]{:S(2)}, u32[]{:S(2)}) %collective-permute-start.22) | collective-permute-done | bytes 524320 | tf_op jit(solution)/shard_map/ppermute | solution.py:755
  188.5 7.7 %mlp_up.2 = (bf16[1024,2048]{1,0:T(8,128)(2,1)S(1)}, bf16[1024,2048]{1,0:T(8,128)(2,1)S(1)}) custom-call(bf16[512,1024]{1,0:T(8,128)(2,1)S(1)} %get-tuple-element.103.refs_0_.refs_1_, bf16[512,1024]{1,0:T(8,128)(2,1)S(1)} %collective-permute-done.20.refs_1_.refs_2_, bf16[512,512]{1,0:T(8,128)(2,1)S(1)} %copy-done.83, ...), custom_call_target="tpu_custom_call" | custom-call | flops 4294967296 | bytes 14680064 | tf_op jit(solution)/shard_map/mlp_up/pallas_call | solution.py:667
  199.8 10.8 %collective-permute-done.24.refs_8_.refs_10_ = bf16[512,512]{1,0:T(8,128)(2,1)S(1)} collective-permute-done((bf16[512,512]{1,0:T(8,128)(2,1)S(1)}, bf16[512,512]{1,0:T(8,128)(2,1)S(1)}, u32[]{:S(2)}, u32[]{:S(2)}) %collective-permute-start.24) | collective-permute-done | bytes 524320 | tf_op jit(solution)/shard_map/ppermute | solution.py:755
  210.5 4.5 mlp_down.2
  215.1 2.6 collective-permute-done.25.refs_3_
  219.7 3.4 collective-permute-start.26
  223.0 22.4 %collective-permute-done.26.refs_1_ = bf16[512,1024]{1,0:T(8,128)(2,1)S(1)} collective-permute-done((bf16[512,1024]{1,0:T(8,128)(2,1)S(1)}, bf16[512,1024]{1,0:T(8,128)(2,1)S(1)}, u32[]{:S(2)}, u32[]{:S(2)}) %collective-permute-start.26) | collective-permute-done | bytes 1048608 | tf_op jit(solution)/shard_map/ppermute | solution.py:28
  247.3 2.6 collective-permute-done.27.refs_4_.refs_8_
  249.9 16.8 %attend.3 = (bf16[4,1024,128]{2,1,0:T(8,128)(2,1)S(1)}, bf16[4,1024,128]{2,1,0:T(8,128)(2,1)S(1)}, bf16[4,1024,128]{2,1,0:T(8,128)(2,1)S(1)}, f32[4,2,1024]{2,1,0:T(2,128)S(1)}, bf16[1024,512]{1,0:T(8,128)(2,1)S(1)}) custom-call(s32[1]{0:T(128)} %bitcast.refs_0_, f32[1024,128]{1,0:T(8,128)S(1)} %pad_maximum_fusion.1.refs_1_, ...), custom_call_target="tpu_custom_call" | custom-call | flops 11811160064 | bytes 11567104 | tf_op jit(solution)/shard_map/attend/pallas_call | solution.py:685
  266.7 3.2 attn_out.3
  270.1 2.5 collective-permute-done.28.refs_3_
  272.7 3.4 after_attn.3
  276.3 2.5 collective-permute-done.29.refs_1_.refs_8_
  278.8 7.7 %mlp_up.3 = (bf16[1024,2048]{1,0:T(8,128)(2,1)S(1)}, bf16[1024,2048]{1,0:T(8,128)(2,1)S(1)}) custom-call(bf16[512,1024]{1,0:T(8,128)(2,1)S(1)} %get-tuple-element.112.refs_0_.refs_7_, bf16[512,1024]{1,0:T(8,128)(2,1)S(1)} %collective-permute-done.29.refs_1_.refs_8_, bf16[512,512]{1,0:T(8,128)(2,1)S(1)} %copy-done.83, ...), custom_call_target="tpu_custom_call" | custom-call | flops 4294967296 | bytes 14680064 | tf_op jit(solution)/shard_map/mlp_up/pallas_call | solution.py:667
  286.6 4.5 mlp_down.3
  291.3 2.5 collective-permute-done.30.refs_3_
  295.7 2.6 into_mlp_back.2
  298.5 2.5 collective-permute-done.31.refs_1_.refs_12_
  301.0 4.5 mlp_up_back.2.refs_0_.refs_9_
  307.6 4.5 mlp_back.2
  314.9 4.0 into_attn_back.2
  319.1 2.5 collective-permute-done.33.refs_4_.refs_12_
  321.6 12.9 %attend_back.4.refs_0_.refs_9_ = bf16[1024,768]{1,0:T(8,128)(2,1)S(1)} custom-call(s32[1]{0:T(128)} %bitcast.refs_0_, f32[1024,128]{1,0:T(8,128)S(1)} %pad_maximum_fusion.1.refs_1_, f32[1024,128]{1,0:T(8,128)S(1)} %pad_maximum_fusion.2.refs_2_, bf16[512,1024]{1,0:T(8,128)(2,1)S(1)} %get-tuple-element.123.refs_3_.refs_11_, ...), custom_call_target="tpu_custom_call" | custom-call | flops 11274289152 | bytes 6815744 | tf_op jit(solution)/shard_map/attend_back/pallas_call | solution.py:685
  334.6 12.8 %attend_back.5.refs_1_.refs_9_ = bf16[1024,768]{1,0:T(8,128)(2,1)S(1)} custom-call(s32[1]{0:T(128)} %bitcast.refs_0_, f32[1024,128]{1,0:T(8,128)S(1)} %pad_maximum_fusion.1.refs_1_, f32[1024,128]{1,0:T(8,128)S(1)} %pad_maximum_fusion.2.refs_2_, bf16[512,1024]{1,0:T(8,128)(2,1)S(1)} %get-tuple-element.123.refs_3_.refs_11_, ...), custom_call_target="tpu_custom_call" | custom-call | flops 11274289152 | bytes 6815744 | tf_op jit(solution)/shard_map/attend_back/pallas_call | solution.py:685
  347.5 5.5 attn_back.2
  355.7 3.2 out_of_layer.2
  361.7 4.3 all-to-all-start.1
  366.0 20.4 %collective-permute-done.35.refs_1_ = bf16[512,1024]{1,0:T(8,128)(2,1)S(1)} collective-permute-done((bf16[512,1024]{1,0:T(8,128)(2,1)}, bf16[512,1024]{1,0:T(8,128)(2,1)S(1)}, u32[]{:S(2)}, u32[]{:S(2)}) %collective-permute-start.35) | collective-permute-done | bytes 1048608 | tf_op jit(solution)/shard_map/ppermute | solution.py:28
  388.3 3.1 into_mlp_back.3
  404.9 6.2 mlp_up_back.3.refs_3_.refs_0_
  415.0 8.7 %mlp_grads.2 = (f32[1024,512]{1,0:T(8,128)S(1)}, bf16[1024,512]{1,0:T(8,128)(2,1)}, f32[1024,512]{1,0:T(8,128)S(1)}, bf16[1024,512]{1,0:T(8,128)(2,1)S(1)}) custom-call(s32[1]{0:T(128)} %bitcast.12.refs_0_, bf16[512,1024]{1,0:T(8,128)(2,1)S(1)} %copy-done.21, bf16[512,1024]{1,0:T(8,128)(2,1)S(1)} %copy-done.23, ...), custom_call_target="tpu_custom_call" | custom-call | tf_op jit(solution)/shard_map/mlp_grads/pallas_call | solution.py:846
  425.3 4.5 mlp_back.3
  430.5 19.2 %collective-permute-done.40.refs_13_ = bf16[1024,512]{1,0:T(8,128)(2,1)S(1)} collective-permute-done((bf16[1024,512]{1,0:T(8,128)(2,1)S(1)}, bf16[1024,512]{1,0:T(8,128)(2,1)S(1)}, u32[]{:S(2)}, u32[]{:S(2)}) %collective-permute-start.40) | collective-permute-done | bytes 1048608 | tf_op jit(solution)/shard_map/ppermute | solution.py:755
  451.3 7.4 %mlp_grads.3 = (f32[1024,512]{1,0:T(8,128)S(1)}, bf16[1024,512]{1,0:T(8,128)(2,1)S(1)}, f32[1024,512]{1,0:T(8,128)S(1)}, bf16[1024,512]{1,0:T(8,128)(2,1)S(1)}) custom-call(s32[1]{0:T(128)} %bitcast.12.refs_0_, bf16[512,1024]{1,0:T(8,128)(2,1)S(1)} %copy-done.21, bf16[512,1024]{1,0:T(8,128)(2,1)S(1)} %copy-done.23, ...), custom_call_target="tpu_custom_call" | custom-call | tf_op jit(solution)/shard_map/mlp_grads/pallas_call | solution.py:846
  463.0 4.0 into_attn_back.3
  469.2 3.1 collective-permute-done.39.refs_13_
  472.3 2.9 collective-permute-done.41.refs_14_
  480.0 12.5 %attend_back.6.refs_3_.refs_1_ = bf16[1024,768]{1,0:T(8,128)(2,1)S(1)} custom-call(s32[1]{0:T(128)} %bitcast.refs_0_, f32[1024,128]{1,0:T(8,128)S(1)} %copy-done.98, f32[1024,128]{1,0:T(8,128)S(1)} %copy-done.80, bf16[512,1024]{1,0:T(8,128)(2,1)S(1)} %get-tuple-element.142.refs_3_.refs_5_, bf16[512,1024]{1,0:T(8,128)(2,1)S(1)} %collective-permute-done.38.refs_4_.refs_6_, ...), custom_call_target="tpu_custom_call" | custom-call | flops 11274289152 | bytes 6815744 | tf_op jit(solution)/shard_map/attend_back/pallas_call | solution.py:685
  492.6 5.7 attn_grads.2
  499.2 12.8 %attend_back.7.refs_3_.refs_0_ = bf16[1024,768]{1,0:T(8,128)(2,1)S(1)} custom-call(s32[1]{0:T(128)} %bitcast.refs_0_, f32[1024,128]{1,0:T(8,128)S(1)} %copy-done.98, f32[1024,128]{1,0:T(8,128)S(1)} %copy-done.80, bf16[512,1024]{1,0:T(8,128)(2,1)S(1)} %get-tuple-element.142.refs_3_.refs_5_, bf16[512,1024]{1,0:T(8,128)(2,1)S(1)} %collective-permute-done.38.refs_4_.refs_6_, ...), custom_call_target="tpu_custom_call" | custom-call | flops 11274289152 | bytes 6815744 | tf_op jit(solution)/shard_map/attend_back/pallas_call | solution.py:685
  512.0 5.0 attn_grads.3
  517.1 5.9 attn_back.3
  526.1 12.7 %collective-permute-done.52 = bf16[512,512]{1,0:T(8,128)(2,1)S(1)} collective-permute-done((bf16[512,512]{1,0:T(8,128)(2,1)S(1)}, bf16[512,512]{1,0:T(8,128)(2,1)S(1)}, u32[]{:S(2)}, u32[]{:S(2)}) %collective-permute-start.52) | collective-permute-done | bytes 524320 | tf_op jit(solution)/shard_map/ppermute | solution.py:755
  541.4 8.2 %collective-permute-done.46.refs_6_.refs_3_ = bf16[1024,512]{1,0:T(8,128)(2,1)S(1)} collective-permute-done((bf16[1024,512]{1,0:T(8,128)(2,1)S(1)}, bf16[1024,512]{1,0:T(8,128)(2,1)S(1)}, u32[]{:S(2)}, u32[]{:S(2)}) %collective-permute-start.46) | collective-permute-done | bytes 1048608 | tf_op jit(solution)/shard_map/ppermute | solution.py:760
  553.3 3.7 all-to-all-start.2
  557.0 3.9 collective-permute-done.53
  566.6 21.9 %collective-permute-done.54 = bf16[512,512]{1,0:T(8,128)(2,1)S(1)} collective-permute-done((bf16[512,512]{1,0:T(8,128)(2,1)S(1)}, bf16[512,512]{1,0:T(8,128)(2,1)S(1)}, u32[]{:S(2)}, u32[]{:S(2)}) %collective-permute-start.54) | collective-permute-done | bytes 524320 | tf_op jit(solution)/shard_map/ppermute | solution.py:760
  592.2 14.7 %collective-permute-done.55.refs_3_ = bf16[512,512]{1,0:T(8,128)(2,1)S(1)} collective-permute-done((bf16[512,512]{1,0:T(8,128)(2,1)S(1)}, bf16[512,512]{1,0:T(8,128)(2,1)S(1)}, u32[]{:S(2)}, u32[]{:S(2)}) %collective-permute-start.55) | collective-permute-done | bytes 524320 | tf_op jit(solution)/shard_map/ppermute | solution.py:760
  621.4 10.4 %all_to_all.20 = f32[16,1,256]{2,1,0:T(1,128)S(1)} all-to-all(f32[16,1,256]{2,1,0:T(1,128)S(1)} %reshape.136), channel_id=1, replica_groups=mesh['section'=2,'dp'=4,'tensor'=4] {'dp','tensor'}, dimensions={0} | all-to-all | bytes 32768 | tf_op jit(solution)/shard_map/all_to_all | solution.py:1249
  642.3 2.8 mlp_join.1
  (433 shorter events, 150.7 us)
Async XLA Ops:
  6.8 2.1 collective-permute-start
  11.1 58.4 %all-to-all-start = ((bf16[4,128,1024]{2,1,0:T(8,128)(2,1)}), bf16[4,128,1024]{2,1,0:T(8,128)(2,1)S(1)}, u32[]{:S(2)}, u32[]{:S(2)}) async-start(bf16[4,128,1024]{2,1,0:T(8,128)(2,1)} %pad_maximum_fusion), calls=%async_computation | async-start | bytes 2097152 | tf_op jit(solution)/shard_map/all_to_all | solution.py:990
  18.9 328.5 %copy-start.18 = (bf16[512,512]{1,0:T(8,128)(2,1)}, bf16[512,512]{1,0:T(8,128)(2,1)S(1)}, u32[]{:S(2)}) copy-start(bf16[512,512]{1,0:T(8,128)(2,1)S(1)} %pad_maximum_fusion.3.refs_5_.refs_1_.refs_2_) | copy-start | bytes 1572868
  18.9 31.2 %collective-permute-start.1 = (bf16[512,512]{1,0:T(8,128)(2,1)S(1)}, bf16[512,512]{1,0:T(8,128)(2,1)}, u32[]{:S(2)}, u32[]{:S(2)}) collective-permute-start(bf16[512,512]{1,0:T(8,128)(2,1)S(1)} %pad_maximum_fusion.3.refs_5_.refs_1_.refs_2_), channel_id=1, source_target_pairs={{0,1},{1,2},{2,3},{3,0},{4,5},{5,6},{6,7},{7,4},{8,9},{9,10},{10,1... | collective-permute-start | bytes 1572872 | tf_op jit(solution)/shard_map/ppermute | solution.py:760
  50.1 14.9 %collective-permute-start.2 = (bf16[512,512]{1,0:T(8,128)(2,1)}, bf16[512,512]{1,0:T(8,128)(2,1)S(1)}, u32[]{:S(2)}, u32[]{:S(2)}) collective-permute-start(bf16[512,512]{1,0:T(8,128)(2,1)} %collective-permute-done.1.refs_6_.refs_2_.refs_3_), channel_id=1, source_target_pairs={{0,1},{1,2},{2,3},{3,0},{4,5},{5,6},{6,7},{7,4},{8,9},{9,10},{10,1... | collective-permute-start | bytes 1572872 | tf_op jit(solution)/shard_map/ppermute | solution.py:760
  53.2 21.6 %collective-permute-start.5 = (bf16[512,512]{1,0:T(8,128)(2,1)S(1)}, bf16[512,512]{1,0:T(8,128)(2,1)}, u32[]{:S(2)}, u32[]{:S(2)}) collective-permute-start(bf16[512,512]{1,0:T(8,128)(2,1)S(1)} %pad_maximum_fusion.3.refs_5_.refs_1_.refs_2_), channel_id=1, source_target_pairs={{0,8},{4,12},{8,0},{12,4},{1,9},{5,13},{9,1},{13,5},{2,10},{6,14},... | collective-permute-start | bytes 1572872 | tf_op jit(solution)/shard_map/ppermute | solution.py:755
  54.8 22.3 %collective-permute-start.6 = (bf16[512,512]{1,0:T(8,128)(2,1)}, bf16[512,512]{1,0:T(8,128)(2,1)}, u32[]{:S(2)}, u32[]{:S(2)}) collective-permute-start(bf16[512,512]{1,0:T(8,128)(2,1)} %collective-permute-done.1.refs_6_.refs_2_.refs_3_), channel_id=1, source_target_pairs={{0,8},{4,12},{8,0},{12,4},{1,9},{5,13},{9,1},{13,5},{2,10},{6,14},... | collective-permute-start | bytes 1572872 | tf_op jit(solution)/shard_map/ppermute | solution.py:755
  65.0 14.9 %collective-permute-start.4 = (bf16[512,512]{1,0:T(8,128)(2,1)S(1)}, bf16[512,512]{1,0:T(8,128)(2,1)}, u32[]{:S(2)}, u32[]{:S(2)}) collective-permute-start(bf16[512,512]{1,0:T(8,128)(2,1)S(1)} %collective-permute-done.2.refs_2_.refs_7_.refs_3_.refs_5_.refs_4_), channel_id=1, source_target_pairs={{0,1},{1,2},{2,3},{3,0},{4,5},{5,6},{6,7},{7,4},{8,9},{9,10},{10,1... | collective-permute-start | bytes 1572872 | tf_op jit(solution)/shard_map/ppermute | solution.py:760
  72.3 33.5 %collective-permute-start.3 = (bf16[512,1024]{1,0:T(8,128)(2,1)S(1)}, bf16[512,1024]{1,0:T(8,128)(2,1)}, u32[]{:S(2)}, u32[]{:S(2)}) collective-permute-start(bf16[512,1024]{1,0:T(8,128)(2,1)S(1)} %norm_in.2.refs_3_.refs_1_), channel_id=1, source_target_pairs={{0,4},{4,0},{8,12},{12,8},{1,5},{5,1},{9,13},{13,9},{2,6},{6,2},{1... | collective-permute-start | bytes 3145736 | tf_op jit(solution)/shard_map/ppermute | solution.py:755
  72.4 21.1 %collective-permute-start.9 = (bf16[512,512]{1,0:T(8,128)(2,1)}, bf16[512,512]{1,0:T(8,128)(2,1)S(1)}, u32[]{:S(2)}, u32[]{:S(2)}) collective-permute-start(bf16[512,512]{1,0:T(8,128)(2,1)} %copy-done.81), channel_id=1, source_target_pairs={{0,1},{1,2},{2,3},{3,0},{4,5},{5,6},{6,7},{7,4},{8,9},{9,10},{10,1... | collective-permute-start | bytes 1572872 | tf_op jit(solution)/shard_map/ppermute | solution.py:760
  74.8 26.3 %collective-permute-start.10 = (bf16[512,512]{1,0:T(8,128)(2,1)}, bf16[512,512]{1,0:T(8,128)(2,1)S(1)}, u32[]{:S(2)}, u32[]{:S(2)}) collective-permute-start(bf16[512,512]{1,0:T(8,128)(2,1)} %copy-done.105), channel_id=1, source_target_pairs={{0,1},{1,2},{2,3},{3,0},{4,5},{5,6},{6,7},{7,4},{8,9},{9,10},{10,1... | collective-permute-start | bytes 1572872 | tf_op jit(solution)/shard_map/ppermute | solution.py:760
  77.1 14.9 %collective-permute-start.7 = (bf16[512,512]{1,0:T(8,128)(2,1)S(1)}, bf16[512,512]{1,0:T(8,128)(2,1)S(1)}, u32[]{:S(2)}, u32[]{:S(2)}) collective-permute-start(bf16[512,512]{1,0:T(8,128)(2,1)S(1)} %collective-permute-done.2.refs_2_.refs_7_.refs_3_.refs_5_.refs_4_), channel_id=1, source_target_pairs={{0,8},{4,12},{8,0},{12,4},{1,9},{5,13},{9,1},{13,5},{2,10},{6,14},... | collective-permute-start | bytes 1572872 | tf_op jit(solution)/shard_map/ppermute | solution.py:755
  79.9 23.4 %collective-permute-start.8 = (bf16[512,512]{1,0:T(8,128)(2,1)}, bf16[512,512]{1,0:T(8,128)(2,1)S(1)}, u32[]{:S(2)}, u32[]{:S(2)}) collective-permute-start(bf16[512,512]{1,0:T(8,128)(2,1)} %collective-permute-done.4.refs_8_.refs_4_.refs_6_.refs_5_), channel_id=1, source_target_pairs={{0,8},{4,12},{8,0},{12,4},{1,9},{5,13},{9,1},{13,5},{2,10},{6,14},... | collective-permute-start | bytes 1572872 | tf_op jit(solution)/shard_map/ppermute | solution.py:755
  92.0 255.4 %copy-start.46 = (bf16[512,512]{1,0:T(8,128)(2,1)}, bf16[512,512]{1,0:T(8,128)(2,1)S(1)}, u32[]{:S(2)}) copy-start(bf16[512,512]{1,0:T(8,128)(2,1)S(1)} %collective-permute-done.7.refs_11_.refs_7_.refs_8_) | copy-start | bytes 1572868
  92.0 32.5 %collective-permute-start.13 = (bf16[512,512]{1,0:T(8,128)(2,1)S(1)}, bf16[512,512]{1,0:T(8,128)(2,1)S(1)}, u32[]{:S(2)}, u32[]{:S(2)}) collective-permute-start(bf16[512,512]{1,0:T(8,128)(2,1)S(1)} %copy-done.83), channel_id=1, source_target_pairs={{0,8},{4,12},{8,0},{12,4},{1,9},{5,13},{9,1},{13,5},{2,10},{6,14},... | collective-permute-start | bytes 1572872 | tf_op jit(solution)/shard_map/ppermute | solution.py:755
  93.5 31.0 %collective-permute-start.14 = (bf16[512,512]{1,0:T(8,128)(2,1)S(1)}, bf16[512,512]{1,0:T(8,128)(2,1)S(1)}, u32[]{:S(2)}, u32[]{:S(2)}) collective-permute-start(bf16[512,512]{1,0:T(8,128)(2,1)S(1)} %copy-done.106), channel_id=1, source_target_pairs={{0,8},{4,12},{8,0},{12,4},{1,9},{5,13},{9,1},{13,5},{2,10},{6,14},... | collective-permute-start | bytes 1572872 | tf_op jit(solution)/shard_map/ppermute | solution.py:755
  101.1 23.4 %collective-permute-start.11 = (bf16[512,512]{1,0:T(8,128)(2,1)S(1)}, bf16[512,512]{1,0:T(8,128)(2,1)S(1)}, u32[]{:S(2)}, u32[]{:S(2)}) collective-permute-start(bf16[512,512]{1,0:T(8,128)(2,1)S(1)} %collective-permute-done.9.refs_13_.refs_3_.refs_2_), channel_id=1, source_target_pairs={{0,1},{1,2},{2,3},{3,0},{4,5},{5,6},{6,7},{7,4},{8,9},{9,10},{10,1... | collective-permute-start | bytes 1572872 | tf_op jit(solution)/shard_map/ppermute | solution.py:760
  103.2 23.8 %collective-permute-start.12 = (bf16[512,512]{1,0:T(8,128)(2,1)S(1)}, bf16[512,512]{1,0:T(8,128)(2,1)S(1)}, u32[]{:S(2)}, u32[]{:S(2)}) collective-permute-start(bf16[512,512]{1,0:T(8,128)(2,1)S(1)} %collective-permute-done.10.refs_14_.refs_2_.refs_4_), channel_id=1, source_target_pairs={{0,1},{1,2},{2,3},{3,0},{4,5},{5,6},{6,7},{7,4},{8,9},{9,10},{10,1... | collective-permute-start | bytes 1572872 | tf_op jit(solution)/shard_map/ppermute | solution.py:760
  130.1 28.9 %collective-permute-start.15 = (bf16[512,1024]{1,0:T(8,128)(2,1)S(1)}, bf16[512,1024]{1,0:T(8,128)(2,1)S(1)}, u32[]{:S(2)}, u32[]{:S(2)}) collective-permute-start(bf16[512,1024]{1,0:T(8,128)(2,1)S(1)} %get-tuple-element.101), channel_id=1, source_target_pairs={{0,4},{4,0},{8,12},{12,8},{1,5},{5,1},{9,13},{13,9},{2,6},{6,2},{1... | collective-permute-start | bytes 3145736 | tf_op jit(solution)/shard_map/ppermute | solution.py:755
  130.1 14.8 %collective-permute-start.18 = (bf16[512,512]{1,0:T(8,128)(2,1)S(1)}, bf16[512,512]{1,0:T(8,128)(2,1)S(1)}, u32[]{:S(2)}, u32[]{:S(2)}) collective-permute-start(bf16[512,512]{1,0:T(8,128)(2,1)S(1)} %collective-permute-done.9.refs_13_.refs_3_.refs_2_), channel_id=1, source_target_pairs={{0,8},{4,12},{8,0},{12,4},{1,9},{5,13},{9,1},{13,5},{2,10},{6,14},... | collective-permute-start | bytes 1572872 | tf_op jit(solution)/shard_map/ppermute | solution.py:755
  131.7 24.0 %collective-permute-start.19 = (bf16[512,512]{1,0:T(8,128)(2,1)S(1)}, bf16[512,512]{1,0:T(8,128)(2,1)S(1)}, u32[]{:S(2)}, u32[]{:S(2)}) collective-permute-start(bf16[512,512]{1,0:T(8,128)(2,1)S(1)} %collective-permute-done.10.refs_14_.refs_2_.refs_4_), channel_id=1, source_target_pairs={{0,8},{4,12},{8,0},{12,4},{1,9},{5,13},{9,1},{13,5},{2,10},{6,14},... | collective-permute-start | bytes 1572872 | tf_op jit(solution)/shard_map/ppermute | solution.py:755
  132.2 23.5 %collective-permute-start.16 = (bf16[512,512]{1,0:T(8,128)(2,1)S(1)}, bf16[512,512]{1,0:T(8,128)(2,1)S(1)}, u32[]{:S(2)}, u32[]{:S(2)}) collective-permute-start(bf16[512,512]{1,0:T(8,128)(2,1)S(1)} %collective-permute-done.11.refs_9_.refs_4_.refs_3_), channel_id=1, source_target_pairs={{0,1},{1,2},{2,3},{3,0},{4,5},{5,6},{6,7},{7,4},{8,9},{9,10},{10,1... | collective-permute-start | bytes 1572872 | tf_op jit(solution)/shard_map/ppermute | solution.py:760
  132.2 26.7 %collective-permute-start.17 = (bf16[512,512]{1,0:T(8,128)(2,1)S(1)}, bf16[512,512]{1,0:T(8,128)(2,1)S(1)}, u32[]{:S(2)}, u32[]{:S(2)}) collective-permute-start(bf16[512,512]{1,0:T(8,128)(2,1)S(1)} %collective-permute-done.12.refs_10_.refs_3_.refs_5_), channel_id=1, source_target_pairs={{0,1},{1,2},{2,3},{3,0},{4,5},{5,6},{6,7},{7,4},{8,9},{9,10},{10,1... | collective-permute-start | bytes 1572872 | tf_op jit(solution)/shard_map/ppermute | solution.py:760
  162.4 26.1 %collective-permute-start.20 = (bf16[512,1024]{1,0:T(8,128)(2,1)S(1)}, bf16[512,1024]{1,0:T(8,128)(2,1)S(1)}, u32[]{:S(2)}, u32[]{:S(2)}) collective-permute-start(bf16[512,1024]{1,0:T(8,128)(2,1)S(1)} %get-tuple-element.103.refs_0_.refs_1_), channel_id=1, source_target_pairs={{0,4},{4,0},{8,12},{12,8},{1,5},{5,1},{9,13},{13,9},{2,6},{6,2},{1... | collective-permute-start | bytes 3145736 | tf_op jit(solution)/shard_map/ppermute | solution.py:755
  162.5 14.8 %collective-permute-start.21 = (bf16[512,512]{1,0:T(8,128)(2,1)S(1)}, bf16[512,512]{1,0:T(8,128)(2,1)S(1)}, u32[]{:S(2)}, u32[]{:S(2)}) collective-permute-start(bf16[512,512]{1,0:T(8,128)(2,1)S(1)} %collective-permute-done.11.refs_9_.refs_4_.refs_3_), channel_id=1, source_target_pairs={{0,8},{4,12},{8,0},{12,4},{1,9},{5,13},{9,1},{13,5},{2,10},{6,14},... | collective-permute-start | bytes 1572872 | tf_op jit(solution)/shard_map/ppermute | solution.py:755
  164.1 24.4 %collective-permute-start.22 = (bf16[512,512]{1,0:T(8,128)(2,1)S(1)}, bf16[512,512]{1,0:T(8,128)(2,1)S(1)}, u32[]{:S(2)}, u32[]{:S(2)}) collective-permute-start(bf16[512,512]{1,0:T(8,128)(2,1)S(1)} %collective-permute-done.16.refs_4_.refs_5_), channel_id=1, source_target_pairs={{0,8},{4,12},{8,0},{12,4},{1,9},{5,13},{9,1},{13,5},{2,10},{6,14},... | collective-permute-start | bytes 1572872 | tf_op jit(solution)/shard_map/ppermute | solution.py:755
  164.6 35.2 %collective-permute-start.23 = (bf16[512,512]{1,0:T(8,128)(2,1)S(1)}, bf16[512,512]{1,0:T(8,128)(2,1)S(1)}, u32[]{:S(2)}, u32[]{:S(2)}) collective-permute-start(bf16[512,512]{1,0:T(8,128)(2,1)S(1)} %collective-permute-done.12.refs_10_.refs_3_.refs_5_), channel_id=1, source_target_pairs={{0,8},{4,12},{8,0},{12,4},{1,9},{5,13},{9,1},{13,5},{2,10},{6,14},... | collective-permute-start | bytes 1572872 | tf_op jit(solution)/shard_map/ppermute | solution.py:755
  166.1 44.4 %collective-permute-start.24 = (bf16[512,512]{1,0:T(8,128)(2,1)S(1)}, bf16[512,512]{1,0:T(8,128)(2,1)S(1)}, u32[]{:S(2)}, u32[]{:S(2)}) collective-permute-start(bf16[512,512]{1,0:T(8,128)(2,1)S(1)} %collective-permute-done.17.refs_5_.refs_4_.refs_6_), channel_id=1, source_target_pairs={{0,8},{4,12},{8,0},{12,4},{1,9},{5,13},{9,1},{13,5},{2,10},{6,14},... | collective-permute-start | bytes 1572872 | tf_op jit(solution)/shard_map/ppermute | solution.py:755
  215.0 2.7 collective-permute-start.25
  219.7 25.8 %collective-permute-start.26 = (bf16[512,1024]{1,0:T(8,128)(2,1)S(1)}, bf16[512,1024]{1,0:T(8,128)(2,1)S(1)}, u32[]{:S(2)}, u32[]{:S(2)}) collective-permute-start(bf16[512,1024]{1,0:T(8,128)(2,1)S(1)} %get-tuple-element.132), channel_id=1, source_target_pairs={{0,16},{1,17},{2,18},{3,19},{4,20},{5,21},{6,22},{7,23},{8,24},{9,... | collective-permute-start | bytes 3145736 | tf_op jit(solution)/shard_map/ppermute | solution.py:28
  247.2 2.7 collective-permute-start.27
  269.9 2.7 collective-permute-start.28
  276.1 2.7 collective-permute-start.29
  291.1 2.7 collective-permute-start.30
  298.2 2.7 collective-permute-start.31
  312.2 2.7 collective-permute-start.32
  318.9 2.7 collective-permute-start.33
  353.0 2.7 collective-permute-start.34
  358.9 27.4 %collective-permute-start.35 = (bf16[512,1024]{1,0:T(8,128)(2,1)}, bf16[512,1024]{1,0:T(8,128)(2,1)S(1)}, u32[]{:S(2)}, u32[]{:S(2)}) collective-permute-start(bf16[512,1024]{1,0:T(8,128)(2,1)} %get-tuple-element.131), channel_id=1, source_target_pairs={{16,0},{17,1},{18,2},{19,3},{20,4},{21,5},{22,6},{23,7},{24,8},{25... | collective-permute-start | bytes 3145736 | tf_op jit(solution)/shard_map/ppermute | solution.py:28
  361.7 30.6 %all-to-all-start.1 = ((bf16[4,128,1024]{2,1,0:T(8,128)(2,1)}), bf16[4,128,1024]{2,1,0:T(8,128)(2,1)}, u32[]{:S(2)}, u32[]{:S(2)}) async-start(bf16[4,128,1024]{2,1,0:T(8,128)(2,1)} %bitcast.44), calls=%async_computation.1 | async-start | bytes 2097152 | tf_op jit(solution)/shard_map/all_to_all | solution.py:1140
  391.4 3.0 collective-permute-start.36
  423.7 26.1 %collective-permute-start.40 = (bf16[1024,512]{1,0:T(8,128)(2,1)S(1)}, bf16[1024,512]{1,0:T(8,128)(2,1)S(1)}, u32[]{:S(2)}, u32[]{:S(2)}) collective-permute-start(bf16[1024,512]{1,0:T(8,128)(2,1)S(1)} %get-tuple-element.148), channel_id=1, source_target_pairs={{0,8},{4,12},{8,0},{12,4},{1,9},{5,13},{9,1},{13,5},{2,10},{6,14},... | collective-permute-start | bytes 3145736 | tf_op jit(solution)/shard_map/ppermute | solution.py:755
  429.8 30.9 %collective-permute-start.37 = (bf16[512,1024]{1,0:T(8,128)(2,1)S(1)}, bf16[512,1024]{1,0:T(8,128)(2,1)S(1)}, u32[]{:S(2)}, u32[]{:S(2)}) collective-permute-start(bf16[512,1024]{1,0:T(8,128)(2,1)S(1)} %get-tuple-element.139), channel_id=1, source_target_pairs={{0,4},{4,0},{8,12},{12,8},{1,5},{5,1},{9,13},{13,9},{2,6},{6,2},{1... | collective-permute-start | bytes 3145736 | tf_op jit(solution)/shard_map/ppermute | solution.py:755
  429.9 42.4 %collective-permute-start.39 = (bf16[1024,512]{1,0:T(8,128)(2,1)}, bf16[1024,512]{1,0:T(8,128)(2,1)}, u32[]{:S(2)}, u32[]{:S(2)}) collective-permute-start(bf16[1024,512]{1,0:T(8,128)(2,1)} %get-tuple-element.147), channel_id=1, source_target_pairs={{0,8},{4,12},{8,0},{12,4},{1,9},{5,13},{9,1},{13,5},{2,10},{6,14},... | collective-permute-start | bytes 3145736 | tf_op jit(solution)/shard_map/ppermute | solution.py:755
  451.2 24.0 %collective-permute-start.41 = (bf16[1024,512]{1,0:T(8,128)(2,1)}, bf16[1024,512]{1,0:T(8,128)(2,1)}, u32[]{:S(2)}, u32[]{:S(2)}) collective-permute-start(bf16[1024,512]{1,0:T(8,128)(2,1)} %add_convert_fusion.2), channel_id=1, source_target_pairs={{0,3},{1,0},{2,1},{3,2},{4,7},{5,4},{6,5},{7,6},{8,11},{9,8},{10,9... | collective-permute-start | bytes 3145736 | tf_op jit(solution)/shard_map/ppermute | solution.py:760
  467.0 12.9 %collective-permute-start.38 = (bf16[512,1024]{1,0:T(8,128)(2,1)S(1)}, bf16[512,1024]{1,0:T(8,128)(2,1)S(1)}, u32[]{:S(2)}, u32[]{:S(2)}) collective-permute-start(bf16[512,1024]{1,0:T(8,128)(2,1)S(1)} %get-tuple-element.142.refs_3_.refs_5_), channel_id=1, source_target_pairs={{0,4},{4,0},{8,12},{12,8},{1,5},{5,1},{9,13},{13,9},{2,6},{6,2},{1... | collective-permute-start | bytes 3145736 | tf_op jit(solution)/shard_map/ppermute | solution.py:755
  467.1 50.0 %collective-permute-start.42 = (bf16[1024,512]{1,0:T(8,128)(2,1)S(1)}, bf16[1024,512]{1,0:T(8,128)(2,1)S(1)}, u32[]{:S(2)}, u32[]{:S(2)}) collective-permute-start(bf16[1024,512]{1,0:T(8,128)(2,1)S(1)} %copy-done.104), channel_id=1, source_target_pairs={{0,8},{4,12},{8,0},{12,4},{1,9},{5,13},{9,1},{13,5},{2,10},{6,14},... | collective-permute-start | bytes 3145736 | tf_op jit(solution)/shard_map/ppermute | solution.py:755
  468.7 72.7 %collective-permute-start.45 = (bf16[1024,512]{1,0:T(8,128)(2,1)S(1)}, bf16[1024,512]{1,0:T(8,128)(2,1)S(1)}, u32[]{:S(2)}, u32[]{:S(2)}) collective-permute-start(bf16[1024,512]{1,0:T(8,128)(2,1)S(1)} %copy-done.102), channel_id=1, source_target_pairs={{0,8},{4,12},{8,0},{12,4},{1,9},{5,13},{9,1},{13,5},{2,10},{6,14},... | collective-permute-start | bytes 3145736 | tf_op jit(solution)/shard_map/ppermute | solution.py:755
  477.5 39.6 %collective-permute-start.43 = (bf16[1024,512]{1,0:T(8,128)(2,1)S(1)}, bf16[1024,512]{1,0:T(8,128)(2,1)S(1)}, u32[]{:S(2)}, u32[]{:S(2)}) collective-permute-start(bf16[1024,512]{1,0:T(8,128)(2,1)S(1)} %add_convert_fusion.1), channel_id=1, source_target_pairs={{0,3},{1,0},{2,1},{3,2},{4,7},{5,4},{6,5},{7,6},{8,11},{9,8},{10,9... | collective-permute-start | bytes 3145736 | tf_op jit(solution)/shard_map/ppermute | solution.py:760
  523.0 18.4 %collective-permute-start.44 = (bf16[512,1024]{1,0:T(8,128)(2,1)S(1)}, bf16[512,1024]{1,0:T(8,128)(2,1)S(1)}, u32[]{:S(2)}, u32[]{:S(2)}) collective-permute-start(bf16[512,1024]{1,0:T(8,128)(2,1)S(1)} %get-tuple-element.154), channel_id=1, source_target_pairs={{0,4},{4,0},{8,12},{12,8},{1,5},{5,1},{9,13},{13,9},{2,6},{6,2},{1... | collective-permute-start | bytes 3145736 | tf_op jit(solution)/shard_map/ppermute | solution.py:755
  523.5 26.0 %collective-permute-start.46 = (bf16[1024,512]{1,0:T(8,128)(2,1)S(1)}, bf16[1024,512]{1,0:T(8,128)(2,1)S(1)}, u32[]{:S(2)}, u32[]{:S(2)}) collective-permute-start(bf16[1024,512]{1,0:T(8,128)(2,1)S(1)} %add_convert_fusion), channel_id=1, source_target_pairs={{0,3},{1,0},{2,1},{3,2},{4,7},{5,4},{6,5},{7,6},{8,11},{9,8},{10,9... | collective-permute-start | bytes 3145736 | tf_op jit(solution)/shard_map/ppermute | solution.py:760
  524.1 14.8 %collective-permute-start.52 = (bf16[512,512]{1,0:T(8,128)(2,1)S(1)}, bf16[512,512]{1,0:T(8,128)(2,1)S(1)}, u32[]{:S(2)}, u32[]{:S(2)}) collective-permute-start(bf16[512,512]{1,0:T(8,128)(2,1)S(1)} %get-tuple-element.175), channel_id=1, source_target_pairs={{0,8},{4,12},{8,0},{12,4},{1,9},{5,13},{9,1},{13,5},{2,10},{6,14},... | collective-permute-start | bytes 1572872 | tf_op jit(solution)/shard_map/ppermute | solution.py:755
  525.6 31.4 %collective-permute-start.51 = (bf16[512,512]{1,0:T(8,128)(2,1)}, bf16[512,512]{1,0:T(8,128)(2,1)}, u32[]{:S(2)}, u32[]{:S(2)}) collective-permute-start(bf16[512,512]{1,0:T(8,128)(2,1)} %get-tuple-element.174), channel_id=1, source_target_pairs={{0,8},{4,12},{8,0},{12,4},{1,9},{5,13},{9,1},{13,5},{2,10},{6,14},... | collective-permute-start | bytes 1572872 | tf_op jit(solution)/shard_map/ppermute | solution.py:755
  538.8 27.7 %collective-permute-start.50 = (bf16[512,512]{1,0:T(8,128)(2,1)}, bf16[512,512]{1,0:T(8,128)(2,1)}, u32[]{:S(2)}, u32[]{:S(2)}) collective-permute-start(bf16[512,512]{1,0:T(8,128)(2,1)} %get-tuple-element.172), channel_id=1, source_target_pairs={{0,8},{4,12},{8,0},{12,4},{1,9},{5,13},{9,1},{13,5},{2,10},{6,14},... | collective-permute-start | bytes 1572872 | tf_op jit(solution)/shard_map/ppermute | solution.py:755
  541.3 19.6 %collective-permute-start.53 = (bf16[512,512]{1,0:T(8,128)(2,1)}, bf16[512,512]{1,0:T(8,128)(2,1)}, u32[]{:S(2)}, u32[]{:S(2)}) collective-permute-start(bf16[512,512]{1,0:T(8,128)(2,1)} %add_convert_fusion.5), channel_id=1, source_target_pairs={{0,3},{1,0},{2,1},{3,2},{4,7},{5,4},{6,5},{7,6},{8,11},{9,8},{10,9... | collective-permute-start | bytes 1572872 | tf_op jit(solution)/shard_map/ppermute | solution.py:760
  553.3 59.6 %all-to-all-start.2 = ((bf16[4,128,1024]{2,1,0:T(8,128)(2,1)}), bf16[4,128,1024]{2,1,0:T(8,128)(2,1)S(1)}, u32[]{:S(2)}, u32[]{:S(2)}) async-start(bf16[4,128,1024]{2,1,0:T(8,128)(2,1)} %bitcast.43), calls=%async_computation.2 | async-start | bytes 2097152 | tf_op jit(solution)/shard_map/all_to_all | solution.py:1214
  562.7 25.8 %collective-permute-start.54 = (bf16[512,512]{1,0:T(8,128)(2,1)S(1)}, bf16[512,512]{1,0:T(8,128)(2,1)S(1)}, u32[]{:S(2)}, u32[]{:S(2)}) collective-permute-start(bf16[512,512]{1,0:T(8,128)(2,1)S(1)} %add_convert_fusion.4), channel_id=1, source_target_pairs={{0,3},{1,0},{2,1},{3,2},{4,7},{5,4},{6,5},{7,6},{8,11},{9,8},{10,9... | collective-permute-start | bytes 1572872 | tf_op jit(solution)/shard_map/ppermute | solution.py:760
  565.0 27.1 %collective-permute-start.49 = (bf16[512,512]{1,0:T(8,128)(2,1)S(1)}, bf16[512,512]{1,0:T(8,128)(2,1)S(1)}, u32[]{:S(2)}, u32[]{:S(2)}) collective-permute-start(bf16[512,512]{1,0:T(8,128)(2,1)S(1)} %copy-done.121), channel_id=1, source_target_pairs={{0,8},{4,12},{8,0},{12,4},{1,9},{5,13},{9,1},{13,5},{2,10},{6,14},... | collective-permute-start | bytes 1572872 | tf_op jit(solution)/shard_map/ppermute | solution.py:755
  589.7 17.1 %collective-permute-start.55 = (bf16[512,512]{1,0:T(8,128)(2,1)S(1)}, bf16[512,512]{1,0:T(8,128)(2,1)S(1)}, u32[]{:S(2)}, u32[]{:S(2)}) collective-permute-start(bf16[512,512]{1,0:T(8,128)(2,1)S(1)} %add_convert_fusion.3), channel_id=1, source_target_pairs={{0,3},{1,0},{2,1},{3,2},{4,7},{5,4},{6,5},{7,6},{8,11},{9,8},{10,9... | collective-permute-start | bytes 1572872 | tf_op jit(solution)/shard_map/ppermute | solution.py:760
  608.5 25.2 %collective-permute-start.56 = (f32[256,512]{1,0:T(8,128)}, f32[256,512]{1,0:T(8,128)}, u32[]{:S(2)}, u32[]{:S(2)}) collective-permute-start(f32[256,512]{1,0:T(8,128)} %get-tuple-element.177), channel_id=1, source_target_pairs={{0,4},{4,0},{8,12},{12,8},{1,5},{5,1},{9,13},{13,9},{2,6},{6,2},{1... | collective-permute-start | bytes 1572872 | tf_op jit(solution)/shard_map/ppermute | solution.py:755
  610.6 29.5 %collective-permute-start.47 = (bf16[2,128,1024]{2,1,0:T(8,128)(2,1)}, bf16[2,128,1024]{2,1,0:T(8,128)(2,1)}, u32[]{:S(2)}, u32[]{:S(2)}) collective-permute-start(bf16[2,128,1024]{2,1,0:T(8,128)(2,1)} %get-tuple-element.159), channel_id=1, source_target_pairs={{0,4},{4,0},{8,12},{12,8},{1,5},{5,1},{9,13},{13,9},{2,6},{6,2},{1... | collective-permute-start | bytes 1572872 | tf_op jit(solution)/shard_map/ppermute | solution.py:755
  612.4 29.9 %collective-permute-start.57 = (f32[256,512]{1,0:T(8,128)}, f32[256,512]{1,0:T(8,128)}, u32[]{:S(2)}, u32[]{:S(2)}) collective-permute-start(f32[256,512]{1,0:T(8,128)} %get-tuple-element.183), channel_id=1, source_target_pairs={{0,4},{4,0},{8,12},{12,8},{1,5},{5,1},{9,13},{13,9},{2,6},{6,2},{1... | collective-permute-start | bytes 1572872 | tf_op jit(solution)/shard_map/ppermute | solution.py:755
  612.4 29.9 %collective-permute-start.58 = (f32[512,256]{1,0:T(8,128)}, f32[512,256]{1,0:T(8,128)}, u32[]{:S(2)}, u32[]{:S(2)}) collective-permute-start(f32[512,256]{1,0:T(8,128)} %get-tuple-element.184), channel_id=1, source_target_pairs={{0,4},{4,0},{8,12},{12,8},{1,5},{5,1},{9,13},{13,9},{2,6},{6,2},{1... | collective-permute-start | bytes 1572872 | tf_op jit(solution)/shard_map/ppermute | solution.py:755
  614.6 30.5 %collective-permute-start.48 = (bf16[2,128,1024]{2,1,0:T(8,128)(2,1)}, bf16[2,128,1024]{2,1,0:T(8,128)(2,1)S(1)}, u32[]{:S(2)}, u32[]{:S(2)}) collective-permute-start(bf16[2,128,1024]{2,1,0:T(8,128)(2,1)} %get-tuple-element.161), channel_id=1, source_target_pairs={{0,4},{4,0},{8,12},{12,8},{1,5},{5,1},{9,13},{13,9},{2,6},{6,2},{1... | collective-permute-start | bytes 1572872 | tf_op jit(solution)/shard_map/ppermute | solution.py:755
  (130 other events, 3906.9 us)

commit v8 on v7

--- a/solution.py
+++ b/solution.py
@@ -544,14 +544,33 @@
 
 def mlp_up_back_kernel(pieces, own_rows, other_rows, slope_ref, *refs):
     owns, others = refs[:pieces], refs[pieces : 2 * pieces]
-    out_ref = refs[-1]
+    out_ref, weight, slope, sems = refs[2 * pieces :]
+    half = own_rows.shape[1] // 2
     size = owns[0].shape[0]
+    order = list(reversed(range(pieces)))
+    copies = []
+    for j in order:
+        sources = (owns[j], others[j], slope_ref.at[:, pl.ds(j * size, size)])
+        targets = (
+            weight.at[j, :, pl.ds(0, half)],
+            weight.at[j, :, pl.ds(half, half)],
+            slope.at[:, pl.ds(j * size, size)],
+        )
+        copies.append(
+            [
+                pltpu.make_async_copy(source, target, sems.at[j, i])
+                for i, (source, target) in enumerate(zip(sources, targets))
+            ]
+        )
+        for copy in copies[-1]:
+            copy.start()
     rows = stacked_up([own_rows[...], other_rows[...]])
-    for j in range(pieces):
+    for j, arriving in zip(order, copies):
         cols = slice(j * size, (j + 1) * size)
-        weight = jnp.concatenate([owns[j][...], others[j][...]], axis=1)
-        d_gelu = dot_nt(rows, weight)
-        out_ref[:, cols] = (d_gelu * slope_ref[:, cols].astype(jnp.float32)).astype(jnp.bfloat16)
+        for copy in arriving:
+            copy.wait()
+        d_gelu = dot_nt(rows, weight[j])
+        out_ref[:, cols] = (d_gelu * slope[:, cols].astype(jnp.float32)).astype(jnp.bfloat16)
 
 
 def inverse_size(rows):
@@ -696,6 +715,26 @@
         cost_estimate=work(flops, (*operands, *pieces[0], *pieces[1], *shapes)),
         name=name,
     )(core, *operands, *pieces[0], *pieces[1], *[array for array, _ in blocks], *waits)
+
+
+def mlp_up_back(rows, slope, pieces, waits):
+    length, units = slope.shape
+    unit, half = pieces[0][0].shape
+    count = len(pieces[0])
+    every, space = pl.BlockSpec(memory_space=pl.ANY), pl.BlockSpec(memory_space=pltpu.VMEM)
+    return pl.pallas_call(
+        without(functools.partial(mlp_up_back_kernel, count), 3 + 2 * count, len(waits)),
+        in_specs=[space] * 2 + [every] * (1 + 2 * count + len(waits)),
+        out_specs=space,
+        out_shape=jax.ShapeDtypeStruct((length, units), jnp.bfloat16),
+        scratch_shapes=[
+            pltpu.VMEM((count, unit, 2 * half), jnp.bfloat16),
+            pltpu.VMEM((length, units), jnp.bfloat16),
+            pltpu.SemaphoreType.DMA((count, 3)),
+        ],
+        compiler_params=pltpu.CompilerParams(vmem_limit_bytes=KERNEL_VMEM),
+        name="mlp_up_back",
+    )(*rows, slope, *pieces[0], *pieces[1], *waits)
 
 
 def attend(core, tables, rows, pieces, waits):
@@ -771,14 +810,14 @@
 
         @pl.when(first_ref[0] == section)
         def _():
-            copies = [
-                pltpu.make_async_copy(source, buffer, sems.at[i])
-                for i, (source, buffer) in enumerate(zip(sources, buffers))
-            ]
-            for copy in copies:
-                copy.start()
-            for copy in copies:
-                copy.wait()
+            for i, (source, buffer) in enumerate(zip(sources, buffers)):
+                pltpu.make_async_copy(source, buffer, sems.at[i]).start()
+
+    def arrived(*places):
+        for i in places:
+            pltpu.make_async_copy(zeros[i], buffers[i], sems.at[i]).wait()
+
+    return arrived
 
 
 def mlp_grads_kernel(base, section_ref, *refs):
@@ -799,12 +838,16 @@
         d_down.at[pl.ds(0, count)],
         d_down.at[pl.ds(count, count)],
     )
-    fetch(section_ref, parts(*refs[:6]), parts(*refs[6:12]), buffers, sems)
+    arrived = fetch(section_ref, parts(*refs[:6]), parts(*refs[6:12]), buffers, sems)
     for j, own, other in ((1, own_two, other_two), (0, own_one, other_one)):
         cols = slice(j * size, (j + 1) * size)
+        if j == 1:
+            arrived(0, 1, 2)
         up = dot_tn(rows[...], d_up[:, cols])
         own[:half] = up[:half]
         other[:half] = up[half:].astype(jnp.bfloat16)
+        if j == 1:
+            arrived(3, 4, 5)
         down = dot_tn(gelu[:, cols], d_down[...])
         own[half:] = down[:, :half]
         other[half:] = down[:, half:].astype(jnp.bfloat16)
@@ -827,9 +870,13 @@
         d_attn.at[pl.ds(0, count)],
         d_attn.at[pl.ds(count, count)],
     )
-    fetch(section_ref, parts(*refs[:6]), parts(*refs[6:12]), buffers, sems)
+    arrived = fetch(section_ref, parts(*refs[:6]), parts(*refs[6:12]), buffers, sems)
     for j, own, other in ((1, own_two, other_two), (0, own_one, other_one)):
+        if j == 1:
+            arrived(0, 1, 2)
         qkv = dot_tn(rows[...], d_qkv[:, j * size : (j + 1) * size])
+        if j == 1:
+            arrived(3, 4, 5)
         out = dot_tn(d_attn[...], mixed[:, j * 128 : (j + 1) * 128])
         own[:, :size] = qkv[:half]
         own[:, size:] = out[:half]
@@ -865,6 +912,20 @@
     return [(first, flip_pairs(second, 2)), (third, flip_pairs(fourth, 2))]
 
 
+def moved_kernel(own_ref, other_ref, *refs):
+    out_ref = refs[-1]
+
+    def body(i, carry):
+        spot = pl.ds(pl.multiple_of(i * CHUNK, CHUNK), CHUNK)
+        total = own_ref[spot, :]
+        for ref in (other_ref, *refs[:-1]):
+            total = total + wide(ref, spot)
+        out_ref[spot, :] = total.astype(jnp.bfloat16)
+        return carry
+
+    lax.fori_loop(0, own_ref.shape[0] // CHUNK, body, 0)
+
+
 def gate_kernel(up_ref, down_ref, up_out, down_out):
     up_out[...] = up_ref[...]
     down_out[...] = down_ref[...]
@@ -1028,13 +1089,14 @@
     attn_own = spread(attn_piece)
     attn_other = [flip_pairs(piece, 2) for piece in attn_own]
     up_piece, down_piece = columns(up_weight[0]), rows(down_weight[0])
+    up_other, down_other = [flip_pairs(up_piece, 2)], [flip_pairs(down_piece, 2)]
     outs = tuple((piece.shape, piece.dtype) for piece in (up_piece, down_piece))
     up_piece, down_piece = on_chip(
-        gate_kernel, "gate", outs, up_piece, down_piece, waits=(attn_own[2],)
+        gate_kernel, "gate", outs, up_piece, down_piece, waits=(attn_own[2], attn_other[0])
     )
     up_own, down_own = spread(up_piece), spread(down_piece)
-    up_other = [flip_pairs(piece, 2) for piece in up_own]
-    down_other = [flip_pairs(piece, 2) for piece in down_own]
+    up_other += [flip_pairs(piece, 2) for piece in up_own[1:]]
+    down_other += [flip_pairs(piece, 2) for piece in down_own[1:]]
     w_attn, w_up, w_down = (attn_own, attn_other), (up_own, up_other), (down_own, down_other)
     unit = up_piece.shape[1]
     units = tensor * unit
@@ -1095,9 +1157,7 @@
             into_mlp_back_kernel, "into_mlp_back", (row16, sum32), *operands
         )
         d_down = both_rows(d_down)
-        kernel = functools.partial(mlp_up_back_kernel, tensor)
-        operands = (*d_down, slope, *w_down[0], *w_down[1])
-        (d_up,) = on_chip(kernel, "mlp_up_back", (unit16,), *operands, **mlp_cost, waits=late)
+        d_up = mlp_up_back(d_down, slope, w_down, late)
         waits = hook(d_down, d_up)
         parts = model_rows(model_kernel(every), "mlp_back", [d_up], w_up, waits)
         waits = hook()
@@ -1125,10 +1185,10 @@
     low_zero, saved_zero, lefts_zero = forward(
         start,
         (
-            (up_piece,),
+            (up_piece, up_other[0], down_other[0]),
             (up_own[1], down_own[1]),
-            (up_own[2], down_own[2], up_other[0], down_other[0]),
-            (up_own[3], down_own[3], up_other[1], down_other[1]),
+            (up_own[2], down_own[2], up_other[1], down_other[1]),
+            (up_own[3], down_own[3], up_other[2], down_other[2]),
         ),
     )
     low_one, saved_one, lefts_one = forward(shifted(low_zero, "section", 1), ((),) * 4)
@@ -1169,12 +1229,10 @@
             (768, 256),
         )
 
-    def moves_on(piece, moved=None):
-        own, other = piece
-        total = own + other.astype(jnp.float32)
-        if moved is not None:
-            total = total + moved.astype(jnp.float32)
-        return passed_on(total.astype(jnp.bfloat16), -1)
+    def moves_on(piece, *moved, waits=()):
+        outs = ((piece[1].shape, jnp.bfloat16),)
+        (total,) = on_chip(moved_kernel, "moved", outs, *piece, *moved, waits=waits)
+        return passed_on(total, -1)
 
     mlp_sums, attn_sums = [None] * tensor, [None] * tensor
     mlp_moves, attn_moves = [None] * tensor, [None] * tensor
@@ -1192,26 +1250,31 @@
             return (mlp_sums[1][0],)
         if turn == 2:
             (d_attn,) = new
+            mlp_moves[3] = moves_on(mlp_sums[3], waits=d_attn[:1])
             return (mlp_sums[3][1],)
         if turn == 3:
-            mlp_moves[3] = moves_on(mlp_sums[3])
+            mlp_moves[2] = moves_on(mlp_sums[2], mlp_moves[3], waits=new)
             attn_leaves(2, new[0])
             return (mlp_sums[2][1], mlp_moves[3], attn_sums[3][0])
         if turn == 4:
-            mlp_moves[2] = moves_on(mlp_sums[2], mlp_moves[3])
+            mlp_moves[1] = moves_on(mlp_sums[1], mlp_moves[2], waits=new)
             attn_leaves(0, new[0])
             return (mlp_sums[1][1], mlp_moves[2], attn_sums[1][0])
-        mlp_moves[1] = moves_on(mlp_sums[1], mlp_moves[2])
-        return (mlp_sums[0][1], mlp_moves[1])
+        return (mlp_sums[0][1], attn_sums[3][1], attn_sums[2][1])
 
     d_down = d_up = d_attn = None
     grad_zero, rights_zero, gain_zero = backward(received, saved_zero, hook, (lows,))
     attn_moves[3] = moves_on(attn_sums[3])
     attn_moves[2] = moves_on(attn_sums[2], attn_moves[3])
     attn_moves[1] = moves_on(attn_sums[1], attn_moves[2])
-    outputs = from_chip(lows, (grad_zero,))
+    gain_total = own_first(jnp.where(first, gain_zero, gain_one))
+    count = tensor * lax.axis_size("dp")
+    gain_parts = gain_total.reshape(4, count, width // count).swapaxes(0, 1)
+    gain_parts = lax.all_to_all(gain_parts, ("dp", "tensor"), 0, 0, tiled=True)
+    gains_grad = jnp.sum(gain_parts, axis=0)
+    outputs = from_chip(lows, (grad_zero, attn_sums[1][1]))
     grads = own_first(jnp.where(first, grad_zero, grad_one)).reshape(tensor, part, width)
-    grads = from_chip(lax.all_to_all(grads, "tensor", 0, 0, tiled=True))
+    grads = from_chip(lax.all_to_all(grads, "tensor", 0, 0, tiled=True), attn_sums[0][1:])
 
     block32 = ((wide_half // 2, unit), jnp.float32)
     down32 = ((unit, wide_half // 2), jnp.float32)
@@ -1233,7 +1296,13 @@
     )
     outs = (((wide_half // 2, 512), jnp.float32),) * 2
     keep, send = with_core(
-        last_sum_kernel, "attn_sum", core_word, outs, *attn_sums[0], attn_moves[1]
+        last_sum_kernel,
+        "attn_sum",
+        core_word,
+        outs,
+        *attn_sums[0],
+        attn_moves[1],
+        waits=(outputs, grads, gain_parts, up_grad),
     )
     spots = tuple((i * 128, (i + 1) * 128, i * 256) for i in range(3))
     outs = (((wide_half // 2, 768), jnp.float32), ((256, wide_half // 2), jnp.float32))
@@ -1243,11 +1312,6 @@
     )
     qkv_grad = qkv_grad.reshape(wide_half // 2, 3, -1)
 
-    gain_total = own_first(jnp.where(first, gain_zero, gain_one))
-    count = tensor * lax.axis_size("dp")
-    gain_parts = gain_total.reshape(4, count, width // count).swapaxes(0, 1)
-    gain_parts = lax.all_to_all(gain_parts, ("dp", "tensor"), 0, 0, tiled=True)
-    gains_grad = jnp.sum(gain_parts, axis=0)
     return (
         outputs[None],
         grads[None],

time: 656 us -> 667 us (1.017)
  waiting for transfers between devices: 279 us -> 261 us
  Pallas kernels: 219 us -> 233 us
  starting transfers between devices: 65 us -> 75.8 us
  local copies, waits for them, and re-layouts: 43.2 us -> 53.4 us
    ppermute x42, waiting for transfers between devices: 131 us -> 99.5 us  [flip_pairs(): return lax.ppermute(block, 'dp', [(i, i ^ distance) for i in range(size)])]
    pallas_call x0 -> x2, Pallas kernels: none -> 16 us  [mlp_up_back(): pl.pallas_call(without(functools.partial(mlp_up_back_kernel, count), 3 +...]
    ppermute x15, waiting for transfers between devices: 104 us -> 119 us  [passed_on(): lax.ppermute(block, 'tensor', [(i, (i + step) % size) for i in range(size)])]
    ppermute x15, starting transfers between devices: 19.9 us -> 29 us  [passed_on(): lax.ppermute(block, 'tensor', [(i, (i + step) % size) for i in range(size)])]
    convert_element_type x6 -> x0, other arithmetic: 8.27 us -> none  [moves_on(): return passed_on(total.astype(jnp.bfloat16), -1)]
    unnamed x268 -> x308, local copies, waits for them, and re-layouts: 36.6 us -> 44.2 us
    pallas_call x25 -> x29, Pallas kernels: 94.9 us -> 94.5 us  [on_chip(): pl.pallas_call(without(kernel, len(operands), len(waits)), in_specs=[spac...]
  transfers between devices with their start and end apart: 62 -> 62, of which waited for: 37 -> 37; matrix products, arithmetic and copies ran while one was open for 4% -> 3% of each run, Pallas kernels for 16% -> 16%
where the time goes in v8:
time: 667 us; the launch traced here: 657 us
  waiting for transfers between devices  261 us (39%)
  Pallas kernels  233 us (35%)
  starting transfers between devices  75.8 us (11%)
  local copies, waits for them, and re-layouts  53.4 us (8%)
  other arithmetic  20.7 us (3%)
  blocking collectives  10.2 us (2%)
    ppermute x15, waiting for transfers between devices, passed_on(): lax.ppermute(block, 'tensor', [(i, (i + step) % size) for i in range(size)])  119 us
    ppermute x42, waiting for transfers between devices, flip_pairs(): return lax.ppermute(block, 'dp', [(i, i ^ distance) for i in range(size)])  99.5 us
    pallas_call x29, Pallas kernels, on_chip(): pl.pallas_call(without(kernel, len(operands), len(waits)), in_specs=[spac...  94.5 us
    pallas_call x6, Pallas kernels, by_pairs(): pl.pallas_call(without(functools.partial(kernel, len(pieces[0])), taken,...  85.2 us
    unnamed x308, local copies, waits for them, and re-layouts  44.2 us
    ppermute x2, waiting for transfers between devices, shifted(): return lax.ppermute(block, axis, route)  41.8 us
    ppermute x15, starting transfers between devices, passed_on(): lax.ppermute(block, 'tensor', [(i, (i + step) % size) for i in range(size)])  29 us
    ppermute x42, starting transfers between devices, flip_pairs(): return lax.ppermute(block, 'dp', [(i, i ^ distance) for i in range(size)])  26.4 us
  transfers between devices with their start and end apart: 62, of which 37 were waited for; matrix products, arithmetic and copies ran while one was open for 3% of the time, Pallas kernels for 16%

profile of v8, /device:TPU:0, one launch (start us, length us, event | category | flops | bytes accessed | tf_op | source)
XLA Modules:
  0.0 656.6 jit_solution(5454143245842633084)
XLA Ops:
  11.4 6.2 all-to-all-start
  27.8 22.6 %collective-permute-done.1.refs_6_.refs_2_.refs_3_ = bf16[512,512]{1,0:T(8,128)(2,1)} collective-permute-done((bf16[512,512]{1,0:T(8,128)(2,1)}, bf16[512,512]{1,0:T(8,128)(2,1)}, u32[]{:S(2)}, u32[]{:S(2)}) %collective-permute-start.1) | collective-permute-done | bytes 524320 | tf_op jit(solution)/shard_map/ppermute | solution.py:799
  50.4 3.3 collective-permute-start.2
  58.5 7.0 %collective-permute-done.2.refs_2_.refs_7_.refs_3_.refs_5_.refs_4_ = bf16[512,512]{1,0:T(8,128)(2,1)} collective-permute-done((bf16[512,512]{1,0:T(8,128)(2,1)}, bf16[512,512]{1,0:T(8,128)(2,1)}, u32[]{:S(2)}, u32[]{:S(2)}) %collective-permute-start.2) | collective-permute-done | bytes 524320 | tf_op jit(solution)/shard_map/ppermute | solution.py:799
  69.5 10.4 %collective-permute-done.5.refs_4_.refs_5_.refs_7_ = bf16[512,512]{1,0:T(8,128)(2,1)S(1)} collective-permute-done((bf16[512,512]{1,0:T(8,128)(2,1)S(1)}, bf16[512,512]{1,0:T(8,128)(2,1)S(1)}, u32[]{:S(2)}, u32[]{:S(2)}) %collective-permute-start.5) | collective-permute-done | bytes 524320 | tf_op jit(solution)/shard_map/ppermute | solution.py:794
  84.1 2.5 collective-permute-start.11
  93.7 7.2 %collective-permute-done.11.refs_13_.refs_3_.refs_2_ = bf16[512,512]{1,0:T(8,128)(2,1)S(1)} collective-permute-done((bf16[512,512]{1,0:T(8,128)(2,1)}, bf16[512,512]{1,0:T(8,128)(2,1)S(1)}, u32[]{:S(2)}, u32[]{:S(2)}) %collective-permute-start.11) | collective-permute-done | bytes 524320 | tf_op jit(solution)/shard_map/ppermute | solution.py:799
  105.4 6.7 %collective-permute-done.12.refs_14_.refs_2_.refs_4_ = bf16[512,512]{1,0:T(8,128)(2,1)S(1)} collective-permute-done((bf16[512,512]{1,0:T(8,128)(2,1)}, bf16[512,512]{1,0:T(8,128)(2,1)S(1)}, u32[]{:S(2)}, u32[]{:S(2)}) %collective-permute-start.12) | collective-permute-done | bytes 524320 | tf_op jit(solution)/shard_map/ppermute | solution.py:799
  117.7 17.0 %attend.2 = (bf16[4,1024,128]{2,1,0:T(8,128)(2,1)S(1)}, bf16[4,1024,128]{2,1,0:T(8,128)(2,1)S(1)}, bf16[4,1024,128]{2,1,0:T(8,128)(2,1)S(1)}, f32[4,2,1024]{2,1,0:T(2,128)S(1)}, bf16[1024,512]{1,0:T(8,128)(2,1)S(1)}) custom-call(s32[1]{0:T(128)} %bitcast.refs_0_, f32[1024,128]{1,0:T(8,128)S(1)} %get-tuple-element.230.refs_1_, ...), custom_call_target="tpu_custom_call" | custom-call | flops 11811160064 | bytes 11567104 | tf_op jit(solution)/shard_map/attend/pallas_call | solution.py:704
  137.7 4.0 attn_out.2
  141.8 2.5 collective-permute-start.18
  146.8 11.5 %collective-permute-done.18.refs_4_.refs_5_ = bf16[512,512]{1,0:T(8,128)(2,1)S(1)} collective-permute-done((bf16[512,512]{1,0:T(8,128)(2,1)S(1)}, bf16[512,512]{1,0:T(8,128)(2,1)S(1)}, u32[]{:S(2)}, u32[]{:S(2)}) %collective-permute-start.18) | collective-permute-done | bytes 524320 | tf_op jit(solution)/shard_map/ppermute | solution.py:799
  158.4 10.8 %collective-permute-done.19.refs_5_.refs_4_.refs_6_ = bf16[512,512]{1,0:T(8,128)(2,1)S(1)} collective-permute-done((bf16[512,512]{1,0:T(8,128)(2,1)S(1)}, bf16[512,512]{1,0:T(8,128)(2,1)S(1)}, u32[]{:S(2)}, u32[]{:S(2)}) %collective-permute-start.19) | collective-permute-done | bytes 524320 | tf_op jit(solution)/shard_map/ppermute | solution.py:799
  169.8 3.4 after_attn.2
  175.5 12.7 %collective-permute-done.23.refs_9_.refs_8_ = bf16[512,512]{1,0:T(8,128)(2,1)S(1)} collective-permute-done((bf16[512,512]{1,0:T(8,128)(2,1)S(1)}, bf16[512,512]{1,0:T(8,128)(2,1)S(1)}, u32[]{:S(2)}, u32[]{:S(2)}) %collective-permute-start.23) | collective-permute-done | bytes 524320 | tf_op jit(solution)/shard_map/ppermute | solution.py:794
  188.2 7.7 %mlp_up.2 = (bf16[1024,2048]{1,0:T(8,128)(2,1)S(1)}, bf16[1024,2048]{1,0:T(8,128)(2,1)S(1)}) custom-call(bf16[512,1024]{1,0:T(8,128)(2,1)S(1)} %get-tuple-element.103.refs_0_.refs_1_, bf16[512,1024]{1,0:T(8,128)(2,1)S(1)} %collective-permute-done.22.refs_1_.refs_2_, bf16[512,512]{1,0:T(8,128)(2,1)S(1)} %copy-done.116, ...), custom_call_target="tpu_custom_call" | custom-call | flops 4294967296 | bytes 14680064 | tf_op jit(solution)/shard_map/mlp_up/pallas_call | solution.py:686
  199.0 4.5 mlp_down.2
  203.5 2.6 collective-permute-done.25.refs_3_
  208.1 3.6 collective-permute-start.26
  211.6 22.2 %collective-permute-done.26.refs_1_ = bf16[512,1024]{1,0:T(8,128)(2,1)S(1)} collective-permute-done((bf16[512,1024]{1,0:T(8,128)(2,1)S(1)}, bf16[512,1024]{1,0:T(8,128)(2,1)S(1)}, u32[]{:S(2)}, u32[]{:S(2)}) %collective-permute-start.26) | collective-permute-done | bytes 1048608 | tf_op jit(solution)/shard_map/ppermute | solution.py:28
  235.7 2.6 collective-permute-done.27.refs_4_.refs_8_
  238.4 16.9 %attend.3 = (bf16[4,1024,128]{2,1,0:T(8,128)(2,1)S(1)}, bf16[4,1024,128]{2,1,0:T(8,128)(2,1)S(1)}, bf16[4,1024,128]{2,1,0:T(8,128)(2,1)S(1)}, f32[4,2,1024]{2,1,0:T(2,128)S(1)}, bf16[1024,512]{1,0:T(8,128)(2,1)S(1)}) custom-call(s32[1]{0:T(128)} %bitcast.refs_0_, f32[1024,128]{1,0:T(8,128)S(1)} %get-tuple-element.230.refs_1_, ...), custom_call_target="tpu_custom_call" | custom-call | flops 11811160064 | bytes 11567104 | tf_op jit(solution)/shard_map/attend/pallas_call | solution.py:704
  256.3 3.3 attn_out.3
  259.8 2.5 collective-permute-done.28.refs_3_
  262.4 3.4 after_attn.3
  266.0 2.5 collective-permute-done.29.refs_1_.refs_8_
  268.5 7.7 %mlp_up.3 = (bf16[1024,2048]{1,0:T(8,128)(2,1)S(1)}, bf16[1024,2048]{1,0:T(8,128)(2,1)S(1)}) custom-call(bf16[512,1024]{1,0:T(8,128)(2,1)S(1)} %get-tuple-element.112.refs_0_.refs_7_, bf16[512,1024]{1,0:T(8,128)(2,1)S(1)} %collective-permute-done.29.refs_1_.refs_8_, bf16[512,512]{1,0:T(8,128)(2,1)S(1)} %copy-done.116, ...), custom_call_target="tpu_custom_call" | custom-call | flops 4294967296 | bytes 14680064 | tf_op jit(solution)/shard_map/mlp_up/pallas_call | solution.py:686
  276.3 4.5 mlp_down.3
  281.0 2.5 collective-permute-done.30.refs_3_
  287.7 2.5 collective-permute-done.31.refs_1_.refs_12_
  290.2 7.2 %mlp_up_back.2.refs_0_.refs_9_ = bf16[1024,2048]{1,0:T(8,128)(2,1)S(1)} custom-call(bf16[512,1024]{1,0:T(8,128)(2,1)S(1)} %get-tuple-element.118.refs_0_.refs_11_, bf16[512,1024]{1,0:T(8,128)(2,1)S(1)} %collective-permute-done.31.refs_1_.refs_12_, bf16[1024,2048]{1,0:T(8,128)(2,1)S(1)} %get-tuple-element.119.refs_2_, bf16[512,512]{1,0:T(8,128)(2,1)S(1)} %copy-done.69, ...), custom_call_target="tpu_custom_call" | custom-call | tf_op jit(solution)/shard_map/mlp_up_back/pallas_call | solution.py:725
  297.5 4.5 mlp_back.2
  304.8 3.9 into_attn_back.2
  308.9 2.5 collective-permute-done.33.refs_4_.refs_12_
  311.5 13.0 %attend_back.4.refs_0_.refs_9_ = bf16[1024,768]{1,0:T(8,128)(2,1)S(1)} custom-call(s32[1]{0:T(128)} %bitcast.refs_0_, f32[1024,128]{1,0:T(8,128)S(1)} %get-tuple-element.230.refs_1_, f32[1024,128]{1,0:T(8,128)S(1)} %get-tuple-element.231.refs_2_, bf16[512,1024]{1,0:T(8,128)(2,1)S(1)} %get-tuple-element.123.refs_3_.refs_11_, ...), custom_call_target="tpu_custom_call" | custom-call | flops 11274289152 | bytes 6815744 | tf_op jit(solution)/shard_map/attend_back/pallas_call | solution.py:704
  324.5 13.0 %attend_back.5.refs_1_.refs_9_ = bf16[1024,768]{1,0:T(8,128)(2,1)S(1)} custom-call(s32[1]{0:T(128)} %bitcast.refs_0_, f32[1024,128]{1,0:T(8,128)S(1)} %get-tuple-element.230.refs_1_, f32[1024,128]{1,0:T(8,128)S(1)} %get-tuple-element.231.refs_2_, bf16[512,1024]{1,0:T(8,128)(2,1)S(1)} %get-tuple-element.123.refs_3_.refs_11_, ...), custom_call_target="tpu_custom_call" | custom-call | flops 11274289152 | bytes 6815744 | tf_op jit(solution)/shard_map/attend_back/pallas_call | solution.py:704
  337.5 5.7 attn_back.2
  345.9 3.1 out_of_layer.2
  351.8 5.1 all-to-all-start.1
  357.0 19.6 %collective-permute-done.35.refs_1_ = bf16[512,1024]{1,0:T(8,128)(2,1)} collective-permute-done((bf16[512,1024]{1,0:T(8,128)(2,1)}, bf16[512,1024]{1,0:T(8,128)(2,1)}, u32[]{:S(2)}, u32[]{:S(2)}) %collective-permute-start.35) | collective-permute-done | bytes 1048608 | tf_op jit(solution)/shard_map/ppermute | solution.py:28
  378.1 4.3 into_mlp_back.3
  396.0 8.8 %mlp_up_back.3.refs_3_.refs_0_ = bf16[1024,2048]{1,0:T(8,128)(2,1)S(1)} custom-call(bf16[512,1024]{1,0:T(8,128)(2,1)} %get-tuple-element.135.refs_0_.refs_5_, bf16[512,1024]{1,0:T(8,128)(2,1)} %collective-permute-done.36.refs_1_.refs_6_, bf16[1024,2048]{1,0:T(8,128)(2,1)S(1)} %copy-done.49, bf16[512,512]{1,0:T(8,128)(2,1)S(1)} %copy-done.70, ...), custom_call_target="tpu_custom_call" | custom-call | tf_op jit(solution)/shard_map/mlp_up_back/pallas_call | solution.py:725
  406.1 6.2 mlp_grads.2
  412.5 5.5 mlp_back.3
  418.7 7.1 %mlp_grads.3 = (f32[1024,512]{1,0:T(8,128)S(1)}, bf16[1024,512]{1,0:T(8,128)(2,1)}, f32[1024,512]{1,0:T(8,128)S(1)}, bf16[1024,512]{1,0:T(8,128)(2,1)}) custom-call(s32[1]{0:T(128)} %bitcast.12.refs_0_, bf16[512,1024]{1,0:T(8,128)(2,1)S(1)} %copy-done.34, bf16[512,1024]{1,0:T(8,128)(2,1)S(1)} %copy-done.37, ...), custom_call_target="tpu_custom_call" | custom-call | tf_op jit(solution)/shard_map/mlp_grads/pallas_call | solution.py:893
  425.8 6.1 into_attn_back.3
  435.7 8.6 %collective-permute-done.40.refs_1_.refs_13_ = bf16[1024,512]{1,0:T(8,128)(2,1)S(1)} collective-permute-done((bf16[1024,512]{1,0:T(8,128)(2,1)}, bf16[1024,512]{1,0:T(8,128)(2,1)S(1)}, u32[]{:S(2)}, u32[]{:S(2)}) %collective-permute-start.40) | collective-permute-done | bytes 1048608 | tf_op jit(solution)/shard_map/ppermute | solution.py:794
  444.7 3.5 collective-permute-start.41
  448.3 12.7 %attend_back.6.refs_3_.refs_1_ = bf16[1024,768]{1,0:T(8,128)(2,1)S(1)} custom-call(s32[1]{0:T(128)} %bitcast.refs_0_, f32[1024,128]{1,0:T(8,128)S(1)} %copy-done.107, f32[1024,128]{1,0:T(8,128)S(1)} %copy-done.109, bf16[512,1024]{1,0:T(8,128)(2,1)S(1)} %get-tuple-element.142.refs_2_.refs_3_.refs_5_, ...), custom_call_target="tpu_custom_call" | custom-call | flops 11274289152 | bytes 6815744 | tf_op jit(solution)/shard_map/attend_back/pallas_call | solution.py:704
  461.0 5.8 collective-permute-done.39.refs_13_.refs_1_
  466.8 3.0 collective-permute-done.41.refs_14_.refs_2_
  470.4 4.3 collective-permute-start.43
  474.7 5.2 attn_grads.2
  480.9 12.8 %attend_back.7.refs_3_.refs_0_ = bf16[1024,768]{1,0:T(8,128)(2,1)S(1)} custom-call(s32[1]{0:T(128)} %bitcast.refs_0_, f32[1024,128]{1,0:T(8,128)S(1)} %copy-done.107, f32[1024,128]{1,0:T(8,128)S(1)} %copy-done.109, bf16[512,1024]{1,0:T(8,128)(2,1)S(1)} %get-tuple-element.142.refs_2_.refs_3_.refs_5_, ...), custom_call_target="tpu_custom_call" | custom-call | flops 11274289152 | bytes 6815744 | tf_op jit(solution)/shard_map/attend_back/pallas_call | solution.py:704
  494.6 5.6 attn_grads.3
  502.1 6.4 attn_back.3
  511.2 12.2 %collective-permute-done.46.refs_6_.refs_1_ = bf16[512,512]{1,0:T(8,128)(2,1)S(1)} collective-permute-done((bf16[512,512]{1,0:T(8,128)(2,1)S(1)}, bf16[512,512]{1,0:T(8,128)(2,1)S(1)}, u32[]{:S(2)}, u32[]{:S(2)}) %collective-permute-start.46) | collective-permute-done | bytes 524320 | tf_op jit(solution)/shard_map/ppermute | solution.py:794
  523.4 10.8 %collective-permute-done.47.refs_7_.refs_1_ = bf16[512,512]{1,0:T(8,128)(2,1)S(1)} collective-permute-done((bf16[512,512]{1,0:T(8,128)(2,1)S(1)}, bf16[512,512]{1,0:T(8,128)(2,1)S(1)}, u32[]{:S(2)}, u32[]{:S(2)}) %collective-permute-start.47) | collective-permute-done | bytes 524320 | tf_op jit(solution)/shard_map/ppermute | solution.py:794
  538.8 4.2 all-to-all-start.2
  547.4 3.9 collective-permute-start.55
  554.3 41.3 %collective-permute-done.52.refs_2_ = bf16[512,512]{1,0:T(8,128)(2,1)S(1)} collective-permute-done((bf16[512,512]{1,0:T(8,128)(2,1)S(1)}, bf16[512,512]{1,0:T(8,128)(2,1)S(1)}, u32[]{:S(2)}, u32[]{:S(2)}) %collective-permute-start.52) | collective-permute-done | bytes 524320 | tf_op jit(solution)/shard_map/ppermute | solution.py:799
  606.6 8.6 %collective-permute-done.53.refs_2_ = bf16[512,512]{1,0:T(8,128)(2,1)} collective-permute-done((bf16[512,512]{1,0:T(8,128)(2,1)}, bf16[512,512]{1,0:T(8,128)(2,1)}, u32[]{:S(2)}, u32[]{:S(2)}) %collective-permute-start.53) | collective-permute-done | bytes 524320 | tf_op jit(solution)/shard_map/ppermute | solution.py:799
  624.9 10.2 %all_to_all.20 = f32[16,1,256]{2,1,0:T(1,128)S(1)} all-to-all(f32[16,1,256]{2,1,0:T(1,128)S(1)} %reshape.144), channel_id=1, replica_groups=mesh['section'=2,'dp'=4,'tensor'=4] {'dp','tensor'}, dimensions={0} | all-to-all | bytes 32768 | tf_op jit(solution)/shard_map/all_to_all | solution.py:1273
  640.6 2.8 mlp_join.1
  (474 shorter events, 159.2 us)
Async XLA Ops:
  7.2 2.1 collective-permute-start
  11.4 68.5 %all-to-all-start = ((bf16[4,128,1024]{2,1,0:T(8,128)(2,1)}), bf16[4,128,1024]{2,1,0:T(8,128)(2,1)S(1)}, u32[]{:S(2)}, u32[]{:S(2)}) async-start(bf16[4,128,1024]{2,1,0:T(8,128)(2,1)} %pad_maximum_fusion), calls=%async_computation | async-start | bytes 2097152 | tf_op jit(solution)/shard_map/all_to_all | solution.py:1051
  24.2 26.2 %collective-permute-start.1 = (bf16[512,512]{1,0:T(8,128)(2,1)}, bf16[512,512]{1,0:T(8,128)(2,1)}, u32[]{:S(2)}, u32[]{:S(2)}) collective-permute-start(bf16[512,512]{1,0:T(8,128)(2,1)} %pad_maximum_fusion.3.refs_5_.refs_1_.refs_2_), channel_id=1, source_target_pairs={{0,1},{1,2},{2,3},{3,0},{4,5},{5,6},{6,7},{7,4},{8,9},{9,10},{10,1... | collective-permute-start | bytes 1572872 | tf_op jit(solution)/shard_map/ppermute | solution.py:799
  26.3 40.6 %collective-permute-start.3 = (bf16[512,512]{1,0:T(8,128)(2,1)}, bf16[512,512]{1,0:T(8,128)(2,1)}, u32[]{:S(2)}, u32[]{:S(2)}) collective-permute-start(bf16[512,512]{1,0:T(8,128)(2,1)} %pad_maximum_fusion.3.refs_5_.refs_1_.refs_2_), channel_id=1, source_target_pairs={{0,8},{4,12},{8,0},{12,4},{1,9},{5,13},{9,1},{13,5},{2,10},{6,14},... | collective-permute-start | bytes 1572872 | tf_op jit(solution)/shard_map/ppermute | solution.py:794
  50.4 15.0 %collective-permute-start.2 = (bf16[512,512]{1,0:T(8,128)(2,1)}, bf16[512,512]{1,0:T(8,128)(2,1)}, u32[]{:S(2)}, u32[]{:S(2)}) collective-permute-start(bf16[512,512]{1,0:T(8,128)(2,1)} %collective-permute-done.1.refs_6_.refs_2_.refs_3_), channel_id=1, source_target_pairs={{0,1},{1,2},{2,3},{3,0},{4,5},{5,6},{6,7},{7,4},{8,9},{9,10},{10,1... | collective-permute-start | bytes 1572872 | tf_op jit(solution)/shard_map/ppermute | solution.py:799
  53.7 14.9 %collective-permute-start.4 = (bf16[512,512]{1,0:T(8,128)(2,1)S(1)}, bf16[512,512]{1,0:T(8,128)(2,1)S(1)}, u32[]{:S(2)}, u32[]{:S(2)}) collective-permute-start(bf16[512,512]{1,0:T(8,128)(2,1)S(1)} %dynamic-slice_bitcast_fusion.1.refs_0_), channel_id=1, source_target_pairs={{0,8},{4,12},{8,0},{12,4},{1,9},{5,13},{9,1},{13,5},{2,10},{6,14},... | collective-permute-start | bytes 1572872 | tf_op jit(solution)/shard_map/ppermute | solution.py:794
  56.4 23.5 %collective-permute-start.5 = (bf16[512,512]{1,0:T(8,128)(2,1)S(1)}, bf16[512,512]{1,0:T(8,128)(2,1)S(1)}, u32[]{:S(2)}, u32[]{:S(2)}) collective-permute-start(bf16[512,512]{1,0:T(8,128)(2,1)S(1)} %dynamic-slice_bitcast_fusion.refs_1_), channel_id=1, source_target_pairs={{0,8},{4,12},{8,0},{12,4},{1,9},{5,13},{9,1},{13,5},{2,10},{6,14},... | collective-permute-start | bytes 1572872 | tf_op jit(solution)/shard_map/ppermute | solution.py:794
  57.0 31.8 %collective-permute-start.8 = (bf16[512,512]{1,0:T(8,128)(2,1)}, bf16[512,512]{1,0:T(8,128)(2,1)S(1)}, u32[]{:S(2)}, u32[]{:S(2)}) collective-permute-start(bf16[512,512]{1,0:T(8,128)(2,1)} %collective-permute-done.1.refs_6_.refs_2_.refs_3_), channel_id=1, source_target_pairs={{0,8},{4,12},{8,0},{12,4},{1,9},{5,13},{9,1},{13,5},{2,10},{6,14},... | collective-permute-start | bytes 1572872 | tf_op jit(solution)/shard_map/ppermute | solution.py:794
  65.5 24.9 %collective-permute-start.7 = (bf16[512,512]{1,0:T(8,128)(2,1)}, bf16[512,512]{1,0:T(8,128)(2,1)}, u32[]{:S(2)}, u32[]{:S(2)}) collective-permute-start(bf16[512,512]{1,0:T(8,128)(2,1)} %collective-permute-done.2.refs_2_.refs_7_.refs_3_.refs_5_.refs_4_), channel_id=1, source_target_pairs={{0,1},{1,2},{2,3},{3,0},{4,5},{5,6},{6,7},{7,4},{8,9},{9,10},{10,1... | collective-permute-start | bytes 1572872 | tf_op jit(solution)/shard_map/ppermute | solution.py:799
  84.0 32.7 %collective-permute-start.6 = (bf16[512,1024]{1,0:T(8,128)(2,1)S(1)}, bf16[512,1024]{1,0:T(8,128)(2,1)}, u32[]{:S(2)}, u32[]{:S(2)}) collective-permute-start(bf16[512,1024]{1,0:T(8,128)(2,1)S(1)} %norm_in.2.refs_3_.refs_1_), channel_id=1, source_target_pairs={{0,4},{4,0},{8,12},{12,8},{1,5},{5,1},{9,13},{13,9},{2,6},{6,2},{1... | collective-permute-start | bytes 3145736 | tf_op jit(solution)/shard_map/ppermute | solution.py:794
  84.1 16.8 %collective-permute-start.11 = (bf16[512,512]{1,0:T(8,128)(2,1)}, bf16[512,512]{1,0:T(8,128)(2,1)S(1)}, u32[]{:S(2)}, u32[]{:S(2)}) collective-permute-start(bf16[512,512]{1,0:T(8,128)(2,1)} %copy-done.114), channel_id=1, source_target_pairs={{0,1},{1,2},{2,3},{3,0},{4,5},{5,6},{6,7},{7,4},{8,9},{9,10},{10,1... | collective-permute-start | bytes 1572872 | tf_op jit(solution)/shard_map/ppermute | solution.py:799
  86.6 25.5 %collective-permute-start.12 = (bf16[512,512]{1,0:T(8,128)(2,1)}, bf16[512,512]{1,0:T(8,128)(2,1)S(1)}, u32[]{:S(2)}, u32[]{:S(2)}) collective-permute-start(bf16[512,512]{1,0:T(8,128)(2,1)} %copy-done.68), channel_id=1, source_target_pairs={{0,1},{1,2},{2,3},{3,0},{4,5},{5,6},{6,7},{7,4},{8,9},{9,10},{10,1... | collective-permute-start | bytes 1572872 | tf_op jit(solution)/shard_map/ppermute | solution.py:799
  88.8 15.1 %collective-permute-start.9 = (bf16[512,512]{1,0:T(8,128)(2,1)}, bf16[512,512]{1,0:T(8,128)(2,1)S(1)}, u32[]{:S(2)}, u32[]{:S(2)}) collective-permute-start(bf16[512,512]{1,0:T(8,128)(2,1)} %collective-permute-done.2.refs_2_.refs_7_.refs_3_.refs_5_.refs_4_), channel_id=1, source_target_pairs={{0,8},{4,12},{8,0},{12,4},{1,9},{5,13},{9,1},{13,5},{2,10},{6,14},... | collective-permute-start | bytes 1572872 | tf_op jit(solution)/shard_map/ppermute | solution.py:794
  90.3 24.8 %collective-permute-start.10 = (bf16[512,512]{1,0:T(8,128)(2,1)}, bf16[512,512]{1,0:T(8,128)(2,1)S(1)}, u32[]{:S(2)}, u32[]{:S(2)}) collective-permute-start(bf16[512,512]{1,0:T(8,128)(2,1)} %collective-permute-done.7.refs_8_.refs_4_.refs_6_.refs_5_), channel_id=1, source_target_pairs={{0,8},{4,12},{8,0},{12,4},{1,9},{5,13},{9,1},{13,5},{2,10},{6,14},... | collective-permute-start | bytes 1572872 | tf_op jit(solution)/shard_map/ppermute | solution.py:794
  93.7 230.8 %copy-start.106 = (f32[1024,128]{1,0:T(8,128)}, f32[1024,128]{1,0:T(8,128)S(1)}, u32[]{:S(2)}) copy-start(f32[1024,128]{1,0:T(8,128)S(1)} %get-tuple-element.230.refs_1_) | copy-start | bytes 1572868
  100.9 36.7 %collective-permute-start.13 = (bf16[512,512]{1,0:T(8,128)(2,1)S(1)}, bf16[512,512]{1,0:T(8,128)(2,1)S(1)}, u32[]{:S(2)}, u32[]{:S(2)}) collective-permute-start(bf16[512,512]{1,0:T(8,128)(2,1)S(1)} %collective-permute-done.11.refs_13_.refs_3_.refs_2_), channel_id=1, source_target_pairs={{0,1},{1,2},{2,3},{3,0},{4,5},{5,6},{6,7},{7,4},{8,9},{9,10},{10,1... | collective-permute-start | bytes 1572872 | tf_op jit(solution)/shard_map/ppermute | solution.py:799
  103.9 233.6 %copy-start.62 = (bf16[512,512]{1,0:T(8,128)(2,1)}, bf16[512,512]{1,0:T(8,128)(2,1)S(1)}, u32[]{:S(2)}) copy-start(bf16[512,512]{1,0:T(8,128)(2,1)S(1)} %collective-permute-done.9.refs_11_.refs_7_.refs_8_) | copy-start | bytes 1572868
  103.9 33.7 %collective-permute-start.15 = (bf16[512,512]{1,0:T(8,128)(2,1)S(1)}, bf16[512,512]{1,0:T(8,128)(2,1)S(1)}, u32[]{:S(2)}, u32[]{:S(2)}) collective-permute-start(bf16[512,512]{1,0:T(8,128)(2,1)S(1)} %collective-permute-done.11.refs_13_.refs_3_.refs_2_), channel_id=1, source_target_pairs={{0,8},{4,12},{8,0},{12,4},{1,9},{5,13},{9,1},{13,5},{2,10},{6,14},... | collective-permute-start | bytes 1572872 | tf_op jit(solution)/shard_map/ppermute | solution.py:794
  112.1 25.5 %collective-permute-start.14 = (bf16[512,512]{1,0:T(8,128)(2,1)S(1)}, bf16[512,512]{1,0:T(8,128)(2,1)S(1)}, u32[]{:S(2)}, u32[]{:S(2)}) collective-permute-start(bf16[512,512]{1,0:T(8,128)(2,1)S(1)} %collective-permute-done.12.refs_14_.refs_2_.refs_4_), channel_id=1, source_target_pairs={{0,1},{1,2},{2,3},{3,0},{4,5},{5,6},{6,7},{7,4},{8,9},{9,10},{10,1... | collective-permute-start | bytes 1572872 | tf_op jit(solution)/shard_map/ppermute | solution.py:799
  115.1 22.5 %collective-permute-start.16 = (bf16[512,512]{1,0:T(8,128)(2,1)S(1)}, bf16[512,512]{1,0:T(8,128)(2,1)S(1)}, u32[]{:S(2)}, u32[]{:S(2)}) collective-permute-start(bf16[512,512]{1,0:T(8,128)(2,1)S(1)} %collective-permute-done.12.refs_14_.refs_2_.refs_4_), channel_id=1, source_target_pairs={{0,8},{4,12},{8,0},{12,4},{1,9},{5,13},{9,1},{13,5},{2,10},{6,14},... | collective-permute-start | bytes 1572872 | tf_op jit(solution)/shard_map/ppermute | solution.py:794
  141.7 28.1 %collective-permute-start.17 = (bf16[512,1024]{1,0:T(8,128)(2,1)S(1)}, bf16[512,1024]{1,0:T(8,128)(2,1)S(1)}, u32[]{:S(2)}, u32[]{:S(2)}) collective-permute-start(bf16[512,1024]{1,0:T(8,128)(2,1)S(1)} %get-tuple-element.101), channel_id=1, source_target_pairs={{0,4},{4,0},{8,12},{12,8},{1,5},{5,1},{9,13},{13,9},{2,6},{6,2},{1... | collective-permute-start | bytes 3145736 | tf_op jit(solution)/shard_map/ppermute | solution.py:794
  141.8 16.6 %collective-permute-start.18 = (bf16[512,512]{1,0:T(8,128)(2,1)S(1)}, bf16[512,512]{1,0:T(8,128)(2,1)S(1)}, u32[]{:S(2)}, u32[]{:S(2)}) collective-permute-start(bf16[512,512]{1,0:T(8,128)(2,1)S(1)} %collective-permute-done.13.refs_9_.refs_4_.refs_3_), channel_id=1, source_target_pairs={{0,1},{1,2},{2,3},{3,0},{4,5},{5,6},{6,7},{7,4},{8,9},{9,10},{10,1... | collective-permute-start | bytes 1572872 | tf_op jit(solution)/shard_map/ppermute | solution.py:799
  144.3 24.8 %collective-permute-start.19 = (bf16[512,512]{1,0:T(8,128)(2,1)S(1)}, bf16[512,512]{1,0:T(8,128)(2,1)S(1)}, u32[]{:S(2)}, u32[]{:S(2)}) collective-permute-start(bf16[512,512]{1,0:T(8,128)(2,1)S(1)} %collective-permute-done.14.refs_10_.refs_3_.refs_5_), channel_id=1, source_target_pairs={{0,1},{1,2},{2,3},{3,0},{4,5},{5,6},{6,7},{7,4},{8,9},{9,10},{10,1... | collective-permute-start | bytes 1572872 | tf_op jit(solution)/shard_map/ppermute | solution.py:799
  144.8 24.4 %collective-permute-start.20 = (bf16[512,512]{1,0:T(8,128)(2,1)S(1)}, bf16[512,512]{1,0:T(8,128)(2,1)S(1)}, u32[]{:S(2)}, u32[]{:S(2)}) collective-permute-start(bf16[512,512]{1,0:T(8,128)(2,1)S(1)} %collective-permute-done.13.refs_9_.refs_4_.refs_3_), channel_id=1, source_target_pairs={{0,8},{4,12},{8,0},{12,4},{1,9},{5,13},{9,1},{13,5},{2,10},{6,14},... | collective-permute-start | bytes 1572872 | tf_op jit(solution)/shard_map/ppermute | solution.py:794
  145.3 24.5 %collective-permute-start.21 = (bf16[512,512]{1,0:T(8,128)(2,1)S(1)}, bf16[512,512]{1,0:T(8,128)(2,1)S(1)}, u32[]{:S(2)}, u32[]{:S(2)}) collective-permute-start(bf16[512,512]{1,0:T(8,128)(2,1)S(1)} %collective-permute-done.14.refs_10_.refs_3_.refs_5_), channel_id=1, source_target_pairs={{0,8},{4,12},{8,0},{12,4},{1,9},{5,13},{9,1},{13,5},{2,10},{6,14},... | collective-permute-start | bytes 1572872 | tf_op jit(solution)/shard_map/ppermute | solution.py:794
  173.3 14.9 %collective-permute-start.22 = (bf16[512,1024]{1,0:T(8,128)(2,1)S(1)}, bf16[512,1024]{1,0:T(8,128)(2,1)S(1)}, u32[]{:S(2)}, u32[]{:S(2)}) collective-permute-start(bf16[512,1024]{1,0:T(8,128)(2,1)S(1)} %get-tuple-element.103.refs_0_.refs_1_), channel_id=1, source_target_pairs={{0,4},{4,0},{8,12},{12,8},{1,5},{5,1},{9,13},{13,9},{2,6},{6,2},{1... | collective-permute-start | bytes 3145736 | tf_op jit(solution)/shard_map/ppermute | solution.py:794
  173.4 14.8 %collective-permute-start.23 = (bf16[512,512]{1,0:T(8,128)(2,1)S(1)}, bf16[512,512]{1,0:T(8,128)(2,1)S(1)}, u32[]{:S(2)}, u32[]{:S(2)}) collective-permute-start(bf16[512,512]{1,0:T(8,128)(2,1)S(1)} %collective-permute-done.18.refs_4_.refs_5_), channel_id=1, source_target_pairs={{0,8},{4,12},{8,0},{12,4},{1,9},{5,13},{9,1},{13,5},{2,10},{6,14},... | collective-permute-start | bytes 1572872 | tf_op jit(solution)/shard_map/ppermute | solution.py:794
  173.9 25.0 %collective-permute-start.24 = (bf16[512,512]{1,0:T(8,128)(2,1)S(1)}, bf16[512,512]{1,0:T(8,128)(2,1)S(1)}, u32[]{:S(2)}, u32[]{:S(2)}) collective-permute-start(bf16[512,512]{1,0:T(8,128)(2,1)S(1)} %collective-permute-done.19.refs_5_.refs_4_.refs_6_), channel_id=1, source_target_pairs={{0,8},{4,12},{8,0},{12,4},{1,9},{5,13},{9,1},{13,5},{2,10},{6,14},... | collective-permute-start | bytes 1572872 | tf_op jit(solution)/shard_map/ppermute | solution.py:794
  203.4 2.7 collective-permute-start.25
  208.1 25.8 %collective-permute-start.26 = (bf16[512,1024]{1,0:T(8,128)(2,1)S(1)}, bf16[512,1024]{1,0:T(8,128)(2,1)S(1)}, u32[]{:S(2)}, u32[]{:S(2)}) collective-permute-start(bf16[512,1024]{1,0:T(8,128)(2,1)S(1)} %get-tuple-element.132), channel_id=1, source_target_pairs={{0,16},{1,17},{2,18},{3,19},{4,20},{5,21},{6,22},{7,23},{8,24},{9,... | collective-permute-start | bytes 3145736 | tf_op jit(solution)/shard_map/ppermute | solution.py:28
  235.6 2.7 collective-permute-start.27
  259.6 2.7 collective-permute-start.28
  265.8 2.7 collective-permute-start.29
  280.8 2.7 collective-permute-start.30
  287.5 2.7 collective-permute-start.31
  302.1 2.7 collective-permute-start.32
  308.7 2.7 collective-permute-start.33
  343.2 2.7 collective-permute-start.34
  349.0 27.5 %collective-permute-start.35 = (bf16[512,1024]{1,0:T(8,128)(2,1)}, bf16[512,1024]{1,0:T(8,128)(2,1)}, u32[]{:S(2)}, u32[]{:S(2)}) collective-permute-start(bf16[512,1024]{1,0:T(8,128)(2,1)} %get-tuple-element.131), channel_id=1, source_target_pairs={{16,0},{17,1},{18,2},{19,3},{20,4},{21,5},{22,6},{23,7},{24,8},{25... | collective-permute-start | bytes 3145736 | tf_op jit(solution)/shard_map/ppermute | solution.py:28
  351.8 31.3 %all-to-all-start.1 = ((bf16[4,128,1024]{2,1,0:T(8,128)(2,1)}), bf16[4,128,1024]{2,1,0:T(8,128)(2,1)}, u32[]{:S(2)}, u32[]{:S(2)}) async-start(bf16[4,128,1024]{2,1,0:T(8,128)(2,1)} %bitcast.43), calls=%async_computation.1 | async-start | bytes 2097152 | tf_op jit(solution)/shard_map/all_to_all | solution.py:1200
  382.4 3.0 collective-permute-start.36
  418.0 7.8 %collective-permute-start.37 = (bf16[512,1024]{1,0:T(8,128)(2,1)}, bf16[512,1024]{1,0:T(8,128)(2,1)S(1)}, u32[]{:S(2)}, u32[]{:S(2)}) collective-permute-start(bf16[512,1024]{1,0:T(8,128)(2,1)} %get-tuple-element.139), channel_id=1, source_target_pairs={{0,4},{4,0},{8,12},{12,8},{1,5},{5,1},{9,13},{13,9},{2,6},{6,2},{1... | collective-permute-start | bytes 3145736 | tf_op jit(solution)/shard_map/ppermute | solution.py:794
  418.1 26.2 %collective-permute-start.40 = (bf16[1024,512]{1,0:T(8,128)(2,1)}, bf16[1024,512]{1,0:T(8,128)(2,1)S(1)}, u32[]{:S(2)}, u32[]{:S(2)}) collective-permute-start(bf16[1024,512]{1,0:T(8,128)(2,1)} %get-tuple-element.148), channel_id=1, source_target_pairs={{0,8},{4,12},{8,0},{12,4},{1,9},{5,13},{9,1},{13,5},{2,10},{6,14},... | collective-permute-start | bytes 3145736 | tf_op jit(solution)/shard_map/ppermute | solution.py:794
  431.9 16.3 %collective-permute-start.38 = (bf16[512,1024]{1,0:T(8,128)(2,1)S(1)}, bf16[512,1024]{1,0:T(8,128)(2,1)S(1)}, u32[]{:S(2)}, u32[]{:S(2)}) collective-permute-start(bf16[512,1024]{1,0:T(8,128)(2,1)S(1)} %get-tuple-element.142.refs_2_.refs_3_.refs_5_), channel_id=1, source_target_pairs={{0,4},{4,0},{8,12},{12,8},{1,5},{5,1},{9,13},{13,9},{2,6},{6,2},{1... | collective-permute-start | bytes 3145736 | tf_op jit(solution)/shard_map/ppermute | solution.py:794
  432.2 34.6 %collective-permute-start.39 = (bf16[1024,512]{1,0:T(8,128)(2,1)S(1)}, bf16[1024,512]{1,0:T(8,128)(2,1)S(1)}, u32[]{:S(2)}, u32[]{:S(2)}) collective-permute-start(bf16[1024,512]{1,0:T(8,128)(2,1)S(1)} %copy-done.133), channel_id=1, source_target_pairs={{0,8},{4,12},{8,0},{12,4},{1,9},{5,13},{9,1},{13,5},{2,10},{6,14},... | collective-permute-start | bytes 3145736 | tf_op jit(solution)/shard_map/ppermute | solution.py:794
  433.6 68.4 %collective-permute-start.42 = (bf16[1024,512]{1,0:T(8,128)(2,1)}, bf16[1024,512]{1,0:T(8,128)(2,1)S(1)}, u32[]{:S(2)}, u32[]{:S(2)}) collective-permute-start(bf16[1024,512]{1,0:T(8,128)(2,1)} %get-tuple-element.150), channel_id=1, source_target_pairs={{0,8},{4,12},{8,0},{12,4},{1,9},{5,13},{9,1},{13,5},{2,10},{6,14},... | collective-permute-start | bytes 3145736 | tf_op jit(solution)/shard_map/ppermute | solution.py:794
  434.2 77.0 %collective-permute-start.45 = (bf16[1024,512]{1,0:T(8,128)(2,1)}, bf16[1024,512]{1,0:T(8,128)(2,1)S(1)}, u32[]{:S(2)}, u32[]{:S(2)}) collective-permute-start(bf16[1024,512]{1,0:T(8,128)(2,1)} %get-tuple-element.156), channel_id=1, source_target_pairs={{0,8},{4,12},{8,0},{12,4},{1,9},{5,13},{9,1},{13,5},{2,10},{6,14},... | collective-permute-start | bytes 3145736 | tf_op jit(solution)/shard_map/ppermute | solution.py:794
  444.7 25.1 %collective-permute-start.41 = (bf16[1024,512]{1,0:T(8,128)(2,1)S(1)}, bf16[1024,512]{1,0:T(8,128)(2,1)S(1)}, u32[]{:S(2)}, u32[]{:S(2)}) collective-permute-start(bf16[1024,512]{1,0:T(8,128)(2,1)S(1)} %moved.6), channel_id=1, source_target_pairs={{0,3},{1,0},{2,1},{3,2},{4,7},{5,4},{6,5},{7,6},{8,11},{9,8},{10,9... | collective-permute-start | bytes 3145736 | tf_op jit(solution)/shard_map/ppermute | solution.py:799
  470.4 31.7 %collective-permute-start.43 = (bf16[1024,512]{1,0:T(8,128)(2,1)S(1)}, bf16[1024,512]{1,0:T(8,128)(2,1)S(1)}, u32[]{:S(2)}, u32[]{:S(2)}) collective-permute-start(bf16[1024,512]{1,0:T(8,128)(2,1)S(1)} %moved.7), channel_id=1, source_target_pairs={{0,3},{1,0},{2,1},{3,2},{4,7},{5,4},{6,5},{7,6},{8,11},{9,8},{10,9... | collective-permute-start | bytes 3145736 | tf_op jit(solution)/shard_map/ppermute | solution.py:799
  508.5 25.7 %collective-permute-start.44 = (bf16[512,1024]{1,0:T(8,128)(2,1)S(1)}, bf16[512,1024]{1,0:T(8,128)(2,1)S(1)}, u32[]{:S(2)}, u32[]{:S(2)}) collective-permute-start(bf16[512,1024]{1,0:T(8,128)(2,1)S(1)} %get-tuple-element.154), channel_id=1, source_target_pairs={{0,4},{4,0},{8,12},{12,8},{1,5},{5,1},{9,13},{13,9},{2,6},{6,2},{1... | collective-permute-start | bytes 3145736 | tf_op jit(solution)/shard_map/ppermute | solution.py:794
  508.6 14.8 %collective-permute-start.46 = (bf16[512,512]{1,0:T(8,128)(2,1)S(1)}, bf16[512,512]{1,0:T(8,128)(2,1)S(1)}, u32[]{:S(2)}, u32[]{:S(2)}) collective-permute-start(bf16[512,512]{1,0:T(8,128)(2,1)S(1)} %get-tuple-element.157), channel_id=1, source_target_pairs={{0,8},{4,12},{8,0},{12,4},{1,9},{5,13},{9,1},{13,5},{2,10},{6,14},... | collective-permute-start | bytes 1572872 | tf_op jit(solution)/shard_map/ppermute | solution.py:794
  509.2 25.0 %collective-permute-start.47 = (bf16[512,512]{1,0:T(8,128)(2,1)S(1)}, bf16[512,512]{1,0:T(8,128)(2,1)S(1)}, u32[]{:S(2)}, u32[]{:S(2)}) collective-permute-start(bf16[512,512]{1,0:T(8,128)(2,1)S(1)} %get-tuple-element.158), channel_id=1, source_target_pairs={{0,8},{4,12},{8,0},{12,4},{1,9},{5,13},{9,1},{13,5},{2,10},{6,14},... | collective-permute-start | bytes 1572872 | tf_op jit(solution)/shard_map/ppermute | solution.py:794
  538.8 66.5 %all-to-all-start.2 = ((bf16[4,128,1024]{2,1,0:T(8,128)(2,1)}), bf16[4,128,1024]{2,1,0:T(8,128)(2,1)S(1)}, u32[]{:S(2)}, u32[]{:S(2)}) async-start(bf16[4,128,1024]{2,1,0:T(8,128)(2,1)} %bitcast.42), calls=%async_computation.2 | async-start | bytes 2097152 | tf_op jit(solution)/shard_map/all_to_all | solution.py:1277
  547.4 54.4 %collective-permute-start.55 = (bf16[1024,512]{1,0:T(8,128)(2,1)S(1)}, bf16[1024,512]{1,0:T(8,128)(2,1)S(1)}, u32[]{:S(2)}, u32[]{:S(2)}) collective-permute-start(bf16[1024,512]{1,0:T(8,128)(2,1)S(1)} %moved.11), channel_id=1, source_target_pairs={{0,3},{1,0},{2,1},{3,2},{4,7},{5,4},{6,5},{7,6},{8,11},{9,8},{10,9... | collective-permute-start | bytes 3145736 | tf_op jit(solution)/shard_map/ppermute | solution.py:799
  551.4 44.2 %collective-permute-start.52 = (bf16[512,512]{1,0:T(8,128)(2,1)S(1)}, bf16[512,512]{1,0:T(8,128)(2,1)S(1)}, u32[]{:S(2)}, u32[]{:S(2)}) collective-permute-start(bf16[512,512]{1,0:T(8,128)(2,1)S(1)} %moved.8), channel_id=1, source_target_pairs={{0,3},{1,0},{2,1},{3,2},{4,7},{5,4},{6,5},{7,6},{8,11},{9,8},{10,9... | collective-permute-start | bytes 1572872 | tf_op jit(solution)/shard_map/ppermute | solution.py:799
  552.2 46.6 %collective-permute-start.48 = (bf16[512,512]{1,0:T(8,128)(2,1)S(1)}, bf16[512,512]{1,0:T(8,128)(2,1)S(1)}, u32[]{:S(2)}, u32[]{:S(2)}) collective-permute-start(bf16[512,512]{1,0:T(8,128)(2,1)S(1)} %copy-done.141), channel_id=1, source_target_pairs={{0,8},{4,12},{8,0},{12,4},{1,9},{5,13},{9,1},{13,5},{2,10},{6,14},... | collective-permute-start | bytes 1572872 | tf_op jit(solution)/shard_map/ppermute | solution.py:794
  552.8 52.4 %collective-permute-start.50 = (bf16[512,512]{1,0:T(8,128)(2,1)S(1)}, bf16[512,512]{1,0:T(8,128)(2,1)S(1)}, u32[]{:S(2)}, u32[]{:S(2)}) collective-permute-start(bf16[512,512]{1,0:T(8,128)(2,1)S(1)} %copy-done.139), channel_id=1, source_target_pairs={{0,8},{4,12},{8,0},{12,4},{1,9},{5,13},{9,1},{13,5},{2,10},{6,14},... | collective-permute-start | bytes 1572872 | tf_op jit(solution)/shard_map/ppermute | solution.py:794
  596.7 18.6 %collective-permute-start.53 = (bf16[512,512]{1,0:T(8,128)(2,1)}, bf16[512,512]{1,0:T(8,128)(2,1)}, u32[]{:S(2)}, u32[]{:S(2)}) collective-permute-start(bf16[512,512]{1,0:T(8,128)(2,1)} %moved.9), channel_id=1, source_target_pairs={{0,3},{1,0},{2,1},{3,2},{4,7},{5,4},{6,5},{7,6},{8,11},{9,8},{10,9... | collective-permute-start | bytes 1572872 | tf_op jit(solution)/shard_map/ppermute | solution.py:799
  601.7 34.6 %collective-permute-start.49 = (bf16[2,128,1024]{2,1,0:T(8,128)(2,1)}, bf16[2,128,1024]{2,1,0:T(8,128)(2,1)}, u32[]{:S(2)}, u32[]{:S(2)}) collective-permute-start(bf16[2,128,1024]{2,1,0:T(8,128)(2,1)} %get-tuple-element.162), channel_id=1, source_target_pairs={{0,4},{4,0},{8,12},{12,8},{1,5},{5,1},{9,13},{13,9},{2,6},{6,2},{1... | collective-permute-start | bytes 1572872 | tf_op jit(solution)/shard_map/ppermute | solution.py:794
  604.7 33.8 %collective-permute-start.56 = (f32[256,512]{1,0:T(8,128)}, f32[256,512]{1,0:T(8,128)}, u32[]{:S(2)}, u32[]{:S(2)}) collective-permute-start(f32[256,512]{1,0:T(8,128)} %get-tuple-element.179), channel_id=1, source_target_pairs={{0,4},{4,0},{8,12},{12,8},{1,5},{5,1},{9,13},{13,9},{2,6},{6,2},{1... | collective-permute-start | bytes 1572872 | tf_op jit(solution)/shard_map/ppermute | solution.py:794
  605.2 33.3 %collective-permute-start.57 = (f32[512,256]{1,0:T(8,128)}, f32[512,256]{1,0:T(8,128)}, u32[]{:S(2)}, u32[]{:S(2)}) collective-permute-start(f32[512,256]{1,0:T(8,128)} %get-tuple-element.180), channel_id=1, source_target_pairs={{0,4},{4,0},{8,12},{12,8},{1,5},{5,1},{9,13},{13,9},{2,6},{6,2},{1... | collective-permute-start | bytes 1572872 | tf_op jit(solution)/shard_map/ppermute | solution.py:794
  606.1 37.3 %collective-permute-start.51 = (bf16[2,128,1024]{2,1,0:T(8,128)(2,1)}, bf16[2,128,1024]{2,1,0:T(8,128)(2,1)}, u32[]{:S(2)}, u32[]{:S(2)}) collective-permute-start(bf16[2,128,1024]{2,1,0:T(8,128)(2,1)} %get-tuple-element.165), channel_id=1, source_target_pairs={{0,4},{4,0},{8,12},{12,8},{1,5},{5,1},{9,13},{13,9},{2,6},{6,2},{1... | collective-permute-start | bytes 1572872 | tf_op jit(solution)/shard_map/ppermute | solution.py:794
  617.3 28.2 %collective-permute-start.54 = (bf16[512,512]{1,0:T(8,128)(2,1)}, bf16[512,512]{1,0:T(8,128)(2,1)S(1)}, u32[]{:S(2)}, u32[]{:S(2)}) collective-permute-start(bf16[512,512]{1,0:T(8,128)(2,1)} %moved.10), channel_id=1, source_target_pairs={{0,3},{1,0},{2,1},{3,2},{4,7},{5,4},{6,5},{7,6},{8,11},{9,8},{10,9... | collective-permute-start | bytes 1572872 | tf_op jit(solution)/shard_map/ppermute | solution.py:799
  648.5 2.1 collective-permute-start.58
  (150 other events, 3428.8 us)

commit v9 on v8

--- a/solution.py
+++ b/solution.py
@@ -722,9 +722,10 @@
     unit, half = pieces[0][0].shape
     count = len(pieces[0])
     every, space = pl.BlockSpec(memory_space=pl.ANY), pl.BlockSpec(memory_space=pltpu.VMEM)
+    far = pl.BlockSpec(memory_space=pltpu.HBM)
     return pl.pallas_call(
         without(functools.partial(mlp_up_back_kernel, count), 3 + 2 * count, len(waits)),
-        in_specs=[space] * 2 + [every] * (1 + 2 * count + len(waits)),
+        in_specs=[space] * 2 + [far] * (1 + 2 * count) + [every] * len(waits),
         out_specs=space,
         out_shape=jax.ShapeDtypeStruct((length, units), jnp.bfloat16),
         scratch_shapes=[
@@ -968,6 +969,12 @@
     send_ref[...] = rows_ref[pl.ds((1 - core_ref[0]) * count, count)]
 
 
+def both_kernel(core_ref, keep_ref, sent_ref, out_ref):
+    count = keep_ref.shape[0]
+    out_ref[pl.ds(core_ref[0] * count, count)] = keep_ref[...]
+    out_ref[pl.ds((1 - core_ref[0]) * count, count)] = sent_ref[...]
+
+
 def in_order_kernel(core_ref, keep_ref, sent_ref, out_ref):
     out_ref[:, pl.ds(core_ref[0], 1)] = keep_ref[...][:, None]
     out_ref[:, pl.ds(1 - core_ref[0], 1)] = sent_ref[...][:, None]
@@ -1048,9 +1055,11 @@
         split = block.reshape((micro, 2, part) + block.shape[2:])
         mine = lax.dynamic_index_in_dim(split, core, 1, keepdims=False)
         other = lax.dynamic_index_in_dim(split, 1 - core, 1, keepdims=False)
-        return lax.all_to_all(
-            jnp.concatenate(ordered(mine, flip_pairs(other, 1))), "tensor", 0, 0, tiled=True
-        )
+        outs = (((2 * micro, part, width), jnp.bfloat16),)
+        (rows,) = with_core(
+            both_kernel, "both", core_word, outs, mine, flip_pairs(other, 1), waits=(attn_piece,)
+        )
+        return lax.all_to_all(rows, "tensor", 0, 0, tiled=True)
 
     def from_chip(spread_out, waits=()):
         piece = ((micro, part, width), jnp.bfloat16)
@@ -1260,18 +1269,18 @@
             mlp_moves[1] = moves_on(mlp_sums[1], mlp_moves[2], waits=new)
             attn_leaves(0, new[0])
             return (mlp_sums[1][1], mlp_moves[2], attn_sums[1][0])
-        return (mlp_sums[0][1], attn_sums[3][1], attn_sums[2][1])
+        return (mlp_sums[0][1], attn_sums[3][1], attn_sums[2][1], mlp_moves[1])
 
     d_down = d_up = d_attn = None
     grad_zero, rights_zero, gain_zero = backward(received, saved_zero, hook, (lows,))
-    attn_moves[3] = moves_on(attn_sums[3])
-    attn_moves[2] = moves_on(attn_sums[2], attn_moves[3])
-    attn_moves[1] = moves_on(attn_sums[1], attn_moves[2])
     gain_total = own_first(jnp.where(first, gain_zero, gain_one))
     count = tensor * lax.axis_size("dp")
     gain_parts = gain_total.reshape(4, count, width // count).swapaxes(0, 1)
     gain_parts = lax.all_to_all(gain_parts, ("dp", "tensor"), 0, 0, tiled=True)
     gains_grad = jnp.sum(gain_parts, axis=0)
+    attn_moves[3] = moves_on(attn_sums[3])
+    attn_moves[2] = moves_on(attn_sums[2], attn_moves[3])
+    attn_moves[1] = moves_on(attn_sums[1], attn_moves[2], waits=(gains_grad,))
     outputs = from_chip(lows, (grad_zero, attn_sums[1][1]))
     grads = own_first(jnp.where(first, grad_zero, grad_one)).reshape(tensor, part, width)
     grads = from_chip(lax.all_to_all(grads, "tensor", 0, 0, tiled=True), attn_sums[0][1:])
@@ -1302,7 +1311,7 @@
         outs,
         *attn_sums[0],
         attn_moves[1],
-        waits=(outputs, grads, gain_parts, up_grad),
+        waits=(outputs, grads, gains_grad, up_grad),
     )
     spots = tuple((i * 128, (i + 1) * 128, i * 256) for i in range(3))
     outs = (((wide_half // 2, 768), jnp.float32), ((256, wide_half // 2), jnp.float32))

time: 667 us -> 667 us (level)
  local copies, waits for them, and re-layouts: 53.4 us -> 72.5 us
  waiting for transfers between devices: 261 us -> 248 us
  blocking collectives: 10.2 us -> 0 us
    unnamed x308, local copies, waits for them, and re-layouts: 44.2 us -> 63.1 us
    ppermute x42, waiting for transfers between devices: 99.5 us -> 87.6 us  [flip_pairs(): return lax.ppermute(block, 'dp', [(i, i ^ distance) for i in range(size)])]
    all_to_all x1 -> x0, blocking collectives: 10.2 us -> none  [per_chip(): gain_parts = lax.all_to_all(gain_parts, ('dp', 'tensor'), 0, 0, tiled=True)]
    pallas_call x8 -> x9, Pallas kernels: 13.1 us -> 14.1 us  [with_core(): pl.pallas_call(without(kernel, 1 + len(operands), len(waits)), in_specs=[...]
  transfers between devices with their start and end apart: 62 -> 63, of which waited for: 37 -> 37; matrix products, arithmetic and copies ran while one was open for 3% -> 3% of each run, Pallas kernels for 16% -> 16%
where the time goes in v9:
time: 667 us; the launch traced here: 657 us
  waiting for transfers between devices  248 us (37%)
  Pallas kernels  234 us (35%)
  starting transfers between devices  80.4 us (12%)
  local copies, waits for them, and re-layouts  72.5 us (11%)
  other arithmetic  18.6 us (3%)
    ppermute x15, waiting for transfers between devices, passed_on(): lax.ppermute(block, 'tensor', [(i, (i + step) % size) for i in range(size)])  114 us
    pallas_call x29, Pallas kernels, on_chip(): pl.pallas_call(without(kernel, len(operands), len(waits)), in_specs=[spac...  96.1 us
    ppermute x42, waiting for transfers between devices, flip_pairs(): return lax.ppermute(block, 'dp', [(i, i ^ distance) for i in range(size)])  87.6 us
    pallas_call x6, Pallas kernels, by_pairs(): pl.pallas_call(without(functools.partial(kernel, len(pieces[0])), taken,...  84.8 us
    unnamed x308, local copies, waits for them, and re-layouts  63.1 us
    ppermute x2, waiting for transfers between devices, shifted(): return lax.ppermute(block, axis, route)  41.8 us
    ppermute x15, starting transfers between devices, passed_on(): lax.ppermute(block, 'tensor', [(i, (i + step) % size) for i in range(size)])  30.4 us
    ppermute x42, starting transfers between devices, flip_pairs(): return lax.ppermute(block, 'dp', [(i, i ^ distance) for i in range(size)])  26.1 us
  transfers between devices with their start and end apart: 63, of which 37 were waited for; matrix products, arithmetic and copies ran while one was open for 3% of the time, Pallas kernels for 16%

profile of v9, /device:TPU:0, one launch (start us, length us, event | category | flops | bytes accessed | tf_op | source)
XLA Modules:
  0.0 656.6 jit_solution(15108101172148011967)
XLA Ops:
  14.9 6.0 all-to-all-start
  24.5 29.6 %collective-permute-done.1.refs_6_.refs_2_.refs_3_ = bf16[512,512]{1,0:T(8,128)(2,1)} collective-permute-done((bf16[512,512]{1,0:T(8,128)(2,1)}, bf16[512,512]{1,0:T(8,128)(2,1)}, u32[]{:S(2)}, u32[]{:S(2)}) %collective-permute-start.1) | collective-permute-done | bytes 524320 | tf_op jit(solution)/shard_map/ppermute | solution.py:800
  54.1 3.3 collective-permute-start.2
  62.2 7.3 %collective-permute-done.2.refs_2_.refs_7_.refs_3_.refs_5_.refs_4_ = bf16[512,512]{1,0:T(8,128)(2,1)} collective-permute-done((bf16[512,512]{1,0:T(8,128)(2,1)}, bf16[512,512]{1,0:T(8,128)(2,1)}, u32[]{:S(2)}, u32[]{:S(2)}) %collective-permute-start.2) | collective-permute-done | bytes 524320 | tf_op jit(solution)/shard_map/ppermute | solution.py:800
  73.1 10.4 %collective-permute-done.5.refs_4_.refs_5_.refs_7_ = bf16[512,512]{1,0:T(8,128)(2,1)S(1)} collective-permute-done((bf16[512,512]{1,0:T(8,128)(2,1)S(1)}, bf16[512,512]{1,0:T(8,128)(2,1)S(1)}, u32[]{:S(2)}, u32[]{:S(2)}) %collective-permute-start.5) | collective-permute-done | bytes 524320 | tf_op jit(solution)/shard_map/ppermute | solution.py:795
  89.4 2.5 collective-permute-start.11
  97.8 8.3 %collective-permute-done.11.refs_13_.refs_3_.refs_2_ = bf16[512,512]{1,0:T(8,128)(2,1)S(1)} collective-permute-done((bf16[512,512]{1,0:T(8,128)(2,1)}, bf16[512,512]{1,0:T(8,128)(2,1)S(1)}, u32[]{:S(2)}, u32[]{:S(2)}) %collective-permute-start.11) | collective-permute-done | bytes 524320 | tf_op jit(solution)/shard_map/ppermute | solution.py:800
  109.6 7.8 %collective-permute-done.12.refs_14_.refs_2_.refs_4_ = bf16[512,512]{1,0:T(8,128)(2,1)S(1)} collective-permute-done((bf16[512,512]{1,0:T(8,128)(2,1)}, bf16[512,512]{1,0:T(8,128)(2,1)S(1)}, u32[]{:S(2)}, u32[]{:S(2)}) %collective-permute-start.12) | collective-permute-done | bytes 524320 | tf_op jit(solution)/shard_map/ppermute | solution.py:800
  123.0 16.5 %attend.2 = (bf16[4,1024,128]{2,1,0:T(8,128)(2,1)S(1)}, bf16[4,1024,128]{2,1,0:T(8,128)(2,1)S(1)}, bf16[4,1024,128]{2,1,0:T(8,128)(2,1)S(1)}, f32[4,2,1024]{2,1,0:T(2,128)S(1)}, bf16[1024,512]{1,0:T(8,128)(2,1)S(1)}) custom-call(s32[1]{0:T(128)} %bitcast.refs_0_, f32[1024,128]{1,0:T(8,128)S(1)} %get-tuple-element.237.refs_1_, ...), custom_call_target="tpu_custom_call" | custom-call | flops 11811160064 | bytes 11567104 | tf_op jit(solution)/shard_map/attend/pallas_call | solution.py:704
  142.6 4.0 attn_out.2
  146.7 2.5 collective-permute-start.18
  151.7 11.5 %collective-permute-done.18.refs_4_.refs_5_ = bf16[512,512]{1,0:T(8,128)(2,1)S(1)} collective-permute-done((bf16[512,512]{1,0:T(8,128)(2,1)S(1)}, bf16[512,512]{1,0:T(8,128)(2,1)S(1)}, u32[]{:S(2)}, u32[]{:S(2)}) %collective-permute-start.18) | collective-permute-done | bytes 524320 | tf_op jit(solution)/shard_map/ppermute | solution.py:800
  163.3 10.8 %collective-permute-done.19.refs_5_.refs_4_.refs_6_ = bf16[512,512]{1,0:T(8,128)(2,1)S(1)} collective-permute-done((bf16[512,512]{1,0:T(8,128)(2,1)S(1)}, bf16[512,512]{1,0:T(8,128)(2,1)S(1)}, u32[]{:S(2)}, u32[]{:S(2)}) %collective-permute-start.19) | collective-permute-done | bytes 524320 | tf_op jit(solution)/shard_map/ppermute | solution.py:800
  174.7 3.4 after_attn.2
  181.7 12.7 %collective-permute-done.23.refs_9_.refs_8_ = bf16[512,512]{1,0:T(8,128)(2,1)S(1)} collective-permute-done((bf16[512,512]{1,0:T(8,128)(2,1)S(1)}, bf16[512,512]{1,0:T(8,128)(2,1)S(1)}, u32[]{:S(2)}, u32[]{:S(2)}) %collective-permute-start.23) | collective-permute-done | bytes 524320 | tf_op jit(solution)/shard_map/ppermute | solution.py:795
  194.4 7.7 %mlp_up.2 = (bf16[1024,2048]{1,0:T(8,128)(2,1)S(1)}, bf16[1024,2048]{1,0:T(8,128)(2,1)S(1)}) custom-call(bf16[512,1024]{1,0:T(8,128)(2,1)S(1)} %get-tuple-element.103.refs_0_.refs_1_, bf16[512,1024]{1,0:T(8,128)(2,1)S(1)} %collective-permute-done.22.refs_1_.refs_2_, bf16[512,512]{1,0:T(8,128)(2,1)S(1)} %copy-done.120, ...), custom_call_target="tpu_custom_call" | custom-call | flops 4294967296 | bytes 14680064 | tf_op jit(solution)/shard_map/mlp_up/pallas_call | solution.py:686
  205.2 4.5 mlp_down.2
  209.7 2.6 collective-permute-done.25.refs_3_
  215.7 3.5 collective-permute-start.26
  219.2 22.2 %collective-permute-done.26.refs_1_ = bf16[512,1024]{1,0:T(8,128)(2,1)S(1)} collective-permute-done((bf16[512,1024]{1,0:T(8,128)(2,1)S(1)}, bf16[512,1024]{1,0:T(8,128)(2,1)S(1)}, u32[]{:S(2)}, u32[]{:S(2)}) %collective-permute-start.26) | collective-permute-done | bytes 1048608 | tf_op jit(solution)/shard_map/ppermute | solution.py:28
  243.3 2.6 collective-permute-done.27.refs_4_.refs_8_
  246.0 16.9 %attend.3 = (bf16[4,1024,128]{2,1,0:T(8,128)(2,1)S(1)}, bf16[4,1024,128]{2,1,0:T(8,128)(2,1)S(1)}, bf16[4,1024,128]{2,1,0:T(8,128)(2,1)S(1)}, f32[4,2,1024]{2,1,0:T(2,128)S(1)}, bf16[1024,512]{1,0:T(8,128)(2,1)S(1)}) custom-call(s32[1]{0:T(128)} %bitcast.refs_0_, f32[1024,128]{1,0:T(8,128)S(1)} %get-tuple-element.237.refs_1_, ...), custom_call_target="tpu_custom_call" | custom-call | flops 11811160064 | bytes 11567104 | tf_op jit(solution)/shard_map/attend/pallas_call | solution.py:704
  262.9 3.3 attn_out.3
  269.0 3.4 after_attn.3
  272.6 2.5 collective-permute-done.29.refs_1_.refs_8_
  275.1 7.7 %mlp_up.3 = (bf16[1024,2048]{1,0:T(8,128)(2,1)S(1)}, bf16[1024,2048]{1,0:T(8,128)(2,1)S(1)}) custom-call(bf16[512,1024]{1,0:T(8,128)(2,1)S(1)} %get-tuple-element.112.refs_0_.refs_7_, bf16[512,1024]{1,0:T(8,128)(2,1)S(1)} %collective-permute-done.29.refs_1_.refs_8_, bf16[512,512]{1,0:T(8,128)(2,1)S(1)} %copy-done.120, ...), custom_call_target="tpu_custom_call" | custom-call | flops 4294967296 | bytes 14680064 | tf_op jit(solution)/shard_map/mlp_up/pallas_call | solution.py:686
  282.9 4.5 mlp_down.3
  296.8 7.2 %mlp_up_back.2.refs_0_.refs_9_ = bf16[1024,2048]{1,0:T(8,128)(2,1)S(1)} custom-call(bf16[512,1024]{1,0:T(8,128)(2,1)S(1)} %get-tuple-element.118.refs_0_.refs_11_, bf16[512,1024]{1,0:T(8,128)(2,1)S(1)} %collective-permute-done.31.refs_1_.refs_12_, bf16[1024,2048]{1,0:T(8,128)(2,1)S(1)} %get-tuple-element.119.refs_2_, bf16[512,512]{1,0:T(8,128)(2,1)S(1)} %copy-done.68, ...), custom_call_target="tpu_custom_call" | custom-call | tf_op jit(solution)/shard_map/mlp_up_back/pallas_call | solution.py:726
  304.9 4.5 mlp_back.2
  312.9 3.9 into_attn_back.2
  317.0 2.5 collective-permute-done.33.refs_4_.refs_12_
  319.5 12.9 %attend_back.4.refs_0_.refs_9_ = bf16[1024,768]{1,0:T(8,128)(2,1)S(1)} custom-call(s32[1]{0:T(128)} %bitcast.refs_0_, f32[1024,128]{1,0:T(8,128)S(1)} %get-tuple-element.237.refs_1_, f32[1024,128]{1,0:T(8,128)S(1)} %get-tuple-element.238.refs_2_, bf16[512,1024]{1,0:T(8,128)(2,1)S(1)} %get-tuple-element.123.refs_3_.refs_11_, ...), custom_call_target="tpu_custom_call" | custom-call | flops 11274289152 | bytes 6815744 | tf_op jit(solution)/shard_map/attend_back/pallas_call | solution.py:704
  332.5 12.9 %attend_back.5.refs_1_.refs_9_ = bf16[1024,768]{1,0:T(8,128)(2,1)S(1)} custom-call(s32[1]{0:T(128)} %bitcast.refs_0_, f32[1024,128]{1,0:T(8,128)S(1)} %get-tuple-element.237.refs_1_, f32[1024,128]{1,0:T(8,128)S(1)} %get-tuple-element.238.refs_2_, bf16[512,1024]{1,0:T(8,128)(2,1)S(1)} %get-tuple-element.123.refs_3_.refs_11_, ...), custom_call_target="tpu_custom_call" | custom-call | flops 11274289152 | bytes 6815744 | tf_op jit(solution)/shard_map/attend_back/pallas_call | solution.py:704
  347.1 5.7 attn_back.2
  357.0 3.1 out_of_layer.2
  362.9 5.2 all-to-all-start.1
  368.1 19.6 %collective-permute-done.35.refs_1_ = bf16[512,1024]{1,0:T(8,128)(2,1)} collective-permute-done((bf16[512,1024]{1,0:T(8,128)(2,1)}, bf16[512,1024]{1,0:T(8,128)(2,1)}, u32[]{:S(2)}, u32[]{:S(2)}) %collective-permute-start.35) | collective-permute-done | bytes 1048608 | tf_op jit(solution)/shard_map/ppermute | solution.py:28
  389.3 4.3 into_mlp_back.3
  407.1 8.7 %mlp_up_back.3.refs_3_.refs_0_ = bf16[1024,2048]{1,0:T(8,128)(2,1)S(1)} custom-call(bf16[512,1024]{1,0:T(8,128)(2,1)} %get-tuple-element.135.refs_0_.refs_5_, bf16[512,1024]{1,0:T(8,128)(2,1)} %collective-permute-done.36.refs_1_.refs_6_, bf16[1024,2048]{1,0:T(8,128)(2,1)S(1)} %copy-done.51, bf16[512,512]{1,0:T(8,128)(2,1)S(1)} %copy-done.69, ...), custom_call_target="tpu_custom_call" | custom-call | tf_op jit(solution)/shard_map/mlp_up_back/pallas_call | solution.py:726
  417.2 6.2 mlp_grads.2
  423.6 5.5 mlp_back.3
  429.7 6.0 mlp_grads.3
  435.8 6.1 into_attn_back.3
  445.7 9.7 %collective-permute-done.40.refs_1_.refs_13_ = bf16[1024,512]{1,0:T(8,128)(2,1)S(1)} collective-permute-done((bf16[1024,512]{1,0:T(8,128)(2,1)}, bf16[1024,512]{1,0:T(8,128)(2,1)S(1)}, u32[]{:S(2)}, u32[]{:S(2)}) %collective-permute-start.40) | collective-permute-done | bytes 1048608 | tf_op jit(solution)/shard_map/ppermute | solution.py:795
  456.4 3.5 collective-permute-start.41
  461.1 12.5 %attend_back.6.refs_3_.refs_1_ = bf16[1024,768]{1,0:T(8,128)(2,1)S(1)} custom-call(s32[1]{0:T(128)} %bitcast.refs_0_, f32[1024,128]{1,0:T(8,128)S(1)} %copy-done.111, f32[1024,128]{1,0:T(8,128)S(1)} %copy-done.113, bf16[512,1024]{1,0:T(8,128)(2,1)S(1)} %get-tuple-element.142.refs_2_.refs_3_.refs_5_, ...), custom_call_target="tpu_custom_call" | custom-call | flops 11274289152 | bytes 6815744 | tf_op jit(solution)/shard_map/attend_back/pallas_call | solution.py:704
  473.7 4.2 collective-permute-done.39.refs_13_.refs_1_
  477.9 3.6 collective-permute-done.41.refs_14_.refs_2_
  482.0 4.3 collective-permute-start.43
  486.4 5.4 attn_grads.2
  492.9 13.0 %attend_back.7.refs_3_.refs_0_ = bf16[1024,768]{1,0:T(8,128)(2,1)S(1)} custom-call(s32[1]{0:T(128)} %bitcast.refs_0_, f32[1024,128]{1,0:T(8,128)S(1)} %copy-done.111, f32[1024,128]{1,0:T(8,128)S(1)} %copy-done.113, bf16[512,1024]{1,0:T(8,128)(2,1)S(1)} %get-tuple-element.142.refs_2_.refs_3_.refs_5_, ...), custom_call_target="tpu_custom_call" | custom-call | flops 11274289152 | bytes 6815744 | tf_op jit(solution)/shard_map/attend_back/pallas_call | solution.py:704
  505.9 5.3 attn_grads.3
  512.2 6.7 %attn_back.3 = (f32[512,1024]{1,0:T(8,128)S(1)}, bf16[512,1024]{1,0:T(8,128)(2,1)}) custom-call(bf16[1024,768]{1,0:T(8,128)(2,1)S(1)} %attend_back.7.refs_3_.refs_0_, bf16[1024,768]{1,0:T(8,128)(2,1)S(1)} %attend_back.6.refs_3_.refs_1_, bf16[512,512]{1,0:T(8,128)(2,1)S(1)} %copy-done.18, bf16[512,512]{1,0:T(8,128)(2,1)} %collective-permute-done.1.refs_6_.refs_2_.refs_3_, ...), custom_call_target="tpu_custom_call" | custom-call | flops 3221225472 | bytes 10485760 | tf_op jit(solution)/shard_map/attn_back/pallas_call | solution.py:686
  531.6 7.3 %collective-permute-done.46.refs_6_.refs_1_ = bf16[512,512]{1,0:T(8,128)(2,1)S(1)} collective-permute-done((bf16[512,512]{1,0:T(8,128)(2,1)}, bf16[512,512]{1,0:T(8,128)(2,1)S(1)}, u32[]{:S(2)}, u32[]{:S(2)}) %collective-permute-start.46) | collective-permute-done | bytes 524320 | tf_op jit(solution)/shard_map/ppermute | solution.py:795
  539.6 9.7 %collective-permute-done.47.refs_7_.refs_1_ = bf16[512,512]{1,0:T(8,128)(2,1)S(1)} collective-permute-done((bf16[512,512]{1,0:T(8,128)(2,1)}, bf16[512,512]{1,0:T(8,128)(2,1)S(1)}, u32[]{:S(2)}, u32[]{:S(2)}) %collective-permute-start.47) | collective-permute-done | bytes 524320 | tf_op jit(solution)/shard_map/ppermute | solution.py:795
  557.7 3.4 out_of_layer.3
  566.0 3.5 all-to-all-start.3
  572.0 3.8 all-to-all-done.3
  575.8 4.4 all-to-all-start.2
  580.5 3.8 collective-permute-start.53
  586.3 24.9 %collective-permute-done.53.refs_2_ = bf16[512,512]{1,0:T(8,128)(2,1)S(1)} collective-permute-done((bf16[512,512]{1,0:T(8,128)(2,1)S(1)}, bf16[512,512]{1,0:T(8,128)(2,1)S(1)}, u32[]{:S(2)}, u32[]{:S(2)}) %collective-permute-start.53) | collective-permute-done | bytes 524320 | tf_op jit(solution)/shard_map/ppermute | solution.py:800
  625.4 5.7 collective-permute-done.54.refs_2_
  638.8 2.8 mlp_join.1
  642.6 4.8 collective-permute-done.55.refs_3_
  (474 shorter events, 178.7 us)
Async XLA Ops:
  7.2 3.0 collective-permute-start
  14.9 69.4 %all-to-all-start = ((bf16[4,128,1024]{2,1,0:T(8,128)(2,1)}), bf16[4,128,1024]{2,1,0:T(8,128)(2,1)S(1)}, u32[]{:S(2)}, u32[]{:S(2)}) async-start(bf16[4,128,1024]{2,1,0:T(8,128)(2,1)} %copy-done.49), calls=%async_computation | async-start | bytes 2097152 | tf_op jit(solution)/shard_map/all_to_all | solution.py:1062
  20.9 33.2 %collective-permute-start.1 = (bf16[512,512]{1,0:T(8,128)(2,1)}, bf16[512,512]{1,0:T(8,128)(2,1)}, u32[]{:S(2)}, u32[]{:S(2)}) collective-permute-start(bf16[512,512]{1,0:T(8,128)(2,1)} %copy-done.16), channel_id=1, source_target_pairs={{0,1},{1,2},{2,3},{3,0},{4,5},{5,6},{6,7},{7,4},{8,9},{9,10},{10,1... | collective-permute-start | bytes 1572872 | tf_op jit(solution)/shard_map/ppermute | solution.py:800
  23.0 48.0 %collective-permute-start.3 = (bf16[512,512]{1,0:T(8,128)(2,1)}, bf16[512,512]{1,0:T(8,128)(2,1)}, u32[]{:S(2)}, u32[]{:S(2)}) collective-permute-start(bf16[512,512]{1,0:T(8,128)(2,1)} %copy-done.16), channel_id=1, source_target_pairs={{0,8},{4,12},{8,0},{12,4},{1,9},{5,13},{9,1},{13,5},{2,10},{6,14},... | collective-permute-start | bytes 1572872 | tf_op jit(solution)/shard_map/ppermute | solution.py:795
  54.1 15.4 %collective-permute-start.2 = (bf16[512,512]{1,0:T(8,128)(2,1)}, bf16[512,512]{1,0:T(8,128)(2,1)}, u32[]{:S(2)}, u32[]{:S(2)}) collective-permute-start(bf16[512,512]{1,0:T(8,128)(2,1)} %collective-permute-done.1.refs_6_.refs_2_.refs_3_), channel_id=1, source_target_pairs={{0,1},{1,2},{2,3},{3,0},{4,5},{5,6},{6,7},{7,4},{8,9},{9,10},{10,1... | collective-permute-start | bytes 1572872 | tf_op jit(solution)/shard_map/ppermute | solution.py:800
  57.4 14.9 %collective-permute-start.4 = (bf16[512,512]{1,0:T(8,128)(2,1)S(1)}, bf16[512,512]{1,0:T(8,128)(2,1)S(1)}, u32[]{:S(2)}, u32[]{:S(2)}) collective-permute-start(bf16[512,512]{1,0:T(8,128)(2,1)S(1)} %dynamic-slice_bitcast_fusion.1.refs_0_), channel_id=1, source_target_pairs={{0,8},{4,12},{8,0},{12,4},{1,9},{5,13},{9,1},{13,5},{2,10},{6,14},... | collective-permute-start | bytes 1572872 | tf_op jit(solution)/shard_map/ppermute | solution.py:795
  60.1 23.5 %collective-permute-start.5 = (bf16[512,512]{1,0:T(8,128)(2,1)S(1)}, bf16[512,512]{1,0:T(8,128)(2,1)S(1)}, u32[]{:S(2)}, u32[]{:S(2)}) collective-permute-start(bf16[512,512]{1,0:T(8,128)(2,1)S(1)} %dynamic-slice_bitcast_fusion.refs_1_), channel_id=1, source_target_pairs={{0,8},{4,12},{8,0},{12,4},{1,9},{5,13},{9,1},{13,5},{2,10},{6,14},... | collective-permute-start | bytes 1572872 | tf_op jit(solution)/shard_map/ppermute | solution.py:795
  60.6 32.4 %collective-permute-start.8 = (bf16[512,512]{1,0:T(8,128)(2,1)}, bf16[512,512]{1,0:T(8,128)(2,1)}, u32[]{:S(2)}, u32[]{:S(2)}) collective-permute-start(bf16[512,512]{1,0:T(8,128)(2,1)} %collective-permute-done.1.refs_6_.refs_2_.refs_3_), channel_id=1, source_target_pairs={{0,8},{4,12},{8,0},{12,4},{1,9},{5,13},{9,1},{13,5},{2,10},{6,14},... | collective-permute-start | bytes 1572872 | tf_op jit(solution)/shard_map/ppermute | solution.py:795
  69.5 25.0 %collective-permute-start.7 = (bf16[512,512]{1,0:T(8,128)(2,1)}, bf16[512,512]{1,0:T(8,128)(2,1)}, u32[]{:S(2)}, u32[]{:S(2)}) collective-permute-start(bf16[512,512]{1,0:T(8,128)(2,1)} %collective-permute-done.2.refs_2_.refs_7_.refs_3_.refs_5_.refs_4_), channel_id=1, source_target_pairs={{0,1},{1,2},{2,3},{3,0},{4,5},{5,6},{6,7},{7,4},{8,9},{9,10},{10,1... | collective-permute-start | bytes 1572872 | tf_op jit(solution)/shard_map/ppermute | solution.py:800
  89.3 31.6 %collective-permute-start.6 = (bf16[512,1024]{1,0:T(8,128)(2,1)S(1)}, bf16[512,1024]{1,0:T(8,128)(2,1)S(1)}, u32[]{:S(2)}, u32[]{:S(2)}) collective-permute-start(bf16[512,1024]{1,0:T(8,128)(2,1)S(1)} %norm_in.2.refs_3_.refs_1_), channel_id=1, source_target_pairs={{0,4},{4,0},{8,12},{12,8},{1,5},{5,1},{9,13},{13,9},{2,6},{6,2},{1... | collective-permute-start | bytes 3145736 | tf_op jit(solution)/shard_map/ppermute | solution.py:795
  89.4 16.8 %collective-permute-start.11 = (bf16[512,512]{1,0:T(8,128)(2,1)}, bf16[512,512]{1,0:T(8,128)(2,1)S(1)}, u32[]{:S(2)}, u32[]{:S(2)}) collective-permute-start(bf16[512,512]{1,0:T(8,128)(2,1)} %copy-done.118), channel_id=1, source_target_pairs={{0,1},{1,2},{2,3},{3,0},{4,5},{5,6},{6,7},{7,4},{8,9},{9,10},{10,1... | collective-permute-start | bytes 1572872 | tf_op jit(solution)/shard_map/ppermute | solution.py:800
  91.9 25.5 %collective-permute-start.12 = (bf16[512,512]{1,0:T(8,128)(2,1)}, bf16[512,512]{1,0:T(8,128)(2,1)S(1)}, u32[]{:S(2)}, u32[]{:S(2)}) collective-permute-start(bf16[512,512]{1,0:T(8,128)(2,1)} %copy-done.67), channel_id=1, source_target_pairs={{0,1},{1,2},{2,3},{3,0},{4,5},{5,6},{6,7},{7,4},{8,9},{9,10},{10,1... | collective-permute-start | bytes 1572872 | tf_op jit(solution)/shard_map/ppermute | solution.py:800
  93.0 15.1 %collective-permute-start.9 = (bf16[512,512]{1,0:T(8,128)(2,1)}, bf16[512,512]{1,0:T(8,128)(2,1)S(1)}, u32[]{:S(2)}, u32[]{:S(2)}) collective-permute-start(bf16[512,512]{1,0:T(8,128)(2,1)} %collective-permute-done.2.refs_2_.refs_7_.refs_3_.refs_5_.refs_4_), channel_id=1, source_target_pairs={{0,8},{4,12},{8,0},{12,4},{1,9},{5,13},{9,1},{13,5},{2,10},{6,14},... | collective-permute-start | bytes 1572872 | tf_op jit(solution)/shard_map/ppermute | solution.py:795
  94.5 24.8 %collective-permute-start.10 = (bf16[512,512]{1,0:T(8,128)(2,1)}, bf16[512,512]{1,0:T(8,128)(2,1)S(1)}, u32[]{:S(2)}, u32[]{:S(2)}) collective-permute-start(bf16[512,512]{1,0:T(8,128)(2,1)} %collective-permute-done.7.refs_8_.refs_4_.refs_6_.refs_5_), channel_id=1, source_target_pairs={{0,8},{4,12},{8,0},{12,4},{1,9},{5,13},{9,1},{13,5},{2,10},{6,14},... | collective-permute-start | bytes 1572872 | tf_op jit(solution)/shard_map/ppermute | solution.py:795
  106.2 36.3 %collective-permute-start.13 = (bf16[512,512]{1,0:T(8,128)(2,1)S(1)}, bf16[512,512]{1,0:T(8,128)(2,1)S(1)}, u32[]{:S(2)}, u32[]{:S(2)}) collective-permute-start(bf16[512,512]{1,0:T(8,128)(2,1)S(1)} %collective-permute-done.11.refs_13_.refs_3_.refs_2_), channel_id=1, source_target_pairs={{0,1},{1,2},{2,3},{3,0},{4,5},{5,6},{6,7},{7,4},{8,9},{9,10},{10,1... | collective-permute-start | bytes 1572872 | tf_op jit(solution)/shard_map/ppermute | solution.py:800
  108.1 34.5 %collective-permute-start.15 = (bf16[512,512]{1,0:T(8,128)(2,1)S(1)}, bf16[512,512]{1,0:T(8,128)(2,1)S(1)}, u32[]{:S(2)}, u32[]{:S(2)}) collective-permute-start(bf16[512,512]{1,0:T(8,128)(2,1)S(1)} %collective-permute-done.11.refs_13_.refs_3_.refs_2_), channel_id=1, source_target_pairs={{0,8},{4,12},{8,0},{12,4},{1,9},{5,13},{9,1},{13,5},{2,10},{6,14},... | collective-permute-start | bytes 1572872 | tf_op jit(solution)/shard_map/ppermute | solution.py:795
  117.4 25.1 %collective-permute-start.14 = (bf16[512,512]{1,0:T(8,128)(2,1)S(1)}, bf16[512,512]{1,0:T(8,128)(2,1)S(1)}, u32[]{:S(2)}, u32[]{:S(2)}) collective-permute-start(bf16[512,512]{1,0:T(8,128)(2,1)S(1)} %collective-permute-done.12.refs_14_.refs_2_.refs_4_), channel_id=1, source_target_pairs={{0,1},{1,2},{2,3},{3,0},{4,5},{5,6},{6,7},{7,4},{8,9},{9,10},{10,1... | collective-permute-start | bytes 1572872 | tf_op jit(solution)/shard_map/ppermute | solution.py:800
  119.3 23.2 %collective-permute-start.16 = (bf16[512,512]{1,0:T(8,128)(2,1)S(1)}, bf16[512,512]{1,0:T(8,128)(2,1)S(1)}, u32[]{:S(2)}, u32[]{:S(2)}) collective-permute-start(bf16[512,512]{1,0:T(8,128)(2,1)S(1)} %collective-permute-done.12.refs_14_.refs_2_.refs_4_), channel_id=1, source_target_pairs={{0,8},{4,12},{8,0},{12,4},{1,9},{5,13},{9,1},{13,5},{2,10},{6,14},... | collective-permute-start | bytes 1572872 | tf_op jit(solution)/shard_map/ppermute | solution.py:795
  142.5 161.5 %copy-start.106 = (bf16[512,512]{1,0:T(8,128)(2,1)}, bf16[512,512]{1,0:T(8,128)(2,1)S(1)}, u32[]{:S(2)}) copy-start(bf16[512,512]{1,0:T(8,128)(2,1)S(1)} %collective-permute-done.13.refs_9_.refs_4_.refs_3_) | copy-start | bytes 1572868
  146.6 28.1 %collective-permute-start.17 = (bf16[512,1024]{1,0:T(8,128)(2,1)S(1)}, bf16[512,1024]{1,0:T(8,128)(2,1)S(1)}, u32[]{:S(2)}, u32[]{:S(2)}) collective-permute-start(bf16[512,1024]{1,0:T(8,128)(2,1)S(1)} %get-tuple-element.101), channel_id=1, source_target_pairs={{0,4},{4,0},{8,12},{12,8},{1,5},{5,1},{9,13},{13,9},{2,6},{6,2},{1... | collective-permute-start | bytes 3145736 | tf_op jit(solution)/shard_map/ppermute | solution.py:795
  146.7 16.6 %collective-permute-start.18 = (bf16[512,512]{1,0:T(8,128)(2,1)S(1)}, bf16[512,512]{1,0:T(8,128)(2,1)S(1)}, u32[]{:S(2)}, u32[]{:S(2)}) collective-permute-start(bf16[512,512]{1,0:T(8,128)(2,1)S(1)} %collective-permute-done.13.refs_9_.refs_4_.refs_3_), channel_id=1, source_target_pairs={{0,1},{1,2},{2,3},{3,0},{4,5},{5,6},{6,7},{7,4},{8,9},{9,10},{10,1... | collective-permute-start | bytes 1572872 | tf_op jit(solution)/shard_map/ppermute | solution.py:800
  149.2 24.8 %collective-permute-start.19 = (bf16[512,512]{1,0:T(8,128)(2,1)S(1)}, bf16[512,512]{1,0:T(8,128)(2,1)S(1)}, u32[]{:S(2)}, u32[]{:S(2)}) collective-permute-start(bf16[512,512]{1,0:T(8,128)(2,1)S(1)} %collective-permute-done.14.refs_10_.refs_3_.refs_5_), channel_id=1, source_target_pairs={{0,1},{1,2},{2,3},{3,0},{4,5},{5,6},{6,7},{7,4},{8,9},{9,10},{10,1... | collective-permute-start | bytes 1572872 | tf_op jit(solution)/shard_map/ppermute | solution.py:800
  149.7 24.4 %collective-permute-start.20 = (bf16[512,512]{1,0:T(8,128)(2,1)S(1)}, bf16[512,512]{1,0:T(8,128)(2,1)S(1)}, u32[]{:S(2)}, u32[]{:S(2)}) collective-permute-start(bf16[512,512]{1,0:T(8,128)(2,1)S(1)} %collective-permute-done.13.refs_9_.refs_4_.refs_3_), channel_id=1, source_target_pairs={{0,8},{4,12},{8,0},{12,4},{1,9},{5,13},{9,1},{13,5},{2,10},{6,14},... | collective-permute-start | bytes 1572872 | tf_op jit(solution)/shard_map/ppermute | solution.py:795
  150.2 24.5 %collective-permute-start.21 = (bf16[512,512]{1,0:T(8,128)(2,1)S(1)}, bf16[512,512]{1,0:T(8,128)(2,1)S(1)}, u32[]{:S(2)}, u32[]{:S(2)}) collective-permute-start(bf16[512,512]{1,0:T(8,128)(2,1)S(1)} %collective-permute-done.14.refs_10_.refs_3_.refs_5_), channel_id=1, source_target_pairs={{0,8},{4,12},{8,0},{12,4},{1,9},{5,13},{9,1},{13,5},{2,10},{6,14},... | collective-permute-start | bytes 1572872 | tf_op jit(solution)/shard_map/ppermute | solution.py:795
  179.5 14.9 %collective-permute-start.22 = (bf16[512,1024]{1,0:T(8,128)(2,1)S(1)}, bf16[512,1024]{1,0:T(8,128)(2,1)S(1)}, u32[]{:S(2)}, u32[]{:S(2)}) collective-permute-start(bf16[512,1024]{1,0:T(8,128)(2,1)S(1)} %get-tuple-element.103.refs_0_.refs_1_), channel_id=1, source_target_pairs={{0,4},{4,0},{8,12},{12,8},{1,5},{5,1},{9,13},{13,9},{2,6},{6,2},{1... | collective-permute-start | bytes 3145736 | tf_op jit(solution)/shard_map/ppermute | solution.py:795
  179.6 14.8 %collective-permute-start.23 = (bf16[512,512]{1,0:T(8,128)(2,1)S(1)}, bf16[512,512]{1,0:T(8,128)(2,1)S(1)}, u32[]{:S(2)}, u32[]{:S(2)}) collective-permute-start(bf16[512,512]{1,0:T(8,128)(2,1)S(1)} %collective-permute-done.18.refs_4_.refs_5_), channel_id=1, source_target_pairs={{0,8},{4,12},{8,0},{12,4},{1,9},{5,13},{9,1},{13,5},{2,10},{6,14},... | collective-permute-start | bytes 1572872 | tf_op jit(solution)/shard_map/ppermute | solution.py:795
  180.2 25.0 %collective-permute-start.24 = (bf16[512,512]{1,0:T(8,128)(2,1)S(1)}, bf16[512,512]{1,0:T(8,128)(2,1)S(1)}, u32[]{:S(2)}, u32[]{:S(2)}) collective-permute-start(bf16[512,512]{1,0:T(8,128)(2,1)S(1)} %collective-permute-done.19.refs_5_.refs_4_.refs_6_), channel_id=1, source_target_pairs={{0,8},{4,12},{8,0},{12,4},{1,9},{5,13},{9,1},{13,5},{2,10},{6,14},... | collective-permute-start | bytes 1572872 | tf_op jit(solution)/shard_map/ppermute | solution.py:795
  209.7 2.7 collective-permute-start.25
  215.7 25.8 %collective-permute-start.26 = (bf16[512,1024]{1,0:T(8,128)(2,1)S(1)}, bf16[512,1024]{1,0:T(8,128)(2,1)S(1)}, u32[]{:S(2)}, u32[]{:S(2)}) collective-permute-start(bf16[512,1024]{1,0:T(8,128)(2,1)S(1)} %get-tuple-element.132), channel_id=1, source_target_pairs={{0,16},{1,17},{2,18},{3,19},{4,20},{5,21},{6,22},{7,23},{8,24},{9,... | collective-permute-start | bytes 3145736 | tf_op jit(solution)/shard_map/ppermute | solution.py:28
  243.2 2.7 collective-permute-start.27
  266.2 2.7 collective-permute-start.28
  272.4 2.7 collective-permute-start.29
  287.4 2.7 collective-permute-start.30
  294.1 2.7 collective-permute-start.31
  310.2 2.7 collective-permute-start.32
  316.8 2.7 collective-permute-start.33
  354.4 2.7 collective-permute-start.34
  360.1 27.5 %collective-permute-start.35 = (bf16[512,1024]{1,0:T(8,128)(2,1)}, bf16[512,1024]{1,0:T(8,128)(2,1)}, u32[]{:S(2)}, u32[]{:S(2)}) collective-permute-start(bf16[512,1024]{1,0:T(8,128)(2,1)} %get-tuple-element.131), channel_id=1, source_target_pairs={{16,0},{17,1},{18,2},{19,3},{20,4},{21,5},{22,6},{23,7},{24,8},{25... | collective-permute-start | bytes 3145736 | tf_op jit(solution)/shard_map/ppermute | solution.py:28
  362.9 31.3 %all-to-all-start.1 = ((bf16[4,128,1024]{2,1,0:T(8,128)(2,1)}), bf16[4,128,1024]{2,1,0:T(8,128)(2,1)}, u32[]{:S(2)}, u32[]{:S(2)}) async-start(bf16[4,128,1024]{2,1,0:T(8,128)(2,1)} %bitcast.55), calls=%async_computation.1 | async-start | bytes 2097152 | tf_op jit(solution)/shard_map/all_to_all | solution.py:1209
  393.5 3.0 collective-permute-start.36
  429.1 6.7 %collective-permute-start.37 = (bf16[512,1024]{1,0:T(8,128)(2,1)}, bf16[512,1024]{1,0:T(8,128)(2,1)S(1)}, u32[]{:S(2)}, u32[]{:S(2)}) collective-permute-start(bf16[512,1024]{1,0:T(8,128)(2,1)} %get-tuple-element.139), channel_id=1, source_target_pairs={{0,4},{4,0},{8,12},{12,8},{1,5},{5,1},{9,13},{13,9},{2,6},{6,2},{1... | collective-permute-start | bytes 3145736 | tf_op jit(solution)/shard_map/ppermute | solution.py:795
  429.2 26.2 %collective-permute-start.40 = (bf16[1024,512]{1,0:T(8,128)(2,1)}, bf16[1024,512]{1,0:T(8,128)(2,1)S(1)}, u32[]{:S(2)}, u32[]{:S(2)}) collective-permute-start(bf16[1024,512]{1,0:T(8,128)(2,1)} %get-tuple-element.148), channel_id=1, source_target_pairs={{0,8},{4,12},{8,0},{12,4},{1,9},{5,13},{9,1},{13,5},{2,10},{6,14},... | collective-permute-start | bytes 3145736 | tf_op jit(solution)/shard_map/ppermute | solution.py:795
  441.9 17.9 %collective-permute-start.38 = (bf16[512,1024]{1,0:T(8,128)(2,1)S(1)}, bf16[512,1024]{1,0:T(8,128)(2,1)S(1)}, u32[]{:S(2)}, u32[]{:S(2)}) collective-permute-start(bf16[512,1024]{1,0:T(8,128)(2,1)S(1)} %get-tuple-element.142.refs_2_.refs_3_.refs_5_), channel_id=1, source_target_pairs={{0,4},{4,0},{8,12},{12,8},{1,5},{5,1},{9,13},{13,9},{2,6},{6,2},{1... | collective-permute-start | bytes 3145736 | tf_op jit(solution)/shard_map/ppermute | solution.py:795
  442.1 35.7 %collective-permute-start.39 = (bf16[1024,512]{1,0:T(8,128)(2,1)S(1)}, bf16[1024,512]{1,0:T(8,128)(2,1)S(1)}, u32[]{:S(2)}, u32[]{:S(2)}) collective-permute-start(bf16[1024,512]{1,0:T(8,128)(2,1)S(1)} %copy-done.138), channel_id=1, source_target_pairs={{0,8},{4,12},{8,0},{12,4},{1,9},{5,13},{9,1},{13,5},{2,10},{6,14},... | collective-permute-start | bytes 3145736 | tf_op jit(solution)/shard_map/ppermute | solution.py:795
  443.6 68.6 %collective-permute-start.42 = (bf16[1024,512]{1,0:T(8,128)(2,1)}, bf16[1024,512]{1,0:T(8,128)(2,1)S(1)}, u32[]{:S(2)}, u32[]{:S(2)}) collective-permute-start(bf16[1024,512]{1,0:T(8,128)(2,1)} %copy-done.136), channel_id=1, source_target_pairs={{0,8},{4,12},{8,0},{12,4},{1,9},{5,13},{9,1},{13,5},{2,10},{6,14},... | collective-permute-start | bytes 3145736 | tf_op jit(solution)/shard_map/ppermute | solution.py:795
  444.2 87.3 %collective-permute-start.45 = (bf16[1024,512]{1,0:T(8,128)(2,1)}, bf16[1024,512]{1,0:T(8,128)(2,1)}, u32[]{:S(2)}, u32[]{:S(2)}) collective-permute-start(bf16[1024,512]{1,0:T(8,128)(2,1)} %copy-done.135), channel_id=1, source_target_pairs={{0,8},{4,12},{8,0},{12,4},{1,9},{5,13},{9,1},{13,5},{2,10},{6,14},... | collective-permute-start | bytes 3145736 | tf_op jit(solution)/shard_map/ppermute | solution.py:795
  456.4 25.1 %collective-permute-start.41 = (bf16[1024,512]{1,0:T(8,128)(2,1)S(1)}, bf16[1024,512]{1,0:T(8,128)(2,1)S(1)}, u32[]{:S(2)}, u32[]{:S(2)}) collective-permute-start(bf16[1024,512]{1,0:T(8,128)(2,1)S(1)} %moved.6), channel_id=1, source_target_pairs={{0,3},{1,0},{2,1},{3,2},{4,7},{5,4},{6,5},{7,6},{8,11},{9,8},{10,9... | collective-permute-start | bytes 3145736 | tf_op jit(solution)/shard_map/ppermute | solution.py:800
  482.0 30.2 %collective-permute-start.43 = (bf16[1024,512]{1,0:T(8,128)(2,1)S(1)}, bf16[1024,512]{1,0:T(8,128)(2,1)S(1)}, u32[]{:S(2)}, u32[]{:S(2)}) collective-permute-start(bf16[1024,512]{1,0:T(8,128)(2,1)S(1)} %moved.7), channel_id=1, source_target_pairs={{0,3},{1,0},{2,1},{3,2},{4,7},{5,4},{6,5},{7,6},{8,11},{9,8},{10,9... | collective-permute-start | bytes 3145736 | tf_op jit(solution)/shard_map/ppermute | solution.py:800
  520.3 29.9 %collective-permute-start.44 = (bf16[512,1024]{1,0:T(8,128)(2,1)}, bf16[512,1024]{1,0:T(8,128)(2,1)}, u32[]{:S(2)}, u32[]{:S(2)}) collective-permute-start(bf16[512,1024]{1,0:T(8,128)(2,1)} %get-tuple-element.154), channel_id=1, source_target_pairs={{0,4},{4,0},{8,12},{12,8},{1,5},{5,1},{9,13},{13,9},{2,6},{6,2},{1... | collective-permute-start | bytes 3145736 | tf_op jit(solution)/shard_map/ppermute | solution.py:795
  521.8 28.4 %collective-permute-start.48 = (bf16[1024,512]{1,0:T(8,128)(2,1)}, bf16[1024,512]{1,0:T(8,128)(2,1)S(1)}, u32[]{:S(2)}, u32[]{:S(2)}) collective-permute-start(bf16[1024,512]{1,0:T(8,128)(2,1)} %moved.8), channel_id=1, source_target_pairs={{0,3},{1,0},{2,1},{3,2},{4,7},{5,4},{6,5},{7,6},{8,11},{9,8},{10,9... | collective-permute-start | bytes 3145736 | tf_op jit(solution)/shard_map/ppermute | solution.py:800
  523.9 15.0 %collective-permute-start.46 = (bf16[512,512]{1,0:T(8,128)(2,1)}, bf16[512,512]{1,0:T(8,128)(2,1)S(1)}, u32[]{:S(2)}, u32[]{:S(2)}) collective-permute-start(bf16[512,512]{1,0:T(8,128)(2,1)} %get-tuple-element.157), channel_id=1, source_target_pairs={{0,8},{4,12},{8,0},{12,4},{1,9},{5,13},{9,1},{13,5},{2,10},{6,14},... | collective-permute-start | bytes 1572872 | tf_op jit(solution)/shard_map/ppermute | solution.py:795
  524.4 25.0 %collective-permute-start.47 = (bf16[512,512]{1,0:T(8,128)(2,1)}, bf16[512,512]{1,0:T(8,128)(2,1)S(1)}, u32[]{:S(2)}, u32[]{:S(2)}) collective-permute-start(bf16[512,512]{1,0:T(8,128)(2,1)} %get-tuple-element.158), channel_id=1, source_target_pairs={{0,8},{4,12},{8,0},{12,4},{1,9},{5,13},{9,1},{13,5},{2,10},{6,14},... | collective-permute-start | bytes 1572872 | tf_op jit(solution)/shard_map/ppermute | solution.py:795
  566.0 9.9 %all-to-all-start.3 = ((f32[16,1,256]{2,1,0:T(1,128)}), f32[16,1,256]{2,1,0:T(1,128)S(1)}, u32[]{:S(2)}, u32[]{:S(2)}) async-start(f32[16,1,256]{2,1,0:T(1,128)} %reshape.144), calls=%async_computation.3 | async-start | bytes 32768 | tf_op jit(solution)/shard_map/all_to_all | solution.py:1279
  575.8 47.7 %all-to-all-start.2 = ((bf16[4,128,1024]{2,1,0:T(8,128)(2,1)}), bf16[4,128,1024]{2,1,0:T(8,128)(2,1)}, u32[]{:S(2)}, u32[]{:S(2)}) async-start(bf16[4,128,1024]{2,1,0:T(8,128)(2,1)} %bitcast.54), calls=%async_computation.2 | async-start | bytes 2097152 | tf_op jit(solution)/shard_map/all_to_all | solution.py:1286
  580.5 30.7 %collective-permute-start.53 = (bf16[512,512]{1,0:T(8,128)(2,1)S(1)}, bf16[512,512]{1,0:T(8,128)(2,1)S(1)}, u32[]{:S(2)}, u32[]{:S(2)}) collective-permute-start(bf16[512,512]{1,0:T(8,128)(2,1)S(1)} %moved.9), channel_id=1, source_target_pairs={{0,3},{1,0},{2,1},{3,2},{4,7},{5,4},{6,5},{7,6},{8,11},{9,8},{10,9... | collective-permute-start | bytes 1572872 | tf_op jit(solution)/shard_map/ppermute | solution.py:800
  584.3 30.2 %collective-permute-start.49 = (bf16[512,512]{1,0:T(8,128)(2,1)S(1)}, bf16[512,512]{1,0:T(8,128)(2,1)S(1)}, u32[]{:S(2)}, u32[]{:S(2)}) collective-permute-start(bf16[512,512]{1,0:T(8,128)(2,1)S(1)} %copy-done.144), channel_id=1, source_target_pairs={{0,8},{4,12},{8,0},{12,4},{1,9},{5,13},{9,1},{13,5},{2,10},{6,14},... | collective-permute-start | bytes 1572872 | tf_op jit(solution)/shard_map/ppermute | solution.py:795
  584.9 38.6 %collective-permute-start.51 = (bf16[512,512]{1,0:T(8,128)(2,1)}, bf16[512,512]{1,0:T(8,128)(2,1)}, u32[]{:S(2)}, u32[]{:S(2)}) collective-permute-start(bf16[512,512]{1,0:T(8,128)(2,1)} %get-tuple-element.163), channel_id=1, source_target_pairs={{0,8},{4,12},{8,0},{12,4},{1,9},{5,13},{9,1},{13,5},{2,10},{6,14},... | collective-permute-start | bytes 1572872 | tf_op jit(solution)/shard_map/ppermute | solution.py:795
  612.3 18.8 %collective-permute-start.54 = (bf16[512,512]{1,0:T(8,128)(2,1)}, bf16[512,512]{1,0:T(8,128)(2,1)}, u32[]{:S(2)}, u32[]{:S(2)}) collective-permute-start(bf16[512,512]{1,0:T(8,128)(2,1)} %moved.10), channel_id=1, source_target_pairs={{0,3},{1,0},{2,1},{3,2},{4,7},{5,4},{6,5},{7,6},{8,11},{9,8},{10,9... | collective-permute-start | bytes 1572872 | tf_op jit(solution)/shard_map/ppermute | solution.py:800
  617.6 18.1 %collective-permute-start.50 = (bf16[2,128,1024]{2,1,0:T(8,128)(2,1)}, bf16[2,128,1024]{2,1,0:T(8,128)(2,1)}, u32[]{:S(2)}, u32[]{:S(2)}) collective-permute-start(bf16[2,128,1024]{2,1,0:T(8,128)(2,1)} %get-tuple-element.162), channel_id=1, source_target_pairs={{0,4},{4,0},{8,12},{12,8},{1,5},{5,1},{9,13},{13,9},{2,6},{6,2},{1... | collective-permute-start | bytes 1572872 | tf_op jit(solution)/shard_map/ppermute | solution.py:795
  621.7 17.0 %collective-permute-start.56 = (f32[256,512]{1,0:T(8,128)}, f32[256,512]{1,0:T(8,128)}, u32[]{:S(2)}, u32[]{:S(2)}) collective-permute-start(f32[256,512]{1,0:T(8,128)} %get-tuple-element.179), channel_id=1, source_target_pairs={{0,4},{4,0},{8,12},{12,8},{1,5},{5,1},{9,13},{13,9},{2,6},{6,2},{1... | collective-permute-start | bytes 1572872 | tf_op jit(solution)/shard_map/ppermute | solution.py:795
  622.2 16.6 %collective-permute-start.57 = (f32[512,256]{1,0:T(8,128)}, f32[512,256]{1,0:T(8,128)}, u32[]{:S(2)}, u32[]{:S(2)}) collective-permute-start(f32[512,256]{1,0:T(8,128)} %get-tuple-element.180), channel_id=1, source_target_pairs={{0,4},{4,0},{8,12},{12,8},{1,5},{5,1},{9,13},{13,9},{2,6},{6,2},{1... | collective-permute-start | bytes 1572872 | tf_op jit(solution)/shard_map/ppermute | solution.py:795
  624.8 16.7 %collective-permute-start.52 = (bf16[2,128,1024]{2,1,0:T(8,128)(2,1)S(1)}, bf16[2,128,1024]{2,1,0:T(8,128)(2,1)S(1)}, u32[]{:S(2)}, u32[]{:S(2)}) collective-permute-start(bf16[2,128,1024]{2,1,0:T(8,128)(2,1)S(1)} %get-tuple-element.165), channel_id=1, source_target_pairs={{0,4},{4,0},{8,12},{12,8},{1,5},{5,1},{9,13},{13,9},{2,6},{6,2},{1... | collective-permute-start | bytes 1572872 | tf_op jit(solution)/shard_map/ppermute | solution.py:795
  634.7 12.7 %collective-permute-start.55 = (bf16[512,512]{1,0:T(8,128)(2,1)S(1)}, bf16[512,512]{1,0:T(8,128)(2,1)S(1)}, u32[]{:S(2)}, u32[]{:S(2)}) collective-permute-start(bf16[512,512]{1,0:T(8,128)(2,1)S(1)} %moved.11), channel_id=1, source_target_pairs={{0,3},{1,0},{2,1},{3,2},{4,7},{5,4},{6,5},{7,6},{8,11},{9,8},{10,9... | collective-permute-start | bytes 1572872 | tf_op jit(solution)/shard_map/ppermute | solution.py:800
  649.9 2.0 collective-permute-start.58
  (151 other events, 2332.9 us)

commit v10 on v9

--- a/solution.py
+++ b/solution.py
@@ -676,6 +676,10 @@
     return pl.CostEstimate(flops=flops, bytes_accessed=size, transcendentals=0)
 
 
+def far(array):
+    return pltpu.with_memory_space_constraint(array, pltpu.HBM)
+
+
 def without(kernel, first, count):
     return lambda *refs: kernel(*refs[:first], *refs[first + count :])
 
@@ -691,7 +695,7 @@
         compiler_params=pltpu.CompilerParams(vmem_limit_bytes=limit),
         cost_estimate=work(flops, (*operands, *shapes)),
         name=name,
-    )(*operands, *waits)
+    )(*operands, *map(far, waits))
 
 
 def whole_block(array):
@@ -714,7 +718,7 @@
         compiler_params=pltpu.CompilerParams(vmem_limit_bytes=KERNEL_VMEM),
         cost_estimate=work(flops, (*operands, *pieces[0], *pieces[1], *shapes)),
         name=name,
-    )(core, *operands, *pieces[0], *pieces[1], *[array for array, _ in blocks], *waits)
+    )(core, *operands, *pieces[0], *pieces[1], *[array for array, _ in blocks], *map(far, waits))
 
 
 def mlp_up_back(rows, slope, pieces, waits):
@@ -722,10 +726,9 @@
     unit, half = pieces[0][0].shape
     count = len(pieces[0])
     every, space = pl.BlockSpec(memory_space=pl.ANY), pl.BlockSpec(memory_space=pltpu.VMEM)
-    far = pl.BlockSpec(memory_space=pltpu.HBM)
     return pl.pallas_call(
         without(functools.partial(mlp_up_back_kernel, count), 3 + 2 * count, len(waits)),
-        in_specs=[space] * 2 + [far] * (1 + 2 * count) + [every] * len(waits),
+        in_specs=[space] * 2 + [every] * (1 + 2 * count + len(waits)),
         out_specs=space,
         out_shape=jax.ShapeDtypeStruct((length, units), jnp.bfloat16),
         scratch_shapes=[
@@ -735,7 +738,7 @@
         ],
         compiler_params=pltpu.CompilerParams(vmem_limit_bytes=KERNEL_VMEM),
         name="mlp_up_back",
-    )(*rows, slope, *pieces[0], *pieces[1], *waits)
+    )(*rows, *map(far, (slope, *pieces[0], *pieces[1], *waits)))
 
 
 def attend(core, tables, rows, pieces, waits):
@@ -909,7 +912,7 @@
         ],
         compiler_params=pltpu.CompilerParams(vmem_limit_bytes=KERNEL_VMEM),
         name=name,
-    )(section, *arrays, *waits)
+    )(section, *map(far, (*arrays, *waits)))
     return [(first, flip_pairs(second, 2)), (third, flip_pairs(fourth, 2))]
 
 
@@ -927,9 +930,8 @@
     lax.fori_loop(0, own_ref.shape[0] // CHUNK, body, 0)
 
 
-def gate_kernel(up_ref, down_ref, up_out, down_out):
-    up_out[...] = up_ref[...]
-    down_out[...] = down_ref[...]
+def gate_kernel(piece_ref, out_ref):
+    out_ref[...] = piece_ref[...]
 
 
 def mlp_sum_kernel(core_ref, own_ref, other_ref, moved_ref, up_keep, down_keep, up_send, down_send):
@@ -991,7 +993,7 @@
         out_shape=[jax.ShapeDtypeStruct(shape, dtype) for shape, dtype in outs],
         compiler_params=pltpu.CompilerParams(vmem_limit_bytes=ROWS_VMEM),
         name=name,
-    )(core, *operands, *waits)
+    )(core, *operands, *map(far, waits))
 
 
 def last_sum_kernel(core_ref, own_ref, other_ref, moved_ref, keep_ref, send_ref):
@@ -1099,9 +1101,19 @@
     attn_other = [flip_pairs(piece, 2) for piece in attn_own]
     up_piece, down_piece = columns(up_weight[0]), rows(down_weight[0])
     up_other, down_other = [flip_pairs(up_piece, 2)], [flip_pairs(down_piece, 2)]
-    outs = tuple((piece.shape, piece.dtype) for piece in (up_piece, down_piece))
-    up_piece, down_piece = on_chip(
-        gate_kernel, "gate", outs, up_piece, down_piece, waits=(attn_own[2], attn_other[0])
+    (up_piece,) = on_chip(
+        gate_kernel,
+        "gate",
+        ((up_piece.shape, up_piece.dtype),),
+        up_piece,
+        waits=(attn_own[2], attn_other[0]),
+    )
+    (down_piece,) = on_chip(
+        gate_kernel,
+        "gate",
+        ((down_piece.shape, down_piece.dtype),),
+        down_piece,
+        waits=(attn_own[3],),
     )
     up_own, down_own = spread(up_piece), spread(down_piece)
     up_other += [flip_pairs(piece, 2) for piece in up_own[1:]]
@@ -1196,8 +1208,8 @@
         (
             (up_piece, up_other[0], down_other[0]),
             (up_own[1], down_own[1]),
-            (up_own[2], down_own[2], up_other[1], down_other[1]),
-            (up_own[3], down_own[3], up_other[2], down_other[2]),
+            (up_own[2], down_own[2], up_other[1]),
+            (up_own[3], down_own[3], down_other[1], up_other[2]),
         ),
     )
     low_one, saved_one, lefts_one = forward(shifted(low_zero, "section", 1), ((),) * 4)
@@ -1224,7 +1236,7 @@
             (2 * unit, 2 * unit),
         )
 
-    def attn_leaves(base, d_qkv):
+    def attn_leaves(base, d_qkv, waits):
         zeros = (*lefts_zero[0], d_qkv, lefts_zero[1], *d_attn)
         ones = (*lefts_one[0], rights_one[0][base // 2], lefts_one[1], *rights_one[1])
         attn_sums[base : base + 2] = weight_grads(
@@ -1236,12 +1248,13 @@
             ones,
             (wide_half, 512),
             (768, 256),
+            waits,
         )
 
     def moves_on(piece, *moved, waits=()):
         outs = ((piece[1].shape, jnp.bfloat16),)
         (total,) = on_chip(moved_kernel, "moved", outs, *piece, *moved, waits=waits)
-        return passed_on(total, -1)
+        return total, passed_on(total, -1)
 
     mlp_sums, attn_sums = [None] * tensor, [None] * tensor
     mlp_moves, attn_moves = [None] * tensor, [None] * tensor
@@ -1259,31 +1272,35 @@
             return (mlp_sums[1][0],)
         if turn == 2:
             (d_attn,) = new
-            mlp_moves[3] = moves_on(mlp_sums[3], waits=d_attn[:1])
+            _, mlp_moves[3] = moves_on(mlp_sums[3], waits=d_attn[:1])
             return (mlp_sums[3][1],)
         if turn == 3:
-            mlp_moves[2] = moves_on(mlp_sums[2], mlp_moves[3], waits=new)
-            attn_leaves(2, new[0])
+            total, mlp_moves[2] = moves_on(mlp_sums[2], mlp_moves[3], waits=new)
+            attn_leaves(2, new[0], (total,))
             return (mlp_sums[2][1], mlp_moves[3], attn_sums[3][0])
         if turn == 4:
-            mlp_moves[1] = moves_on(mlp_sums[1], mlp_moves[2], waits=new)
-            attn_leaves(0, new[0])
-            return (mlp_sums[1][1], mlp_moves[2], attn_sums[1][0])
-        return (mlp_sums[0][1], attn_sums[3][1], attn_sums[2][1], mlp_moves[1])
+            total, mlp_moves[1] = moves_on(mlp_sums[1], mlp_moves[2], waits=new)
+            attn_leaves(0, new[0], (total,))
+            return (attn_sums[1][0],)
+        total, attn_moves[3] = moves_on(attn_sums[3])
+        return (mlp_sums[0][1], total, mlp_moves[1])
 
     d_down = d_up = d_attn = None
     grad_zero, rights_zero, gain_zero = backward(received, saved_zero, hook, (lows,))
+    _, attn_moves[2] = moves_on(attn_sums[2], attn_moves[3])
+    last, attn_moves[1] = moves_on(attn_sums[1], attn_moves[2], waits=attn_sums[0][1:])
+    gain_zero, gain_one = lax.optimization_barrier((gain_zero, gain_one))
     gain_total = own_first(jnp.where(first, gain_zero, gain_one))
     count = tensor * lax.axis_size("dp")
     gain_parts = gain_total.reshape(4, count, width // count).swapaxes(0, 1)
+    (gain_parts,) = on_chip(
+        gate_kernel, "gate", ((gain_parts.shape, gain_parts.dtype),), gain_parts, waits=(last,)
+    )
     gain_parts = lax.all_to_all(gain_parts, ("dp", "tensor"), 0, 0, tiled=True)
     gains_grad = jnp.sum(gain_parts, axis=0)
-    attn_moves[3] = moves_on(attn_sums[3])
-    attn_moves[2] = moves_on(attn_sums[2], attn_moves[3])
-    attn_moves[1] = moves_on(attn_sums[1], attn_moves[2], waits=(gains_grad,))
-    outputs = from_chip(lows, (grad_zero, attn_sums[1][1]))
+    outputs = from_chip(lows, (last,))
     grads = own_first(jnp.where(first, grad_zero, grad_one)).reshape(tensor, part, width)
-    grads = from_chip(lax.all_to_all(grads, "tensor", 0, 0, tiled=True), attn_sums[0][1:])
+    grads = from_chip(lax.all_to_all(grads, "tensor", 0, 0, tiled=True), (last,))
 
     block32 = ((wide_half // 2, unit), jnp.float32)
     down32 = ((unit, wide_half // 2), jnp.float32)
@@ -1294,6 +1311,7 @@
         (block32, down32, block32, down32),
         *mlp_sums[0],
         mlp_moves[1],
+        waits=(last,),
     )
     outs = (
         ((wide_half // 2, 2 * unit), jnp.float32),

time: 667 us -> 660 us (0.990)
  waiting for transfers between devices: 248 us -> 260 us
  local copies, waits for them, and re-layouts: 72.5 us -> 62 us
    ppermute x42, waiting for transfers between devices: 87.6 us -> 112 us  [flip_pairs(): return lax.ppermute(block, 'dp', [(i, i ^ distance) for i in range(size)])]
    ppermute x15, waiting for transfers between devices: 114 us -> 101 us  [passed_on(): lax.ppermute(block, 'tensor', [(i, (i + step) % size) for i in range(size)])]
    unnamed x308 -> x286, local copies, waits for them, and re-layouts: 63.1 us -> 54.6 us
    pallas_call x29 -> x31, Pallas kernels: 96.1 us -> 91 us  [on_chip(): pl.pallas_call(without(kernel, len(operands), len(waits)), in_specs=[spac...]
  transfers between devices with their start and end apart: 63 -> 63, of which waited for: 37 -> 36; matrix products, arithmetic and copies ran while one was open for 3% -> 2% of each run, Pallas kernels for 16% -> 15%
where the time goes in v10:
time: 660 us; the launch traced here: 650 us
  waiting for transfers between devices  260 us (39%)
  Pallas kernels  233 us (35%)
  starting transfers between devices  81.2 us (12%)
  local copies, waits for them, and re-layouts  62 us (9%)
  other arithmetic  12.3 us (2%)
    ppermute x42, waiting for transfers between devices, flip_pairs(): return lax.ppermute(block, 'dp', [(i, i ^ distance) for i in range(size)])  112 us
    ppermute x15, waiting for transfers between devices, passed_on(): lax.ppermute(block, 'tensor', [(i, (i + step) % size) for i in range(size)])  101 us
    pallas_call x31, Pallas kernels, on_chip(): pl.pallas_call(without(kernel, len(operands), len(waits)), in_specs=[spac...  91 us
    pallas_call x6, Pallas kernels, by_pairs(): pl.pallas_call(without(functools.partial(kernel, len(pieces[0])), taken,...  85.2 us
    unnamed x286, local copies, waits for them, and re-layouts  54.6 us
    ppermute x2, waiting for transfers between devices, shifted(): return lax.ppermute(block, axis, route)  42.6 us
    ppermute x42, starting transfers between devices, flip_pairs(): return lax.ppermute(block, 'dp', [(i, i ^ distance) for i in range(size)])  28.6 us
    ppermute x15, starting transfers between devices, passed_on(): lax.ppermute(block, 'tensor', [(i, (i + step) % size) for i in range(size)])  27.6 us
  transfers between devices with their start and end apart: 63, of which 36 were waited for; matrix products, arithmetic and copies ran while one was open for 2% of the time, Pallas kernels for 15%

profile of v10, /device:TPU:0, one launch (start us, length us, event | category | flops | bytes accessed | tf_op | source)
XLA Modules:
  0.0 650.3 jit_solution(13445419033644653711)
XLA Ops:
  14.9 6.0 all-to-all-start
  24.5 29.6 %collective-permute-done.1.refs_6_.refs_2_.refs_3_ = bf16[512,512]{1,0:T(8,128)(2,1)} collective-permute-done((bf16[512,512]{1,0:T(8,128)(2,1)}, bf16[512,512]{1,0:T(8,128)(2,1)}, u32[]{:S(2)}, u32[]{:S(2)}) %collective-permute-start.1) | collective-permute-done | bytes 524320 | tf_op jit(solution)/shard_map/ppermute | solution.py:803
  54.1 3.3 collective-permute-start.2
  62.2 7.3 %collective-permute-done.2.refs_1_.refs_7_.refs_3_.refs_5_.refs_4_ = bf16[512,512]{1,0:T(8,128)(2,1)} collective-permute-done((bf16[512,512]{1,0:T(8,128)(2,1)}, bf16[512,512]{1,0:T(8,128)(2,1)}, u32[]{:S(2)}, u32[]{:S(2)}) %collective-permute-start.2) | collective-permute-done | bytes 524320 | tf_op jit(solution)/shard_map/ppermute | solution.py:803
  72.3 11.2 %collective-permute-done.5.refs_4_.refs_5_.refs_7_ = bf16[512,512]{1,0:T(8,128)(2,1)S(1)} collective-permute-done((bf16[512,512]{1,0:T(8,128)(2,1)S(1)}, bf16[512,512]{1,0:T(8,128)(2,1)S(1)}, u32[]{:S(2)}, u32[]{:S(2)}) %collective-permute-start.5) | collective-permute-done | bytes 524320 | tf_op jit(solution)/shard_map/ppermute | solution.py:798
  86.2 2.5 collective-permute-start.11
  91.5 2.5 collective-permute-done.8.refs_10_.refs_6_.refs_8_.refs_7_
  98.4 4.6 collective-permute-done.11.refs_13_.refs_3_.refs_2_
  106.7 7.6 %collective-permute-done.12.refs_14_.refs_2_.refs_4_ = bf16[512,512]{1,0:T(8,128)(2,1)S(1)} collective-permute-done((bf16[512,512]{1,0:T(8,128)(2,1)S(1)}, bf16[512,512]{1,0:T(8,128)(2,1)S(1)}, u32[]{:S(2)}, u32[]{:S(2)}) %collective-permute-start.12) | collective-permute-done | bytes 524320 | tf_op jit(solution)/shard_map/ppermute | solution.py:803
  116.5 16.9 %attend.2 = (bf16[4,1024,128]{2,1,0:T(8,128)(2,1)S(1)}, bf16[4,1024,128]{2,1,0:T(8,128)(2,1)S(1)}, bf16[4,1024,128]{2,1,0:T(8,128)(2,1)S(1)}, f32[4,2,1024]{2,1,0:T(2,128)S(1)}, bf16[1024,512]{1,0:T(8,128)(2,1)S(1)}) custom-call(s32[1]{0:T(128)} %bitcast.refs_0_, f32[1024,128]{1,0:T(8,128)S(1)} %get-tuple-element.230.refs_1_, ...), custom_call_target="tpu_custom_call" | custom-call | flops 11811160064 | bytes 11567104 | tf_op jit(solution)/shard_map/attend/pallas_call | solution.py:708
  137.6 3.0 attn_out.2
  140.7 3.4 collective-permute-start.17
  146.4 11.1 %collective-permute-done.17.refs_4_.refs_5_ = bf16[512,512]{1,0:T(8,128)(2,1)S(1)} collective-permute-done((bf16[512,512]{1,0:T(8,128)(2,1)}, bf16[512,512]{1,0:T(8,128)(2,1)S(1)}, u32[]{:S(2)}, u32[]{:S(2)}) %collective-permute-start.17) | collective-permute-done | bytes 524320 | tf_op jit(solution)/shard_map/ppermute | solution.py:803
  158.8 10.5 %collective-permute-done.20.refs_7_.refs_8_ = bf16[512,512]{1,0:T(8,128)(2,1)S(1)} collective-permute-done((bf16[512,512]{1,0:T(8,128)(2,1)}, bf16[512,512]{1,0:T(8,128)(2,1)S(1)}, u32[]{:S(2)}, u32[]{:S(2)}) %collective-permute-start.20) | collective-permute-done | bytes 524320 | tf_op jit(solution)/shard_map/ppermute | solution.py:798
  170.3 3.4 after_attn.2
  178.8 11.4 %collective-permute-done.22.refs_9_.refs_8_ = bf16[512,512]{1,0:T(8,128)(2,1)S(1)} collective-permute-done((bf16[512,512]{1,0:T(8,128)(2,1)}, bf16[512,512]{1,0:T(8,128)(2,1)S(1)}, u32[]{:S(2)}, u32[]{:S(2)}) %collective-permute-start.22) | collective-permute-done | bytes 524320 | tf_op jit(solution)/shard_map/ppermute | solution.py:798
  192.5 9.1 %mlp_up.2 = (bf16[1024,2048]{1,0:T(8,128)(2,1)S(1)}, bf16[1024,2048]{1,0:T(8,128)(2,1)S(1)}) custom-call(bf16[512,1024]{1,0:T(8,128)(2,1)S(1)} %get-tuple-element.101.refs_0_.refs_1_, bf16[512,1024]{1,0:T(8,128)(2,1)S(1)} %collective-permute-done.21.refs_1_.refs_2_, bf16[512,512]{1,0:T(8,128)(2,1)} %gate.3.refs_2_.refs_1_, bf16[512,512]{1,0:T(8,128)(2,1)S(1)} %copy-done.128, ...), custom_call_target="tpu_custom_call" | custom-call | flops 4294967296 | bytes 14680064 | tf_op jit(solution)/shard_map/mlp_up/pallas_call | solution.py:690
  203.6 8.6 %collective-permute-done.24.refs_8_.refs_10_ = bf16[512,512]{1,0:T(8,128)(2,1)S(1)} collective-permute-done((bf16[512,512]{1,0:T(8,128)(2,1)}, bf16[512,512]{1,0:T(8,128)(2,1)S(1)}, u32[]{:S(2)}, u32[]{:S(2)}) %collective-permute-start.24) | collective-permute-done | bytes 524320 | tf_op jit(solution)/shard_map/ppermute | solution.py:798
  212.2 4.5 mlp_down.2
  216.8 2.6 collective-permute-done.25.refs_3_
  221.3 3.5 collective-permute-start.26
  224.9 22.2 %collective-permute-done.26.refs_1_ = bf16[512,1024]{1,0:T(8,128)(2,1)S(1)} collective-permute-done((bf16[512,1024]{1,0:T(8,128)(2,1)S(1)}, bf16[512,1024]{1,0:T(8,128)(2,1)S(1)}, u32[]{:S(2)}, u32[]{:S(2)}) %collective-permute-start.26) | collective-permute-done | bytes 1048608 | tf_op jit(solution)/shard_map/ppermute | solution.py:28
  249.0 2.6 collective-permute-done.27.refs_4_.refs_8_
  251.6 16.9 %attend.3 = (bf16[4,1024,128]{2,1,0:T(8,128)(2,1)S(1)}, bf16[4,1024,128]{2,1,0:T(8,128)(2,1)S(1)}, bf16[4,1024,128]{2,1,0:T(8,128)(2,1)S(1)}, f32[4,2,1024]{2,1,0:T(2,128)S(1)}, bf16[1024,512]{1,0:T(8,128)(2,1)S(1)}) custom-call(s32[1]{0:T(128)} %bitcast.refs_0_, f32[1024,128]{1,0:T(8,128)S(1)} %get-tuple-element.230.refs_1_, ...), custom_call_target="tpu_custom_call" | custom-call | flops 11811160064 | bytes 11567104 | tf_op jit(solution)/shard_map/attend/pallas_call | solution.py:708
  268.5 3.3 attn_out.3
  272.1 2.5 collective-permute-done.28.refs_3_
  274.6 3.4 after_attn.3
  278.2 2.5 collective-permute-done.29.refs_1_.refs_8_
  280.7 9.1 %mlp_up.3 = (bf16[1024,2048]{1,0:T(8,128)(2,1)S(1)}, bf16[1024,2048]{1,0:T(8,128)(2,1)S(1)}) custom-call(bf16[512,1024]{1,0:T(8,128)(2,1)S(1)} %get-tuple-element.110.refs_0_.refs_7_, bf16[512,1024]{1,0:T(8,128)(2,1)S(1)} %collective-permute-done.29.refs_1_.refs_8_, bf16[512,512]{1,0:T(8,128)(2,1)} %gate.3.refs_2_.refs_1_, bf16[512,512]{1,0:T(8,128)(2,1)S(1)} %copy-done.128, ...), custom_call_target="tpu_custom_call" | custom-call | flops 4294967296 | bytes 14680064 | tf_op jit(solution)/shard_map/mlp_up/pallas_call | solution.py:690
  291.9 4.5 mlp_down.3
  306.0 7.2 %mlp_up_back.2.refs_0_.refs_9_ = bf16[1024,2048]{1,0:T(8,128)(2,1)S(1)} custom-call(bf16[512,1024]{1,0:T(8,128)(2,1)S(1)} %get-tuple-element.116.refs_0_.refs_11_, bf16[512,1024]{1,0:T(8,128)(2,1)S(1)} %collective-permute-done.31.refs_1_.refs_12_, bf16[1024,2048]{1,0:T(8,128)(2,1)} %copy-done.38, bf16[512,512]{1,0:T(8,128)(2,1)} %copy-done.31, ...), custom_call_target="tpu_custom_call" | custom-call | tf_op jit(solution)/shard_map/mlp_up_back/pallas_call | solution.py:729
  313.2 5.9 mlp_back.2
  321.9 3.9 into_attn_back.2
  326.0 2.5 collective-permute-done.33.refs_4_.refs_12_
  328.5 12.9 %attend_back.4.refs_0_.refs_9_ = bf16[1024,768]{1,0:T(8,128)(2,1)S(1)} custom-call(s32[1]{0:T(128)} %bitcast.refs_0_, f32[1024,128]{1,0:T(8,128)S(1)} %get-tuple-element.230.refs_1_, f32[1024,128]{1,0:T(8,128)S(1)} %get-tuple-element.231.refs_2_, bf16[512,1024]{1,0:T(8,128)(2,1)S(1)} %get-tuple-element.121.refs_3_.refs_11_, ...), custom_call_target="tpu_custom_call" | custom-call | flops 11274289152 | bytes 6815744 | tf_op jit(solution)/shard_map/attend_back/pallas_call | solution.py:708
  341.5 13.0 %attend_back.5.refs_1_.refs_9_ = bf16[1024,768]{1,0:T(8,128)(2,1)S(1)} custom-call(s32[1]{0:T(128)} %bitcast.refs_0_, f32[1024,128]{1,0:T(8,128)S(1)} %get-tuple-element.230.refs_1_, f32[1024,128]{1,0:T(8,128)S(1)} %get-tuple-element.231.refs_2_, bf16[512,1024]{1,0:T(8,128)(2,1)S(1)} %get-tuple-element.121.refs_3_.refs_11_, ...), custom_call_target="tpu_custom_call" | custom-call | flops 11274289152 | bytes 6815744 | tf_op jit(solution)/shard_map/attend_back/pallas_call | solution.py:708
  356.1 5.7 attn_back.2
  365.3 3.2 out_of_layer.2
  371.3 4.2 all-to-all-start.1
  375.5 20.4 %collective-permute-done.35.refs_1_ = bf16[512,1024]{1,0:T(8,128)(2,1)S(1)} collective-permute-done((bf16[512,1024]{1,0:T(8,128)(2,1)}, bf16[512,1024]{1,0:T(8,128)(2,1)S(1)}, u32[]{:S(2)}, u32[]{:S(2)}) %collective-permute-start.35) | collective-permute-done | bytes 1048608 | tf_op jit(solution)/shard_map/ppermute | solution.py:28
  402.3 2.6 collective-permute-done.36.refs_1_.refs_6_
  404.9 7.2 %mlp_up_back.3.refs_3_.refs_0_ = bf16[1024,2048]{1,0:T(8,128)(2,1)S(1)} custom-call(bf16[512,1024]{1,0:T(8,128)(2,1)S(1)} %get-tuple-element.133.refs_0_.refs_5_, bf16[512,1024]{1,0:T(8,128)(2,1)S(1)} %collective-permute-done.36.refs_1_.refs_6_, bf16[1024,2048]{1,0:T(8,128)(2,1)} %copy-done.59, bf16[512,512]{1,0:T(8,128)(2,1)} %copy-done.31, ...), custom_call_target="tpu_custom_call" | custom-call | tf_op jit(solution)/shard_map/mlp_up_back/pallas_call | solution.py:729
  414.1 7.2 %mlp_grads.2 = (f32[1024,512]{1,0:T(8,128)S(1)}, bf16[1024,512]{1,0:T(8,128)(2,1)S(1)}, f32[1024,512]{1,0:T(8,128)S(1)}, bf16[1024,512]{1,0:T(8,128)(2,1)S(1)}) custom-call(s32[1]{0:T(128)} %bitcast.12.refs_0_, bf16[512,1024]{1,0:T(8,128)(2,1)} %copy-done.40, bf16[512,1024]{1,0:T(8,128)(2,1)} %copy-done.41, bf16[1024,2048]{1,0:T(8,128)(2,1)} %copy-done.3, ...), custom_call_target="tpu_custom_call" | custom-call | tf_op jit(solution)/shard_map/mlp_grads/pallas_call | solution.py:897
  422.8 5.6 mlp_back.3
  430.1 7.2 %mlp_grads.3 = (f32[1024,512]{1,0:T(8,128)S(1)}, bf16[1024,512]{1,0:T(8,128)(2,1)S(1)}, f32[1024,512]{1,0:T(8,128)S(1)}, bf16[1024,512]{1,0:T(8,128)(2,1)S(1)}) custom-call(s32[1]{0:T(128)} %bitcast.12.refs_0_, bf16[512,1024]{1,0:T(8,128)(2,1)} %copy-done.40, bf16[512,1024]{1,0:T(8,128)(2,1)} %copy-done.41, bf16[1024,2048]{1,0:T(8,128)(2,1)} %copy-done.3, ...), custom_call_target="tpu_custom_call" | custom-call | tf_op jit(solution)/shard_map/mlp_grads/pallas_call | solution.py:897
  438.7 4.0 into_attn_back.3
  445.7 8.9 %collective-permute-done.40.refs_1_.refs_13_ = bf16[1024,512]{1,0:T(8,128)(2,1)S(1)} collective-permute-done((bf16[1024,512]{1,0:T(8,128)(2,1)S(1)}, bf16[1024,512]{1,0:T(8,128)(2,1)S(1)}, u32[]{:S(2)}, u32[]{:S(2)}) %collective-permute-start.40) | collective-permute-done | bytes 1048608 | tf_op jit(solution)/shard_map/ppermute | solution.py:798
  457.7 12.5 %attend_back.6.refs_3_.refs_1_ = bf16[1024,768]{1,0:T(8,128)(2,1)S(1)} custom-call(s32[1]{0:T(128)} %bitcast.refs_0_, f32[1024,128]{1,0:T(8,128)S(1)} %copy-done.97, f32[1024,128]{1,0:T(8,128)S(1)} %copy-done.99, bf16[512,1024]{1,0:T(8,128)(2,1)S(1)} %copy-done.13, bf16[512,1024]{1,0:T(8,128)(2,1)S(1)} %collective-permute-done.38.refs_4_.refs_6_, ...), custom_call_target="tpu_custom_call" | custom-call | flops 11274289152 | bytes 6815744 | tf_op jit(solution)/shard_map/attend_back/pallas_call | solution.py:708
  471.4 5.6 collective-permute-done.39.refs_1_.refs_13_
  477.0 2.6 collective-permute-done.41.refs_2_.refs_14_
  483.0 5.9 attn_grads.2
  491.7 13.0 %attend_back.7.refs_3_.refs_0_ = bf16[1024,768]{1,0:T(8,128)(2,1)S(1)} custom-call(s32[1]{0:T(128)} %bitcast.refs_0_, f32[1024,128]{1,0:T(8,128)S(1)} %copy-done.97, f32[1024,128]{1,0:T(8,128)S(1)} %copy-done.99, bf16[512,1024]{1,0:T(8,128)(2,1)S(1)} %copy-done.14, bf16[512,1024]{1,0:T(8,128)(2,1)S(1)} %copy-done.54, bf16[512,512]{1,0:T(8,128)(2,1)S(1)} %copy-done.24, ...), custom_call_target="tpu_custom_call" | custom-call | flops 11274289152 | bytes 6815744 | tf_op jit(solution)/shard_map/attend_back/pallas_call | solution.py:708
  507.3 6.9 %attn_grads.3 = (f32[512,512]{1,0:T(8,128)S(1)}, bf16[512,512]{1,0:T(8,128)(2,1)}, f32[512,512]{1,0:T(8,128)S(1)}, bf16[512,512]{1,0:T(8,128)(2,1)}) custom-call(s32[1]{0:T(128)} %bitcast.12.refs_0_, bf16[512,1024]{1,0:T(8,128)(2,1)} %copy-done.10, bf16[512,1024]{1,0:T(8,128)(2,1)} %collective-permute-done.6.refs_4_.refs_2_, bf16[1024,768]{1,0:T(8,128)(2,1)} %copy-done.27, ...), custom_call_target="tpu_custom_call" | custom-call | tf_op jit(solution)/shard_map/attn_grads/pallas_call | solution.py:897
  516.2 5.3 attn_back.3
  525.2 12.5 %collective-permute-done.46.refs_1_ = bf16[512,512]{1,0:T(8,128)(2,1)S(1)} collective-permute-done((bf16[512,512]{1,0:T(8,128)(2,1)S(1)}, bf16[512,512]{1,0:T(8,128)(2,1)S(1)}, u32[]{:S(2)}, u32[]{:S(2)}) %collective-permute-start.46) | collective-permute-done | bytes 524320 | tf_op jit(solution)/shard_map/ppermute | solution.py:798
  538.7 8.4 %collective-permute-done.53.refs_7_.refs_3_ = bf16[1024,512]{1,0:T(8,128)(2,1)S(1)} collective-permute-done((bf16[1024,512]{1,0:T(8,128)(2,1)S(1)}, bf16[1024,512]{1,0:T(8,128)(2,1)S(1)}, u32[]{:S(2)}, u32[]{:S(2)}) %collective-permute-start.53) | collective-permute-done | bytes 1048608 | tf_op jit(solution)/shard_map/ppermute | solution.py:803
  551.9 5.1 all-to-all-start.2
  558.6 3.8 collective-permute-start.47
  562.9 9.0 %collective-permute-done.45.refs_1_ = bf16[512,512]{1,0:T(8,128)(2,1)S(1)} collective-permute-done((bf16[512,512]{1,0:T(8,128)(2,1)S(1)}, bf16[512,512]{1,0:T(8,128)(2,1)S(1)}, u32[]{:S(2)}, u32[]{:S(2)}) %collective-permute-start.45) | collective-permute-done | bytes 524320 | tf_op jit(solution)/shard_map/ppermute | solution.py:798
  571.9 15.4 %collective-permute-done.47.refs_2_ = bf16[512,512]{1,0:T(8,128)(2,1)S(1)} collective-permute-done((bf16[512,512]{1,0:T(8,128)(2,1)S(1)}, bf16[512,512]{1,0:T(8,128)(2,1)S(1)}, u32[]{:S(2)}, u32[]{:S(2)}) %collective-permute-start.47) | collective-permute-done | bytes 524320 | tf_op jit(solution)/shard_map/ppermute | solution.py:803
  592.6 14.5 %collective-permute-done.48.refs_2_ = bf16[512,512]{1,0:T(8,128)(2,1)S(1)} collective-permute-done((bf16[512,512]{1,0:T(8,128)(2,1)S(1)}, bf16[512,512]{1,0:T(8,128)(2,1)S(1)}, u32[]{:S(2)}, u32[]{:S(2)}) %collective-permute-start.48) | collective-permute-done | bytes 524320 | tf_op jit(solution)/shard_map/ppermute | solution.py:803
  621.2 4.8 all-to-all-start.3
  629.2 3.3 all-to-all-done.3
  636.4 2.8 mlp_join.1
  (437 shorter events, 164.8 us)
Async XLA Ops:
  7.2 3.8 collective-permute-start
  14.9 68.6 %all-to-all-start = ((bf16[4,128,1024]{2,1,0:T(8,128)(2,1)}), bf16[4,128,1024]{2,1,0:T(8,128)(2,1)S(1)}, u32[]{:S(2)}, u32[]{:S(2)}) async-start(bf16[4,128,1024]{2,1,0:T(8,128)(2,1)} %copy-done.55), calls=%async_computation | async-start | bytes 2097152 | tf_op jit(solution)/shard_map/all_to_all | solution.py:1064
  20.9 33.2 %collective-permute-start.1 = (bf16[512,512]{1,0:T(8,128)(2,1)}, bf16[512,512]{1,0:T(8,128)(2,1)}, u32[]{:S(2)}, u32[]{:S(2)}) collective-permute-start(bf16[512,512]{1,0:T(8,128)(2,1)} %pad_maximum_fusion.refs_3_.refs_5_.refs_1_.refs_2_), channel_id=1, source_target_pairs={{0,1},{1,2},{2,3},{3,0},{4,5},{5,6},{6,7},{7,4},{8,9},{9,10},{10,1... | collective-permute-start | bytes 1572872 | tf_op jit(solution)/shard_map/ppermute | solution.py:803
  22.9 48.0 %collective-permute-start.3 = (bf16[512,512]{1,0:T(8,128)(2,1)}, bf16[512,512]{1,0:T(8,128)(2,1)}, u32[]{:S(2)}, u32[]{:S(2)}) collective-permute-start(bf16[512,512]{1,0:T(8,128)(2,1)} %pad_maximum_fusion.refs_3_.refs_5_.refs_1_.refs_2_), channel_id=1, source_target_pairs={{0,8},{4,12},{8,0},{12,4},{1,9},{5,13},{9,1},{13,5},{2,10},{6,14},... | collective-permute-start | bytes 1572872 | tf_op jit(solution)/shard_map/ppermute | solution.py:798
  54.1 15.4 %collective-permute-start.2 = (bf16[512,512]{1,0:T(8,128)(2,1)}, bf16[512,512]{1,0:T(8,128)(2,1)}, u32[]{:S(2)}, u32[]{:S(2)}) collective-permute-start(bf16[512,512]{1,0:T(8,128)(2,1)} %collective-permute-done.1.refs_6_.refs_2_.refs_3_), channel_id=1, source_target_pairs={{0,1},{1,2},{2,3},{3,0},{4,5},{5,6},{6,7},{7,4},{8,9},{9,10},{10,1... | collective-permute-start | bytes 1572872 | tf_op jit(solution)/shard_map/ppermute | solution.py:803
  57.4 14.9 %collective-permute-start.4 = (bf16[512,512]{1,0:T(8,128)(2,1)S(1)}, bf16[512,512]{1,0:T(8,128)(2,1)S(1)}, u32[]{:S(2)}, u32[]{:S(2)}) collective-permute-start(bf16[512,512]{1,0:T(8,128)(2,1)S(1)} %dynamic-slice_bitcast_fusion.1.refs_0_), channel_id=1, source_target_pairs={{0,8},{4,12},{8,0},{12,4},{1,9},{5,13},{9,1},{13,5},{2,10},{6,14},... | collective-permute-start | bytes 1572872 | tf_op jit(solution)/shard_map/ppermute | solution.py:798
  60.1 23.5 %collective-permute-start.5 = (bf16[512,512]{1,0:T(8,128)(2,1)S(1)}, bf16[512,512]{1,0:T(8,128)(2,1)S(1)}, u32[]{:S(2)}, u32[]{:S(2)}) collective-permute-start(bf16[512,512]{1,0:T(8,128)(2,1)S(1)} %dynamic-slice_bitcast_fusion.refs_0_), channel_id=1, source_target_pairs={{0,8},{4,12},{8,0},{12,4},{1,9},{5,13},{9,1},{13,5},{2,10},{6,14},... | collective-permute-start | bytes 1572872 | tf_op jit(solution)/shard_map/ppermute | solution.py:798
  60.6 33.4 %collective-permute-start.8 = (bf16[512,512]{1,0:T(8,128)(2,1)}, bf16[512,512]{1,0:T(8,128)(2,1)}, u32[]{:S(2)}, u32[]{:S(2)}) collective-permute-start(bf16[512,512]{1,0:T(8,128)(2,1)} %collective-permute-done.1.refs_6_.refs_2_.refs_3_), channel_id=1, source_target_pairs={{0,8},{4,12},{8,0},{12,4},{1,9},{5,13},{9,1},{13,5},{2,10},{6,14},... | collective-permute-start | bytes 1572872 | tf_op jit(solution)/shard_map/ppermute | solution.py:798
  69.5 20.8 %collective-permute-start.7 = (bf16[512,512]{1,0:T(8,128)(2,1)}, bf16[512,512]{1,0:T(8,128)(2,1)}, u32[]{:S(2)}, u32[]{:S(2)}) collective-permute-start(bf16[512,512]{1,0:T(8,128)(2,1)} %collective-permute-done.2.refs_1_.refs_7_.refs_3_.refs_5_.refs_4_), channel_id=1, source_target_pairs={{0,1},{1,2},{2,3},{3,0},{4,5},{5,6},{6,7},{7,4},{8,9},{9,10},{10,1... | collective-permute-start | bytes 1572872 | tf_op jit(solution)/shard_map/ppermute | solution.py:803
  86.1 30.3 %collective-permute-start.6 = (bf16[512,1024]{1,0:T(8,128)(2,1)S(1)}, bf16[512,1024]{1,0:T(8,128)(2,1)}, u32[]{:S(2)}, u32[]{:S(2)}) collective-permute-start(bf16[512,1024]{1,0:T(8,128)(2,1)S(1)} %norm_in.2.refs_3_.refs_1_), channel_id=1, source_target_pairs={{0,4},{4,0},{8,12},{12,8},{1,5},{5,1},{9,13},{13,9},{2,6},{6,2},{1... | collective-permute-start | bytes 3145736 | tf_op jit(solution)/shard_map/ppermute | solution.py:798
  86.2 16.8 %collective-permute-start.11 = (bf16[512,512]{1,0:T(8,128)(2,1)}, bf16[512,512]{1,0:T(8,128)(2,1)S(1)}, u32[]{:S(2)}, u32[]{:S(2)}) collective-permute-start(bf16[512,512]{1,0:T(8,128)(2,1)} %gate.3.refs_2_.refs_1_), channel_id=1, source_target_pairs={{0,1},{1,2},{2,3},{3,0},{4,5},{5,6},{6,7},{7,4},{8,9},{9,10},{10,1... | collective-permute-start | bytes 1572872 | tf_op jit(solution)/shard_map/ppermute | solution.py:803
  88.8 16.4 %collective-permute-start.9 = (bf16[512,512]{1,0:T(8,128)(2,1)}, bf16[512,512]{1,0:T(8,128)(2,1)S(1)}, u32[]{:S(2)}, u32[]{:S(2)}) collective-permute-start(bf16[512,512]{1,0:T(8,128)(2,1)} %collective-permute-done.2.refs_1_.refs_7_.refs_3_.refs_5_.refs_4_), channel_id=1, source_target_pairs={{0,8},{4,12},{8,0},{12,4},{1,9},{5,13},{9,1},{13,5},{2,10},{6,14},... | collective-permute-start | bytes 1572872 | tf_op jit(solution)/shard_map/ppermute | solution.py:798
  91.4 22.9 %collective-permute-start.12 = (bf16[512,512]{1,0:T(8,128)(2,1)S(1)}, bf16[512,512]{1,0:T(8,128)(2,1)S(1)}, u32[]{:S(2)}, u32[]{:S(2)}) collective-permute-start(bf16[512,512]{1,0:T(8,128)(2,1)S(1)} %gate.4.refs_1_.refs_3_), channel_id=1, source_target_pairs={{0,1},{1,2},{2,3},{3,0},{4,5},{5,6},{6,7},{7,4},{8,9},{9,10},{10,1... | collective-permute-start | bytes 1572872 | tf_op jit(solution)/shard_map/ppermute | solution.py:803
  94.0 22.4 %collective-permute-start.10 = (bf16[512,512]{1,0:T(8,128)(2,1)}, bf16[512,512]{1,0:T(8,128)(2,1)S(1)}, u32[]{:S(2)}, u32[]{:S(2)}) collective-permute-start(bf16[512,512]{1,0:T(8,128)(2,1)} %collective-permute-done.7.refs_1_.refs_8_.refs_4_.refs_6_.refs_5_), channel_id=1, source_target_pairs={{0,8},{4,12},{8,0},{12,4},{1,9},{5,13},{9,1},{13,5},{2,10},{6,14},... | collective-permute-start | bytes 1572872 | tf_op jit(solution)/shard_map/ppermute | solution.py:798
  103.0 33.3 %collective-permute-start.13 = (bf16[512,512]{1,0:T(8,128)(2,1)S(1)}, bf16[512,512]{1,0:T(8,128)(2,1)S(1)}, u32[]{:S(2)}, u32[]{:S(2)}) collective-permute-start(bf16[512,512]{1,0:T(8,128)(2,1)S(1)} %collective-permute-done.11.refs_13_.refs_3_.refs_2_), channel_id=1, source_target_pairs={{0,1},{1,2},{2,3},{3,0},{4,5},{5,6},{6,7},{7,4},{8,9},{9,10},{10,1... | collective-permute-start | bytes 1572872 | tf_op jit(solution)/shard_map/ppermute | solution.py:803
  105.2 31.2 %collective-permute-start.15 = (bf16[512,512]{1,0:T(8,128)(2,1)S(1)}, bf16[512,512]{1,0:T(8,128)(2,1)S(1)}, u32[]{:S(2)}, u32[]{:S(2)}) collective-permute-start(bf16[512,512]{1,0:T(8,128)(2,1)S(1)} %collective-permute-done.11.refs_13_.refs_3_.refs_2_), channel_id=1, source_target_pairs={{0,8},{4,12},{8,0},{12,4},{1,9},{5,13},{9,1},{13,5},{2,10},{6,14},... | collective-permute-start | bytes 1572872 | tf_op jit(solution)/shard_map/ppermute | solution.py:798
  114.3 22.1 %collective-permute-start.14 = (bf16[512,512]{1,0:T(8,128)(2,1)S(1)}, bf16[512,512]{1,0:T(8,128)(2,1)S(1)}, u32[]{:S(2)}, u32[]{:S(2)}) collective-permute-start(bf16[512,512]{1,0:T(8,128)(2,1)S(1)} %collective-permute-done.12.refs_14_.refs_2_.refs_4_), channel_id=1, source_target_pairs={{0,1},{1,2},{2,3},{3,0},{4,5},{5,6},{6,7},{7,4},{8,9},{9,10},{10,1... | collective-permute-start | bytes 1572872 | tf_op jit(solution)/shard_map/ppermute | solution.py:803
  116.4 238.1 %copy-start.80 = (bf16[512,512]{1,0:T(8,128)(2,1)}, bf16[512,512]{1,0:T(8,128)(2,1)S(1)}, u32[]{:S(2)}) copy-start(bf16[512,512]{1,0:T(8,128)(2,1)S(1)} %collective-permute-done.10.refs_12_.refs_8_.refs_9_) | copy-start | bytes 1572868
  140.6 28.7 %collective-permute-start.16 = (bf16[512,1024]{1,0:T(8,128)(2,1)S(1)}, bf16[512,1024]{1,0:T(8,128)(2,1)S(1)}, u32[]{:S(2)}, u32[]{:S(2)}) collective-permute-start(bf16[512,1024]{1,0:T(8,128)(2,1)S(1)} %get-tuple-element.99), channel_id=1, source_target_pairs={{0,4},{4,0},{8,12},{12,8},{1,5},{5,1},{9,13},{13,9},{2,6},{6,2},{1... | collective-permute-start | bytes 3145736 | tf_op jit(solution)/shard_map/ppermute | solution.py:798
  140.7 16.8 %collective-permute-start.17 = (bf16[512,512]{1,0:T(8,128)(2,1)}, bf16[512,512]{1,0:T(8,128)(2,1)S(1)}, u32[]{:S(2)}, u32[]{:S(2)}) collective-permute-start(bf16[512,512]{1,0:T(8,128)(2,1)} %copy-done.121), channel_id=1, source_target_pairs={{0,1},{1,2},{2,3},{3,0},{4,5},{5,6},{6,7},{7,4},{8,9},{9,10},{10,1... | collective-permute-start | bytes 1572872 | tf_op jit(solution)/shard_map/ppermute | solution.py:803
  144.1 14.8 %collective-permute-start.19 = (bf16[512,512]{1,0:T(8,128)(2,1)S(1)}, bf16[512,512]{1,0:T(8,128)(2,1)S(1)}, u32[]{:S(2)}, u32[]{:S(2)}) collective-permute-start(bf16[512,512]{1,0:T(8,128)(2,1)S(1)} %copy-done.63), channel_id=1, source_target_pairs={{0,8},{4,12},{8,0},{12,4},{1,9},{5,13},{9,1},{13,5},{2,10},{6,14},... | collective-permute-start | bytes 1572872 | tf_op jit(solution)/shard_map/ppermute | solution.py:798
  145.6 23.7 %collective-permute-start.20 = (bf16[512,512]{1,0:T(8,128)(2,1)}, bf16[512,512]{1,0:T(8,128)(2,1)S(1)}, u32[]{:S(2)}, u32[]{:S(2)}) collective-permute-start(bf16[512,512]{1,0:T(8,128)(2,1)} %copy-done.121), channel_id=1, source_target_pairs={{0,8},{4,12},{8,0},{12,4},{1,9},{5,13},{9,1},{13,5},{2,10},{6,14},... | collective-permute-start | bytes 1572872 | tf_op jit(solution)/shard_map/ppermute | solution.py:798
  146.1 23.2 %collective-permute-start.18 = (bf16[512,512]{1,0:T(8,128)(2,1)}, bf16[512,512]{1,0:T(8,128)(2,1)S(1)}, u32[]{:S(2)}, u32[]{:S(2)}) collective-permute-start(bf16[512,512]{1,0:T(8,128)(2,1)} %copy-done.36), channel_id=1, source_target_pairs={{0,1},{1,2},{2,3},{3,0},{4,5},{5,6},{6,7},{7,4},{8,9},{9,10},{10,1... | collective-permute-start | bytes 1572872 | tf_op jit(solution)/shard_map/ppermute | solution.py:803
  175.1 15.1 %collective-permute-start.21 = (bf16[512,1024]{1,0:T(8,128)(2,1)S(1)}, bf16[512,1024]{1,0:T(8,128)(2,1)S(1)}, u32[]{:S(2)}, u32[]{:S(2)}) collective-permute-start(bf16[512,1024]{1,0:T(8,128)(2,1)S(1)} %get-tuple-element.101.refs_0_.refs_1_), channel_id=1, source_target_pairs={{0,4},{4,0},{8,12},{12,8},{1,5},{5,1},{9,13},{13,9},{2,6},{6,2},{1... | collective-permute-start | bytes 3145736 | tf_op jit(solution)/shard_map/ppermute | solution.py:798
  175.2 15.0 %collective-permute-start.22 = (bf16[512,512]{1,0:T(8,128)(2,1)}, bf16[512,512]{1,0:T(8,128)(2,1)S(1)}, u32[]{:S(2)}, u32[]{:S(2)}) collective-permute-start(bf16[512,512]{1,0:T(8,128)(2,1)} %copy-done.103), channel_id=1, source_target_pairs={{0,8},{4,12},{8,0},{12,4},{1,9},{5,13},{9,1},{13,5},{2,10},{6,14},... | collective-permute-start | bytes 1572872 | tf_op jit(solution)/shard_map/ppermute | solution.py:798
  176.7 26.8 %collective-permute-start.23 = (bf16[512,512]{1,0:T(8,128)(2,1)S(1)}, bf16[512,512]{1,0:T(8,128)(2,1)S(1)}, u32[]{:S(2)}, u32[]{:S(2)}) collective-permute-start(bf16[512,512]{1,0:T(8,128)(2,1)S(1)} %copy-done.37), channel_id=1, source_target_pairs={{0,8},{4,12},{8,0},{12,4},{1,9},{5,13},{9,1},{13,5},{2,10},{6,14},... | collective-permute-start | bytes 1572872 | tf_op jit(solution)/shard_map/ppermute | solution.py:798
  177.3 34.9 %collective-permute-start.24 = (bf16[512,512]{1,0:T(8,128)(2,1)}, bf16[512,512]{1,0:T(8,128)(2,1)S(1)}, u32[]{:S(2)}, u32[]{:S(2)}) collective-permute-start(bf16[512,512]{1,0:T(8,128)(2,1)} %copy-done.34), channel_id=1, source_target_pairs={{0,8},{4,12},{8,0},{12,4},{1,9},{5,13},{9,1},{13,5},{2,10},{6,14},... | collective-permute-start | bytes 1572872 | tf_op jit(solution)/shard_map/ppermute | solution.py:798
  216.7 2.7 collective-permute-start.25
  221.3 25.8 %collective-permute-start.26 = (bf16[512,1024]{1,0:T(8,128)(2,1)S(1)}, bf16[512,1024]{1,0:T(8,128)(2,1)S(1)}, u32[]{:S(2)}, u32[]{:S(2)}) collective-permute-start(bf16[512,1024]{1,0:T(8,128)(2,1)S(1)} %get-tuple-element.130), channel_id=1, source_target_pairs={{0,16},{1,17},{2,18},{3,19},{4,20},{5,21},{6,22},{7,23},{8,24},{9,... | collective-permute-start | bytes 3145736 | tf_op jit(solution)/shard_map/ppermute | solution.py:28
  248.9 2.7 collective-permute-start.27
  271.9 2.7 collective-permute-start.28
  278.0 2.7 collective-permute-start.29
  296.3 2.7 collective-permute-start.30
  303.2 2.7 collective-permute-start.31
  319.2 2.7 collective-permute-start.32
  325.8 2.7 collective-permute-start.33
  362.6 2.7 collective-permute-start.34
  368.5 27.4 %collective-permute-start.35 = (bf16[512,1024]{1,0:T(8,128)(2,1)}, bf16[512,1024]{1,0:T(8,128)(2,1)S(1)}, u32[]{:S(2)}, u32[]{:S(2)}) collective-permute-start(bf16[512,1024]{1,0:T(8,128)(2,1)} %get-tuple-element.129), channel_id=1, source_target_pairs={{16,0},{17,1},{18,2},{19,3},{20,4},{21,5},{22,6},{23,7},{24,8},{25... | collective-permute-start | bytes 3145736 | tf_op jit(solution)/shard_map/ppermute | solution.py:28
  371.3 31.0 %all-to-all-start.1 = ((bf16[4,128,1024]{2,1,0:T(8,128)(2,1)}), bf16[4,128,1024]{2,1,0:T(8,128)(2,1)}, u32[]{:S(2)}, u32[]{:S(2)}) async-start(bf16[4,128,1024]{2,1,0:T(8,128)(2,1)} %bitcast.46), calls=%async_computation.1 | async-start | bytes 2097152 | tf_op jit(solution)/shard_map/all_to_all | solution.py:1221
  402.2 2.7 collective-permute-start.36
  428.3 10.3 %collective-permute-start.37 = (bf16[512,1024]{1,0:T(8,128)(2,1)S(1)}, bf16[512,1024]{1,0:T(8,128)(2,1)S(1)}, u32[]{:S(2)}, u32[]{:S(2)}) collective-permute-start(bf16[512,1024]{1,0:T(8,128)(2,1)S(1)} %get-tuple-element.137), channel_id=1, source_target_pairs={{0,4},{4,0},{8,12},{12,8},{1,5},{5,1},{9,13},{13,9},{2,6},{6,2},{1... | collective-permute-start | bytes 3145736 | tf_op jit(solution)/shard_map/ppermute | solution.py:798
  428.6 26.0 %collective-permute-start.40 = (bf16[1024,512]{1,0:T(8,128)(2,1)S(1)}, bf16[1024,512]{1,0:T(8,128)(2,1)S(1)}, u32[]{:S(2)}, u32[]{:S(2)}) collective-permute-start(bf16[1024,512]{1,0:T(8,128)(2,1)S(1)} %get-tuple-element.146), channel_id=1, source_target_pairs={{0,8},{4,12},{8,0},{12,4},{1,9},{5,13},{9,1},{13,5},{2,10},{6,14},... | collective-permute-start | bytes 3145736 | tf_op jit(solution)/shard_map/ppermute | solution.py:798
  442.7 13.4 %collective-permute-start.38 = (bf16[512,1024]{1,0:T(8,128)(2,1)S(1)}, bf16[512,1024]{1,0:T(8,128)(2,1)S(1)}, u32[]{:S(2)}, u32[]{:S(2)}) collective-permute-start(bf16[512,1024]{1,0:T(8,128)(2,1)S(1)} %get-tuple-element.140.refs_2_.refs_3_.refs_5_), channel_id=1, source_target_pairs={{0,4},{4,0},{8,12},{12,8},{1,5},{5,1},{9,13},{13,9},{2,6},{6,2},{1... | collective-permute-start | bytes 3145736 | tf_op jit(solution)/shard_map/ppermute | solution.py:798
  443.1 33.9 %collective-permute-start.39 = (bf16[1024,512]{1,0:T(8,128)(2,1)S(1)}, bf16[1024,512]{1,0:T(8,128)(2,1)S(1)}, u32[]{:S(2)}, u32[]{:S(2)}) collective-permute-start(bf16[1024,512]{1,0:T(8,128)(2,1)S(1)} %get-tuple-element.145), channel_id=1, source_target_pairs={{0,8},{4,12},{8,0},{12,4},{1,9},{5,13},{9,1},{13,5},{2,10},{6,14},... | collective-permute-start | bytes 3145736 | tf_op jit(solution)/shard_map/ppermute | solution.py:798
  443.5 62.3 %collective-permute-start.42 = (bf16[1024,512]{1,0:T(8,128)(2,1)S(1)}, bf16[1024,512]{1,0:T(8,128)(2,1)S(1)}, u32[]{:S(2)}, u32[]{:S(2)}) collective-permute-start(bf16[1024,512]{1,0:T(8,128)(2,1)S(1)} %get-tuple-element.149), channel_id=1, source_target_pairs={{0,8},{4,12},{8,0},{12,4},{1,9},{5,13},{9,1},{13,5},{2,10},{6,14},... | collective-permute-start | bytes 3145736 | tf_op jit(solution)/shard_map/ppermute | solution.py:798
  445.2 93.5 %collective-permute-start.52 = (bf16[1024,512]{1,0:T(8,128)(2,1)S(1)}, bf16[1024,512]{1,0:T(8,128)(2,1)S(1)}, u32[]{:S(2)}, u32[]{:S(2)}) collective-permute-start(bf16[1024,512]{1,0:T(8,128)(2,1)S(1)} %get-tuple-element.161), channel_id=1, source_target_pairs={{0,8},{4,12},{8,0},{12,4},{1,9},{5,13},{9,1},{13,5},{2,10},{6,14},... | collective-permute-start | bytes 3145736 | tf_op jit(solution)/shard_map/ppermute | solution.py:798
  455.6 24.1 %collective-permute-start.41 = (bf16[1024,512]{1,0:T(8,128)(2,1)S(1)}, bf16[1024,512]{1,0:T(8,128)(2,1)S(1)}, u32[]{:S(2)}, u32[]{:S(2)}) collective-permute-start(bf16[1024,512]{1,0:T(8,128)(2,1)S(1)} %moved.6), channel_id=1, source_target_pairs={{0,3},{1,0},{2,1},{3,2},{4,7},{5,4},{6,5},{7,6},{8,11},{9,8},{10,9... | collective-permute-start | bytes 3145736 | tf_op jit(solution)/shard_map/ppermute | solution.py:803
  480.7 25.2 %collective-permute-start.43 = (bf16[1024,512]{1,0:T(8,128)(2,1)S(1)}, bf16[1024,512]{1,0:T(8,128)(2,1)S(1)}, u32[]{:S(2)}, u32[]{:S(2)}) collective-permute-start(bf16[1024,512]{1,0:T(8,128)(2,1)S(1)} %moved.7.refs_13_), channel_id=1, source_target_pairs={{0,3},{1,0},{2,1},{3,2},{4,7},{5,4},{6,5},{7,6},{8,11},{9,8},{10,9... | collective-permute-start | bytes 3145736 | tf_op jit(solution)/shard_map/ppermute | solution.py:803
  521.5 17.2 %collective-permute-start.51 = (bf16[512,1024]{1,0:T(8,128)(2,1)S(1)}, bf16[512,1024]{1,0:T(8,128)(2,1)S(1)}, u32[]{:S(2)}, u32[]{:S(2)}) collective-permute-start(bf16[512,1024]{1,0:T(8,128)(2,1)S(1)} %get-tuple-element.159), channel_id=1, source_target_pairs={{0,4},{4,0},{8,12},{12,8},{1,5},{5,1},{9,13},{13,9},{2,6},{6,2},{1... | collective-permute-start | bytes 3145736 | tf_op jit(solution)/shard_map/ppermute | solution.py:798
  521.6 25.6 %collective-permute-start.53 = (bf16[1024,512]{1,0:T(8,128)(2,1)S(1)}, bf16[1024,512]{1,0:T(8,128)(2,1)S(1)}, u32[]{:S(2)}, u32[]{:S(2)}) collective-permute-start(bf16[1024,512]{1,0:T(8,128)(2,1)S(1)} %copy-done.57), channel_id=1, source_target_pairs={{0,3},{1,0},{2,1},{3,2},{4,7},{5,4},{6,5},{7,6},{8,11},{9,8},{10,9... | collective-permute-start | bytes 3145736 | tf_op jit(solution)/shard_map/ppermute | solution.py:803
  523.7 14.0 %collective-permute-start.46 = (bf16[512,512]{1,0:T(8,128)(2,1)S(1)}, bf16[512,512]{1,0:T(8,128)(2,1)S(1)}, u32[]{:S(2)}, u32[]{:S(2)}) collective-permute-start(bf16[512,512]{1,0:T(8,128)(2,1)S(1)} %get-tuple-element.154), channel_id=1, source_target_pairs={{0,8},{4,12},{8,0},{12,4},{1,9},{5,13},{9,1},{13,5},{2,10},{6,14},... | collective-permute-start | bytes 1572872 | tf_op jit(solution)/shard_map/ppermute | solution.py:798
  551.9 65.0 %all-to-all-start.2 = ((bf16[4,128,1024]{2,1,0:T(8,128)(2,1)}), bf16[4,128,1024]{2,1,0:T(8,128)(2,1)}, u32[]{:S(2)}, u32[]{:S(2)}) async-start(bf16[4,128,1024]{2,1,0:T(8,128)(2,1)} %bitcast.14), calls=%async_computation.2 | async-start | bytes 2097152 | tf_op jit(solution)/shard_map/all_to_all | solution.py:1303
  557.0 14.9 %collective-permute-start.45 = (bf16[512,512]{1,0:T(8,128)(2,1)S(1)}, bf16[512,512]{1,0:T(8,128)(2,1)S(1)}, u32[]{:S(2)}, u32[]{:S(2)}) collective-permute-start(bf16[512,512]{1,0:T(8,128)(2,1)S(1)} %copy-done.133), channel_id=1, source_target_pairs={{0,8},{4,12},{8,0},{12,4},{1,9},{5,13},{9,1},{13,5},{2,10},{6,14},... | collective-permute-start | bytes 1572872 | tf_op jit(solution)/shard_map/ppermute | solution.py:798
  558.6 28.7 %collective-permute-start.47 = (bf16[512,512]{1,0:T(8,128)(2,1)S(1)}, bf16[512,512]{1,0:T(8,128)(2,1)S(1)}, u32[]{:S(2)}, u32[]{:S(2)}) collective-permute-start(bf16[512,512]{1,0:T(8,128)(2,1)S(1)} %copy-done.77), channel_id=1, source_target_pairs={{0,3},{1,0},{2,1},{3,2},{4,7},{5,4},{6,5},{7,6},{8,11},{9,8},{10,9... | collective-permute-start | bytes 1572872 | tf_op jit(solution)/shard_map/ppermute | solution.py:803
  562.4 30.2 %collective-permute-start.44 = (bf16[512,512]{1,0:T(8,128)(2,1)}, bf16[512,512]{1,0:T(8,128)(2,1)S(1)}, u32[]{:S(2)}, u32[]{:S(2)}) collective-permute-start(bf16[512,512]{1,0:T(8,128)(2,1)} %get-tuple-element.151), channel_id=1, source_target_pairs={{0,8},{4,12},{8,0},{12,4},{1,9},{5,13},{9,1},{13,5},{2,10},{6,14},... | collective-permute-start | bytes 1572872 | tf_op jit(solution)/shard_map/ppermute | solution.py:798
  588.8 18.3 %collective-permute-start.48 = (bf16[512,512]{1,0:T(8,128)(2,1)S(1)}, bf16[512,512]{1,0:T(8,128)(2,1)S(1)}, u32[]{:S(2)}, u32[]{:S(2)}) collective-permute-start(bf16[512,512]{1,0:T(8,128)(2,1)S(1)} %moved.10), channel_id=1, source_target_pairs={{0,3},{1,0},{2,1},{3,2},{4,7},{5,4},{6,5},{7,6},{8,11},{9,8},{10,9... | collective-permute-start | bytes 1572872 | tf_op jit(solution)/shard_map/ppermute | solution.py:803
  591.0 16.1 %collective-permute-start.49 = (bf16[512,512]{1,0:T(8,128)(2,1)}, bf16[512,512]{1,0:T(8,128)(2,1)S(1)}, u32[]{:S(2)}, u32[]{:S(2)}) collective-permute-start(bf16[512,512]{1,0:T(8,128)(2,1)} %get-tuple-element.155), channel_id=1, source_target_pairs={{0,8},{4,12},{8,0},{12,4},{1,9},{5,13},{9,1},{13,5},{2,10},{6,14},... | collective-permute-start | bytes 1572872 | tf_op jit(solution)/shard_map/ppermute | solution.py:798
  608.1 34.2 %collective-permute-start.55 = (bf16[512,512]{1,0:T(8,128)(2,1)S(1)}, bf16[512,512]{1,0:T(8,128)(2,1)}, u32[]{:S(2)}, u32[]{:S(2)}) collective-permute-start(bf16[512,512]{1,0:T(8,128)(2,1)S(1)} %moved.11.refs_2_.refs_1_.refs_4_), channel_id=1, source_target_pairs={{0,3},{1,0},{2,1},{3,2},{4,7},{5,4},{6,5},{7,6},{8,11},{9,8},{10,9... | collective-permute-start | bytes 1572872 | tf_op jit(solution)/shard_map/ppermute | solution.py:803
  613.2 12.8 %collective-permute-start.50 = (bf16[2,128,1024]{2,1,0:T(8,128)(2,1)}, bf16[2,128,1024]{2,1,0:T(8,128)(2,1)}, u32[]{:S(2)}, u32[]{:S(2)}) collective-permute-start(bf16[2,128,1024]{2,1,0:T(8,128)(2,1)} %get-tuple-element.157), channel_id=1, source_target_pairs={{0,4},{4,0},{8,12},{12,8},{1,5},{5,1},{9,13},{13,9},{2,6},{6,2},{1... | collective-permute-start | bytes 1572872 | tf_op jit(solution)/shard_map/ppermute | solution.py:798
  616.4 17.9 %collective-permute-start.56 = (f32[256,512]{1,0:T(8,128)}, f32[256,512]{1,0:T(8,128)}, u32[]{:S(2)}, u32[]{:S(2)}) collective-permute-start(f32[256,512]{1,0:T(8,128)} %get-tuple-element.179), channel_id=1, source_target_pairs={{0,4},{4,0},{8,12},{12,8},{1,5},{5,1},{9,13},{13,9},{2,6},{6,2},{1... | collective-permute-start | bytes 1572872 | tf_op jit(solution)/shard_map/ppermute | solution.py:798
  616.9 17.4 %collective-permute-start.57 = (f32[512,256]{1,0:T(8,128)}, f32[512,256]{1,0:T(8,128)}, u32[]{:S(2)}, u32[]{:S(2)}) collective-permute-start(f32[512,256]{1,0:T(8,128)} %get-tuple-element.180), channel_id=1, source_target_pairs={{0,4},{4,0},{8,12},{12,8},{1,5},{5,1},{9,13},{13,9},{2,6},{6,2},{1... | collective-permute-start | bytes 1572872 | tf_op jit(solution)/shard_map/ppermute | solution.py:798
  619.8 19.4 %collective-permute-start.54 = (bf16[2,128,1024]{2,1,0:T(8,128)(2,1)}, bf16[2,128,1024]{2,1,0:T(8,128)(2,1)}, u32[]{:S(2)}, u32[]{:S(2)}) collective-permute-start(bf16[2,128,1024]{2,1,0:T(8,128)(2,1)} %get-tuple-element.164), channel_id=1, source_target_pairs={{0,4},{4,0},{8,12},{12,8},{1,5},{5,1},{9,13},{13,9},{2,6},{6,2},{1... | collective-permute-start | bytes 1572872 | tf_op jit(solution)/shard_map/ppermute | solution.py:798
  621.2 11.3 %all-to-all-start.3 = ((f32[16,1,256]{2,1,0:T(1,128)}), f32[16,1,256]{2,1,0:T(1,128)S(1)}, u32[]{:S(2)}, u32[]{:S(2)}) async-start(f32[16,1,256]{2,1,0:T(1,128)} %reshape.79), calls=%async_computation.3 | async-start | bytes 32768 | tf_op jit(solution)/shard_map/all_to_all | solution.py:1299
  643.6 2.0 collective-permute-start.58
  (140 other events, 1740.0 us)

commit v11 on v10

--- a/solution.py
+++ b/solution.py
@@ -971,10 +971,23 @@
     send_ref[...] = rows_ref[pl.ds((1 - core_ref[0]) * count, count)]
 
 
-def both_kernel(core_ref, keep_ref, sent_ref, out_ref):
+def turned_kernel(place_ref, keep_ref, sent_ref, *outs):
     count = keep_ref.shape[0]
-    out_ref[pl.ds(core_ref[0] * count, count)] = keep_ref[...]
-    out_ref[pl.ds((1 - core_ref[0]) * count, count)] = sent_ref[...]
+    for step, out in enumerate(outs):
+        goal = lax.rem(place_ref[1] + step, len(outs))
+        for k in range(len(outs)):
+            for here in range(2):
+
+                @pl.when(jnp.logical_and(goal == k, (place_ref[0] == k // count) == (here == 0)))
+                def _():
+                    out[...] = (keep_ref, sent_ref)[here][k % count]
+
+
+def placed_kernel(place_ref, *refs):
+    blocks, out_ref = refs[:-1], refs[-1]
+    for step, block in enumerate(blocks):
+        source = lax.rem(place_ref[1] + len(blocks) - step, len(blocks))
+        out_ref[pl.ds(source, 1)] = block[...][None]
 
 
 def in_order_kernel(core_ref, keep_ref, sent_ref, out_ref):
@@ -1053,15 +1066,27 @@
     def both_rows(own):
         return own, flip_pairs(own, 1)
 
-    def to_chip(block):
-        split = block.reshape((micro, 2, part) + block.shape[2:])
+    def turned(block, waits=()):
+        split = block.reshape(micro, 2, part, width)
         mine = lax.dynamic_index_in_dim(split, core, 1, keepdims=False)
         other = lax.dynamic_index_in_dim(split, 1 - core, 1, keepdims=False)
-        outs = (((2 * micro, part, width), jnp.bfloat16),)
-        (rows,) = with_core(
-            both_kernel, "both", core_word, outs, mine, flip_pairs(other, 1), waits=(attn_piece,)
+        outs = (((part, width), jnp.bfloat16),) * tensor
+        return with_core(
+            turned_kernel, "turned", place_word, outs, mine, flip_pairs(other, 1), waits=waits
         )
-        return lax.all_to_all(rows, "tensor", 0, 0, tiled=True)
+
+    def along(block, step, section=None):
+        pairs = [(i, (i + step) % tensor) for i in range(tensor)]
+        if section is None:
+            return lax.ppermute(block, "tensor", pairs)
+        pairs = [(section * tensor + i, section * tensor + k) for i, k in pairs]
+        return lax.ppermute(block, ("section", "tensor"), pairs)
+
+    def on_chips(blocks, section=None):
+        moved = [along(block, step, section) if step else block for step, block in enumerate(blocks)]
+        outs = (((tensor, part, width), jnp.bfloat16),)
+        (rows,) = with_core(placed_kernel, "placed", place_word, outs, *moved)
+        return rows.reshape(half, width)
 
     def from_chip(spread_out, waits=()):
         piece = ((micro, part, width), jnp.bfloat16)
@@ -1089,6 +1114,7 @@
         return lax.dynamic_slice(local, (size * core, wide_half * upper), (size, wide_half))
 
     core_word = core.astype(jnp.int32).reshape(1)
+    place_word = jnp.stack([core, lax.axis_index("tensor")]).astype(jnp.int32)
     attn_piece = jnp.concatenate([columns(qkv_weight[0]), rows(out_weight[0]).T], axis=1)
 
     def spread(piece):
@@ -1101,20 +1127,11 @@
     attn_other = [flip_pairs(piece, 2) for piece in attn_own]
     up_piece, down_piece = columns(up_weight[0]), rows(down_weight[0])
     up_other, down_other = [flip_pairs(up_piece, 2)], [flip_pairs(down_piece, 2)]
-    (up_piece,) = on_chip(
-        gate_kernel,
-        "gate",
-        ((up_piece.shape, up_piece.dtype),),
-        up_piece,
-        waits=(attn_own[2], attn_other[0]),
-    )
-    (down_piece,) = on_chip(
-        gate_kernel,
-        "gate",
-        ((down_piece.shape, down_piece.dtype),),
-        down_piece,
-        waits=(attn_own[3],),
-    )
+    gates = []
+    for piece in (up_piece, down_piece):
+        outs = ((piece.shape, piece.dtype),)
+        gates += on_chip(gate_kernel, "gate", outs, piece, waits=(attn_own[2], attn_other[0]))
+    up_piece, down_piece = gates
     up_own, down_own = spread(up_piece), spread(down_piece)
     up_other += [flip_pairs(piece, 2) for piece in up_own[1:]]
     down_other += [flip_pairs(piece, 2) for piece in down_own[1:]]
@@ -1122,11 +1139,11 @@
     unit = up_piece.shape[1]
     units = tensor * unit
 
+    start = shifted(on_chips(turned(own_first(inputs), (attn_piece,)), 1), "section", -1)
     group_count = group_weights.shape[0]
     matches = group_ids[..., None] == jnp.arange(group_count, dtype=jnp.int32)
     row_scale = jnp.sum(jnp.where(matches, group_weights, 0.0), axis=-1)
     weighted = (out_cotangent.astype(jnp.float32) * row_scale[..., None]).astype(jnp.bfloat16)
-    start = to_chip(own_first(jnp.where(first, inputs, weighted))).reshape(half, width)
     gain = own_first(gains[0])
 
     turns = jnp.arange(half, dtype=jnp.int32)
@@ -1208,12 +1225,15 @@
         (
             (up_piece, up_other[0], down_other[0]),
             (up_own[1], down_own[1]),
-            (up_own[2], down_own[2], up_other[1]),
-            (up_own[3], down_own[3], down_other[1], up_other[2]),
+            (up_own[2], down_own[2], up_other[1], down_other[1]),
+            (up_own[3], down_own[3], up_other[2], down_other[2]),
         ),
     )
-    low_one, saved_one, lefts_one = forward(shifted(low_zero, "section", 1), ((),) * 4)
-    grad_one, rights_one, gain_one = backward(start, saved_one, lambda *new: ())
+    goals = on_chips(turned(own_first(weighted), (low_zero,)))
+    low_one, saved_one, lefts_one = forward(
+        shifted(low_zero, "section", 1), ((goals,), (), (), ())
+    )
+    grad_one, rights_one, gain_one = backward(goals, saved_one, lambda *new: ())
     received = shifted(grad_one, "section", -1)
 
     lows = lax.optimization_barrier((low_zero, low_one, grad_one))[:2]
@@ -1287,20 +1307,12 @@
 
     d_down = d_up = d_attn = None
     grad_zero, rights_zero, gain_zero = backward(received, saved_zero, hook, (lows,))
-    _, attn_moves[2] = moves_on(attn_sums[2], attn_moves[3])
-    last, attn_moves[1] = moves_on(attn_sums[1], attn_moves[2], waits=attn_sums[0][1:])
-    gain_zero, gain_one = lax.optimization_barrier((gain_zero, gain_one))
     gain_total = own_first(jnp.where(first, gain_zero, gain_one))
     count = tensor * lax.axis_size("dp")
     gain_parts = gain_total.reshape(4, count, width // count).swapaxes(0, 1)
-    (gain_parts,) = on_chip(
-        gate_kernel, "gate", ((gain_parts.shape, gain_parts.dtype),), gain_parts, waits=(last,)
-    )
-    gain_parts = lax.all_to_all(gain_parts, ("dp", "tensor"), 0, 0, tiled=True)
-    gains_grad = jnp.sum(gain_parts, axis=0)
-    outputs = from_chip(lows, (last,))
+    outputs = from_chip(lows, (grad_zero,))
     grads = own_first(jnp.where(first, grad_zero, grad_one)).reshape(tensor, part, width)
-    grads = from_chip(lax.all_to_all(grads, "tensor", 0, 0, tiled=True), (last,))
+    grads = from_chip(lax.all_to_all(grads, "tensor", 0, 0, tiled=True))
 
     block32 = ((wide_half // 2, unit), jnp.float32)
     down32 = ((unit, wide_half // 2), jnp.float32)
@@ -1311,7 +1323,6 @@
         (block32, down32, block32, down32),
         *mlp_sums[0],
         mlp_moves[1],
-        waits=(last,),
     )
     outs = (
         ((wide_half // 2, 2 * unit), jnp.float32),
@@ -1321,6 +1332,14 @@
     up_grad, down_grad = with_core(
         mlp_join_kernel, "mlp_join", core_word, outs, up_keep, down_keep, *sent
     )
+    waits = (outputs, attn_sums[1][1])
+    total, attn_moves[2] = moves_on(attn_sums[2], attn_moves[3], waits=waits)
+    outs = ((gain_parts.shape, gain_parts.dtype),)
+    (gain_parts,) = on_chip(gate_kernel, "gate", outs, gain_parts, waits=(total,))
+    gain_parts = lax.all_to_all(gain_parts, ("dp", "tensor"), 0, 0, tiled=True)
+    gains_grad = jnp.sum(gain_parts, axis=0)
+    waits = (up_grad, gains_grad, attn_sums[0][1])
+    last, attn_moves[1] = moves_on(attn_sums[1], attn_moves[2], waits=waits)
     outs = (((wide_half // 2, 512), jnp.float32),) * 2
     keep, send = with_core(
         last_sum_kernel,
@@ -1329,7 +1348,7 @@
         outs,
         *attn_sums[0],
         attn_moves[1],
-        waits=(outputs, grads, gains_grad, up_grad),
+        waits=(grads,),
     )
     spots = tuple((i * 128, (i + 1) * 128, i * 256) for i in range(3))
     outs = (((wide_half // 2, 768), jnp.float32), ((256, wide_half // 2), jnp.float32))

time: 660 us -> 680 us (1.030)
  starting transfers between devices: 81.2 us -> 126 us
  waiting for transfers between devices: 260 us -> 221 us
  local copies, waits for them, and re-layouts: 62 us -> 71.6 us
    ppermute x42 -> x43, waiting for transfers between devices: 112 us -> 71.9 us  [flip_pairs(): return lax.ppermute(block, 'dp', [(i, i ^ distance) for i in range(size)])]
    ppermute x15, starting transfers between devices: 27.6 us -> 56.5 us  [passed_on(): lax.ppermute(block, 'tensor', [(i, (i + step) % size) for i in range(size)])]
    ppermute x15, waiting for transfers between devices: 101 us -> 82.6 us  [passed_on(): lax.ppermute(block, 'tensor', [(i, (i + step) % size) for i in range(size)])]
    ppermute x2 -> x3, waiting for transfers between devices: 42.6 us -> 24.2 us  [shifted(): return lax.ppermute(block, axis, route)]
    ppermute x0 -> x6, waiting for transfers between devices: none -> 17.3 us  [the longest x3 17.3 us: along(): return lax.ppermute(block, 'tensor', pairs)]
    all_to_all x2 -> x1, waiting for transfers between devices: 0.01 us -> 16.8 us  [per_chip(): grads = from_chip(lax.all_to_all(grads, 'tensor', 0, 0, tiled=True))]
    ppermute x2 -> x3, starting transfers between devices: 4.82 us -> 21.5 us  [shifted(): return lax.ppermute(block, axis, route)]
    all_to_all x2 -> x1, starting transfers between devices: 11.1 us -> 3.52 us  [per_chip(): grads = from_chip(lax.all_to_all(grads, 'tensor', 0, 0, tiled=True))]
  transfers between devices with their start and end apart: 63 -> 70, of which waited for: 36 -> 37; matrix products, arithmetic and copies ran while one was open for 2% -> 4% of each run, Pallas kernels for 15% -> 15%
where the time goes in v11:
time: 680 us; the launch traced here: 669 us
  Pallas kernels  229 us (34%)
  waiting for transfers between devices  221 us (32%)
  starting transfers between devices  126 us (19%)
  local copies, waits for them, and re-layouts  71.6 us (11%)
  other arithmetic  18.1 us (3%)
    pallas_call x31, Pallas kernels, on_chip(): pl.pallas_call(without(kernel, len(operands), len(waits)), in_specs=[spac...  92.4 us
    pallas_call x6, Pallas kernels, by_pairs(): pl.pallas_call(without(functools.partial(kernel, len(pieces[0])), taken,...  84.9 us
    ppermute x15, waiting for transfers between devices, passed_on(): lax.ppermute(block, 'tensor', [(i, (i + step) % size) for i in range(size)])  82.6 us
    ppermute x43, waiting for transfers between devices, flip_pairs(): return lax.ppermute(block, 'dp', [(i, i ^ distance) for i in range(size)])  71.9 us
    unnamed x330, local copies, waits for them, and re-layouts  58.3 us
    ppermute x15, starting transfers between devices, passed_on(): lax.ppermute(block, 'tensor', [(i, (i + step) % size) for i in range(size)])  56.5 us
    pallas_call x4, Pallas kernels, weight_grads(): pl.pallas_call(without(functools.partial(kernel, base), 1 + len(arrays),...  29.1 us
    ppermute x43, starting transfers between devices, flip_pairs(): return lax.ppermute(block, 'dp', [(i, i ^ distance) for i in range(size)])  25.2 us
  transfers between devices with their start and end apart: 70, of which 37 were waited for; matrix products, arithmetic and copies ran while one was open for 4% of the time, Pallas kernels for 15%

profile of v11, /device:TPU:0, one launch (start us, length us, event | category | flops | bytes accessed | tf_op | source)
XLA Modules:
  0.0 668.6 jit_solution(16476692243608062078)
XLA Ops:
  16.5 2.6 collective-permute-start.5
  23.6 10.5 %collective-permute-done.5.refs_6_.refs_2_.refs_3_ = bf16[512,512]{1,0:T(8,128)(2,1)} collective-permute-done((bf16[512,512]{1,0:T(8,128)(2,1)}, bf16[512,512]{1,0:T(8,128)(2,1)}, u32[]{:S(2)}, u32[]{:S(2)}) %collective-permute-start.5) | collective-permute-done | bytes 524320 | tf_op jit(solution)/shard_map/ppermute | solution.py:803
  39.0 11.0 %collective-permute-done.6.refs_1_.refs_7_.refs_3_.refs_5_.refs_4_ = bf16[512,512]{1,0:T(8,128)(2,1)} collective-permute-done((bf16[512,512]{1,0:T(8,128)(2,1)}, bf16[512,512]{1,0:T(8,128)(2,1)}, u32[]{:S(2)}, u32[]{:S(2)}) %collective-permute-start.6) | collective-permute-done | bytes 524320 | tf_op jit(solution)/shard_map/ppermute | solution.py:803
  50.0 10.2 %collective-permute-done.9.refs_4_.refs_5_.refs_7_ = bf16[512,512]{1,0:T(8,128)(2,1)S(1)} collective-permute-done((bf16[512,512]{1,0:T(8,128)(2,1)S(1)}, bf16[512,512]{1,0:T(8,128)(2,1)S(1)}, u32[]{:S(2)}, u32[]{:S(2)}) %collective-permute-start.9) | collective-permute-done | bytes 524320 | tf_op jit(solution)/shard_map/ppermute | solution.py:798
  60.2 7.1 %collective-permute-done.4.refs_1_ = bf16[512,1024]{1,0:T(8,128)(2,1)S(1)} collective-permute-done((bf16[512,1024]{1,0:T(8,128)(2,1)}, bf16[512,1024]{1,0:T(8,128)(2,1)S(1)}, u32[]{:S(2)}, u32[]{:S(2)}) %collective-permute-start.4) | collective-permute-done | bytes 1048608 | tf_op jit(solution)/shard_map/ppermute | solution.py:28
  71.4 28.5 %collective-permute-start.15 = (bf16[512,512]{1,0:T(8,128)(2,1)}, bf16[512,512]{1,0:T(8,128)(2,1)S(1)}, u32[]{:S(2)}, u32[]{:S(2)}) collective-permute-start(bf16[512,512]{1,0:T(8,128)(2,1)} %copy-done.99), channel_id=1, source_target_pairs={{0,1},{1,2},{2,3},{3,0},{4,5},{5,6},{6,7},{7,4},{8,9},{9,10},{10,1... | collective-permute-start | bytes 1572872 | tf_op jit(solution)/shard_map/ppermute | solution.py:803
  106.1 6.4 collective-permute-done.15.refs_13_.refs_3_.refs_2_
  117.8 5.8 collective-permute-done.16.refs_14_.refs_2_.refs_4_
  129.1 16.7 %attend.2 = (bf16[4,1024,128]{2,1,0:T(8,128)(2,1)S(1)}, bf16[4,1024,128]{2,1,0:T(8,128)(2,1)S(1)}, bf16[4,1024,128]{2,1,0:T(8,128)(2,1)S(1)}, f32[4,2,1024]{2,1,0:T(2,128)S(1)}, bf16[1024,512]{1,0:T(8,128)(2,1)S(1)}) custom-call(s32[1]{0:T(128)} %bitcast.refs_0_, f32[1024,128]{1,0:T(8,128)S(1)} %get-tuple-element.246.refs_1_, ...), custom_call_target="tpu_custom_call" | custom-call | flops 11811160064 | bytes 11567104 | tf_op jit(solution)/shard_map/attend/pallas_call | solution.py:708
  150.3 2.9 attn_out.2
  156.0 14.1 %collective-permute-done.22.refs_4_.refs_5_ = bf16[512,512]{1,0:T(8,128)(2,1)S(1)} collective-permute-done((bf16[512,512]{1,0:T(8,128)(2,1)}, bf16[512,512]{1,0:T(8,128)(2,1)S(1)}, u32[]{:S(2)}, u32[]{:S(2)}) %collective-permute-start.22) | collective-permute-done | bytes 524320 | tf_op jit(solution)/shard_map/ppermute | solution.py:803
  170.1 10.9 %collective-permute-done.23.refs_5_.refs_4_.refs_6_ = bf16[512,512]{1,0:T(8,128)(2,1)S(1)} collective-permute-done((bf16[512,512]{1,0:T(8,128)(2,1)}, bf16[512,512]{1,0:T(8,128)(2,1)S(1)}, u32[]{:S(2)}, u32[]{:S(2)}) %collective-permute-start.23) | collective-permute-done | bytes 524320 | tf_op jit(solution)/shard_map/ppermute | solution.py:803
  182.2 3.4 after_attn.2
  189.1 12.9 %collective-permute-done.27.refs_9_.refs_8_ = bf16[512,512]{1,0:T(8,128)(2,1)S(1)} collective-permute-done((bf16[512,512]{1,0:T(8,128)(2,1)}, bf16[512,512]{1,0:T(8,128)(2,1)S(1)}, u32[]{:S(2)}, u32[]{:S(2)}) %collective-permute-start.27) | collective-permute-done | bytes 524320 | tf_op jit(solution)/shard_map/ppermute | solution.py:798
  204.3 7.7 %mlp_up.2 = (bf16[1024,2048]{1,0:T(8,128)(2,1)S(1)}, bf16[1024,2048]{1,0:T(8,128)(2,1)S(1)}) custom-call(bf16[512,1024]{1,0:T(8,128)(2,1)S(1)} %get-tuple-element.111.refs_0_.refs_1_, bf16[512,1024]{1,0:T(8,128)(2,1)S(1)} %collective-permute-done.26.refs_1_.refs_2_, bf16[512,512]{1,0:T(8,128)(2,1)S(1)} %copy-done.100, bf16[512,512]{1,0:T(8,128)(2,1)S(1)} %copy-done.145, ...), custom_call_target="tpu_custom_call" | custom-call | flops 4294967296 | bytes 14680064 | tf_op jit(solution)/shard_map/mlp_up/pallas_call | solution.py:690
  214.1 4.5 mlp_down.2
  224.6 18.9 %collective-permute-start.30 = (bf16[512,1024]{1,0:T(8,128)(2,1)S(1)}, bf16[512,1024]{1,0:T(8,128)(2,1)S(1)}, u32[]{:S(2)}, u32[]{:S(2)}) collective-permute-start(bf16[512,1024]{1,0:T(8,128)(2,1)S(1)} %get-tuple-element.144.refs_3_), channel_id=1, source_target_pairs={{0,16},{1,17},{2,18},{3,19},{4,20},{5,21},{6,22},{7,23},{8,24},{9,... | collective-permute-start | bytes 3145736 | tf_op jit(solution)/shard_map/ppermute | solution.py:28
  247.3 3.7 collective-permute-start.33
  251.2 6.9 %collective-permute-done.32.refs_2_ = bf16[128,1024]{1,0:T(8,128)(2,1)S(1)} collective-permute-done((bf16[128,1024]{1,0:T(8,128)(2,1)S(1)}, bf16[128,1024]{1,0:T(8,128)(2,1)S(1)}, u32[]{:S(2)}, u32[]{:S(2)}) %collective-permute-start.32) | collective-permute-done | bytes 262176 | tf_op jit(solution)/shard_map/ppermute | solution.py:1081
  258.1 10.4 %collective-permute-done.33.refs_3_ = bf16[128,1024]{1,0:T(8,128)(2,1)S(1)} collective-permute-done((bf16[128,1024]{1,0:T(8,128)(2,1)S(1)}, bf16[128,1024]{1,0:T(8,128)(2,1)S(1)}, u32[]{:S(2)}, u32[]{:S(2)}) %collective-permute-start.33) | collective-permute-done | bytes 262176 | tf_op jit(solution)/shard_map/ppermute | solution.py:1081
  271.9 2.6 collective-permute-done.35.refs_4_.refs_8_
  274.6 16.7 %attend.3 = (bf16[4,1024,128]{2,1,0:T(8,128)(2,1)S(1)}, bf16[4,1024,128]{2,1,0:T(8,128)(2,1)S(1)}, bf16[4,1024,128]{2,1,0:T(8,128)(2,1)S(1)}, f32[4,2,1024]{2,1,0:T(2,128)S(1)}, bf16[1024,512]{1,0:T(8,128)(2,1)S(1)}) custom-call(s32[1]{0:T(128)} %bitcast.refs_0_, f32[1024,128]{1,0:T(8,128)S(1)} %get-tuple-element.246.refs_1_, ...), custom_call_target="tpu_custom_call" | custom-call | flops 11811160064 | bytes 11567104 | tf_op jit(solution)/shard_map/attend/pallas_call | solution.py:708
  291.4 3.2 attn_out.3
  294.7 2.5 collective-permute-done.36.refs_3_
  297.3 3.4 after_attn.3
  300.9 2.5 collective-permute-done.37.refs_1_.refs_8_
  303.5 7.7 %mlp_up.3 = (bf16[1024,2048]{1,0:T(8,128)(2,1)S(1)}, bf16[1024,2048]{1,0:T(8,128)(2,1)S(1)}) custom-call(bf16[512,1024]{1,0:T(8,128)(2,1)S(1)} %get-tuple-element.124.refs_0_.refs_7_, bf16[512,1024]{1,0:T(8,128)(2,1)S(1)} %collective-permute-done.37.refs_1_.refs_8_, bf16[512,512]{1,0:T(8,128)(2,1)S(1)} %copy-done.100, bf16[512,512]{1,0:T(8,128)(2,1)S(1)} %copy-done.145, ...), custom_call_target="tpu_custom_call" | custom-call | flops 4294967296 | bytes 14680064 | tf_op jit(solution)/shard_map/mlp_up/pallas_call | solution.py:690
  313.2 4.5 mlp_down.3
  317.9 2.5 collective-permute-done.38.refs_3_
  327.4 7.2 %mlp_up_back.2.refs_0_.refs_9_ = bf16[1024,2048]{1,0:T(8,128)(2,1)S(1)} custom-call(bf16[512,1024]{1,0:T(8,128)(2,1)S(1)} %get-tuple-element.130.refs_0_.refs_11_, bf16[512,1024]{1,0:T(8,128)(2,1)S(1)} %collective-permute-done.39.refs_1_.refs_12_, bf16[1024,2048]{1,0:T(8,128)(2,1)} %copy-done.47, bf16[512,512]{1,0:T(8,128)(2,1)} %copy-done.46, ...), custom_call_target="tpu_custom_call" | custom-call | tf_op jit(solution)/shard_map/mlp_up_back/pallas_call | solution.py:729
  334.6 4.5 mlp_back.2
  341.9 3.9 into_attn_back.2
  349.7 13.0 %attend_back.4.refs_0_.refs_9_ = bf16[1024,768]{1,0:T(8,128)(2,1)S(1)} custom-call(s32[1]{0:T(128)} %bitcast.refs_0_, f32[1024,128]{1,0:T(8,128)S(1)} %get-tuple-element.246.refs_1_, f32[1024,128]{1,0:T(8,128)S(1)} %get-tuple-element.247.refs_2_, bf16[512,1024]{1,0:T(8,128)(2,1)S(1)} %get-tuple-element.135.refs_3_.refs_11_, ...), custom_call_target="tpu_custom_call" | custom-call | flops 11274289152 | bytes 6815744 | tf_op jit(solution)/shard_map/attend_back/pallas_call | solution.py:708
  362.8 12.8 %attend_back.5.refs_1_.refs_9_ = bf16[1024,768]{1,0:T(8,128)(2,1)S(1)} custom-call(s32[1]{0:T(128)} %bitcast.refs_0_, f32[1024,128]{1,0:T(8,128)S(1)} %get-tuple-element.246.refs_1_, f32[1024,128]{1,0:T(8,128)S(1)} %get-tuple-element.247.refs_2_, bf16[512,1024]{1,0:T(8,128)(2,1)S(1)} %get-tuple-element.135.refs_3_.refs_11_, ...), custom_call_target="tpu_custom_call" | custom-call | flops 11274289152 | bytes 6815744 | tf_op jit(solution)/shard_map/attend_back/pallas_call | solution.py:708
  377.2 5.6 attn_back.2
  392.2 3.1 out_of_layer.2
  398.1 7.4 %all-to-all-start = ((bf16[4,128,1024]{2,1,0:T(8,128)(2,1)}), bf16[4,128,1024]{2,1,0:T(8,128)(2,1)S(1)}, u32[]{:S(2)}, u32[]{:S(2)}) async-start(bf16[4,128,1024]{2,1,0:T(8,128)(2,1)} %bitcast.16), calls=%async_computation | async-start | bytes 2097152 | tf_op jit(solution)/shard_map/all_to_all | solution.py:1241
  405.5 17.1 %collective-permute-done.43.refs_1_ = bf16[512,1024]{1,0:T(8,128)(2,1)S(1)} collective-permute-done((bf16[512,1024]{1,0:T(8,128)(2,1)}, bf16[512,1024]{1,0:T(8,128)(2,1)S(1)}, u32[]{:S(2)}, u32[]{:S(2)}) %collective-permute-start.43) | collective-permute-done | bytes 1048608 | tf_op jit(solution)/shard_map/ppermute | solution.py:28
  426.9 4.6 all-to-all-done.refs_11_.refs_1_
  432.5 6.8 %mlp_up_back.3.refs_3_.refs_0_ = bf16[1024,2048]{1,0:T(8,128)(2,1)S(1)} custom-call(bf16[512,1024]{1,0:T(8,128)(2,1)S(1)} %get-tuple-element.147.refs_0_.refs_5_, bf16[512,1024]{1,0:T(8,128)(2,1)S(1)} %collective-permute-done.44.refs_1_.refs_6_, bf16[1024,2048]{1,0:T(8,128)(2,1)} %copy-done.69, bf16[512,512]{1,0:T(8,128)(2,1)} %copy-done.46, ...), custom_call_target="tpu_custom_call" | custom-call | tf_op jit(solution)/shard_map/mlp_up_back/pallas_call | solution.py:729
  441.3 7.2 %mlp_grads.2 = (f32[1024,512]{1,0:T(8,128)S(1)}, bf16[1024,512]{1,0:T(8,128)(2,1)S(1)}, f32[1024,512]{1,0:T(8,128)S(1)}, bf16[1024,512]{1,0:T(8,128)(2,1)S(1)}) custom-call(s32[1]{0:T(128)} %bitcast.17.refs_0_, bf16[512,1024]{1,0:T(8,128)(2,1)} %copy-done.49, bf16[512,1024]{1,0:T(8,128)(2,1)} %copy-done.50, bf16[1024,2048]{1,0:T(8,128)(2,1)} %copy-done.3, ...), custom_call_target="tpu_custom_call" | custom-call | tf_op jit(solution)/shard_map/mlp_grads/pallas_call | solution.py:897
  449.9 4.5 mlp_back.3
  455.2 8.5 %mlp_grads.3 = (f32[1024,512]{1,0:T(8,128)S(1)}, bf16[1024,512]{1,0:T(8,128)(2,1)}, f32[1024,512]{1,0:T(8,128)S(1)}, bf16[1024,512]{1,0:T(8,128)(2,1)S(1)}) custom-call(s32[1]{0:T(128)} %bitcast.17.refs_0_, bf16[512,1024]{1,0:T(8,128)(2,1)} %copy-done.49, bf16[512,1024]{1,0:T(8,128)(2,1)} %copy-done.50, bf16[1024,2048]{1,0:T(8,128)(2,1)} %copy-done.3, ...), custom_call_target="tpu_custom_call" | custom-call | tf_op jit(solution)/shard_map/mlp_grads/pallas_call | solution.py:897
  465.1 4.0 into_attn_back.3
  473.1 7.6 %collective-permute-done.48.refs_1_.refs_13_ = bf16[1024,512]{1,0:T(8,128)(2,1)S(1)} collective-permute-done((bf16[1024,512]{1,0:T(8,128)(2,1)S(1)}, bf16[1024,512]{1,0:T(8,128)(2,1)S(1)}, u32[]{:S(2)}, u32[]{:S(2)}) %collective-permute-start.48) | collective-permute-done | bytes 1048608 | tf_op jit(solution)/shard_map/ppermute | solution.py:798
  485.6 12.3 %attend_back.6.refs_3_.refs_1_ = bf16[1024,768]{1,0:T(8,128)(2,1)S(1)} custom-call(s32[1]{0:T(128)} %bitcast.refs_0_, f32[1024,128]{1,0:T(8,128)S(1)} %copy-done.130, f32[1024,128]{1,0:T(8,128)S(1)} %copy-done.132, bf16[512,1024]{1,0:T(8,128)(2,1)S(1)} %copy-done.16, bf16[512,1024]{1,0:T(8,128)(2,1)S(1)} %collective-permute-done.46.refs_4_.refs_6_, ...), custom_call_target="tpu_custom_call" | custom-call | flops 11274289152 | bytes 6815744 | tf_op jit(solution)/shard_map/attend_back/pallas_call | solution.py:708
  499.0 4.1 collective-permute-done.47.refs_1_.refs_13_
  503.1 4.5 collective-permute-done.49.refs_2_.refs_14_
  510.9 6.6 attn_grads.2
  519.4 13.4 %attend_back.7.refs_3_.refs_0_ = bf16[1024,768]{1,0:T(8,128)(2,1)S(1)} custom-call(s32[1]{0:T(128)} %bitcast.refs_0_, f32[1024,128]{1,0:T(8,128)S(1)} %copy-done.130, f32[1024,128]{1,0:T(8,128)S(1)} %copy-done.132, bf16[512,1024]{1,0:T(8,128)(2,1)S(1)} %copy-done.17, bf16[512,1024]{1,0:T(8,128)(2,1)S(1)} %copy-done.63, ...), custom_call_target="tpu_custom_call" | custom-call | flops 11274289152 | bytes 6815744 | tf_op jit(solution)/shard_map/attend_back/pallas_call | solution.py:708
  535.6 6.9 %attn_grads.3 = (f32[512,512]{1,0:T(8,128)S(1)}, bf16[512,512]{1,0:T(8,128)(2,1)}, f32[512,512]{1,0:T(8,128)S(1)}, bf16[512,512]{1,0:T(8,128)(2,1)}) custom-call(s32[1]{0:T(128)} %bitcast.17.refs_0_, bf16[512,1024]{1,0:T(8,128)(2,1)} %copy-done.11, bf16[512,1024]{1,0:T(8,128)(2,1)} %copy-done.48, bf16[1024,768]{1,0:T(8,128)(2,1)} %copy-done.34, ...), custom_call_target="tpu_custom_call" | custom-call | tf_op jit(solution)/shard_map/attn_grads/pallas_call | solution.py:897
  544.5 5.9 attn_back.3
  561.3 7.3 %collective-permute-done.54.refs_1_ = bf16[512,512]{1,0:T(8,128)(2,1)} collective-permute-done((bf16[512,512]{1,0:T(8,128)(2,1)}, bf16[512,512]{1,0:T(8,128)(2,1)}, u32[]{:S(2)}, u32[]{:S(2)}) %collective-permute-start.54) | collective-permute-done | bytes 524320 | tf_op jit(solution)/shard_map/ppermute | solution.py:798
  573.1 4.9 collective-permute-done.55.refs_7_.refs_3_
  582.2 3.5 out_of_layer.3
  593.6 5.4 all-to-all-start.2
  599.0 2.7 maximum_select_fusion.3
  601.7 3.5 all-to-all-done.2
  605.2 3.5 all-to-all-start.1
  611.9 3.8 collective-permute-start.62
  619.0 16.8 %all-to-all-done.1.refs_1_ = bf16[4,128,1024]{2,1,0:T(8,128)(2,1)S(1)} async-done(((bf16[4,128,1024]{2,1,0:T(8,128)(2,1)}), bf16[4,128,1024]{2,1,0:T(8,128)(2,1)S(1)}, u32[]{:S(2)}, u32[]{:S(2)}) %all-to-all-start.1) | async-done | bytes 1048608 | tf_op jit(solution)/shard_map/all_to_all | solution.py:1315
  636.0 3.8 collective-permute-done.62.refs_2_
  641.3 8.9 %collective-permute-start.65 = (bf16[512,512]{1,0:T(8,128)(2,1)S(1)}, bf16[512,512]{1,0:T(8,128)(2,1)S(1)}, u32[]{:S(2)}, u32[]{:S(2)}) collective-permute-start(bf16[512,512]{1,0:T(8,128)(2,1)S(1)} %moved.11), channel_id=1, source_target_pairs={{0,3},{1,0},{2,1},{3,2},{4,7},{5,4},{6,5},{7,6},{8,11},{9,8},{10,9... | collective-permute-start | bytes 1572872 | tf_op jit(solution)/shard_map/ppermute | solution.py:803
  651.2 10.8 %collective-permute-done.65.refs_3_ = bf16[512,512]{1,0:T(8,128)(2,1)S(1)} collective-permute-done((bf16[512,512]{1,0:T(8,128)(2,1)S(1)}, bf16[512,512]{1,0:T(8,128)(2,1)S(1)}, u32[]{:S(2)}, u32[]{:S(2)}) %collective-permute-start.65) | collective-permute-done | bytes 524320 | tf_op jit(solution)/shard_map/ppermute | solution.py:803
  (519 shorter events, 178.8 us)
Async XLA Ops:
  5.6 8.0 %collective-permute-start = (bf16[2,128,1024]{2,1,0:T(8,128)(2,1)}, bf16[2,128,1024]{2,1,0:T(8,128)(2,1)S(1)}, u32[]{:S(2)}, u32[]{:S(2)}) collective-permute-start(bf16[2,128,1024]{2,1,0:T(8,128)(2,1)} %get-tuple-element.235), channel_id=1, source_target_pairs={{0,4},{4,0},{8,12},{12,8},{1,5},{5,1},{9,13},{13,9},{2,6},{6,2},{1... | collective-permute-start | bytes 1572872 | tf_op jit(solution)/shard_map/ppermute | solution.py:798
  14.5 4.7 collective-permute-start.1
  15.2 4.0 collective-permute-start.2
  15.8 3.3 collective-permute-start.3
  16.5 17.6 %collective-permute-start.5 = (bf16[512,512]{1,0:T(8,128)(2,1)}, bf16[512,512]{1,0:T(8,128)(2,1)}, u32[]{:S(2)}, u32[]{:S(2)}) collective-permute-start(bf16[512,512]{1,0:T(8,128)(2,1)} %pad_maximum_fusion.refs_3_.refs_5_.refs_1_.refs_2_), channel_id=1, source_target_pairs={{0,1},{1,2},{2,3},{3,0},{4,5},{5,6},{6,7},{7,4},{8,9},{9,10},{10,1... | collective-permute-start | bytes 1572872 | tf_op jit(solution)/shard_map/ppermute | solution.py:803
  20.8 46.6 %collective-permute-start.4 = (bf16[512,1024]{1,0:T(8,128)(2,1)}, bf16[512,1024]{1,0:T(8,128)(2,1)S(1)}, u32[]{:S(2)}, u32[]{:S(2)}) collective-permute-start(bf16[512,1024]{1,0:T(8,128)(2,1)} %bitcast.9), channel_id=1, source_target_pairs={{16,0},{17,1},{18,2},{19,3},{20,4},{21,5},{22,6},{23,7},{24,8},{25... | collective-permute-start | bytes 3145736 | tf_op jit(solution)/shard_map/ppermute | solution.py:28
  22.0 15.3 %collective-permute-start.7 = (bf16[512,512]{1,0:T(8,128)(2,1)}, bf16[512,512]{1,0:T(8,128)(2,1)}, u32[]{:S(2)}, u32[]{:S(2)}) collective-permute-start(bf16[512,512]{1,0:T(8,128)(2,1)} %pad_maximum_fusion.refs_3_.refs_5_.refs_1_.refs_2_), channel_id=1, source_target_pairs={{0,8},{4,12},{8,0},{12,4},{1,9},{5,13},{9,1},{13,5},{2,10},{6,14},... | collective-permute-start | bytes 1572872 | tf_op jit(solution)/shard_map/ppermute | solution.py:798
  34.1 15.9 %collective-permute-start.6 = (bf16[512,512]{1,0:T(8,128)(2,1)}, bf16[512,512]{1,0:T(8,128)(2,1)}, u32[]{:S(2)}, u32[]{:S(2)}) collective-permute-start(bf16[512,512]{1,0:T(8,128)(2,1)} %collective-permute-done.5.refs_6_.refs_2_.refs_3_), channel_id=1, source_target_pairs={{0,1},{1,2},{2,3},{3,0},{4,5},{5,6},{6,7},{7,4},{8,9},{9,10},{10,1... | collective-permute-start | bytes 1572872 | tf_op jit(solution)/shard_map/ppermute | solution.py:803
  34.1 15.9 %collective-permute-start.8 = (bf16[512,512]{1,0:T(8,128)(2,1)S(1)}, bf16[512,512]{1,0:T(8,128)(2,1)S(1)}, u32[]{:S(2)}, u32[]{:S(2)}) collective-permute-start(bf16[512,512]{1,0:T(8,128)(2,1)S(1)} %dynamic-slice_bitcast_fusion.3.refs_0_), channel_id=1, source_target_pairs={{0,8},{4,12},{8,0},{12,4},{1,9},{5,13},{9,1},{13,5},{2,10},{6,14},... | collective-permute-start | bytes 1572872 | tf_op jit(solution)/shard_map/ppermute | solution.py:798
  36.8 23.4 %collective-permute-start.9 = (bf16[512,512]{1,0:T(8,128)(2,1)S(1)}, bf16[512,512]{1,0:T(8,128)(2,1)S(1)}, u32[]{:S(2)}, u32[]{:S(2)}) collective-permute-start(bf16[512,512]{1,0:T(8,128)(2,1)S(1)} %dynamic-slice_bitcast_fusion.2.refs_0_), channel_id=1, source_target_pairs={{0,8},{4,12},{8,0},{12,4},{1,9},{5,13},{9,1},{13,5},{2,10},{6,14},... | collective-permute-start | bytes 1572872 | tf_op jit(solution)/shard_map/ppermute | solution.py:798
  37.4 63.9 %collective-permute-start.12 = (bf16[512,512]{1,0:T(8,128)(2,1)}, bf16[512,512]{1,0:T(8,128)(2,1)S(1)}, u32[]{:S(2)}, u32[]{:S(2)}) collective-permute-start(bf16[512,512]{1,0:T(8,128)(2,1)} %collective-permute-done.5.refs_6_.refs_2_.refs_3_), channel_id=1, source_target_pairs={{0,8},{4,12},{8,0},{12,4},{1,9},{5,13},{9,1},{13,5},{2,10},{6,14},... | collective-permute-start | bytes 1572872 | tf_op jit(solution)/shard_map/ppermute | solution.py:798
  50.0 52.9 %collective-permute-start.11 = (bf16[512,512]{1,0:T(8,128)(2,1)}, bf16[512,512]{1,0:T(8,128)(2,1)S(1)}, u32[]{:S(2)}, u32[]{:S(2)}) collective-permute-start(bf16[512,512]{1,0:T(8,128)(2,1)} %collective-permute-done.6.refs_1_.refs_7_.refs_3_.refs_5_.refs_4_), channel_id=1, source_target_pairs={{0,1},{1,2},{2,3},{3,0},{4,5},{5,6},{6,7},{7,4},{8,9},{9,10},{10,1... | collective-permute-start | bytes 1572872 | tf_op jit(solution)/shard_map/ppermute | solution.py:803
  71.3 57.7 %collective-permute-start.10 = (bf16[512,1024]{1,0:T(8,128)(2,1)S(1)}, bf16[512,1024]{1,0:T(8,128)(2,1)S(1)}, u32[]{:S(2)}, u32[]{:S(2)}) collective-permute-start(bf16[512,1024]{1,0:T(8,128)(2,1)S(1)} %norm_in.2.refs_3_.refs_1_), channel_id=1, source_target_pairs={{0,4},{4,0},{8,12},{12,8},{1,5},{5,1},{9,13},{13,9},{2,6},{6,2},{1... | collective-permute-start | bytes 3145736 | tf_op jit(solution)/shard_map/ppermute | solution.py:798
  71.4 41.1 %collective-permute-start.15 = (bf16[512,512]{1,0:T(8,128)(2,1)}, bf16[512,512]{1,0:T(8,128)(2,1)S(1)}, u32[]{:S(2)}, u32[]{:S(2)}) collective-permute-start(bf16[512,512]{1,0:T(8,128)(2,1)} %copy-done.99), channel_id=1, source_target_pairs={{0,1},{1,2},{2,3},{3,0},{4,5},{5,6},{6,7},{7,4},{8,9},{9,10},{10,1... | collective-permute-start | bytes 1572872 | tf_op jit(solution)/shard_map/ppermute | solution.py:803
  101.0 22.6 %collective-permute-start.16 = (bf16[512,512]{1,0:T(8,128)(2,1)S(1)}, bf16[512,512]{1,0:T(8,128)(2,1)S(1)}, u32[]{:S(2)}, u32[]{:S(2)}) collective-permute-start(bf16[512,512]{1,0:T(8,128)(2,1)S(1)} %gate.4.refs_1_.refs_3_), channel_id=1, source_target_pairs={{0,1},{1,2},{2,3},{3,0},{4,5},{5,6},{6,7},{7,4},{8,9},{9,10},{10,1... | collective-permute-start | bytes 1572872 | tf_op jit(solution)/shard_map/ppermute | solution.py:803
  101.3 15.0 %collective-permute-start.13 = (bf16[512,512]{1,0:T(8,128)(2,1)}, bf16[512,512]{1,0:T(8,128)(2,1)S(1)}, u32[]{:S(2)}, u32[]{:S(2)}) collective-permute-start(bf16[512,512]{1,0:T(8,128)(2,1)} %collective-permute-done.6.refs_1_.refs_7_.refs_3_.refs_5_.refs_4_), channel_id=1, source_target_pairs={{0,8},{4,12},{8,0},{12,4},{1,9},{5,13},{9,1},{13,5},{2,10},{6,14},... | collective-permute-start | bytes 1572872 | tf_op jit(solution)/shard_map/ppermute | solution.py:798
  102.8 24.7 %collective-permute-start.14 = (bf16[512,512]{1,0:T(8,128)(2,1)S(1)}, bf16[512,512]{1,0:T(8,128)(2,1)S(1)}, u32[]{:S(2)}, u32[]{:S(2)}) collective-permute-start(bf16[512,512]{1,0:T(8,128)(2,1)S(1)} %collective-permute-done.11.refs_8_.refs_4_.refs_6_.refs_5_), channel_id=1, source_target_pairs={{0,8},{4,12},{8,0},{12,4},{1,9},{5,13},{9,1},{13,5},{2,10},{6,14},... | collective-permute-start | bytes 1572872 | tf_op jit(solution)/shard_map/ppermute | solution.py:798
  112.5 36.3 %collective-permute-start.17 = (bf16[512,512]{1,0:T(8,128)(2,1)S(1)}, bf16[512,512]{1,0:T(8,128)(2,1)S(1)}, u32[]{:S(2)}, u32[]{:S(2)}) collective-permute-start(bf16[512,512]{1,0:T(8,128)(2,1)S(1)} %collective-permute-done.15.refs_13_.refs_3_.refs_2_), channel_id=1, source_target_pairs={{0,1},{1,2},{2,3},{3,0},{4,5},{5,6},{6,7},{7,4},{8,9},{9,10},{10,1... | collective-permute-start | bytes 1572872 | tf_op jit(solution)/shard_map/ppermute | solution.py:803
  116.3 32.5 %collective-permute-start.19 = (bf16[512,512]{1,0:T(8,128)(2,1)S(1)}, bf16[512,512]{1,0:T(8,128)(2,1)S(1)}, u32[]{:S(2)}, u32[]{:S(2)}) collective-permute-start(bf16[512,512]{1,0:T(8,128)(2,1)S(1)} %collective-permute-done.15.refs_13_.refs_3_.refs_2_), channel_id=1, source_target_pairs={{0,8},{4,12},{8,0},{12,4},{1,9},{5,13},{9,1},{13,5},{2,10},{6,14},... | collective-permute-start | bytes 1572872 | tf_op jit(solution)/shard_map/ppermute | solution.py:798
  123.6 25.1 %collective-permute-start.18 = (bf16[512,512]{1,0:T(8,128)(2,1)S(1)}, bf16[512,512]{1,0:T(8,128)(2,1)S(1)}, u32[]{:S(2)}, u32[]{:S(2)}) collective-permute-start(bf16[512,512]{1,0:T(8,128)(2,1)S(1)} %collective-permute-done.16.refs_14_.refs_2_.refs_4_), channel_id=1, source_target_pairs={{0,1},{1,2},{2,3},{3,0},{4,5},{5,6},{6,7},{7,4},{8,9},{9,10},{10,1... | collective-permute-start | bytes 1572872 | tf_op jit(solution)/shard_map/ppermute | solution.py:803
  127.5 21.6 %collective-permute-start.20 = (bf16[512,512]{1,0:T(8,128)(2,1)S(1)}, bf16[512,512]{1,0:T(8,128)(2,1)S(1)}, u32[]{:S(2)}, u32[]{:S(2)}) collective-permute-start(bf16[512,512]{1,0:T(8,128)(2,1)S(1)} %collective-permute-done.16.refs_14_.refs_2_.refs_4_), channel_id=1, source_target_pairs={{0,8},{4,12},{8,0},{12,4},{1,9},{5,13},{9,1},{13,5},{2,10},{6,14},... | collective-permute-start | bytes 1572872 | tf_op jit(solution)/shard_map/ppermute | solution.py:798
  153.2 27.8 %collective-permute-start.21 = (bf16[512,1024]{1,0:T(8,128)(2,1)S(1)}, bf16[512,1024]{1,0:T(8,128)(2,1)S(1)}, u32[]{:S(2)}, u32[]{:S(2)}) collective-permute-start(bf16[512,1024]{1,0:T(8,128)(2,1)S(1)} %get-tuple-element.109), channel_id=1, source_target_pairs={{0,4},{4,0},{8,12},{12,8},{1,5},{5,1},{9,13},{13,9},{2,6},{6,2},{1... | collective-permute-start | bytes 3145736 | tf_op jit(solution)/shard_map/ppermute | solution.py:798
  153.3 16.8 %collective-permute-start.22 = (bf16[512,512]{1,0:T(8,128)(2,1)}, bf16[512,512]{1,0:T(8,128)(2,1)S(1)}, u32[]{:S(2)}, u32[]{:S(2)}) collective-permute-start(bf16[512,512]{1,0:T(8,128)(2,1)} %copy-done.123), channel_id=1, source_target_pairs={{0,1},{1,2},{2,3},{3,0},{4,5},{5,6},{6,7},{7,4},{8,9},{9,10},{10,1... | collective-permute-start | bytes 1572872 | tf_op jit(solution)/shard_map/ppermute | solution.py:803
  153.4 27.5 %collective-permute-start.23 = (bf16[512,512]{1,0:T(8,128)(2,1)}, bf16[512,512]{1,0:T(8,128)(2,1)S(1)}, u32[]{:S(2)}, u32[]{:S(2)}) collective-permute-start(bf16[512,512]{1,0:T(8,128)(2,1)} %copy-done.36), channel_id=1, source_target_pairs={{0,1},{1,2},{2,3},{3,0},{4,5},{5,6},{6,7},{7,4},{8,9},{9,10},{10,1... | collective-permute-start | bytes 1572872 | tf_op jit(solution)/shard_map/ppermute | solution.py:803
  154.0 27.0 %collective-permute-start.24 = (bf16[512,512]{1,0:T(8,128)(2,1)}, bf16[512,512]{1,0:T(8,128)(2,1)S(1)}, u32[]{:S(2)}, u32[]{:S(2)}) collective-permute-start(bf16[512,512]{1,0:T(8,128)(2,1)} %copy-done.123), channel_id=1, source_target_pairs={{0,8},{4,12},{8,0},{12,4},{1,9},{5,13},{9,1},{13,5},{2,10},{6,14},... | collective-permute-start | bytes 1572872 | tf_op jit(solution)/shard_map/ppermute | solution.py:798
  155.3 25.7 %collective-permute-start.25 = (bf16[512,512]{1,0:T(8,128)(2,1)}, bf16[512,512]{1,0:T(8,128)(2,1)S(1)}, u32[]{:S(2)}, u32[]{:S(2)}) collective-permute-start(bf16[512,512]{1,0:T(8,128)(2,1)} %copy-done.36), channel_id=1, source_target_pairs={{0,8},{4,12},{8,0},{12,4},{1,9},{5,13},{9,1},{13,5},{2,10},{6,14},... | collective-permute-start | bytes 1572872 | tf_op jit(solution)/shard_map/ppermute | solution.py:798
  187.0 15.1 %collective-permute-start.26 = (bf16[512,1024]{1,0:T(8,128)(2,1)S(1)}, bf16[512,1024]{1,0:T(8,128)(2,1)S(1)}, u32[]{:S(2)}, u32[]{:S(2)}) collective-permute-start(bf16[512,1024]{1,0:T(8,128)(2,1)S(1)} %get-tuple-element.111.refs_0_.refs_1_), channel_id=1, source_target_pairs={{0,4},{4,0},{8,12},{12,8},{1,5},{5,1},{9,13},{13,9},{2,6},{6,2},{1... | collective-permute-start | bytes 3145736 | tf_op jit(solution)/shard_map/ppermute | solution.py:798
  187.0 15.0 %collective-permute-start.27 = (bf16[512,512]{1,0:T(8,128)(2,1)}, bf16[512,512]{1,0:T(8,128)(2,1)S(1)}, u32[]{:S(2)}, u32[]{:S(2)}) collective-permute-start(bf16[512,512]{1,0:T(8,128)(2,1)} %copy-done.136), channel_id=1, source_target_pairs={{0,8},{4,12},{8,0},{12,4},{1,9},{5,13},{9,1},{13,5},{2,10},{6,14},... | collective-permute-start | bytes 1572872 | tf_op jit(solution)/shard_map/ppermute | solution.py:798
  188.1 25.9 %collective-permute-start.28 = (bf16[512,512]{1,0:T(8,128)(2,1)}, bf16[512,512]{1,0:T(8,128)(2,1)S(1)}, u32[]{:S(2)}, u32[]{:S(2)}) collective-permute-start(bf16[512,512]{1,0:T(8,128)(2,1)} %copy-done.42), channel_id=1, source_target_pairs={{0,8},{4,12},{8,0},{12,4},{1,9},{5,13},{9,1},{13,5},{2,10},{6,14},... | collective-permute-start | bytes 1572872 | tf_op jit(solution)/shard_map/ppermute | solution.py:798
  218.6 2.7 collective-permute-start.29
  224.6 45.4 %collective-permute-start.30 = (bf16[512,1024]{1,0:T(8,128)(2,1)S(1)}, bf16[512,1024]{1,0:T(8,128)(2,1)S(1)}, u32[]{:S(2)}, u32[]{:S(2)}) collective-permute-start(bf16[512,1024]{1,0:T(8,128)(2,1)S(1)} %get-tuple-element.144.refs_3_), channel_id=1, source_target_pairs={{0,16},{1,17},{2,18},{3,19},{4,20},{5,21},{6,22},{7,23},{8,24},{9,... | collective-permute-start | bytes 3145736 | tf_op jit(solution)/shard_map/ppermute | solution.py:28
  246.9 11.1 %collective-permute-start.32 = (bf16[128,1024]{1,0:T(8,128)(2,1)S(1)}, bf16[128,1024]{1,0:T(8,128)(2,1)S(1)}, u32[]{:S(2)}, u32[]{:S(2)}) collective-permute-start(bf16[128,1024]{1,0:T(8,128)(2,1)S(1)} %get-tuple-element.117), channel_id=1, source_target_pairs={{0,1},{1,2},{2,3},{3,0},{4,5},{5,6},{6,7},{7,4},{8,9},{9,10},{10,1... | collective-permute-start | bytes 786440 | tf_op jit(solution)/shard_map/ppermute | solution.py:1081
  247.3 21.2 %collective-permute-start.33 = (bf16[128,1024]{1,0:T(8,128)(2,1)S(1)}, bf16[128,1024]{1,0:T(8,128)(2,1)S(1)}, u32[]{:S(2)}, u32[]{:S(2)}) collective-permute-start(bf16[128,1024]{1,0:T(8,128)(2,1)S(1)} %get-tuple-element.118), channel_id=1, source_target_pairs={{0,2},{1,3},{2,0},{3,1},{4,6},{5,7},{6,4},{7,5},{8,10},{9,11},{10,... | collective-permute-start | bytes 786440 | tf_op jit(solution)/shard_map/ppermute | solution.py:1081
  251.0 17.5 %collective-permute-start.34 = (bf16[128,1024]{1,0:T(8,128)(2,1)S(1)}, bf16[128,1024]{1,0:T(8,128)(2,1)S(1)}, u32[]{:S(2)}, u32[]{:S(2)}) collective-permute-start(bf16[128,1024]{1,0:T(8,128)(2,1)S(1)} %get-tuple-element.119), channel_id=1, source_target_pairs={{0,3},{1,0},{2,1},{3,2},{4,7},{5,4},{6,5},{7,6},{8,11},{9,8},{10,9... | collective-permute-start | bytes 786440 | tf_op jit(solution)/shard_map/ppermute | solution.py:1081
  271.9 2.7 collective-permute-start.35
  294.6 2.7 collective-permute-start.36
  300.7 2.7 collective-permute-start.37
  317.7 2.7 collective-permute-start.38
  324.6 2.7 collective-permute-start.39
  395.3 27.3 %collective-permute-start.43 = (bf16[512,1024]{1,0:T(8,128)(2,1)}, bf16[512,1024]{1,0:T(8,128)(2,1)S(1)}, u32[]{:S(2)}, u32[]{:S(2)}) collective-permute-start(bf16[512,1024]{1,0:T(8,128)(2,1)} %get-tuple-element.143), channel_id=1, source_target_pairs={{16,0},{17,1},{18,2},{19,3},{20,4},{21,5},{22,6},{23,7},{24,8},{25... | collective-permute-start | bytes 3145736 | tf_op jit(solution)/shard_map/ppermute | solution.py:28
  398.1 33.4 %all-to-all-start = ((bf16[4,128,1024]{2,1,0:T(8,128)(2,1)}), bf16[4,128,1024]{2,1,0:T(8,128)(2,1)S(1)}, u32[]{:S(2)}, u32[]{:S(2)}) async-start(bf16[4,128,1024]{2,1,0:T(8,128)(2,1)} %bitcast.16), calls=%async_computation | async-start | bytes 2097152 | tf_op jit(solution)/shard_map/all_to_all | solution.py:1241
  426.9 4.6 collective-permute-start.44
  454.5 10.6 %collective-permute-start.45 = (bf16[512,1024]{1,0:T(8,128)(2,1)S(1)}, bf16[512,1024]{1,0:T(8,128)(2,1)S(1)}, u32[]{:S(2)}, u32[]{:S(2)}) collective-permute-start(bf16[512,1024]{1,0:T(8,128)(2,1)S(1)} %get-tuple-element.151), channel_id=1, source_target_pairs={{0,4},{4,0},{8,12},{12,8},{1,5},{5,1},{9,13},{13,9},{2,6},{6,2},{1... | collective-permute-start | bytes 3145736 | tf_op jit(solution)/shard_map/ppermute | solution.py:798
  454.6 26.0 %collective-permute-start.48 = (bf16[1024,512]{1,0:T(8,128)(2,1)S(1)}, bf16[1024,512]{1,0:T(8,128)(2,1)S(1)}, u32[]{:S(2)}, u32[]{:S(2)}) collective-permute-start(bf16[1024,512]{1,0:T(8,128)(2,1)S(1)} %get-tuple-element.160), channel_id=1, source_target_pairs={{0,8},{4,12},{8,0},{12,4},{1,9},{5,13},{9,1},{13,5},{2,10},{6,14},... | collective-permute-start | bytes 3145736 | tf_op jit(solution)/shard_map/ppermute | solution.py:798
  469.2 14.8 %collective-permute-start.46 = (bf16[512,1024]{1,0:T(8,128)(2,1)S(1)}, bf16[512,1024]{1,0:T(8,128)(2,1)S(1)}, u32[]{:S(2)}, u32[]{:S(2)}) collective-permute-start(bf16[512,1024]{1,0:T(8,128)(2,1)S(1)} %get-tuple-element.154.refs_2_.refs_3_.refs_5_), channel_id=1, source_target_pairs={{0,4},{4,0},{8,12},{12,8},{1,5},{5,1},{9,13},{13,9},{2,6},{6,2},{1... | collective-permute-start | bytes 3145736 | tf_op jit(solution)/shard_map/ppermute | solution.py:798
  469.3 33.9 %collective-permute-start.47 = (bf16[1024,512]{1,0:T(8,128)(2,1)S(1)}, bf16[1024,512]{1,0:T(8,128)(2,1)S(1)}, u32[]{:S(2)}, u32[]{:S(2)}) collective-permute-start(bf16[1024,512]{1,0:T(8,128)(2,1)S(1)} %get-tuple-element.159), channel_id=1, source_target_pairs={{0,8},{4,12},{8,0},{12,4},{1,9},{5,13},{9,1},{13,5},{2,10},{6,14},... | collective-permute-start | bytes 3145736 | tf_op jit(solution)/shard_map/ppermute | solution.py:798
  470.9 63.2 %collective-permute-start.50 = (bf16[1024,512]{1,0:T(8,128)(2,1)S(1)}, bf16[1024,512]{1,0:T(8,128)(2,1)S(1)}, u32[]{:S(2)}, u32[]{:S(2)}) collective-permute-start(bf16[1024,512]{1,0:T(8,128)(2,1)S(1)} %get-tuple-element.163), channel_id=1, source_target_pairs={{0,8},{4,12},{8,0},{12,4},{1,9},{5,13},{9,1},{13,5},{2,10},{6,14},... | collective-permute-start | bytes 3145736 | tf_op jit(solution)/shard_map/ppermute | solution.py:798
  471.4 101.2 %collective-permute-start.53 = (bf16[1024,512]{1,0:T(8,128)(2,1)}, bf16[1024,512]{1,0:T(8,128)(2,1)S(1)}, u32[]{:S(2)}, u32[]{:S(2)}) collective-permute-start(bf16[1024,512]{1,0:T(8,128)(2,1)} %get-tuple-element.168), channel_id=1, source_target_pairs={{0,8},{4,12},{8,0},{12,4},{1,9},{5,13},{9,1},{13,5},{2,10},{6,14},... | collective-permute-start | bytes 3145736 | tf_op jit(solution)/shard_map/ppermute | solution.py:798
  481.7 26.0 %collective-permute-start.49 = (bf16[1024,512]{1,0:T(8,128)(2,1)S(1)}, bf16[1024,512]{1,0:T(8,128)(2,1)S(1)}, u32[]{:S(2)}, u32[]{:S(2)}) collective-permute-start(bf16[1024,512]{1,0:T(8,128)(2,1)S(1)} %moved.6), channel_id=1, source_target_pairs={{0,3},{1,0},{2,1},{3,2},{4,7},{5,4},{6,5},{7,6},{8,11},{9,8},{10,9... | collective-permute-start | bytes 3145736 | tf_op jit(solution)/shard_map/ppermute | solution.py:803
  508.6 25.5 %collective-permute-start.51 = (bf16[1024,512]{1,0:T(8,128)(2,1)S(1)}, bf16[1024,512]{1,0:T(8,128)(2,1)S(1)}, u32[]{:S(2)}, u32[]{:S(2)}) collective-permute-start(bf16[1024,512]{1,0:T(8,128)(2,1)S(1)} %moved.7.refs_13_), channel_id=1, source_target_pairs={{0,3},{1,0},{2,1},{3,2},{4,7},{5,4},{6,5},{7,6},{8,11},{9,8},{10,9... | collective-permute-start | bytes 3145736 | tf_op jit(solution)/shard_map/ppermute | solution.py:803
  551.8 21.3 %collective-permute-start.52 = (bf16[512,1024]{1,0:T(8,128)(2,1)}, bf16[512,1024]{1,0:T(8,128)(2,1)}, u32[]{:S(2)}, u32[]{:S(2)}) collective-permute-start(bf16[512,1024]{1,0:T(8,128)(2,1)} %get-tuple-element.166), channel_id=1, source_target_pairs={{0,4},{4,0},{8,12},{12,8},{1,5},{5,1},{9,13},{13,9},{2,6},{6,2},{1... | collective-permute-start | bytes 3145736 | tf_op jit(solution)/shard_map/ppermute | solution.py:798
  551.8 26.2 %collective-permute-start.55 = (bf16[1024,512]{1,0:T(8,128)(2,1)}, bf16[1024,512]{1,0:T(8,128)(2,1)S(1)}, u32[]{:S(2)}, u32[]{:S(2)}) collective-permute-start(bf16[1024,512]{1,0:T(8,128)(2,1)} %moved.8.refs_13_), channel_id=1, source_target_pairs={{0,3},{1,0},{2,1},{3,2},{4,7},{5,4},{6,5},{7,6},{8,11},{9,8},{10,9... | collective-permute-start | bytes 3145736 | tf_op jit(solution)/shard_map/ppermute | solution.py:803
  553.5 15.1 %collective-permute-start.54 = (bf16[512,512]{1,0:T(8,128)(2,1)}, bf16[512,512]{1,0:T(8,128)(2,1)}, u32[]{:S(2)}, u32[]{:S(2)}) collective-permute-start(bf16[512,512]{1,0:T(8,128)(2,1)} %get-tuple-element.169), channel_id=1, source_target_pairs={{0,8},{4,12},{8,0},{12,4},{1,9},{5,13},{9,1},{13,5},{2,10},{6,14},... | collective-permute-start | bytes 1572872 | tf_op jit(solution)/shard_map/ppermute | solution.py:798
  560.1 30.4 %collective-permute-start.58 = (bf16[512,512]{1,0:T(8,128)(2,1)}, bf16[512,512]{1,0:T(8,128)(2,1)}, u32[]{:S(2)}, u32[]{:S(2)}) collective-permute-start(bf16[512,512]{1,0:T(8,128)(2,1)} %copy-done.149), channel_id=1, source_target_pairs={{0,8},{4,12},{8,0},{12,4},{1,9},{5,13},{9,1},{13,5},{2,10},{6,14},... | collective-permute-start | bytes 1572872 | tf_op jit(solution)/shard_map/ppermute | solution.py:798
  571.8 18.7 %collective-permute-start.59 = (bf16[512,512]{1,0:T(8,128)(2,1)}, bf16[512,512]{1,0:T(8,128)(2,1)}, u32[]{:S(2)}, u32[]{:S(2)}) collective-permute-start(bf16[512,512]{1,0:T(8,128)(2,1)} %moved.9.refs_6_), channel_id=1, source_target_pairs={{0,3},{1,0},{2,1},{3,2},{4,7},{5,4},{6,5},{7,6},{8,11},{9,8},{10,9... | collective-permute-start | bytes 1572872 | tf_op jit(solution)/shard_map/ppermute | solution.py:803
  572.6 17.9 %collective-permute-start.60 = (bf16[512,512]{1,0:T(8,128)(2,1)}, bf16[512,512]{1,0:T(8,128)(2,1)}, u32[]{:S(2)}, u32[]{:S(2)}) collective-permute-start(bf16[512,512]{1,0:T(8,128)(2,1)} %get-tuple-element.185), channel_id=1, source_target_pairs={{0,8},{4,12},{8,0},{12,4},{1,9},{5,13},{9,1},{13,5},{2,10},{6,14},... | collective-permute-start | bytes 1572872 | tf_op jit(solution)/shard_map/ppermute | solution.py:798
  593.6 11.6 %all-to-all-start.2 = ((f32[16,1,256]{2,1,0:T(1,128)}), f32[16,1,256]{2,1,0:T(1,128)S(1)}, u32[]{:S(2)}, u32[]{:S(2)}) async-start(f32[16,1,256]{2,1,0:T(1,128)} %reshape.152), calls=%async_computation.2 | async-start | bytes 32768 | tf_op jit(solution)/shard_map/all_to_all | solution.py:1339
  605.2 30.7 %all-to-all-start.1 = ((bf16[4,128,1024]{2,1,0:T(8,128)(2,1)}), bf16[4,128,1024]{2,1,0:T(8,128)(2,1)S(1)}, u32[]{:S(2)}, u32[]{:S(2)}) async-start(bf16[4,128,1024]{2,1,0:T(8,128)(2,1)} %bitcast.52), calls=%async_computation.1 | async-start | bytes 2097152 | tf_op jit(solution)/shard_map/all_to_all | solution.py:1315
  610.7 5.0 collective-permute-start.63
  610.9 4.8 collective-permute-start.64
  611.3 24.7 %collective-permute-start.61 = (bf16[512,512]{1,0:T(8,128)(2,1)}, bf16[512,512]{1,0:T(8,128)(2,1)S(1)}, u32[]{:S(2)}, u32[]{:S(2)}) collective-permute-start(bf16[512,512]{1,0:T(8,128)(2,1)} %get-tuple-element.187), channel_id=1, source_target_pairs={{0,8},{4,12},{8,0},{12,4},{1,9},{5,13},{9,1},{13,5},{2,10},{6,14},... | collective-permute-start | bytes 1572872 | tf_op jit(solution)/shard_map/ppermute | solution.py:798
  611.9 27.9 %collective-permute-start.62 = (bf16[512,512]{1,0:T(8,128)(2,1)}, bf16[512,512]{1,0:T(8,128)(2,1)}, u32[]{:S(2)}, u32[]{:S(2)}) collective-permute-start(bf16[512,512]{1,0:T(8,128)(2,1)} %moved.10.refs_1_), channel_id=1, source_target_pairs={{0,3},{1,0},{2,1},{3,2},{4,7},{5,4},{6,5},{7,6},{8,11},{9,8},{10,9... | collective-permute-start | bytes 1572872 | tf_op jit(solution)/shard_map/ppermute | solution.py:803
  635.9 14.2 %collective-permute-start.57 = (bf16[2,128,1024]{2,1,0:T(8,128)(2,1)S(1)}, bf16[2,128,1024]{2,1,0:T(8,128)(2,1)S(1)}, u32[]{:S(2)}, u32[]{:S(2)}) collective-permute-start(bf16[2,128,1024]{2,1,0:T(8,128)(2,1)S(1)} %get-tuple-element.174), channel_id=1, source_target_pairs={{0,4},{4,0},{8,12},{12,8},{1,5},{5,1},{9,13},{13,9},{2,6},{6,2},{1... | collective-permute-start | bytes 1572872 | tf_op jit(solution)/shard_map/ppermute | solution.py:798
  641.3 20.7 %collective-permute-start.65 = (bf16[512,512]{1,0:T(8,128)(2,1)S(1)}, bf16[512,512]{1,0:T(8,128)(2,1)S(1)}, u32[]{:S(2)}, u32[]{:S(2)}) collective-permute-start(bf16[512,512]{1,0:T(8,128)(2,1)S(1)} %moved.11), channel_id=1, source_target_pairs={{0,3},{1,0},{2,1},{3,2},{4,7},{5,4},{6,5},{7,6},{8,11},{9,8},{10,9... | collective-permute-start | bytes 1572872 | tf_op jit(solution)/shard_map/ppermute | solution.py:803
  (169 other events, 2806.3 us)

commit v12 on v8

--- a/solution.py
+++ b/solution.py
@@ -676,6 +676,10 @@
     return pl.CostEstimate(flops=flops, bytes_accessed=size, transcendentals=0)
 
 
+def far(array):
+    return pltpu.with_memory_space_constraint(array, pltpu.HBM)
+
+
 def without(kernel, first, count):
     return lambda *refs: kernel(*refs[:first], *refs[first + count :])
 
@@ -691,7 +695,7 @@
         compiler_params=pltpu.CompilerParams(vmem_limit_bytes=limit),
         cost_estimate=work(flops, (*operands, *shapes)),
         name=name,
-    )(*operands, *waits)
+    )(*operands, *map(far, waits))
 
 
 def whole_block(array):
@@ -714,7 +718,7 @@
         compiler_params=pltpu.CompilerParams(vmem_limit_bytes=KERNEL_VMEM),
         cost_estimate=work(flops, (*operands, *pieces[0], *pieces[1], *shapes)),
         name=name,
-    )(core, *operands, *pieces[0], *pieces[1], *[array for array, _ in blocks], *waits)
+    )(core, *operands, *pieces[0], *pieces[1], *[array for array, _ in blocks], *map(far, waits))
 
 
 def mlp_up_back(rows, slope, pieces, waits):
@@ -734,7 +738,7 @@
         ],
         compiler_params=pltpu.CompilerParams(vmem_limit_bytes=KERNEL_VMEM),
         name="mlp_up_back",
-    )(*rows, slope, *pieces[0], *pieces[1], *waits)
+    )(*rows, *map(far, (slope, *pieces[0], *pieces[1], *waits)))
 
 
 def attend(core, tables, rows, pieces, waits):
@@ -908,7 +912,7 @@
         ],
         compiler_params=pltpu.CompilerParams(vmem_limit_bytes=KERNEL_VMEM),
         name=name,
-    )(section, *arrays, *waits)
+    )(section, *map(far, (*arrays, *waits)))
     return [(first, flip_pairs(second, 2)), (third, flip_pairs(fourth, 2))]
 
 
@@ -926,9 +930,13 @@
     lax.fori_loop(0, own_ref.shape[0] // CHUNK, body, 0)
 
 
-def gate_kernel(up_ref, down_ref, up_out, down_out):
+def gates_kernel(up_ref, down_ref, up_out, down_out):
     up_out[...] = up_ref[...]
     down_out[...] = down_ref[...]
+
+
+def gate_kernel(piece_ref, out_ref):
+    out_ref[...] = piece_ref[...]
 
 
 def mlp_sum_kernel(core_ref, own_ref, other_ref, moved_ref, up_keep, down_keep, up_send, down_send):
@@ -984,7 +992,7 @@
         out_shape=[jax.ShapeDtypeStruct(shape, dtype) for shape, dtype in outs],
         compiler_params=pltpu.CompilerParams(vmem_limit_bytes=ROWS_VMEM),
         name=name,
-    )(core, *operands, *waits)
+    )(core, *operands, *map(far, waits))
 
 
 def last_sum_kernel(core_ref, own_ref, other_ref, moved_ref, keep_ref, send_ref):
@@ -1092,7 +1100,7 @@
     up_other, down_other = [flip_pairs(up_piece, 2)], [flip_pairs(down_piece, 2)]
     outs = tuple((piece.shape, piece.dtype) for piece in (up_piece, down_piece))
     up_piece, down_piece = on_chip(
-        gate_kernel, "gate", outs, up_piece, down_piece, waits=(attn_own[2], attn_other[0])
+        gates_kernel, "gate", outs, up_piece, down_piece, waits=(attn_own[2], attn_other[0])
     )
     up_own, down_own = spread(up_piece), spread(down_piece)
     up_other += [flip_pairs(piece, 2) for piece in up_own[1:]]
@@ -1201,7 +1209,7 @@
 
     section_word = lax.axis_index("section").astype(jnp.int32).reshape(1)
 
-    def mlp_leaves(base):
+    def mlp_leaves(base, waits=()):
         zeros = (*lefts_zero[2], d_up, lefts_zero[3], *d_down)
         ones = (*lefts_one[2], rights_one[2], lefts_one[3], *rights_one[3])
         mlp_sums[base : base + 2] = weight_grads(
@@ -1213,9 +1221,10 @@
             ones,
             (wide_half + unit, unit),
             (2 * unit, 2 * unit),
-        )
-
-    def attn_leaves(base, d_qkv):
+            waits,
+        )
+
+    def attn_leaves(base, d_qkv, waits):
         zeros = (*lefts_zero[0], d_qkv, lefts_zero[1], *d_attn)
         ones = (*lefts_one[0], rights_one[0][base // 2], lefts_one[1], *rights_one[1])
         attn_sums[base : base + 2] = weight_grads(
@@ -1227,12 +1236,13 @@
             ones,
             (wide_half, 512),
             (768, 256),
+            waits,
         )
 
     def moves_on(piece, *moved, waits=()):
         outs = ((piece[1].shape, jnp.bfloat16),)
         (total,) = on_chip(moved_kernel, "moved", outs, *piece, *moved, waits=waits)
-        return passed_on(total, -1)
+        return total, passed_on(total, -1)
 
     mlp_sums, attn_sums = [None] * tensor, [None] * tensor
     mlp_moves, attn_moves = [None] * tensor, [None] * tensor
@@ -1246,35 +1256,28 @@
             mlp_leaves(2)
             return (mlp_sums[3][0],)
         if turn == 1:
-            mlp_leaves(0)
-            return (mlp_sums[1][0],)
+            return ()
         if turn == 2:
             (d_attn,) = new
-            mlp_moves[3] = moves_on(mlp_sums[3], waits=d_attn[:1])
-            return (mlp_sums[3][1],)
+            total, mlp_moves[3] = moves_on(mlp_sums[3], waits=d_attn[:1])
+            mlp_leaves(0, (total,))
+            return (mlp_sums[1][0],)
         if turn == 3:
-            mlp_moves[2] = moves_on(mlp_sums[2], mlp_moves[3], waits=new)
-            attn_leaves(2, new[0])
+            total, mlp_moves[2] = moves_on(mlp_sums[2], mlp_moves[3], waits=new)
+            attn_leaves(2, new[0], (total,))
             return (mlp_sums[2][1], mlp_moves[3], attn_sums[3][0])
         if turn == 4:
-            mlp_moves[1] = moves_on(mlp_sums[1], mlp_moves[2], waits=new)
-            attn_leaves(0, new[0])
-            return (mlp_sums[1][1], mlp_moves[2], attn_sums[1][0])
-        return (mlp_sums[0][1], attn_sums[3][1], attn_sums[2][1])
+            total, mlp_moves[1] = moves_on(mlp_sums[1], mlp_moves[2], waits=new)
+            attn_leaves(0, new[0], (total,))
+            return (attn_sums[1][0],)
+        total, attn_moves[3] = moves_on(attn_sums[3])
+        return (mlp_sums[0][1], total, mlp_moves[1])
 
     d_down = d_up = d_attn = None
     grad_zero, rights_zero, gain_zero = backward(received, saved_zero, hook, (lows,))
-    attn_moves[3] = moves_on(attn_sums[3])
-    attn_moves[2] = moves_on(attn_sums[2], attn_moves[3])
-    attn_moves[1] = moves_on(attn_sums[1], attn_moves[2])
-    gain_total = own_first(jnp.where(first, gain_zero, gain_one))
-    count = tensor * lax.axis_size("dp")
-    gain_parts = gain_total.reshape(4, count, width // count).swapaxes(0, 1)
-    gain_parts = lax.all_to_all(gain_parts, ("dp", "tensor"), 0, 0, tiled=True)
-    gains_grad = jnp.sum(gain_parts, axis=0)
-    outputs = from_chip(lows, (grad_zero, attn_sums[1][1]))
+    outputs = from_chip(lows, (grad_zero,))
     grads = own_first(jnp.where(first, grad_zero, grad_one)).reshape(tensor, part, width)
-    grads = from_chip(lax.all_to_all(grads, "tensor", 0, 0, tiled=True), attn_sums[0][1:])
+    grads = lax.all_to_all(grads, "tensor", 0, 0, tiled=True)
 
     block32 = ((wide_half // 2, unit), jnp.float32)
     down32 = ((unit, wide_half // 2), jnp.float32)
@@ -1294,6 +1297,18 @@
     up_grad, down_grad = with_core(
         mlp_join_kernel, "mlp_join", core_word, outs, up_keep, down_keep, *sent
     )
+    waits = (outputs, attn_sums[1][1])
+    _, attn_moves[2] = moves_on(attn_sums[2], attn_moves[3], waits=waits)
+    waits = (up_grad, grads, attn_sums[0][1])
+    last, attn_moves[1] = moves_on(attn_sums[1], attn_moves[2], waits=waits)
+    grads = from_chip(grads, (last,))
+    gain_total = own_first(jnp.where(first, gain_zero, gain_one))
+    count = tensor * lax.axis_size("dp")
+    gain_parts = gain_total.reshape(4, count, width // count).swapaxes(0, 1)
+    outs = ((gain_parts.shape, gain_parts.dtype),)
+    (gain_parts,) = on_chip(gate_kernel, "gate", outs, gain_parts, waits=(last,))
+    gain_parts = lax.all_to_all(gain_parts, ("dp", "tensor"), 0, 0, tiled=True)
+    gains_grad = jnp.sum(gain_parts, axis=0)
     outs = (((wide_half // 2, 512), jnp.float32),) * 2
     keep, send = with_core(
         last_sum_kernel,
@@ -1302,7 +1317,7 @@
         outs,
         *attn_sums[0],
         attn_moves[1],
-        waits=(outputs, grads, gain_parts, up_grad),
+        waits=(grads, gains_grad),
     )
     spots = tuple((i * 128, (i + 1) * 128, i * 256) for i in range(3))
     outs = (((wide_half // 2, 768), jnp.float32), ((256, wide_half // 2), jnp.float32))

time: 667 us -> 641 us (0.961)
  waiting for transfers between devices: 261 us -> 246 us
  Pallas kernels: 233 us -> 219 us
    ppermute x15, waiting for transfers between devices: 119 us -> 94.9 us  [passed_on(): lax.ppermute(block, 'tensor', [(i, (i + step) % size) for i in range(size)])]
    pallas_call x29 -> x30, Pallas kernels: 94.5 us -> 85.1 us  [on_chip(): pl.pallas_call(without(kernel, len(operands), len(waits)), in_specs=[spac...]
    ppermute x42, waiting for transfers between devices: 99.5 us -> 107 us  [flip_pairs(): return lax.ppermute(block, 'dp', [(i, i ^ distance) for i in range(size)])]
    unnamed x308 -> x276, local copies, waits for them, and re-layouts: 44.2 us -> 49 us
  transfers between devices with their start and end apart: 62 -> 62, of which waited for: 37 -> 35; matrix products, arithmetic and copies ran while one was open for 3% -> 3% of each run, Pallas kernels for 16% -> 15%
where the time goes in v12:
time: 641 us; the launch traced here: 632 us
  waiting for transfers between devices  246 us (38%)
  Pallas kernels  219 us (34%)
  starting transfers between devices  73 us (11%)
  local copies, waits for them, and re-layouts  58.3 us (9%)
  other arithmetic  20.7 us (3%)
  blocking collectives  10.8 us (2%)
    ppermute x42, waiting for transfers between devices, flip_pairs(): return lax.ppermute(block, 'dp', [(i, i ^ distance) for i in range(size)])  107 us
    ppermute x15, waiting for transfers between devices, passed_on(): lax.ppermute(block, 'tensor', [(i, (i + step) % size) for i in range(size)])  94.9 us
    pallas_call x6, Pallas kernels, by_pairs(): pl.pallas_call(without(functools.partial(kernel, len(pieces[0])), taken,...  86.6 us
    pallas_call x30, Pallas kernels, on_chip(): pl.pallas_call(without(kernel, len(operands), len(waits)), in_specs=[spac...  85.1 us
    unnamed x276, local copies, waits for them, and re-layouts  49 us
    ppermute x2, waiting for transfers between devices, shifted(): return lax.ppermute(block, axis, route)  41.5 us
    ppermute x15, starting transfers between devices, passed_on(): lax.ppermute(block, 'tensor', [(i, (i + step) % size) for i in range(size)])  27.5 us
    pallas_call x4, Pallas kernels, weight_grads(): pl.pallas_call(without(functools.partial(kernel, base), 1 + len(arrays),...  26.1 us
  transfers between devices with their start and end apart: 62, of which 35 were waited for; matrix products, arithmetic and copies ran while one was open for 3% of the time, Pallas kernels for 15%

profile of v12, /device:TPU:0, one launch (start us, length us, event | category | flops | bytes accessed | tf_op | source)
XLA Modules:
  0.0 631.6 jit_solution(3664328047136458504)
XLA Ops:
  11.4 6.2 all-to-all-start
  27.8 22.6 %collective-permute-done.1.refs_6_.refs_2_.refs_3_ = bf16[512,512]{1,0:T(8,128)(2,1)} collective-permute-done((bf16[512,512]{1,0:T(8,128)(2,1)}, bf16[512,512]{1,0:T(8,128)(2,1)}, u32[]{:S(2)}, u32[]{:S(2)}) %collective-permute-start.1) | collective-permute-done | bytes 524320 | tf_op jit(solution)/shard_map/ppermute | solution.py:803
  50.4 3.3 collective-permute-start.2
  58.5 7.0 %collective-permute-done.2.refs_2_.refs_7_.refs_3_.refs_5_.refs_4_ = bf16[512,512]{1,0:T(8,128)(2,1)} collective-permute-done((bf16[512,512]{1,0:T(8,128)(2,1)}, bf16[512,512]{1,0:T(8,128)(2,1)}, u32[]{:S(2)}, u32[]{:S(2)}) %collective-permute-start.2) | collective-permute-done | bytes 524320 | tf_op jit(solution)/shard_map/ppermute | solution.py:803
  69.5 10.4 %collective-permute-done.5.refs_4_.refs_5_.refs_7_ = bf16[512,512]{1,0:T(8,128)(2,1)S(1)} collective-permute-done((bf16[512,512]{1,0:T(8,128)(2,1)S(1)}, bf16[512,512]{1,0:T(8,128)(2,1)S(1)}, u32[]{:S(2)}, u32[]{:S(2)}) %collective-permute-start.5) | collective-permute-done | bytes 524320 | tf_op jit(solution)/shard_map/ppermute | solution.py:798
  82.6 2.5 collective-permute-start.11
  85.2 3.7 collective-permute-done.8.refs_10_.refs_6_.refs_8_.refs_7_
  93.8 5.6 collective-permute-done.11.refs_13_.refs_3_.refs_2_
  100.0 4.0 collective-permute-done.9.refs_11_.refs_7_.refs_8_
  105.5 5.1 collective-permute-done.12.refs_14_.refs_2_.refs_4_
  111.3 4.0 collective-permute-done.10.refs_12_.refs_8_.refs_9_
  119.0 16.8 %attend.2 = (bf16[4,1024,128]{2,1,0:T(8,128)(2,1)S(1)}, bf16[4,1024,128]{2,1,0:T(8,128)(2,1)S(1)}, bf16[4,1024,128]{2,1,0:T(8,128)(2,1)S(1)}, f32[4,2,1024]{2,1,0:T(2,128)S(1)}, bf16[1024,512]{1,0:T(8,128)(2,1)S(1)}) custom-call(s32[1]{0:T(128)} %bitcast.refs_0_, f32[1024,128]{1,0:T(8,128)S(1)} %get-tuple-element.230.refs_1_, ...), custom_call_target="tpu_custom_call" | custom-call | flops 11811160064 | bytes 11567104 | tf_op jit(solution)/shard_map/attend/pallas_call | solution.py:708
  140.1 3.1 attn_out.2
  143.3 2.5 collective-permute-start.18
  148.3 11.8 %collective-permute-done.18.refs_4_.refs_5_ = bf16[512,512]{1,0:T(8,128)(2,1)S(1)} collective-permute-done((bf16[512,512]{1,0:T(8,128)(2,1)}, bf16[512,512]{1,0:T(8,128)(2,1)S(1)}, u32[]{:S(2)}, u32[]{:S(2)}) %collective-permute-start.18) | collective-permute-done | bytes 524320 | tf_op jit(solution)/shard_map/ppermute | solution.py:803
  160.1 10.8 %collective-permute-done.19.refs_5_.refs_4_.refs_6_ = bf16[512,512]{1,0:T(8,128)(2,1)S(1)} collective-permute-done((bf16[512,512]{1,0:T(8,128)(2,1)}, bf16[512,512]{1,0:T(8,128)(2,1)S(1)}, u32[]{:S(2)}, u32[]{:S(2)}) %collective-permute-start.19) | collective-permute-done | bytes 524320 | tf_op jit(solution)/shard_map/ppermute | solution.py:803
  172.3 3.4 after_attn.2
  179.3 12.9 %collective-permute-done.23.refs_9_.refs_8_ = bf16[512,512]{1,0:T(8,128)(2,1)S(1)} collective-permute-done((bf16[512,512]{1,0:T(8,128)(2,1)}, bf16[512,512]{1,0:T(8,128)(2,1)S(1)}, u32[]{:S(2)}, u32[]{:S(2)}) %collective-permute-start.23) | collective-permute-done | bytes 524320 | tf_op jit(solution)/shard_map/ppermute | solution.py:798
  194.5 7.7 %mlp_up.2 = (bf16[1024,2048]{1,0:T(8,128)(2,1)S(1)}, bf16[1024,2048]{1,0:T(8,128)(2,1)S(1)}) custom-call(bf16[512,1024]{1,0:T(8,128)(2,1)S(1)} %get-tuple-element.103.refs_0_.refs_1_, bf16[512,1024]{1,0:T(8,128)(2,1)S(1)} %collective-permute-done.22.refs_1_.refs_2_, bf16[512,512]{1,0:T(8,128)(2,1)S(1)} %copy-done.110, bf16[512,512]{1,0:T(8,128)(2,1)S(1)} %copy-done.121, ...), custom_call_target="tpu_custom_call" | custom-call | flops 4294967296 | bytes 14680064 | tf_op jit(solution)/shard_map/mlp_up/pallas_call | solution.py:690
  204.3 4.5 mlp_down.2
  208.9 2.6 collective-permute-done.25.refs_3_
  213.4 3.6 collective-permute-start.26
  217.0 22.2 %collective-permute-done.26.refs_1_ = bf16[512,1024]{1,0:T(8,128)(2,1)S(1)} collective-permute-done((bf16[512,1024]{1,0:T(8,128)(2,1)S(1)}, bf16[512,1024]{1,0:T(8,128)(2,1)S(1)}, u32[]{:S(2)}, u32[]{:S(2)}) %collective-permute-start.26) | collective-permute-done | bytes 1048608 | tf_op jit(solution)/shard_map/ppermute | solution.py:28
  241.1 2.6 collective-permute-done.27.refs_4_.refs_8_
  243.7 17.1 %attend.3 = (bf16[4,1024,128]{2,1,0:T(8,128)(2,1)S(1)}, bf16[4,1024,128]{2,1,0:T(8,128)(2,1)S(1)}, bf16[4,1024,128]{2,1,0:T(8,128)(2,1)S(1)}, f32[4,2,1024]{2,1,0:T(2,128)S(1)}, bf16[1024,512]{1,0:T(8,128)(2,1)S(1)}) custom-call(s32[1]{0:T(128)} %bitcast.refs_0_, f32[1024,128]{1,0:T(8,128)S(1)} %get-tuple-element.230.refs_1_, ...), custom_call_target="tpu_custom_call" | custom-call | flops 11811160064 | bytes 11567104 | tf_op jit(solution)/shard_map/attend/pallas_call | solution.py:708
  260.8 3.5 attn_out.3
  264.6 2.5 collective-permute-done.28.refs_3_
  267.1 3.4 after_attn.3
  270.7 2.5 collective-permute-done.29.refs_1_.refs_8_
  273.2 7.7 %mlp_up.3 = (bf16[1024,2048]{1,0:T(8,128)(2,1)S(1)}, bf16[1024,2048]{1,0:T(8,128)(2,1)S(1)}) custom-call(bf16[512,1024]{1,0:T(8,128)(2,1)S(1)} %get-tuple-element.112.refs_0_.refs_7_, bf16[512,1024]{1,0:T(8,128)(2,1)S(1)} %collective-permute-done.29.refs_1_.refs_8_, bf16[512,512]{1,0:T(8,128)(2,1)S(1)} %copy-done.110, bf16[512,512]{1,0:T(8,128)(2,1)S(1)} %copy-done.121, ...), custom_call_target="tpu_custom_call" | custom-call | flops 4294967296 | bytes 14680064 | tf_op jit(solution)/shard_map/mlp_up/pallas_call | solution.py:690
  282.9 4.5 mlp_down.3
  297.1 7.2 %mlp_up_back.2.refs_0_.refs_9_ = bf16[1024,2048]{1,0:T(8,128)(2,1)S(1)} custom-call(bf16[512,1024]{1,0:T(8,128)(2,1)S(1)} %get-tuple-element.118.refs_0_.refs_11_, bf16[512,1024]{1,0:T(8,128)(2,1)S(1)} %collective-permute-done.31.refs_1_.refs_12_, bf16[1024,2048]{1,0:T(8,128)(2,1)} %copy-done.34, bf16[512,512]{1,0:T(8,128)(2,1)} %copy-done.62, ...), custom_call_target="tpu_custom_call" | custom-call | tf_op jit(solution)/shard_map/mlp_up_back/pallas_call | solution.py:729
  304.3 4.5 mlp_back.2
  311.5 3.9 into_attn_back.2
  315.7 2.5 collective-permute-done.33.refs_4_.refs_12_
  318.2 13.1 %attend_back.4.refs_0_.refs_9_ = bf16[1024,768]{1,0:T(8,128)(2,1)S(1)} custom-call(s32[1]{0:T(128)} %bitcast.refs_0_, f32[1024,128]{1,0:T(8,128)S(1)} %get-tuple-element.230.refs_1_, f32[1024,128]{1,0:T(8,128)S(1)} %get-tuple-element.231.refs_2_, bf16[512,1024]{1,0:T(8,128)(2,1)S(1)} %get-tuple-element.123.refs_3_.refs_11_, ...), custom_call_target="tpu_custom_call" | custom-call | flops 11274289152 | bytes 6815744 | tf_op jit(solution)/shard_map/attend_back/pallas_call | solution.py:708
  331.4 13.0 %attend_back.5.refs_1_.refs_9_ = bf16[1024,768]{1,0:T(8,128)(2,1)S(1)} custom-call(s32[1]{0:T(128)} %bitcast.refs_0_, f32[1024,128]{1,0:T(8,128)S(1)} %get-tuple-element.230.refs_1_, f32[1024,128]{1,0:T(8,128)S(1)} %get-tuple-element.231.refs_2_, bf16[512,1024]{1,0:T(8,128)(2,1)S(1)} %get-tuple-element.123.refs_3_.refs_11_, ...), custom_call_target="tpu_custom_call" | custom-call | flops 11274289152 | bytes 6815744 | tf_op jit(solution)/shard_map/attend_back/pallas_call | solution.py:708
  346.0 5.8 attn_back.2
  353.6 2.5 collective-permute-done.34.refs_3_
  361.1 5.2 all-to-all-start.1
  366.3 19.2 %collective-permute-done.35.refs_1_ = bf16[512,1024]{1,0:T(8,128)(2,1)S(1)} collective-permute-done((bf16[512,1024]{1,0:T(8,128)(2,1)S(1)}, bf16[512,1024]{1,0:T(8,128)(2,1)S(1)}, u32[]{:S(2)}, u32[]{:S(2)}) %collective-permute-start.35) | collective-permute-done | bytes 1048608 | tf_op jit(solution)/shard_map/ppermute | solution.py:28
  389.7 2.7 all-to-all-done.1.refs_11_.refs_1_
  392.4 7.2 %mlp_up_back.3.refs_3_.refs_0_ = bf16[1024,2048]{1,0:T(8,128)(2,1)S(1)} custom-call(bf16[512,1024]{1,0:T(8,128)(2,1)S(1)} %get-tuple-element.135.refs_0_.refs_5_, bf16[512,1024]{1,0:T(8,128)(2,1)S(1)} %collective-permute-done.36.refs_1_.refs_6_, bf16[1024,2048]{1,0:T(8,128)(2,1)} %copy-done.55, bf16[512,512]{1,0:T(8,128)(2,1)} %copy-done.62, ...), custom_call_target="tpu_custom_call" | custom-call | tf_op jit(solution)/shard_map/mlp_up_back/pallas_call | solution.py:729
  401.7 7.2 %mlp_grads.2 = (f32[1024,512]{1,0:T(8,128)S(1)}, bf16[1024,512]{1,0:T(8,128)(2,1)S(1)}, f32[1024,512]{1,0:T(8,128)S(1)}, bf16[1024,512]{1,0:T(8,128)(2,1)S(1)}) custom-call(s32[1]{0:T(128)} %bitcast.12.refs_0_, bf16[512,1024]{1,0:T(8,128)(2,1)} %copy-done.38, bf16[512,1024]{1,0:T(8,128)(2,1)} %copy-done.39, bf16[1024,2048]{1,0:T(8,128)(2,1)} %copy-done.3, ...), custom_call_target="tpu_custom_call" | custom-call | tf_op jit(solution)/shard_map/mlp_grads/pallas_call | solution.py:897
  410.3 4.5 mlp_back.3
  417.6 4.9 into_attn_back.3
  423.1 17.8 %collective-permute-done.40.refs_1_ = bf16[1024,512]{1,0:T(8,128)(2,1)S(1)} collective-permute-done((bf16[1024,512]{1,0:T(8,128)(2,1)S(1)}, bf16[1024,512]{1,0:T(8,128)(2,1)S(1)}, u32[]{:S(2)}, u32[]{:S(2)}) %collective-permute-start.40) | collective-permute-done | bytes 1048608 | tf_op jit(solution)/shard_map/ppermute | solution.py:798
  441.4 3.7 collective-permute-start.41
  445.1 7.0 %mlp_grads.3 = (f32[1024,512]{1,0:T(8,128)S(1)}, bf16[1024,512]{1,0:T(8,128)(2,1)S(1)}, f32[1024,512]{1,0:T(8,128)S(1)}, bf16[1024,512]{1,0:T(8,128)(2,1)S(1)}) custom-call(s32[1]{0:T(128)} %bitcast.12.refs_0_, bf16[512,1024]{1,0:T(8,128)(2,1)} %copy-done.38, bf16[512,1024]{1,0:T(8,128)(2,1)} %copy-done.39, bf16[1024,2048]{1,0:T(8,128)(2,1)} %copy-done.3, ...), custom_call_target="tpu_custom_call" | custom-call | tf_op jit(solution)/shard_map/mlp_grads/pallas_call | solution.py:897
  457.0 13.1 %attend_back.6.refs_3_.refs_1_ = bf16[1024,768]{1,0:T(8,128)(2,1)S(1)} custom-call(s32[1]{0:T(128)} %bitcast.refs_0_, f32[1024,128]{1,0:T(8,128)S(1)} %copy-done.103, f32[1024,128]{1,0:T(8,128)S(1)} %copy-done.105, bf16[512,1024]{1,0:T(8,128)(2,1)} %get-tuple-element.141.refs_2_.refs_3_.refs_5_, ...), custom_call_target="tpu_custom_call" | custom-call | flops 11274289152 | bytes 6815744 | tf_op jit(solution)/shard_map/attend_back/pallas_call | solution.py:708
  474.1 5.9 attn_grads.2
  482.0 13.6 %attend_back.7.refs_3_.refs_0_ = bf16[1024,768]{1,0:T(8,128)(2,1)S(1)} custom-call(s32[1]{0:T(128)} %bitcast.refs_0_, f32[1024,128]{1,0:T(8,128)S(1)} %copy-done.103, f32[1024,128]{1,0:T(8,128)S(1)} %copy-done.105, bf16[512,1024]{1,0:T(8,128)(2,1)} %get-tuple-element.141.refs_2_.refs_3_.refs_5_, bf16[512,1024]{1,0:T(8,128)(2,1)S(1)} %copy-done.47, ...), custom_call_target="tpu_custom_call" | custom-call | flops 11274289152 | bytes 6815744 | tf_op jit(solution)/shard_map/attend_back/pallas_call | solution.py:708
  498.4 6.0 attn_grads.3
  508.0 5.4 attn_back.3
  513.5 2.6 collective-permute-start.47
  516.6 13.5 %collective-permute-done.46.refs_1_ = bf16[512,512]{1,0:T(8,128)(2,1)S(1)} collective-permute-done((bf16[512,512]{1,0:T(8,128)(2,1)S(1)}, bf16[512,512]{1,0:T(8,128)(2,1)S(1)}, u32[]{:S(2)}, u32[]{:S(2)}) %collective-permute-start.46) | collective-permute-done | bytes 524320 | tf_op jit(solution)/shard_map/ppermute | solution.py:798
  531.1 8.0 %collective-permute-done.47.refs_7_.refs_3_ = bf16[1024,512]{1,0:T(8,128)(2,1)S(1)} collective-permute-done((bf16[1024,512]{1,0:T(8,128)(2,1)S(1)}, bf16[1024,512]{1,0:T(8,128)(2,1)S(1)}, u32[]{:S(2)}, u32[]{:S(2)}) %collective-permute-start.47) | collective-permute-done | bytes 1048608 | tf_op jit(solution)/shard_map/ppermute | solution.py:803
  544.6 5.7 all-to-all-start.2
  552.3 3.8 collective-permute-start.51
  559.9 6.8 %collective-permute-done.50.refs_1_ = bf16[512,512]{1,0:T(8,128)(2,1)S(1)} collective-permute-done((bf16[512,512]{1,0:T(8,128)(2,1)}, bf16[512,512]{1,0:T(8,128)(2,1)S(1)}, u32[]{:S(2)}, u32[]{:S(2)}) %collective-permute-start.50) | collective-permute-done | bytes 524320 | tf_op jit(solution)/shard_map/ppermute | solution.py:798
  566.8 13.7 %collective-permute-done.51.refs_2_ = bf16[512,512]{1,0:T(8,128)(2,1)S(1)} collective-permute-done((bf16[512,512]{1,0:T(8,128)(2,1)}, bf16[512,512]{1,0:T(8,128)(2,1)S(1)}, u32[]{:S(2)}, u32[]{:S(2)}) %collective-permute-start.51) | collective-permute-done | bytes 524320 | tf_op jit(solution)/shard_map/ppermute | solution.py:803
  585.3 3.5 collective-permute-done.55.refs_5_.refs_2_
  589.6 10.3 %collective-permute-done.52.refs_2_ = bf16[512,512]{1,0:T(8,128)(2,1)S(1)} collective-permute-done((bf16[512,512]{1,0:T(8,128)(2,1)S(1)}, bf16[512,512]{1,0:T(8,128)(2,1)S(1)}, u32[]{:S(2)}, u32[]{:S(2)}) %collective-permute-start.52) | collective-permute-done | bytes 524320 | tf_op jit(solution)/shard_map/ppermute | solution.py:803
  611.0 10.8 %all_to_all.20 = f32[16,1,256]{2,1,0:T(1,128)S(1)} all-to-all(f32[16,1,256]{2,1,0:T(1,128)S(1)} %reshape.144), channel_id=1, replica_groups=mesh['section'=2,'dp'=4,'tensor'=4] {'dp','tensor'}, dimensions={0} | all-to-all | bytes 32768 | tf_op jit(solution)/shard_map/all_to_all | solution.py:1310
  (443 shorter events, 153.9 us)
Async XLA Ops:
  7.2 2.1 collective-permute-start
  11.4 68.5 %all-to-all-start = ((bf16[4,128,1024]{2,1,0:T(8,128)(2,1)}), bf16[4,128,1024]{2,1,0:T(8,128)(2,1)S(1)}, u32[]{:S(2)}, u32[]{:S(2)}) async-start(bf16[4,128,1024]{2,1,0:T(8,128)(2,1)} %pad_maximum_fusion), calls=%async_computation | async-start | bytes 2097152 | tf_op jit(solution)/shard_map/all_to_all | solution.py:1059
  24.2 26.2 %collective-permute-start.1 = (bf16[512,512]{1,0:T(8,128)(2,1)}, bf16[512,512]{1,0:T(8,128)(2,1)}, u32[]{:S(2)}, u32[]{:S(2)}) collective-permute-start(bf16[512,512]{1,0:T(8,128)(2,1)} %pad_maximum_fusion.3.refs_5_.refs_1_.refs_2_), channel_id=1, source_target_pairs={{0,1},{1,2},{2,3},{3,0},{4,5},{5,6},{6,7},{7,4},{8,9},{9,10},{10,1... | collective-permute-start | bytes 1572872 | tf_op jit(solution)/shard_map/ppermute | solution.py:803
  26.3 40.6 %collective-permute-start.3 = (bf16[512,512]{1,0:T(8,128)(2,1)}, bf16[512,512]{1,0:T(8,128)(2,1)}, u32[]{:S(2)}, u32[]{:S(2)}) collective-permute-start(bf16[512,512]{1,0:T(8,128)(2,1)} %pad_maximum_fusion.3.refs_5_.refs_1_.refs_2_), channel_id=1, source_target_pairs={{0,8},{4,12},{8,0},{12,4},{1,9},{5,13},{9,1},{13,5},{2,10},{6,14},... | collective-permute-start | bytes 1572872 | tf_op jit(solution)/shard_map/ppermute | solution.py:798
  50.4 15.0 %collective-permute-start.2 = (bf16[512,512]{1,0:T(8,128)(2,1)}, bf16[512,512]{1,0:T(8,128)(2,1)}, u32[]{:S(2)}, u32[]{:S(2)}) collective-permute-start(bf16[512,512]{1,0:T(8,128)(2,1)} %collective-permute-done.1.refs_6_.refs_2_.refs_3_), channel_id=1, source_target_pairs={{0,1},{1,2},{2,3},{3,0},{4,5},{5,6},{6,7},{7,4},{8,9},{9,10},{10,1... | collective-permute-start | bytes 1572872 | tf_op jit(solution)/shard_map/ppermute | solution.py:803
  53.7 14.9 %collective-permute-start.4 = (bf16[512,512]{1,0:T(8,128)(2,1)S(1)}, bf16[512,512]{1,0:T(8,128)(2,1)S(1)}, u32[]{:S(2)}, u32[]{:S(2)}) collective-permute-start(bf16[512,512]{1,0:T(8,128)(2,1)S(1)} %dynamic-slice_bitcast_fusion.1.refs_0_), channel_id=1, source_target_pairs={{0,8},{4,12},{8,0},{12,4},{1,9},{5,13},{9,1},{13,5},{2,10},{6,14},... | collective-permute-start | bytes 1572872 | tf_op jit(solution)/shard_map/ppermute | solution.py:798
  56.4 23.5 %collective-permute-start.5 = (bf16[512,512]{1,0:T(8,128)(2,1)S(1)}, bf16[512,512]{1,0:T(8,128)(2,1)S(1)}, u32[]{:S(2)}, u32[]{:S(2)}) collective-permute-start(bf16[512,512]{1,0:T(8,128)(2,1)S(1)} %dynamic-slice_bitcast_fusion.refs_1_), channel_id=1, source_target_pairs={{0,8},{4,12},{8,0},{12,4},{1,9},{5,13},{9,1},{13,5},{2,10},{6,14},... | collective-permute-start | bytes 1572872 | tf_op jit(solution)/shard_map/ppermute | solution.py:798
  57.0 31.9 %collective-permute-start.8 = (bf16[512,512]{1,0:T(8,128)(2,1)}, bf16[512,512]{1,0:T(8,128)(2,1)}, u32[]{:S(2)}, u32[]{:S(2)}) collective-permute-start(bf16[512,512]{1,0:T(8,128)(2,1)} %collective-permute-done.1.refs_6_.refs_2_.refs_3_), channel_id=1, source_target_pairs={{0,8},{4,12},{8,0},{12,4},{1,9},{5,13},{9,1},{13,5},{2,10},{6,14},... | collective-permute-start | bytes 1572872 | tf_op jit(solution)/shard_map/ppermute | solution.py:798
  65.5 25.0 %collective-permute-start.7 = (bf16[512,512]{1,0:T(8,128)(2,1)}, bf16[512,512]{1,0:T(8,128)(2,1)}, u32[]{:S(2)}, u32[]{:S(2)}) collective-permute-start(bf16[512,512]{1,0:T(8,128)(2,1)} %collective-permute-done.2.refs_2_.refs_7_.refs_3_.refs_5_.refs_4_), channel_id=1, source_target_pairs={{0,1},{1,2},{2,3},{3,0},{4,5},{5,6},{6,7},{7,4},{8,9},{9,10},{10,1... | collective-permute-start | bytes 1572872 | tf_op jit(solution)/shard_map/ppermute | solution.py:803
  82.5 34.3 %collective-permute-start.6 = (bf16[512,1024]{1,0:T(8,128)(2,1)S(1)}, bf16[512,1024]{1,0:T(8,128)(2,1)S(1)}, u32[]{:S(2)}, u32[]{:S(2)}) collective-permute-start(bf16[512,1024]{1,0:T(8,128)(2,1)S(1)} %norm_in.2.refs_3_.refs_1_), channel_id=1, source_target_pairs={{0,4},{4,0},{8,12},{12,8},{1,5},{5,1},{9,13},{13,9},{2,6},{6,2},{1... | collective-permute-start | bytes 3145736 | tf_op jit(solution)/shard_map/ppermute | solution.py:798
  82.6 16.8 %collective-permute-start.11 = (bf16[512,512]{1,0:T(8,128)(2,1)}, bf16[512,512]{1,0:T(8,128)(2,1)S(1)}, u32[]{:S(2)}, u32[]{:S(2)}) collective-permute-start(bf16[512,512]{1,0:T(8,128)(2,1)} %copy-done.109), channel_id=1, source_target_pairs={{0,1},{1,2},{2,3},{3,0},{4,5},{5,6},{6,7},{7,4},{8,9},{9,10},{10,1... | collective-permute-start | bytes 1572872 | tf_op jit(solution)/shard_map/ppermute | solution.py:803
  85.1 25.5 %collective-permute-start.12 = (bf16[512,512]{1,0:T(8,128)(2,1)}, bf16[512,512]{1,0:T(8,128)(2,1)S(1)}, u32[]{:S(2)}, u32[]{:S(2)}) collective-permute-start(bf16[512,512]{1,0:T(8,128)(2,1)} %copy-done.62), channel_id=1, source_target_pairs={{0,1},{1,2},{2,3},{3,0},{4,5},{5,6},{6,7},{7,4},{8,9},{9,10},{10,1... | collective-permute-start | bytes 1572872 | tf_op jit(solution)/shard_map/ppermute | solution.py:803
  88.9 15.1 %collective-permute-start.9 = (bf16[512,512]{1,0:T(8,128)(2,1)}, bf16[512,512]{1,0:T(8,128)(2,1)S(1)}, u32[]{:S(2)}, u32[]{:S(2)}) collective-permute-start(bf16[512,512]{1,0:T(8,128)(2,1)} %collective-permute-done.2.refs_2_.refs_7_.refs_3_.refs_5_.refs_4_), channel_id=1, source_target_pairs={{0,8},{4,12},{8,0},{12,4},{1,9},{5,13},{9,1},{13,5},{2,10},{6,14},... | collective-permute-start | bytes 1572872 | tf_op jit(solution)/shard_map/ppermute | solution.py:798
  90.4 24.8 %collective-permute-start.10 = (bf16[512,512]{1,0:T(8,128)(2,1)}, bf16[512,512]{1,0:T(8,128)(2,1)S(1)}, u32[]{:S(2)}, u32[]{:S(2)}) collective-permute-start(bf16[512,512]{1,0:T(8,128)(2,1)} %collective-permute-done.7.refs_8_.refs_4_.refs_6_.refs_5_), channel_id=1, source_target_pairs={{0,8},{4,12},{8,0},{12,4},{1,9},{5,13},{9,1},{13,5},{2,10},{6,14},... | collective-permute-start | bytes 1572872 | tf_op jit(solution)/shard_map/ppermute | solution.py:798
  99.4 39.3 %collective-permute-start.13 = (bf16[512,512]{1,0:T(8,128)(2,1)S(1)}, bf16[512,512]{1,0:T(8,128)(2,1)S(1)}, u32[]{:S(2)}, u32[]{:S(2)}) collective-permute-start(bf16[512,512]{1,0:T(8,128)(2,1)S(1)} %collective-permute-done.11.refs_13_.refs_3_.refs_2_), channel_id=1, source_target_pairs={{0,1},{1,2},{2,3},{3,0},{4,5},{5,6},{6,7},{7,4},{8,9},{9,10},{10,1... | collective-permute-start | bytes 1572872 | tf_op jit(solution)/shard_map/ppermute | solution.py:803
  104.0 34.7 %collective-permute-start.15 = (bf16[512,512]{1,0:T(8,128)(2,1)S(1)}, bf16[512,512]{1,0:T(8,128)(2,1)S(1)}, u32[]{:S(2)}, u32[]{:S(2)}) collective-permute-start(bf16[512,512]{1,0:T(8,128)(2,1)S(1)} %collective-permute-done.11.refs_13_.refs_3_.refs_2_), channel_id=1, source_target_pairs={{0,8},{4,12},{8,0},{12,4},{1,9},{5,13},{9,1},{13,5},{2,10},{6,14},... | collective-permute-start | bytes 1572872 | tf_op jit(solution)/shard_map/ppermute | solution.py:798
  110.6 28.1 %collective-permute-start.14 = (bf16[512,512]{1,0:T(8,128)(2,1)S(1)}, bf16[512,512]{1,0:T(8,128)(2,1)S(1)}, u32[]{:S(2)}, u32[]{:S(2)}) collective-permute-start(bf16[512,512]{1,0:T(8,128)(2,1)S(1)} %collective-permute-done.12.refs_14_.refs_2_.refs_4_), channel_id=1, source_target_pairs={{0,1},{1,2},{2,3},{3,0},{4,5},{5,6},{6,7},{7,4},{8,9},{9,10},{10,1... | collective-permute-start | bytes 1572872 | tf_op jit(solution)/shard_map/ppermute | solution.py:803
  115.2 23.5 %collective-permute-start.16 = (bf16[512,512]{1,0:T(8,128)(2,1)S(1)}, bf16[512,512]{1,0:T(8,128)(2,1)S(1)}, u32[]{:S(2)}, u32[]{:S(2)}) collective-permute-start(bf16[512,512]{1,0:T(8,128)(2,1)S(1)} %collective-permute-done.12.refs_14_.refs_2_.refs_4_), channel_id=1, source_target_pairs={{0,8},{4,12},{8,0},{12,4},{1,9},{5,13},{9,1},{13,5},{2,10},{6,14},... | collective-permute-start | bytes 1572872 | tf_op jit(solution)/shard_map/ppermute | solution.py:798
  143.2 28.3 %collective-permute-start.17 = (bf16[512,1024]{1,0:T(8,128)(2,1)S(1)}, bf16[512,1024]{1,0:T(8,128)(2,1)S(1)}, u32[]{:S(2)}, u32[]{:S(2)}) collective-permute-start(bf16[512,1024]{1,0:T(8,128)(2,1)S(1)} %get-tuple-element.101), channel_id=1, source_target_pairs={{0,4},{4,0},{8,12},{12,8},{1,5},{5,1},{9,13},{13,9},{2,6},{6,2},{1... | collective-permute-start | bytes 3145736 | tf_op jit(solution)/shard_map/ppermute | solution.py:798
  143.3 16.8 %collective-permute-start.18 = (bf16[512,512]{1,0:T(8,128)(2,1)}, bf16[512,512]{1,0:T(8,128)(2,1)S(1)}, u32[]{:S(2)}, u32[]{:S(2)}) collective-permute-start(bf16[512,512]{1,0:T(8,128)(2,1)} %copy-done.96), channel_id=1, source_target_pairs={{0,1},{1,2},{2,3},{3,0},{4,5},{5,6},{6,7},{7,4},{8,9},{9,10},{10,1... | collective-permute-start | bytes 1572872 | tf_op jit(solution)/shard_map/ppermute | solution.py:803
  145.8 25.0 %collective-permute-start.19 = (bf16[512,512]{1,0:T(8,128)(2,1)}, bf16[512,512]{1,0:T(8,128)(2,1)S(1)}, u32[]{:S(2)}, u32[]{:S(2)}) collective-permute-start(bf16[512,512]{1,0:T(8,128)(2,1)} %copy-done.23), channel_id=1, source_target_pairs={{0,1},{1,2},{2,3},{3,0},{4,5},{5,6},{6,7},{7,4},{8,9},{9,10},{10,1... | collective-permute-start | bytes 1572872 | tf_op jit(solution)/shard_map/ppermute | solution.py:803
  146.3 24.6 %collective-permute-start.20 = (bf16[512,512]{1,0:T(8,128)(2,1)}, bf16[512,512]{1,0:T(8,128)(2,1)S(1)}, u32[]{:S(2)}, u32[]{:S(2)}) collective-permute-start(bf16[512,512]{1,0:T(8,128)(2,1)} %copy-done.96), channel_id=1, source_target_pairs={{0,8},{4,12},{8,0},{12,4},{1,9},{5,13},{9,1},{13,5},{2,10},{6,14},... | collective-permute-start | bytes 1572872 | tf_op jit(solution)/shard_map/ppermute | solution.py:798
  146.8 24.7 %collective-permute-start.21 = (bf16[512,512]{1,0:T(8,128)(2,1)}, bf16[512,512]{1,0:T(8,128)(2,1)S(1)}, u32[]{:S(2)}, u32[]{:S(2)}) collective-permute-start(bf16[512,512]{1,0:T(8,128)(2,1)} %copy-done.23), channel_id=1, source_target_pairs={{0,8},{4,12},{8,0},{12,4},{1,9},{5,13},{9,1},{13,5},{2,10},{6,14},... | collective-permute-start | bytes 1572872 | tf_op jit(solution)/shard_map/ppermute | solution.py:798
  177.2 15.1 %collective-permute-start.22 = (bf16[512,1024]{1,0:T(8,128)(2,1)S(1)}, bf16[512,1024]{1,0:T(8,128)(2,1)S(1)}, u32[]{:S(2)}, u32[]{:S(2)}) collective-permute-start(bf16[512,1024]{1,0:T(8,128)(2,1)S(1)} %get-tuple-element.103.refs_0_.refs_1_), channel_id=1, source_target_pairs={{0,4},{4,0},{8,12},{12,8},{1,5},{5,1},{9,13},{13,9},{2,6},{6,2},{1... | collective-permute-start | bytes 3145736 | tf_op jit(solution)/shard_map/ppermute | solution.py:798
  177.2 15.0 %collective-permute-start.23 = (bf16[512,512]{1,0:T(8,128)(2,1)}, bf16[512,512]{1,0:T(8,128)(2,1)S(1)}, u32[]{:S(2)}, u32[]{:S(2)}) collective-permute-start(bf16[512,512]{1,0:T(8,128)(2,1)} %copy-done.112), channel_id=1, source_target_pairs={{0,8},{4,12},{8,0},{12,4},{1,9},{5,13},{9,1},{13,5},{2,10},{6,14},... | collective-permute-start | bytes 1572872 | tf_op jit(solution)/shard_map/ppermute | solution.py:798
  177.8 26.4 %collective-permute-start.24 = (bf16[512,512]{1,0:T(8,128)(2,1)}, bf16[512,512]{1,0:T(8,128)(2,1)S(1)}, u32[]{:S(2)}, u32[]{:S(2)}) collective-permute-start(bf16[512,512]{1,0:T(8,128)(2,1)} %copy-done.29), channel_id=1, source_target_pairs={{0,8},{4,12},{8,0},{12,4},{1,9},{5,13},{9,1},{13,5},{2,10},{6,14},... | collective-permute-start | bytes 1572872 | tf_op jit(solution)/shard_map/ppermute | solution.py:798
  192.2 112.0 %copy-start.123 = (bf16[512,512]{1,0:T(8,128)(2,1)}, bf16[512,512]{1,0:T(8,128)(2,1)S(1)}, u32[]{:S(2)}) copy-start(bf16[512,512]{1,0:T(8,128)(2,1)S(1)} %collective-permute-done.23.refs_9_.refs_8_) | copy-start | bytes 1572868
  204.2 78.7 %copy-start.66 = (bf16[512,512]{1,0:T(8,128)(2,1)}, bf16[512,512]{1,0:T(8,128)(2,1)S(1)}, u32[]{:S(2)}) copy-start(bf16[512,512]{1,0:T(8,128)(2,1)S(1)} %collective-permute-done.24.refs_8_.refs_10_) | copy-start | bytes 1572868
  208.8 2.7 collective-permute-start.25
  213.4 25.8 %collective-permute-start.26 = (bf16[512,1024]{1,0:T(8,128)(2,1)S(1)}, bf16[512,1024]{1,0:T(8,128)(2,1)S(1)}, u32[]{:S(2)}, u32[]{:S(2)}) collective-permute-start(bf16[512,1024]{1,0:T(8,128)(2,1)S(1)} %get-tuple-element.132), channel_id=1, source_target_pairs={{0,16},{1,17},{2,18},{3,19},{4,20},{5,21},{6,22},{7,23},{8,24},{9,... | collective-permute-start | bytes 3145736 | tf_op jit(solution)/shard_map/ppermute | solution.py:28
  241.0 2.7 collective-permute-start.27
  264.4 2.7 collective-permute-start.28
  270.5 2.7 collective-permute-start.29
  287.4 2.7 collective-permute-start.30
  294.3 2.7 collective-permute-start.31
  308.8 2.7 collective-permute-start.32
  315.5 2.7 collective-permute-start.33
  353.4 2.7 collective-permute-start.34
  358.3 27.2 %collective-permute-start.35 = (bf16[512,1024]{1,0:T(8,128)(2,1)S(1)}, bf16[512,1024]{1,0:T(8,128)(2,1)S(1)}, u32[]{:S(2)}, u32[]{:S(2)}) collective-permute-start(bf16[512,1024]{1,0:T(8,128)(2,1)S(1)} %get-tuple-element.131), channel_id=1, source_target_pairs={{16,0},{17,1},{18,2},{19,3},{20,4},{21,5},{22,6},{23,7},{24,8},{25... | collective-permute-start | bytes 3145736 | tf_op jit(solution)/shard_map/ppermute | solution.py:28
  361.1 31.3 %all-to-all-start.1 = ((bf16[4,128,1024]{2,1,0:T(8,128)(2,1)}), bf16[4,128,1024]{2,1,0:T(8,128)(2,1)}, u32[]{:S(2)}, u32[]{:S(2)}) async-start(bf16[4,128,1024]{2,1,0:T(8,128)(2,1)} %bitcast.40), calls=%async_computation.1 | async-start | bytes 2097152 | tf_op jit(solution)/shard_map/all_to_all | solution.py:1208
  389.6 2.8 collective-permute-start.36
  414.9 2.7 collective-permute-start.37
  415.0 26.0 %collective-permute-start.40 = (bf16[1024,512]{1,0:T(8,128)(2,1)S(1)}, bf16[1024,512]{1,0:T(8,128)(2,1)S(1)}, u32[]{:S(2)}, u32[]{:S(2)}) collective-permute-start(bf16[1024,512]{1,0:T(8,128)(2,1)S(1)} %get-tuple-element.147), channel_id=1, source_target_pairs={{0,8},{4,12},{8,0},{12,4},{1,9},{5,13},{9,1},{13,5},{2,10},{6,14},... | collective-permute-start | bytes 3145736 | tf_op jit(solution)/shard_map/ppermute | solution.py:798
  422.5 34.5 %collective-permute-start.38 = (bf16[512,1024]{1,0:T(8,128)(2,1)}, bf16[512,1024]{1,0:T(8,128)(2,1)S(1)}, u32[]{:S(2)}, u32[]{:S(2)}) collective-permute-start(bf16[512,1024]{1,0:T(8,128)(2,1)} %get-tuple-element.141.refs_2_.refs_3_.refs_5_), channel_id=1, source_target_pairs={{0,4},{4,0},{8,12},{12,8},{1,5},{5,1},{9,13},{13,9},{2,6},{6,2},{1... | collective-permute-start | bytes 3145736 | tf_op jit(solution)/shard_map/ppermute | solution.py:798
  422.6 48.6 %collective-permute-start.39 = (bf16[1024,512]{1,0:T(8,128)(2,1)S(1)}, bf16[1024,512]{1,0:T(8,128)(2,1)S(1)}, u32[]{:S(2)}, u32[]{:S(2)}) collective-permute-start(bf16[1024,512]{1,0:T(8,128)(2,1)S(1)} %get-tuple-element.146), channel_id=1, source_target_pairs={{0,8},{4,12},{8,0},{12,4},{1,9},{5,13},{9,1},{13,5},{2,10},{6,14},... | collective-permute-start | bytes 3145736 | tf_op jit(solution)/shard_map/ppermute | solution.py:798
  441.4 29.8 %collective-permute-start.41 = (bf16[1024,512]{1,0:T(8,128)(2,1)S(1)}, bf16[1024,512]{1,0:T(8,128)(2,1)S(1)}, u32[]{:S(2)}, u32[]{:S(2)}) collective-permute-start(bf16[1024,512]{1,0:T(8,128)(2,1)S(1)} %moved.6.refs_13_), channel_id=1, source_target_pairs={{0,3},{1,0},{2,1},{3,2},{4,7},{5,4},{6,5},{7,6},{8,11},{9,8},{10,9... | collective-permute-start | bytes 3145736 | tf_op jit(solution)/shard_map/ppermute | solution.py:803
  454.9 42.0 %collective-permute-start.42 = (bf16[1024,512]{1,0:T(8,128)(2,1)S(1)}, bf16[1024,512]{1,0:T(8,128)(2,1)S(1)}, u32[]{:S(2)}, u32[]{:S(2)}) collective-permute-start(bf16[1024,512]{1,0:T(8,128)(2,1)S(1)} %get-tuple-element.151), channel_id=1, source_target_pairs={{0,8},{4,12},{8,0},{12,4},{1,9},{5,13},{9,1},{13,5},{2,10},{6,14},... | collective-permute-start | bytes 3145736 | tf_op jit(solution)/shard_map/ppermute | solution.py:798
  455.4 75.6 %collective-permute-start.45 = (bf16[1024,512]{1,0:T(8,128)(2,1)S(1)}, bf16[1024,512]{1,0:T(8,128)(2,1)S(1)}, u32[]{:S(2)}, u32[]{:S(2)}) collective-permute-start(bf16[1024,512]{1,0:T(8,128)(2,1)S(1)} %get-tuple-element.156), channel_id=1, source_target_pairs={{0,8},{4,12},{8,0},{12,4},{1,9},{5,13},{9,1},{13,5},{2,10},{6,14},... | collective-permute-start | bytes 3145736 | tf_op jit(solution)/shard_map/ppermute | solution.py:798
  472.6 24.3 %collective-permute-start.43 = (bf16[1024,512]{1,0:T(8,128)(2,1)S(1)}, bf16[1024,512]{1,0:T(8,128)(2,1)S(1)}, u32[]{:S(2)}, u32[]{:S(2)}) collective-permute-start(bf16[1024,512]{1,0:T(8,128)(2,1)S(1)} %moved.7.refs_13_), channel_id=1, source_target_pairs={{0,3},{1,0},{2,1},{3,2},{4,7},{5,4},{6,5},{7,6},{8,11},{9,8},{10,9... | collective-permute-start | bytes 3145736 | tf_op jit(solution)/shard_map/ppermute | solution.py:803
  513.4 17.7 %collective-permute-start.44 = (bf16[512,1024]{1,0:T(8,128)(2,1)S(1)}, bf16[512,1024]{1,0:T(8,128)(2,1)S(1)}, u32[]{:S(2)}, u32[]{:S(2)}) collective-permute-start(bf16[512,1024]{1,0:T(8,128)(2,1)S(1)} %get-tuple-element.154), channel_id=1, source_target_pairs={{0,4},{4,0},{8,12},{12,8},{1,5},{5,1},{9,13},{13,9},{2,6},{6,2},{1... | collective-permute-start | bytes 3145736 | tf_op jit(solution)/shard_map/ppermute | solution.py:798
  513.5 25.6 %collective-permute-start.47 = (bf16[1024,512]{1,0:T(8,128)(2,1)S(1)}, bf16[1024,512]{1,0:T(8,128)(2,1)S(1)}, u32[]{:S(2)}, u32[]{:S(2)}) collective-permute-start(bf16[1024,512]{1,0:T(8,128)(2,1)S(1)} %copy-done.53), channel_id=1, source_target_pairs={{0,3},{1,0},{2,1},{3,2},{4,7},{5,4},{6,5},{7,6},{8,11},{9,8},{10,9... | collective-permute-start | bytes 3145736 | tf_op jit(solution)/shard_map/ppermute | solution.py:803
  516.1 14.0 %collective-permute-start.46 = (bf16[512,512]{1,0:T(8,128)(2,1)S(1)}, bf16[512,512]{1,0:T(8,128)(2,1)S(1)}, u32[]{:S(2)}, u32[]{:S(2)}) collective-permute-start(bf16[512,512]{1,0:T(8,128)(2,1)S(1)} %get-tuple-element.157), channel_id=1, source_target_pairs={{0,8},{4,12},{8,0},{12,4},{1,9},{5,13},{9,1},{13,5},{2,10},{6,14},... | collective-permute-start | bytes 1572872 | tf_op jit(solution)/shard_map/ppermute | solution.py:798
  544.6 55.3 %all-to-all-start.2 = ((bf16[4,128,1024]{2,1,0:T(8,128)(2,1)}), bf16[4,128,1024]{2,1,0:T(8,128)(2,1)S(1)}, u32[]{:S(2)}, u32[]{:S(2)}) async-start(bf16[4,128,1024]{2,1,0:T(8,128)(2,1)} %bitcast.39), calls=%async_computation.2 | async-start | bytes 2097152 | tf_op jit(solution)/shard_map/all_to_all | solution.py:1280
  551.7 7.1 %collective-permute-start.48 = (bf16[2,128,1024]{2,1,0:T(8,128)(2,1)S(1)}, bf16[2,128,1024]{2,1,0:T(8,128)(2,1)S(1)}, u32[]{:S(2)}, u32[]{:S(2)}) collective-permute-start(bf16[2,128,1024]{2,1,0:T(8,128)(2,1)S(1)} %get-tuple-element.160), channel_id=1, source_target_pairs={{0,4},{4,0},{8,12},{12,8},{1,5},{5,1},{9,13},{13,9},{2,6},{6,2},{1... | collective-permute-start | bytes 1572872 | tf_op jit(solution)/shard_map/ppermute | solution.py:798
  551.8 15.0 %collective-permute-start.50 = (bf16[512,512]{1,0:T(8,128)(2,1)}, bf16[512,512]{1,0:T(8,128)(2,1)S(1)}, u32[]{:S(2)}, u32[]{:S(2)}) collective-permute-start(bf16[512,512]{1,0:T(8,128)(2,1)} %copy-done.126), channel_id=1, source_target_pairs={{0,8},{4,12},{8,0},{12,4},{1,9},{5,13},{9,1},{13,5},{2,10},{6,14},... | collective-permute-start | bytes 1572872 | tf_op jit(solution)/shard_map/ppermute | solution.py:798
  552.3 28.2 %collective-permute-start.51 = (bf16[512,512]{1,0:T(8,128)(2,1)}, bf16[512,512]{1,0:T(8,128)(2,1)S(1)}, u32[]{:S(2)}, u32[]{:S(2)}) collective-permute-start(bf16[512,512]{1,0:T(8,128)(2,1)} %copy-done.77), channel_id=1, source_target_pairs={{0,3},{1,0},{2,1},{3,2},{4,7},{5,4},{6,5},{7,6},{8,11},{9,8},{10,9... | collective-permute-start | bytes 1572872 | tf_op jit(solution)/shard_map/ppermute | solution.py:803
  556.2 24.3 %collective-permute-start.49 = (bf16[512,512]{1,0:T(8,128)(2,1)}, bf16[512,512]{1,0:T(8,128)(2,1)S(1)}, u32[]{:S(2)}, u32[]{:S(2)}) collective-permute-start(bf16[512,512]{1,0:T(8,128)(2,1)} %copy-done.127), channel_id=1, source_target_pairs={{0,8},{4,12},{8,0},{12,4},{1,9},{5,13},{9,1},{13,5},{2,10},{6,14},... | collective-permute-start | bytes 1572872 | tf_op jit(solution)/shard_map/ppermute | solution.py:798
  557.7 31.1 %collective-permute-start.55 = (bf16[512,512]{1,0:T(8,128)(2,1)}, bf16[512,512]{1,0:T(8,128)(2,1)S(1)}, u32[]{:S(2)}, u32[]{:S(2)}) collective-permute-start(bf16[512,512]{1,0:T(8,128)(2,1)} %copy-done.125), channel_id=1, source_target_pairs={{0,8},{4,12},{8,0},{12,4},{1,9},{5,13},{9,1},{13,5},{2,10},{6,14},... | collective-permute-start | bytes 1572872 | tf_op jit(solution)/shard_map/ppermute | solution.py:798
  558.8 25.0 %collective-permute-start.53 = (f32[256,512]{1,0:T(8,128)S(1)}, f32[256,512]{1,0:T(8,128)S(1)}, u32[]{:S(2)}, u32[]{:S(2)}) collective-permute-start(f32[256,512]{1,0:T(8,128)S(1)} %get-tuple-element.167), channel_id=1, source_target_pairs={{0,4},{4,0},{8,12},{12,8},{1,5},{5,1},{9,13},{13,9},{2,6},{6,2},{1... | collective-permute-start | bytes 1572872 | tf_op jit(solution)/shard_map/ppermute | solution.py:798
  566.8 17.0 %collective-permute-start.54 = (f32[512,256]{1,0:T(8,128)S(1)}, f32[512,256]{1,0:T(8,128)S(1)}, u32[]{:S(2)}, u32[]{:S(2)}) collective-permute-start(f32[512,256]{1,0:T(8,128)S(1)} %get-tuple-element.168), channel_id=1, source_target_pairs={{0,4},{4,0},{8,12},{12,8},{1,5},{5,1},{9,13},{13,9},{2,6},{6,2},{1... | collective-permute-start | bytes 1572872 | tf_op jit(solution)/shard_map/ppermute | solution.py:798
  581.6 18.3 %collective-permute-start.52 = (bf16[512,512]{1,0:T(8,128)(2,1)S(1)}, bf16[512,512]{1,0:T(8,128)(2,1)S(1)}, u32[]{:S(2)}, u32[]{:S(2)}) collective-permute-start(bf16[512,512]{1,0:T(8,128)(2,1)S(1)} %moved.10), channel_id=1, source_target_pairs={{0,3},{1,0},{2,1},{3,2},{4,7},{5,4},{6,5},{7,6},{8,11},{9,8},{10,9... | collective-permute-start | bytes 1572872 | tf_op jit(solution)/shard_map/ppermute | solution.py:803
  604.0 19.6 %collective-permute-start.56 = (bf16[2,128,1024]{2,1,0:T(8,128)(2,1)}, bf16[2,128,1024]{2,1,0:T(8,128)(2,1)S(1)}, u32[]{:S(2)}, u32[]{:S(2)}) collective-permute-start(bf16[2,128,1024]{2,1,0:T(8,128)(2,1)} %get-tuple-element.172), channel_id=1, source_target_pairs={{0,4},{4,0},{8,12},{12,8},{1,5},{5,1},{9,13},{13,9},{2,6},{6,2},{1... | collective-permute-start | bytes 1572872 | tf_op jit(solution)/shard_map/ppermute | solution.py:798
  604.0 20.6 %collective-permute-start.57 = (bf16[512,512]{1,0:T(8,128)(2,1)}, bf16[512,512]{1,0:T(8,128)(2,1)S(1)}, u32[]{:S(2)}, u32[]{:S(2)}) collective-permute-start(bf16[512,512]{1,0:T(8,128)(2,1)} %copy-done.33), channel_id=1, source_target_pairs={{0,3},{1,0},{2,1},{3,2},{4,7},{5,4},{6,5},{7,6},{8,11},{9,8},{10,9... | collective-permute-start | bytes 1572872 | tf_op jit(solution)/shard_map/ppermute | solution.py:803
  624.9 2.0 collective-permute-start.58
  (134 other events, 1276.4 us)

commit v13 on v12

--- a/solution.py
+++ b/solution.py
@@ -1249,7 +1249,7 @@
     hooks = iter(range(6))
 
     def hook(*new):
-        nonlocal d_down, d_up, d_attn
+        nonlocal d_down, d_up, d_attn, outputs
         turn = next(hooks)
         if turn == 0:
             d_down, d_up = new
@@ -1259,7 +1259,8 @@
             return ()
         if turn == 2:
             (d_attn,) = new
-            total, mlp_moves[3] = moves_on(mlp_sums[3], waits=d_attn[:1])
+            outputs = from_chip(lows, d_attn[:1])
+            total, mlp_moves[3] = moves_on(mlp_sums[3], waits=(outputs,))
             mlp_leaves(0, (total,))
             return (mlp_sums[1][0],)
         if turn == 3:
@@ -1269,13 +1270,12 @@
         if turn == 4:
             total, mlp_moves[1] = moves_on(mlp_sums[1], mlp_moves[2], waits=new)
             attn_leaves(0, new[0], (total,))
-            return (attn_sums[1][0],)
-        total, attn_moves[3] = moves_on(attn_sums[3])
-        return (mlp_sums[0][1], total, mlp_moves[1])
-
-    d_down = d_up = d_attn = None
+            total, attn_moves[3] = moves_on(attn_sums[3], waits=attn_sums[1][:1])
+            return (total, mlp_moves[1], mlp_sums[0][1])
+        return attn_sums[2][1:]
+
+    d_down = d_up = d_attn = outputs = None
     grad_zero, rights_zero, gain_zero = backward(received, saved_zero, hook, (lows,))
-    outputs = from_chip(lows, (grad_zero,))
     grads = own_first(jnp.where(first, grad_zero, grad_one)).reshape(tensor, part, width)
     grads = lax.all_to_all(grads, "tensor", 0, 0, tiled=True)
 
@@ -1297,9 +1297,8 @@
     up_grad, down_grad = with_core(
         mlp_join_kernel, "mlp_join", core_word, outs, up_keep, down_keep, *sent
     )
-    waits = (outputs, attn_sums[1][1])
-    _, attn_moves[2] = moves_on(attn_sums[2], attn_moves[3], waits=waits)
-    waits = (up_grad, grads, attn_sums[0][1])
+    total, attn_moves[2] = moves_on(attn_sums[2], attn_moves[3], waits=(grad_zero, attn_sums[1][1]))
+    waits = (up_grad, attn_sums[0][1], grads)
     last, attn_moves[1] = moves_on(attn_sums[1], attn_moves[2], waits=waits)
     grads = from_chip(grads, (last,))
     gain_total = own_first(jnp.where(first, gain_zero, gain_one))
@@ -1317,7 +1316,7 @@
         outs,
         *attn_sums[0],
         attn_moves[1],
-        waits=(grads, gains_grad),
+        waits=(grads, outputs, gains_grad),
     )
     spots = tuple((i * 128, (i + 1) * 128, i * 256) for i in range(3))
     outs = (((wide_half // 2, 768), jnp.float32), ((256, wide_half // 2), jnp.float32))

time: 641 us -> 642 us (level)
  transfers between devices with their start and end apart: 62 -> 62, of which waited for: 35 -> 36; matrix products, arithmetic and copies ran while one was open for 3% -> 3% of each run, Pallas kernels for 15% -> 14%
where the time goes in v13:
time: 642 us; the launch traced here: 633 us
  waiting for transfers between devices  248 us (39%)
  Pallas kernels  219 us (34%)
  starting transfers between devices  74.7 us (12%)
  local copies, waits for them, and re-layouts  57.9 us (9%)
  other arithmetic  20.7 us (3%)
  blocking collectives  10.2 us (2%)
    ppermute x42, waiting for transfers between devices, flip_pairs(): return lax.ppermute(block, 'dp', [(i, i ^ distance) for i in range(size)])  112 us
    ppermute x15, waiting for transfers between devices, passed_on(): lax.ppermute(block, 'tensor', [(i, (i + step) % size) for i in range(size)])  92.3 us
    pallas_call x6, Pallas kernels, by_pairs(): pl.pallas_call(without(functools.partial(kernel, len(pieces[0])), taken,...  86.2 us
    pallas_call x30, Pallas kernels, on_chip(): pl.pallas_call(without(kernel, len(operands), len(waits)), in_specs=[spac...  85.1 us
    unnamed x276, local copies, waits for them, and re-layouts  48.6 us
    ppermute x2, waiting for transfers between devices, shifted(): return lax.ppermute(block, axis, route)  41.5 us
    ppermute x15, starting transfers between devices, passed_on(): lax.ppermute(block, 'tensor', [(i, (i + step) % size) for i in range(size)])  29 us
    pallas_call x4, Pallas kernels, weight_grads(): pl.pallas_call(without(functools.partial(kernel, base), 1 + len(arrays),...  26 us
  transfers between devices with their start and end apart: 62, of which 36 were waited for; matrix products, arithmetic and copies ran while one was open for 3% of the time, Pallas kernels for 14%

profile of v13, /device:TPU:0, one launch (start us, length us, event | category | flops | bytes accessed | tf_op | source)
XLA Modules:
  0.0 632.9 jit_solution(11519332663487414457)
XLA Ops:
  11.4 6.2 all-to-all-start
  27.8 22.6 %collective-permute-done.1.refs_6_.refs_2_.refs_3_ = bf16[512,512]{1,0:T(8,128)(2,1)} collective-permute-done((bf16[512,512]{1,0:T(8,128)(2,1)}, bf16[512,512]{1,0:T(8,128)(2,1)}, u32[]{:S(2)}, u32[]{:S(2)}) %collective-permute-start.1) | collective-permute-done | bytes 524320 | tf_op jit(solution)/shard_map/ppermute | solution.py:803
  50.4 3.3 collective-permute-start.2
  58.5 7.0 %collective-permute-done.2.refs_2_.refs_7_.refs_3_.refs_5_.refs_4_ = bf16[512,512]{1,0:T(8,128)(2,1)} collective-permute-done((bf16[512,512]{1,0:T(8,128)(2,1)}, bf16[512,512]{1,0:T(8,128)(2,1)}, u32[]{:S(2)}, u32[]{:S(2)}) %collective-permute-start.2) | collective-permute-done | bytes 524320 | tf_op jit(solution)/shard_map/ppermute | solution.py:803
  69.5 10.4 %collective-permute-done.5.refs_4_.refs_5_.refs_7_ = bf16[512,512]{1,0:T(8,128)(2,1)S(1)} collective-permute-done((bf16[512,512]{1,0:T(8,128)(2,1)S(1)}, bf16[512,512]{1,0:T(8,128)(2,1)S(1)}, u32[]{:S(2)}, u32[]{:S(2)}) %collective-permute-start.5) | collective-permute-done | bytes 524320 | tf_op jit(solution)/shard_map/ppermute | solution.py:798
  82.6 2.5 collective-permute-start.11
  85.2 3.7 collective-permute-done.8.refs_10_.refs_6_.refs_8_.refs_7_
  93.8 5.6 collective-permute-done.11.refs_13_.refs_3_.refs_2_
  100.1 3.9 collective-permute-done.9.refs_11_.refs_7_.refs_8_
  105.5 5.1 collective-permute-done.12.refs_14_.refs_2_.refs_4_
  111.3 3.9 collective-permute-done.10.refs_12_.refs_8_.refs_9_
  119.0 16.8 %attend.2 = (bf16[4,1024,128]{2,1,0:T(8,128)(2,1)S(1)}, bf16[4,1024,128]{2,1,0:T(8,128)(2,1)S(1)}, bf16[4,1024,128]{2,1,0:T(8,128)(2,1)S(1)}, f32[4,2,1024]{2,1,0:T(2,128)S(1)}, bf16[1024,512]{1,0:T(8,128)(2,1)S(1)}) custom-call(s32[1]{0:T(128)} %bitcast.refs_0_, f32[1024,128]{1,0:T(8,128)S(1)} %get-tuple-element.230.refs_1_, ...), custom_call_target="tpu_custom_call" | custom-call | flops 11811160064 | bytes 11567104 | tf_op jit(solution)/shard_map/attend/pallas_call | solution.py:708
  140.1 3.1 attn_out.2
  143.3 2.5 collective-permute-start.18
  148.3 11.8 %collective-permute-done.18.refs_4_.refs_5_ = bf16[512,512]{1,0:T(8,128)(2,1)S(1)} collective-permute-done((bf16[512,512]{1,0:T(8,128)(2,1)}, bf16[512,512]{1,0:T(8,128)(2,1)S(1)}, u32[]{:S(2)}, u32[]{:S(2)}) %collective-permute-start.18) | collective-permute-done | bytes 524320 | tf_op jit(solution)/shard_map/ppermute | solution.py:803
  160.1 10.8 %collective-permute-done.19.refs_5_.refs_4_.refs_6_ = bf16[512,512]{1,0:T(8,128)(2,1)S(1)} collective-permute-done((bf16[512,512]{1,0:T(8,128)(2,1)}, bf16[512,512]{1,0:T(8,128)(2,1)S(1)}, u32[]{:S(2)}, u32[]{:S(2)}) %collective-permute-start.19) | collective-permute-done | bytes 524320 | tf_op jit(solution)/shard_map/ppermute | solution.py:803
  172.3 3.4 after_attn.2
  179.3 12.9 %collective-permute-done.23.refs_9_.refs_8_ = bf16[512,512]{1,0:T(8,128)(2,1)S(1)} collective-permute-done((bf16[512,512]{1,0:T(8,128)(2,1)}, bf16[512,512]{1,0:T(8,128)(2,1)S(1)}, u32[]{:S(2)}, u32[]{:S(2)}) %collective-permute-start.23) | collective-permute-done | bytes 524320 | tf_op jit(solution)/shard_map/ppermute | solution.py:798
  194.5 7.7 %mlp_up.2 = (bf16[1024,2048]{1,0:T(8,128)(2,1)S(1)}, bf16[1024,2048]{1,0:T(8,128)(2,1)S(1)}) custom-call(bf16[512,1024]{1,0:T(8,128)(2,1)S(1)} %get-tuple-element.103.refs_0_.refs_1_, bf16[512,1024]{1,0:T(8,128)(2,1)S(1)} %collective-permute-done.22.refs_1_.refs_2_, bf16[512,512]{1,0:T(8,128)(2,1)S(1)} %copy-done.110, bf16[512,512]{1,0:T(8,128)(2,1)S(1)} %copy-done.122, ...), custom_call_target="tpu_custom_call" | custom-call | flops 4294967296 | bytes 14680064 | tf_op jit(solution)/shard_map/mlp_up/pallas_call | solution.py:690
  204.3 4.5 mlp_down.2
  208.9 2.6 collective-permute-done.25.refs_3_
  213.5 3.6 collective-permute-start.26
  217.0 22.2 %collective-permute-done.26.refs_1_ = bf16[512,1024]{1,0:T(8,128)(2,1)S(1)} collective-permute-done((bf16[512,1024]{1,0:T(8,128)(2,1)S(1)}, bf16[512,1024]{1,0:T(8,128)(2,1)S(1)}, u32[]{:S(2)}, u32[]{:S(2)}) %collective-permute-start.26) | collective-permute-done | bytes 1048608 | tf_op jit(solution)/shard_map/ppermute | solution.py:28
  241.1 2.6 collective-permute-done.27.refs_4_.refs_8_
  243.8 17.1 %attend.3 = (bf16[4,1024,128]{2,1,0:T(8,128)(2,1)S(1)}, bf16[4,1024,128]{2,1,0:T(8,128)(2,1)S(1)}, bf16[4,1024,128]{2,1,0:T(8,128)(2,1)S(1)}, f32[4,2,1024]{2,1,0:T(2,128)S(1)}, bf16[1024,512]{1,0:T(8,128)(2,1)S(1)}) custom-call(s32[1]{0:T(128)} %bitcast.refs_0_, f32[1024,128]{1,0:T(8,128)S(1)} %get-tuple-element.230.refs_1_, ...), custom_call_target="tpu_custom_call" | custom-call | flops 11811160064 | bytes 11567104 | tf_op jit(solution)/shard_map/attend/pallas_call | solution.py:708
  260.9 3.5 attn_out.3
  264.6 2.5 collective-permute-done.28.refs_3_
  267.1 3.4 after_attn.3
  270.7 2.5 collective-permute-done.29.refs_1_.refs_8_
  273.3 7.7 %mlp_up.3 = (bf16[1024,2048]{1,0:T(8,128)(2,1)S(1)}, bf16[1024,2048]{1,0:T(8,128)(2,1)S(1)}) custom-call(bf16[512,1024]{1,0:T(8,128)(2,1)S(1)} %get-tuple-element.112.refs_0_.refs_7_, bf16[512,1024]{1,0:T(8,128)(2,1)S(1)} %collective-permute-done.29.refs_1_.refs_8_, bf16[512,512]{1,0:T(8,128)(2,1)S(1)} %copy-done.110, bf16[512,512]{1,0:T(8,128)(2,1)S(1)} %copy-done.122, ...), custom_call_target="tpu_custom_call" | custom-call | flops 4294967296 | bytes 14680064 | tf_op jit(solution)/shard_map/mlp_up/pallas_call | solution.py:690
  283.1 4.5 mlp_down.3
  287.8 2.5 collective-permute-done.30.refs_3_
  294.7 2.5 collective-permute-done.31.refs_1_.refs_12_
  297.2 7.2 %mlp_up_back.2.refs_0_.refs_9_ = bf16[1024,2048]{1,0:T(8,128)(2,1)S(1)} custom-call(bf16[512,1024]{1,0:T(8,128)(2,1)S(1)} %get-tuple-element.118.refs_0_.refs_11_, bf16[512,1024]{1,0:T(8,128)(2,1)S(1)} %collective-permute-done.31.refs_1_.refs_12_, bf16[1024,2048]{1,0:T(8,128)(2,1)} %copy-done.34, bf16[512,512]{1,0:T(8,128)(2,1)} %copy-done.59, ...), custom_call_target="tpu_custom_call" | custom-call | tf_op jit(solution)/shard_map/mlp_up_back/pallas_call | solution.py:729
  304.4 4.5 mlp_back.2
  311.7 3.9 into_attn_back.2
  315.8 2.5 collective-permute-done.33.refs_4_.refs_12_
  318.4 13.1 %attend_back.4.refs_0_.refs_9_ = bf16[1024,768]{1,0:T(8,128)(2,1)S(1)} custom-call(s32[1]{0:T(128)} %bitcast.refs_0_, f32[1024,128]{1,0:T(8,128)S(1)} %get-tuple-element.230.refs_1_, f32[1024,128]{1,0:T(8,128)S(1)} %get-tuple-element.231.refs_2_, bf16[512,1024]{1,0:T(8,128)(2,1)S(1)} %get-tuple-element.123.refs_3_.refs_11_, ...), custom_call_target="tpu_custom_call" | custom-call | flops 11274289152 | bytes 6815744 | tf_op jit(solution)/shard_map/attend_back/pallas_call | solution.py:708
  331.5 13.0 %attend_back.5.refs_1_.refs_9_ = bf16[1024,768]{1,0:T(8,128)(2,1)S(1)} custom-call(s32[1]{0:T(128)} %bitcast.refs_0_, f32[1024,128]{1,0:T(8,128)S(1)} %get-tuple-element.230.refs_1_, f32[1024,128]{1,0:T(8,128)S(1)} %get-tuple-element.231.refs_2_, bf16[512,1024]{1,0:T(8,128)(2,1)S(1)} %get-tuple-element.123.refs_3_.refs_11_, ...), custom_call_target="tpu_custom_call" | custom-call | flops 11274289152 | bytes 6815744 | tf_op jit(solution)/shard_map/attend_back/pallas_call | solution.py:708
  346.1 5.8 attn_back.2
  361.3 5.2 all-to-all-start.1
  366.5 19.2 %collective-permute-done.35.refs_1_ = bf16[512,1024]{1,0:T(8,128)(2,1)S(1)} collective-permute-done((bf16[512,1024]{1,0:T(8,128)(2,1)S(1)}, bf16[512,1024]{1,0:T(8,128)(2,1)S(1)}, u32[]{:S(2)}, u32[]{:S(2)}) %collective-permute-start.35) | collective-permute-done | bytes 1048608 | tf_op jit(solution)/shard_map/ppermute | solution.py:28
  389.9 2.7 all-to-all-done.1.refs_11_.refs_1_
  392.6 7.2 %mlp_up_back.3.refs_3_.refs_0_ = bf16[1024,2048]{1,0:T(8,128)(2,1)S(1)} custom-call(bf16[512,1024]{1,0:T(8,128)(2,1)S(1)} %get-tuple-element.135.refs_0_.refs_5_, bf16[512,1024]{1,0:T(8,128)(2,1)S(1)} %collective-permute-done.36.refs_1_.refs_6_, bf16[1024,2048]{1,0:T(8,128)(2,1)} %copy-done.52, bf16[512,512]{1,0:T(8,128)(2,1)} %copy-done.59, ...), custom_call_target="tpu_custom_call" | custom-call | tf_op jit(solution)/shard_map/mlp_up_back/pallas_call | solution.py:729
  401.8 7.2 %mlp_grads.2 = (f32[1024,512]{1,0:T(8,128)S(1)}, bf16[1024,512]{1,0:T(8,128)(2,1)S(1)}, f32[1024,512]{1,0:T(8,128)S(1)}, bf16[1024,512]{1,0:T(8,128)(2,1)S(1)}) custom-call(s32[1]{0:T(128)} %bitcast.12.refs_0_, bf16[512,1024]{1,0:T(8,128)(2,1)} %copy-done.38, bf16[512,1024]{1,0:T(8,128)(2,1)} %copy-done.39, bf16[1024,2048]{1,0:T(8,128)(2,1)} %copy-done.3, ...), custom_call_target="tpu_custom_call" | custom-call | tf_op jit(solution)/shard_map/mlp_grads/pallas_call | solution.py:897
  410.5 4.5 mlp_back.3
  417.7 4.9 into_attn_back.3
  427.3 13.8 %collective-permute-done.41.refs_1_ = bf16[1024,512]{1,0:T(8,128)(2,1)S(1)} collective-permute-done((bf16[1024,512]{1,0:T(8,128)(2,1)S(1)}, bf16[1024,512]{1,0:T(8,128)(2,1)S(1)}, u32[]{:S(2)}, u32[]{:S(2)}) %collective-permute-start.41) | collective-permute-done | bytes 1048608 | tf_op jit(solution)/shard_map/ppermute | solution.py:798
  441.6 3.7 collective-permute-start.42
  445.3 7.0 %mlp_grads.3 = (f32[1024,512]{1,0:T(8,128)S(1)}, bf16[1024,512]{1,0:T(8,128)(2,1)S(1)}, f32[1024,512]{1,0:T(8,128)S(1)}, bf16[1024,512]{1,0:T(8,128)(2,1)S(1)}) custom-call(s32[1]{0:T(128)} %bitcast.12.refs_0_, bf16[512,1024]{1,0:T(8,128)(2,1)} %copy-done.38, bf16[512,1024]{1,0:T(8,128)(2,1)} %copy-done.39, bf16[1024,2048]{1,0:T(8,128)(2,1)} %copy-done.3, ...), custom_call_target="tpu_custom_call" | custom-call | tf_op jit(solution)/shard_map/mlp_grads/pallas_call | solution.py:897
  457.1 13.1 %attend_back.6.refs_3_.refs_1_ = bf16[1024,768]{1,0:T(8,128)(2,1)S(1)} custom-call(s32[1]{0:T(128)} %bitcast.refs_0_, f32[1024,128]{1,0:T(8,128)S(1)} %copy-done.103, f32[1024,128]{1,0:T(8,128)S(1)} %copy-done.105, bf16[512,1024]{1,0:T(8,128)(2,1)} %get-tuple-element.141.refs_2_.refs_3_.refs_5_, ...), custom_call_target="tpu_custom_call" | custom-call | flops 11274289152 | bytes 6815744 | tf_op jit(solution)/shard_map/attend_back/pallas_call | solution.py:708
  474.4 5.9 attn_grads.2
  482.3 13.2 %attend_back.7.refs_3_.refs_0_ = bf16[1024,768]{1,0:T(8,128)(2,1)S(1)} custom-call(s32[1]{0:T(128)} %bitcast.refs_0_, f32[1024,128]{1,0:T(8,128)S(1)} %copy-done.103, f32[1024,128]{1,0:T(8,128)S(1)} %copy-done.105, bf16[512,1024]{1,0:T(8,128)(2,1)} %get-tuple-element.141.refs_2_.refs_3_.refs_5_, bf16[512,1024]{1,0:T(8,128)(2,1)S(1)} %copy-done.47, ...), custom_call_target="tpu_custom_call" | custom-call | flops 11274289152 | bytes 6815744 | tf_op jit(solution)/shard_map/attend_back/pallas_call | solution.py:708
  497.2 3.4 collective-permute-start.46
  501.1 5.9 attn_grads.3
  508.0 11.3 %collective-permute-done.43.refs_1_ = bf16[512,512]{1,0:T(8,128)(2,1)S(1)} collective-permute-done((bf16[512,512]{1,0:T(8,128)(2,1)S(1)}, bf16[512,512]{1,0:T(8,128)(2,1)S(1)}, u32[]{:S(2)}, u32[]{:S(2)}) %collective-permute-start.43) | collective-permute-done | bytes 524320 | tf_op jit(solution)/shard_map/ppermute | solution.py:798
  522.3 5.3 attn_back.3
  528.2 13.8 %collective-permute-done.49.refs_5_.refs_1_ = bf16[512,512]{1,0:T(8,128)(2,1)S(1)} collective-permute-done((bf16[512,512]{1,0:T(8,128)(2,1)S(1)}, bf16[512,512]{1,0:T(8,128)(2,1)S(1)}, u32[]{:S(2)}, u32[]{:S(2)}) %collective-permute-start.49) | collective-permute-done | bytes 524320 | tf_op jit(solution)/shard_map/ppermute | solution.py:798
  547.3 5.0 all-to-all-start.2
  552.8 3.8 collective-permute-start.51
  561.5 5.9 collective-permute-done.50.refs_4_.refs_1_
  567.4 15.2 %collective-permute-done.51.refs_2_ = bf16[512,512]{1,0:T(8,128)(2,1)S(1)} collective-permute-done((bf16[512,512]{1,0:T(8,128)(2,1)}, bf16[512,512]{1,0:T(8,128)(2,1)S(1)}, u32[]{:S(2)}, u32[]{:S(2)}) %collective-permute-start.51) | collective-permute-done | bytes 524320 | tf_op jit(solution)/shard_map/ppermute | solution.py:803
  587.4 13.8 %collective-permute-done.52.refs_2_ = bf16[512,512]{1,0:T(8,128)(2,1)S(1)} collective-permute-done((bf16[512,512]{1,0:T(8,128)(2,1)S(1)}, bf16[512,512]{1,0:T(8,128)(2,1)S(1)}, u32[]{:S(2)}, u32[]{:S(2)}) %collective-permute-start.52) | collective-permute-done | bytes 524320 | tf_op jit(solution)/shard_map/ppermute | solution.py:803
  612.9 10.2 %all_to_all.20 = f32[16,1,256]{2,1,0:T(1,128)S(1)} all-to-all(f32[16,1,256]{2,1,0:T(1,128)S(1)} %reshape.144), channel_id=1, replica_groups=mesh['section'=2,'dp'=4,'tensor'=4] {'dp','tensor'}, dimensions={0} | all-to-all | bytes 32768 | tf_op jit(solution)/shard_map/all_to_all | solution.py:1309
  (443 shorter events, 153.7 us)
Async XLA Ops:
  7.2 2.1 collective-permute-start
  11.4 68.5 %all-to-all-start = ((bf16[4,128,1024]{2,1,0:T(8,128)(2,1)}), bf16[4,128,1024]{2,1,0:T(8,128)(2,1)S(1)}, u32[]{:S(2)}, u32[]{:S(2)}) async-start(bf16[4,128,1024]{2,1,0:T(8,128)(2,1)} %pad_maximum_fusion), calls=%async_computation | async-start | bytes 2097152 | tf_op jit(solution)/shard_map/all_to_all | solution.py:1059
  24.2 26.2 %collective-permute-start.1 = (bf16[512,512]{1,0:T(8,128)(2,1)}, bf16[512,512]{1,0:T(8,128)(2,1)}, u32[]{:S(2)}, u32[]{:S(2)}) collective-permute-start(bf16[512,512]{1,0:T(8,128)(2,1)} %pad_maximum_fusion.3.refs_5_.refs_1_.refs_2_), channel_id=1, source_target_pairs={{0,1},{1,2},{2,3},{3,0},{4,5},{5,6},{6,7},{7,4},{8,9},{9,10},{10,1... | collective-permute-start | bytes 1572872 | tf_op jit(solution)/shard_map/ppermute | solution.py:803
  26.3 40.6 %collective-permute-start.3 = (bf16[512,512]{1,0:T(8,128)(2,1)}, bf16[512,512]{1,0:T(8,128)(2,1)}, u32[]{:S(2)}, u32[]{:S(2)}) collective-permute-start(bf16[512,512]{1,0:T(8,128)(2,1)} %pad_maximum_fusion.3.refs_5_.refs_1_.refs_2_), channel_id=1, source_target_pairs={{0,8},{4,12},{8,0},{12,4},{1,9},{5,13},{9,1},{13,5},{2,10},{6,14},... | collective-permute-start | bytes 1572872 | tf_op jit(solution)/shard_map/ppermute | solution.py:798
  50.4 15.0 %collective-permute-start.2 = (bf16[512,512]{1,0:T(8,128)(2,1)}, bf16[512,512]{1,0:T(8,128)(2,1)}, u32[]{:S(2)}, u32[]{:S(2)}) collective-permute-start(bf16[512,512]{1,0:T(8,128)(2,1)} %collective-permute-done.1.refs_6_.refs_2_.refs_3_), channel_id=1, source_target_pairs={{0,1},{1,2},{2,3},{3,0},{4,5},{5,6},{6,7},{7,4},{8,9},{9,10},{10,1... | collective-permute-start | bytes 1572872 | tf_op jit(solution)/shard_map/ppermute | solution.py:803
  53.7 14.9 %collective-permute-start.4 = (bf16[512,512]{1,0:T(8,128)(2,1)S(1)}, bf16[512,512]{1,0:T(8,128)(2,1)S(1)}, u32[]{:S(2)}, u32[]{:S(2)}) collective-permute-start(bf16[512,512]{1,0:T(8,128)(2,1)S(1)} %dynamic-slice_bitcast_fusion.1.refs_0_), channel_id=1, source_target_pairs={{0,8},{4,12},{8,0},{12,4},{1,9},{5,13},{9,1},{13,5},{2,10},{6,14},... | collective-permute-start | bytes 1572872 | tf_op jit(solution)/shard_map/ppermute | solution.py:798
  56.4 23.5 %collective-permute-start.5 = (bf16[512,512]{1,0:T(8,128)(2,1)S(1)}, bf16[512,512]{1,0:T(8,128)(2,1)S(1)}, u32[]{:S(2)}, u32[]{:S(2)}) collective-permute-start(bf16[512,512]{1,0:T(8,128)(2,1)S(1)} %dynamic-slice_bitcast_fusion.refs_1_), channel_id=1, source_target_pairs={{0,8},{4,12},{8,0},{12,4},{1,9},{5,13},{9,1},{13,5},{2,10},{6,14},... | collective-permute-start | bytes 1572872 | tf_op jit(solution)/shard_map/ppermute | solution.py:798
  57.0 31.9 %collective-permute-start.8 = (bf16[512,512]{1,0:T(8,128)(2,1)}, bf16[512,512]{1,0:T(8,128)(2,1)}, u32[]{:S(2)}, u32[]{:S(2)}) collective-permute-start(bf16[512,512]{1,0:T(8,128)(2,1)} %collective-permute-done.1.refs_6_.refs_2_.refs_3_), channel_id=1, source_target_pairs={{0,8},{4,12},{8,0},{12,4},{1,9},{5,13},{9,1},{13,5},{2,10},{6,14},... | collective-permute-start | bytes 1572872 | tf_op jit(solution)/shard_map/ppermute | solution.py:798
  65.5 25.0 %collective-permute-start.7 = (bf16[512,512]{1,0:T(8,128)(2,1)}, bf16[512,512]{1,0:T(8,128)(2,1)}, u32[]{:S(2)}, u32[]{:S(2)}) collective-permute-start(bf16[512,512]{1,0:T(8,128)(2,1)} %collective-permute-done.2.refs_2_.refs_7_.refs_3_.refs_5_.refs_4_), channel_id=1, source_target_pairs={{0,1},{1,2},{2,3},{3,0},{4,5},{5,6},{6,7},{7,4},{8,9},{9,10},{10,1... | collective-permute-start | bytes 1572872 | tf_op jit(solution)/shard_map/ppermute | solution.py:803
  82.5 34.3 %collective-permute-start.6 = (bf16[512,1024]{1,0:T(8,128)(2,1)S(1)}, bf16[512,1024]{1,0:T(8,128)(2,1)S(1)}, u32[]{:S(2)}, u32[]{:S(2)}) collective-permute-start(bf16[512,1024]{1,0:T(8,128)(2,1)S(1)} %norm_in.2.refs_3_.refs_1_), channel_id=1, source_target_pairs={{0,4},{4,0},{8,12},{12,8},{1,5},{5,1},{9,13},{13,9},{2,6},{6,2},{1... | collective-permute-start | bytes 3145736 | tf_op jit(solution)/shard_map/ppermute | solution.py:798
  82.6 16.8 %collective-permute-start.11 = (bf16[512,512]{1,0:T(8,128)(2,1)}, bf16[512,512]{1,0:T(8,128)(2,1)S(1)}, u32[]{:S(2)}, u32[]{:S(2)}) collective-permute-start(bf16[512,512]{1,0:T(8,128)(2,1)} %copy-done.109), channel_id=1, source_target_pairs={{0,1},{1,2},{2,3},{3,0},{4,5},{5,6},{6,7},{7,4},{8,9},{9,10},{10,1... | collective-permute-start | bytes 1572872 | tf_op jit(solution)/shard_map/ppermute | solution.py:803
  85.1 25.5 %collective-permute-start.12 = (bf16[512,512]{1,0:T(8,128)(2,1)}, bf16[512,512]{1,0:T(8,128)(2,1)S(1)}, u32[]{:S(2)}, u32[]{:S(2)}) collective-permute-start(bf16[512,512]{1,0:T(8,128)(2,1)} %copy-done.59), channel_id=1, source_target_pairs={{0,1},{1,2},{2,3},{3,0},{4,5},{5,6},{6,7},{7,4},{8,9},{9,10},{10,1... | collective-permute-start | bytes 1572872 | tf_op jit(solution)/shard_map/ppermute | solution.py:803
  88.9 15.1 %collective-permute-start.9 = (bf16[512,512]{1,0:T(8,128)(2,1)}, bf16[512,512]{1,0:T(8,128)(2,1)S(1)}, u32[]{:S(2)}, u32[]{:S(2)}) collective-permute-start(bf16[512,512]{1,0:T(8,128)(2,1)} %collective-permute-done.2.refs_2_.refs_7_.refs_3_.refs_5_.refs_4_), channel_id=1, source_target_pairs={{0,8},{4,12},{8,0},{12,4},{1,9},{5,13},{9,1},{13,5},{2,10},{6,14},... | collective-permute-start | bytes 1572872 | tf_op jit(solution)/shard_map/ppermute | solution.py:798
  90.4 24.8 %collective-permute-start.10 = (bf16[512,512]{1,0:T(8,128)(2,1)}, bf16[512,512]{1,0:T(8,128)(2,1)S(1)}, u32[]{:S(2)}, u32[]{:S(2)}) collective-permute-start(bf16[512,512]{1,0:T(8,128)(2,1)} %collective-permute-done.7.refs_8_.refs_4_.refs_6_.refs_5_), channel_id=1, source_target_pairs={{0,8},{4,12},{8,0},{12,4},{1,9},{5,13},{9,1},{13,5},{2,10},{6,14},... | collective-permute-start | bytes 1572872 | tf_op jit(solution)/shard_map/ppermute | solution.py:798
  99.4 39.3 %collective-permute-start.13 = (bf16[512,512]{1,0:T(8,128)(2,1)S(1)}, bf16[512,512]{1,0:T(8,128)(2,1)S(1)}, u32[]{:S(2)}, u32[]{:S(2)}) collective-permute-start(bf16[512,512]{1,0:T(8,128)(2,1)S(1)} %collective-permute-done.11.refs_13_.refs_3_.refs_2_), channel_id=1, source_target_pairs={{0,1},{1,2},{2,3},{3,0},{4,5},{5,6},{6,7},{7,4},{8,9},{9,10},{10,1... | collective-permute-start | bytes 1572872 | tf_op jit(solution)/shard_map/ppermute | solution.py:803
  104.0 34.7 %collective-permute-start.15 = (bf16[512,512]{1,0:T(8,128)(2,1)S(1)}, bf16[512,512]{1,0:T(8,128)(2,1)S(1)}, u32[]{:S(2)}, u32[]{:S(2)}) collective-permute-start(bf16[512,512]{1,0:T(8,128)(2,1)S(1)} %collective-permute-done.11.refs_13_.refs_3_.refs_2_), channel_id=1, source_target_pairs={{0,8},{4,12},{8,0},{12,4},{1,9},{5,13},{9,1},{13,5},{2,10},{6,14},... | collective-permute-start | bytes 1572872 | tf_op jit(solution)/shard_map/ppermute | solution.py:798
  110.6 28.1 %collective-permute-start.14 = (bf16[512,512]{1,0:T(8,128)(2,1)S(1)}, bf16[512,512]{1,0:T(8,128)(2,1)S(1)}, u32[]{:S(2)}, u32[]{:S(2)}) collective-permute-start(bf16[512,512]{1,0:T(8,128)(2,1)S(1)} %collective-permute-done.12.refs_14_.refs_2_.refs_4_), channel_id=1, source_target_pairs={{0,1},{1,2},{2,3},{3,0},{4,5},{5,6},{6,7},{7,4},{8,9},{9,10},{10,1... | collective-permute-start | bytes 1572872 | tf_op jit(solution)/shard_map/ppermute | solution.py:803
  115.2 23.5 %collective-permute-start.16 = (bf16[512,512]{1,0:T(8,128)(2,1)S(1)}, bf16[512,512]{1,0:T(8,128)(2,1)S(1)}, u32[]{:S(2)}, u32[]{:S(2)}) collective-permute-start(bf16[512,512]{1,0:T(8,128)(2,1)S(1)} %collective-permute-done.12.refs_14_.refs_2_.refs_4_), channel_id=1, source_target_pairs={{0,8},{4,12},{8,0},{12,4},{1,9},{5,13},{9,1},{13,5},{2,10},{6,14},... | collective-permute-start | bytes 1572872 | tf_op jit(solution)/shard_map/ppermute | solution.py:798
  143.2 28.3 %collective-permute-start.17 = (bf16[512,1024]{1,0:T(8,128)(2,1)S(1)}, bf16[512,1024]{1,0:T(8,128)(2,1)S(1)}, u32[]{:S(2)}, u32[]{:S(2)}) collective-permute-start(bf16[512,1024]{1,0:T(8,128)(2,1)S(1)} %get-tuple-element.101), channel_id=1, source_target_pairs={{0,4},{4,0},{8,12},{12,8},{1,5},{5,1},{9,13},{13,9},{2,6},{6,2},{1... | collective-permute-start | bytes 3145736 | tf_op jit(solution)/shard_map/ppermute | solution.py:798
  143.3 16.8 %collective-permute-start.18 = (bf16[512,512]{1,0:T(8,128)(2,1)}, bf16[512,512]{1,0:T(8,128)(2,1)S(1)}, u32[]{:S(2)}, u32[]{:S(2)}) collective-permute-start(bf16[512,512]{1,0:T(8,128)(2,1)} %copy-done.96), channel_id=1, source_target_pairs={{0,1},{1,2},{2,3},{3,0},{4,5},{5,6},{6,7},{7,4},{8,9},{9,10},{10,1... | collective-permute-start | bytes 1572872 | tf_op jit(solution)/shard_map/ppermute | solution.py:803
  145.8 25.0 %collective-permute-start.19 = (bf16[512,512]{1,0:T(8,128)(2,1)}, bf16[512,512]{1,0:T(8,128)(2,1)S(1)}, u32[]{:S(2)}, u32[]{:S(2)}) collective-permute-start(bf16[512,512]{1,0:T(8,128)(2,1)} %copy-done.23), channel_id=1, source_target_pairs={{0,1},{1,2},{2,3},{3,0},{4,5},{5,6},{6,7},{7,4},{8,9},{9,10},{10,1... | collective-permute-start | bytes 1572872 | tf_op jit(solution)/shard_map/ppermute | solution.py:803
  146.3 24.6 %collective-permute-start.20 = (bf16[512,512]{1,0:T(8,128)(2,1)}, bf16[512,512]{1,0:T(8,128)(2,1)S(1)}, u32[]{:S(2)}, u32[]{:S(2)}) collective-permute-start(bf16[512,512]{1,0:T(8,128)(2,1)} %copy-done.96), channel_id=1, source_target_pairs={{0,8},{4,12},{8,0},{12,4},{1,9},{5,13},{9,1},{13,5},{2,10},{6,14},... | collective-permute-start | bytes 1572872 | tf_op jit(solution)/shard_map/ppermute | solution.py:798
  146.8 24.7 %collective-permute-start.21 = (bf16[512,512]{1,0:T(8,128)(2,1)}, bf16[512,512]{1,0:T(8,128)(2,1)S(1)}, u32[]{:S(2)}, u32[]{:S(2)}) collective-permute-start(bf16[512,512]{1,0:T(8,128)(2,1)} %copy-done.23), channel_id=1, source_target_pairs={{0,8},{4,12},{8,0},{12,4},{1,9},{5,13},{9,1},{13,5},{2,10},{6,14},... | collective-permute-start | bytes 1572872 | tf_op jit(solution)/shard_map/ppermute | solution.py:798
  177.2 15.1 %collective-permute-start.22 = (bf16[512,1024]{1,0:T(8,128)(2,1)S(1)}, bf16[512,1024]{1,0:T(8,128)(2,1)S(1)}, u32[]{:S(2)}, u32[]{:S(2)}) collective-permute-start(bf16[512,1024]{1,0:T(8,128)(2,1)S(1)} %get-tuple-element.103.refs_0_.refs_1_), channel_id=1, source_target_pairs={{0,4},{4,0},{8,12},{12,8},{1,5},{5,1},{9,13},{13,9},{2,6},{6,2},{1... | collective-permute-start | bytes 3145736 | tf_op jit(solution)/shard_map/ppermute | solution.py:798
  177.3 15.0 %collective-permute-start.23 = (bf16[512,512]{1,0:T(8,128)(2,1)}, bf16[512,512]{1,0:T(8,128)(2,1)S(1)}, u32[]{:S(2)}, u32[]{:S(2)}) collective-permute-start(bf16[512,512]{1,0:T(8,128)(2,1)} %copy-done.112), channel_id=1, source_target_pairs={{0,8},{4,12},{8,0},{12,4},{1,9},{5,13},{9,1},{13,5},{2,10},{6,14},... | collective-permute-start | bytes 1572872 | tf_op jit(solution)/shard_map/ppermute | solution.py:798
  177.8 26.5 %collective-permute-start.24 = (bf16[512,512]{1,0:T(8,128)(2,1)}, bf16[512,512]{1,0:T(8,128)(2,1)S(1)}, u32[]{:S(2)}, u32[]{:S(2)}) collective-permute-start(bf16[512,512]{1,0:T(8,128)(2,1)} %copy-done.29), channel_id=1, source_target_pairs={{0,8},{4,12},{8,0},{12,4},{1,9},{5,13},{9,1},{13,5},{2,10},{6,14},... | collective-permute-start | bytes 1572872 | tf_op jit(solution)/shard_map/ppermute | solution.py:798
  192.3 112.1 %copy-start.124 = (bf16[512,512]{1,0:T(8,128)(2,1)}, bf16[512,512]{1,0:T(8,128)(2,1)S(1)}, u32[]{:S(2)}) copy-start(bf16[512,512]{1,0:T(8,128)(2,1)S(1)} %collective-permute-done.23.refs_9_.refs_8_) | copy-start | bytes 1572868
  204.3 78.8 %copy-start.63 = (bf16[512,512]{1,0:T(8,128)(2,1)}, bf16[512,512]{1,0:T(8,128)(2,1)S(1)}, u32[]{:S(2)}) copy-start(bf16[512,512]{1,0:T(8,128)(2,1)S(1)} %collective-permute-done.24.refs_8_.refs_10_) | copy-start | bytes 1572868
  208.8 2.7 collective-permute-start.25
  213.5 25.8 %collective-permute-start.26 = (bf16[512,1024]{1,0:T(8,128)(2,1)S(1)}, bf16[512,1024]{1,0:T(8,128)(2,1)S(1)}, u32[]{:S(2)}, u32[]{:S(2)}) collective-permute-start(bf16[512,1024]{1,0:T(8,128)(2,1)S(1)} %get-tuple-element.132), channel_id=1, source_target_pairs={{0,16},{1,17},{2,18},{3,19},{4,20},{5,21},{6,22},{7,23},{8,24},{9,... | collective-permute-start | bytes 3145736 | tf_op jit(solution)/shard_map/ppermute | solution.py:28
  241.0 2.7 collective-permute-start.27
  264.4 2.7 collective-permute-start.28
  270.5 2.7 collective-permute-start.29
  287.6 2.7 collective-permute-start.30
  294.5 2.7 collective-permute-start.31
  308.9 2.7 collective-permute-start.32
  315.6 2.7 collective-permute-start.33
  353.6 2.7 collective-permute-start.34
  358.5 27.2 %collective-permute-start.35 = (bf16[512,1024]{1,0:T(8,128)(2,1)S(1)}, bf16[512,1024]{1,0:T(8,128)(2,1)S(1)}, u32[]{:S(2)}, u32[]{:S(2)}) collective-permute-start(bf16[512,1024]{1,0:T(8,128)(2,1)S(1)} %get-tuple-element.131), channel_id=1, source_target_pairs={{16,0},{17,1},{18,2},{19,3},{20,4},{21,5},{22,6},{23,7},{24,8},{25... | collective-permute-start | bytes 3145736 | tf_op jit(solution)/shard_map/ppermute | solution.py:28
  361.3 31.3 %all-to-all-start.1 = ((bf16[4,128,1024]{2,1,0:T(8,128)(2,1)}), bf16[4,128,1024]{2,1,0:T(8,128)(2,1)}, u32[]{:S(2)}, u32[]{:S(2)}) async-start(bf16[4,128,1024]{2,1,0:T(8,128)(2,1)} %bitcast.41), calls=%async_computation.1 | async-start | bytes 2097152 | tf_op jit(solution)/shard_map/all_to_all | solution.py:1208
  389.8 2.8 collective-permute-start.36
  415.0 2.7 collective-permute-start.37
  415.2 26.0 %collective-permute-start.41 = (bf16[1024,512]{1,0:T(8,128)(2,1)S(1)}, bf16[1024,512]{1,0:T(8,128)(2,1)S(1)}, u32[]{:S(2)}, u32[]{:S(2)}) collective-permute-start(bf16[1024,512]{1,0:T(8,128)(2,1)S(1)} %get-tuple-element.149), channel_id=1, source_target_pairs={{0,8},{4,12},{8,0},{12,4},{1,9},{5,13},{9,1},{13,5},{2,10},{6,14},... | collective-permute-start | bytes 3145736 | tf_op jit(solution)/shard_map/ppermute | solution.py:798
  422.7 34.4 %collective-permute-start.39 = (bf16[512,1024]{1,0:T(8,128)(2,1)}, bf16[512,1024]{1,0:T(8,128)(2,1)S(1)}, u32[]{:S(2)}, u32[]{:S(2)}) collective-permute-start(bf16[512,1024]{1,0:T(8,128)(2,1)} %get-tuple-element.141.refs_2_.refs_3_.refs_5_), channel_id=1, source_target_pairs={{0,4},{4,0},{8,12},{12,8},{1,5},{5,1},{9,13},{13,9},{2,6},{6,2},{1... | collective-permute-start | bytes 3145736 | tf_op jit(solution)/shard_map/ppermute | solution.py:798
  424.2 2.0 collective-permute-start.38
  424.7 46.7 %collective-permute-start.40 = (bf16[1024,512]{1,0:T(8,128)(2,1)S(1)}, bf16[1024,512]{1,0:T(8,128)(2,1)S(1)}, u32[]{:S(2)}, u32[]{:S(2)}) collective-permute-start(bf16[1024,512]{1,0:T(8,128)(2,1)S(1)} %get-tuple-element.148), channel_id=1, source_target_pairs={{0,8},{4,12},{8,0},{12,4},{1,9},{5,13},{9,1},{13,5},{2,10},{6,14},... | collective-permute-start | bytes 3145736 | tf_op jit(solution)/shard_map/ppermute | solution.py:798
  441.6 29.9 %collective-permute-start.42 = (bf16[1024,512]{1,0:T(8,128)(2,1)S(1)}, bf16[1024,512]{1,0:T(8,128)(2,1)S(1)}, u32[]{:S(2)}, u32[]{:S(2)}) collective-permute-start(bf16[1024,512]{1,0:T(8,128)(2,1)S(1)} %moved.6.refs_13_), channel_id=1, source_target_pairs={{0,3},{1,0},{2,1},{3,2},{4,7},{5,4},{6,5},{7,6},{8,11},{9,8},{10,9... | collective-permute-start | bytes 3145736 | tf_op jit(solution)/shard_map/ppermute | solution.py:803
  455.0 41.6 %collective-permute-start.44 = (bf16[1024,512]{1,0:T(8,128)(2,1)S(1)}, bf16[1024,512]{1,0:T(8,128)(2,1)S(1)}, u32[]{:S(2)}, u32[]{:S(2)}) collective-permute-start(bf16[1024,512]{1,0:T(8,128)(2,1)S(1)} %get-tuple-element.154), channel_id=1, source_target_pairs={{0,8},{4,12},{8,0},{12,4},{1,9},{5,13},{9,1},{13,5},{2,10},{6,14},... | collective-permute-start | bytes 3145736 | tf_op jit(solution)/shard_map/ppermute | solution.py:798
  455.5 64.0 %collective-permute-start.47 = (bf16[1024,512]{1,0:T(8,128)(2,1)S(1)}, bf16[1024,512]{1,0:T(8,128)(2,1)S(1)}, u32[]{:S(2)}, u32[]{:S(2)}) collective-permute-start(bf16[1024,512]{1,0:T(8,128)(2,1)S(1)} %get-tuple-element.156), channel_id=1, source_target_pairs={{0,8},{4,12},{8,0},{12,4},{1,9},{5,13},{9,1},{13,5},{2,10},{6,14},... | collective-permute-start | bytes 3145736 | tf_op jit(solution)/shard_map/ppermute | solution.py:798
  472.8 23.9 %collective-permute-start.45 = (bf16[1024,512]{1,0:T(8,128)(2,1)S(1)}, bf16[1024,512]{1,0:T(8,128)(2,1)S(1)}, u32[]{:S(2)}, u32[]{:S(2)}) collective-permute-start(bf16[1024,512]{1,0:T(8,128)(2,1)S(1)} %moved.7.refs_13_), channel_id=1, source_target_pairs={{0,3},{1,0},{2,1},{3,2},{4,7},{5,4},{6,5},{7,6},{8,11},{9,8},{10,9... | collective-permute-start | bytes 3145736 | tf_op jit(solution)/shard_map/ppermute | solution.py:803
  497.2 23.5 %collective-permute-start.46 = (bf16[1024,512]{1,0:T(8,128)(2,1)S(1)}, bf16[1024,512]{1,0:T(8,128)(2,1)S(1)}, u32[]{:S(2)}, u32[]{:S(2)}) collective-permute-start(bf16[1024,512]{1,0:T(8,128)(2,1)S(1)} %moved.8.refs_13_), channel_id=1, source_target_pairs={{0,3},{1,0},{2,1},{3,2},{4,7},{5,4},{6,5},{7,6},{8,11},{9,8},{10,9... | collective-permute-start | bytes 3145736 | tf_op jit(solution)/shard_map/ppermute | solution.py:803
  500.6 18.7 %collective-permute-start.43 = (bf16[512,512]{1,0:T(8,128)(2,1)S(1)}, bf16[512,512]{1,0:T(8,128)(2,1)S(1)}, u32[]{:S(2)}, u32[]{:S(2)}) collective-permute-start(bf16[512,512]{1,0:T(8,128)(2,1)S(1)} %get-tuple-element.153), channel_id=1, source_target_pairs={{0,8},{4,12},{8,0},{12,4},{1,9},{5,13},{9,1},{13,5},{2,10},{6,14},... | collective-permute-start | bytes 1572872 | tf_op jit(solution)/shard_map/ppermute | solution.py:798
  527.5 14.4 %collective-permute-start.48 = (bf16[512,1024]{1,0:T(8,128)(2,1)S(1)}, bf16[512,1024]{1,0:T(8,128)(2,1)S(1)}, u32[]{:S(2)}, u32[]{:S(2)}) collective-permute-start(bf16[512,1024]{1,0:T(8,128)(2,1)S(1)} %get-tuple-element.158), channel_id=1, source_target_pairs={{0,4},{4,0},{8,12},{12,8},{1,5},{5,1},{9,13},{13,9},{2,6},{6,2},{1... | collective-permute-start | bytes 3145736 | tf_op jit(solution)/shard_map/ppermute | solution.py:798
  527.6 14.3 %collective-permute-start.49 = (bf16[512,512]{1,0:T(8,128)(2,1)S(1)}, bf16[512,512]{1,0:T(8,128)(2,1)S(1)}, u32[]{:S(2)}, u32[]{:S(2)}) collective-permute-start(bf16[512,512]{1,0:T(8,128)(2,1)S(1)} %get-tuple-element.160), channel_id=1, source_target_pairs={{0,8},{4,12},{8,0},{12,4},{1,9},{5,13},{9,1},{13,5},{2,10},{6,14},... | collective-permute-start | bytes 1572872 | tf_op jit(solution)/shard_map/ppermute | solution.py:798
  547.3 53.9 %all-to-all-start.2 = ((bf16[4,128,1024]{2,1,0:T(8,128)(2,1)}), bf16[4,128,1024]{2,1,0:T(8,128)(2,1)S(1)}, u32[]{:S(2)}, u32[]{:S(2)}) async-start(bf16[4,128,1024]{2,1,0:T(8,128)(2,1)} %bitcast.40), calls=%async_computation.2 | async-start | bytes 2097152 | tf_op jit(solution)/shard_map/all_to_all | solution.py:1280
  552.3 15.1 %collective-permute-start.50 = (bf16[512,512]{1,0:T(8,128)(2,1)}, bf16[512,512]{1,0:T(8,128)(2,1)S(1)}, u32[]{:S(2)}, u32[]{:S(2)}) collective-permute-start(bf16[512,512]{1,0:T(8,128)(2,1)} %copy-done.127), channel_id=1, source_target_pairs={{0,8},{4,12},{8,0},{12,4},{1,9},{5,13},{9,1},{13,5},{2,10},{6,14},... | collective-permute-start | bytes 1572872 | tf_op jit(solution)/shard_map/ppermute | solution.py:798
  552.8 29.8 %collective-permute-start.51 = (bf16[512,512]{1,0:T(8,128)(2,1)}, bf16[512,512]{1,0:T(8,128)(2,1)S(1)}, u32[]{:S(2)}, u32[]{:S(2)}) collective-permute-start(bf16[512,512]{1,0:T(8,128)(2,1)} %copy-done.120), channel_id=1, source_target_pairs={{0,3},{1,0},{2,1},{3,2},{4,7},{5,4},{6,5},{7,6},{8,11},{9,8},{10,9... | collective-permute-start | bytes 1572872 | tf_op jit(solution)/shard_map/ppermute | solution.py:803
  556.7 29.9 %collective-permute-start.55 = (bf16[512,512]{1,0:T(8,128)(2,1)}, bf16[512,512]{1,0:T(8,128)(2,1)S(1)}, u32[]{:S(2)}, u32[]{:S(2)}) collective-permute-start(bf16[512,512]{1,0:T(8,128)(2,1)} %copy-done.126), channel_id=1, source_target_pairs={{0,8},{4,12},{8,0},{12,4},{1,9},{5,13},{9,1},{13,5},{2,10},{6,14},... | collective-permute-start | bytes 1572872 | tf_op jit(solution)/shard_map/ppermute | solution.py:798
  560.9 24.2 %collective-permute-start.53 = (f32[256,512]{1,0:T(8,128)S(1)}, f32[256,512]{1,0:T(8,128)S(1)}, u32[]{:S(2)}, u32[]{:S(2)}) collective-permute-start(f32[256,512]{1,0:T(8,128)S(1)} %get-tuple-element.167), channel_id=1, source_target_pairs={{0,4},{4,0},{8,12},{12,8},{1,5},{5,1},{9,13},{13,9},{2,6},{6,2},{1... | collective-permute-start | bytes 1572872 | tf_op jit(solution)/shard_map/ppermute | solution.py:798
  561.0 24.1 %collective-permute-start.54 = (f32[512,256]{1,0:T(8,128)S(1)}, f32[512,256]{1,0:T(8,128)S(1)}, u32[]{:S(2)}, u32[]{:S(2)}) collective-permute-start(f32[512,256]{1,0:T(8,128)S(1)} %get-tuple-element.168), channel_id=1, source_target_pairs={{0,4},{4,0},{8,12},{12,8},{1,5},{5,1},{9,13},{13,9},{2,6},{6,2},{1... | collective-permute-start | bytes 1572872 | tf_op jit(solution)/shard_map/ppermute | solution.py:798
  582.9 18.3 %collective-permute-start.52 = (bf16[512,512]{1,0:T(8,128)(2,1)S(1)}, bf16[512,512]{1,0:T(8,128)(2,1)S(1)}, u32[]{:S(2)}, u32[]{:S(2)}) collective-permute-start(bf16[512,512]{1,0:T(8,128)(2,1)S(1)} %moved.10), channel_id=1, source_target_pairs={{0,3},{1,0},{2,1},{3,2},{4,7},{5,4},{6,5},{7,6},{8,11},{9,8},{10,9... | collective-permute-start | bytes 1572872 | tf_op jit(solution)/shard_map/ppermute | solution.py:803
  605.4 19.6 %collective-permute-start.56 = (bf16[2,128,1024]{2,1,0:T(8,128)(2,1)}, bf16[2,128,1024]{2,1,0:T(8,128)(2,1)S(1)}, u32[]{:S(2)}, u32[]{:S(2)}) collective-permute-start(bf16[2,128,1024]{2,1,0:T(8,128)(2,1)} %get-tuple-element.172), channel_id=1, source_target_pairs={{0,4},{4,0},{8,12},{12,8},{1,5},{5,1},{9,13},{13,9},{2,6},{6,2},{1... | collective-permute-start | bytes 1572872 | tf_op jit(solution)/shard_map/ppermute | solution.py:798
  605.4 20.6 %collective-permute-start.57 = (bf16[512,512]{1,0:T(8,128)(2,1)}, bf16[512,512]{1,0:T(8,128)(2,1)S(1)}, u32[]{:S(2)}, u32[]{:S(2)}) collective-permute-start(bf16[512,512]{1,0:T(8,128)(2,1)} %copy-done.33), channel_id=1, source_target_pairs={{0,3},{1,0},{2,1},{3,2},{4,7},{5,4},{6,5},{7,6},{8,11},{9,8},{10,9... | collective-permute-start | bytes 1572872 | tf_op jit(solution)/shard_map/ppermute | solution.py:803
  626.2 2.0 collective-permute-start.58
  (134 other events, 1302.7 us)

commit v14 on v13

--- a/solution.py
+++ b/solution.py
@@ -970,6 +970,18 @@
                 down_out[spot] = down[...]
 
 
+def chosen_kernel(place_ref, zero_ref, one_ref, out_ref):
+    half = out_ref.shape[1] // 2
+    for section, rows_ref in enumerate((zero_ref, one_ref)):
+        for upper in range(2):
+
+            @pl.when(jnp.logical_and(place_ref[0] == section, place_ref[1] == upper))
+            def _():
+                for side in range(2):
+                    place = (side + upper) % 2 * half
+                    out_ref[:, place : place + half] = rows_ref[:, side * half : (side + 1) * half]
+
+
 def pick_kernel(core_ref, rows_ref, keep_ref, send_ref):
     count = keep_ref.shape[0]
     keep_ref[...] = rows_ref[pl.ds(core_ref[0] * count, count)]
@@ -1094,13 +1106,17 @@
             pieces.append(passed_on(pieces[-1], 1))
         return pieces
 
-    attn_own = spread(attn_piece)
-    attn_other = [flip_pairs(piece, 2) for piece in attn_own]
     up_piece, down_piece = columns(up_weight[0]), rows(down_weight[0])
     up_other, down_other = [flip_pairs(up_piece, 2)], [flip_pairs(down_piece, 2)]
+    attn_own = [attn_piece, passed_on(attn_piece, 1)]
+    attn_first = flip_pairs(attn_piece, 2)
+    outs = ((attn_piece.shape, attn_piece.dtype),)
+    attn_own[1] = on_chip(gate_kernel, "gate", outs, attn_own[1], waits=(attn_first, up_other[0]))[0]
+    attn_own += spread(attn_own[1])[1:-1]
+    attn_other = [attn_first] + [flip_pairs(piece, 2) for piece in attn_own[1:]]
     outs = tuple((piece.shape, piece.dtype) for piece in (up_piece, down_piece))
     up_piece, down_piece = on_chip(
-        gates_kernel, "gate", outs, up_piece, down_piece, waits=(attn_own[2], attn_other[0])
+        gates_kernel, "gate", outs, up_piece, down_piece, waits=(attn_own[2], attn_other[0], down_other[0])
     )
     up_own, down_own = spread(up_piece), spread(down_piece)
     up_other += [flip_pairs(piece, 2) for piece in up_own[1:]]
@@ -1276,8 +1292,17 @@
 
     d_down = d_up = d_attn = outputs = None
     grad_zero, rights_zero, gain_zero = backward(received, saved_zero, hook, (lows,))
-    grads = own_first(jnp.where(first, grad_zero, grad_one)).reshape(tensor, part, width)
-    grads = lax.all_to_all(grads, "tensor", 0, 0, tiled=True)
+    place_word = jnp.stack([lax.axis_index("section"), upper]).astype(jnp.int32)
+    (grads,) = with_core(
+        chosen_kernel,
+        "chosen",
+        place_word,
+        (row16,),
+        grad_zero,
+        grad_one,
+        waits=(attn_moves[3], attn_sums[1][1]),
+    )
+    grads = lax.all_to_all(grads.reshape(tensor, part, width), "tensor", 0, 0, tiled=True)
 
     block32 = ((wide_half // 2, unit), jnp.float32)
     down32 = ((unit, wide_half // 2), jnp.float32)
@@ -1288,6 +1313,7 @@
         (block32, down32, block32, down32),
         *mlp_sums[0],
         mlp_moves[1],
+        waits=(grad_zero,),
     )
     outs = (
         ((wide_half // 2, 2 * unit), jnp.float32),
@@ -1297,7 +1323,7 @@
     up_grad, down_grad = with_core(
         mlp_join_kernel, "mlp_join", core_word, outs, up_keep, down_keep, *sent
     )
-    total, attn_moves[2] = moves_on(attn_sums[2], attn_moves[3], waits=(grad_zero, attn_sums[1][1]))
+    total, attn_moves[2] = moves_on(attn_sums[2], attn_moves[3], waits=(grad_zero,))
     waits = (up_grad, attn_sums[0][1], grads)
     last, attn_moves[1] = moves_on(attn_sums[1], attn_moves[2], waits=waits)
     grads = from_chip(grads, (last,))

time: 642 us -> 627 us (0.977)
  waiting for transfers between devices: 248 us -> 226 us
    ppermute x15, waiting for transfers between devices: 92.3 us -> 80.3 us  [passed_on(): lax.ppermute(block, 'tensor', [(i, (i + step) % size) for i in range(size)])]
    ppermute x42, waiting for transfers between devices: 112 us -> 102 us  [flip_pairs(): return lax.ppermute(block, 'dp', [(i, i ^ distance) for i in range(size)])]
    ppermute x15, starting transfers between devices: 29 us -> 35.7 us  [passed_on(): lax.ppermute(block, 'tensor', [(i, (i + step) % size) for i in range(size)])]
    pallas_call x30 -> x31, Pallas kernels: 85.1 us -> 86.2 us  [on_chip(): pl.pallas_call(without(kernel, len(operands), len(waits)), in_specs=[spac...]
    unnamed x276 -> x290, local copies, waits for them, and re-layouts: 48.6 us -> 47.9 us
  transfers between devices with their start and end apart: 62 -> 62, of which waited for: 36 -> 36; matrix products, arithmetic and copies ran while one was open for 3% -> 4% of each run, Pallas kernels for 14% -> 14%
where the time goes in v14:
time: 627 us; the launch traced here: 617 us
  waiting for transfers between devices  226 us (36%)
  Pallas kernels  221 us (35%)
  starting transfers between devices  80.3 us (13%)
  local copies, waits for them, and re-layouts  58.7 us (9%)
  other arithmetic  19.3 us (3%)
  blocking collectives  9.02 us (1%)
    ppermute x42, waiting for transfers between devices, flip_pairs(): return lax.ppermute(block, 'dp', [(i, i ^ distance) for i in range(size)])  102 us
    pallas_call x31, Pallas kernels, on_chip(): pl.pallas_call(without(kernel, len(operands), len(waits)), in_specs=[spac...  86.2 us
    pallas_call x6, Pallas kernels, by_pairs(): pl.pallas_call(without(functools.partial(kernel, len(pieces[0])), taken,...  85.8 us
    ppermute x15, waiting for transfers between devices, passed_on(): lax.ppermute(block, 'tensor', [(i, (i + step) % size) for i in range(size)])  80.3 us
    unnamed x290, local copies, waits for them, and re-layouts  47.9 us
    ppermute x2, waiting for transfers between devices, shifted(): return lax.ppermute(block, axis, route)  41.5 us
    ppermute x15, starting transfers between devices, passed_on(): lax.ppermute(block, 'tensor', [(i, (i + step) % size) for i in range(size)])  35.7 us
    pallas_call x4, Pallas kernels, weight_grads(): pl.pallas_call(without(functools.partial(kernel, base), 1 + len(arrays),...  26 us
  transfers between devices with their start and end apart: 62, of which 36 were waited for; matrix products, arithmetic and copies ran while one was open for 4% of the time, Pallas kernels for 14%

profile of v14, /device:TPU:0, one launch (start us, length us, event | category | flops | bytes accessed | tf_op | source)
XLA Modules:
  0.0 617.2 jit_solution(11032649441012522109)
XLA Ops:
  11.4 6.2 %all-to-all-start = ((bf16[4,128,1024]{2,1,0:T(8,128)(2,1)}), bf16[4,128,1024]{2,1,0:T(8,128)(2,1)S(1)}, u32[]{:S(2)}, u32[]{:S(2)}) async-start(bf16[4,128,1024]{2,1,0:T(8,128)(2,1)} %pad_maximum_fusion), calls=%async_computation | async-start | bytes 2097152 | tf_op jit(solution)/shard_map/all_to_all | solution.py:1071
  28.9 21.5 %collective-permute-done.1.refs_0_ = bf16[512,512]{1,0:T(8,128)(2,1)} collective-permute-done((bf16[512,512]{1,0:T(8,128)(2,1)}, bf16[512,512]{1,0:T(8,128)(2,1)}, u32[]{:S(2)}, u32[]{:S(2)}) %collective-permute-start.1) | collective-permute-done | bytes 524320 | tf_op jit(solution)/shard_map/ppermute | solution.py:803
  59.5 8.8 %collective-permute-done.4.refs_2_.refs_7_.refs_3_.refs_5_.refs_4_ = bf16[512,512]{1,0:T(8,128)(2,1)S(1)} collective-permute-done((bf16[512,512]{1,0:T(8,128)(2,1)}, bf16[512,512]{1,0:T(8,128)(2,1)S(1)}, u32[]{:S(2)}, u32[]{:S(2)}) %collective-permute-start.4) | collective-permute-done | bytes 524320 | tf_op jit(solution)/shard_map/ppermute | solution.py:803
  69.5 2.9 collective-permute-done.5.refs_4_.refs_5_.refs_7_
  76.8 2.5 collective-permute-start.11
  86.2 7.3 %collective-permute-done.11.refs_13_.refs_3_.refs_2_ = bf16[512,512]{1,0:T(8,128)(2,1)S(1)} collective-permute-done((bf16[512,512]{1,0:T(8,128)(2,1)}, bf16[512,512]{1,0:T(8,128)(2,1)S(1)}, u32[]{:S(2)}, u32[]{:S(2)}) %collective-permute-start.11) | collective-permute-done | bytes 524320 | tf_op jit(solution)/shard_map/ppermute | solution.py:803
  97.8 7.0 %collective-permute-done.12.refs_14_.refs_2_.refs_4_ = bf16[512,512]{1,0:T(8,128)(2,1)S(1)} collective-permute-done((bf16[512,512]{1,0:T(8,128)(2,1)}, bf16[512,512]{1,0:T(8,128)(2,1)S(1)}, u32[]{:S(2)}, u32[]{:S(2)}) %collective-permute-start.12) | collective-permute-done | bytes 524320 | tf_op jit(solution)/shard_map/ppermute | solution.py:803
  109.0 16.9 %attend.2 = (bf16[4,1024,128]{2,1,0:T(8,128)(2,1)S(1)}, bf16[4,1024,128]{2,1,0:T(8,128)(2,1)S(1)}, bf16[4,1024,128]{2,1,0:T(8,128)(2,1)S(1)}, f32[4,2,1024]{2,1,0:T(2,128)S(1)}, bf16[1024,512]{1,0:T(8,128)(2,1)S(1)}) custom-call(s32[1]{0:T(128)} %bitcast.refs_0_, f32[1024,128]{1,0:T(8,128)S(1)} %get-tuple-element.228.refs_1_, ...), custom_call_target="tpu_custom_call" | custom-call | flops 11811160064 | bytes 11567104 | tf_op jit(solution)/shard_map/attend/pallas_call | solution.py:708
  130.3 3.0 attn_out.2
  133.3 2.5 collective-permute-start.18
  138.4 11.7 %collective-permute-done.18.refs_4_.refs_5_ = bf16[512,512]{1,0:T(8,128)(2,1)S(1)} collective-permute-done((bf16[512,512]{1,0:T(8,128)(2,1)}, bf16[512,512]{1,0:T(8,128)(2,1)S(1)}, u32[]{:S(2)}, u32[]{:S(2)}) %collective-permute-start.18) | collective-permute-done | bytes 524320 | tf_op jit(solution)/shard_map/ppermute | solution.py:803
  150.1 10.8 %collective-permute-done.19.refs_5_.refs_4_.refs_6_ = bf16[512,512]{1,0:T(8,128)(2,1)S(1)} collective-permute-done((bf16[512,512]{1,0:T(8,128)(2,1)}, bf16[512,512]{1,0:T(8,128)(2,1)S(1)}, u32[]{:S(2)}, u32[]{:S(2)}) %collective-permute-start.19) | collective-permute-done | bytes 524320 | tf_op jit(solution)/shard_map/ppermute | solution.py:803
  162.4 3.4 after_attn.2
  169.4 12.9 %collective-permute-done.23.refs_9_.refs_8_ = bf16[512,512]{1,0:T(8,128)(2,1)S(1)} collective-permute-done((bf16[512,512]{1,0:T(8,128)(2,1)}, bf16[512,512]{1,0:T(8,128)(2,1)S(1)}, u32[]{:S(2)}, u32[]{:S(2)}) %collective-permute-start.23) | collective-permute-done | bytes 524320 | tf_op jit(solution)/shard_map/ppermute | solution.py:798
  184.6 7.7 %mlp_up.2 = (bf16[1024,2048]{1,0:T(8,128)(2,1)S(1)}, bf16[1024,2048]{1,0:T(8,128)(2,1)S(1)}) custom-call(bf16[512,1024]{1,0:T(8,128)(2,1)S(1)} %get-tuple-element.103.refs_0_.refs_1_, bf16[512,1024]{1,0:T(8,128)(2,1)S(1)} %collective-permute-done.22.refs_1_.refs_2_, bf16[512,512]{1,0:T(8,128)(2,1)S(1)} %copy-done.114, bf16[512,512]{1,0:T(8,128)(2,1)S(1)} %copy-done.129, ...), custom_call_target="tpu_custom_call" | custom-call | flops 4294967296 | bytes 14680064 | tf_op jit(solution)/shard_map/mlp_up/pallas_call | solution.py:690
  194.4 4.5 mlp_down.2
  198.9 2.6 collective-permute-done.25.refs_3_
  203.5 3.6 collective-permute-start.26
  207.1 22.2 %collective-permute-done.26.refs_1_ = bf16[512,1024]{1,0:T(8,128)(2,1)S(1)} collective-permute-done((bf16[512,1024]{1,0:T(8,128)(2,1)S(1)}, bf16[512,1024]{1,0:T(8,128)(2,1)S(1)}, u32[]{:S(2)}, u32[]{:S(2)}) %collective-permute-start.26) | collective-permute-done | bytes 1048608 | tf_op jit(solution)/shard_map/ppermute | solution.py:28
  231.1 2.6 collective-permute-done.27.refs_4_.refs_8_
  233.8 16.9 %attend.3 = (bf16[4,1024,128]{2,1,0:T(8,128)(2,1)S(1)}, bf16[4,1024,128]{2,1,0:T(8,128)(2,1)S(1)}, bf16[4,1024,128]{2,1,0:T(8,128)(2,1)S(1)}, f32[4,2,1024]{2,1,0:T(2,128)S(1)}, bf16[1024,512]{1,0:T(8,128)(2,1)S(1)}) custom-call(s32[1]{0:T(128)} %bitcast.refs_0_, f32[1024,128]{1,0:T(8,128)S(1)} %get-tuple-element.228.refs_1_, ...), custom_call_target="tpu_custom_call" | custom-call | flops 11811160064 | bytes 11567104 | tf_op jit(solution)/shard_map/attend/pallas_call | solution.py:708
  250.7 3.3 attn_out.3
  254.3 2.5 collective-permute-done.28.refs_3_
  256.8 3.4 after_attn.3
  260.4 2.5 collective-permute-done.29.refs_1_.refs_8_
  263.0 7.7 %mlp_up.3 = (bf16[1024,2048]{1,0:T(8,128)(2,1)S(1)}, bf16[1024,2048]{1,0:T(8,128)(2,1)S(1)}) custom-call(bf16[512,1024]{1,0:T(8,128)(2,1)S(1)} %get-tuple-element.112.refs_0_.refs_7_, bf16[512,1024]{1,0:T(8,128)(2,1)S(1)} %collective-permute-done.29.refs_1_.refs_8_, bf16[512,512]{1,0:T(8,128)(2,1)S(1)} %copy-done.114, bf16[512,512]{1,0:T(8,128)(2,1)S(1)} %copy-done.129, ...), custom_call_target="tpu_custom_call" | custom-call | flops 4294967296 | bytes 14680064 | tf_op jit(solution)/shard_map/mlp_up/pallas_call | solution.py:690
  272.7 4.5 mlp_down.3
  277.4 2.5 collective-permute-done.30.refs_3_
  284.3 2.5 collective-permute-done.31.refs_1_.refs_12_
  286.9 7.2 %mlp_up_back.2.refs_0_.refs_9_ = bf16[1024,2048]{1,0:T(8,128)(2,1)S(1)} custom-call(bf16[512,1024]{1,0:T(8,128)(2,1)S(1)} %get-tuple-element.118.refs_0_.refs_11_, bf16[512,1024]{1,0:T(8,128)(2,1)S(1)} %collective-permute-done.31.refs_1_.refs_12_, bf16[1024,2048]{1,0:T(8,128)(2,1)} %copy-done.39, bf16[512,512]{1,0:T(8,128)(2,1)} %copy-done.61, ...), custom_call_target="tpu_custom_call" | custom-call | tf_op jit(solution)/shard_map/mlp_up_back/pallas_call | solution.py:729
  294.1 4.5 mlp_back.2
  298.8 2.5 collective-permute-done.32.refs_3_
  301.4 3.9 into_attn_back.2
  305.5 2.5 collective-permute-done.33.refs_4_.refs_12_
  308.0 13.1 %attend_back.4.refs_0_.refs_9_ = bf16[1024,768]{1,0:T(8,128)(2,1)S(1)} custom-call(s32[1]{0:T(128)} %bitcast.refs_0_, f32[1024,128]{1,0:T(8,128)S(1)} %get-tuple-element.228.refs_1_, f32[1024,128]{1,0:T(8,128)S(1)} %get-tuple-element.229.refs_2_, bf16[512,1024]{1,0:T(8,128)(2,1)S(1)} %get-tuple-element.123.refs_3_.refs_11_, ...), custom_call_target="tpu_custom_call" | custom-call | flops 11274289152 | bytes 6815744 | tf_op jit(solution)/shard_map/attend_back/pallas_call | solution.py:708
  321.2 12.8 %attend_back.5.refs_1_.refs_9_ = bf16[1024,768]{1,0:T(8,128)(2,1)S(1)} custom-call(s32[1]{0:T(128)} %bitcast.refs_0_, f32[1024,128]{1,0:T(8,128)S(1)} %get-tuple-element.228.refs_1_, f32[1024,128]{1,0:T(8,128)S(1)} %get-tuple-element.229.refs_2_, bf16[512,1024]{1,0:T(8,128)(2,1)S(1)} %get-tuple-element.123.refs_3_.refs_11_, ...), custom_call_target="tpu_custom_call" | custom-call | flops 11274289152 | bytes 6815744 | tf_op jit(solution)/shard_map/attend_back/pallas_call | solution.py:708
  335.6 5.7 attn_back.2
  341.5 2.5 collective-permute-done.34.refs_3_
  349.1 5.1 all-to-all-start.1
  354.3 19.2 %collective-permute-done.35.refs_1_ = bf16[512,1024]{1,0:T(8,128)(2,1)S(1)} collective-permute-done((bf16[512,1024]{1,0:T(8,128)(2,1)S(1)}, bf16[512,1024]{1,0:T(8,128)(2,1)S(1)}, u32[]{:S(2)}, u32[]{:S(2)}) %collective-permute-start.35) | collective-permute-done | bytes 1048608 | tf_op jit(solution)/shard_map/ppermute | solution.py:28
  377.7 2.7 all-to-all-done.1.refs_11_.refs_1_
  380.4 7.2 %mlp_up_back.3.refs_3_.refs_0_ = bf16[1024,2048]{1,0:T(8,128)(2,1)S(1)} custom-call(bf16[512,1024]{1,0:T(8,128)(2,1)S(1)} %get-tuple-element.135.refs_0_.refs_5_, bf16[512,1024]{1,0:T(8,128)(2,1)S(1)} %collective-permute-done.36.refs_1_.refs_6_, bf16[1024,2048]{1,0:T(8,128)(2,1)} %copy-done.54, bf16[512,512]{1,0:T(8,128)(2,1)} %copy-done.61, ...), custom_call_target="tpu_custom_call" | custom-call | tf_op jit(solution)/shard_map/mlp_up_back/pallas_call | solution.py:729
  389.6 7.2 %mlp_grads.2 = (f32[1024,512]{1,0:T(8,128)S(1)}, bf16[1024,512]{1,0:T(8,128)(2,1)S(1)}, f32[1024,512]{1,0:T(8,128)S(1)}, bf16[1024,512]{1,0:T(8,128)(2,1)S(1)}) custom-call(s32[1]{0:T(128)} %bitcast.12.refs_0_, bf16[512,1024]{1,0:T(8,128)(2,1)} %copy-done.41, bf16[512,1024]{1,0:T(8,128)(2,1)} %copy-done.42, bf16[1024,2048]{1,0:T(8,128)(2,1)} %copy-done.3, ...), custom_call_target="tpu_custom_call" | custom-call | tf_op jit(solution)/shard_map/mlp_grads/pallas_call | solution.py:897
  398.3 4.5 mlp_back.3
  405.5 4.9 into_attn_back.3
  415.0 13.9 %collective-permute-done.41.refs_1_ = bf16[1024,512]{1,0:T(8,128)(2,1)S(1)} collective-permute-done((bf16[1024,512]{1,0:T(8,128)(2,1)S(1)}, bf16[1024,512]{1,0:T(8,128)(2,1)S(1)}, u32[]{:S(2)}, u32[]{:S(2)}) %collective-permute-start.41) | collective-permute-done | bytes 1048608 | tf_op jit(solution)/shard_map/ppermute | solution.py:798
  429.4 3.7 collective-permute-start.42
  433.1 7.0 %mlp_grads.3 = (f32[1024,512]{1,0:T(8,128)S(1)}, bf16[1024,512]{1,0:T(8,128)(2,1)S(1)}, f32[1024,512]{1,0:T(8,128)S(1)}, bf16[1024,512]{1,0:T(8,128)(2,1)S(1)}) custom-call(s32[1]{0:T(128)} %bitcast.12.refs_0_, bf16[512,1024]{1,0:T(8,128)(2,1)} %copy-done.41, bf16[512,1024]{1,0:T(8,128)(2,1)} %copy-done.42, bf16[1024,2048]{1,0:T(8,128)(2,1)} %copy-done.3, ...), custom_call_target="tpu_custom_call" | custom-call | tf_op jit(solution)/shard_map/mlp_grads/pallas_call | solution.py:897
  444.9 12.9 %attend_back.6.refs_3_.refs_1_ = bf16[1024,768]{1,0:T(8,128)(2,1)S(1)} custom-call(s32[1]{0:T(128)} %bitcast.refs_0_, f32[1024,128]{1,0:T(8,128)S(1)} %copy-done.110, f32[1024,128]{1,0:T(8,128)S(1)} %copy-done.112, bf16[512,1024]{1,0:T(8,128)(2,1)} %get-tuple-element.141.refs_2_.refs_3_.refs_5_, ...), custom_call_target="tpu_custom_call" | custom-call | flops 11274289152 | bytes 6815744 | tf_op jit(solution)/shard_map/attend_back/pallas_call | solution.py:708
  462.0 5.9 attn_grads.2
  469.9 13.2 %attend_back.7.refs_3_.refs_0_ = bf16[1024,768]{1,0:T(8,128)(2,1)S(1)} custom-call(s32[1]{0:T(128)} %bitcast.refs_0_, f32[1024,128]{1,0:T(8,128)S(1)} %copy-done.110, f32[1024,128]{1,0:T(8,128)S(1)} %copy-done.112, bf16[512,1024]{1,0:T(8,128)(2,1)} %get-tuple-element.141.refs_2_.refs_3_.refs_5_, bf16[512,1024]{1,0:T(8,128)(2,1)S(1)} %copy-done.50, ...), custom_call_target="tpu_custom_call" | custom-call | flops 11274289152 | bytes 6815744 | tf_op jit(solution)/shard_map/attend_back/pallas_call | solution.py:708
  484.8 3.4 collective-permute-start.46
  488.6 5.9 attn_grads.3
  495.5 11.6 %collective-permute-done.43.refs_1_ = bf16[512,512]{1,0:T(8,128)(2,1)S(1)} collective-permute-done((bf16[512,512]{1,0:T(8,128)(2,1)S(1)}, bf16[512,512]{1,0:T(8,128)(2,1)S(1)}, u32[]{:S(2)}, u32[]{:S(2)}) %collective-permute-start.43) | collective-permute-done | bytes 524320 | tf_op jit(solution)/shard_map/ppermute | solution.py:798
  510.0 5.1 attn_back.3
  515.8 3.5 collective-permute-start.50
  520.9 9.2 %collective-permute-done.49.refs_5_.refs_1_ = bf16[512,512]{1,0:T(8,128)(2,1)S(1)} collective-permute-done((bf16[512,512]{1,0:T(8,128)(2,1)S(1)}, bf16[512,512]{1,0:T(8,128)(2,1)S(1)}, u32[]{:S(2)}, u32[]{:S(2)}) %collective-permute-start.49) | collective-permute-done | bytes 524320 | tf_op jit(solution)/shard_map/ppermute | solution.py:798
  533.0 7.8 %collective-permute-done.51.refs_4_.refs_1_ = bf16[512,512]{1,0:T(8,128)(2,1)S(1)} collective-permute-done((bf16[512,512]{1,0:T(8,128)(2,1)S(1)}, bf16[512,512]{1,0:T(8,128)(2,1)S(1)}, u32[]{:S(2)}, u32[]{:S(2)}) %collective-permute-start.51) | collective-permute-done | bytes 524320 | tf_op jit(solution)/shard_map/ppermute | solution.py:798
  543.2 4.9 all-to-all-start.2
  552.5 3.9 collective-permute-start.52
  557.9 7.5 %collective-permute-done.55.refs_4_.refs_2_ = bf16[512,512]{1,0:T(8,128)(2,1)S(1)} collective-permute-done((bf16[512,512]{1,0:T(8,128)(2,1)S(1)}, bf16[512,512]{1,0:T(8,128)(2,1)S(1)}, u32[]{:S(2)}, u32[]{:S(2)}) %collective-permute-start.55) | collective-permute-done | bytes 524320 | tf_op jit(solution)/shard_map/ppermute | solution.py:798
  565.4 13.0 %collective-permute-done.52.refs_2_ = bf16[512,512]{1,0:T(8,128)(2,1)S(1)} collective-permute-done((bf16[512,512]{1,0:T(8,128)(2,1)S(1)}, bf16[512,512]{1,0:T(8,128)(2,1)S(1)}, u32[]{:S(2)}, u32[]{:S(2)}) %collective-permute-start.52) | collective-permute-done | bytes 524320 | tf_op jit(solution)/shard_map/ppermute | solution.py:803
  584.3 7.2 %collective-permute-start.57 = (bf16[512,512]{1,0:T(8,128)(2,1)}, bf16[512,512]{1,0:T(8,128)(2,1)S(1)}, u32[]{:S(2)}, u32[]{:S(2)}) collective-permute-start(bf16[512,512]{1,0:T(8,128)(2,1)} %copy-done.38), channel_id=1, source_target_pairs={{0,3},{1,0},{2,1},{3,2},{4,7},{5,4},{6,5},{7,6},{8,11},{9,8},{10,9... | collective-permute-start | bytes 1572872 | tf_op jit(solution)/shard_map/ppermute | solution.py:803
  598.4 9.0 %all_to_all.20 = f32[16,1,256]{2,1,0:T(1,128)S(1)} all-to-all(f32[16,1,256]{2,1,0:T(1,128)S(1)} %reshape.144), channel_id=1, replica_groups=mesh['section'=2,'dp'=4,'tensor'=4] {'dp','tensor'}, dimensions={0} | all-to-all | bytes 32768 | tf_op jit(solution)/shard_map/all_to_all | solution.py:1335
  (457 shorter events, 153.9 us)
Async XLA Ops:
  7.2 2.1 collective-permute-start
  11.4 63.5 %all-to-all-start = ((bf16[4,128,1024]{2,1,0:T(8,128)(2,1)}), bf16[4,128,1024]{2,1,0:T(8,128)(2,1)S(1)}, u32[]{:S(2)}, u32[]{:S(2)}) async-start(bf16[4,128,1024]{2,1,0:T(8,128)(2,1)} %pad_maximum_fusion), calls=%async_computation | async-start | bytes 2097152 | tf_op jit(solution)/shard_map/all_to_all | solution.py:1071
  24.8 25.7 %collective-permute-start.1 = (bf16[512,512]{1,0:T(8,128)(2,1)}, bf16[512,512]{1,0:T(8,128)(2,1)}, u32[]{:S(2)}, u32[]{:S(2)}) collective-permute-start(bf16[512,512]{1,0:T(8,128)(2,1)} %pad_maximum_fusion.3.refs_5_.refs_1_.refs_2_), channel_id=1, source_target_pairs={{0,1},{1,2},{2,3},{3,0},{4,5},{5,6},{6,7},{7,4},{8,9},{9,10},{10,1... | collective-permute-start | bytes 1572872 | tf_op jit(solution)/shard_map/ppermute | solution.py:803
  26.8 23.7 %collective-permute-start.2 = (bf16[512,512]{1,0:T(8,128)(2,1)}, bf16[512,512]{1,0:T(8,128)(2,1)}, u32[]{:S(2)}, u32[]{:S(2)}) collective-permute-start(bf16[512,512]{1,0:T(8,128)(2,1)} %pad_maximum_fusion.3.refs_5_.refs_1_.refs_2_), channel_id=1, source_target_pairs={{0,8},{4,12},{8,0},{12,4},{1,9},{5,13},{9,1},{13,5},{2,10},{6,14},... | collective-permute-start | bytes 1572872 | tf_op jit(solution)/shard_map/ppermute | solution.py:798
  28.3 23.0 %collective-permute-start.3 = (bf16[512,512]{1,0:T(8,128)(2,1)S(1)}, bf16[512,512]{1,0:T(8,128)(2,1)S(1)}, u32[]{:S(2)}, u32[]{:S(2)}) collective-permute-start(bf16[512,512]{1,0:T(8,128)(2,1)S(1)} %dynamic-slice_bitcast_fusion.1.refs_0_), channel_id=1, source_target_pairs={{0,8},{4,12},{8,0},{12,4},{1,9},{5,13},{9,1},{13,5},{2,10},{6,14},... | collective-permute-start | bytes 1572872 | tf_op jit(solution)/shard_map/ppermute | solution.py:798
  54.0 14.3 %collective-permute-start.4 = (bf16[512,512]{1,0:T(8,128)(2,1)}, bf16[512,512]{1,0:T(8,128)(2,1)S(1)}, u32[]{:S(2)}, u32[]{:S(2)}) collective-permute-start(bf16[512,512]{1,0:T(8,128)(2,1)} %gate.3.refs_6_.refs_2_.refs_3_), channel_id=1, source_target_pairs={{0,1},{1,2},{2,3},{3,0},{4,5},{5,6},{6,7},{7,4},{8,9},{9,10},{10,1... | collective-permute-start | bytes 1572872 | tf_op jit(solution)/shard_map/ppermute | solution.py:803
  57.4 14.9 %collective-permute-start.5 = (bf16[512,512]{1,0:T(8,128)(2,1)S(1)}, bf16[512,512]{1,0:T(8,128)(2,1)S(1)}, u32[]{:S(2)}, u32[]{:S(2)}) collective-permute-start(bf16[512,512]{1,0:T(8,128)(2,1)S(1)} %dynamic-slice_bitcast_fusion.refs_1_), channel_id=1, source_target_pairs={{0,8},{4,12},{8,0},{12,4},{1,9},{5,13},{9,1},{13,5},{2,10},{6,14},... | collective-permute-start | bytes 1572872 | tf_op jit(solution)/shard_map/ppermute | solution.py:798
  59.0 22.4 %collective-permute-start.8 = (bf16[512,512]{1,0:T(8,128)(2,1)}, bf16[512,512]{1,0:T(8,128)(2,1)}, u32[]{:S(2)}, u32[]{:S(2)}) collective-permute-start(bf16[512,512]{1,0:T(8,128)(2,1)} %gate.3.refs_6_.refs_2_.refs_3_), channel_id=1, source_target_pairs={{0,8},{4,12},{8,0},{12,4},{1,9},{5,13},{9,1},{13,5},{2,10},{6,14},... | collective-permute-start | bytes 1572872 | tf_op jit(solution)/shard_map/ppermute | solution.py:798
  68.3 14.6 %collective-permute-start.7 = (bf16[512,512]{1,0:T(8,128)(2,1)S(1)}, bf16[512,512]{1,0:T(8,128)(2,1)}, u32[]{:S(2)}, u32[]{:S(2)}) collective-permute-start(bf16[512,512]{1,0:T(8,128)(2,1)S(1)} %collective-permute-done.4.refs_2_.refs_7_.refs_3_.refs_5_.refs_4_), channel_id=1, source_target_pairs={{0,1},{1,2},{2,3},{3,0},{4,5},{5,6},{6,7},{7,4},{8,9},{9,10},{10,1... | collective-permute-start | bytes 1572872 | tf_op jit(solution)/shard_map/ppermute | solution.py:803
  76.7 32.4 %collective-permute-start.6 = (bf16[512,1024]{1,0:T(8,128)(2,1)S(1)}, bf16[512,1024]{1,0:T(8,128)(2,1)}, u32[]{:S(2)}, u32[]{:S(2)}) collective-permute-start(bf16[512,1024]{1,0:T(8,128)(2,1)S(1)} %norm_in.2.refs_3_.refs_1_), channel_id=1, source_target_pairs={{0,4},{4,0},{8,12},{12,8},{1,5},{5,1},{9,13},{13,9},{2,6},{6,2},{1... | collective-permute-start | bytes 3145736 | tf_op jit(solution)/shard_map/ppermute | solution.py:798
  76.8 16.8 %collective-permute-start.11 = (bf16[512,512]{1,0:T(8,128)(2,1)}, bf16[512,512]{1,0:T(8,128)(2,1)S(1)}, u32[]{:S(2)}, u32[]{:S(2)}) collective-permute-start(bf16[512,512]{1,0:T(8,128)(2,1)} %copy-done.113), channel_id=1, source_target_pairs={{0,1},{1,2},{2,3},{3,0},{4,5},{5,6},{6,7},{7,4},{8,9},{9,10},{10,1... | collective-permute-start | bytes 1572872 | tf_op jit(solution)/shard_map/ppermute | solution.py:803
  79.3 25.5 %collective-permute-start.12 = (bf16[512,512]{1,0:T(8,128)(2,1)}, bf16[512,512]{1,0:T(8,128)(2,1)S(1)}, u32[]{:S(2)}, u32[]{:S(2)}) collective-permute-start(bf16[512,512]{1,0:T(8,128)(2,1)} %copy-done.61), channel_id=1, source_target_pairs={{0,1},{1,2},{2,3},{3,0},{4,5},{5,6},{6,7},{7,4},{8,9},{9,10},{10,1... | collective-permute-start | bytes 1572872 | tf_op jit(solution)/shard_map/ppermute | solution.py:803
  81.4 14.9 %collective-permute-start.9 = (bf16[512,512]{1,0:T(8,128)(2,1)S(1)}, bf16[512,512]{1,0:T(8,128)(2,1)S(1)}, u32[]{:S(2)}, u32[]{:S(2)}) collective-permute-start(bf16[512,512]{1,0:T(8,128)(2,1)S(1)} %copy-done.27), channel_id=1, source_target_pairs={{0,8},{4,12},{8,0},{12,4},{1,9},{5,13},{9,1},{13,5},{2,10},{6,14},... | collective-permute-start | bytes 1572872 | tf_op jit(solution)/shard_map/ppermute | solution.py:798
  82.9 24.6 %collective-permute-start.10 = (bf16[512,512]{1,0:T(8,128)(2,1)}, bf16[512,512]{1,0:T(8,128)(2,1)S(1)}, u32[]{:S(2)}, u32[]{:S(2)}) collective-permute-start(bf16[512,512]{1,0:T(8,128)(2,1)} %collective-permute-done.7.refs_8_.refs_4_.refs_6_.refs_5_), channel_id=1, source_target_pairs={{0,8},{4,12},{8,0},{12,4},{1,9},{5,13},{9,1},{13,5},{2,10},{6,14},... | collective-permute-start | bytes 1572872 | tf_op jit(solution)/shard_map/ppermute | solution.py:798
  93.5 35.3 %collective-permute-start.13 = (bf16[512,512]{1,0:T(8,128)(2,1)S(1)}, bf16[512,512]{1,0:T(8,128)(2,1)S(1)}, u32[]{:S(2)}, u32[]{:S(2)}) collective-permute-start(bf16[512,512]{1,0:T(8,128)(2,1)S(1)} %collective-permute-done.11.refs_13_.refs_3_.refs_2_), channel_id=1, source_target_pairs={{0,1},{1,2},{2,3},{3,0},{4,5},{5,6},{6,7},{7,4},{8,9},{9,10},{10,1... | collective-permute-start | bytes 1572872 | tf_op jit(solution)/shard_map/ppermute | solution.py:803
  96.2 237.8 %copy-start.57 = (bf16[512,512]{1,0:T(8,128)(2,1)}, bf16[512,512]{1,0:T(8,128)(2,1)S(1)}, u32[]{:S(2)}) copy-start(bf16[512,512]{1,0:T(8,128)(2,1)S(1)} %collective-permute-done.9.refs_11_.refs_7_.refs_8_) | copy-start | bytes 1572868
  96.3 32.6 %collective-permute-start.15 = (bf16[512,512]{1,0:T(8,128)(2,1)S(1)}, bf16[512,512]{1,0:T(8,128)(2,1)S(1)}, u32[]{:S(2)}, u32[]{:S(2)}) collective-permute-start(bf16[512,512]{1,0:T(8,128)(2,1)S(1)} %collective-permute-done.11.refs_13_.refs_3_.refs_2_), channel_id=1, source_target_pairs={{0,8},{4,12},{8,0},{12,4},{1,9},{5,13},{9,1},{13,5},{2,10},{6,14},... | collective-permute-start | bytes 1572872 | tf_op jit(solution)/shard_map/ppermute | solution.py:798
  104.8 24.1 %collective-permute-start.14 = (bf16[512,512]{1,0:T(8,128)(2,1)S(1)}, bf16[512,512]{1,0:T(8,128)(2,1)S(1)}, u32[]{:S(2)}, u32[]{:S(2)}) collective-permute-start(bf16[512,512]{1,0:T(8,128)(2,1)S(1)} %collective-permute-done.12.refs_14_.refs_2_.refs_4_), channel_id=1, source_target_pairs={{0,1},{1,2},{2,3},{3,0},{4,5},{5,6},{6,7},{7,4},{8,9},{9,10},{10,1... | collective-permute-start | bytes 1572872 | tf_op jit(solution)/shard_map/ppermute | solution.py:803
  107.5 226.5 %copy-start.59 = (bf16[512,512]{1,0:T(8,128)(2,1)}, bf16[512,512]{1,0:T(8,128)(2,1)S(1)}, u32[]{:S(2)}) copy-start(bf16[512,512]{1,0:T(8,128)(2,1)S(1)} %collective-permute-done.10.refs_12_.refs_8_.refs_9_) | copy-start | bytes 1572868
  107.5 21.4 %collective-permute-start.16 = (bf16[512,512]{1,0:T(8,128)(2,1)S(1)}, bf16[512,512]{1,0:T(8,128)(2,1)S(1)}, u32[]{:S(2)}, u32[]{:S(2)}) collective-permute-start(bf16[512,512]{1,0:T(8,128)(2,1)S(1)} %collective-permute-done.12.refs_14_.refs_2_.refs_4_), channel_id=1, source_target_pairs={{0,8},{4,12},{8,0},{12,4},{1,9},{5,13},{9,1},{13,5},{2,10},{6,14},... | collective-permute-start | bytes 1572872 | tf_op jit(solution)/shard_map/ppermute | solution.py:798
  133.3 28.3 %collective-permute-start.17 = (bf16[512,1024]{1,0:T(8,128)(2,1)S(1)}, bf16[512,1024]{1,0:T(8,128)(2,1)S(1)}, u32[]{:S(2)}, u32[]{:S(2)}) collective-permute-start(bf16[512,1024]{1,0:T(8,128)(2,1)S(1)} %get-tuple-element.101), channel_id=1, source_target_pairs={{0,4},{4,0},{8,12},{12,8},{1,5},{5,1},{9,13},{13,9},{2,6},{6,2},{1... | collective-permute-start | bytes 3145736 | tf_op jit(solution)/shard_map/ppermute | solution.py:798
  133.3 16.8 %collective-permute-start.18 = (bf16[512,512]{1,0:T(8,128)(2,1)}, bf16[512,512]{1,0:T(8,128)(2,1)S(1)}, u32[]{:S(2)}, u32[]{:S(2)}) collective-permute-start(bf16[512,512]{1,0:T(8,128)(2,1)} %copy-done.103), channel_id=1, source_target_pairs={{0,1},{1,2},{2,3},{3,0},{4,5},{5,6},{6,7},{7,4},{8,9},{9,10},{10,1... | collective-permute-start | bytes 1572872 | tf_op jit(solution)/shard_map/ppermute | solution.py:803
  135.9 25.0 %collective-permute-start.19 = (bf16[512,512]{1,0:T(8,128)(2,1)}, bf16[512,512]{1,0:T(8,128)(2,1)S(1)}, u32[]{:S(2)}, u32[]{:S(2)}) collective-permute-start(bf16[512,512]{1,0:T(8,128)(2,1)} %copy-done.30), channel_id=1, source_target_pairs={{0,1},{1,2},{2,3},{3,0},{4,5},{5,6},{6,7},{7,4},{8,9},{9,10},{10,1... | collective-permute-start | bytes 1572872 | tf_op jit(solution)/shard_map/ppermute | solution.py:803
  136.3 24.6 %collective-permute-start.20 = (bf16[512,512]{1,0:T(8,128)(2,1)}, bf16[512,512]{1,0:T(8,128)(2,1)S(1)}, u32[]{:S(2)}, u32[]{:S(2)}) collective-permute-start(bf16[512,512]{1,0:T(8,128)(2,1)} %copy-done.103), channel_id=1, source_target_pairs={{0,8},{4,12},{8,0},{12,4},{1,9},{5,13},{9,1},{13,5},{2,10},{6,14},... | collective-permute-start | bytes 1572872 | tf_op jit(solution)/shard_map/ppermute | solution.py:798
  136.8 24.7 %collective-permute-start.21 = (bf16[512,512]{1,0:T(8,128)(2,1)}, bf16[512,512]{1,0:T(8,128)(2,1)S(1)}, u32[]{:S(2)}, u32[]{:S(2)}) collective-permute-start(bf16[512,512]{1,0:T(8,128)(2,1)} %copy-done.30), channel_id=1, source_target_pairs={{0,8},{4,12},{8,0},{12,4},{1,9},{5,13},{9,1},{13,5},{2,10},{6,14},... | collective-permute-start | bytes 1572872 | tf_op jit(solution)/shard_map/ppermute | solution.py:798
  167.2 15.1 %collective-permute-start.22 = (bf16[512,1024]{1,0:T(8,128)(2,1)S(1)}, bf16[512,1024]{1,0:T(8,128)(2,1)S(1)}, u32[]{:S(2)}, u32[]{:S(2)}) collective-permute-start(bf16[512,1024]{1,0:T(8,128)(2,1)S(1)} %get-tuple-element.103.refs_0_.refs_1_), channel_id=1, source_target_pairs={{0,4},{4,0},{8,12},{12,8},{1,5},{5,1},{9,13},{13,9},{2,6},{6,2},{1... | collective-permute-start | bytes 3145736 | tf_op jit(solution)/shard_map/ppermute | solution.py:798
  167.3 15.0 %collective-permute-start.23 = (bf16[512,512]{1,0:T(8,128)(2,1)}, bf16[512,512]{1,0:T(8,128)(2,1)S(1)}, u32[]{:S(2)}, u32[]{:S(2)}) collective-permute-start(bf16[512,512]{1,0:T(8,128)(2,1)} %copy-done.116), channel_id=1, source_target_pairs={{0,8},{4,12},{8,0},{12,4},{1,9},{5,13},{9,1},{13,5},{2,10},{6,14},... | collective-permute-start | bytes 1572872 | tf_op jit(solution)/shard_map/ppermute | solution.py:798
  167.9 26.4 %collective-permute-start.24 = (bf16[512,512]{1,0:T(8,128)(2,1)}, bf16[512,512]{1,0:T(8,128)(2,1)S(1)}, u32[]{:S(2)}, u32[]{:S(2)}) collective-permute-start(bf16[512,512]{1,0:T(8,128)(2,1)} %copy-done.34), channel_id=1, source_target_pairs={{0,8},{4,12},{8,0},{12,4},{1,9},{5,13},{9,1},{13,5},{2,10},{6,14},... | collective-permute-start | bytes 1572872 | tf_op jit(solution)/shard_map/ppermute | solution.py:798
  198.9 2.7 collective-permute-start.25
  203.5 25.8 %collective-permute-start.26 = (bf16[512,1024]{1,0:T(8,128)(2,1)S(1)}, bf16[512,1024]{1,0:T(8,128)(2,1)S(1)}, u32[]{:S(2)}, u32[]{:S(2)}) collective-permute-start(bf16[512,1024]{1,0:T(8,128)(2,1)S(1)} %get-tuple-element.132), channel_id=1, source_target_pairs={{0,16},{1,17},{2,18},{3,19},{4,20},{5,21},{6,22},{7,23},{8,24},{9,... | collective-permute-start | bytes 3145736 | tf_op jit(solution)/shard_map/ppermute | solution.py:28
  231.1 2.7 collective-permute-start.27
  254.1 2.7 collective-permute-start.28
  260.2 2.7 collective-permute-start.29
  277.2 2.7 collective-permute-start.30
  284.1 2.7 collective-permute-start.31
  298.6 2.7 collective-permute-start.32
  305.3 2.7 collective-permute-start.33
  341.3 2.7 collective-permute-start.34
  346.3 27.2 %collective-permute-start.35 = (bf16[512,1024]{1,0:T(8,128)(2,1)S(1)}, bf16[512,1024]{1,0:T(8,128)(2,1)S(1)}, u32[]{:S(2)}, u32[]{:S(2)}) collective-permute-start(bf16[512,1024]{1,0:T(8,128)(2,1)S(1)} %get-tuple-element.131.refs_2_), channel_id=1, source_target_pairs={{16,0},{17,1},{18,2},{19,3},{20,4},{21,5},{22,6},{23,7},{24,8},{25... | collective-permute-start | bytes 3145736 | tf_op jit(solution)/shard_map/ppermute | solution.py:28
  349.1 31.3 %all-to-all-start.1 = ((bf16[4,128,1024]{2,1,0:T(8,128)(2,1)}), bf16[4,128,1024]{2,1,0:T(8,128)(2,1)}, u32[]{:S(2)}, u32[]{:S(2)}) async-start(bf16[4,128,1024]{2,1,0:T(8,128)(2,1)} %bitcast.41), calls=%async_computation.1 | async-start | bytes 2097152 | tf_op jit(solution)/shard_map/all_to_all | solution.py:1224
  377.6 2.8 collective-permute-start.36
  402.8 2.7 collective-permute-start.37
  403.0 26.0 %collective-permute-start.41 = (bf16[1024,512]{1,0:T(8,128)(2,1)S(1)}, bf16[1024,512]{1,0:T(8,128)(2,1)S(1)}, u32[]{:S(2)}, u32[]{:S(2)}) collective-permute-start(bf16[1024,512]{1,0:T(8,128)(2,1)S(1)} %get-tuple-element.149), channel_id=1, source_target_pairs={{0,8},{4,12},{8,0},{12,4},{1,9},{5,13},{9,1},{13,5},{2,10},{6,14},... | collective-permute-start | bytes 3145736 | tf_op jit(solution)/shard_map/ppermute | solution.py:798
  410.4 34.4 %collective-permute-start.39 = (bf16[512,1024]{1,0:T(8,128)(2,1)}, bf16[512,1024]{1,0:T(8,128)(2,1)S(1)}, u32[]{:S(2)}, u32[]{:S(2)}) collective-permute-start(bf16[512,1024]{1,0:T(8,128)(2,1)} %get-tuple-element.141.refs_2_.refs_3_.refs_5_), channel_id=1, source_target_pairs={{0,4},{4,0},{8,12},{12,8},{1,5},{5,1},{9,13},{13,9},{2,6},{6,2},{1... | collective-permute-start | bytes 3145736 | tf_op jit(solution)/shard_map/ppermute | solution.py:798
  412.0 2.0 collective-permute-start.38
  412.5 46.6 %collective-permute-start.40 = (bf16[1024,512]{1,0:T(8,128)(2,1)S(1)}, bf16[1024,512]{1,0:T(8,128)(2,1)S(1)}, u32[]{:S(2)}, u32[]{:S(2)}) collective-permute-start(bf16[1024,512]{1,0:T(8,128)(2,1)S(1)} %get-tuple-element.148), channel_id=1, source_target_pairs={{0,8},{4,12},{8,0},{12,4},{1,9},{5,13},{9,1},{13,5},{2,10},{6,14},... | collective-permute-start | bytes 3145736 | tf_op jit(solution)/shard_map/ppermute | solution.py:798
  429.4 29.7 %collective-permute-start.42 = (bf16[1024,512]{1,0:T(8,128)(2,1)S(1)}, bf16[1024,512]{1,0:T(8,128)(2,1)S(1)}, u32[]{:S(2)}, u32[]{:S(2)}) collective-permute-start(bf16[1024,512]{1,0:T(8,128)(2,1)S(1)} %moved.6.refs_13_), channel_id=1, source_target_pairs={{0,3},{1,0},{2,1},{3,2},{4,7},{5,4},{6,5},{7,6},{8,11},{9,8},{10,9... | collective-permute-start | bytes 3145736 | tf_op jit(solution)/shard_map/ppermute | solution.py:803
  442.8 41.4 %collective-permute-start.44 = (bf16[1024,512]{1,0:T(8,128)(2,1)S(1)}, bf16[1024,512]{1,0:T(8,128)(2,1)S(1)}, u32[]{:S(2)}, u32[]{:S(2)}) collective-permute-start(bf16[1024,512]{1,0:T(8,128)(2,1)S(1)} %get-tuple-element.154), channel_id=1, source_target_pairs={{0,8},{4,12},{8,0},{12,4},{1,9},{5,13},{9,1},{13,5},{2,10},{6,14},... | collective-permute-start | bytes 3145736 | tf_op jit(solution)/shard_map/ppermute | solution.py:798
  443.3 64.8 %collective-permute-start.47 = (bf16[1024,512]{1,0:T(8,128)(2,1)S(1)}, bf16[1024,512]{1,0:T(8,128)(2,1)S(1)}, u32[]{:S(2)}, u32[]{:S(2)}) collective-permute-start(bf16[1024,512]{1,0:T(8,128)(2,1)S(1)} %get-tuple-element.156), channel_id=1, source_target_pairs={{0,8},{4,12},{8,0},{12,4},{1,9},{5,13},{9,1},{13,5},{2,10},{6,14},... | collective-permute-start | bytes 3145736 | tf_op jit(solution)/shard_map/ppermute | solution.py:798
  460.4 23.8 %collective-permute-start.45 = (bf16[1024,512]{1,0:T(8,128)(2,1)S(1)}, bf16[1024,512]{1,0:T(8,128)(2,1)S(1)}, u32[]{:S(2)}, u32[]{:S(2)}) collective-permute-start(bf16[1024,512]{1,0:T(8,128)(2,1)S(1)} %moved.7.refs_13_), channel_id=1, source_target_pairs={{0,3},{1,0},{2,1},{3,2},{4,7},{5,4},{6,5},{7,6},{8,11},{9,8},{10,9... | collective-permute-start | bytes 3145736 | tf_op jit(solution)/shard_map/ppermute | solution.py:803
  484.8 23.5 %collective-permute-start.46 = (bf16[1024,512]{1,0:T(8,128)(2,1)S(1)}, bf16[1024,512]{1,0:T(8,128)(2,1)S(1)}, u32[]{:S(2)}, u32[]{:S(2)}) collective-permute-start(bf16[1024,512]{1,0:T(8,128)(2,1)S(1)} %moved.8.refs_13_), channel_id=1, source_target_pairs={{0,3},{1,0},{2,1},{3,2},{4,7},{5,4},{6,5},{7,6},{8,11},{9,8},{10,9... | collective-permute-start | bytes 3145736 | tf_op jit(solution)/shard_map/ppermute | solution.py:803
  488.1 19.0 %collective-permute-start.43 = (bf16[512,512]{1,0:T(8,128)(2,1)S(1)}, bf16[512,512]{1,0:T(8,128)(2,1)S(1)}, u32[]{:S(2)}, u32[]{:S(2)}) collective-permute-start(bf16[512,512]{1,0:T(8,128)(2,1)S(1)} %get-tuple-element.153), channel_id=1, source_target_pairs={{0,8},{4,12},{8,0},{12,4},{1,9},{5,13},{9,1},{13,5},{2,10},{6,14},... | collective-permute-start | bytes 1572872 | tf_op jit(solution)/shard_map/ppermute | solution.py:798
  515.2 14.9 %collective-permute-start.48 = (bf16[512,1024]{1,0:T(8,128)(2,1)S(1)}, bf16[512,1024]{1,0:T(8,128)(2,1)S(1)}, u32[]{:S(2)}, u32[]{:S(2)}) collective-permute-start(bf16[512,1024]{1,0:T(8,128)(2,1)S(1)} %get-tuple-element.158), channel_id=1, source_target_pairs={{0,4},{4,0},{8,12},{12,8},{1,5},{5,1},{9,13},{13,9},{2,6},{6,2},{1... | collective-permute-start | bytes 3145736 | tf_op jit(solution)/shard_map/ppermute | solution.py:798
  515.2 14.8 %collective-permute-start.49 = (bf16[512,512]{1,0:T(8,128)(2,1)S(1)}, bf16[512,512]{1,0:T(8,128)(2,1)S(1)}, u32[]{:S(2)}, u32[]{:S(2)}) collective-permute-start(bf16[512,512]{1,0:T(8,128)(2,1)S(1)} %get-tuple-element.160), channel_id=1, source_target_pairs={{0,8},{4,12},{8,0},{12,4},{1,9},{5,13},{9,1},{13,5},{2,10},{6,14},... | collective-permute-start | bytes 1572872 | tf_op jit(solution)/shard_map/ppermute | solution.py:798
  515.8 17.2 %collective-permute-start.50 = (bf16[512,512]{1,0:T(8,128)(2,1)S(1)}, bf16[512,512]{1,0:T(8,128)(2,1)S(1)}, u32[]{:S(2)}, u32[]{:S(2)}) collective-permute-start(bf16[512,512]{1,0:T(8,128)(2,1)S(1)} %copy-done.127), channel_id=1, source_target_pairs={{0,3},{1,0},{2,1},{3,2},{4,7},{5,4},{6,5},{7,6},{8,11},{9,8},{10,9... | collective-permute-start | bytes 1572872 | tf_op jit(solution)/shard_map/ppermute | solution.py:803
  519.3 21.5 %collective-permute-start.51 = (bf16[512,512]{1,0:T(8,128)(2,1)S(1)}, bf16[512,512]{1,0:T(8,128)(2,1)S(1)}, u32[]{:S(2)}, u32[]{:S(2)}) collective-permute-start(bf16[512,512]{1,0:T(8,128)(2,1)S(1)} %get-tuple-element.162), channel_id=1, source_target_pairs={{0,8},{4,12},{8,0},{12,4},{1,9},{5,13},{9,1},{13,5},{2,10},{6,14},... | collective-permute-start | bytes 1572872 | tf_op jit(solution)/shard_map/ppermute | solution.py:798
  543.2 35.9 %all-to-all-start.2 = ((bf16[4,128,1024]{2,1,0:T(8,128)(2,1)}), bf16[4,128,1024]{2,1,0:T(8,128)(2,1)S(1)}, u32[]{:S(2)}, u32[]{:S(2)}) async-start(bf16[4,128,1024]{2,1,0:T(8,128)(2,1)} %bitcast.16), calls=%async_computation.2 | async-start | bytes 2097152 | tf_op jit(solution)/shard_map/all_to_all | solution.py:1305
  550.9 5.5 collective-permute-start.53
  550.9 5.5 collective-permute-start.54
  551.6 13.8 %collective-permute-start.55 = (bf16[512,512]{1,0:T(8,128)(2,1)S(1)}, bf16[512,512]{1,0:T(8,128)(2,1)S(1)}, u32[]{:S(2)}, u32[]{:S(2)}) collective-permute-start(bf16[512,512]{1,0:T(8,128)(2,1)S(1)} %copy-done.134), channel_id=1, source_target_pairs={{0,8},{4,12},{8,0},{12,4},{1,9},{5,13},{9,1},{13,5},{2,10},{6,14},... | collective-permute-start | bytes 1572872 | tf_op jit(solution)/shard_map/ppermute | solution.py:798
  552.5 25.8 %collective-permute-start.52 = (bf16[512,512]{1,0:T(8,128)(2,1)S(1)}, bf16[512,512]{1,0:T(8,128)(2,1)S(1)}, u32[]{:S(2)}, u32[]{:S(2)}) collective-permute-start(bf16[512,512]{1,0:T(8,128)(2,1)S(1)} %moved.10), channel_id=1, source_target_pairs={{0,3},{1,0},{2,1},{3,2},{4,7},{5,4},{6,5},{7,6},{8,11},{9,8},{10,9... | collective-permute-start | bytes 1572872 | tf_op jit(solution)/shard_map/ppermute | solution.py:803
  584.3 25.0 %collective-permute-start.56 = (bf16[2,128,1024]{2,1,0:T(8,128)(2,1)}, bf16[2,128,1024]{2,1,0:T(8,128)(2,1)S(1)}, u32[]{:S(2)}, u32[]{:S(2)}) collective-permute-start(bf16[2,128,1024]{2,1,0:T(8,128)(2,1)} %get-tuple-element.172), channel_id=1, source_target_pairs={{0,4},{4,0},{8,12},{12,8},{1,5},{5,1},{9,13},{13,9},{2,6},{6,2},{1... | collective-permute-start | bytes 1572872 | tf_op jit(solution)/shard_map/ppermute | solution.py:798
  584.3 26.0 %collective-permute-start.57 = (bf16[512,512]{1,0:T(8,128)(2,1)}, bf16[512,512]{1,0:T(8,128)(2,1)S(1)}, u32[]{:S(2)}, u32[]{:S(2)}) collective-permute-start(bf16[512,512]{1,0:T(8,128)(2,1)} %copy-done.38), channel_id=1, source_target_pairs={{0,3},{1,0},{2,1},{3,2},{4,7},{5,4},{6,5},{7,6},{8,11},{9,8},{10,9... | collective-permute-start | bytes 1572872 | tf_op jit(solution)/shard_map/ppermute | solution.py:803
  610.5 2.0 collective-permute-start.58
  (141 other events, 1494.7 us)

commit v15 on v14

--- a/solution.py
+++ b/solution.py
@@ -1212,7 +1212,7 @@
             (up_piece, up_other[0], down_other[0]),
             (up_own[1], down_own[1]),
             (up_own[2], down_own[2], up_other[1], down_other[1]),
-            (up_own[3], down_own[3], up_other[2], down_other[2]),
+            (down_own[3], up_other[2], down_other[2], up_other[3]),
         ),
     )
     low_one, saved_one, lefts_one = forward(shifted(low_zero, "section", 1), ((),) * 4)
@@ -1292,17 +1292,20 @@
 
     d_down = d_up = d_attn = outputs = None
     grad_zero, rights_zero, gain_zero = backward(received, saved_zero, hook, (lows,))
+    _, attn_moves[2] = moves_on(attn_sums[2], attn_moves[3])
     place_word = jnp.stack([lax.axis_index("section"), upper]).astype(jnp.int32)
-    (grads,) = with_core(
+    (grads_chosen,) = with_core(
         chosen_kernel,
         "chosen",
         place_word,
         (row16,),
         grad_zero,
         grad_one,
-        waits=(attn_moves[3], attn_sums[1][1]),
-    )
-    grads = lax.all_to_all(grads.reshape(tensor, part, width), "tensor", 0, 0, tiled=True)
+        waits=(attn_moves[2], attn_sums[1][1]),
+    )
+    grads = lax.all_to_all(
+        grads_chosen.reshape(tensor, part, width), "tensor", 0, 0, tiled=True
+    )
 
     block32 = ((wide_half // 2, unit), jnp.float32)
     down32 = ((unit, wide_half // 2), jnp.float32)
@@ -1313,7 +1316,7 @@
         (block32, down32, block32, down32),
         *mlp_sums[0],
         mlp_moves[1],
-        waits=(grad_zero,),
+        waits=(grads_chosen,),
     )
     outs = (
         ((wide_half // 2, 2 * unit), jnp.float32),
@@ -1323,10 +1326,9 @@
     up_grad, down_grad = with_core(
         mlp_join_kernel, "mlp_join", core_word, outs, up_keep, down_keep, *sent
     )
-    total, attn_moves[2] = moves_on(attn_sums[2], attn_moves[3], waits=(grad_zero,))
-    waits = (up_grad, attn_sums[0][1], grads)
+    waits = (grads_chosen, attn_sums[0][1])
     last, attn_moves[1] = moves_on(attn_sums[1], attn_moves[2], waits=waits)
-    grads = from_chip(grads, (last,))
+    grads = from_chip(grads, (attn_moves[1],))
     gain_total = own_first(jnp.where(first, gain_zero, gain_one))
     count = tensor * lax.axis_size("dp")
     gain_parts = gain_total.reshape(4, count, width // count).swapaxes(0, 1)
@@ -1342,7 +1344,7 @@
         outs,
         *attn_sums[0],
         attn_moves[1],
-        waits=(grads, outputs, gains_grad),
+        waits=(grads, outputs, gains_grad, up_grad),
     )
     spots = tuple((i * 128, (i + 1) * 128, i * 256) for i in range(3))
     outs = (((wide_half // 2, 768), jnp.float32), ((256, wide_half // 2), jnp.float32))

time: 627 us -> 646 us (1.030)
  waiting for transfers between devices: 226 us -> 240 us
  Pallas kernels: 221 us -> 229 us
    ppermute x42, waiting for transfers between devices: 102 us -> 110 us  [flip_pairs(): return lax.ppermute(block, 'dp', [(i, i ^ distance) for i in range(size)])]
    pallas_call x31, Pallas kernels: 86.2 us -> 93.8 us  [on_chip(): pl.pallas_call(without(kernel, len(operands), len(waits)), in_specs=[spac...]
    ppermute x15, starting transfers between devices: 35.7 us -> 29.2 us  [passed_on(): lax.ppermute(block, 'tensor', [(i, (i + step) % size) for i in range(size)])]
    unnamed x290 -> x270, local copies, waits for them, and re-layouts: 47.9 us -> 42 us
  transfers between devices with their start and end apart: 62 -> 62, of which waited for: 36 -> 38; matrix products, arithmetic and copies ran while one was open for 4% -> 4% of each run, Pallas kernels for 14% -> 15%
where the time goes in v15:
time: 646 us; the launch traced here: 637 us
  waiting for transfers between devices  240 us (37%)
  Pallas kernels  229 us (35%)
  starting transfers between devices  79.4 us (12%)
  local copies, waits for them, and re-layouts  52.8 us (8%)
  other arithmetic  19.3 us (3%)
  blocking collectives  13.3 us (2%)
    ppermute x42, waiting for transfers between devices, flip_pairs(): return lax.ppermute(block, 'dp', [(i, i ^ distance) for i in range(size)])  110 us
    pallas_call x31, Pallas kernels, on_chip(): pl.pallas_call(without(kernel, len(operands), len(waits)), in_specs=[spac...  93.8 us
    ppermute x15, waiting for transfers between devices, passed_on(): lax.ppermute(block, 'tensor', [(i, (i + step) % size) for i in range(size)])  85.2 us
    pallas_call x6, Pallas kernels, by_pairs(): pl.pallas_call(without(functools.partial(kernel, len(pieces[0])), taken,...  84 us
    unnamed x270, local copies, waits for them, and re-layouts  42 us
    ppermute x2, waiting for transfers between devices, shifted(): return lax.ppermute(block, axis, route)  42 us
    ppermute x15, starting transfers between devices, passed_on(): lax.ppermute(block, 'tensor', [(i, (i + step) % size) for i in range(size)])  29.2 us
    ppermute x42, starting transfers between devices, flip_pairs(): return lax.ppermute(block, 'dp', [(i, i ^ distance) for i in range(size)])  28.8 us
  transfers between devices with their start and end apart: 62, of which 38 were waited for; matrix products, arithmetic and copies ran while one was open for 4% of the time, Pallas kernels for 15%

profile of v15, /device:TPU:0, one launch (start us, length us, event | category | flops | bytes accessed | tf_op | source)
XLA Modules:
  0.0 636.6 jit_solution(5442560954952285224)
XLA Ops:
  11.4 6.2 all-to-all-start
  31.6 18.8 %collective-permute-done.1.refs_0_ = bf16[512,512]{1,0:T(8,128)(2,1)} collective-permute-done((bf16[512,512]{1,0:T(8,128)(2,1)}, bf16[512,512]{1,0:T(8,128)(2,1)}, u32[]{:S(2)}, u32[]{:S(2)}) %collective-permute-start.1) | collective-permute-done | bytes 524320 | tf_op jit(solution)/shard_map/ppermute | solution.py:803
  50.4 2.7 collective-permute-done.3.refs_2_.refs_3_.refs_6_.refs_5_
  58.7 5.6 collective-permute-done.5.refs_4_.refs_5_.refs_7_
  64.3 4.0 collective-permute-done.4.refs_2_.refs_7_.refs_3_.refs_5_.refs_4_
  77.3 20.8 %collective-permute-done.7.refs_8_.refs_4_.refs_6_.refs_5_ = bf16[512,512]{1,0:T(8,128)(2,1)S(1)} collective-permute-done((bf16[512,512]{1,0:T(8,128)(2,1)}, bf16[512,512]{1,0:T(8,128)(2,1)S(1)}, u32[]{:S(2)}, u32[]{:S(2)}) %collective-permute-start.7) | collective-permute-done | bytes 524320 | tf_op jit(solution)/shard_map/ppermute | solution.py:803
  103.1 6.3 collective-permute-done.12.refs_14_.refs_2_.refs_4_
  109.4 3.6 collective-permute-done.10.refs_12_.refs_8_.refs_9_
  114.5 6.2 collective-permute-done.13.refs_9_.refs_4_.refs_3_
  121.8 16.7 %attend.2 = (bf16[4,1024,128]{2,1,0:T(8,128)(2,1)S(1)}, bf16[4,1024,128]{2,1,0:T(8,128)(2,1)S(1)}, bf16[4,1024,128]{2,1,0:T(8,128)(2,1)S(1)}, f32[4,2,1024]{2,1,0:T(2,128)S(1)}, bf16[1024,512]{1,0:T(8,128)(2,1)S(1)}) custom-call(s32[1]{0:T(128)} %bitcast.refs_0_, f32[1024,128]{1,0:T(8,128)S(1)} %get-tuple-element.228.refs_1_, ...), custom_call_target="tpu_custom_call" | custom-call | flops 11811160064 | bytes 11567104 | tf_op jit(solution)/shard_map/attend/pallas_call | solution.py:708
  142.7 2.8 attn_out.2
  151.2 11.2 %collective-permute-done.18.refs_4_.refs_6_ = bf16[512,512]{1,0:T(8,128)(2,1)S(1)} collective-permute-done((bf16[512,512]{1,0:T(8,128)(2,1)}, bf16[512,512]{1,0:T(8,128)(2,1)S(1)}, u32[]{:S(2)}, u32[]{:S(2)}) %collective-permute-start.18) | collective-permute-done | bytes 524320 | tf_op jit(solution)/shard_map/ppermute | solution.py:803
  162.6 11.2 %collective-permute-done.20.refs_6_.refs_7_.refs_9_ = bf16[512,512]{1,0:T(8,128)(2,1)S(1)} collective-permute-done((bf16[512,512]{1,0:T(8,128)(2,1)}, bf16[512,512]{1,0:T(8,128)(2,1)S(1)}, u32[]{:S(2)}, u32[]{:S(2)}) %collective-permute-start.20) | collective-permute-done | bytes 524320 | tf_op jit(solution)/shard_map/ppermute | solution.py:798
  173.8 10.4 %collective-permute-done.22.refs_7_.refs_9_.refs_8_ = bf16[512,512]{1,0:T(8,128)(2,1)S(1)} collective-permute-done((bf16[512,512]{1,0:T(8,128)(2,1)S(1)}, bf16[512,512]{1,0:T(8,128)(2,1)S(1)}, u32[]{:S(2)}, u32[]{:S(2)}) %collective-permute-start.22) | collective-permute-done | bytes 524320 | tf_op jit(solution)/shard_map/ppermute | solution.py:798
  185.1 3.4 after_attn.2
  194.7 9.5 %mlp_up.2 = (bf16[1024,2048]{1,0:T(8,128)(2,1)S(1)}, bf16[1024,2048]{1,0:T(8,128)(2,1)S(1)}) custom-call(bf16[512,1024]{1,0:T(8,128)(2,1)S(1)} %get-tuple-element.103.refs_0_.refs_1_, bf16[512,1024]{1,0:T(8,128)(2,1)S(1)} %collective-permute-done.23.refs_1_.refs_2_, bf16[512,512]{1,0:T(8,128)(2,1)} %get-tuple-element.97.refs_2_.refs_1_, ...), custom_call_target="tpu_custom_call" | custom-call | flops 4294967296 | bytes 14680064 | tf_op jit(solution)/shard_map/mlp_up/pallas_call | solution.py:690
  206.2 4.5 mlp_down.2
  210.9 2.5 collective-permute-done.25.refs_3_
  215.3 3.6 collective-permute-start.26
  218.9 22.2 %collective-permute-done.26.refs_1_ = bf16[512,1024]{1,0:T(8,128)(2,1)S(1)} collective-permute-done((bf16[512,1024]{1,0:T(8,128)(2,1)S(1)}, bf16[512,1024]{1,0:T(8,128)(2,1)S(1)}, u32[]{:S(2)}, u32[]{:S(2)}) %collective-permute-start.26) | collective-permute-done | bytes 1048608 | tf_op jit(solution)/shard_map/ppermute | solution.py:28
  243.0 2.6 collective-permute-done.27.refs_4_.refs_8_
  245.6 16.7 %attend.3 = (bf16[4,1024,128]{2,1,0:T(8,128)(2,1)S(1)}, bf16[4,1024,128]{2,1,0:T(8,128)(2,1)S(1)}, bf16[4,1024,128]{2,1,0:T(8,128)(2,1)S(1)}, f32[4,2,1024]{2,1,0:T(2,128)S(1)}, bf16[1024,512]{1,0:T(8,128)(2,1)S(1)}) custom-call(s32[1]{0:T(128)} %bitcast.refs_0_, f32[1024,128]{1,0:T(8,128)S(1)} %get-tuple-element.228.refs_1_, ...), custom_call_target="tpu_custom_call" | custom-call | flops 11811160064 | bytes 11567104 | tf_op jit(solution)/shard_map/attend/pallas_call | solution.py:708
  262.4 3.2 attn_out.3
  265.8 2.5 collective-permute-done.28.refs_3_
  268.3 3.4 after_attn.3
  272.0 2.5 collective-permute-done.29.refs_1_.refs_8_
  274.5 9.5 %mlp_up.3 = (bf16[1024,2048]{1,0:T(8,128)(2,1)S(1)}, bf16[1024,2048]{1,0:T(8,128)(2,1)S(1)}) custom-call(bf16[512,1024]{1,0:T(8,128)(2,1)S(1)} %get-tuple-element.112.refs_0_.refs_7_, bf16[512,1024]{1,0:T(8,128)(2,1)S(1)} %collective-permute-done.29.refs_1_.refs_8_, bf16[512,512]{1,0:T(8,128)(2,1)} %get-tuple-element.97.refs_2_.refs_1_, ...), custom_call_target="tpu_custom_call" | custom-call | flops 4294967296 | bytes 14680064 | tf_op jit(solution)/shard_map/mlp_up/pallas_call | solution.py:690
  286.0 4.5 mlp_down.3
  290.7 2.5 collective-permute-done.30.refs_3_
  297.6 2.5 collective-permute-done.31.refs_1_.refs_12_
  300.1 7.2 %mlp_up_back.2.refs_0_.refs_9_ = bf16[1024,2048]{1,0:T(8,128)(2,1)S(1)} custom-call(bf16[512,1024]{1,0:T(8,128)(2,1)S(1)} %get-tuple-element.118.refs_0_.refs_11_, bf16[512,1024]{1,0:T(8,128)(2,1)S(1)} %collective-permute-done.31.refs_1_.refs_12_, bf16[1024,2048]{1,0:T(8,128)(2,1)} %copy-done.35, bf16[512,512]{1,0:T(8,128)(2,1)} %copy-done.61, ...), custom_call_target="tpu_custom_call" | custom-call | tf_op jit(solution)/shard_map/mlp_up_back/pallas_call | solution.py:729
  307.3 7.1 %mlp_back.2 = (f32[512,1024]{1,0:T(8,128)S(1)}, bf16[512,1024]{1,0:T(8,128)(2,1)S(1)}) custom-call(bf16[1024,2048]{1,0:T(8,128)(2,1)S(1)} %mlp_up_back.2.refs_0_.refs_9_, bf16[512,512]{1,0:T(8,128)(2,1)} %get-tuple-element.97.refs_2_.refs_1_, bf16[512,512]{1,0:T(8,128)(2,1)} %collective-permute-done.11.refs_13_.refs_3_.refs_2_, ...), custom_call_target="tpu_custom_call" | custom-call | flops 4294967296 | bytes 11534336 | tf_op jit(solution)/shard_map/mlp_back/pallas_call | solution.py:690
  317.9 3.9 into_attn_back.2
  322.0 2.5 collective-permute-done.33.refs_4_.refs_12_
  324.5 13.1 %attend_back.4.refs_0_.refs_9_ = bf16[1024,768]{1,0:T(8,128)(2,1)S(1)} custom-call(s32[1]{0:T(128)} %bitcast.refs_0_, f32[1024,128]{1,0:T(8,128)S(1)} %get-tuple-element.228.refs_1_, f32[1024,128]{1,0:T(8,128)S(1)} %get-tuple-element.229.refs_2_, bf16[512,1024]{1,0:T(8,128)(2,1)S(1)} %get-tuple-element.123.refs_3_.refs_11_, ...), custom_call_target="tpu_custom_call" | custom-call | flops 11274289152 | bytes 6815744 | tf_op jit(solution)/shard_map/attend_back/pallas_call | solution.py:708
  337.7 11.5 %attend_back.5.refs_1_.refs_9_ = bf16[1024,768]{1,0:T(8,128)(2,1)S(1)} custom-call(s32[1]{0:T(128)} %bitcast.refs_0_, f32[1024,128]{1,0:T(8,128)S(1)} %get-tuple-element.228.refs_1_, f32[1024,128]{1,0:T(8,128)S(1)} %get-tuple-element.229.refs_2_, bf16[512,1024]{1,0:T(8,128)(2,1)S(1)} %get-tuple-element.123.refs_3_.refs_11_, ...), custom_call_target="tpu_custom_call" | custom-call | flops 11274289152 | bytes 6815744 | tf_op jit(solution)/shard_map/attend_back/pallas_call | solution.py:708
  350.8 5.5 attn_back.2
  364.1 4.6 all-to-all-start.1
  368.8 19.7 %collective-permute-done.35.refs_1_ = bf16[512,1024]{1,0:T(8,128)(2,1)S(1)} collective-permute-done((bf16[512,1024]{1,0:T(8,128)(2,1)S(1)}, bf16[512,1024]{1,0:T(8,128)(2,1)S(1)}, u32[]{:S(2)}, u32[]{:S(2)}) %collective-permute-start.35) | collective-permute-done | bytes 1048608 | tf_op jit(solution)/shard_map/ppermute | solution.py:28
  395.3 7.2 %mlp_up_back.3.refs_3_.refs_0_ = bf16[1024,2048]{1,0:T(8,128)(2,1)S(1)} custom-call(bf16[512,1024]{1,0:T(8,128)(2,1)S(1)} %get-tuple-element.135.refs_0_.refs_5_, bf16[512,1024]{1,0:T(8,128)(2,1)S(1)} %collective-permute-done.36.refs_1_.refs_6_, bf16[1024,2048]{1,0:T(8,128)(2,1)} %copy-done.50, bf16[512,512]{1,0:T(8,128)(2,1)} %copy-done.61, ...), custom_call_target="tpu_custom_call" | custom-call | tf_op jit(solution)/shard_map/mlp_up_back/pallas_call | solution.py:729
  404.5 7.2 %mlp_grads.2 = (f32[1024,512]{1,0:T(8,128)S(1)}, bf16[1024,512]{1,0:T(8,128)(2,1)S(1)}, f32[1024,512]{1,0:T(8,128)S(1)}, bf16[1024,512]{1,0:T(8,128)(2,1)S(1)}) custom-call(s32[1]{0:T(128)} %bitcast.12.refs_0_, bf16[512,1024]{1,0:T(8,128)(2,1)} %copy-done.37, bf16[512,1024]{1,0:T(8,128)(2,1)} %copy-done.38, bf16[1024,2048]{1,0:T(8,128)(2,1)} %copy-done.3, ...), custom_call_target="tpu_custom_call" | custom-call | tf_op jit(solution)/shard_map/mlp_grads/pallas_call | solution.py:897
  413.2 6.0 mlp_back.3
  421.9 4.9 into_attn_back.3
  431.4 13.9 %collective-permute-done.41.refs_1_ = bf16[1024,512]{1,0:T(8,128)(2,1)S(1)} collective-permute-done((bf16[1024,512]{1,0:T(8,128)(2,1)S(1)}, bf16[1024,512]{1,0:T(8,128)(2,1)S(1)}, u32[]{:S(2)}, u32[]{:S(2)}) %collective-permute-start.41) | collective-permute-done | bytes 1048608 | tf_op jit(solution)/shard_map/ppermute | solution.py:798
  445.8 2.7 collective-permute-start.42
  448.5 7.0 %mlp_grads.3 = (f32[1024,512]{1,0:T(8,128)S(1)}, bf16[1024,512]{1,0:T(8,128)(2,1)S(1)}, f32[1024,512]{1,0:T(8,128)S(1)}, bf16[1024,512]{1,0:T(8,128)(2,1)S(1)}) custom-call(s32[1]{0:T(128)} %bitcast.12.refs_0_, bf16[512,1024]{1,0:T(8,128)(2,1)} %copy-done.37, bf16[512,1024]{1,0:T(8,128)(2,1)} %copy-done.38, bf16[1024,2048]{1,0:T(8,128)(2,1)} %copy-done.3, ...), custom_call_target="tpu_custom_call" | custom-call | tf_op jit(solution)/shard_map/mlp_grads/pallas_call | solution.py:897
  460.4 12.7 %attend_back.6.refs_3_.refs_1_ = bf16[1024,768]{1,0:T(8,128)(2,1)S(1)} custom-call(s32[1]{0:T(128)} %bitcast.refs_0_, f32[1024,128]{1,0:T(8,128)S(1)} %copy-done.107, f32[1024,128]{1,0:T(8,128)S(1)} %copy-done.109, bf16[512,1024]{1,0:T(8,128)(2,1)} %get-tuple-element.141.refs_2_.refs_3_.refs_5_, ...), custom_call_target="tpu_custom_call" | custom-call | flops 11274289152 | bytes 6815744 | tf_op jit(solution)/shard_map/attend_back/pallas_call | solution.py:708
  477.8 5.9 attn_grads.2
  484.7 13.2 %attend_back.7.refs_3_.refs_0_ = bf16[1024,768]{1,0:T(8,128)(2,1)S(1)} custom-call(s32[1]{0:T(128)} %bitcast.refs_0_, f32[1024,128]{1,0:T(8,128)S(1)} %copy-done.107, f32[1024,128]{1,0:T(8,128)S(1)} %copy-done.109, bf16[512,1024]{1,0:T(8,128)(2,1)} %get-tuple-element.141.refs_2_.refs_3_.refs_5_, bf16[512,1024]{1,0:T(8,128)(2,1)S(1)} %copy-done.44, ...), custom_call_target="tpu_custom_call" | custom-call | flops 11274289152 | bytes 6815744 | tf_op jit(solution)/shard_map/attend_back/pallas_call | solution.py:708
  499.6 4.3 collective-permute-start.46
  505.5 5.9 attn_grads.3
  512.3 11.2 %collective-permute-done.43.refs_1_ = bf16[512,512]{1,0:T(8,128)(2,1)S(1)} collective-permute-done((bf16[512,512]{1,0:T(8,128)(2,1)S(1)}, bf16[512,512]{1,0:T(8,128)(2,1)S(1)}, u32[]{:S(2)}, u32[]{:S(2)}) %collective-permute-start.43) | collective-permute-done | bytes 524320 | tf_op jit(solution)/shard_map/ppermute | solution.py:798
  526.4 4.9 attn_back.3
  533.1 2.9 collective-permute-start.50
  536.4 9.8 %collective-permute-done.49.refs_5_.refs_1_ = bf16[512,512]{1,0:T(8,128)(2,1)S(1)} collective-permute-done((bf16[512,512]{1,0:T(8,128)(2,1)S(1)}, bf16[512,512]{1,0:T(8,128)(2,1)S(1)}, u32[]{:S(2)}, u32[]{:S(2)}) %collective-permute-start.49) | collective-permute-done | bytes 524320 | tf_op jit(solution)/shard_map/ppermute | solution.py:798
  547.7 4.3 collective-permute-start.51
  554.2 2.8 collective-permute-done.52.refs_4_.refs_1_
  557.0 5.7 collective-permute-done.51.refs_3_.refs_2_
  565.1 5.7 all-to-all-start.2
  571.3 11.7 %collective-permute-done.53.refs_4_.refs_2_ = bf16[512,512]{1,0:T(8,128)(2,1)S(1)} collective-permute-done((bf16[512,512]{1,0:T(8,128)(2,1)}, bf16[512,512]{1,0:T(8,128)(2,1)S(1)}, u32[]{:S(2)}, u32[]{:S(2)}) %collective-permute-start.53) | collective-permute-done | bytes 524320 | tf_op jit(solution)/shard_map/ppermute | solution.py:798
  585.1 3.6 collective-permute-start.54
  590.5 11.0 %collective-permute-done.54.refs_2_.refs_3_ = bf16[512,512]{1,0:T(8,128)(2,1)S(1)} collective-permute-done((bf16[512,512]{1,0:T(8,128)(2,1)S(1)}, bf16[512,512]{1,0:T(8,128)(2,1)S(1)}, u32[]{:S(2)}, u32[]{:S(2)}) %collective-permute-start.54) | collective-permute-done | bytes 524320 | tf_op jit(solution)/shard_map/ppermute | solution.py:803
  610.8 13.3 %all_to_all.20 = f32[16,1,256]{2,1,0:T(1,128)S(1)} all-to-all(f32[16,1,256]{2,1,0:T(1,128)S(1)} %reshape.144), channel_id=1, replica_groups=mesh['section'=2,'dp'=4,'tensor'=4] {'dp','tensor'}, dimensions={0} | all-to-all | bytes 32768 | tf_op jit(solution)/shard_map/all_to_all | solution.py:1337
  626.0 2.6 mlp_join.1
  (437 shorter events, 156.2 us)
Async XLA Ops:
  7.2 2.1 collective-permute-start
  11.4 62.2 %all-to-all-start = ((bf16[4,128,1024]{2,1,0:T(8,128)(2,1)}), bf16[4,128,1024]{2,1,0:T(8,128)(2,1)S(1)}, u32[]{:S(2)}, u32[]{:S(2)}) async-start(bf16[4,128,1024]{2,1,0:T(8,128)(2,1)} %pad_maximum_fusion), calls=%async_computation | async-start | bytes 2097152 | tf_op jit(solution)/shard_map/all_to_all | solution.py:1071
  24.8 25.7 %collective-permute-start.1 = (bf16[512,512]{1,0:T(8,128)(2,1)}, bf16[512,512]{1,0:T(8,128)(2,1)}, u32[]{:S(2)}, u32[]{:S(2)}) collective-permute-start(bf16[512,512]{1,0:T(8,128)(2,1)} %pad_maximum_fusion.3.refs_5_.refs_1_.refs_2_), channel_id=1, source_target_pairs={{0,1},{1,2},{2,3},{3,0},{4,5},{5,6},{6,7},{7,4},{8,9},{9,10},{10,1... | collective-permute-start | bytes 1572872 | tf_op jit(solution)/shard_map/ppermute | solution.py:803
  26.8 23.7 %collective-permute-start.2 = (bf16[512,512]{1,0:T(8,128)(2,1)}, bf16[512,512]{1,0:T(8,128)(2,1)}, u32[]{:S(2)}, u32[]{:S(2)}) collective-permute-start(bf16[512,512]{1,0:T(8,128)(2,1)} %pad_maximum_fusion.3.refs_5_.refs_1_.refs_2_), channel_id=1, source_target_pairs={{0,8},{4,12},{8,0},{12,4},{1,9},{5,13},{9,1},{13,5},{2,10},{6,14},... | collective-permute-start | bytes 1572872 | tf_op jit(solution)/shard_map/ppermute | solution.py:798
  28.3 24.7 %collective-permute-start.3 = (bf16[512,512]{1,0:T(8,128)(2,1)S(1)}, bf16[512,512]{1,0:T(8,128)(2,1)S(1)}, u32[]{:S(2)}, u32[]{:S(2)}) collective-permute-start(bf16[512,512]{1,0:T(8,128)(2,1)S(1)} %dynamic-slice_bitcast_fusion.1.refs_0_), channel_id=1, source_target_pairs={{0,8},{4,12},{8,0},{12,4},{1,9},{5,13},{9,1},{13,5},{2,10},{6,14},... | collective-permute-start | bytes 1572872 | tf_op jit(solution)/shard_map/ppermute | solution.py:798
  30.0 34.3 %collective-permute-start.5 = (bf16[512,512]{1,0:T(8,128)(2,1)S(1)}, bf16[512,512]{1,0:T(8,128)(2,1)S(1)}, u32[]{:S(2)}, u32[]{:S(2)}) collective-permute-start(bf16[512,512]{1,0:T(8,128)(2,1)S(1)} %dynamic-slice_bitcast_fusion.refs_1_), channel_id=1, source_target_pairs={{0,8},{4,12},{8,0},{12,4},{1,9},{5,13},{9,1},{13,5},{2,10},{6,14},... | collective-permute-start | bytes 1572872 | tf_op jit(solution)/shard_map/ppermute | solution.py:798
  55.7 12.6 %collective-permute-start.4 = (bf16[512,512]{1,0:T(8,128)(2,1)}, bf16[512,512]{1,0:T(8,128)(2,1)S(1)}, u32[]{:S(2)}, u32[]{:S(2)}) collective-permute-start(bf16[512,512]{1,0:T(8,128)(2,1)} %gate.3.refs_6_.refs_2_.refs_3_), channel_id=1, source_target_pairs={{0,1},{1,2},{2,3},{3,0},{4,5},{5,6},{6,7},{7,4},{8,9},{9,10},{10,1... | collective-permute-start | bytes 1572872 | tf_op jit(solution)/shard_map/ppermute | solution.py:803
  57.2 18.6 %collective-permute-start.8 = (bf16[512,512]{1,0:T(8,128)(2,1)}, bf16[512,512]{1,0:T(8,128)(2,1)}, u32[]{:S(2)}, u32[]{:S(2)}) collective-permute-start(bf16[512,512]{1,0:T(8,128)(2,1)} %gate.3.refs_6_.refs_2_.refs_3_), channel_id=1, source_target_pairs={{0,8},{4,12},{8,0},{12,4},{1,9},{5,13},{9,1},{13,5},{2,10},{6,14},... | collective-permute-start | bytes 1572872 | tf_op jit(solution)/shard_map/ppermute | solution.py:798
  70.0 29.6 %collective-permute-start.11 = (bf16[512,512]{1,0:T(8,128)(2,1)}, bf16[512,512]{1,0:T(8,128)(2,1)}, u32[]{:S(2)}, u32[]{:S(2)}) collective-permute-start(bf16[512,512]{1,0:T(8,128)(2,1)} %get-tuple-element.97.refs_2_.refs_1_), channel_id=1, source_target_pairs={{0,1},{1,2},{2,3},{3,0},{4,5},{5,6},{6,7},{7,4},{8,9},{9,10},{10,1... | collective-permute-start | bytes 1572872 | tf_op jit(solution)/shard_map/ppermute | solution.py:803
  71.2 26.9 %collective-permute-start.7 = (bf16[512,512]{1,0:T(8,128)(2,1)}, bf16[512,512]{1,0:T(8,128)(2,1)S(1)}, u32[]{:S(2)}, u32[]{:S(2)}) collective-permute-start(bf16[512,512]{1,0:T(8,128)(2,1)} %copy-done.23), channel_id=1, source_target_pairs={{0,1},{1,2},{2,3},{3,0},{4,5},{5,6},{6,7},{7,4},{8,9},{9,10},{10,1... | collective-permute-start | bytes 1572872 | tf_op jit(solution)/shard_map/ppermute | solution.py:803
  75.4 45.3 %collective-permute-start.6 = (bf16[512,1024]{1,0:T(8,128)(2,1)S(1)}, bf16[512,1024]{1,0:T(8,128)(2,1)}, u32[]{:S(2)}, u32[]{:S(2)}) collective-permute-start(bf16[512,1024]{1,0:T(8,128)(2,1)S(1)} %norm_in.2.refs_3_.refs_1_), channel_id=1, source_target_pairs={{0,4},{4,0},{8,12},{12,8},{1,5},{5,1},{9,13},{13,9},{2,6},{6,2},{1... | collective-permute-start | bytes 3145736 | tf_op jit(solution)/shard_map/ppermute | solution.py:798
  75.5 33.9 %collective-permute-start.12 = (bf16[512,512]{1,0:T(8,128)(2,1)}, bf16[512,512]{1,0:T(8,128)(2,1)S(1)}, u32[]{:S(2)}, u32[]{:S(2)}) collective-permute-start(bf16[512,512]{1,0:T(8,128)(2,1)} %copy-done.61), channel_id=1, source_target_pairs={{0,1},{1,2},{2,3},{3,0},{4,5},{5,6},{6,7},{7,4},{8,9},{9,10},{10,1... | collective-permute-start | bytes 1572872 | tf_op jit(solution)/shard_map/ppermute | solution.py:803
  75.8 26.7 %collective-permute-start.9 = (bf16[512,512]{1,0:T(8,128)(2,1)S(1)}, bf16[512,512]{1,0:T(8,128)(2,1)S(1)}, u32[]{:S(2)}, u32[]{:S(2)}) collective-permute-start(bf16[512,512]{1,0:T(8,128)(2,1)S(1)} %copy-done.24), channel_id=1, source_target_pairs={{0,8},{4,12},{8,0},{12,4},{1,9},{5,13},{9,1},{13,5},{2,10},{6,14},... | collective-permute-start | bytes 1572872 | tf_op jit(solution)/shard_map/ppermute | solution.py:798
  98.1 14.9 %collective-permute-start.10 = (bf16[512,512]{1,0:T(8,128)(2,1)S(1)}, bf16[512,512]{1,0:T(8,128)(2,1)S(1)}, u32[]{:S(2)}, u32[]{:S(2)}) collective-permute-start(bf16[512,512]{1,0:T(8,128)(2,1)S(1)} %collective-permute-done.7.refs_8_.refs_4_.refs_6_.refs_5_), channel_id=1, source_target_pairs={{0,8},{4,12},{8,0},{12,4},{1,9},{5,13},{9,1},{13,5},{2,10},{6,14},... | collective-permute-start | bytes 1572872 | tf_op jit(solution)/shard_map/ppermute | solution.py:798
  99.6 21.1 %collective-permute-start.13 = (bf16[512,512]{1,0:T(8,128)(2,1)}, bf16[512,512]{1,0:T(8,128)(2,1)}, u32[]{:S(2)}, u32[]{:S(2)}) collective-permute-start(bf16[512,512]{1,0:T(8,128)(2,1)} %collective-permute-done.11.refs_13_.refs_3_.refs_2_), channel_id=1, source_target_pairs={{0,1},{1,2},{2,3},{3,0},{4,5},{5,6},{6,7},{7,4},{8,9},{9,10},{10,1... | collective-permute-start | bytes 1572872 | tf_op jit(solution)/shard_map/ppermute | solution.py:803
  102.5 246.7 %copy-start.57 = (bf16[512,512]{1,0:T(8,128)(2,1)}, bf16[512,512]{1,0:T(8,128)(2,1)S(1)}, u32[]{:S(2)}) copy-start(bf16[512,512]{1,0:T(8,128)(2,1)S(1)} %collective-permute-done.9.refs_11_.refs_7_.refs_8_) | copy-start | bytes 1572868
  102.5 39.0 %collective-permute-start.15 = (bf16[512,512]{1,0:T(8,128)(2,1)}, bf16[512,512]{1,0:T(8,128)(2,1)S(1)}, u32[]{:S(2)}, u32[]{:S(2)}) collective-permute-start(bf16[512,512]{1,0:T(8,128)(2,1)} %collective-permute-done.11.refs_13_.refs_3_.refs_2_), channel_id=1, source_target_pairs={{0,8},{4,12},{8,0},{12,4},{1,9},{5,13},{9,1},{13,5},{2,10},{6,14},... | collective-permute-start | bytes 1572872 | tf_op jit(solution)/shard_map/ppermute | solution.py:798
  109.4 32.2 %collective-permute-start.14 = (bf16[512,512]{1,0:T(8,128)(2,1)S(1)}, bf16[512,512]{1,0:T(8,128)(2,1)S(1)}, u32[]{:S(2)}, u32[]{:S(2)}) collective-permute-start(bf16[512,512]{1,0:T(8,128)(2,1)S(1)} %collective-permute-done.12.refs_14_.refs_2_.refs_4_), channel_id=1, source_target_pairs={{0,1},{1,2},{2,3},{3,0},{4,5},{5,6},{6,7},{7,4},{8,9},{9,10},{10,1... | collective-permute-start | bytes 1572872 | tf_op jit(solution)/shard_map/ppermute | solution.py:803
  113.0 236.2 %copy-start.59 = (bf16[512,512]{1,0:T(8,128)(2,1)}, bf16[512,512]{1,0:T(8,128)(2,1)S(1)}, u32[]{:S(2)}) copy-start(bf16[512,512]{1,0:T(8,128)(2,1)S(1)} %collective-permute-done.10.refs_12_.refs_8_.refs_9_) | copy-start | bytes 1572868
  113.0 28.5 %collective-permute-start.16 = (bf16[512,512]{1,0:T(8,128)(2,1)S(1)}, bf16[512,512]{1,0:T(8,128)(2,1)S(1)}, u32[]{:S(2)}, u32[]{:S(2)}) collective-permute-start(bf16[512,512]{1,0:T(8,128)(2,1)S(1)} %collective-permute-done.12.refs_14_.refs_2_.refs_4_), channel_id=1, source_target_pairs={{0,8},{4,12},{8,0},{12,4},{1,9},{5,13},{9,1},{13,5},{2,10},{6,14},... | collective-permute-start | bytes 1572872 | tf_op jit(solution)/shard_map/ppermute | solution.py:798
  120.7 28.9 %collective-permute-start.21 = (bf16[512,512]{1,0:T(8,128)(2,1)}, bf16[512,512]{1,0:T(8,128)(2,1)S(1)}, u32[]{:S(2)}, u32[]{:S(2)}) collective-permute-start(bf16[512,512]{1,0:T(8,128)(2,1)} %collective-permute-done.13.refs_9_.refs_4_.refs_3_), channel_id=1, source_target_pairs={{0,1},{1,2},{2,3},{3,0},{4,5},{5,6},{6,7},{7,4},{8,9},{9,10},{10,1... | collective-permute-start | bytes 1572872 | tf_op jit(solution)/shard_map/ppermute | solution.py:803
  145.5 38.8 %collective-permute-start.17 = (bf16[512,1024]{1,0:T(8,128)(2,1)S(1)}, bf16[512,1024]{1,0:T(8,128)(2,1)S(1)}, u32[]{:S(2)}, u32[]{:S(2)}) collective-permute-start(bf16[512,1024]{1,0:T(8,128)(2,1)S(1)} %get-tuple-element.101), channel_id=1, source_target_pairs={{0,4},{4,0},{8,12},{12,8},{1,5},{5,1},{9,13},{13,9},{2,6},{6,2},{1... | collective-permute-start | bytes 3145736 | tf_op jit(solution)/shard_map/ppermute | solution.py:798
  145.6 16.8 %collective-permute-start.18 = (bf16[512,512]{1,0:T(8,128)(2,1)}, bf16[512,512]{1,0:T(8,128)(2,1)S(1)}, u32[]{:S(2)}, u32[]{:S(2)}) collective-permute-start(bf16[512,512]{1,0:T(8,128)(2,1)} %copy-done.27), channel_id=1, source_target_pairs={{0,1},{1,2},{2,3},{3,0},{4,5},{5,6},{6,7},{7,4},{8,9},{9,10},{10,1... | collective-permute-start | bytes 1572872 | tf_op jit(solution)/shard_map/ppermute | solution.py:803
  147.6 15.0 %collective-permute-start.19 = (bf16[512,512]{1,0:T(8,128)(2,1)}, bf16[512,512]{1,0:T(8,128)(2,1)S(1)}, u32[]{:S(2)}, u32[]{:S(2)}) collective-permute-start(bf16[512,512]{1,0:T(8,128)(2,1)} %collective-permute-done.13.refs_9_.refs_4_.refs_3_), channel_id=1, source_target_pairs={{0,8},{4,12},{8,0},{12,4},{1,9},{5,13},{9,1},{13,5},{2,10},{6,14},... | collective-permute-start | bytes 1572872 | tf_op jit(solution)/shard_map/ppermute | solution.py:798
  149.1 24.7 %collective-permute-start.20 = (bf16[512,512]{1,0:T(8,128)(2,1)}, bf16[512,512]{1,0:T(8,128)(2,1)S(1)}, u32[]{:S(2)}, u32[]{:S(2)}) collective-permute-start(bf16[512,512]{1,0:T(8,128)(2,1)} %copy-done.27), channel_id=1, source_target_pairs={{0,8},{4,12},{8,0},{12,4},{1,9},{5,13},{9,1},{13,5},{2,10},{6,14},... | collective-permute-start | bytes 1572872 | tf_op jit(solution)/shard_map/ppermute | solution.py:798
  149.6 34.6 %collective-permute-start.22 = (bf16[512,512]{1,0:T(8,128)(2,1)S(1)}, bf16[512,512]{1,0:T(8,128)(2,1)S(1)}, u32[]{:S(2)}, u32[]{:S(2)}) collective-permute-start(bf16[512,512]{1,0:T(8,128)(2,1)S(1)} %collective-permute-done.21.refs_5_.refs_4_), channel_id=1, source_target_pairs={{0,8},{4,12},{8,0},{12,4},{1,9},{5,13},{9,1},{13,5},{2,10},{6,14},... | collective-permute-start | bytes 1572872 | tf_op jit(solution)/shard_map/ppermute | solution.py:798
  189.9 2.7 collective-permute-start.23
  190.0 16.2 %collective-permute-start.24 = (bf16[512,512]{1,0:T(8,128)(2,1)}, bf16[512,512]{1,0:T(8,128)(2,1)S(1)}, u32[]{:S(2)}, u32[]{:S(2)}) collective-permute-start(bf16[512,512]{1,0:T(8,128)(2,1)} %copy-done.31), channel_id=1, source_target_pairs={{0,8},{4,12},{8,0},{12,4},{1,9},{5,13},{9,1},{13,5},{2,10},{6,14},... | collective-permute-start | bytes 1572872 | tf_op jit(solution)/shard_map/ppermute | solution.py:798
  210.7 2.7 collective-permute-start.25
  215.3 25.8 %collective-permute-start.26 = (bf16[512,1024]{1,0:T(8,128)(2,1)S(1)}, bf16[512,1024]{1,0:T(8,128)(2,1)S(1)}, u32[]{:S(2)}, u32[]{:S(2)}) collective-permute-start(bf16[512,1024]{1,0:T(8,128)(2,1)S(1)} %get-tuple-element.132), channel_id=1, source_target_pairs={{0,16},{1,17},{2,18},{3,19},{4,20},{5,21},{6,22},{7,23},{8,24},{9,... | collective-permute-start | bytes 3145736 | tf_op jit(solution)/shard_map/ppermute | solution.py:28
  242.9 2.7 collective-permute-start.27
  265.6 2.7 collective-permute-start.28
  271.8 2.7 collective-permute-start.29
  290.5 2.7 collective-permute-start.30
  297.4 2.7 collective-permute-start.31
  315.2 2.7 collective-permute-start.32
  321.8 2.7 collective-permute-start.33
  356.3 2.7 collective-permute-start.34
  361.3 27.2 %collective-permute-start.35 = (bf16[512,1024]{1,0:T(8,128)(2,1)S(1)}, bf16[512,1024]{1,0:T(8,128)(2,1)S(1)}, u32[]{:S(2)}, u32[]{:S(2)}) collective-permute-start(bf16[512,1024]{1,0:T(8,128)(2,1)S(1)} %get-tuple-element.131.refs_2_), channel_id=1, source_target_pairs={{16,0},{17,1},{18,2},{19,3},{20,4},{21,5},{22,6},{23,7},{24,8},{25... | collective-permute-start | bytes 3145736 | tf_op jit(solution)/shard_map/ppermute | solution.py:28
  364.1 31.0 %all-to-all-start.1 = ((bf16[4,128,1024]{2,1,0:T(8,128)(2,1)}), bf16[4,128,1024]{2,1,0:T(8,128)(2,1)}, u32[]{:S(2)}, u32[]{:S(2)}) async-start(bf16[4,128,1024]{2,1,0:T(8,128)(2,1)} %bitcast.43), calls=%async_computation.1 | async-start | bytes 2097152 | tf_op jit(solution)/shard_map/all_to_all | solution.py:1224
  392.6 2.7 collective-permute-start.36
  419.2 2.7 collective-permute-start.37
  419.4 26.0 %collective-permute-start.41 = (bf16[1024,512]{1,0:T(8,128)(2,1)S(1)}, bf16[1024,512]{1,0:T(8,128)(2,1)S(1)}, u32[]{:S(2)}, u32[]{:S(2)}) collective-permute-start(bf16[1024,512]{1,0:T(8,128)(2,1)S(1)} %get-tuple-element.149), channel_id=1, source_target_pairs={{0,8},{4,12},{8,0},{12,4},{1,9},{5,13},{9,1},{13,5},{2,10},{6,14},... | collective-permute-start | bytes 3145736 | tf_op jit(solution)/shard_map/ppermute | solution.py:798
  426.8 33.5 %collective-permute-start.39 = (bf16[512,1024]{1,0:T(8,128)(2,1)}, bf16[512,1024]{1,0:T(8,128)(2,1)S(1)}, u32[]{:S(2)}, u32[]{:S(2)}) collective-permute-start(bf16[512,1024]{1,0:T(8,128)(2,1)} %get-tuple-element.141.refs_2_.refs_3_.refs_5_), channel_id=1, source_target_pairs={{0,4},{4,0},{8,12},{12,8},{1,5},{5,1},{9,13},{13,9},{2,6},{6,2},{1... | collective-permute-start | bytes 3145736 | tf_op jit(solution)/shard_map/ppermute | solution.py:798
  428.4 2.0 collective-permute-start.38
  428.9 45.5 %collective-permute-start.40 = (bf16[1024,512]{1,0:T(8,128)(2,1)S(1)}, bf16[1024,512]{1,0:T(8,128)(2,1)S(1)}, u32[]{:S(2)}, u32[]{:S(2)}) collective-permute-start(bf16[1024,512]{1,0:T(8,128)(2,1)S(1)} %get-tuple-element.148), channel_id=1, source_target_pairs={{0,8},{4,12},{8,0},{12,4},{1,9},{5,13},{9,1},{13,5},{2,10},{6,14},... | collective-permute-start | bytes 3145736 | tf_op jit(solution)/shard_map/ppermute | solution.py:798
  445.8 28.5 %collective-permute-start.42 = (bf16[1024,512]{1,0:T(8,128)(2,1)S(1)}, bf16[1024,512]{1,0:T(8,128)(2,1)S(1)}, u32[]{:S(2)}, u32[]{:S(2)}) collective-permute-start(bf16[1024,512]{1,0:T(8,128)(2,1)S(1)} %moved.6.refs_13_), channel_id=1, source_target_pairs={{0,3},{1,0},{2,1},{3,2},{4,7},{5,4},{6,5},{7,6},{8,11},{9,8},{10,9... | collective-permute-start | bytes 3145736 | tf_op jit(solution)/shard_map/ppermute | solution.py:803
  458.3 40.8 %collective-permute-start.44 = (bf16[1024,512]{1,0:T(8,128)(2,1)S(1)}, bf16[1024,512]{1,0:T(8,128)(2,1)S(1)}, u32[]{:S(2)}, u32[]{:S(2)}) collective-permute-start(bf16[1024,512]{1,0:T(8,128)(2,1)S(1)} %get-tuple-element.154), channel_id=1, source_target_pairs={{0,8},{4,12},{8,0},{12,4},{1,9},{5,13},{9,1},{13,5},{2,10},{6,14},... | collective-permute-start | bytes 3145736 | tf_op jit(solution)/shard_map/ppermute | solution.py:798
  459.8 64.7 %collective-permute-start.47 = (bf16[1024,512]{1,0:T(8,128)(2,1)S(1)}, bf16[1024,512]{1,0:T(8,128)(2,1)S(1)}, u32[]{:S(2)}, u32[]{:S(2)}) collective-permute-start(bf16[1024,512]{1,0:T(8,128)(2,1)S(1)} %get-tuple-element.156), channel_id=1, source_target_pairs={{0,8},{4,12},{8,0},{12,4},{1,9},{5,13},{9,1},{13,5},{2,10},{6,14},... | collective-permute-start | bytes 3145736 | tf_op jit(solution)/shard_map/ppermute | solution.py:798
  475.7 23.4 %collective-permute-start.45 = (bf16[1024,512]{1,0:T(8,128)(2,1)S(1)}, bf16[1024,512]{1,0:T(8,128)(2,1)S(1)}, u32[]{:S(2)}, u32[]{:S(2)}) collective-permute-start(bf16[1024,512]{1,0:T(8,128)(2,1)S(1)} %moved.7.refs_13_), channel_id=1, source_target_pairs={{0,3},{1,0},{2,1},{3,2},{4,7},{5,4},{6,5},{7,6},{8,11},{9,8},{10,9... | collective-permute-start | bytes 3145736 | tf_op jit(solution)/shard_map/ppermute | solution.py:803
  499.6 24.9 %collective-permute-start.46 = (bf16[1024,512]{1,0:T(8,128)(2,1)S(1)}, bf16[1024,512]{1,0:T(8,128)(2,1)S(1)}, u32[]{:S(2)}, u32[]{:S(2)}) collective-permute-start(bf16[1024,512]{1,0:T(8,128)(2,1)S(1)} %moved.8.refs_13_), channel_id=1, source_target_pairs={{0,3},{1,0},{2,1},{3,2},{4,7},{5,4},{6,5},{7,6},{8,11},{9,8},{10,9... | collective-permute-start | bytes 3145736 | tf_op jit(solution)/shard_map/ppermute | solution.py:803
  503.9 19.5 %collective-permute-start.43 = (bf16[512,512]{1,0:T(8,128)(2,1)S(1)}, bf16[512,512]{1,0:T(8,128)(2,1)S(1)}, u32[]{:S(2)}, u32[]{:S(2)}) collective-permute-start(bf16[512,512]{1,0:T(8,128)(2,1)S(1)} %get-tuple-element.153), channel_id=1, source_target_pairs={{0,8},{4,12},{8,0},{12,4},{1,9},{5,13},{9,1},{13,5},{2,10},{6,14},... | collective-permute-start | bytes 1572872 | tf_op jit(solution)/shard_map/ppermute | solution.py:798
  531.4 20.7 %collective-permute-start.48 = (bf16[512,1024]{1,0:T(8,128)(2,1)S(1)}, bf16[512,1024]{1,0:T(8,128)(2,1)S(1)}, u32[]{:S(2)}, u32[]{:S(2)}) collective-permute-start(bf16[512,1024]{1,0:T(8,128)(2,1)S(1)} %get-tuple-element.158), channel_id=1, source_target_pairs={{0,4},{4,0},{8,12},{12,8},{1,5},{5,1},{9,13},{13,9},{2,6},{6,2},{1... | collective-permute-start | bytes 3145736 | tf_op jit(solution)/shard_map/ppermute | solution.py:798
  531.5 14.8 %collective-permute-start.49 = (bf16[512,512]{1,0:T(8,128)(2,1)S(1)}, bf16[512,512]{1,0:T(8,128)(2,1)S(1)}, u32[]{:S(2)}, u32[]{:S(2)}) collective-permute-start(bf16[512,512]{1,0:T(8,128)(2,1)S(1)} %get-tuple-element.160), channel_id=1, source_target_pairs={{0,8},{4,12},{8,0},{12,4},{1,9},{5,13},{9,1},{13,5},{2,10},{6,14},... | collective-permute-start | bytes 1572872 | tf_op jit(solution)/shard_map/ppermute | solution.py:798
  533.1 14.4 %collective-permute-start.50 = (bf16[512,512]{1,0:T(8,128)(2,1)S(1)}, bf16[512,512]{1,0:T(8,128)(2,1)S(1)}, u32[]{:S(2)}, u32[]{:S(2)}) collective-permute-start(bf16[512,512]{1,0:T(8,128)(2,1)S(1)} %copy-done.121), channel_id=1, source_target_pairs={{0,3},{1,0},{2,1},{3,2},{4,7},{5,4},{6,5},{7,6},{8,11},{9,8},{10,9... | collective-permute-start | bytes 1572872 | tf_op jit(solution)/shard_map/ppermute | solution.py:803
  535.9 21.1 %collective-permute-start.52 = (bf16[512,512]{1,0:T(8,128)(2,1)S(1)}, bf16[512,512]{1,0:T(8,128)(2,1)S(1)}, u32[]{:S(2)}, u32[]{:S(2)}) collective-permute-start(bf16[512,512]{1,0:T(8,128)(2,1)S(1)} %get-tuple-element.163), channel_id=1, source_target_pairs={{0,8},{4,12},{8,0},{12,4},{1,9},{5,13},{9,1},{13,5},{2,10},{6,14},... | collective-permute-start | bytes 1572872 | tf_op jit(solution)/shard_map/ppermute | solution.py:798
  547.7 15.0 %collective-permute-start.51 = (bf16[512,512]{1,0:T(8,128)(2,1)S(1)}, bf16[512,512]{1,0:T(8,128)(2,1)S(1)}, u32[]{:S(2)}, u32[]{:S(2)}) collective-permute-start(bf16[512,512]{1,0:T(8,128)(2,1)S(1)} %moved.10), channel_id=1, source_target_pairs={{0,3},{1,0},{2,1},{3,2},{4,7},{5,4},{6,5},{7,6},{8,11},{9,8},{10,9... | collective-permute-start | bytes 1572872 | tf_op jit(solution)/shard_map/ppermute | solution.py:803
  565.1 36.4 %all-to-all-start.2 = ((bf16[4,128,1024]{2,1,0:T(8,128)(2,1)}), bf16[4,128,1024]{2,1,0:T(8,128)(2,1)S(1)}, u32[]{:S(2)}, u32[]{:S(2)}) async-start(bf16[4,128,1024]{2,1,0:T(8,128)(2,1)} %bitcast.16), calls=%async_computation.2 | async-start | bytes 2097152 | tf_op jit(solution)/shard_map/all_to_all | solution.py:1306
  570.8 12.2 %collective-permute-start.53 = (bf16[512,512]{1,0:T(8,128)(2,1)}, bf16[512,512]{1,0:T(8,128)(2,1)S(1)}, u32[]{:S(2)}, u32[]{:S(2)}) collective-permute-start(bf16[512,512]{1,0:T(8,128)(2,1)} %copy-done.124), channel_id=1, source_target_pairs={{0,8},{4,12},{8,0},{12,4},{1,9},{5,13},{9,1},{13,5},{2,10},{6,14},... | collective-permute-start | bytes 1572872 | tf_op jit(solution)/shard_map/ppermute | solution.py:798
  585.1 16.4 %collective-permute-start.54 = (bf16[512,512]{1,0:T(8,128)(2,1)S(1)}, bf16[512,512]{1,0:T(8,128)(2,1)S(1)}, u32[]{:S(2)}, u32[]{:S(2)}) collective-permute-start(bf16[512,512]{1,0:T(8,128)(2,1)S(1)} %moved.11.refs_1_), channel_id=1, source_target_pairs={{0,3},{1,0},{2,1},{3,2},{4,7},{5,4},{6,5},{7,6},{8,11},{9,8},{10,9... | collective-permute-start | bytes 1572872 | tf_op jit(solution)/shard_map/ppermute | solution.py:803
  590.0 36.0 %collective-permute-start.56 = (f32[256,512]{1,0:T(8,128)}, f32[256,512]{1,0:T(8,128)S(1)}, u32[]{:S(2)}, u32[]{:S(2)}) collective-permute-start(f32[256,512]{1,0:T(8,128)} %get-tuple-element.179), channel_id=1, source_target_pairs={{0,4},{4,0},{8,12},{12,8},{1,5},{5,1},{9,13},{13,9},{2,6},{6,2},{1... | collective-permute-start | bytes 1572872 | tf_op jit(solution)/shard_map/ppermute | solution.py:798
  590.0 36.0 %collective-permute-start.57 = (f32[512,256]{1,0:T(8,128)}, f32[512,256]{1,0:T(8,128)}, u32[]{:S(2)}, u32[]{:S(2)}) collective-permute-start(f32[512,256]{1,0:T(8,128)} %get-tuple-element.180), channel_id=1, source_target_pairs={{0,4},{4,0},{8,12},{12,8},{1,5},{5,1},{9,13},{13,9},{2,6},{6,2},{1... | collective-permute-start | bytes 1572872 | tf_op jit(solution)/shard_map/ppermute | solution.py:798
  603.9 24.7 %collective-permute-start.55 = (bf16[2,128,1024]{2,1,0:T(8,128)(2,1)}, bf16[2,128,1024]{2,1,0:T(8,128)(2,1)S(1)}, u32[]{:S(2)}, u32[]{:S(2)}) collective-permute-start(bf16[2,128,1024]{2,1,0:T(8,128)(2,1)} %get-tuple-element.166), channel_id=1, source_target_pairs={{0,4},{4,0},{8,12},{12,8},{1,5},{5,1},{9,13},{13,9},{2,6},{6,2},{1... | collective-permute-start | bytes 1572872 | tf_op jit(solution)/shard_map/ppermute | solution.py:798
  629.9 2.0 collective-permute-start.58
  (131 other events, 1218.7 us)

commit v16 on v15

--- a/solution.py
+++ b/solution.py
@@ -1212,7 +1212,7 @@
             (up_piece, up_other[0], down_other[0]),
             (up_own[1], down_own[1]),
             (up_own[2], down_own[2], up_other[1], down_other[1]),
-            (down_own[3], up_other[2], down_other[2], up_other[3]),
+            (up_own[3], down_own[3], up_other[2], down_other[2]),
         ),
     )
     low_one, saved_one, lefts_one = forward(shifted(low_zero, "section", 1), ((),) * 4)
@@ -1328,7 +1328,6 @@
     )
     waits = (grads_chosen, attn_sums[0][1])
     last, attn_moves[1] = moves_on(attn_sums[1], attn_moves[2], waits=waits)
-    grads = from_chip(grads, (attn_moves[1],))
     gain_total = own_first(jnp.where(first, gain_zero, gain_one))
     count = tensor * lax.axis_size("dp")
     gain_parts = gain_total.reshape(4, count, width // count).swapaxes(0, 1)
@@ -1336,6 +1335,7 @@
     (gain_parts,) = on_chip(gate_kernel, "gate", outs, gain_parts, waits=(last,))
     gain_parts = lax.all_to_all(gain_parts, ("dp", "tensor"), 0, 0, tiled=True)
     gains_grad = jnp.sum(gain_parts, axis=0)
+    grads = from_chip(grads, (attn_moves[1], gains_grad))
     outs = (((wide_half // 2, 512), jnp.float32),) * 2
     keep, send = with_core(
         last_sum_kernel,

time: 646 us -> 632 us (0.978)
  the two profiles are of different devices: /device:TPU:0 before, /device:TPU:9 now
where the time goes in v16:
time: 632 us; the launch traced here: 623 us
  Pallas kernels  228 us (36%)
  waiting for transfers between devices  221 us (35%)
  starting transfers between devices  74.3 us (12%)
  local copies, waits for them, and re-layouts  64.2 us (10%)
  other arithmetic  19.3 us (3%)
  blocking collectives  13.6 us (2%)
    ppermute x15, waiting for transfers between devices, passed_on(): lax.ppermute(block, 'tensor', [(i, (i + step) % size) for i in range(size)])  99.4 us
    pallas_call x31, Pallas kernels, on_chip(): pl.pallas_call(without(kernel, len(operands), len(waits)), in_specs=[spac...  90.4 us
    pallas_call x6, Pallas kernels, by_pairs(): pl.pallas_call(without(functools.partial(kernel, len(pieces[0])), taken,...  85.8 us
    ppermute x42, waiting for transfers between devices, flip_pairs(): return lax.ppermute(block, 'dp', [(i, i ^ distance) for i in range(size)])  82.1 us
    unnamed x280, local copies, waits for them, and re-layouts  53.5 us
    ppermute x2, waiting for transfers between devices, shifted(): return lax.ppermute(block, axis, route)  39.3 us
    ppermute x42, starting transfers between devices, flip_pairs(): return lax.ppermute(block, 'dp', [(i, i ^ distance) for i in range(size)])  37.3 us
    pallas_call x4, Pallas kernels, weight_grads(): pl.pallas_call(without(functools.partial(kernel, base), 1 + len(arrays),...  27.2 us
  transfers between devices with their start and end apart: 62, of which 31 were waited for; matrix products, arithmetic and copies ran while one was open for 4% of the time, Pallas kernels for 15%

profile of v16, /device:TPU:9, one launch (start us, length us, event | category | flops | bytes accessed | tf_op | source)
XLA Modules:
  0.0 622.6 jit_solution(10301996256859380023)
XLA Ops:
  11.6 4.8 all-to-all-start
  26.3 23.6 %collective-permute-done.1.refs_0_ = bf16[512,512]{1,0:T(8,128)(2,1)} collective-permute-done((bf16[512,512]{1,0:T(8,128)(2,1)}, bf16[512,512]{1,0:T(8,128)(2,1)}, u32[]{:S(2)}, u32[]{:S(2)}) %collective-permute-start.1) | collective-permute-done | bytes 524320 | tf_op jit(solution)/shard_map/ppermute | solution.py:803
  52.5 2.2 collective-permute-start.4
  57.3 7.4 %collective-permute-done.4.refs_2_.refs_7_.refs_3_.refs_5_.refs_4_ = bf16[512,512]{1,0:T(8,128)(2,1)S(1)} collective-permute-done((bf16[512,512]{1,0:T(8,128)(2,1)}, bf16[512,512]{1,0:T(8,128)(2,1)S(1)}, u32[]{:S(2)}, u32[]{:S(2)}) %collective-permute-start.4) | collective-permute-done | bytes 524320 | tf_op jit(solution)/shard_map/ppermute | solution.py:803
  71.7 5.1 collective-permute-start.6
  83.1 7.6 %collective-permute-done.11.refs_13_.refs_3_.refs_2_ = bf16[512,512]{1,0:T(8,128)(2,1)S(1)} collective-permute-done((bf16[512,512]{1,0:T(8,128)(2,1)}, bf16[512,512]{1,0:T(8,128)(2,1)S(1)}, u32[]{:S(2)}, u32[]{:S(2)}) %collective-permute-start.11) | collective-permute-done | bytes 524320 | tf_op jit(solution)/shard_map/ppermute | solution.py:803
  92.4 9.5 %collective-permute-done.12.refs_14_.refs_2_.refs_4_ = bf16[512,512]{1,0:T(8,128)(2,1)S(1)} collective-permute-done((bf16[512,512]{1,0:T(8,128)(2,1)}, bf16[512,512]{1,0:T(8,128)(2,1)S(1)}, u32[]{:S(2)}, u32[]{:S(2)}) %collective-permute-start.12) | collective-permute-done | bytes 524320 | tf_op jit(solution)/shard_map/ppermute | solution.py:803
  103.6 16.9 %attend.2 = (bf16[4,1024,128]{2,1,0:T(8,128)(2,1)S(1)}, bf16[4,1024,128]{2,1,0:T(8,128)(2,1)S(1)}, bf16[4,1024,128]{2,1,0:T(8,128)(2,1)S(1)}, f32[4,2,1024]{2,1,0:T(2,128)S(1)}, bf16[1024,512]{1,0:T(8,128)(2,1)S(1)}) custom-call(s32[1]{0:T(128)} %bitcast.refs_0_, f32[1024,128]{1,0:T(8,128)S(1)} %get-tuple-element.228.refs_1_, ...), custom_call_target="tpu_custom_call" | custom-call | flops 11811160064 | bytes 11567104 | tf_op jit(solution)/shard_map/attend/pallas_call | solution.py:708
  125.6 3.0 attn_out.2
  128.6 4.9 collective-permute-start.17
  135.2 12.0 %collective-permute-done.18.refs_4_.refs_5_ = bf16[512,512]{1,0:T(8,128)(2,1)S(1)} collective-permute-done((bf16[512,512]{1,0:T(8,128)(2,1)}, bf16[512,512]{1,0:T(8,128)(2,1)S(1)}, u32[]{:S(2)}, u32[]{:S(2)}) %collective-permute-start.18) | collective-permute-done | bytes 524320 | tf_op jit(solution)/shard_map/ppermute | solution.py:803
  147.1 11.2 %collective-permute-done.19.refs_5_.refs_4_.refs_6_ = bf16[512,512]{1,0:T(8,128)(2,1)S(1)} collective-permute-done((bf16[512,512]{1,0:T(8,128)(2,1)}, bf16[512,512]{1,0:T(8,128)(2,1)S(1)}, u32[]{:S(2)}, u32[]{:S(2)}) %collective-permute-start.19) | collective-permute-done | bytes 524320 | tf_op jit(solution)/shard_map/ppermute | solution.py:803
  159.6 3.4 after_attn.2
  166.9 12.2 %collective-permute-done.23.refs_9_.refs_8_ = bf16[512,512]{1,0:T(8,128)(2,1)S(1)} collective-permute-done((bf16[512,512]{1,0:T(8,128)(2,1)}, bf16[512,512]{1,0:T(8,128)(2,1)S(1)}, u32[]{:S(2)}, u32[]{:S(2)}) %collective-permute-start.23) | collective-permute-done | bytes 524320 | tf_op jit(solution)/shard_map/ppermute | solution.py:798
  181.4 7.7 %mlp_up.2 = (bf16[1024,2048]{1,0:T(8,128)(2,1)S(1)}, bf16[1024,2048]{1,0:T(8,128)(2,1)S(1)}) custom-call(bf16[512,1024]{1,0:T(8,128)(2,1)S(1)} %get-tuple-element.103.refs_0_.refs_1_, bf16[512,1024]{1,0:T(8,128)(2,1)S(1)} %collective-permute-done.22.refs_1_.refs_2_, bf16[512,512]{1,0:T(8,128)(2,1)S(1)} %copy-done.109, bf16[512,512]{1,0:T(8,128)(2,1)S(1)} %copy-done.126, ...), custom_call_target="tpu_custom_call" | custom-call | flops 4294967296 | bytes 14680064 | tf_op jit(solution)/shard_map/mlp_up/pallas_call | solution.py:690
  191.2 4.5 mlp_down.2
  197.0 2.3 collective-permute-done.25.refs_3_
  201.2 3.3 collective-permute-start.26
  204.5 21.7 %collective-permute-done.26.refs_1_ = bf16[512,1024]{1,0:T(8,128)(2,1)S(1)} collective-permute-done((bf16[512,1024]{1,0:T(8,128)(2,1)S(1)}, bf16[512,1024]{1,0:T(8,128)(2,1)S(1)}, u32[]{:S(2)}, u32[]{:S(2)}) %collective-permute-start.26) | collective-permute-done | bytes 1048608 | tf_op jit(solution)/shard_map/ppermute | solution.py:28
  229.2 2.3 collective-permute-done.27.refs_4_.refs_8_
  231.5 16.9 %attend.3 = (bf16[4,1024,128]{2,1,0:T(8,128)(2,1)S(1)}, bf16[4,1024,128]{2,1,0:T(8,128)(2,1)S(1)}, bf16[4,1024,128]{2,1,0:T(8,128)(2,1)S(1)}, f32[4,2,1024]{2,1,0:T(2,128)S(1)}, bf16[1024,512]{1,0:T(8,128)(2,1)S(1)}) custom-call(s32[1]{0:T(128)} %bitcast.refs_0_, f32[1024,128]{1,0:T(8,128)S(1)} %get-tuple-element.228.refs_1_, ...), custom_call_target="tpu_custom_call" | custom-call | flops 11811160064 | bytes 11567104 | tf_op jit(solution)/shard_map/attend/pallas_call | solution.py:708
  248.5 3.3 attn_out.3
  252.3 2.3 collective-permute-done.28.refs_3_
  254.5 3.4 after_attn.3
  258.4 2.3 collective-permute-done.29.refs_1_.refs_8_
  260.7 7.7 %mlp_up.3 = (bf16[1024,2048]{1,0:T(8,128)(2,1)S(1)}, bf16[1024,2048]{1,0:T(8,128)(2,1)S(1)}) custom-call(bf16[512,1024]{1,0:T(8,128)(2,1)S(1)} %get-tuple-element.112.refs_0_.refs_7_, bf16[512,1024]{1,0:T(8,128)(2,1)S(1)} %collective-permute-done.29.refs_1_.refs_8_, bf16[512,512]{1,0:T(8,128)(2,1)S(1)} %copy-done.109, bf16[512,512]{1,0:T(8,128)(2,1)S(1)} %copy-done.126, ...), custom_call_target="tpu_custom_call" | custom-call | flops 4294967296 | bytes 14680064 | tf_op jit(solution)/shard_map/mlp_up/pallas_call | solution.py:690
  270.5 4.5 mlp_down.3
  275.4 2.3 collective-permute-done.30.refs_3_
  279.6 2.3 into_mlp_back.2
  282.3 2.3 collective-permute-done.31.refs_1_.refs_12_
  284.6 7.2 %mlp_up_back.2.refs_0_.refs_9_ = bf16[1024,2048]{1,0:T(8,128)(2,1)S(1)} custom-call(bf16[512,1024]{1,0:T(8,128)(2,1)S(1)} %get-tuple-element.118.refs_0_.refs_11_, bf16[512,1024]{1,0:T(8,128)(2,1)S(1)} %collective-permute-done.31.refs_1_.refs_12_, bf16[1024,2048]{1,0:T(8,128)(2,1)} %copy-done.35, bf16[512,512]{1,0:T(8,128)(2,1)} %copy-done.57, ...), custom_call_target="tpu_custom_call" | custom-call | tf_op jit(solution)/shard_map/mlp_up_back/pallas_call | solution.py:729
  291.8 4.5 mlp_back.2
  296.8 2.3 collective-permute-done.32.refs_3_
  299.1 3.9 into_attn_back.2
  303.5 2.3 collective-permute-done.33.refs_4_.refs_12_
  305.8 13.1 %attend_back.4.refs_0_.refs_9_ = bf16[1024,768]{1,0:T(8,128)(2,1)S(1)} custom-call(s32[1]{0:T(128)} %bitcast.refs_0_, f32[1024,128]{1,0:T(8,128)S(1)} %get-tuple-element.228.refs_1_, f32[1024,128]{1,0:T(8,128)S(1)} %get-tuple-element.229.refs_2_, bf16[512,1024]{1,0:T(8,128)(2,1)S(1)} %get-tuple-element.123.refs_3_.refs_11_, ...), custom_call_target="tpu_custom_call" | custom-call | flops 11274289152 | bytes 6815744 | tf_op jit(solution)/shard_map/attend_back/pallas_call | solution.py:708
  318.9 12.8 %attend_back.5.refs_1_.refs_9_ = bf16[1024,768]{1,0:T(8,128)(2,1)S(1)} custom-call(s32[1]{0:T(128)} %bitcast.refs_0_, f32[1024,128]{1,0:T(8,128)S(1)} %get-tuple-element.228.refs_1_, f32[1024,128]{1,0:T(8,128)S(1)} %get-tuple-element.229.refs_2_, bf16[512,1024]{1,0:T(8,128)(2,1)S(1)} %get-tuple-element.123.refs_3_.refs_11_, ...), custom_call_target="tpu_custom_call" | custom-call | flops 11274289152 | bytes 6815744 | tf_op jit(solution)/shard_map/attend_back/pallas_call | solution.py:708
  333.4 5.7 attn_back.2
  339.5 2.3 collective-permute-done.34.refs_3_
  341.8 2.2 out_of_layer.2
  346.9 6.2 all-to-all-start.1
  353.0 17.6 %collective-permute-done.35.refs_1_ = bf16[512,1024]{1,0:T(8,128)(2,1)S(1)} collective-permute-done((bf16[512,1024]{1,0:T(8,128)(2,1)S(1)}, bf16[512,1024]{1,0:T(8,128)(2,1)S(1)}, u32[]{:S(2)}, u32[]{:S(2)}) %collective-permute-start.35) | collective-permute-done | bytes 1048608 | tf_op jit(solution)/shard_map/ppermute | solution.py:28
  372.6 2.1 into_mlp_back.3
  375.8 2.3 collective-permute-done.36.refs_1_.refs_6_
  378.1 7.2 %mlp_up_back.3.refs_3_.refs_0_ = bf16[1024,2048]{1,0:T(8,128)(2,1)S(1)} custom-call(bf16[512,1024]{1,0:T(8,128)(2,1)S(1)} %get-tuple-element.135.refs_0_.refs_5_, bf16[512,1024]{1,0:T(8,128)(2,1)S(1)} %collective-permute-done.36.refs_1_.refs_6_, bf16[1024,2048]{1,0:T(8,128)(2,1)} %copy-done.50, bf16[512,512]{1,0:T(8,128)(2,1)} %copy-done.57, ...), custom_call_target="tpu_custom_call" | custom-call | tf_op jit(solution)/shard_map/mlp_up_back/pallas_call | solution.py:729
  387.3 7.2 %mlp_grads.2 = (f32[1024,512]{1,0:T(8,128)S(1)}, bf16[1024,512]{1,0:T(8,128)(2,1)S(1)}, f32[1024,512]{1,0:T(8,128)S(1)}, bf16[1024,512]{1,0:T(8,128)(2,1)S(1)}) custom-call(s32[1]{0:T(128)} %bitcast.12.refs_0_, bf16[512,1024]{1,0:T(8,128)(2,1)} %copy-done.37, bf16[512,1024]{1,0:T(8,128)(2,1)} %copy-done.38, bf16[1024,2048]{1,0:T(8,128)(2,1)} %copy-done.3, ...), custom_call_target="tpu_custom_call" | custom-call | tf_op jit(solution)/shard_map/mlp_grads/pallas_call | solution.py:897
  396.0 4.5 mlp_back.3
  403.2 4.9 into_attn_back.3
  413.0 12.6 %collective-permute-done.41.refs_1_ = bf16[1024,512]{1,0:T(8,128)(2,1)S(1)} collective-permute-done((bf16[1024,512]{1,0:T(8,128)(2,1)S(1)}, bf16[1024,512]{1,0:T(8,128)(2,1)S(1)}, u32[]{:S(2)}, u32[]{:S(2)}) %collective-permute-start.41) | collective-permute-done | bytes 1048608 | tf_op jit(solution)/shard_map/ppermute | solution.py:798
  427.7 7.3 %mlp_grads.3 = (f32[1024,512]{1,0:T(8,128)S(1)}, bf16[1024,512]{1,0:T(8,128)(2,1)S(1)}, f32[1024,512]{1,0:T(8,128)S(1)}, bf16[1024,512]{1,0:T(8,128)(2,1)S(1)}) custom-call(s32[1]{0:T(128)} %bitcast.12.refs_0_, bf16[512,1024]{1,0:T(8,128)(2,1)} %copy-done.37, bf16[512,1024]{1,0:T(8,128)(2,1)} %copy-done.38, bf16[1024,2048]{1,0:T(8,128)(2,1)} %copy-done.3, ...), custom_call_target="tpu_custom_call" | custom-call | tf_op jit(solution)/shard_map/mlp_grads/pallas_call | solution.py:897
  439.3 12.9 %attend_back.6.refs_3_.refs_1_ = bf16[1024,768]{1,0:T(8,128)(2,1)S(1)} custom-call(s32[1]{0:T(128)} %bitcast.refs_0_, f32[1024,128]{1,0:T(8,128)S(1)} %copy-done.105, f32[1024,128]{1,0:T(8,128)S(1)} %copy-done.107, bf16[512,1024]{1,0:T(8,128)(2,1)} %get-tuple-element.141.refs_2_.refs_3_.refs_5_, ...), custom_call_target="tpu_custom_call" | custom-call | flops 11274289152 | bytes 6815744 | tf_op jit(solution)/shard_map/attend_back/pallas_call | solution.py:708
  454.8 2.9 collective-permute-start.45
  457.7 5.9 attn_grads.2
  464.5 13.2 %attend_back.7.refs_3_.refs_0_ = bf16[1024,768]{1,0:T(8,128)(2,1)S(1)} custom-call(s32[1]{0:T(128)} %bitcast.refs_0_, f32[1024,128]{1,0:T(8,128)S(1)} %copy-done.105, f32[1024,128]{1,0:T(8,128)S(1)} %copy-done.107, bf16[512,1024]{1,0:T(8,128)(2,1)} %get-tuple-element.141.refs_2_.refs_3_.refs_5_, bf16[512,1024]{1,0:T(8,128)(2,1)S(1)} %copy-done.44, ...), custom_call_target="tpu_custom_call" | custom-call | flops 11274289152 | bytes 6815744 | tf_op jit(solution)/shard_map/attend_back/pallas_call | solution.py:708
  481.4 6.8 %attn_grads.3 = (f32[512,512]{1,0:T(8,128)S(1)}, bf16[512,512]{1,0:T(8,128)(2,1)}, f32[512,512]{1,0:T(8,128)S(1)}, bf16[512,512]{1,0:T(8,128)(2,1)}) custom-call(s32[1]{0:T(128)} %bitcast.12.refs_0_, bf16[512,1024]{1,0:T(8,128)(2,1)} %copy-done.9, bf16[512,1024]{1,0:T(8,128)(2,1)} %collective-permute-done.6.refs_4_.refs_2_, bf16[1024,768]{1,0:T(8,128)(2,1)} %copy-done.21, ...), custom_call_target="tpu_custom_call" | custom-call | tf_op jit(solution)/shard_map/attn_grads/pallas_call | solution.py:897
  489.2 14.9 %collective-permute-done.43.refs_1_ = bf16[512,512]{1,0:T(8,128)(2,1)S(1)} collective-permute-done((bf16[512,512]{1,0:T(8,128)(2,1)S(1)}, bf16[512,512]{1,0:T(8,128)(2,1)S(1)}, u32[]{:S(2)}, u32[]{:S(2)}) %collective-permute-start.43) | collective-permute-done | bytes 524320 | tf_op jit(solution)/shard_map/ppermute | solution.py:798
  507.1 6.1 attn_back.3
  518.5 10.7 %collective-permute-done.49.refs_5_.refs_1_ = bf16[512,512]{1,0:T(8,128)(2,1)S(1)} collective-permute-done((bf16[512,512]{1,0:T(8,128)(2,1)S(1)}, bf16[512,512]{1,0:T(8,128)(2,1)S(1)}, u32[]{:S(2)}, u32[]{:S(2)}) %collective-permute-start.49) | collective-permute-done | bytes 524320 | tf_op jit(solution)/shard_map/ppermute | solution.py:798
  531.0 2.3 collective-permute-start.51
  541.9 3.4 out_of_layer.3
  554.1 13.6 %all_to_all.20 = f32[16,1,256]{2,1,0:T(1,128)S(1)} all-to-all(f32[16,1,256]{2,1,0:T(1,128)S(1)} %reshape.144), channel_id=1, replica_groups=mesh['section'=2,'dp'=4,'tensor'=4] {'dp','tensor'}, dimensions={0} | all-to-all | bytes 32768 | tf_op jit(solution)/shard_map/all_to_all | solution.py:1336
  567.7 4.7 all-to-all-start.2
  580.8 27.2 %collective-permute-done.54.refs_2_.refs_3_ = bf16[512,512]{1,0:T(8,128)(2,1)S(1)} collective-permute-done((bf16[512,512]{1,0:T(8,128)(2,1)S(1)}, bf16[512,512]{1,0:T(8,128)(2,1)S(1)}, u32[]{:S(2)}, u32[]{:S(2)}) %collective-permute-start.54) | collective-permute-done | bytes 524320 | tf_op jit(solution)/shard_map/ppermute | solution.py:803
  619.9 2.3 copy.40
  (447 shorter events, 152.3 us)
Async XLA Ops:
  7.2 2.3 collective-permute-start
  11.6 58.3 %all-to-all-start = ((bf16[4,128,1024]{2,1,0:T(8,128)(2,1)}), bf16[4,128,1024]{2,1,0:T(8,128)(2,1)S(1)}, u32[]{:S(2)}, u32[]{:S(2)}) async-start(bf16[4,128,1024]{2,1,0:T(8,128)(2,1)} %pad_maximum_fusion), calls=%async_computation | async-start | bytes 2097152 | tf_op jit(solution)/shard_map/all_to_all | solution.py:1071
  23.5 26.3 %collective-permute-start.1 = (bf16[512,512]{1,0:T(8,128)(2,1)}, bf16[512,512]{1,0:T(8,128)(2,1)}, u32[]{:S(2)}, u32[]{:S(2)}) collective-permute-start(bf16[512,512]{1,0:T(8,128)(2,1)} %pad_maximum_fusion.3.refs_5_.refs_1_.refs_2_), channel_id=1, source_target_pairs={{0,1},{1,2},{2,3},{3,0},{4,5},{5,6},{6,7},{7,4},{8,9},{9,10},{10,1... | collective-permute-start | bytes 1572872 | tf_op jit(solution)/shard_map/ppermute | solution.py:803
  24.7 25.1 %collective-permute-start.2 = (bf16[512,512]{1,0:T(8,128)(2,1)}, bf16[512,512]{1,0:T(8,128)(2,1)}, u32[]{:S(2)}, u32[]{:S(2)}) collective-permute-start(bf16[512,512]{1,0:T(8,128)(2,1)} %pad_maximum_fusion.3.refs_5_.refs_1_.refs_2_), channel_id=1, source_target_pairs={{0,8},{4,12},{8,0},{12,4},{1,9},{5,13},{9,1},{13,5},{2,10},{6,14},... | collective-permute-start | bytes 1572872 | tf_op jit(solution)/shard_map/ppermute | solution.py:798
  26.0 23.9 %collective-permute-start.3 = (bf16[512,512]{1,0:T(8,128)(2,1)S(1)}, bf16[512,512]{1,0:T(8,128)(2,1)S(1)}, u32[]{:S(2)}, u32[]{:S(2)}) collective-permute-start(bf16[512,512]{1,0:T(8,128)(2,1)S(1)} %dynamic-slice_bitcast_fusion.1.refs_0_), channel_id=1, source_target_pairs={{0,8},{4,12},{8,0},{12,4},{1,9},{5,13},{9,1},{13,5},{2,10},{6,14},... | collective-permute-start | bytes 1572872 | tf_op jit(solution)/shard_map/ppermute | solution.py:798
  52.5 12.2 %collective-permute-start.4 = (bf16[512,512]{1,0:T(8,128)(2,1)}, bf16[512,512]{1,0:T(8,128)(2,1)S(1)}, u32[]{:S(2)}, u32[]{:S(2)}) collective-permute-start(bf16[512,512]{1,0:T(8,128)(2,1)} %gate.3.refs_6_.refs_2_.refs_3_), channel_id=1, source_target_pairs={{0,1},{1,2},{2,3},{3,0},{4,5},{5,6},{6,7},{7,4},{8,9},{9,10},{10,1... | collective-permute-start | bytes 1572872 | tf_op jit(solution)/shard_map/ppermute | solution.py:803
  55.8 11.7 %collective-permute-start.5 = (bf16[512,512]{1,0:T(8,128)(2,1)S(1)}, bf16[512,512]{1,0:T(8,128)(2,1)S(1)}, u32[]{:S(2)}, u32[]{:S(2)}) collective-permute-start(bf16[512,512]{1,0:T(8,128)(2,1)S(1)} %dynamic-slice_bitcast_fusion.refs_1_), channel_id=1, source_target_pairs={{0,8},{4,12},{8,0},{12,4},{1,9},{5,13},{9,1},{13,5},{2,10},{6,14},... | collective-permute-start | bytes 1572872 | tf_op jit(solution)/shard_map/ppermute | solution.py:798
  57.1 21.7 %collective-permute-start.8 = (bf16[512,512]{1,0:T(8,128)(2,1)}, bf16[512,512]{1,0:T(8,128)(2,1)}, u32[]{:S(2)}, u32[]{:S(2)}) collective-permute-start(bf16[512,512]{1,0:T(8,128)(2,1)} %gate.3.refs_6_.refs_2_.refs_3_), channel_id=1, source_target_pairs={{0,8},{4,12},{8,0},{12,4},{1,9},{5,13},{9,1},{13,5},{2,10},{6,14},... | collective-permute-start | bytes 1572872 | tf_op jit(solution)/shard_map/ppermute | solution.py:798
  64.7 15.3 %collective-permute-start.7 = (bf16[512,512]{1,0:T(8,128)(2,1)S(1)}, bf16[512,512]{1,0:T(8,128)(2,1)}, u32[]{:S(2)}, u32[]{:S(2)}) collective-permute-start(bf16[512,512]{1,0:T(8,128)(2,1)S(1)} %collective-permute-done.4.refs_2_.refs_7_.refs_3_.refs_5_.refs_4_), channel_id=1, source_target_pairs={{0,1},{1,2},{2,3},{3,0},{4,5},{5,6},{6,7},{7,4},{8,9},{9,10},{10,1... | collective-permute-start | bytes 1572872 | tf_op jit(solution)/shard_map/ppermute | solution.py:803
  71.7 31.9 %collective-permute-start.6 = (bf16[512,1024]{1,0:T(8,128)(2,1)S(1)}, bf16[512,1024]{1,0:T(8,128)(2,1)}, u32[]{:S(2)}, u32[]{:S(2)}) collective-permute-start(bf16[512,1024]{1,0:T(8,128)(2,1)S(1)} %norm_in.2.refs_3_.refs_1_), channel_id=1, source_target_pairs={{0,4},{4,0},{8,12},{12,8},{1,5},{5,1},{9,13},{13,9},{2,6},{6,2},{1... | collective-permute-start | bytes 3145736 | tf_op jit(solution)/shard_map/ppermute | solution.py:798
  76.8 13.8 %collective-permute-start.11 = (bf16[512,512]{1,0:T(8,128)(2,1)}, bf16[512,512]{1,0:T(8,128)(2,1)S(1)}, u32[]{:S(2)}, u32[]{:S(2)}) collective-permute-start(bf16[512,512]{1,0:T(8,128)(2,1)} %copy-done.108), channel_id=1, source_target_pairs={{0,1},{1,2},{2,3},{3,0},{4,5},{5,6},{6,7},{7,4},{8,9},{9,10},{10,1... | collective-permute-start | bytes 1572872 | tf_op jit(solution)/shard_map/ppermute | solution.py:803
  76.9 25.0 %collective-permute-start.12 = (bf16[512,512]{1,0:T(8,128)(2,1)}, bf16[512,512]{1,0:T(8,128)(2,1)S(1)}, u32[]{:S(2)}, u32[]{:S(2)}) collective-permute-start(bf16[512,512]{1,0:T(8,128)(2,1)} %copy-done.57), channel_id=1, source_target_pairs={{0,1},{1,2},{2,3},{3,0},{4,5},{5,6},{6,7},{7,4},{8,9},{9,10},{10,1... | collective-permute-start | bytes 1572872 | tf_op jit(solution)/shard_map/ppermute | solution.py:803
  78.8 12.3 %collective-permute-start.9 = (bf16[512,512]{1,0:T(8,128)(2,1)S(1)}, bf16[512,512]{1,0:T(8,128)(2,1)S(1)}, u32[]{:S(2)}, u32[]{:S(2)}) collective-permute-start(bf16[512,512]{1,0:T(8,128)(2,1)S(1)} %copy-done.24), channel_id=1, source_target_pairs={{0,8},{4,12},{8,0},{12,4},{1,9},{5,13},{9,1},{13,5},{2,10},{6,14},... | collective-permute-start | bytes 1572872 | tf_op jit(solution)/shard_map/ppermute | solution.py:798
  80.0 22.3 %collective-permute-start.10 = (bf16[512,512]{1,0:T(8,128)(2,1)}, bf16[512,512]{1,0:T(8,128)(2,1)S(1)}, u32[]{:S(2)}, u32[]{:S(2)}) collective-permute-start(bf16[512,512]{1,0:T(8,128)(2,1)} %collective-permute-done.7.refs_8_.refs_4_.refs_6_.refs_5_), channel_id=1, source_target_pairs={{0,8},{4,12},{8,0},{12,4},{1,9},{5,13},{9,1},{13,5},{2,10},{6,14},... | collective-permute-start | bytes 1572872 | tf_op jit(solution)/shard_map/ppermute | solution.py:798
  90.7 32.8 %collective-permute-start.13 = (bf16[512,512]{1,0:T(8,128)(2,1)S(1)}, bf16[512,512]{1,0:T(8,128)(2,1)S(1)}, u32[]{:S(2)}, u32[]{:S(2)}) collective-permute-start(bf16[512,512]{1,0:T(8,128)(2,1)S(1)} %collective-permute-done.11.refs_13_.refs_3_.refs_2_), channel_id=1, source_target_pairs={{0,1},{1,2},{2,3},{3,0},{4,5},{5,6},{6,7},{7,4},{8,9},{9,10},{10,1... | collective-permute-start | bytes 1572872 | tf_op jit(solution)/shard_map/ppermute | solution.py:803
  91.1 240.6 %copy-start.53 = (bf16[512,512]{1,0:T(8,128)(2,1)}, bf16[512,512]{1,0:T(8,128)(2,1)S(1)}, u32[]{:S(2)}) copy-start(bf16[512,512]{1,0:T(8,128)(2,1)S(1)} %collective-permute-done.9.refs_11_.refs_7_.refs_8_) | copy-start | bytes 1572868
  91.1 33.3 %collective-permute-start.15 = (bf16[512,512]{1,0:T(8,128)(2,1)S(1)}, bf16[512,512]{1,0:T(8,128)(2,1)S(1)}, u32[]{:S(2)}, u32[]{:S(2)}) collective-permute-start(bf16[512,512]{1,0:T(8,128)(2,1)S(1)} %collective-permute-done.11.refs_13_.refs_3_.refs_2_), channel_id=1, source_target_pairs={{0,8},{4,12},{8,0},{12,4},{1,9},{5,13},{9,1},{13,5},{2,10},{6,14},... | collective-permute-start | bytes 1572872 | tf_op jit(solution)/shard_map/ppermute | solution.py:798
  101.9 22.5 %collective-permute-start.14 = (bf16[512,512]{1,0:T(8,128)(2,1)S(1)}, bf16[512,512]{1,0:T(8,128)(2,1)S(1)}, u32[]{:S(2)}, u32[]{:S(2)}) collective-permute-start(bf16[512,512]{1,0:T(8,128)(2,1)S(1)} %collective-permute-done.12.refs_14_.refs_2_.refs_4_), channel_id=1, source_target_pairs={{0,1},{1,2},{2,3},{3,0},{4,5},{5,6},{6,7},{7,4},{8,9},{9,10},{10,1... | collective-permute-start | bytes 1572872 | tf_op jit(solution)/shard_map/ppermute | solution.py:803
  102.4 229.4 %copy-start.55 = (bf16[512,512]{1,0:T(8,128)(2,1)}, bf16[512,512]{1,0:T(8,128)(2,1)S(1)}, u32[]{:S(2)}) copy-start(bf16[512,512]{1,0:T(8,128)(2,1)S(1)} %collective-permute-done.10.refs_12_.refs_8_.refs_9_) | copy-start | bytes 1572868
  102.4 22.0 %collective-permute-start.16 = (bf16[512,512]{1,0:T(8,128)(2,1)S(1)}, bf16[512,512]{1,0:T(8,128)(2,1)S(1)}, u32[]{:S(2)}, u32[]{:S(2)}) collective-permute-start(bf16[512,512]{1,0:T(8,128)(2,1)S(1)} %collective-permute-done.12.refs_14_.refs_2_.refs_4_), channel_id=1, source_target_pairs={{0,8},{4,12},{8,0},{12,4},{1,9},{5,13},{9,1},{13,5},{2,10},{6,14},... | collective-permute-start | bytes 1572872 | tf_op jit(solution)/shard_map/ppermute | solution.py:798
  128.6 29.8 %collective-permute-start.17 = (bf16[512,1024]{1,0:T(8,128)(2,1)S(1)}, bf16[512,1024]{1,0:T(8,128)(2,1)S(1)}, u32[]{:S(2)}, u32[]{:S(2)}) collective-permute-start(bf16[512,1024]{1,0:T(8,128)(2,1)S(1)} %get-tuple-element.101), channel_id=1, source_target_pairs={{0,4},{4,0},{8,12},{12,8},{1,5},{5,1},{9,13},{13,9},{2,6},{6,2},{1... | collective-permute-start | bytes 3145736 | tf_op jit(solution)/shard_map/ppermute | solution.py:798
  133.4 13.7 %collective-permute-start.18 = (bf16[512,512]{1,0:T(8,128)(2,1)}, bf16[512,512]{1,0:T(8,128)(2,1)S(1)}, u32[]{:S(2)}, u32[]{:S(2)}) collective-permute-start(bf16[512,512]{1,0:T(8,128)(2,1)} %copy-done.98), channel_id=1, source_target_pairs={{0,1},{1,2},{2,3},{3,0},{4,5},{5,6},{6,7},{7,4},{8,9},{9,10},{10,1... | collective-permute-start | bytes 1572872 | tf_op jit(solution)/shard_map/ppermute | solution.py:803
  133.4 24.9 %collective-permute-start.19 = (bf16[512,512]{1,0:T(8,128)(2,1)}, bf16[512,512]{1,0:T(8,128)(2,1)S(1)}, u32[]{:S(2)}, u32[]{:S(2)}) collective-permute-start(bf16[512,512]{1,0:T(8,128)(2,1)} %copy-done.27), channel_id=1, source_target_pairs={{0,1},{1,2},{2,3},{3,0},{4,5},{5,6},{6,7},{7,4},{8,9},{9,10},{10,1... | collective-permute-start | bytes 1572872 | tf_op jit(solution)/shard_map/ppermute | solution.py:803
  133.6 24.7 %collective-permute-start.20 = (bf16[512,512]{1,0:T(8,128)(2,1)}, bf16[512,512]{1,0:T(8,128)(2,1)S(1)}, u32[]{:S(2)}, u32[]{:S(2)}) collective-permute-start(bf16[512,512]{1,0:T(8,128)(2,1)} %copy-done.98), channel_id=1, source_target_pairs={{0,8},{4,12},{8,0},{12,4},{1,9},{5,13},{9,1},{13,5},{2,10},{6,14},... | collective-permute-start | bytes 1572872 | tf_op jit(solution)/shard_map/ppermute | solution.py:798
  134.1 24.3 %collective-permute-start.21 = (bf16[512,512]{1,0:T(8,128)(2,1)}, bf16[512,512]{1,0:T(8,128)(2,1)S(1)}, u32[]{:S(2)}, u32[]{:S(2)}) collective-permute-start(bf16[512,512]{1,0:T(8,128)(2,1)} %copy-done.27), channel_id=1, source_target_pairs={{0,8},{4,12},{8,0},{12,4},{1,9},{5,13},{9,1},{13,5},{2,10},{6,14},... | collective-permute-start | bytes 1572872 | tf_op jit(solution)/shard_map/ppermute | solution.py:798
  164.5 14.6 %collective-permute-start.22 = (bf16[512,1024]{1,0:T(8,128)(2,1)S(1)}, bf16[512,1024]{1,0:T(8,128)(2,1)S(1)}, u32[]{:S(2)}, u32[]{:S(2)}) collective-permute-start(bf16[512,1024]{1,0:T(8,128)(2,1)S(1)} %get-tuple-element.103.refs_0_.refs_1_), channel_id=1, source_target_pairs={{0,4},{4,0},{8,12},{12,8},{1,5},{5,1},{9,13},{13,9},{2,6},{6,2},{1... | collective-permute-start | bytes 3145736 | tf_op jit(solution)/shard_map/ppermute | solution.py:798
  165.4 13.7 %collective-permute-start.23 = (bf16[512,512]{1,0:T(8,128)(2,1)}, bf16[512,512]{1,0:T(8,128)(2,1)S(1)}, u32[]{:S(2)}, u32[]{:S(2)}) collective-permute-start(bf16[512,512]{1,0:T(8,128)(2,1)} %copy-done.111), channel_id=1, source_target_pairs={{0,8},{4,12},{8,0},{12,4},{1,9},{5,13},{9,1},{13,5},{2,10},{6,14},... | collective-permute-start | bytes 1572872 | tf_op jit(solution)/shard_map/ppermute | solution.py:798
  165.6 25.5 %collective-permute-start.24 = (bf16[512,512]{1,0:T(8,128)(2,1)}, bf16[512,512]{1,0:T(8,128)(2,1)S(1)}, u32[]{:S(2)}, u32[]{:S(2)}) collective-permute-start(bf16[512,512]{1,0:T(8,128)(2,1)} %copy-done.31), channel_id=1, source_target_pairs={{0,8},{4,12},{8,0},{12,4},{1,9},{5,13},{9,1},{13,5},{2,10},{6,14},... | collective-permute-start | bytes 1572872 | tf_op jit(solution)/shard_map/ppermute | solution.py:798
  195.7 3.7 collective-permute-start.25
  201.2 25.0 %collective-permute-start.26 = (bf16[512,1024]{1,0:T(8,128)(2,1)S(1)}, bf16[512,1024]{1,0:T(8,128)(2,1)S(1)}, u32[]{:S(2)}, u32[]{:S(2)}) collective-permute-start(bf16[512,1024]{1,0:T(8,128)(2,1)S(1)} %get-tuple-element.132), channel_id=1, source_target_pairs={{0,16},{1,17},{2,18},{3,19},{4,20},{5,21},{6,22},{7,23},{8,24},{9,... | collective-permute-start | bytes 3145736 | tf_op jit(solution)/shard_map/ppermute | solution.py:28
  228.0 3.6 collective-permute-start.27
  251.8 2.7 collective-permute-start.28
  258.0 2.7 collective-permute-start.29
  275.0 2.7 collective-permute-start.30
  281.9 2.7 collective-permute-start.31
  296.4 2.7 collective-permute-start.32
  303.1 2.7 collective-permute-start.33
  339.1 2.7 collective-permute-start.34
  344.0 26.6 %collective-permute-start.35 = (bf16[512,1024]{1,0:T(8,128)(2,1)S(1)}, bf16[512,1024]{1,0:T(8,128)(2,1)S(1)}, u32[]{:S(2)}, u32[]{:S(2)}) collective-permute-start(bf16[512,1024]{1,0:T(8,128)(2,1)S(1)} %get-tuple-element.131.refs_2_), channel_id=1, source_target_pairs={{16,0},{17,1},{18,2},{19,3},{20,4},{21,5},{22,6},{23,7},{24,8},{25... | collective-permute-start | bytes 3145736 | tf_op jit(solution)/shard_map/ppermute | solution.py:28
  346.9 28.9 %all-to-all-start.1 = ((bf16[4,128,1024]{2,1,0:T(8,128)(2,1)}), bf16[4,128,1024]{2,1,0:T(8,128)(2,1)}, u32[]{:S(2)}, u32[]{:S(2)}) async-start(bf16[4,128,1024]{2,1,0:T(8,128)(2,1)} %bitcast.43), calls=%async_computation.1 | async-start | bytes 2097152 | tf_op jit(solution)/shard_map/all_to_all | solution.py:1224
  374.8 3.3 collective-permute-start.36
  400.5 2.7 collective-permute-start.37
  400.9 24.6 %collective-permute-start.41 = (bf16[1024,512]{1,0:T(8,128)(2,1)S(1)}, bf16[1024,512]{1,0:T(8,128)(2,1)S(1)}, u32[]{:S(2)}, u32[]{:S(2)}) collective-permute-start(bf16[1024,512]{1,0:T(8,128)(2,1)S(1)} %get-tuple-element.149), channel_id=1, source_target_pairs={{0,8},{4,12},{8,0},{12,4},{1,9},{5,13},{9,1},{13,5},{2,10},{6,14},... | collective-permute-start | bytes 3145736 | tf_op jit(solution)/shard_map/ppermute | solution.py:798
  408.1 31.1 %collective-permute-start.39 = (bf16[512,1024]{1,0:T(8,128)(2,1)}, bf16[512,1024]{1,0:T(8,128)(2,1)S(1)}, u32[]{:S(2)}, u32[]{:S(2)}) collective-permute-start(bf16[512,1024]{1,0:T(8,128)(2,1)} %get-tuple-element.141.refs_2_.refs_3_.refs_5_), channel_id=1, source_target_pairs={{0,4},{4,0},{8,12},{12,8},{1,5},{5,1},{9,13},{13,9},{2,6},{6,2},{1... | collective-permute-start | bytes 3145736 | tf_op jit(solution)/shard_map/ppermute | solution.py:798
  409.9 2.0 collective-permute-start.38
  410.1 43.3 %collective-permute-start.40 = (bf16[1024,512]{1,0:T(8,128)(2,1)S(1)}, bf16[1024,512]{1,0:T(8,128)(2,1)S(1)}, u32[]{:S(2)}, u32[]{:S(2)}) collective-permute-start(bf16[1024,512]{1,0:T(8,128)(2,1)S(1)} %get-tuple-element.148), channel_id=1, source_target_pairs={{0,8},{4,12},{8,0},{12,4},{1,9},{5,13},{9,1},{13,5},{2,10},{6,14},... | collective-permute-start | bytes 3145736 | tf_op jit(solution)/shard_map/ppermute | solution.py:798
  426.0 27.4 %collective-permute-start.42 = (bf16[1024,512]{1,0:T(8,128)(2,1)S(1)}, bf16[1024,512]{1,0:T(8,128)(2,1)S(1)}, u32[]{:S(2)}, u32[]{:S(2)}) collective-permute-start(bf16[1024,512]{1,0:T(8,128)(2,1)S(1)} %moved.6.refs_13_), channel_id=1, source_target_pairs={{0,3},{1,0},{2,1},{3,2},{4,7},{5,4},{6,5},{7,6},{8,11},{9,8},{10,9... | collective-permute-start | bytes 3145736 | tf_op jit(solution)/shard_map/ppermute | solution.py:803
  437.7 41.2 %collective-permute-start.44 = (bf16[1024,512]{1,0:T(8,128)(2,1)S(1)}, bf16[1024,512]{1,0:T(8,128)(2,1)S(1)}, u32[]{:S(2)}, u32[]{:S(2)}) collective-permute-start(bf16[1024,512]{1,0:T(8,128)(2,1)S(1)} %get-tuple-element.154), channel_id=1, source_target_pairs={{0,8},{4,12},{8,0},{12,4},{1,9},{5,13},{9,1},{13,5},{2,10},{6,14},... | collective-permute-start | bytes 3145736 | tf_op jit(solution)/shard_map/ppermute | solution.py:798
  438.0 67.2 %collective-permute-start.47 = (bf16[1024,512]{1,0:T(8,128)(2,1)S(1)}, bf16[1024,512]{1,0:T(8,128)(2,1)S(1)}, u32[]{:S(2)}, u32[]{:S(2)}) collective-permute-start(bf16[1024,512]{1,0:T(8,128)(2,1)S(1)} %get-tuple-element.156), channel_id=1, source_target_pairs={{0,8},{4,12},{8,0},{12,4},{1,9},{5,13},{9,1},{13,5},{2,10},{6,14},... | collective-permute-start | bytes 3145736 | tf_op jit(solution)/shard_map/ppermute | solution.py:798
  454.8 24.1 %collective-permute-start.45 = (bf16[1024,512]{1,0:T(8,128)(2,1)S(1)}, bf16[1024,512]{1,0:T(8,128)(2,1)S(1)}, u32[]{:S(2)}, u32[]{:S(2)}) collective-permute-start(bf16[1024,512]{1,0:T(8,128)(2,1)S(1)} %moved.7.refs_13_), channel_id=1, source_target_pairs={{0,3},{1,0},{2,1},{3,2},{4,7},{5,4},{6,5},{7,6},{8,11},{9,8},{10,9... | collective-permute-start | bytes 3145736 | tf_op jit(solution)/shard_map/ppermute | solution.py:803
  479.4 25.8 %collective-permute-start.46 = (bf16[1024,512]{1,0:T(8,128)(2,1)S(1)}, bf16[1024,512]{1,0:T(8,128)(2,1)S(1)}, u32[]{:S(2)}, u32[]{:S(2)}) collective-permute-start(bf16[1024,512]{1,0:T(8,128)(2,1)S(1)} %moved.8.refs_13_), channel_id=1, source_target_pairs={{0,3},{1,0},{2,1},{3,2},{4,7},{5,4},{6,5},{7,6},{8,11},{9,8},{10,9... | collective-permute-start | bytes 3145736 | tf_op jit(solution)/shard_map/ppermute | solution.py:803
  481.2 23.0 %collective-permute-start.43 = (bf16[512,512]{1,0:T(8,128)(2,1)S(1)}, bf16[512,512]{1,0:T(8,128)(2,1)S(1)}, u32[]{:S(2)}, u32[]{:S(2)}) collective-permute-start(bf16[512,512]{1,0:T(8,128)(2,1)S(1)} %get-tuple-element.153), channel_id=1, source_target_pairs={{0,8},{4,12},{8,0},{12,4},{1,9},{5,13},{9,1},{13,5},{2,10},{6,14},... | collective-permute-start | bytes 1572872 | tf_op jit(solution)/shard_map/ppermute | solution.py:798
  514.6 25.7 %collective-permute-start.48 = (bf16[512,1024]{1,0:T(8,128)(2,1)}, bf16[512,1024]{1,0:T(8,128)(2,1)}, u32[]{:S(2)}, u32[]{:S(2)}) collective-permute-start(bf16[512,1024]{1,0:T(8,128)(2,1)} %get-tuple-element.158), channel_id=1, source_target_pairs={{0,4},{4,0},{8,12},{12,8},{1,5},{5,1},{9,13},{13,9},{2,6},{6,2},{1... | collective-permute-start | bytes 3145736 | tf_op jit(solution)/shard_map/ppermute | solution.py:798
  515.6 13.6 %collective-permute-start.49 = (bf16[512,512]{1,0:T(8,128)(2,1)S(1)}, bf16[512,512]{1,0:T(8,128)(2,1)S(1)}, u32[]{:S(2)}, u32[]{:S(2)}) collective-permute-start(bf16[512,512]{1,0:T(8,128)(2,1)S(1)} %get-tuple-element.160), channel_id=1, source_target_pairs={{0,8},{4,12},{8,0},{12,4},{1,9},{5,13},{9,1},{13,5},{2,10},{6,14},... | collective-permute-start | bytes 1572872 | tf_op jit(solution)/shard_map/ppermute | solution.py:798
  515.9 13.3 %collective-permute-start.50 = (bf16[512,512]{1,0:T(8,128)(2,1)S(1)}, bf16[512,512]{1,0:T(8,128)(2,1)S(1)}, u32[]{:S(2)}, u32[]{:S(2)}) collective-permute-start(bf16[512,512]{1,0:T(8,128)(2,1)S(1)} %copy-done.124), channel_id=1, source_target_pairs={{0,3},{1,0},{2,1},{3,2},{4,7},{5,4},{6,5},{7,6},{8,11},{9,8},{10,9... | collective-permute-start | bytes 1572872 | tf_op jit(solution)/shard_map/ppermute | solution.py:803
  517.2 30.0 %collective-permute-start.52 = (bf16[512,512]{1,0:T(8,128)(2,1)}, bf16[512,512]{1,0:T(8,128)(2,1)}, u32[]{:S(2)}, u32[]{:S(2)}) collective-permute-start(bf16[512,512]{1,0:T(8,128)(2,1)} %get-tuple-element.163), channel_id=1, source_target_pairs={{0,8},{4,12},{8,0},{12,4},{1,9},{5,13},{9,1},{13,5},{2,10},{6,14},... | collective-permute-start | bytes 1572872 | tf_op jit(solution)/shard_map/ppermute | solution.py:798
  531.0 16.3 %collective-permute-start.51 = (bf16[512,512]{1,0:T(8,128)(2,1)}, bf16[512,512]{1,0:T(8,128)(2,1)}, u32[]{:S(2)}, u32[]{:S(2)}) collective-permute-start(bf16[512,512]{1,0:T(8,128)(2,1)} %moved.10), channel_id=1, source_target_pairs={{0,3},{1,0},{2,1},{3,2},{4,7},{5,4},{6,5},{7,6},{8,11},{9,8},{10,9... | collective-permute-start | bytes 1572872 | tf_op jit(solution)/shard_map/ppermute | solution.py:803
  533.3 18.5 %collective-permute-start.53 = (bf16[512,512]{1,0:T(8,128)(2,1)}, bf16[512,512]{1,0:T(8,128)(2,1)}, u32[]{:S(2)}, u32[]{:S(2)}) collective-permute-start(bf16[512,512]{1,0:T(8,128)(2,1)} %get-tuple-element.164), channel_id=1, source_target_pairs={{0,8},{4,12},{8,0},{12,4},{1,9},{5,13},{9,1},{13,5},{2,10},{6,14},... | collective-permute-start | bytes 1572872 | tf_op jit(solution)/shard_map/ppermute | solution.py:798
  567.7 40.3 %all-to-all-start.2 = ((bf16[4,128,1024]{2,1,0:T(8,128)(2,1)}), bf16[4,128,1024]{2,1,0:T(8,128)(2,1)S(1)}, u32[]{:S(2)}, u32[]{:S(2)}) async-start(bf16[4,128,1024]{2,1,0:T(8,128)(2,1)} %bitcast.16), calls=%async_computation.2 | async-start | bytes 2097152 | tf_op jit(solution)/shard_map/all_to_all | solution.py:1306
  572.4 35.6 %collective-permute-start.54 = (bf16[512,512]{1,0:T(8,128)(2,1)S(1)}, bf16[512,512]{1,0:T(8,128)(2,1)S(1)}, u32[]{:S(2)}, u32[]{:S(2)}) collective-permute-start(bf16[512,512]{1,0:T(8,128)(2,1)S(1)} %copy-done.81), channel_id=1, source_target_pairs={{0,3},{1,0},{2,1},{3,2},{4,7},{5,4},{6,5},{7,6},{8,11},{9,8},{10,9... | collective-permute-start | bytes 1572872 | tf_op jit(solution)/shard_map/ppermute | solution.py:803
  578.2 31.9 %collective-permute-start.56 = (f32[256,512]{1,0:T(8,128)}, f32[256,512]{1,0:T(8,128)S(1)}, u32[]{:S(2)}, u32[]{:S(2)}) collective-permute-start(f32[256,512]{1,0:T(8,128)} %get-tuple-element.179), channel_id=1, source_target_pairs={{0,4},{4,0},{8,12},{12,8},{1,5},{5,1},{9,13},{13,9},{2,6},{6,2},{1... | collective-permute-start | bytes 1572872 | tf_op jit(solution)/shard_map/ppermute | solution.py:798
  578.9 31.2 %collective-permute-start.57 = (f32[512,256]{1,0:T(8,128)}, f32[512,256]{1,0:T(8,128)S(1)}, u32[]{:S(2)}, u32[]{:S(2)}) collective-permute-start(f32[512,256]{1,0:T(8,128)} %get-tuple-element.180), channel_id=1, source_target_pairs={{0,4},{4,0},{8,12},{12,8},{1,5},{5,1},{9,13},{13,9},{2,6},{6,2},{1... | collective-permute-start | bytes 1572872 | tf_op jit(solution)/shard_map/ppermute | solution.py:798
  608.8 4.8 collective-permute-start.55
  615.9 2.0 collective-permute-start.58
  (136 other events, 1356.1 us)

commit v17 on v14

--- a/solution.py
+++ b/solution.py
@@ -542,6 +542,18 @@
         )
 
 
+def mlp_up_back_near_kernel(pieces, own_rows, other_rows, slope_ref, *refs):
+    owns, others = refs[:pieces], refs[pieces : 2 * pieces]
+    out_ref = refs[-1]
+    size = owns[0].shape[0]
+    rows = stacked_up([own_rows[...], other_rows[...]])
+    for j in range(pieces):
+        cols = slice(j * size, (j + 1) * size)
+        weight = jnp.concatenate([owns[j][...], others[j][...]], axis=1)
+        d_gelu = dot_nt(rows, weight)
+        out_ref[:, cols] = (d_gelu * slope_ref[:, cols].astype(jnp.float32)).astype(jnp.bfloat16)
+
+
 def mlp_up_back_kernel(pieces, own_rows, other_rows, slope_ref, *refs):
     owns, others = refs[:pieces], refs[pieces : 2 * pieces]
     out_ref, weight, slope, sems = refs[2 * pieces :]
@@ -1181,7 +1193,12 @@
             into_mlp_back_kernel, "into_mlp_back", (row16, sum32), *operands
         )
         d_down = both_rows(d_down)
-        d_up = mlp_up_back(d_down, slope, w_down, late)
+        if late:
+            d_up = mlp_up_back(d_down, slope, w_down, late)
+        else:
+            kernel = functools.partial(mlp_up_back_near_kernel, tensor)
+            operands = (*d_down, slope, *w_down[0], *w_down[1])
+            (d_up,) = on_chip(kernel, "mlp_up_back", (unit16,), *operands, **mlp_cost)
         waits = hook(d_down, d_up)
         parts = model_rows(model_kernel(every), "mlp_back", [d_up], w_up, waits)
         waits = hook()
@@ -1210,9 +1227,9 @@
         start,
         (
             (up_piece, up_other[0], down_other[0]),
-            (up_own[1], down_own[1]),
             (up_own[2], down_own[2], up_other[1], down_other[1]),
             (up_own[3], down_own[3], up_other[2], down_other[2]),
+            (up_other[3],),
         ),
     )
     low_one, saved_one, lefts_one = forward(shifted(low_zero, "section", 1), ((),) * 4)

time: 627 us -> 632 us (level)
  waiting for transfers between devices: 226 us -> 204 us
  starting transfers between devices: 80.3 us -> 100 us
  Pallas kernels: 221 us -> 232 us
    ppermute x42, starting transfers between devices: 23.5 us -> 44.7 us  [flip_pairs(): return lax.ppermute(block, 'dp', [(i, i ^ distance) for i in range(size)])]
    pallas_call x31 -> x32, Pallas kernels: 86.2 us -> 105 us  [on_chip(): pl.pallas_call(without(kernel, len(operands), len(waits)), in_specs=[spac...]
    ppermute x15, waiting for transfers between devices: 80.3 us -> 62.6 us  [passed_on(): lax.ppermute(block, 'tensor', [(i, (i + step) % size) for i in range(size)])]
    pallas_call x2 -> x1, Pallas kernels: 14.3 us -> 7.17 us  [mlp_up_back(): pl.pallas_call(without(functools.partial(mlp_up_back_kernel, count), 3 +...]
    unnamed x290 -> x274, local copies, waits for them, and re-layouts: 47.9 us -> 43.7 us
  transfers between devices with their start and end apart: 62 -> 62, of which waited for: 36 -> 32; matrix products, arithmetic and copies ran while one was open for 4% -> 3% of each run, Pallas kernels for 14% -> 15%
where the time goes in v17:
time: 632 us; the launch traced here: 622 us
  Pallas kernels  232 us (37%)
  waiting for transfers between devices  204 us (32%)
  starting transfers between devices  100 us (16%)
  local copies, waits for them, and re-layouts  53.8 us (9%)
  other arithmetic  18.8 us (3%)
  blocking collectives  9.97 us (2%)
    pallas_call x32, Pallas kernels, on_chip(): pl.pallas_call(without(kernel, len(operands), len(waits)), in_specs=[spac...  105 us
    ppermute x42, waiting for transfers between devices, flip_pairs(): return lax.ppermute(block, 'dp', [(i, i ^ distance) for i in range(size)])  97.1 us
    pallas_call x6, Pallas kernels, by_pairs(): pl.pallas_call(without(functools.partial(kernel, len(pieces[0])), taken,...  84.9 us
    ppermute x15, waiting for transfers between devices, passed_on(): lax.ppermute(block, 'tensor', [(i, (i + step) % size) for i in range(size)])  62.6 us
    ppermute x42, starting transfers between devices, flip_pairs(): return lax.ppermute(block, 'dp', [(i, i ^ distance) for i in range(size)])  44.7 us
    unnamed x274, local copies, waits for them, and re-layouts  43.7 us
    ppermute x2, waiting for transfers between devices, shifted(): return lax.ppermute(block, axis, route)  42.1 us
    ppermute x15, starting transfers between devices, passed_on(): lax.ppermute(block, 'tensor', [(i, (i + step) % size) for i in range(size)])  36.8 us
  transfers between devices with their start and end apart: 62, of which 32 were waited for; matrix products, arithmetic and copies ran while one was open for 3% of the time, Pallas kernels for 15%

profile of v17, /device:TPU:0, one launch (start us, length us, event | category | flops | bytes accessed | tf_op | source)
XLA Modules:
  0.0 622.0 jit_solution(11238756810748277419)
XLA Ops:
  4.6 2.5 maximum_select_fusion
  12.0 2.6 collective-permute-start.1
  19.8 3.9 all-to-all-start
  23.7 6.0 collective-permute-done.1.refs_0_
  29.7 10.2 %collective-permute-done.3.refs_2_.refs_3_.refs_6_.refs_5_ = bf16[512,512]{1,0:T(8,128)(2,1)S(1)} collective-permute-done((bf16[512,512]{1,0:T(8,128)(2,1)}, bf16[512,512]{1,0:T(8,128)(2,1)S(1)}, u32[]{:S(2)}, u32[]{:S(2)}) %collective-permute-start.3) | collective-permute-done | bytes 524320 | tf_op jit(solution)/shard_map/ppermute | solution.py:810
  46.1 11.4 %collective-permute-done.4.refs_2_.refs_7_.refs_3_.refs_5_.refs_4_ = bf16[512,512]{1,0:T(8,128)(2,1)S(1)} collective-permute-done((bf16[512,512]{1,0:T(8,128)(2,1)S(1)}, bf16[512,512]{1,0:T(8,128)(2,1)S(1)}, u32[]{:S(2)}, u32[]{:S(2)}) %collective-permute-start.4) | collective-permute-done | bytes 524320 | tf_op jit(solution)/shard_map/ppermute | solution.py:815
  57.5 4.3 collective-permute-start.7
  69.6 6.6 %collective-permute-done.7.refs_8_.refs_4_.refs_6_.refs_5_ = bf16[512,512]{1,0:T(8,128)(2,1)} collective-permute-done((bf16[512,512]{1,0:T(8,128)(2,1)S(1)}, bf16[512,512]{1,0:T(8,128)(2,1)}, u32[]{:S(2)}, u32[]{:S(2)}) %collective-permute-start.7) | collective-permute-done | bytes 524320 | tf_op jit(solution)/shard_map/ppermute | solution.py:815
  79.5 7.9 %collective-permute-done.11.refs_3_.refs_2_ = bf16[512,512]{1,0:T(8,128)(2,1)} collective-permute-done((bf16[512,512]{1,0:T(8,128)(2,1)}, bf16[512,512]{1,0:T(8,128)(2,1)}, u32[]{:S(2)}, u32[]{:S(2)}) %collective-permute-start.11) | collective-permute-done | bytes 524320 | tf_op jit(solution)/shard_map/ppermute | solution.py:815
  88.0 12.2 %collective-permute-start.15 = (bf16[512,512]{1,0:T(8,128)(2,1)}, bf16[512,512]{1,0:T(8,128)(2,1)S(1)}, u32[]{:S(2)}, u32[]{:S(2)}) collective-permute-start(bf16[512,512]{1,0:T(8,128)(2,1)} %collective-permute-done.11.refs_3_.refs_2_), channel_id=1, source_target_pairs={{0,8},{4,12},{8,0},{12,4},{1,9},{5,13},{9,1},{13,5},{2,10},{6,14},... | collective-permute-start | bytes 1572872 | tf_op jit(solution)/shard_map/ppermute | solution.py:810
  103.3 6.5 %collective-permute-done.12.refs_13_.refs_4_.refs_3_ = bf16[512,512]{1,0:T(8,128)(2,1)S(1)} collective-permute-done((bf16[512,512]{1,0:T(8,128)(2,1)}, bf16[512,512]{1,0:T(8,128)(2,1)S(1)}, u32[]{:S(2)}, u32[]{:S(2)}) %collective-permute-start.12) | collective-permute-done | bytes 524320 | tf_op jit(solution)/shard_map/ppermute | solution.py:815
  110.5 10.5 %collective-permute-done.14.refs_14_.refs_3_.refs_5_ = bf16[512,512]{1,0:T(8,128)(2,1)S(1)} collective-permute-done((bf16[512,512]{1,0:T(8,128)(2,1)}, bf16[512,512]{1,0:T(8,128)(2,1)S(1)}, u32[]{:S(2)}, u32[]{:S(2)}) %collective-permute-start.14) | collective-permute-done | bytes 524320 | tf_op jit(solution)/shard_map/ppermute | solution.py:815
  121.0 7.1 %collective-permute-start.19 = (bf16[512,512]{1,0:T(8,128)(2,1)S(1)}, bf16[512,512]{1,0:T(8,128)(2,1)S(1)}, u32[]{:S(2)}, u32[]{:S(2)}) collective-permute-start(bf16[512,512]{1,0:T(8,128)(2,1)S(1)} %collective-permute-done.12.refs_13_.refs_4_.refs_3_), channel_id=1, source_target_pairs={{0,8},{4,12},{8,0},{12,4},{1,9},{5,13},{9,1},{13,5},{2,10},{6,14},... | collective-permute-start | bytes 1572872 | tf_op jit(solution)/shard_map/ppermute | solution.py:810
  130.8 16.5 %attend.2 = (bf16[4,1024,128]{2,1,0:T(8,128)(2,1)S(1)}, bf16[4,1024,128]{2,1,0:T(8,128)(2,1)S(1)}, bf16[4,1024,128]{2,1,0:T(8,128)(2,1)S(1)}, f32[4,2,1024]{2,1,0:T(2,128)S(1)}, bf16[1024,512]{1,0:T(8,128)(2,1)S(1)}) custom-call(s32[1]{0:T(128)} %bitcast.refs_0_, f32[1024,128]{1,0:T(8,128)S(1)} %get-tuple-element.228.refs_1_, ...), custom_call_target="tpu_custom_call" | custom-call | flops 11811160064 | bytes 11567104 | tf_op jit(solution)/shard_map/attend/pallas_call | solution.py:720
  151.9 2.8 attn_out.2
  156.6 12.7 %collective-permute-done.22.refs_4_.refs_9_.refs_8_ = bf16[512,512]{1,0:T(8,128)(2,1)S(1)} collective-permute-done((bf16[512,512]{1,0:T(8,128)(2,1)}, bf16[512,512]{1,0:T(8,128)(2,1)S(1)}, u32[]{:S(2)}, u32[]{:S(2)}) %collective-permute-start.22) | collective-permute-done | bytes 524320 | tf_op jit(solution)/shard_map/ppermute | solution.py:810
  170.2 3.6 after_attn.2
  177.6 9.3 %mlp_up.2 = (bf16[1024,2048]{1,0:T(8,128)(2,1)S(1)}, bf16[1024,2048]{1,0:T(8,128)(2,1)S(1)}) custom-call(bf16[512,1024]{1,0:T(8,128)(2,1)S(1)} %get-tuple-element.103.refs_0_.refs_1_, bf16[512,1024]{1,0:T(8,128)(2,1)S(1)} %collective-permute-done.23.refs_1_.refs_2_, bf16[512,512]{1,0:T(8,128)(2,1)} %get-tuple-element.97.refs_2_.refs_1_, ...), custom_call_target="tpu_custom_call" | custom-call | flops 4294967296 | bytes 14680064 | tf_op jit(solution)/shard_map/mlp_up/pallas_call | solution.py:702
  189.0 6.5 %mlp_down.2 = (f32[512,1024]{1,0:T(8,128)S(1)}, bf16[512,1024]{1,0:T(8,128)(2,1)S(1)}) custom-call(bf16[1024,2048]{1,0:T(8,128)(2,1)S(1)} %get-tuple-element.104.refs_0_.refs_4_, bf16[512,512]{1,0:T(8,128)(2,1)} %get-tuple-element.98.refs_1_.refs_3_, bf16[512,512]{1,0:T(8,128)(2,1)} %collective-permute-done.13.refs_2_.refs_4_, ...), custom_call_target="tpu_custom_call" | custom-call | flops 4294967296 | bytes 11534336 | tf_op jit(solution)/shard_map/mlp_down/pallas_call | solution.py:702
  200.1 3.4 collective-permute-start.26
  203.5 22.6 %collective-permute-done.26.refs_1_ = bf16[512,1024]{1,0:T(8,128)(2,1)S(1)} collective-permute-done((bf16[512,1024]{1,0:T(8,128)(2,1)S(1)}, bf16[512,1024]{1,0:T(8,128)(2,1)S(1)}, u32[]{:S(2)}, u32[]{:S(2)}) %collective-permute-start.26) | collective-permute-done | bytes 1048608 | tf_op jit(solution)/shard_map/ppermute | solution.py:28
  228.3 2.6 collective-permute-done.27.refs_4_.refs_8_
  231.0 16.7 %attend.3 = (bf16[4,1024,128]{2,1,0:T(8,128)(2,1)S(1)}, bf16[4,1024,128]{2,1,0:T(8,128)(2,1)S(1)}, bf16[4,1024,128]{2,1,0:T(8,128)(2,1)S(1)}, f32[4,2,1024]{2,1,0:T(2,128)S(1)}, bf16[1024,512]{1,0:T(8,128)(2,1)S(1)}) custom-call(s32[1]{0:T(128)} %bitcast.refs_0_, f32[1024,128]{1,0:T(8,128)S(1)} %get-tuple-element.228.refs_1_, ...), custom_call_target="tpu_custom_call" | custom-call | flops 11811160064 | bytes 11567104 | tf_op jit(solution)/shard_map/attend/pallas_call | solution.py:720
  247.7 3.2 attn_out.3
  251.1 2.5 collective-permute-done.28.refs_3_
  253.7 3.4 after_attn.3
  257.3 2.5 collective-permute-done.29.refs_1_.refs_8_
  259.8 9.3 %mlp_up.3 = (bf16[1024,2048]{1,0:T(8,128)(2,1)S(1)}, bf16[1024,2048]{1,0:T(8,128)(2,1)S(1)}) custom-call(bf16[512,1024]{1,0:T(8,128)(2,1)S(1)} %get-tuple-element.112.refs_0_.refs_7_, bf16[512,1024]{1,0:T(8,128)(2,1)S(1)} %collective-permute-done.29.refs_1_.refs_8_, bf16[512,512]{1,0:T(8,128)(2,1)} %get-tuple-element.97.refs_2_.refs_1_, ...), custom_call_target="tpu_custom_call" | custom-call | flops 4294967296 | bytes 14680064 | tf_op jit(solution)/shard_map/mlp_up/pallas_call | solution.py:702
  269.2 6.5 %mlp_down.3 = (f32[512,1024]{1,0:T(8,128)S(1)}, bf16[512,1024]{1,0:T(8,128)(2,1)S(1)}) custom-call(bf16[1024,2048]{1,0:T(8,128)(2,1)S(1)} %get-tuple-element.113.refs_0_.refs_10_, bf16[512,512]{1,0:T(8,128)(2,1)} %get-tuple-element.98.refs_1_.refs_3_, bf16[512,512]{1,0:T(8,128)(2,1)} %collective-permute-done.13.refs_2_.refs_4_, ...), custom_call_target="tpu_custom_call" | custom-call | flops 4294967296 | bytes 11534336 | tf_op jit(solution)/shard_map/mlp_down/pallas_call | solution.py:702
  275.8 2.5 collective-permute-done.30.refs_3_
  282.7 2.5 collective-permute-done.31.refs_1_.refs_12_
  285.3 5.7 mlp_up_back.2.refs_0_.refs_9_
  292.9 6.5 %mlp_back.2 = (f32[512,1024]{1,0:T(8,128)S(1)}, bf16[512,1024]{1,0:T(8,128)(2,1)S(1)}) custom-call(bf16[1024,2048]{1,0:T(8,128)(2,1)S(1)} %mlp_up_back.2.refs_0_.refs_9_, bf16[512,512]{1,0:T(8,128)(2,1)} %get-tuple-element.97.refs_2_.refs_1_, bf16[512,512]{1,0:T(8,128)(2,1)} %collective-permute-done.11.refs_3_.refs_2_, bf16[512,512]{1,0:T(8,128)(2,1)S(1)} %copy-done.121, ...), custom_call_target="tpu_custom_call" | custom-call | flops 4294967296 | bytes 11534336 | tf_op jit(solution)/shard_map/mlp_back/pallas_call | solution.py:702
  299.6 2.5 collective-permute-done.32.refs_3_
  302.1 3.9 into_attn_back.2
  308.8 12.6 %attend_back.4.refs_0_.refs_9_ = bf16[1024,768]{1,0:T(8,128)(2,1)S(1)} custom-call(s32[1]{0:T(128)} %bitcast.refs_0_, f32[1024,128]{1,0:T(8,128)S(1)} %get-tuple-element.228.refs_1_, f32[1024,128]{1,0:T(8,128)S(1)} %get-tuple-element.229.refs_2_, bf16[512,1024]{1,0:T(8,128)(2,1)S(1)} %get-tuple-element.123.refs_3_.refs_11_, ...), custom_call_target="tpu_custom_call" | custom-call | flops 11274289152 | bytes 6815744 | tf_op jit(solution)/shard_map/attend_back/pallas_call | solution.py:720
  321.4 13.1 %attend_back.5.refs_1_.refs_9_ = bf16[1024,768]{1,0:T(8,128)(2,1)S(1)} custom-call(s32[1]{0:T(128)} %bitcast.refs_0_, f32[1024,128]{1,0:T(8,128)S(1)} %get-tuple-element.228.refs_1_, f32[1024,128]{1,0:T(8,128)S(1)} %get-tuple-element.229.refs_2_, bf16[512,1024]{1,0:T(8,128)(2,1)S(1)} %get-tuple-element.123.refs_3_.refs_11_, ...), custom_call_target="tpu_custom_call" | custom-call | flops 11274289152 | bytes 6815744 | tf_op jit(solution)/shard_map/attend_back/pallas_call | solution.py:720
  336.1 5.5 attn_back.2
  344.4 3.1 out_of_layer.2
  350.3 5.1 all-to-all-start.1
  355.5 19.5 %collective-permute-done.35.refs_1_ = bf16[512,1024]{1,0:T(8,128)(2,1)S(1)} collective-permute-done((bf16[512,1024]{1,0:T(8,128)(2,1)}, bf16[512,1024]{1,0:T(8,128)(2,1)S(1)}, u32[]{:S(2)}, u32[]{:S(2)}) %collective-permute-start.35) | collective-permute-done | bytes 1048608 | tf_op jit(solution)/shard_map/ppermute | solution.py:28
  381.8 7.2 %mlp_up_back.3.refs_3_.refs_0_ = bf16[1024,2048]{1,0:T(8,128)(2,1)S(1)} custom-call(bf16[512,1024]{1,0:T(8,128)(2,1)S(1)} %get-tuple-element.135.refs_0_.refs_5_, bf16[512,1024]{1,0:T(8,128)(2,1)S(1)} %collective-permute-done.36.refs_1_.refs_6_, bf16[1024,2048]{1,0:T(8,128)(2,1)} %copy-done.55, bf16[512,512]{1,0:T(8,128)(2,1)} %get-tuple-element.98.refs_1_.refs_3_, ...), custom_call_target="tpu_custom_call" | custom-call | tf_op jit(solution)/shard_map/mlp_up_back/pallas_call | solution.py:741
  390.9 7.2 %mlp_grads.2 = (f32[1024,512]{1,0:T(8,128)S(1)}, bf16[1024,512]{1,0:T(8,128)(2,1)S(1)}, f32[1024,512]{1,0:T(8,128)S(1)}, bf16[1024,512]{1,0:T(8,128)(2,1)S(1)}) custom-call(s32[1]{0:T(128)} %bitcast.12.refs_0_, bf16[512,1024]{1,0:T(8,128)(2,1)} %copy-done.40, bf16[512,1024]{1,0:T(8,128)(2,1)} %copy-done.41, bf16[1024,2048]{1,0:T(8,128)(2,1)} %copy-done.2, ...), custom_call_target="tpu_custom_call" | custom-call | tf_op jit(solution)/shard_map/mlp_grads/pallas_call | solution.py:909
  399.6 5.9 mlp_back.3
  408.2 4.9 into_attn_back.3
  417.8 13.9 %collective-permute-done.41.refs_1_ = bf16[1024,512]{1,0:T(8,128)(2,1)S(1)} collective-permute-done((bf16[1024,512]{1,0:T(8,128)(2,1)S(1)}, bf16[1024,512]{1,0:T(8,128)(2,1)S(1)}, u32[]{:S(2)}, u32[]{:S(2)}) %collective-permute-start.41) | collective-permute-done | bytes 1048608 | tf_op jit(solution)/shard_map/ppermute | solution.py:810
  432.1 3.7 collective-permute-start.42
  435.8 7.0 %mlp_grads.3 = (f32[1024,512]{1,0:T(8,128)S(1)}, bf16[1024,512]{1,0:T(8,128)(2,1)S(1)}, f32[1024,512]{1,0:T(8,128)S(1)}, bf16[1024,512]{1,0:T(8,128)(2,1)S(1)}) custom-call(s32[1]{0:T(128)} %bitcast.12.refs_0_, bf16[512,1024]{1,0:T(8,128)(2,1)} %copy-done.40, bf16[512,1024]{1,0:T(8,128)(2,1)} %copy-done.41, bf16[1024,2048]{1,0:T(8,128)(2,1)} %copy-done.2, ...), custom_call_target="tpu_custom_call" | custom-call | tf_op jit(solution)/shard_map/mlp_grads/pallas_call | solution.py:909
  447.6 13.2 %attend_back.6.refs_3_.refs_1_ = bf16[1024,768]{1,0:T(8,128)(2,1)S(1)} custom-call(s32[1]{0:T(128)} %bitcast.refs_0_, f32[1024,128]{1,0:T(8,128)S(1)} %copy-done.104, f32[1024,128]{1,0:T(8,128)S(1)} %copy-done.106, bf16[512,1024]{1,0:T(8,128)(2,1)} %get-tuple-element.141.refs_2_.refs_3_.refs_5_, ...), custom_call_target="tpu_custom_call" | custom-call | flops 11274289152 | bytes 6815744 | tf_op jit(solution)/shard_map/attend_back/pallas_call | solution.py:720
  465.3 5.9 attn_grads.2
  473.1 12.7 %attend_back.7.refs_3_.refs_0_ = bf16[1024,768]{1,0:T(8,128)(2,1)S(1)} custom-call(s32[1]{0:T(128)} %bitcast.refs_0_, f32[1024,128]{1,0:T(8,128)S(1)} %copy-done.104, f32[1024,128]{1,0:T(8,128)S(1)} %copy-done.106, bf16[512,1024]{1,0:T(8,128)(2,1)} %get-tuple-element.141.refs_2_.refs_3_.refs_5_, bf16[512,1024]{1,0:T(8,128)(2,1)S(1)} %copy-done.51, ...), custom_call_target="tpu_custom_call" | custom-call | flops 11274289152 | bytes 6815744 | tf_op jit(solution)/shard_map/attend_back/pallas_call | solution.py:720
  487.6 3.8 collective-permute-start.46
  492.9 5.9 attn_grads.3
  499.8 10.0 %collective-permute-done.43.refs_1_ = bf16[512,512]{1,0:T(8,128)(2,1)S(1)} collective-permute-done((bf16[512,512]{1,0:T(8,128)(2,1)S(1)}, bf16[512,512]{1,0:T(8,128)(2,1)S(1)}, u32[]{:S(2)}, u32[]{:S(2)}) %collective-permute-start.43) | collective-permute-done | bytes 524320 | tf_op jit(solution)/shard_map/ppermute | solution.py:810
  512.7 5.0 attn_back.3
  519.4 4.0 collective-permute-start.50
  523.9 8.7 %collective-permute-done.49.refs_5_.refs_1_ = bf16[512,512]{1,0:T(8,128)(2,1)S(1)} collective-permute-done((bf16[512,512]{1,0:T(8,128)(2,1)S(1)}, bf16[512,512]{1,0:T(8,128)(2,1)S(1)}, u32[]{:S(2)}, u32[]{:S(2)}) %collective-permute-start.49) | collective-permute-done | bytes 524320 | tf_op jit(solution)/shard_map/ppermute | solution.py:810
  535.5 7.8 %collective-permute-done.51.refs_4_.refs_1_ = bf16[512,512]{1,0:T(8,128)(2,1)S(1)} collective-permute-done((bf16[512,512]{1,0:T(8,128)(2,1)S(1)}, bf16[512,512]{1,0:T(8,128)(2,1)S(1)}, u32[]{:S(2)}, u32[]{:S(2)}) %collective-permute-start.51) | collective-permute-done | bytes 524320 | tf_op jit(solution)/shard_map/ppermute | solution.py:810
  546.5 5.4 all-to-all-start.2
  557.2 3.9 collective-permute-start.52
  562.6 6.6 %collective-permute-done.55.refs_4_.refs_2_ = bf16[512,512]{1,0:T(8,128)(2,1)S(1)} collective-permute-done((bf16[512,512]{1,0:T(8,128)(2,1)S(1)}, bf16[512,512]{1,0:T(8,128)(2,1)S(1)}, u32[]{:S(2)}, u32[]{:S(2)}) %collective-permute-start.55) | collective-permute-done | bytes 524320 | tf_op jit(solution)/shard_map/ppermute | solution.py:810
  569.2 13.0 %collective-permute-done.52.refs_2_ = bf16[512,512]{1,0:T(8,128)(2,1)S(1)} collective-permute-done((bf16[512,512]{1,0:T(8,128)(2,1)S(1)}, bf16[512,512]{1,0:T(8,128)(2,1)S(1)}, u32[]{:S(2)}, u32[]{:S(2)}) %collective-permute-start.52) | collective-permute-done | bytes 524320 | tf_op jit(solution)/shard_map/ppermute | solution.py:815
  588.2 7.2 %collective-permute-start.57 = (bf16[512,512]{1,0:T(8,128)(2,1)}, bf16[512,512]{1,0:T(8,128)(2,1)S(1)}, u32[]{:S(2)}, u32[]{:S(2)}) collective-permute-start(bf16[512,512]{1,0:T(8,128)(2,1)} %copy-done.36), channel_id=1, source_target_pairs={{0,3},{1,0},{2,1},{3,2},{4,7},{5,4},{6,5},{7,6},{8,11},{9,8},{10,9... | collective-permute-start | bytes 1572872 | tf_op jit(solution)/shard_map/ppermute | solution.py:815
  602.2 10.0 %all_to_all.20 = f32[16,1,256]{2,1,0:T(1,128)S(1)} all-to-all(f32[16,1,256]{2,1,0:T(1,128)S(1)} %reshape.144), channel_id=1, replica_groups=mesh['section'=2,'dp'=4,'tensor'=4] {'dp','tensor'}, dimensions={0} | all-to-all | bytes 32768 | tf_op jit(solution)/shard_map/all_to_all | solution.py:1352
  (441 shorter events, 148.1 us)
Async XLA Ops:
  9.0 8.5 %collective-permute-start = (bf16[2,128,1024]{2,1,0:T(8,128)(2,1)}, bf16[2,128,1024]{2,1,0:T(8,128)(2,1)}, u32[]{:S(2)}, u32[]{:S(2)}) collective-permute-start(bf16[2,128,1024]{2,1,0:T(8,128)(2,1)} %dynamic-slice_bitcast_fusion.2), channel_id=1, source_target_pairs={{0,4},{4,0},{8,12},{12,8},{1,5},{5,1},{9,13},{13,9},{2,6},{6,2},{1... | collective-permute-start | bytes 1572872 | tf_op jit(solution)/shard_map/ppermute | solution.py:810
  12.0 17.7 %collective-permute-start.1 = (bf16[512,512]{1,0:T(8,128)(2,1)S(1)}, bf16[512,512]{1,0:T(8,128)(2,1)}, u32[]{:S(2)}, u32[]{:S(2)}) collective-permute-start(bf16[512,512]{1,0:T(8,128)(2,1)S(1)} %pad_maximum_fusion.3.refs_5_.refs_1_.refs_2_), channel_id=1, source_target_pairs={{0,1},{1,2},{2,3},{3,0},{4,5},{5,6},{6,7},{7,4},{8,9},{9,10},{10,1... | collective-permute-start | bytes 1572872 | tf_op jit(solution)/shard_map/ppermute | solution.py:815
  14.6 15.1 %collective-permute-start.2 = (bf16[512,512]{1,0:T(8,128)(2,1)S(1)}, bf16[512,512]{1,0:T(8,128)(2,1)S(1)}, u32[]{:S(2)}, u32[]{:S(2)}) collective-permute-start(bf16[512,512]{1,0:T(8,128)(2,1)S(1)} %pad_maximum_fusion.3.refs_5_.refs_1_.refs_2_), channel_id=1, source_target_pairs={{0,8},{4,12},{8,0},{12,4},{1,9},{5,13},{9,1},{13,5},{2,10},{6,14},... | collective-permute-start | bytes 1572872 | tf_op jit(solution)/shard_map/ppermute | solution.py:810
  17.0 22.9 %collective-permute-start.3 = (bf16[512,512]{1,0:T(8,128)(2,1)}, bf16[512,512]{1,0:T(8,128)(2,1)S(1)}, u32[]{:S(2)}, u32[]{:S(2)}) collective-permute-start(bf16[512,512]{1,0:T(8,128)(2,1)} %dynamic-slice_bitcast_fusion.1.refs_0_), channel_id=1, source_target_pairs={{0,8},{4,12},{8,0},{12,4},{1,9},{5,13},{9,1},{13,5},{2,10},{6,14},... | collective-permute-start | bytes 1572872 | tf_op jit(solution)/shard_map/ppermute | solution.py:810
  19.8 57.7 %all-to-all-start = ((bf16[4,128,1024]{2,1,0:T(8,128)(2,1)}), bf16[4,128,1024]{2,1,0:T(8,128)(2,1)S(1)}, u32[]{:S(2)}, u32[]{:S(2)}) async-start(bf16[4,128,1024]{2,1,0:T(8,128)(2,1)} %pad_maximum_fusion), calls=%async_computation | async-start | bytes 2097152 | tf_op jit(solution)/shard_map/all_to_all | solution.py:1083
  41.8 15.7 %collective-permute-start.4 = (bf16[512,512]{1,0:T(8,128)(2,1)S(1)}, bf16[512,512]{1,0:T(8,128)(2,1)S(1)}, u32[]{:S(2)}, u32[]{:S(2)}) collective-permute-start(bf16[512,512]{1,0:T(8,128)(2,1)S(1)} %gate.3.refs_6_.refs_2_.refs_3_), channel_id=1, source_target_pairs={{0,1},{1,2},{2,3},{3,0},{4,5},{5,6},{6,7},{7,4},{8,9},{9,10},{10,1... | collective-permute-start | bytes 1572872 | tf_op jit(solution)/shard_map/ppermute | solution.py:815
  44.5 18.8 %collective-permute-start.5 = (bf16[512,512]{1,0:T(8,128)(2,1)S(1)}, bf16[512,512]{1,0:T(8,128)(2,1)S(1)}, u32[]{:S(2)}, u32[]{:S(2)}) collective-permute-start(bf16[512,512]{1,0:T(8,128)(2,1)S(1)} %dynamic-slice_bitcast_fusion.refs_1_), channel_id=1, source_target_pairs={{0,8},{4,12},{8,0},{12,4},{1,9},{5,13},{9,1},{13,5},{2,10},{6,14},... | collective-permute-start | bytes 1572872 | tf_op jit(solution)/shard_map/ppermute | solution.py:810
  57.5 18.7 %collective-permute-start.7 = (bf16[512,512]{1,0:T(8,128)(2,1)S(1)}, bf16[512,512]{1,0:T(8,128)(2,1)}, u32[]{:S(2)}, u32[]{:S(2)}) collective-permute-start(bf16[512,512]{1,0:T(8,128)(2,1)S(1)} %collective-permute-done.4.refs_2_.refs_7_.refs_3_.refs_5_.refs_4_), channel_id=1, source_target_pairs={{0,1},{1,2},{2,3},{3,0},{4,5},{5,6},{6,7},{7,4},{8,9},{9,10},{10,1... | collective-permute-start | bytes 1572872 | tf_op jit(solution)/shard_map/ppermute | solution.py:815
  61.8 17.5 %collective-permute-start.8 = (bf16[512,512]{1,0:T(8,128)(2,1)S(1)}, bf16[512,512]{1,0:T(8,128)(2,1)}, u32[]{:S(2)}, u32[]{:S(2)}) collective-permute-start(bf16[512,512]{1,0:T(8,128)(2,1)S(1)} %gate.3.refs_6_.refs_2_.refs_3_), channel_id=1, source_target_pairs={{0,8},{4,12},{8,0},{12,4},{1,9},{5,13},{9,1},{13,5},{2,10},{6,14},... | collective-permute-start | bytes 1572872 | tf_op jit(solution)/shard_map/ppermute | solution.py:810
  66.3 21.1 %collective-permute-start.11 = (bf16[512,512]{1,0:T(8,128)(2,1)}, bf16[512,512]{1,0:T(8,128)(2,1)}, u32[]{:S(2)}, u32[]{:S(2)}) collective-permute-start(bf16[512,512]{1,0:T(8,128)(2,1)} %get-tuple-element.97.refs_2_.refs_1_), channel_id=1, source_target_pairs={{0,1},{1,2},{2,3},{3,0},{4,5},{5,6},{6,7},{7,4},{8,9},{9,10},{10,1... | collective-permute-start | bytes 1572872 | tf_op jit(solution)/shard_map/ppermute | solution.py:815
  68.8 31.4 %collective-permute-start.13 = (bf16[512,512]{1,0:T(8,128)(2,1)}, bf16[512,512]{1,0:T(8,128)(2,1)}, u32[]{:S(2)}, u32[]{:S(2)}) collective-permute-start(bf16[512,512]{1,0:T(8,128)(2,1)} %get-tuple-element.98.refs_1_.refs_3_), channel_id=1, source_target_pairs={{0,1},{1,2},{2,3},{3,0},{4,5},{5,6},{6,7},{7,4},{8,9},{9,10},{10,1... | collective-permute-start | bytes 1572872 | tf_op jit(solution)/shard_map/ppermute | solution.py:815
  68.8 19.2 %collective-permute-start.9 = (bf16[512,512]{1,0:T(8,128)(2,1)}, bf16[512,512]{1,0:T(8,128)(2,1)}, u32[]{:S(2)}, u32[]{:S(2)}) collective-permute-start(bf16[512,512]{1,0:T(8,128)(2,1)} %copy-done.25), channel_id=1, source_target_pairs={{0,8},{4,12},{8,0},{12,4},{1,9},{5,13},{9,1},{13,5},{2,10},{6,14},... | collective-permute-start | bytes 1572872 | tf_op jit(solution)/shard_map/ppermute | solution.py:810
  76.2 24.3 %collective-permute-start.10 = (bf16[512,512]{1,0:T(8,128)(2,1)}, bf16[512,512]{1,0:T(8,128)(2,1)}, u32[]{:S(2)}, u32[]{:S(2)}) collective-permute-start(bf16[512,512]{1,0:T(8,128)(2,1)} %collective-permute-done.7.refs_8_.refs_4_.refs_6_.refs_5_), channel_id=1, source_target_pairs={{0,8},{4,12},{8,0},{12,4},{1,9},{5,13},{9,1},{13,5},{2,10},{6,14},... | collective-permute-start | bytes 1572872 | tf_op jit(solution)/shard_map/ppermute | solution.py:810
  79.4 50.1 %copy-start.7 = (bf16[512,1024]{1,0:T(8,128)(2,1)}, bf16[512,1024]{1,0:T(8,128)(2,1)S(1)}, u32[]{:S(2)}) copy-start(bf16[512,1024]{1,0:T(8,128)(2,1)S(1)} %norm_in.2.refs_3_.refs_1_) | copy-start | bytes 3145732
  79.4 48.9 %collective-permute-start.6 = (bf16[512,1024]{1,0:T(8,128)(2,1)S(1)}, bf16[512,1024]{1,0:T(8,128)(2,1)S(1)}, u32[]{:S(2)}, u32[]{:S(2)}) collective-permute-start(bf16[512,1024]{1,0:T(8,128)(2,1)S(1)} %norm_in.2.refs_3_.refs_1_), channel_id=1, source_target_pairs={{0,4},{4,0},{8,12},{12,8},{1,5},{5,1},{9,13},{13,9},{2,6},{6,2},{1... | collective-permute-start | bytes 3145736 | tf_op jit(solution)/shard_map/ppermute | solution.py:810
  87.4 22.4 %collective-permute-start.12 = (bf16[512,512]{1,0:T(8,128)(2,1)}, bf16[512,512]{1,0:T(8,128)(2,1)S(1)}, u32[]{:S(2)}, u32[]{:S(2)}) collective-permute-start(bf16[512,512]{1,0:T(8,128)(2,1)} %collective-permute-done.11.refs_3_.refs_2_), channel_id=1, source_target_pairs={{0,1},{1,2},{2,3},{3,0},{4,5},{5,6},{6,7},{7,4},{8,9},{9,10},{10,1... | collective-permute-start | bytes 1572872 | tf_op jit(solution)/shard_map/ppermute | solution.py:815
  88.0 40.1 %collective-permute-start.15 = (bf16[512,512]{1,0:T(8,128)(2,1)}, bf16[512,512]{1,0:T(8,128)(2,1)S(1)}, u32[]{:S(2)}, u32[]{:S(2)}) collective-permute-start(bf16[512,512]{1,0:T(8,128)(2,1)} %collective-permute-done.11.refs_3_.refs_2_), channel_id=1, source_target_pairs={{0,8},{4,12},{8,0},{12,4},{1,9},{5,13},{9,1},{13,5},{2,10},{6,14},... | collective-permute-start | bytes 1572872 | tf_op jit(solution)/shard_map/ppermute | solution.py:810
  100.2 20.8 %collective-permute-start.14 = (bf16[512,512]{1,0:T(8,128)(2,1)}, bf16[512,512]{1,0:T(8,128)(2,1)S(1)}, u32[]{:S(2)}, u32[]{:S(2)}) collective-permute-start(bf16[512,512]{1,0:T(8,128)(2,1)} %collective-permute-done.13.refs_2_.refs_4_), channel_id=1, source_target_pairs={{0,1},{1,2},{2,3},{3,0},{4,5},{5,6},{6,7},{7,4},{8,9},{9,10},{10,1... | collective-permute-start | bytes 1572872 | tf_op jit(solution)/shard_map/ppermute | solution.py:815
  100.4 27.7 %collective-permute-start.16 = (bf16[512,512]{1,0:T(8,128)(2,1)}, bf16[512,512]{1,0:T(8,128)(2,1)S(1)}, u32[]{:S(2)}, u32[]{:S(2)}) collective-permute-start(bf16[512,512]{1,0:T(8,128)(2,1)} %collective-permute-done.13.refs_2_.refs_4_), channel_id=1, source_target_pairs={{0,8},{4,12},{8,0},{12,4},{1,9},{5,13},{9,1},{13,5},{2,10},{6,14},... | collective-permute-start | bytes 1572872 | tf_op jit(solution)/shard_map/ppermute | solution.py:810
  109.8 40.5 %collective-permute-start.17 = (bf16[512,512]{1,0:T(8,128)(2,1)S(1)}, bf16[512,512]{1,0:T(8,128)(2,1)S(1)}, u32[]{:S(2)}, u32[]{:S(2)}) collective-permute-start(bf16[512,512]{1,0:T(8,128)(2,1)S(1)} %collective-permute-done.12.refs_13_.refs_4_.refs_3_), channel_id=1, source_target_pairs={{0,1},{1,2},{2,3},{3,0},{4,5},{5,6},{6,7},{7,4},{8,9},{9,10},{10,1... | collective-permute-start | bytes 1572872 | tf_op jit(solution)/shard_map/ppermute | solution.py:815
  121.0 29.3 %collective-permute-start.19 = (bf16[512,512]{1,0:T(8,128)(2,1)S(1)}, bf16[512,512]{1,0:T(8,128)(2,1)S(1)}, u32[]{:S(2)}, u32[]{:S(2)}) collective-permute-start(bf16[512,512]{1,0:T(8,128)(2,1)S(1)} %collective-permute-done.12.refs_13_.refs_4_.refs_3_), channel_id=1, source_target_pairs={{0,8},{4,12},{8,0},{12,4},{1,9},{5,13},{9,1},{13,5},{2,10},{6,14},... | collective-permute-start | bytes 1572872 | tf_op jit(solution)/shard_map/ppermute | solution.py:810
  128.1 22.1 %collective-permute-start.18 = (bf16[512,512]{1,0:T(8,128)(2,1)S(1)}, bf16[512,512]{1,0:T(8,128)(2,1)S(1)}, u32[]{:S(2)}, u32[]{:S(2)}) collective-permute-start(bf16[512,512]{1,0:T(8,128)(2,1)S(1)} %collective-permute-done.14.refs_14_.refs_3_.refs_5_), channel_id=1, source_target_pairs={{0,1},{1,2},{2,3},{3,0},{4,5},{5,6},{6,7},{7,4},{8,9},{9,10},{10,1... | collective-permute-start | bytes 1572872 | tf_op jit(solution)/shard_map/ppermute | solution.py:815
  128.2 22.6 %collective-permute-start.20 = (bf16[512,512]{1,0:T(8,128)(2,1)S(1)}, bf16[512,512]{1,0:T(8,128)(2,1)S(1)}, u32[]{:S(2)}, u32[]{:S(2)}) collective-permute-start(bf16[512,512]{1,0:T(8,128)(2,1)S(1)} %collective-permute-done.14.refs_14_.refs_3_.refs_5_), channel_id=1, source_target_pairs={{0,8},{4,12},{8,0},{12,4},{1,9},{5,13},{9,1},{13,5},{2,10},{6,14},... | collective-permute-start | bytes 1572872 | tf_op jit(solution)/shard_map/ppermute | solution.py:810
  154.7 14.6 %collective-permute-start.21 = (bf16[512,1024]{1,0:T(8,128)(2,1)S(1)}, bf16[512,1024]{1,0:T(8,128)(2,1)S(1)}, u32[]{:S(2)}, u32[]{:S(2)}) collective-permute-start(bf16[512,1024]{1,0:T(8,128)(2,1)S(1)} %get-tuple-element.101), channel_id=1, source_target_pairs={{0,4},{4,0},{8,12},{12,8},{1,5},{5,1},{9,13},{13,9},{2,6},{6,2},{1... | collective-permute-start | bytes 3145736 | tf_op jit(solution)/shard_map/ppermute | solution.py:810
  154.8 14.6 %collective-permute-start.22 = (bf16[512,512]{1,0:T(8,128)(2,1)}, bf16[512,512]{1,0:T(8,128)(2,1)S(1)}, u32[]{:S(2)}, u32[]{:S(2)}) collective-permute-start(bf16[512,512]{1,0:T(8,128)(2,1)} %copy-done.97), channel_id=1, source_target_pairs={{0,8},{4,12},{8,0},{12,4},{1,9},{5,13},{9,1},{13,5},{2,10},{6,14},... | collective-permute-start | bytes 1572872 | tf_op jit(solution)/shard_map/ppermute | solution.py:810
  173.8 2.7 collective-permute-start.23
  173.9 15.0 %collective-permute-start.24 = (bf16[512,512]{1,0:T(8,128)(2,1)S(1)}, bf16[512,512]{1,0:T(8,128)(2,1)S(1)}, u32[]{:S(2)}, u32[]{:S(2)}) collective-permute-start(bf16[512,512]{1,0:T(8,128)(2,1)S(1)} %copy-done.59), channel_id=1, source_target_pairs={{0,8},{4,12},{8,0},{12,4},{1,9},{5,13},{9,1},{13,5},{2,10},{6,14},... | collective-permute-start | bytes 1572872 | tf_op jit(solution)/shard_map/ppermute | solution.py:810
  188.9 96.3 %copy-start.115 = (bf16[512,512]{1,0:T(8,128)(2,1)}, bf16[512,512]{1,0:T(8,128)(2,1)S(1)}, u32[]{:S(2)}) copy-start(bf16[512,512]{1,0:T(8,128)(2,1)S(1)} %collective-permute-done.24.refs_8_.refs_10_) | copy-start | bytes 1572868
  195.5 2.7 collective-permute-start.25
  200.1 26.0 %collective-permute-start.26 = (bf16[512,1024]{1,0:T(8,128)(2,1)S(1)}, bf16[512,1024]{1,0:T(8,128)(2,1)S(1)}, u32[]{:S(2)}, u32[]{:S(2)}) collective-permute-start(bf16[512,1024]{1,0:T(8,128)(2,1)S(1)} %get-tuple-element.132), channel_id=1, source_target_pairs={{0,16},{1,17},{2,18},{3,19},{4,20},{5,21},{6,22},{7,23},{8,24},{9,... | collective-permute-start | bytes 3145736 | tf_op jit(solution)/shard_map/ppermute | solution.py:28
  228.3 2.7 collective-permute-start.27
  250.9 2.7 collective-permute-start.28
  257.1 2.7 collective-permute-start.29
  275.6 2.7 collective-permute-start.30
  282.5 2.7 collective-permute-start.31
  299.4 2.7 collective-permute-start.32
  306.0 2.7 collective-permute-start.33
  341.7 2.7 collective-permute-start.34
  347.5 27.4 %collective-permute-start.35 = (bf16[512,1024]{1,0:T(8,128)(2,1)}, bf16[512,1024]{1,0:T(8,128)(2,1)S(1)}, u32[]{:S(2)}, u32[]{:S(2)}) collective-permute-start(bf16[512,1024]{1,0:T(8,128)(2,1)} %get-tuple-element.131.refs_2_), channel_id=1, source_target_pairs={{16,0},{17,1},{18,2},{19,3},{20,4},{21,5},{22,6},{23,7},{24,8},{25... | collective-permute-start | bytes 3145736 | tf_op jit(solution)/shard_map/ppermute | solution.py:28
  350.3 31.3 %all-to-all-start.1 = ((bf16[4,128,1024]{2,1,0:T(8,128)(2,1)}), bf16[4,128,1024]{2,1,0:T(8,128)(2,1)}, u32[]{:S(2)}, u32[]{:S(2)}) async-start(bf16[4,128,1024]{2,1,0:T(8,128)(2,1)} %bitcast.41), calls=%async_computation.1 | async-start | bytes 2097152 | tf_op jit(solution)/shard_map/all_to_all | solution.py:1241
  379.0 2.7 collective-permute-start.36
  405.5 2.7 collective-permute-start.37
  405.7 26.0 %collective-permute-start.41 = (bf16[1024,512]{1,0:T(8,128)(2,1)S(1)}, bf16[1024,512]{1,0:T(8,128)(2,1)S(1)}, u32[]{:S(2)}, u32[]{:S(2)}) collective-permute-start(bf16[1024,512]{1,0:T(8,128)(2,1)S(1)} %get-tuple-element.149), channel_id=1, source_target_pairs={{0,8},{4,12},{8,0},{12,4},{1,9},{5,13},{9,1},{13,5},{2,10},{6,14},... | collective-permute-start | bytes 3145736 | tf_op jit(solution)/shard_map/ppermute | solution.py:810
  413.2 34.4 %collective-permute-start.39 = (bf16[512,1024]{1,0:T(8,128)(2,1)}, bf16[512,1024]{1,0:T(8,128)(2,1)S(1)}, u32[]{:S(2)}, u32[]{:S(2)}) collective-permute-start(bf16[512,1024]{1,0:T(8,128)(2,1)} %get-tuple-element.141.refs_2_.refs_3_.refs_5_), channel_id=1, source_target_pairs={{0,4},{4,0},{8,12},{12,8},{1,5},{5,1},{9,13},{13,9},{2,6},{6,2},{1... | collective-permute-start | bytes 3145736 | tf_op jit(solution)/shard_map/ppermute | solution.py:810
  414.7 2.0 collective-permute-start.38
  415.2 46.9 %collective-permute-start.40 = (bf16[1024,512]{1,0:T(8,128)(2,1)S(1)}, bf16[1024,512]{1,0:T(8,128)(2,1)S(1)}, u32[]{:S(2)}, u32[]{:S(2)}) collective-permute-start(bf16[1024,512]{1,0:T(8,128)(2,1)S(1)} %get-tuple-element.148), channel_id=1, source_target_pairs={{0,8},{4,12},{8,0},{12,4},{1,9},{5,13},{9,1},{13,5},{2,10},{6,14},... | collective-permute-start | bytes 3145736 | tf_op jit(solution)/shard_map/ppermute | solution.py:810
  432.1 30.0 %collective-permute-start.42 = (bf16[1024,512]{1,0:T(8,128)(2,1)S(1)}, bf16[1024,512]{1,0:T(8,128)(2,1)S(1)}, u32[]{:S(2)}, u32[]{:S(2)}) collective-permute-start(bf16[1024,512]{1,0:T(8,128)(2,1)S(1)} %moved.6.refs_13_), channel_id=1, source_target_pairs={{0,3},{1,0},{2,1},{3,2},{4,7},{5,4},{6,5},{7,6},{8,11},{9,8},{10,9... | collective-permute-start | bytes 3145736 | tf_op jit(solution)/shard_map/ppermute | solution.py:815
  445.6 41.5 %collective-permute-start.44 = (bf16[1024,512]{1,0:T(8,128)(2,1)S(1)}, bf16[1024,512]{1,0:T(8,128)(2,1)S(1)}, u32[]{:S(2)}, u32[]{:S(2)}) collective-permute-start(bf16[1024,512]{1,0:T(8,128)(2,1)S(1)} %get-tuple-element.154), channel_id=1, source_target_pairs={{0,8},{4,12},{8,0},{12,4},{1,9},{5,13},{9,1},{13,5},{2,10},{6,14},... | collective-permute-start | bytes 3145736 | tf_op jit(solution)/shard_map/ppermute | solution.py:810
  447.1 63.7 %collective-permute-start.47 = (bf16[1024,512]{1,0:T(8,128)(2,1)S(1)}, bf16[1024,512]{1,0:T(8,128)(2,1)S(1)}, u32[]{:S(2)}, u32[]{:S(2)}) collective-permute-start(bf16[1024,512]{1,0:T(8,128)(2,1)S(1)} %get-tuple-element.156), channel_id=1, source_target_pairs={{0,8},{4,12},{8,0},{12,4},{1,9},{5,13},{9,1},{13,5},{2,10},{6,14},... | collective-permute-start | bytes 3145736 | tf_op jit(solution)/shard_map/ppermute | solution.py:810
  463.5 23.5 %collective-permute-start.45 = (bf16[1024,512]{1,0:T(8,128)(2,1)S(1)}, bf16[1024,512]{1,0:T(8,128)(2,1)S(1)}, u32[]{:S(2)}, u32[]{:S(2)}) collective-permute-start(bf16[1024,512]{1,0:T(8,128)(2,1)S(1)} %moved.7.refs_13_), channel_id=1, source_target_pairs={{0,3},{1,0},{2,1},{3,2},{4,7},{5,4},{6,5},{7,6},{8,11},{9,8},{10,9... | collective-permute-start | bytes 3145736 | tf_op jit(solution)/shard_map/ppermute | solution.py:815
  487.6 23.8 %collective-permute-start.46 = (bf16[1024,512]{1,0:T(8,128)(2,1)S(1)}, bf16[1024,512]{1,0:T(8,128)(2,1)S(1)}, u32[]{:S(2)}, u32[]{:S(2)}) collective-permute-start(bf16[1024,512]{1,0:T(8,128)(2,1)S(1)} %moved.8.refs_13_), channel_id=1, source_target_pairs={{0,3},{1,0},{2,1},{3,2},{4,7},{5,4},{6,5},{7,6},{8,11},{9,8},{10,9... | collective-permute-start | bytes 3145736 | tf_op jit(solution)/shard_map/ppermute | solution.py:815
  491.4 18.4 %collective-permute-start.43 = (bf16[512,512]{1,0:T(8,128)(2,1)S(1)}, bf16[512,512]{1,0:T(8,128)(2,1)S(1)}, u32[]{:S(2)}, u32[]{:S(2)}) collective-permute-start(bf16[512,512]{1,0:T(8,128)(2,1)S(1)} %get-tuple-element.153), channel_id=1, source_target_pairs={{0,8},{4,12},{8,0},{12,4},{1,9},{5,13},{9,1},{13,5},{2,10},{6,14},... | collective-permute-start | bytes 1572872 | tf_op jit(solution)/shard_map/ppermute | solution.py:810
  517.7 14.9 %collective-permute-start.48 = (bf16[512,1024]{1,0:T(8,128)(2,1)S(1)}, bf16[512,1024]{1,0:T(8,128)(2,1)S(1)}, u32[]{:S(2)}, u32[]{:S(2)}) collective-permute-start(bf16[512,1024]{1,0:T(8,128)(2,1)S(1)} %get-tuple-element.158), channel_id=1, source_target_pairs={{0,4},{4,0},{8,12},{12,8},{1,5},{5,1},{9,13},{13,9},{2,6},{6,2},{1... | collective-permute-start | bytes 3145736 | tf_op jit(solution)/shard_map/ppermute | solution.py:810
  517.8 14.8 %collective-permute-start.49 = (bf16[512,512]{1,0:T(8,128)(2,1)S(1)}, bf16[512,512]{1,0:T(8,128)(2,1)S(1)}, u32[]{:S(2)}, u32[]{:S(2)}) collective-permute-start(bf16[512,512]{1,0:T(8,128)(2,1)S(1)} %get-tuple-element.160), channel_id=1, source_target_pairs={{0,8},{4,12},{8,0},{12,4},{1,9},{5,13},{9,1},{13,5},{2,10},{6,14},... | collective-permute-start | bytes 1572872 | tf_op jit(solution)/shard_map/ppermute | solution.py:810
  519.4 16.2 %collective-permute-start.50 = (bf16[512,512]{1,0:T(8,128)(2,1)S(1)}, bf16[512,512]{1,0:T(8,128)(2,1)S(1)}, u32[]{:S(2)}, u32[]{:S(2)}) collective-permute-start(bf16[512,512]{1,0:T(8,128)(2,1)S(1)} %copy-done.119), channel_id=1, source_target_pairs={{0,3},{1,0},{2,1},{3,2},{4,7},{5,4},{6,5},{7,6},{8,11},{9,8},{10,9... | collective-permute-start | bytes 1572872 | tf_op jit(solution)/shard_map/ppermute | solution.py:815
  523.3 20.0 %collective-permute-start.51 = (bf16[512,512]{1,0:T(8,128)(2,1)S(1)}, bf16[512,512]{1,0:T(8,128)(2,1)S(1)}, u32[]{:S(2)}, u32[]{:S(2)}) collective-permute-start(bf16[512,512]{1,0:T(8,128)(2,1)S(1)} %get-tuple-element.162), channel_id=1, source_target_pairs={{0,8},{4,12},{8,0},{12,4},{1,9},{5,13},{9,1},{13,5},{2,10},{6,14},... | collective-permute-start | bytes 1572872 | tf_op jit(solution)/shard_map/ppermute | solution.py:810
  546.5 36.4 %all-to-all-start.2 = ((bf16[4,128,1024]{2,1,0:T(8,128)(2,1)}), bf16[4,128,1024]{2,1,0:T(8,128)(2,1)S(1)}, u32[]{:S(2)}, u32[]{:S(2)}) async-start(bf16[4,128,1024]{2,1,0:T(8,128)(2,1)} %bitcast.16), calls=%async_computation.2 | async-start | bytes 2097152 | tf_op jit(solution)/shard_map/all_to_all | solution.py:1322
  554.7 6.4 %collective-permute-start.53 = (f32[256,512]{1,0:T(8,128)S(1)}, f32[256,512]{1,0:T(8,128)S(1)}, u32[]{:S(2)}, u32[]{:S(2)}) collective-permute-start(f32[256,512]{1,0:T(8,128)S(1)} %get-tuple-element.167), channel_id=1, source_target_pairs={{0,4},{4,0},{8,12},{12,8},{1,5},{5,1},{9,13},{13,9},{2,6},{6,2},{1... | collective-permute-start | bytes 1572872 | tf_op jit(solution)/shard_map/ppermute | solution.py:810
  554.8 6.3 %collective-permute-start.54 = (f32[512,256]{1,0:T(8,128)S(1)}, f32[512,256]{1,0:T(8,128)S(1)}, u32[]{:S(2)}, u32[]{:S(2)}) collective-permute-start(f32[512,256]{1,0:T(8,128)S(1)} %get-tuple-element.168), channel_id=1, source_target_pairs={{0,4},{4,0},{8,12},{12,8},{1,5},{5,1},{9,13},{13,9},{2,6},{6,2},{1... | collective-permute-start | bytes 1572872 | tf_op jit(solution)/shard_map/ppermute | solution.py:810
  555.4 13.8 %collective-permute-start.55 = (bf16[512,512]{1,0:T(8,128)(2,1)S(1)}, bf16[512,512]{1,0:T(8,128)(2,1)S(1)}, u32[]{:S(2)}, u32[]{:S(2)}) collective-permute-start(bf16[512,512]{1,0:T(8,128)(2,1)S(1)} %copy-done.127), channel_id=1, source_target_pairs={{0,8},{4,12},{8,0},{12,4},{1,9},{5,13},{9,1},{13,5},{2,10},{6,14},... | collective-permute-start | bytes 1572872 | tf_op jit(solution)/shard_map/ppermute | solution.py:810
  557.2 25.0 %collective-permute-start.52 = (bf16[512,512]{1,0:T(8,128)(2,1)S(1)}, bf16[512,512]{1,0:T(8,128)(2,1)S(1)}, u32[]{:S(2)}, u32[]{:S(2)}) collective-permute-start(bf16[512,512]{1,0:T(8,128)(2,1)S(1)} %moved.10), channel_id=1, source_target_pairs={{0,3},{1,0},{2,1},{3,2},{4,7},{5,4},{6,5},{7,6},{8,11},{9,8},{10,9... | collective-permute-start | bytes 1572872 | tf_op jit(solution)/shard_map/ppermute | solution.py:815
  588.2 25.9 %collective-permute-start.56 = (bf16[2,128,1024]{2,1,0:T(8,128)(2,1)}, bf16[2,128,1024]{2,1,0:T(8,128)(2,1)S(1)}, u32[]{:S(2)}, u32[]{:S(2)}) collective-permute-start(bf16[2,128,1024]{2,1,0:T(8,128)(2,1)} %get-tuple-element.172), channel_id=1, source_target_pairs={{0,4},{4,0},{8,12},{12,8},{1,5},{5,1},{9,13},{13,9},{2,6},{6,2},{1... | collective-permute-start | bytes 1572872 | tf_op jit(solution)/shard_map/ppermute | solution.py:810
  588.2 27.0 %collective-permute-start.57 = (bf16[512,512]{1,0:T(8,128)(2,1)}, bf16[512,512]{1,0:T(8,128)(2,1)S(1)}, u32[]{:S(2)}, u32[]{:S(2)}) collective-permute-start(bf16[512,512]{1,0:T(8,128)(2,1)} %copy-done.36), channel_id=1, source_target_pairs={{0,3},{1,0},{2,1},{3,2},{4,7},{5,4},{6,5},{7,6},{8,11},{9,8},{10,9... | collective-permute-start | bytes 1572872 | tf_op jit(solution)/shard_map/ppermute | solution.py:815
  615.3 2.0 collective-permute-start.58
  (133 other events, 1161.6 us)

commit v18 on v14

--- a/solution.py
+++ b/solution.py
@@ -1210,9 +1210,9 @@
         start,
         (
             (up_piece, up_other[0], down_other[0]),
-            (up_own[1], down_own[1]),
             (up_own[2], down_own[2], up_other[1], down_other[1]),
             (up_own[3], down_own[3], up_other[2], down_other[2]),
+            (up_other[3],),
         ),
     )
     low_one, saved_one, lefts_one = forward(shifted(low_zero, "section", 1), ((),) * 4)

time: 627 us -> 630 us (level)
  Pallas kernels: 221 us -> 236 us
  waiting for transfers between devices: 226 us -> 216 us
    pallas_call x31, Pallas kernels: 86.2 us -> 100 us  [on_chip(): pl.pallas_call(without(kernel, len(operands), len(waits)), in_specs=[spac...]
    ppermute x15, waiting for transfers between devices: 80.3 us -> 73.3 us  [passed_on(): lax.ppermute(block, 'tensor', [(i, (i + step) % size) for i in range(size)])]
    unnamed x290 -> x268, local copies, waits for them, and re-layouts: 47.9 us -> 42.5 us
  transfers between devices with their start and end apart: 62 -> 62, of which waited for: 36 -> 32; matrix products, arithmetic and copies ran while one was open for 4% -> 3% of each run, Pallas kernels for 14% -> 15%
where the time goes in v18:
time: 630 us; the launch traced here: 620 us
  Pallas kernels  236 us (37%)
  waiting for transfers between devices  216 us (34%)
  starting transfers between devices  83.9 us (13%)
  local copies, waits for them, and re-layouts  52.7 us (8%)
  other arithmetic  18.8 us (3%)
  blocking collectives  10 us (2%)
    pallas_call x31, Pallas kernels, on_chip(): pl.pallas_call(without(kernel, len(operands), len(waits)), in_specs=[spac...  100 us
    ppermute x42, waiting for transfers between devices, flip_pairs(): return lax.ppermute(block, 'dp', [(i, i ^ distance) for i in range(size)])  98 us
    pallas_call x6, Pallas kernels, by_pairs(): pl.pallas_call(without(functools.partial(kernel, len(pieces[0])), taken,...  85.7 us
    ppermute x15, waiting for transfers between devices, passed_on(): lax.ppermute(block, 'tensor', [(i, (i + step) % size) for i in range(size)])  73.3 us
    unnamed x268, local copies, waits for them, and re-layouts  42.5 us
    ppermute x2, waiting for transfers between devices, shifted(): return lax.ppermute(block, axis, route)  41.9 us
    ppermute x15, starting transfers between devices, passed_on(): lax.ppermute(block, 'tensor', [(i, (i + step) % size) for i in range(size)])  35.9 us
    ppermute x42, starting transfers between devices, flip_pairs(): return lax.ppermute(block, 'dp', [(i, i ^ distance) for i in range(size)])  29.2 us
  transfers between devices with their start and end apart: 62, of which 32 were waited for; matrix products, arithmetic and copies ran while one was open for 3% of the time, Pallas kernels for 15%

profile of v18, /device:TPU:0, one launch (start us, length us, event | category | flops | bytes accessed | tf_op | source)
XLA Modules:
  0.0 619.5 jit_solution(8855218708950901719)
XLA Ops:
  4.6 2.5 maximum_select_fusion
  12.0 2.6 collective-permute-start.1
  19.8 3.9 all-to-all-start
  23.7 6.0 collective-permute-done.1.refs_0_
  29.7 10.2 %collective-permute-done.3.refs_2_.refs_3_.refs_6_.refs_5_ = bf16[512,512]{1,0:T(8,128)(2,1)S(1)} collective-permute-done((bf16[512,512]{1,0:T(8,128)(2,1)}, bf16[512,512]{1,0:T(8,128)(2,1)S(1)}, u32[]{:S(2)}, u32[]{:S(2)}) %collective-permute-start.3) | collective-permute-done | bytes 524320 | tf_op jit(solution)/shard_map/ppermute | solution.py:798
  46.9 11.0 %collective-permute-done.4.refs_2_.refs_7_.refs_3_.refs_5_.refs_4_ = bf16[512,512]{1,0:T(8,128)(2,1)S(1)} collective-permute-done((bf16[512,512]{1,0:T(8,128)(2,1)}, bf16[512,512]{1,0:T(8,128)(2,1)S(1)}, u32[]{:S(2)}, u32[]{:S(2)}) %collective-permute-start.4) | collective-permute-done | bytes 524320 | tf_op jit(solution)/shard_map/ppermute | solution.py:803
  57.9 4.0 collective-permute-start.7
  70.3 6.8 %collective-permute-done.7.refs_8_.refs_4_.refs_6_.refs_5_ = bf16[512,512]{1,0:T(8,128)(2,1)} collective-permute-done((bf16[512,512]{1,0:T(8,128)(2,1)S(1)}, bf16[512,512]{1,0:T(8,128)(2,1)}, u32[]{:S(2)}, u32[]{:S(2)}) %collective-permute-start.7) | collective-permute-done | bytes 524320 | tf_op jit(solution)/shard_map/ppermute | solution.py:803
  80.4 8.0 %collective-permute-done.11.refs_3_.refs_2_ = bf16[512,512]{1,0:T(8,128)(2,1)} collective-permute-done((bf16[512,512]{1,0:T(8,128)(2,1)}, bf16[512,512]{1,0:T(8,128)(2,1)}, u32[]{:S(2)}, u32[]{:S(2)}) %collective-permute-start.11) | collective-permute-done | bytes 524320 | tf_op jit(solution)/shard_map/ppermute | solution.py:803
  89.9 9.7 %collective-permute-done.13.refs_2_.refs_4_ = bf16[512,512]{1,0:T(8,128)(2,1)} collective-permute-done((bf16[512,512]{1,0:T(8,128)(2,1)}, bf16[512,512]{1,0:T(8,128)(2,1)}, u32[]{:S(2)}, u32[]{:S(2)}) %collective-permute-start.13) | collective-permute-done | bytes 524320 | tf_op jit(solution)/shard_map/ppermute | solution.py:803
  103.9 6.8 %collective-permute-done.12.refs_13_.refs_4_.refs_3_ = bf16[512,512]{1,0:T(8,128)(2,1)S(1)} collective-permute-done((bf16[512,512]{1,0:T(8,128)(2,1)}, bf16[512,512]{1,0:T(8,128)(2,1)S(1)}, u32[]{:S(2)}, u32[]{:S(2)}) %collective-permute-start.12) | collective-permute-done | bytes 524320 | tf_op jit(solution)/shard_map/ppermute | solution.py:803
  110.7 11.2 %collective-permute-done.14.refs_14_.refs_3_.refs_5_ = bf16[512,512]{1,0:T(8,128)(2,1)S(1)} collective-permute-done((bf16[512,512]{1,0:T(8,128)(2,1)}, bf16[512,512]{1,0:T(8,128)(2,1)S(1)}, u32[]{:S(2)}, u32[]{:S(2)}) %collective-permute-start.14) | collective-permute-done | bytes 524320 | tf_op jit(solution)/shard_map/ppermute | solution.py:803
  124.3 16.7 %attend.2 = (bf16[4,1024,128]{2,1,0:T(8,128)(2,1)S(1)}, bf16[4,1024,128]{2,1,0:T(8,128)(2,1)S(1)}, bf16[4,1024,128]{2,1,0:T(8,128)(2,1)S(1)}, f32[4,2,1024]{2,1,0:T(2,128)S(1)}, bf16[1024,512]{1,0:T(8,128)(2,1)S(1)}) custom-call(s32[1]{0:T(128)} %bitcast.refs_0_, f32[1024,128]{1,0:T(8,128)S(1)} %get-tuple-element.228.refs_1_, ...), custom_call_target="tpu_custom_call" | custom-call | flops 11811160064 | bytes 11567104 | tf_op jit(solution)/shard_map/attend/pallas_call | solution.py:708
  145.8 3.0 attn_out.2
  150.1 13.3 %collective-permute-done.22.refs_4_.refs_9_.refs_8_ = bf16[512,512]{1,0:T(8,128)(2,1)S(1)} collective-permute-done((bf16[512,512]{1,0:T(8,128)(2,1)}, bf16[512,512]{1,0:T(8,128)(2,1)S(1)}, u32[]{:S(2)}, u32[]{:S(2)}) %collective-permute-start.22) | collective-permute-done | bytes 524320 | tf_op jit(solution)/shard_map/ppermute | solution.py:798
  164.3 3.6 after_attn.2
  173.1 9.3 %mlp_up.2 = (bf16[1024,2048]{1,0:T(8,128)(2,1)S(1)}, bf16[1024,2048]{1,0:T(8,128)(2,1)S(1)}) custom-call(bf16[512,1024]{1,0:T(8,128)(2,1)S(1)} %get-tuple-element.103.refs_0_.refs_1_, bf16[512,1024]{1,0:T(8,128)(2,1)S(1)} %collective-permute-done.23.refs_1_.refs_2_, bf16[512,512]{1,0:T(8,128)(2,1)} %get-tuple-element.97.refs_2_.refs_1_, ...), custom_call_target="tpu_custom_call" | custom-call | flops 4294967296 | bytes 14680064 | tf_op jit(solution)/shard_map/mlp_up/pallas_call | solution.py:690
  184.4 6.5 %mlp_down.2 = (f32[512,1024]{1,0:T(8,128)S(1)}, bf16[512,1024]{1,0:T(8,128)(2,1)S(1)}) custom-call(bf16[1024,2048]{1,0:T(8,128)(2,1)S(1)} %get-tuple-element.104.refs_0_.refs_4_, bf16[512,512]{1,0:T(8,128)(2,1)} %get-tuple-element.98.refs_1_.refs_3_, bf16[512,512]{1,0:T(8,128)(2,1)} %collective-permute-done.13.refs_2_.refs_4_, ...), custom_call_target="tpu_custom_call" | custom-call | flops 4294967296 | bytes 11534336 | tf_op jit(solution)/shard_map/mlp_down/pallas_call | solution.py:690
  191.1 2.5 collective-permute-done.25.refs_3_
  195.5 2.8 collective-permute-start.26
  198.3 22.6 %collective-permute-done.26.refs_1_ = bf16[512,1024]{1,0:T(8,128)(2,1)S(1)} collective-permute-done((bf16[512,1024]{1,0:T(8,128)(2,1)S(1)}, bf16[512,1024]{1,0:T(8,128)(2,1)S(1)}, u32[]{:S(2)}, u32[]{:S(2)}) %collective-permute-start.26) | collective-permute-done | bytes 1048608 | tf_op jit(solution)/shard_map/ppermute | solution.py:28
  223.2 2.6 collective-permute-done.27.refs_4_.refs_8_
  225.8 16.9 %attend.3 = (bf16[4,1024,128]{2,1,0:T(8,128)(2,1)S(1)}, bf16[4,1024,128]{2,1,0:T(8,128)(2,1)S(1)}, bf16[4,1024,128]{2,1,0:T(8,128)(2,1)S(1)}, f32[4,2,1024]{2,1,0:T(2,128)S(1)}, bf16[1024,512]{1,0:T(8,128)(2,1)S(1)}) custom-call(s32[1]{0:T(128)} %bitcast.refs_0_, f32[1024,128]{1,0:T(8,128)S(1)} %get-tuple-element.228.refs_1_, ...), custom_call_target="tpu_custom_call" | custom-call | flops 11811160064 | bytes 11567104 | tf_op jit(solution)/shard_map/attend/pallas_call | solution.py:708
  242.8 3.4 attn_out.3
  246.3 2.5 collective-permute-done.28.refs_3_
  248.9 3.4 after_attn.3
  252.5 2.5 collective-permute-done.29.refs_1_.refs_8_
  255.0 9.3 %mlp_up.3 = (bf16[1024,2048]{1,0:T(8,128)(2,1)S(1)}, bf16[1024,2048]{1,0:T(8,128)(2,1)S(1)}) custom-call(bf16[512,1024]{1,0:T(8,128)(2,1)S(1)} %get-tuple-element.112.refs_0_.refs_7_, bf16[512,1024]{1,0:T(8,128)(2,1)S(1)} %collective-permute-done.29.refs_1_.refs_8_, bf16[512,512]{1,0:T(8,128)(2,1)} %get-tuple-element.97.refs_2_.refs_1_, ...), custom_call_target="tpu_custom_call" | custom-call | flops 4294967296 | bytes 14680064 | tf_op jit(solution)/shard_map/mlp_up/pallas_call | solution.py:690
  266.4 6.4 %mlp_down.3 = (f32[512,1024]{1,0:T(8,128)S(1)}, bf16[512,1024]{1,0:T(8,128)(2,1)S(1)}) custom-call(bf16[1024,2048]{1,0:T(8,128)(2,1)S(1)} %get-tuple-element.113.refs_0_.refs_10_, bf16[512,512]{1,0:T(8,128)(2,1)} %get-tuple-element.98.refs_1_.refs_3_, bf16[512,512]{1,0:T(8,128)(2,1)} %collective-permute-done.13.refs_2_.refs_4_, ...), custom_call_target="tpu_custom_call" | custom-call | flops 4294967296 | bytes 11534336 | tf_op jit(solution)/shard_map/mlp_down/pallas_call | solution.py:690
  273.0 2.5 collective-permute-done.30.refs_3_
  279.9 2.5 collective-permute-done.31.refs_1_.refs_12_
  282.5 7.2 %mlp_up_back.2.refs_0_.refs_9_ = bf16[1024,2048]{1,0:T(8,128)(2,1)S(1)} custom-call(bf16[512,1024]{1,0:T(8,128)(2,1)S(1)} %get-tuple-element.118.refs_0_.refs_11_, bf16[512,1024]{1,0:T(8,128)(2,1)S(1)} %collective-permute-done.31.refs_1_.refs_12_, bf16[1024,2048]{1,0:T(8,128)(2,1)} %copy-done.40, bf16[512,512]{1,0:T(8,128)(2,1)} %get-tuple-element.98.refs_1_.refs_3_, ...), custom_call_target="tpu_custom_call" | custom-call | tf_op jit(solution)/shard_map/mlp_up_back/pallas_call | solution.py:729
  289.7 6.5 %mlp_back.2 = (f32[512,1024]{1,0:T(8,128)S(1)}, bf16[512,1024]{1,0:T(8,128)(2,1)S(1)}) custom-call(bf16[1024,2048]{1,0:T(8,128)(2,1)S(1)} %mlp_up_back.2.refs_0_.refs_9_, bf16[512,512]{1,0:T(8,128)(2,1)} %get-tuple-element.97.refs_2_.refs_1_, bf16[512,512]{1,0:T(8,128)(2,1)} %collective-permute-done.11.refs_3_.refs_2_, bf16[512,512]{1,0:T(8,128)(2,1)S(1)} %copy-done.118, ...), custom_call_target="tpu_custom_call" | custom-call | flops 4294967296 | bytes 11534336 | tf_op jit(solution)/shard_map/mlp_back/pallas_call | solution.py:690
  298.9 3.9 into_attn_back.2
  305.6 12.8 %attend_back.4.refs_0_.refs_9_ = bf16[1024,768]{1,0:T(8,128)(2,1)S(1)} custom-call(s32[1]{0:T(128)} %bitcast.refs_0_, f32[1024,128]{1,0:T(8,128)S(1)} %get-tuple-element.228.refs_1_, f32[1024,128]{1,0:T(8,128)S(1)} %get-tuple-element.229.refs_2_, bf16[512,1024]{1,0:T(8,128)(2,1)S(1)} %get-tuple-element.123.refs_3_.refs_11_, ...), custom_call_target="tpu_custom_call" | custom-call | flops 11274289152 | bytes 6815744 | tf_op jit(solution)/shard_map/attend_back/pallas_call | solution.py:708
  318.4 13.1 %attend_back.5.refs_1_.refs_9_ = bf16[1024,768]{1,0:T(8,128)(2,1)S(1)} custom-call(s32[1]{0:T(128)} %bitcast.refs_0_, f32[1024,128]{1,0:T(8,128)S(1)} %get-tuple-element.228.refs_1_, f32[1024,128]{1,0:T(8,128)S(1)} %get-tuple-element.229.refs_2_, bf16[512,1024]{1,0:T(8,128)(2,1)S(1)} %get-tuple-element.123.refs_3_.refs_11_, ...), custom_call_target="tpu_custom_call" | custom-call | flops 11274289152 | bytes 6815744 | tf_op jit(solution)/shard_map/attend_back/pallas_call | solution.py:708
  333.1 5.7 attn_back.2
  341.6 3.1 out_of_layer.2
  347.5 5.3 all-to-all-start.1
  352.8 19.3 %collective-permute-done.35.refs_1_ = bf16[512,1024]{1,0:T(8,128)(2,1)S(1)} collective-permute-done((bf16[512,1024]{1,0:T(8,128)(2,1)}, bf16[512,1024]{1,0:T(8,128)(2,1)S(1)}, u32[]{:S(2)}, u32[]{:S(2)}) %collective-permute-start.35) | collective-permute-done | bytes 1048608 | tf_op jit(solution)/shard_map/ppermute | solution.py:28
  376.3 2.6 all-to-all-done.1.refs_11_.refs_1_
  378.9 7.2 %mlp_up_back.3.refs_3_.refs_0_ = bf16[1024,2048]{1,0:T(8,128)(2,1)S(1)} custom-call(bf16[512,1024]{1,0:T(8,128)(2,1)S(1)} %get-tuple-element.135.refs_0_.refs_5_, bf16[512,1024]{1,0:T(8,128)(2,1)S(1)} %collective-permute-done.36.refs_1_.refs_6_, bf16[1024,2048]{1,0:T(8,128)(2,1)} %copy-done.56, bf16[512,512]{1,0:T(8,128)(2,1)} %get-tuple-element.98.refs_1_.refs_3_, ...), custom_call_target="tpu_custom_call" | custom-call | tf_op jit(solution)/shard_map/mlp_up_back/pallas_call | solution.py:729
  388.1 7.2 %mlp_grads.2 = (f32[1024,512]{1,0:T(8,128)S(1)}, bf16[1024,512]{1,0:T(8,128)(2,1)S(1)}, f32[1024,512]{1,0:T(8,128)S(1)}, bf16[1024,512]{1,0:T(8,128)(2,1)S(1)}) custom-call(s32[1]{0:T(128)} %bitcast.12.refs_0_, bf16[512,1024]{1,0:T(8,128)(2,1)} %copy-done.43, bf16[512,1024]{1,0:T(8,128)(2,1)} %copy-done.44, bf16[1024,2048]{1,0:T(8,128)(2,1)} %copy-done.3, ...), custom_call_target="tpu_custom_call" | custom-call | tf_op jit(solution)/shard_map/mlp_grads/pallas_call | solution.py:897
  396.8 5.9 mlp_back.3
  405.4 4.9 into_attn_back.3
  414.9 13.9 %collective-permute-done.41.refs_1_ = bf16[1024,512]{1,0:T(8,128)(2,1)S(1)} collective-permute-done((bf16[1024,512]{1,0:T(8,128)(2,1)S(1)}, bf16[1024,512]{1,0:T(8,128)(2,1)S(1)}, u32[]{:S(2)}, u32[]{:S(2)}) %collective-permute-start.41) | collective-permute-done | bytes 1048608 | tf_op jit(solution)/shard_map/ppermute | solution.py:798
  429.3 3.8 collective-permute-start.42
  433.1 7.0 %mlp_grads.3 = (f32[1024,512]{1,0:T(8,128)S(1)}, bf16[1024,512]{1,0:T(8,128)(2,1)S(1)}, f32[1024,512]{1,0:T(8,128)S(1)}, bf16[1024,512]{1,0:T(8,128)(2,1)S(1)}) custom-call(s32[1]{0:T(128)} %bitcast.12.refs_0_, bf16[512,1024]{1,0:T(8,128)(2,1)} %copy-done.43, bf16[512,1024]{1,0:T(8,128)(2,1)} %copy-done.44, bf16[1024,2048]{1,0:T(8,128)(2,1)} %copy-done.3, ...), custom_call_target="tpu_custom_call" | custom-call | tf_op jit(solution)/shard_map/mlp_grads/pallas_call | solution.py:897
  444.9 13.2 %attend_back.6.refs_3_.refs_1_ = bf16[1024,768]{1,0:T(8,128)(2,1)S(1)} custom-call(s32[1]{0:T(128)} %bitcast.refs_0_, f32[1024,128]{1,0:T(8,128)S(1)} %copy-done.106, f32[1024,128]{1,0:T(8,128)S(1)} %copy-done.108, bf16[512,1024]{1,0:T(8,128)(2,1)} %get-tuple-element.141.refs_2_.refs_3_.refs_5_, ...), custom_call_target="tpu_custom_call" | custom-call | flops 11274289152 | bytes 6815744 | tf_op jit(solution)/shard_map/attend_back/pallas_call | solution.py:708
  462.6 5.9 attn_grads.2
  470.4 12.9 %attend_back.7.refs_3_.refs_0_ = bf16[1024,768]{1,0:T(8,128)(2,1)S(1)} custom-call(s32[1]{0:T(128)} %bitcast.refs_0_, f32[1024,128]{1,0:T(8,128)S(1)} %copy-done.106, f32[1024,128]{1,0:T(8,128)S(1)} %copy-done.108, bf16[512,1024]{1,0:T(8,128)(2,1)} %get-tuple-element.141.refs_2_.refs_3_.refs_5_, bf16[512,1024]{1,0:T(8,128)(2,1)S(1)} %copy-done.52, ...), custom_call_target="tpu_custom_call" | custom-call | flops 11274289152 | bytes 6815744 | tf_op jit(solution)/shard_map/attend_back/pallas_call | solution.py:708
  485.0 3.6 collective-permute-start.46
  490.2 5.9 attn_grads.3
  497.1 9.8 %collective-permute-done.43.refs_1_ = bf16[512,512]{1,0:T(8,128)(2,1)S(1)} collective-permute-done((bf16[512,512]{1,0:T(8,128)(2,1)S(1)}, bf16[512,512]{1,0:T(8,128)(2,1)S(1)}, u32[]{:S(2)}, u32[]{:S(2)}) %collective-permute-start.43) | collective-permute-done | bytes 524320 | tf_op jit(solution)/shard_map/ppermute | solution.py:798
  509.9 5.1 attn_back.3
  516.7 4.1 collective-permute-start.50
  521.4 8.5 %collective-permute-done.49.refs_5_.refs_1_ = bf16[512,512]{1,0:T(8,128)(2,1)S(1)} collective-permute-done((bf16[512,512]{1,0:T(8,128)(2,1)S(1)}, bf16[512,512]{1,0:T(8,128)(2,1)S(1)}, u32[]{:S(2)}, u32[]{:S(2)}) %collective-permute-start.49) | collective-permute-done | bytes 524320 | tf_op jit(solution)/shard_map/ppermute | solution.py:798
  532.8 7.8 %collective-permute-done.51.refs_4_.refs_1_ = bf16[512,512]{1,0:T(8,128)(2,1)S(1)} collective-permute-done((bf16[512,512]{1,0:T(8,128)(2,1)S(1)}, bf16[512,512]{1,0:T(8,128)(2,1)S(1)}, u32[]{:S(2)}, u32[]{:S(2)}) %collective-permute-start.51) | collective-permute-done | bytes 524320 | tf_op jit(solution)/shard_map/ppermute | solution.py:798
  543.8 5.5 all-to-all-start.2
  554.7 3.9 collective-permute-start.52
  560.1 6.6 %collective-permute-done.55.refs_4_.refs_2_ = bf16[512,512]{1,0:T(8,128)(2,1)S(1)} collective-permute-done((bf16[512,512]{1,0:T(8,128)(2,1)S(1)}, bf16[512,512]{1,0:T(8,128)(2,1)S(1)}, u32[]{:S(2)}, u32[]{:S(2)}) %collective-permute-start.55) | collective-permute-done | bytes 524320 | tf_op jit(solution)/shard_map/ppermute | solution.py:798
  566.6 13.0 %collective-permute-done.52.refs_2_ = bf16[512,512]{1,0:T(8,128)(2,1)S(1)} collective-permute-done((bf16[512,512]{1,0:T(8,128)(2,1)S(1)}, bf16[512,512]{1,0:T(8,128)(2,1)S(1)}, u32[]{:S(2)}, u32[]{:S(2)}) %collective-permute-start.52) | collective-permute-done | bytes 524320 | tf_op jit(solution)/shard_map/ppermute | solution.py:803
  585.6 7.2 %collective-permute-start.57 = (bf16[512,512]{1,0:T(8,128)(2,1)}, bf16[512,512]{1,0:T(8,128)(2,1)S(1)}, u32[]{:S(2)}, u32[]{:S(2)}) collective-permute-start(bf16[512,512]{1,0:T(8,128)(2,1)} %copy-done.39), channel_id=1, source_target_pairs={{0,3},{1,0},{2,1},{3,2},{4,7},{5,4},{6,5},{7,6},{8,11},{9,8},{10,9... | collective-permute-start | bytes 1572872 | tf_op jit(solution)/shard_map/ppermute | solution.py:803
  599.7 10.0 %all_to_all.20 = f32[16,1,256]{2,1,0:T(1,128)S(1)} all-to-all(f32[16,1,256]{2,1,0:T(1,128)S(1)} %reshape.144), channel_id=1, replica_groups=mesh['section'=2,'dp'=4,'tensor'=4] {'dp','tensor'}, dimensions={0} | all-to-all | bytes 32768 | tf_op jit(solution)/shard_map/all_to_all | solution.py:1335
  (435 shorter events, 149.2 us)
Async XLA Ops:
  9.0 8.5 %collective-permute-start = (bf16[2,128,1024]{2,1,0:T(8,128)(2,1)}, bf16[2,128,1024]{2,1,0:T(8,128)(2,1)}, u32[]{:S(2)}, u32[]{:S(2)}) collective-permute-start(bf16[2,128,1024]{2,1,0:T(8,128)(2,1)} %dynamic-slice_bitcast_fusion.2), channel_id=1, source_target_pairs={{0,4},{4,0},{8,12},{12,8},{1,5},{5,1},{9,13},{13,9},{2,6},{6,2},{1... | collective-permute-start | bytes 1572872 | tf_op jit(solution)/shard_map/ppermute | solution.py:798
  12.0 17.7 %collective-permute-start.1 = (bf16[512,512]{1,0:T(8,128)(2,1)S(1)}, bf16[512,512]{1,0:T(8,128)(2,1)}, u32[]{:S(2)}, u32[]{:S(2)}) collective-permute-start(bf16[512,512]{1,0:T(8,128)(2,1)S(1)} %pad_maximum_fusion.3.refs_5_.refs_1_.refs_2_), channel_id=1, source_target_pairs={{0,1},{1,2},{2,3},{3,0},{4,5},{5,6},{6,7},{7,4},{8,9},{9,10},{10,1... | collective-permute-start | bytes 1572872 | tf_op jit(solution)/shard_map/ppermute | solution.py:803
  14.6 15.1 %collective-permute-start.2 = (bf16[512,512]{1,0:T(8,128)(2,1)S(1)}, bf16[512,512]{1,0:T(8,128)(2,1)S(1)}, u32[]{:S(2)}, u32[]{:S(2)}) collective-permute-start(bf16[512,512]{1,0:T(8,128)(2,1)S(1)} %pad_maximum_fusion.3.refs_5_.refs_1_.refs_2_), channel_id=1, source_target_pairs={{0,8},{4,12},{8,0},{12,4},{1,9},{5,13},{9,1},{13,5},{2,10},{6,14},... | collective-permute-start | bytes 1572872 | tf_op jit(solution)/shard_map/ppermute | solution.py:798
  17.0 22.9 %collective-permute-start.3 = (bf16[512,512]{1,0:T(8,128)(2,1)}, bf16[512,512]{1,0:T(8,128)(2,1)S(1)}, u32[]{:S(2)}, u32[]{:S(2)}) collective-permute-start(bf16[512,512]{1,0:T(8,128)(2,1)} %dynamic-slice_bitcast_fusion.1.refs_0_), channel_id=1, source_target_pairs={{0,8},{4,12},{8,0},{12,4},{1,9},{5,13},{9,1},{13,5},{2,10},{6,14},... | collective-permute-start | bytes 1572872 | tf_op jit(solution)/shard_map/ppermute | solution.py:798
  19.8 58.7 %all-to-all-start = ((bf16[4,128,1024]{2,1,0:T(8,128)(2,1)}), bf16[4,128,1024]{2,1,0:T(8,128)(2,1)S(1)}, u32[]{:S(2)}, u32[]{:S(2)}) async-start(bf16[4,128,1024]{2,1,0:T(8,128)(2,1)} %pad_maximum_fusion), calls=%async_computation | async-start | bytes 2097152 | tf_op jit(solution)/shard_map/all_to_all | solution.py:1071
  42.6 15.2 %collective-permute-start.4 = (bf16[512,512]{1,0:T(8,128)(2,1)}, bf16[512,512]{1,0:T(8,128)(2,1)S(1)}, u32[]{:S(2)}, u32[]{:S(2)}) collective-permute-start(bf16[512,512]{1,0:T(8,128)(2,1)} %gate.3.refs_6_.refs_2_.refs_3_), channel_id=1, source_target_pairs={{0,1},{1,2},{2,3},{3,0},{4,5},{5,6},{6,7},{7,4},{8,9},{9,10},{10,1... | collective-permute-start | bytes 1572872 | tf_op jit(solution)/shard_map/ppermute | solution.py:803
  45.3 18.2 %collective-permute-start.5 = (bf16[512,512]{1,0:T(8,128)(2,1)S(1)}, bf16[512,512]{1,0:T(8,128)(2,1)S(1)}, u32[]{:S(2)}, u32[]{:S(2)}) collective-permute-start(bf16[512,512]{1,0:T(8,128)(2,1)S(1)} %dynamic-slice_bitcast_fusion.refs_1_), channel_id=1, source_target_pairs={{0,8},{4,12},{8,0},{12,4},{1,9},{5,13},{9,1},{13,5},{2,10},{6,14},... | collective-permute-start | bytes 1572872 | tf_op jit(solution)/shard_map/ppermute | solution.py:798
  57.9 19.2 %collective-permute-start.7 = (bf16[512,512]{1,0:T(8,128)(2,1)S(1)}, bf16[512,512]{1,0:T(8,128)(2,1)}, u32[]{:S(2)}, u32[]{:S(2)}) collective-permute-start(bf16[512,512]{1,0:T(8,128)(2,1)S(1)} %collective-permute-done.4.refs_2_.refs_7_.refs_3_.refs_5_.refs_4_), channel_id=1, source_target_pairs={{0,1},{1,2},{2,3},{3,0},{4,5},{5,6},{6,7},{7,4},{8,9},{9,10},{10,1... | collective-permute-start | bytes 1572872 | tf_op jit(solution)/shard_map/ppermute | solution.py:803
  61.9 18.3 %collective-permute-start.8 = (bf16[512,512]{1,0:T(8,128)(2,1)}, bf16[512,512]{1,0:T(8,128)(2,1)}, u32[]{:S(2)}, u32[]{:S(2)}) collective-permute-start(bf16[512,512]{1,0:T(8,128)(2,1)} %gate.3.refs_6_.refs_2_.refs_3_), channel_id=1, source_target_pairs={{0,8},{4,12},{8,0},{12,4},{1,9},{5,13},{9,1},{13,5},{2,10},{6,14},... | collective-permute-start | bytes 1572872 | tf_op jit(solution)/shard_map/ppermute | solution.py:798
  66.4 22.0 %collective-permute-start.11 = (bf16[512,512]{1,0:T(8,128)(2,1)}, bf16[512,512]{1,0:T(8,128)(2,1)}, u32[]{:S(2)}, u32[]{:S(2)}) collective-permute-start(bf16[512,512]{1,0:T(8,128)(2,1)} %get-tuple-element.97.refs_2_.refs_1_), channel_id=1, source_target_pairs={{0,1},{1,2},{2,3},{3,0},{4,5},{5,6},{6,7},{7,4},{8,9},{9,10},{10,1... | collective-permute-start | bytes 1572872 | tf_op jit(solution)/shard_map/ppermute | solution.py:803
  68.8 30.8 %collective-permute-start.13 = (bf16[512,512]{1,0:T(8,128)(2,1)}, bf16[512,512]{1,0:T(8,128)(2,1)}, u32[]{:S(2)}, u32[]{:S(2)}) collective-permute-start(bf16[512,512]{1,0:T(8,128)(2,1)} %get-tuple-element.98.refs_1_.refs_3_), channel_id=1, source_target_pairs={{0,1},{1,2},{2,3},{3,0},{4,5},{5,6},{6,7},{7,4},{8,9},{9,10},{10,1... | collective-permute-start | bytes 1572872 | tf_op jit(solution)/shard_map/ppermute | solution.py:803
  69.6 18.7 %collective-permute-start.9 = (bf16[512,512]{1,0:T(8,128)(2,1)}, bf16[512,512]{1,0:T(8,128)(2,1)}, u32[]{:S(2)}, u32[]{:S(2)}) collective-permute-start(bf16[512,512]{1,0:T(8,128)(2,1)} %copy-done.29), channel_id=1, source_target_pairs={{0,8},{4,12},{8,0},{12,4},{1,9},{5,13},{9,1},{13,5},{2,10},{6,14},... | collective-permute-start | bytes 1572872 | tf_op jit(solution)/shard_map/ppermute | solution.py:798
  77.1 22.5 %collective-permute-start.10 = (bf16[512,512]{1,0:T(8,128)(2,1)}, bf16[512,512]{1,0:T(8,128)(2,1)}, u32[]{:S(2)}, u32[]{:S(2)}) collective-permute-start(bf16[512,512]{1,0:T(8,128)(2,1)} %collective-permute-done.7.refs_8_.refs_4_.refs_6_.refs_5_), channel_id=1, source_target_pairs={{0,8},{4,12},{8,0},{12,4},{1,9},{5,13},{9,1},{13,5},{2,10},{6,14},... | collective-permute-start | bytes 1572872 | tf_op jit(solution)/shard_map/ppermute | solution.py:798
  80.3 43.8 %copy-start.9 = (bf16[512,1024]{1,0:T(8,128)(2,1)}, bf16[512,1024]{1,0:T(8,128)(2,1)S(1)}, u32[]{:S(2)}) copy-start(bf16[512,1024]{1,0:T(8,128)(2,1)S(1)} %norm_in.2.refs_3_.refs_1_) | copy-start | bytes 3145732
  80.3 43.8 %collective-permute-start.6 = (bf16[512,1024]{1,0:T(8,128)(2,1)S(1)}, bf16[512,1024]{1,0:T(8,128)(2,1)S(1)}, u32[]{:S(2)}, u32[]{:S(2)}) collective-permute-start(bf16[512,1024]{1,0:T(8,128)(2,1)S(1)} %norm_in.2.refs_3_.refs_1_), channel_id=1, source_target_pairs={{0,4},{4,0},{8,12},{12,8},{1,5},{5,1},{9,13},{13,9},{2,6},{6,2},{1... | collective-permute-start | bytes 3145736 | tf_op jit(solution)/shard_map/ppermute | solution.py:798
  88.3 22.4 %collective-permute-start.12 = (bf16[512,512]{1,0:T(8,128)(2,1)}, bf16[512,512]{1,0:T(8,128)(2,1)S(1)}, u32[]{:S(2)}, u32[]{:S(2)}) collective-permute-start(bf16[512,512]{1,0:T(8,128)(2,1)} %collective-permute-done.11.refs_3_.refs_2_), channel_id=1, source_target_pairs={{0,1},{1,2},{2,3},{3,0},{4,5},{5,6},{6,7},{7,4},{8,9},{9,10},{10,1... | collective-permute-start | bytes 1572872 | tf_op jit(solution)/shard_map/ppermute | solution.py:803
  88.4 35.0 %collective-permute-start.15 = (bf16[512,512]{1,0:T(8,128)(2,1)}, bf16[512,512]{1,0:T(8,128)(2,1)S(1)}, u32[]{:S(2)}, u32[]{:S(2)}) collective-permute-start(bf16[512,512]{1,0:T(8,128)(2,1)} %collective-permute-done.11.refs_3_.refs_2_), channel_id=1, source_target_pairs={{0,8},{4,12},{8,0},{12,4},{1,9},{5,13},{9,1},{13,5},{2,10},{6,14},... | collective-permute-start | bytes 1572872 | tf_op jit(solution)/shard_map/ppermute | solution.py:798
  99.6 22.4 %collective-permute-start.14 = (bf16[512,512]{1,0:T(8,128)(2,1)}, bf16[512,512]{1,0:T(8,128)(2,1)S(1)}, u32[]{:S(2)}, u32[]{:S(2)}) collective-permute-start(bf16[512,512]{1,0:T(8,128)(2,1)} %collective-permute-done.13.refs_2_.refs_4_), channel_id=1, source_target_pairs={{0,1},{1,2},{2,3},{3,0},{4,5},{5,6},{6,7},{7,4},{8,9},{9,10},{10,1... | collective-permute-start | bytes 1572872 | tf_op jit(solution)/shard_map/ppermute | solution.py:803
  99.6 23.7 %collective-permute-start.16 = (bf16[512,512]{1,0:T(8,128)(2,1)}, bf16[512,512]{1,0:T(8,128)(2,1)S(1)}, u32[]{:S(2)}, u32[]{:S(2)}) collective-permute-start(bf16[512,512]{1,0:T(8,128)(2,1)} %collective-permute-done.13.refs_2_.refs_4_), channel_id=1, source_target_pairs={{0,8},{4,12},{8,0},{12,4},{1,9},{5,13},{9,1},{13,5},{2,10},{6,14},... | collective-permute-start | bytes 1572872 | tf_op jit(solution)/shard_map/ppermute | solution.py:798
  110.7 33.4 %collective-permute-start.17 = (bf16[512,512]{1,0:T(8,128)(2,1)S(1)}, bf16[512,512]{1,0:T(8,128)(2,1)S(1)}, u32[]{:S(2)}, u32[]{:S(2)}) collective-permute-start(bf16[512,512]{1,0:T(8,128)(2,1)S(1)} %collective-permute-done.12.refs_13_.refs_4_.refs_3_), channel_id=1, source_target_pairs={{0,1},{1,2},{2,3},{3,0},{4,5},{5,6},{6,7},{7,4},{8,9},{9,10},{10,1... | collective-permute-start | bytes 1572872 | tf_op jit(solution)/shard_map/ppermute | solution.py:803
  122.0 22.2 %collective-permute-start.19 = (bf16[512,512]{1,0:T(8,128)(2,1)S(1)}, bf16[512,512]{1,0:T(8,128)(2,1)S(1)}, u32[]{:S(2)}, u32[]{:S(2)}) collective-permute-start(bf16[512,512]{1,0:T(8,128)(2,1)S(1)} %collective-permute-done.12.refs_13_.refs_4_.refs_3_), channel_id=1, source_target_pairs={{0,8},{4,12},{8,0},{12,4},{1,9},{5,13},{9,1},{13,5},{2,10},{6,14},... | collective-permute-start | bytes 1572872 | tf_op jit(solution)/shard_map/ppermute | solution.py:798
  123.3 20.8 %collective-permute-start.18 = (bf16[512,512]{1,0:T(8,128)(2,1)S(1)}, bf16[512,512]{1,0:T(8,128)(2,1)S(1)}, u32[]{:S(2)}, u32[]{:S(2)}) collective-permute-start(bf16[512,512]{1,0:T(8,128)(2,1)S(1)} %collective-permute-done.14.refs_14_.refs_3_.refs_5_), channel_id=1, source_target_pairs={{0,1},{1,2},{2,3},{3,0},{4,5},{5,6},{6,7},{7,4},{8,9},{9,10},{10,1... | collective-permute-start | bytes 1572872 | tf_op jit(solution)/shard_map/ppermute | solution.py:803
  123.4 21.6 %collective-permute-start.20 = (bf16[512,512]{1,0:T(8,128)(2,1)S(1)}, bf16[512,512]{1,0:T(8,128)(2,1)S(1)}, u32[]{:S(2)}, u32[]{:S(2)}) collective-permute-start(bf16[512,512]{1,0:T(8,128)(2,1)S(1)} %collective-permute-done.14.refs_14_.refs_3_.refs_5_), channel_id=1, source_target_pairs={{0,8},{4,12},{8,0},{12,4},{1,9},{5,13},{9,1},{13,5},{2,10},{6,14},... | collective-permute-start | bytes 1572872 | tf_op jit(solution)/shard_map/ppermute | solution.py:798
  148.8 14.6 %collective-permute-start.21 = (bf16[512,1024]{1,0:T(8,128)(2,1)S(1)}, bf16[512,1024]{1,0:T(8,128)(2,1)S(1)}, u32[]{:S(2)}, u32[]{:S(2)}) collective-permute-start(bf16[512,1024]{1,0:T(8,128)(2,1)S(1)} %get-tuple-element.101), channel_id=1, source_target_pairs={{0,4},{4,0},{8,12},{12,8},{1,5},{5,1},{9,13},{13,9},{2,6},{6,2},{1... | collective-permute-start | bytes 3145736 | tf_op jit(solution)/shard_map/ppermute | solution.py:798
  148.8 14.6 %collective-permute-start.22 = (bf16[512,512]{1,0:T(8,128)(2,1)}, bf16[512,512]{1,0:T(8,128)(2,1)S(1)}, u32[]{:S(2)}, u32[]{:S(2)}) collective-permute-start(bf16[512,512]{1,0:T(8,128)(2,1)} %copy-done.99), channel_id=1, source_target_pairs={{0,8},{4,12},{8,0},{12,4},{1,9},{5,13},{9,1},{13,5},{2,10},{6,14},... | collective-permute-start | bytes 1572872 | tf_op jit(solution)/shard_map/ppermute | solution.py:798
  169.3 2.7 collective-permute-start.23
  169.4 15.0 %collective-permute-start.24 = (bf16[512,512]{1,0:T(8,128)(2,1)S(1)}, bf16[512,512]{1,0:T(8,128)(2,1)S(1)}, u32[]{:S(2)}, u32[]{:S(2)}) collective-permute-start(bf16[512,512]{1,0:T(8,128)(2,1)S(1)} %copy-done.33), channel_id=1, source_target_pairs={{0,8},{4,12},{8,0},{12,4},{1,9},{5,13},{9,1},{13,5},{2,10},{6,14},... | collective-permute-start | bytes 1572872 | tf_op jit(solution)/shard_map/ppermute | solution.py:798
  184.4 82.0 %copy-start.63 = (bf16[512,512]{1,0:T(8,128)(2,1)}, bf16[512,512]{1,0:T(8,128)(2,1)S(1)}, u32[]{:S(2)}) copy-start(bf16[512,512]{1,0:T(8,128)(2,1)S(1)} %collective-permute-done.24.refs_8_.refs_10_) | copy-start | bytes 1572868
  190.9 2.7 collective-permute-start.25
  195.5 25.4 %collective-permute-start.26 = (bf16[512,1024]{1,0:T(8,128)(2,1)S(1)}, bf16[512,1024]{1,0:T(8,128)(2,1)S(1)}, u32[]{:S(2)}, u32[]{:S(2)}) collective-permute-start(bf16[512,1024]{1,0:T(8,128)(2,1)S(1)} %get-tuple-element.132), channel_id=1, source_target_pairs={{0,16},{1,17},{2,18},{3,19},{4,20},{5,21},{6,22},{7,23},{8,24},{9,... | collective-permute-start | bytes 3145736 | tf_op jit(solution)/shard_map/ppermute | solution.py:28
  223.1 2.7 collective-permute-start.27
  246.1 2.7 collective-permute-start.28
  252.3 2.7 collective-permute-start.29
  272.8 2.7 collective-permute-start.30
  279.7 2.7 collective-permute-start.31
  296.2 2.7 collective-permute-start.32
  302.9 2.7 collective-permute-start.33
  338.8 2.7 collective-permute-start.34
  344.7 27.4 %collective-permute-start.35 = (bf16[512,1024]{1,0:T(8,128)(2,1)}, bf16[512,1024]{1,0:T(8,128)(2,1)S(1)}, u32[]{:S(2)}, u32[]{:S(2)}) collective-permute-start(bf16[512,1024]{1,0:T(8,128)(2,1)} %get-tuple-element.131.refs_2_), channel_id=1, source_target_pairs={{16,0},{17,1},{18,2},{19,3},{20,4},{21,5},{22,6},{23,7},{24,8},{25... | collective-permute-start | bytes 3145736 | tf_op jit(solution)/shard_map/ppermute | solution.py:28
  347.5 31.4 %all-to-all-start.1 = ((bf16[4,128,1024]{2,1,0:T(8,128)(2,1)}), bf16[4,128,1024]{2,1,0:T(8,128)(2,1)}, u32[]{:S(2)}, u32[]{:S(2)}) async-start(bf16[4,128,1024]{2,1,0:T(8,128)(2,1)} %bitcast.41), calls=%async_computation.1 | async-start | bytes 2097152 | tf_op jit(solution)/shard_map/all_to_all | solution.py:1224
  376.2 2.7 collective-permute-start.36
  402.6 2.7 collective-permute-start.37
  402.8 26.0 %collective-permute-start.41 = (bf16[1024,512]{1,0:T(8,128)(2,1)S(1)}, bf16[1024,512]{1,0:T(8,128)(2,1)S(1)}, u32[]{:S(2)}, u32[]{:S(2)}) collective-permute-start(bf16[1024,512]{1,0:T(8,128)(2,1)S(1)} %get-tuple-element.149), channel_id=1, source_target_pairs={{0,8},{4,12},{8,0},{12,4},{1,9},{5,13},{9,1},{13,5},{2,10},{6,14},... | collective-permute-start | bytes 3145736 | tf_op jit(solution)/shard_map/ppermute | solution.py:798
  410.3 34.6 %collective-permute-start.39 = (bf16[512,1024]{1,0:T(8,128)(2,1)}, bf16[512,1024]{1,0:T(8,128)(2,1)S(1)}, u32[]{:S(2)}, u32[]{:S(2)}) collective-permute-start(bf16[512,1024]{1,0:T(8,128)(2,1)} %get-tuple-element.141.refs_2_.refs_3_.refs_5_), channel_id=1, source_target_pairs={{0,4},{4,0},{8,12},{12,8},{1,5},{5,1},{9,13},{13,9},{2,6},{6,2},{1... | collective-permute-start | bytes 3145736 | tf_op jit(solution)/shard_map/ppermute | solution.py:798
  411.8 2.1 collective-permute-start.38
  412.3 47.1 %collective-permute-start.40 = (bf16[1024,512]{1,0:T(8,128)(2,1)S(1)}, bf16[1024,512]{1,0:T(8,128)(2,1)S(1)}, u32[]{:S(2)}, u32[]{:S(2)}) collective-permute-start(bf16[1024,512]{1,0:T(8,128)(2,1)S(1)} %get-tuple-element.148), channel_id=1, source_target_pairs={{0,8},{4,12},{8,0},{12,4},{1,9},{5,13},{9,1},{13,5},{2,10},{6,14},... | collective-permute-start | bytes 3145736 | tf_op jit(solution)/shard_map/ppermute | solution.py:798
  429.3 30.2 %collective-permute-start.42 = (bf16[1024,512]{1,0:T(8,128)(2,1)S(1)}, bf16[1024,512]{1,0:T(8,128)(2,1)S(1)}, u32[]{:S(2)}, u32[]{:S(2)}) collective-permute-start(bf16[1024,512]{1,0:T(8,128)(2,1)S(1)} %moved.6.refs_13_), channel_id=1, source_target_pairs={{0,3},{1,0},{2,1},{3,2},{4,7},{5,4},{6,5},{7,6},{8,11},{9,8},{10,9... | collective-permute-start | bytes 3145736 | tf_op jit(solution)/shard_map/ppermute | solution.py:803
  442.9 41.6 %collective-permute-start.44 = (bf16[1024,512]{1,0:T(8,128)(2,1)S(1)}, bf16[1024,512]{1,0:T(8,128)(2,1)S(1)}, u32[]{:S(2)}, u32[]{:S(2)}) collective-permute-start(bf16[1024,512]{1,0:T(8,128)(2,1)S(1)} %get-tuple-element.154), channel_id=1, source_target_pairs={{0,8},{4,12},{8,0},{12,4},{1,9},{5,13},{9,1},{13,5},{2,10},{6,14},... | collective-permute-start | bytes 3145736 | tf_op jit(solution)/shard_map/ppermute | solution.py:798
  444.4 63.5 %collective-permute-start.47 = (bf16[1024,512]{1,0:T(8,128)(2,1)S(1)}, bf16[1024,512]{1,0:T(8,128)(2,1)S(1)}, u32[]{:S(2)}, u32[]{:S(2)}) collective-permute-start(bf16[1024,512]{1,0:T(8,128)(2,1)S(1)} %get-tuple-element.156), channel_id=1, source_target_pairs={{0,8},{4,12},{8,0},{12,4},{1,9},{5,13},{9,1},{13,5},{2,10},{6,14},... | collective-permute-start | bytes 3145736 | tf_op jit(solution)/shard_map/ppermute | solution.py:798
  460.8 23.7 %collective-permute-start.45 = (bf16[1024,512]{1,0:T(8,128)(2,1)S(1)}, bf16[1024,512]{1,0:T(8,128)(2,1)S(1)}, u32[]{:S(2)}, u32[]{:S(2)}) collective-permute-start(bf16[1024,512]{1,0:T(8,128)(2,1)S(1)} %moved.7.refs_13_), channel_id=1, source_target_pairs={{0,3},{1,0},{2,1},{3,2},{4,7},{5,4},{6,5},{7,6},{8,11},{9,8},{10,9... | collective-permute-start | bytes 3145736 | tf_op jit(solution)/shard_map/ppermute | solution.py:803
  485.0 23.7 %collective-permute-start.46 = (bf16[1024,512]{1,0:T(8,128)(2,1)S(1)}, bf16[1024,512]{1,0:T(8,128)(2,1)S(1)}, u32[]{:S(2)}, u32[]{:S(2)}) collective-permute-start(bf16[1024,512]{1,0:T(8,128)(2,1)S(1)} %moved.8.refs_13_), channel_id=1, source_target_pairs={{0,3},{1,0},{2,1},{3,2},{4,7},{5,4},{6,5},{7,6},{8,11},{9,8},{10,9... | collective-permute-start | bytes 3145736 | tf_op jit(solution)/shard_map/ppermute | solution.py:803
  488.7 18.2 %collective-permute-start.43 = (bf16[512,512]{1,0:T(8,128)(2,1)S(1)}, bf16[512,512]{1,0:T(8,128)(2,1)S(1)}, u32[]{:S(2)}, u32[]{:S(2)}) collective-permute-start(bf16[512,512]{1,0:T(8,128)(2,1)S(1)} %get-tuple-element.153), channel_id=1, source_target_pairs={{0,8},{4,12},{8,0},{12,4},{1,9},{5,13},{9,1},{13,5},{2,10},{6,14},... | collective-permute-start | bytes 1572872 | tf_op jit(solution)/shard_map/ppermute | solution.py:798
  515.0 14.9 %collective-permute-start.48 = (bf16[512,1024]{1,0:T(8,128)(2,1)S(1)}, bf16[512,1024]{1,0:T(8,128)(2,1)S(1)}, u32[]{:S(2)}, u32[]{:S(2)}) collective-permute-start(bf16[512,1024]{1,0:T(8,128)(2,1)S(1)} %get-tuple-element.158), channel_id=1, source_target_pairs={{0,4},{4,0},{8,12},{12,8},{1,5},{5,1},{9,13},{13,9},{2,6},{6,2},{1... | collective-permute-start | bytes 3145736 | tf_op jit(solution)/shard_map/ppermute | solution.py:798
  515.1 14.8 %collective-permute-start.49 = (bf16[512,512]{1,0:T(8,128)(2,1)S(1)}, bf16[512,512]{1,0:T(8,128)(2,1)S(1)}, u32[]{:S(2)}, u32[]{:S(2)}) collective-permute-start(bf16[512,512]{1,0:T(8,128)(2,1)S(1)} %get-tuple-element.160), channel_id=1, source_target_pairs={{0,8},{4,12},{8,0},{12,4},{1,9},{5,13},{9,1},{13,5},{2,10},{6,14},... | collective-permute-start | bytes 1572872 | tf_op jit(solution)/shard_map/ppermute | solution.py:798
  516.7 16.1 %collective-permute-start.50 = (bf16[512,512]{1,0:T(8,128)(2,1)S(1)}, bf16[512,512]{1,0:T(8,128)(2,1)S(1)}, u32[]{:S(2)}, u32[]{:S(2)}) collective-permute-start(bf16[512,512]{1,0:T(8,128)(2,1)S(1)} %copy-done.116), channel_id=1, source_target_pairs={{0,3},{1,0},{2,1},{3,2},{4,7},{5,4},{6,5},{7,6},{8,11},{9,8},{10,9... | collective-permute-start | bytes 1572872 | tf_op jit(solution)/shard_map/ppermute | solution.py:803
  520.8 19.8 %collective-permute-start.51 = (bf16[512,512]{1,0:T(8,128)(2,1)S(1)}, bf16[512,512]{1,0:T(8,128)(2,1)S(1)}, u32[]{:S(2)}, u32[]{:S(2)}) collective-permute-start(bf16[512,512]{1,0:T(8,128)(2,1)S(1)} %get-tuple-element.162), channel_id=1, source_target_pairs={{0,8},{4,12},{8,0},{12,4},{1,9},{5,13},{9,1},{13,5},{2,10},{6,14},... | collective-permute-start | bytes 1572872 | tf_op jit(solution)/shard_map/ppermute | solution.py:798
  543.8 36.6 %all-to-all-start.2 = ((bf16[4,128,1024]{2,1,0:T(8,128)(2,1)}), bf16[4,128,1024]{2,1,0:T(8,128)(2,1)S(1)}, u32[]{:S(2)}, u32[]{:S(2)}) async-start(bf16[4,128,1024]{2,1,0:T(8,128)(2,1)} %bitcast.16), calls=%async_computation.2 | async-start | bytes 2097152 | tf_op jit(solution)/shard_map/all_to_all | solution.py:1305
  552.1 6.5 %collective-permute-start.53 = (f32[256,512]{1,0:T(8,128)S(1)}, f32[256,512]{1,0:T(8,128)S(1)}, u32[]{:S(2)}, u32[]{:S(2)}) collective-permute-start(f32[256,512]{1,0:T(8,128)S(1)} %get-tuple-element.167), channel_id=1, source_target_pairs={{0,4},{4,0},{8,12},{12,8},{1,5},{5,1},{9,13},{13,9},{2,6},{6,2},{1... | collective-permute-start | bytes 1572872 | tf_op jit(solution)/shard_map/ppermute | solution.py:798
  552.2 6.4 %collective-permute-start.54 = (f32[512,256]{1,0:T(8,128)S(1)}, f32[512,256]{1,0:T(8,128)S(1)}, u32[]{:S(2)}, u32[]{:S(2)}) collective-permute-start(f32[512,256]{1,0:T(8,128)S(1)} %get-tuple-element.168), channel_id=1, source_target_pairs={{0,4},{4,0},{8,12},{12,8},{1,5},{5,1},{9,13},{13,9},{2,6},{6,2},{1... | collective-permute-start | bytes 1572872 | tf_op jit(solution)/shard_map/ppermute | solution.py:798
  552.9 13.8 %collective-permute-start.55 = (bf16[512,512]{1,0:T(8,128)(2,1)S(1)}, bf16[512,512]{1,0:T(8,128)(2,1)S(1)}, u32[]{:S(2)}, u32[]{:S(2)}) collective-permute-start(bf16[512,512]{1,0:T(8,128)(2,1)S(1)} %copy-done.124), channel_id=1, source_target_pairs={{0,8},{4,12},{8,0},{12,4},{1,9},{5,13},{9,1},{13,5},{2,10},{6,14},... | collective-permute-start | bytes 1572872 | tf_op jit(solution)/shard_map/ppermute | solution.py:798
  554.7 24.9 %collective-permute-start.52 = (bf16[512,512]{1,0:T(8,128)(2,1)S(1)}, bf16[512,512]{1,0:T(8,128)(2,1)S(1)}, u32[]{:S(2)}, u32[]{:S(2)}) collective-permute-start(bf16[512,512]{1,0:T(8,128)(2,1)S(1)} %moved.10), channel_id=1, source_target_pairs={{0,3},{1,0},{2,1},{3,2},{4,7},{5,4},{6,5},{7,6},{8,11},{9,8},{10,9... | collective-permute-start | bytes 1572872 | tf_op jit(solution)/shard_map/ppermute | solution.py:803
  585.6 26.0 %collective-permute-start.56 = (bf16[2,128,1024]{2,1,0:T(8,128)(2,1)}, bf16[2,128,1024]{2,1,0:T(8,128)(2,1)S(1)}, u32[]{:S(2)}, u32[]{:S(2)}) collective-permute-start(bf16[2,128,1024]{2,1,0:T(8,128)(2,1)} %get-tuple-element.172), channel_id=1, source_target_pairs={{0,4},{4,0},{8,12},{12,8},{1,5},{5,1},{9,13},{13,9},{2,6},{6,2},{1... | collective-permute-start | bytes 1572872 | tf_op jit(solution)/shard_map/ppermute | solution.py:798
  585.6 27.0 %collective-permute-start.57 = (bf16[512,512]{1,0:T(8,128)(2,1)}, bf16[512,512]{1,0:T(8,128)(2,1)S(1)}, u32[]{:S(2)}, u32[]{:S(2)}) collective-permute-start(bf16[512,512]{1,0:T(8,128)(2,1)} %copy-done.39), channel_id=1, source_target_pairs={{0,3},{1,0},{2,1},{3,2},{4,7},{5,4},{6,5},{7,6},{8,11},{9,8},{10,9... | collective-permute-start | bytes 1572872 | tf_op jit(solution)/shard_map/ppermute | solution.py:803
  612.8 2.0 collective-permute-start.58
  (130 other events, 1082.5 us)

commit v19 on v14

--- a/solution.py
+++ b/solution.py
@@ -17,7 +17,7 @@
 MODEL_HALF = 512
 QKV = slice(0, 384)
 OUT = slice(384, 512)
-CHUNK = 32
+CHUNK = 16
 KERNEL_VMEM = 20 << 20
 ROWS_VMEM = 3 << 20
 

time: 627 us -> 645 us (1.029)
  Pallas kernels: 221 us -> 245 us
    pallas_call x31, Pallas kernels: 86.2 us -> 110 us  [on_chip(): pl.pallas_call(without(kernel, len(operands), len(waits)), in_specs=[spac...]
    ppermute x42, waiting for transfers between devices: 102 us -> 93.6 us  [flip_pairs(): return lax.ppermute(block, 'dp', [(i, i ^ distance) for i in range(size)])]
  transfers between devices with their start and end apart: 62 -> 62, of which waited for: 36 -> 37; matrix products, arithmetic and copies ran while one was open for 4% -> 4% of each run, Pallas kernels for 14% -> 15%
where the time goes in v19:
time: 645 us; the launch traced here: 635 us
  Pallas kernels  245 us (38%)
  waiting for transfers between devices  220 us (34%)
  starting transfers between devices  81.1 us (13%)
  local copies, waits for them, and re-layouts  58.2 us (9%)
  other arithmetic  19.3 us (3%)
  blocking collectives  9.02 us (1%)
    pallas_call x31, Pallas kernels, on_chip(): pl.pallas_call(without(kernel, len(operands), len(waits)), in_specs=[spac...  110 us
    ppermute x42, waiting for transfers between devices, flip_pairs(): return lax.ppermute(block, 'dp', [(i, i ^ distance) for i in range(size)])  93.6 us
    pallas_call x6, Pallas kernels, by_pairs(): pl.pallas_call(without(functools.partial(kernel, len(pieces[0])), taken,...  85.8 us
    ppermute x15, waiting for transfers between devices, passed_on(): lax.ppermute(block, 'tensor', [(i, (i + step) % size) for i in range(size)])  83.6 us
    unnamed x290, local copies, waits for them, and re-layouts  47.4 us
    ppermute x2, waiting for transfers between devices, shifted(): return lax.ppermute(block, axis, route)  41.5 us
    ppermute x15, starting transfers between devices, passed_on(): lax.ppermute(block, 'tensor', [(i, (i + step) % size) for i in range(size)])  36.1 us
    pallas_call x4, Pallas kernels, weight_grads(): pl.pallas_call(without(functools.partial(kernel, base), 1 + len(arrays),...  26 us
  transfers between devices with their start and end apart: 62, of which 37 were waited for; matrix products, arithmetic and copies ran while one was open for 4% of the time, Pallas kernels for 15%

profile of v19, /device:TPU:0, one launch (start us, length us, event | category | flops | bytes accessed | tf_op | source)
XLA Modules:
  0.0 635.2 jit_solution(11123751708132489570)
XLA Ops:
  11.4 6.2 all-to-all-start
  28.9 21.5 %collective-permute-done.1.refs_0_ = bf16[512,512]{1,0:T(8,128)(2,1)} collective-permute-done((bf16[512,512]{1,0:T(8,128)(2,1)}, bf16[512,512]{1,0:T(8,128)(2,1)}, u32[]{:S(2)}, u32[]{:S(2)}) %collective-permute-start.1) | collective-permute-done | bytes 524320 | tf_op jit(solution)/shard_map/ppermute | solution.py:803
  59.5 8.8 %collective-permute-done.4.refs_2_.refs_7_.refs_3_.refs_5_.refs_4_ = bf16[512,512]{1,0:T(8,128)(2,1)S(1)} collective-permute-done((bf16[512,512]{1,0:T(8,128)(2,1)}, bf16[512,512]{1,0:T(8,128)(2,1)S(1)}, u32[]{:S(2)}, u32[]{:S(2)}) %collective-permute-start.4) | collective-permute-done | bytes 524320 | tf_op jit(solution)/shard_map/ppermute | solution.py:803
  69.5 2.9 collective-permute-done.5.refs_4_.refs_5_.refs_7_
  74.9 3.2 norm_in.2.refs_3_.refs_1_
  78.2 2.5 collective-permute-start.11
  86.2 8.8 %collective-permute-done.11.refs_13_.refs_3_.refs_2_ = bf16[512,512]{1,0:T(8,128)(2,1)S(1)} collective-permute-done((bf16[512,512]{1,0:T(8,128)(2,1)}, bf16[512,512]{1,0:T(8,128)(2,1)S(1)}, u32[]{:S(2)}, u32[]{:S(2)}) %collective-permute-start.11) | collective-permute-done | bytes 524320 | tf_op jit(solution)/shard_map/ppermute | solution.py:803
  97.7 8.5 %collective-permute-done.12.refs_14_.refs_2_.refs_4_ = bf16[512,512]{1,0:T(8,128)(2,1)S(1)} collective-permute-done((bf16[512,512]{1,0:T(8,128)(2,1)}, bf16[512,512]{1,0:T(8,128)(2,1)S(1)}, u32[]{:S(2)}, u32[]{:S(2)}) %collective-permute-start.12) | collective-permute-done | bytes 524320 | tf_op jit(solution)/shard_map/ppermute | solution.py:803
  109.0 16.9 %attend.2 = (bf16[4,1024,128]{2,1,0:T(8,128)(2,1)S(1)}, bf16[4,1024,128]{2,1,0:T(8,128)(2,1)S(1)}, bf16[4,1024,128]{2,1,0:T(8,128)(2,1)S(1)}, f32[4,2,1024]{2,1,0:T(2,128)S(1)}, bf16[1024,512]{1,0:T(8,128)(2,1)S(1)}) custom-call(s32[1]{0:T(128)} %bitcast.refs_0_, f32[1024,128]{1,0:T(8,128)S(1)} %get-tuple-element.228.refs_1_, ...), custom_call_target="tpu_custom_call" | custom-call | flops 11811160064 | bytes 11567104 | tf_op jit(solution)/shard_map/attend/pallas_call | solution.py:708
  130.2 3.0 attn_out.2
  133.3 2.6 collective-permute-start.18
  138.4 11.7 %collective-permute-done.18.refs_4_.refs_5_ = bf16[512,512]{1,0:T(8,128)(2,1)S(1)} collective-permute-done((bf16[512,512]{1,0:T(8,128)(2,1)}, bf16[512,512]{1,0:T(8,128)(2,1)S(1)}, u32[]{:S(2)}, u32[]{:S(2)}) %collective-permute-start.18) | collective-permute-done | bytes 524320 | tf_op jit(solution)/shard_map/ppermute | solution.py:803
  150.1 10.8 %collective-permute-done.19.refs_5_.refs_4_.refs_6_ = bf16[512,512]{1,0:T(8,128)(2,1)S(1)} collective-permute-done((bf16[512,512]{1,0:T(8,128)(2,1)}, bf16[512,512]{1,0:T(8,128)(2,1)S(1)}, u32[]{:S(2)}, u32[]{:S(2)}) %collective-permute-start.19) | collective-permute-done | bytes 524320 | tf_op jit(solution)/shard_map/ppermute | solution.py:803
  162.4 6.4 after_attn.2
  172.3 12.9 %collective-permute-done.23.refs_9_.refs_8_ = bf16[512,512]{1,0:T(8,128)(2,1)S(1)} collective-permute-done((bf16[512,512]{1,0:T(8,128)(2,1)}, bf16[512,512]{1,0:T(8,128)(2,1)S(1)}, u32[]{:S(2)}, u32[]{:S(2)}) %collective-permute-start.23) | collective-permute-done | bytes 524320 | tf_op jit(solution)/shard_map/ppermute | solution.py:798
  187.5 7.7 %mlp_up.2 = (bf16[1024,2048]{1,0:T(8,128)(2,1)S(1)}, bf16[1024,2048]{1,0:T(8,128)(2,1)S(1)}) custom-call(bf16[512,1024]{1,0:T(8,128)(2,1)S(1)} %get-tuple-element.103.refs_0_.refs_1_, bf16[512,1024]{1,0:T(8,128)(2,1)S(1)} %collective-permute-done.22.refs_1_.refs_2_, bf16[512,512]{1,0:T(8,128)(2,1)S(1)} %copy-done.114, bf16[512,512]{1,0:T(8,128)(2,1)S(1)} %copy-done.129, ...), custom_call_target="tpu_custom_call" | custom-call | flops 4294967296 | bytes 14680064 | tf_op jit(solution)/shard_map/mlp_up/pallas_call | solution.py:690
  197.3 4.5 mlp_down.2
  201.9 2.6 collective-permute-done.25.refs_3_
  204.6 3.3 after_mlp.2
  207.9 3.5 collective-permute-start.26
  211.5 22.2 %collective-permute-done.26.refs_1_ = bf16[512,1024]{1,0:T(8,128)(2,1)S(1)} collective-permute-done((bf16[512,1024]{1,0:T(8,128)(2,1)S(1)}, bf16[512,1024]{1,0:T(8,128)(2,1)S(1)}, u32[]{:S(2)}, u32[]{:S(2)}) %collective-permute-start.26) | collective-permute-done | bytes 1048608 | tf_op jit(solution)/shard_map/ppermute | solution.py:28
  233.7 3.2 norm_in.3.refs_3_.refs_7_
  237.0 2.6 collective-permute-done.27.refs_4_.refs_8_
  239.7 16.9 %attend.3 = (bf16[4,1024,128]{2,1,0:T(8,128)(2,1)S(1)}, bf16[4,1024,128]{2,1,0:T(8,128)(2,1)S(1)}, bf16[4,1024,128]{2,1,0:T(8,128)(2,1)S(1)}, f32[4,2,1024]{2,1,0:T(2,128)S(1)}, bf16[1024,512]{1,0:T(8,128)(2,1)S(1)}) custom-call(s32[1]{0:T(128)} %bitcast.refs_0_, f32[1024,128]{1,0:T(8,128)S(1)} %get-tuple-element.228.refs_1_, ...), custom_call_target="tpu_custom_call" | custom-call | flops 11811160064 | bytes 11567104 | tf_op jit(solution)/shard_map/attend/pallas_call | solution.py:708
  256.6 3.3 attn_out.3
  262.7 6.3 after_attn.3
  271.8 7.7 %mlp_up.3 = (bf16[1024,2048]{1,0:T(8,128)(2,1)S(1)}, bf16[1024,2048]{1,0:T(8,128)(2,1)S(1)}) custom-call(bf16[512,1024]{1,0:T(8,128)(2,1)S(1)} %get-tuple-element.112.refs_0_.refs_7_, bf16[512,1024]{1,0:T(8,128)(2,1)S(1)} %collective-permute-done.29.refs_1_.refs_8_, bf16[512,512]{1,0:T(8,128)(2,1)S(1)} %copy-done.114, bf16[512,512]{1,0:T(8,128)(2,1)S(1)} %copy-done.129, ...), custom_call_target="tpu_custom_call" | custom-call | flops 4294967296 | bytes 14680064 | tf_op jit(solution)/shard_map/mlp_up/pallas_call | solution.py:690
  281.6 4.5 mlp_down.3
  288.8 3.3 after_mlp.3
  292.1 3.8 into_mlp_back.2
  298.7 7.2 %mlp_up_back.2.refs_0_.refs_9_ = bf16[1024,2048]{1,0:T(8,128)(2,1)S(1)} custom-call(bf16[512,1024]{1,0:T(8,128)(2,1)S(1)} %get-tuple-element.118.refs_0_.refs_11_, bf16[512,1024]{1,0:T(8,128)(2,1)S(1)} %collective-permute-done.31.refs_1_.refs_12_, bf16[1024,2048]{1,0:T(8,128)(2,1)} %copy-done.39, bf16[512,512]{1,0:T(8,128)(2,1)} %copy-done.61, ...), custom_call_target="tpu_custom_call" | custom-call | tf_op jit(solution)/shard_map/mlp_up_back/pallas_call | solution.py:729
  305.9 4.5 mlp_back.2
  313.1 6.7 %into_attn_back.2 = (f32[512,1024]{1,0:T(8,128)S(1)}, bf16[512,1024]{1,0:T(8,128)(2,1)S(1)}, f32[1,1024]{1,0:T(1,128)S(1)}, f32[1,1024]{1,0:T(1,128)S(1)}) custom-call(f32[4,1024]{1,0:T(4,128)S(1)} %maximum_select_fusion.3.refs_0_, bf16[512,1024]{1,0:T(8,128)(2,1)S(1)} %bitcast.36, f32[512,1024]{1,0:T(8,128)S(1)} %get-tuple-element.120.refs_2_, ...), custom_call_target="tpu_custom_call" | custom-call | bytes 11558912 | tf_op jit(solution)/shard_map/into_attn_back/pallas_call | solution.py:690
  322.6 13.1 %attend_back.4.refs_0_.refs_9_ = bf16[1024,768]{1,0:T(8,128)(2,1)S(1)} custom-call(s32[1]{0:T(128)} %bitcast.refs_0_, f32[1024,128]{1,0:T(8,128)S(1)} %get-tuple-element.228.refs_1_, f32[1024,128]{1,0:T(8,128)S(1)} %get-tuple-element.229.refs_2_, bf16[512,1024]{1,0:T(8,128)(2,1)S(1)} %get-tuple-element.123.refs_3_.refs_11_, ...), custom_call_target="tpu_custom_call" | custom-call | flops 11274289152 | bytes 6815744 | tf_op jit(solution)/shard_map/attend_back/pallas_call | solution.py:708
  335.7 12.8 %attend_back.5.refs_1_.refs_9_ = bf16[1024,768]{1,0:T(8,128)(2,1)S(1)} custom-call(s32[1]{0:T(128)} %bitcast.refs_0_, f32[1024,128]{1,0:T(8,128)S(1)} %get-tuple-element.228.refs_1_, f32[1024,128]{1,0:T(8,128)S(1)} %get-tuple-element.229.refs_2_, bf16[512,1024]{1,0:T(8,128)(2,1)S(1)} %get-tuple-element.123.refs_3_.refs_11_, ...), custom_call_target="tpu_custom_call" | custom-call | flops 11274289152 | bytes 6815744 | tf_op jit(solution)/shard_map/attend_back/pallas_call | solution.py:708
  350.2 5.7 attn_back.2
  358.6 3.7 out_of_layer.2
  365.1 5.2 all-to-all-start.1
  370.3 19.2 %collective-permute-done.35.refs_1_ = bf16[512,1024]{1,0:T(8,128)(2,1)S(1)} collective-permute-done((bf16[512,1024]{1,0:T(8,128)(2,1)S(1)}, bf16[512,1024]{1,0:T(8,128)(2,1)S(1)}, u32[]{:S(2)}, u32[]{:S(2)}) %collective-permute-start.35) | collective-permute-done | bytes 1048608 | tf_op jit(solution)/shard_map/ppermute | solution.py:28
  391.5 3.6 into_mlp_back.3
  397.9 7.2 %mlp_up_back.3.refs_3_.refs_0_ = bf16[1024,2048]{1,0:T(8,128)(2,1)S(1)} custom-call(bf16[512,1024]{1,0:T(8,128)(2,1)S(1)} %get-tuple-element.135.refs_0_.refs_5_, bf16[512,1024]{1,0:T(8,128)(2,1)S(1)} %collective-permute-done.36.refs_1_.refs_6_, bf16[1024,2048]{1,0:T(8,128)(2,1)} %copy-done.54, bf16[512,512]{1,0:T(8,128)(2,1)} %copy-done.61, ...), custom_call_target="tpu_custom_call" | custom-call | tf_op jit(solution)/shard_map/mlp_up_back/pallas_call | solution.py:729
  407.1 7.2 %mlp_grads.2 = (f32[1024,512]{1,0:T(8,128)S(1)}, bf16[1024,512]{1,0:T(8,128)(2,1)S(1)}, f32[1024,512]{1,0:T(8,128)S(1)}, bf16[1024,512]{1,0:T(8,128)(2,1)S(1)}) custom-call(s32[1]{0:T(128)} %bitcast.12.refs_0_, bf16[512,1024]{1,0:T(8,128)(2,1)} %copy-done.41, bf16[512,1024]{1,0:T(8,128)(2,1)} %copy-done.42, bf16[1024,2048]{1,0:T(8,128)(2,1)} %copy-done.3, ...), custom_call_target="tpu_custom_call" | custom-call | tf_op jit(solution)/shard_map/mlp_grads/pallas_call | solution.py:897
  415.8 4.5 mlp_back.3
  423.0 7.6 %into_attn_back.3 = (f32[512,1024]{1,0:T(8,128)S(1)}, bf16[512,1024]{1,0:T(8,128)(2,1)}, f32[1,1024]{1,0:T(1,128)S(1)}, f32[1,1024]{1,0:T(1,128)S(1)}) custom-call(f32[4,1024]{1,0:T(4,128)S(1)} %maximum_select_fusion.3.refs_0_, bf16[512,1024]{1,0:T(8,128)(2,1)S(1)} %copy-done.56, f32[512,1024]{1,0:T(8,128)S(1)} %get-tuple-element.138.refs_2_, ...), custom_call_target="tpu_custom_call" | custom-call | bytes 11558912 | tf_op jit(solution)/shard_map/into_attn_back/pallas_call | solution.py:690
  435.3 11.2 %collective-permute-done.41.refs_1_ = bf16[1024,512]{1,0:T(8,128)(2,1)S(1)} collective-permute-done((bf16[1024,512]{1,0:T(8,128)(2,1)S(1)}, bf16[1024,512]{1,0:T(8,128)(2,1)S(1)}, u32[]{:S(2)}, u32[]{:S(2)}) %collective-permute-start.41) | collective-permute-done | bytes 1048608 | tf_op jit(solution)/shard_map/ppermute | solution.py:798
  447.1 3.7 collective-permute-start.42
  450.8 7.0 %mlp_grads.3 = (f32[1024,512]{1,0:T(8,128)S(1)}, bf16[1024,512]{1,0:T(8,128)(2,1)S(1)}, f32[1024,512]{1,0:T(8,128)S(1)}, bf16[1024,512]{1,0:T(8,128)(2,1)S(1)}) custom-call(s32[1]{0:T(128)} %bitcast.12.refs_0_, bf16[512,1024]{1,0:T(8,128)(2,1)} %copy-done.41, bf16[512,1024]{1,0:T(8,128)(2,1)} %copy-done.42, bf16[1024,2048]{1,0:T(8,128)(2,1)} %copy-done.3, ...), custom_call_target="tpu_custom_call" | custom-call | tf_op jit(solution)/shard_map/mlp_grads/pallas_call | solution.py:897
  462.7 12.9 %attend_back.6.refs_3_.refs_1_ = bf16[1024,768]{1,0:T(8,128)(2,1)S(1)} custom-call(s32[1]{0:T(128)} %bitcast.refs_0_, f32[1024,128]{1,0:T(8,128)S(1)} %copy-done.110, f32[1024,128]{1,0:T(8,128)S(1)} %copy-done.112, bf16[512,1024]{1,0:T(8,128)(2,1)} %get-tuple-element.141.refs_2_.refs_3_.refs_5_, ...), custom_call_target="tpu_custom_call" | custom-call | flops 11274289152 | bytes 6815744 | tf_op jit(solution)/shard_map/attend_back/pallas_call | solution.py:708
  479.7 5.9 attn_grads.2
  487.6 13.2 %attend_back.7.refs_3_.refs_0_ = bf16[1024,768]{1,0:T(8,128)(2,1)S(1)} custom-call(s32[1]{0:T(128)} %bitcast.refs_0_, f32[1024,128]{1,0:T(8,128)S(1)} %copy-done.110, f32[1024,128]{1,0:T(8,128)S(1)} %copy-done.112, bf16[512,1024]{1,0:T(8,128)(2,1)} %get-tuple-element.141.refs_2_.refs_3_.refs_5_, bf16[512,1024]{1,0:T(8,128)(2,1)S(1)} %copy-done.50, ...), custom_call_target="tpu_custom_call" | custom-call | flops 11274289152 | bytes 6815744 | tf_op jit(solution)/shard_map/attend_back/pallas_call | solution.py:708
  502.7 3.4 collective-permute-start.46
  506.6 5.9 attn_grads.3
  513.4 11.2 %collective-permute-done.43.refs_1_ = bf16[512,512]{1,0:T(8,128)(2,1)S(1)} collective-permute-done((bf16[512,512]{1,0:T(8,128)(2,1)S(1)}, bf16[512,512]{1,0:T(8,128)(2,1)S(1)}, u32[]{:S(2)}, u32[]{:S(2)}) %collective-permute-start.43) | collective-permute-done | bytes 524320 | tf_op jit(solution)/shard_map/ppermute | solution.py:798
  527.6 5.1 attn_back.3
  533.4 3.8 collective-permute-start.50
  538.8 8.8 %collective-permute-done.49.refs_5_.refs_1_ = bf16[512,512]{1,0:T(8,128)(2,1)S(1)} collective-permute-done((bf16[512,512]{1,0:T(8,128)(2,1)S(1)}, bf16[512,512]{1,0:T(8,128)(2,1)S(1)}, u32[]{:S(2)}, u32[]{:S(2)}) %collective-permute-start.49) | collective-permute-done | bytes 524320 | tf_op jit(solution)/shard_map/ppermute | solution.py:798
  548.4 3.7 out_of_layer.3
  552.1 6.3 collective-permute-done.51.refs_4_.refs_1_
  560.8 5.2 all-to-all-start.2
  570.5 3.9 collective-permute-start.52
  575.9 7.4 %collective-permute-done.55.refs_4_.refs_2_ = bf16[512,512]{1,0:T(8,128)(2,1)S(1)} collective-permute-done((bf16[512,512]{1,0:T(8,128)(2,1)S(1)}, bf16[512,512]{1,0:T(8,128)(2,1)S(1)}, u32[]{:S(2)}, u32[]{:S(2)}) %collective-permute-start.55) | collective-permute-done | bytes 524320 | tf_op jit(solution)/shard_map/ppermute | solution.py:798
  583.3 13.0 %collective-permute-done.52.refs_2_ = bf16[512,512]{1,0:T(8,128)(2,1)S(1)} collective-permute-done((bf16[512,512]{1,0:T(8,128)(2,1)S(1)}, bf16[512,512]{1,0:T(8,128)(2,1)S(1)}, u32[]{:S(2)}, u32[]{:S(2)}) %collective-permute-start.52) | collective-permute-done | bytes 524320 | tf_op jit(solution)/shard_map/ppermute | solution.py:803
  602.3 7.2 %collective-permute-start.57 = (bf16[512,512]{1,0:T(8,128)(2,1)}, bf16[512,512]{1,0:T(8,128)(2,1)S(1)}, u32[]{:S(2)}, u32[]{:S(2)}) collective-permute-start(bf16[512,512]{1,0:T(8,128)(2,1)} %copy-done.38), channel_id=1, source_target_pairs={{0,3},{1,0},{2,1},{3,2},{4,7},{5,4},{6,5},{7,6},{8,11},{9,8},{10,9... | collective-permute-start | bytes 1572872 | tf_op jit(solution)/shard_map/ppermute | solution.py:803
  616.4 9.0 %all_to_all.20 = f32[16,1,256]{2,1,0:T(1,128)S(1)} all-to-all(f32[16,1,256]{2,1,0:T(1,128)S(1)} %reshape.144), channel_id=1, replica_groups=mesh['section'=2,'dp'=4,'tensor'=4] {'dp','tensor'}, dimensions={0} | all-to-all | bytes 32768 | tf_op jit(solution)/shard_map/all_to_all | solution.py:1335
  (457 shorter events, 154.3 us)
Async XLA Ops:
  7.2 2.1 collective-permute-start
  11.4 63.5 %all-to-all-start = ((bf16[4,128,1024]{2,1,0:T(8,128)(2,1)}), bf16[4,128,1024]{2,1,0:T(8,128)(2,1)S(1)}, u32[]{:S(2)}, u32[]{:S(2)}) async-start(bf16[4,128,1024]{2,1,0:T(8,128)(2,1)} %pad_maximum_fusion), calls=%async_computation | async-start | bytes 2097152 | tf_op jit(solution)/shard_map/all_to_all | solution.py:1071
  24.8 25.7 %collective-permute-start.1 = (bf16[512,512]{1,0:T(8,128)(2,1)}, bf16[512,512]{1,0:T(8,128)(2,1)}, u32[]{:S(2)}, u32[]{:S(2)}) collective-permute-start(bf16[512,512]{1,0:T(8,128)(2,1)} %pad_maximum_fusion.3.refs_5_.refs_1_.refs_2_), channel_id=1, source_target_pairs={{0,1},{1,2},{2,3},{3,0},{4,5},{5,6},{6,7},{7,4},{8,9},{9,10},{10,1... | collective-permute-start | bytes 1572872 | tf_op jit(solution)/shard_map/ppermute | solution.py:803
  26.8 23.7 %collective-permute-start.2 = (bf16[512,512]{1,0:T(8,128)(2,1)}, bf16[512,512]{1,0:T(8,128)(2,1)}, u32[]{:S(2)}, u32[]{:S(2)}) collective-permute-start(bf16[512,512]{1,0:T(8,128)(2,1)} %pad_maximum_fusion.3.refs_5_.refs_1_.refs_2_), channel_id=1, source_target_pairs={{0,8},{4,12},{8,0},{12,4},{1,9},{5,13},{9,1},{13,5},{2,10},{6,14},... | collective-permute-start | bytes 1572872 | tf_op jit(solution)/shard_map/ppermute | solution.py:798
  28.3 23.0 %collective-permute-start.3 = (bf16[512,512]{1,0:T(8,128)(2,1)S(1)}, bf16[512,512]{1,0:T(8,128)(2,1)S(1)}, u32[]{:S(2)}, u32[]{:S(2)}) collective-permute-start(bf16[512,512]{1,0:T(8,128)(2,1)S(1)} %dynamic-slice_bitcast_fusion.1.refs_0_), channel_id=1, source_target_pairs={{0,8},{4,12},{8,0},{12,4},{1,9},{5,13},{9,1},{13,5},{2,10},{6,14},... | collective-permute-start | bytes 1572872 | tf_op jit(solution)/shard_map/ppermute | solution.py:798
  54.0 14.3 %collective-permute-start.4 = (bf16[512,512]{1,0:T(8,128)(2,1)}, bf16[512,512]{1,0:T(8,128)(2,1)S(1)}, u32[]{:S(2)}, u32[]{:S(2)}) collective-permute-start(bf16[512,512]{1,0:T(8,128)(2,1)} %gate.3.refs_6_.refs_2_.refs_3_), channel_id=1, source_target_pairs={{0,1},{1,2},{2,3},{3,0},{4,5},{5,6},{6,7},{7,4},{8,9},{9,10},{10,1... | collective-permute-start | bytes 1572872 | tf_op jit(solution)/shard_map/ppermute | solution.py:803
  57.4 14.9 %collective-permute-start.5 = (bf16[512,512]{1,0:T(8,128)(2,1)S(1)}, bf16[512,512]{1,0:T(8,128)(2,1)S(1)}, u32[]{:S(2)}, u32[]{:S(2)}) collective-permute-start(bf16[512,512]{1,0:T(8,128)(2,1)S(1)} %dynamic-slice_bitcast_fusion.refs_1_), channel_id=1, source_target_pairs={{0,8},{4,12},{8,0},{12,4},{1,9},{5,13},{9,1},{13,5},{2,10},{6,14},... | collective-permute-start | bytes 1572872 | tf_op jit(solution)/shard_map/ppermute | solution.py:798
  59.0 22.4 %collective-permute-start.8 = (bf16[512,512]{1,0:T(8,128)(2,1)}, bf16[512,512]{1,0:T(8,128)(2,1)}, u32[]{:S(2)}, u32[]{:S(2)}) collective-permute-start(bf16[512,512]{1,0:T(8,128)(2,1)} %gate.3.refs_6_.refs_2_.refs_3_), channel_id=1, source_target_pairs={{0,8},{4,12},{8,0},{12,4},{1,9},{5,13},{9,1},{13,5},{2,10},{6,14},... | collective-permute-start | bytes 1572872 | tf_op jit(solution)/shard_map/ppermute | solution.py:798
  68.3 14.6 %collective-permute-start.7 = (bf16[512,512]{1,0:T(8,128)(2,1)S(1)}, bf16[512,512]{1,0:T(8,128)(2,1)}, u32[]{:S(2)}, u32[]{:S(2)}) collective-permute-start(bf16[512,512]{1,0:T(8,128)(2,1)S(1)} %collective-permute-done.4.refs_2_.refs_7_.refs_3_.refs_5_.refs_4_), channel_id=1, source_target_pairs={{0,1},{1,2},{2,3},{3,0},{4,5},{5,6},{6,7},{7,4},{8,9},{9,10},{10,1... | collective-permute-start | bytes 1572872 | tf_op jit(solution)/shard_map/ppermute | solution.py:803
  78.1 30.9 %collective-permute-start.6 = (bf16[512,1024]{1,0:T(8,128)(2,1)S(1)}, bf16[512,1024]{1,0:T(8,128)(2,1)}, u32[]{:S(2)}, u32[]{:S(2)}) collective-permute-start(bf16[512,1024]{1,0:T(8,128)(2,1)S(1)} %norm_in.2.refs_3_.refs_1_), channel_id=1, source_target_pairs={{0,4},{4,0},{8,12},{12,8},{1,5},{5,1},{9,13},{13,9},{2,6},{6,2},{1... | collective-permute-start | bytes 3145736 | tf_op jit(solution)/shard_map/ppermute | solution.py:798
  78.2 16.8 %collective-permute-start.11 = (bf16[512,512]{1,0:T(8,128)(2,1)}, bf16[512,512]{1,0:T(8,128)(2,1)S(1)}, u32[]{:S(2)}, u32[]{:S(2)}) collective-permute-start(bf16[512,512]{1,0:T(8,128)(2,1)} %copy-done.113), channel_id=1, source_target_pairs={{0,1},{1,2},{2,3},{3,0},{4,5},{5,6},{6,7},{7,4},{8,9},{9,10},{10,1... | collective-permute-start | bytes 1572872 | tf_op jit(solution)/shard_map/ppermute | solution.py:803
  80.8 25.5 %collective-permute-start.12 = (bf16[512,512]{1,0:T(8,128)(2,1)}, bf16[512,512]{1,0:T(8,128)(2,1)S(1)}, u32[]{:S(2)}, u32[]{:S(2)}) collective-permute-start(bf16[512,512]{1,0:T(8,128)(2,1)} %copy-done.61), channel_id=1, source_target_pairs={{0,1},{1,2},{2,3},{3,0},{4,5},{5,6},{6,7},{7,4},{8,9},{9,10},{10,1... | collective-permute-start | bytes 1572872 | tf_op jit(solution)/shard_map/ppermute | solution.py:803
  81.4 14.8 %collective-permute-start.9 = (bf16[512,512]{1,0:T(8,128)(2,1)S(1)}, bf16[512,512]{1,0:T(8,128)(2,1)S(1)}, u32[]{:S(2)}, u32[]{:S(2)}) collective-permute-start(bf16[512,512]{1,0:T(8,128)(2,1)S(1)} %copy-done.27), channel_id=1, source_target_pairs={{0,8},{4,12},{8,0},{12,4},{1,9},{5,13},{9,1},{13,5},{2,10},{6,14},... | collective-permute-start | bytes 1572872 | tf_op jit(solution)/shard_map/ppermute | solution.py:798
  82.9 24.5 %collective-permute-start.10 = (bf16[512,512]{1,0:T(8,128)(2,1)}, bf16[512,512]{1,0:T(8,128)(2,1)S(1)}, u32[]{:S(2)}, u32[]{:S(2)}) collective-permute-start(bf16[512,512]{1,0:T(8,128)(2,1)} %collective-permute-done.7.refs_8_.refs_4_.refs_6_.refs_5_), channel_id=1, source_target_pairs={{0,8},{4,12},{8,0},{12,4},{1,9},{5,13},{9,1},{13,5},{2,10},{6,14},... | collective-permute-start | bytes 1572872 | tf_op jit(solution)/shard_map/ppermute | solution.py:798
  95.0 33.8 %collective-permute-start.13 = (bf16[512,512]{1,0:T(8,128)(2,1)S(1)}, bf16[512,512]{1,0:T(8,128)(2,1)S(1)}, u32[]{:S(2)}, u32[]{:S(2)}) collective-permute-start(bf16[512,512]{1,0:T(8,128)(2,1)S(1)} %collective-permute-done.11.refs_13_.refs_3_.refs_2_), channel_id=1, source_target_pairs={{0,1},{1,2},{2,3},{3,0},{4,5},{5,6},{6,7},{7,4},{8,9},{9,10},{10,1... | collective-permute-start | bytes 1572872 | tf_op jit(solution)/shard_map/ppermute | solution.py:803
  96.2 252.3 %copy-start.57 = (bf16[512,512]{1,0:T(8,128)(2,1)}, bf16[512,512]{1,0:T(8,128)(2,1)S(1)}, u32[]{:S(2)}) copy-start(bf16[512,512]{1,0:T(8,128)(2,1)S(1)} %collective-permute-done.9.refs_11_.refs_7_.refs_8_) | copy-start | bytes 1572868
  96.2 32.6 %collective-permute-start.15 = (bf16[512,512]{1,0:T(8,128)(2,1)S(1)}, bf16[512,512]{1,0:T(8,128)(2,1)S(1)}, u32[]{:S(2)}, u32[]{:S(2)}) collective-permute-start(bf16[512,512]{1,0:T(8,128)(2,1)S(1)} %collective-permute-done.11.refs_13_.refs_3_.refs_2_), channel_id=1, source_target_pairs={{0,8},{4,12},{8,0},{12,4},{1,9},{5,13},{9,1},{13,5},{2,10},{6,14},... | collective-permute-start | bytes 1572872 | tf_op jit(solution)/shard_map/ppermute | solution.py:798
  106.3 22.6 %collective-permute-start.14 = (bf16[512,512]{1,0:T(8,128)(2,1)S(1)}, bf16[512,512]{1,0:T(8,128)(2,1)S(1)}, u32[]{:S(2)}, u32[]{:S(2)}) collective-permute-start(bf16[512,512]{1,0:T(8,128)(2,1)S(1)} %collective-permute-done.12.refs_14_.refs_2_.refs_4_), channel_id=1, source_target_pairs={{0,1},{1,2},{2,3},{3,0},{4,5},{5,6},{6,7},{7,4},{8,9},{9,10},{10,1... | collective-permute-start | bytes 1572872 | tf_op jit(solution)/shard_map/ppermute | solution.py:803
  107.5 241.1 %copy-start.59 = (bf16[512,512]{1,0:T(8,128)(2,1)}, bf16[512,512]{1,0:T(8,128)(2,1)S(1)}, u32[]{:S(2)}) copy-start(bf16[512,512]{1,0:T(8,128)(2,1)S(1)} %collective-permute-done.10.refs_12_.refs_8_.refs_9_) | copy-start | bytes 1572868
  107.5 21.4 %collective-permute-start.16 = (bf16[512,512]{1,0:T(8,128)(2,1)S(1)}, bf16[512,512]{1,0:T(8,128)(2,1)S(1)}, u32[]{:S(2)}, u32[]{:S(2)}) collective-permute-start(bf16[512,512]{1,0:T(8,128)(2,1)S(1)} %collective-permute-done.12.refs_14_.refs_2_.refs_4_), channel_id=1, source_target_pairs={{0,8},{4,12},{8,0},{12,4},{1,9},{5,13},{9,1},{13,5},{2,10},{6,14},... | collective-permute-start | bytes 1572872 | tf_op jit(solution)/shard_map/ppermute | solution.py:798
  133.2 28.4 %collective-permute-start.17 = (bf16[512,1024]{1,0:T(8,128)(2,1)S(1)}, bf16[512,1024]{1,0:T(8,128)(2,1)S(1)}, u32[]{:S(2)}, u32[]{:S(2)}) collective-permute-start(bf16[512,1024]{1,0:T(8,128)(2,1)S(1)} %get-tuple-element.101), channel_id=1, source_target_pairs={{0,4},{4,0},{8,12},{12,8},{1,5},{5,1},{9,13},{13,9},{2,6},{6,2},{1... | collective-permute-start | bytes 3145736 | tf_op jit(solution)/shard_map/ppermute | solution.py:798
  133.3 16.8 %collective-permute-start.18 = (bf16[512,512]{1,0:T(8,128)(2,1)}, bf16[512,512]{1,0:T(8,128)(2,1)S(1)}, u32[]{:S(2)}, u32[]{:S(2)}) collective-permute-start(bf16[512,512]{1,0:T(8,128)(2,1)} %copy-done.103), channel_id=1, source_target_pairs={{0,1},{1,2},{2,3},{3,0},{4,5},{5,6},{6,7},{7,4},{8,9},{9,10},{10,1... | collective-permute-start | bytes 1572872 | tf_op jit(solution)/shard_map/ppermute | solution.py:803
  135.9 25.0 %collective-permute-start.19 = (bf16[512,512]{1,0:T(8,128)(2,1)}, bf16[512,512]{1,0:T(8,128)(2,1)S(1)}, u32[]{:S(2)}, u32[]{:S(2)}) collective-permute-start(bf16[512,512]{1,0:T(8,128)(2,1)} %copy-done.30), channel_id=1, source_target_pairs={{0,1},{1,2},{2,3},{3,0},{4,5},{5,6},{6,7},{7,4},{8,9},{9,10},{10,1... | collective-permute-start | bytes 1572872 | tf_op jit(solution)/shard_map/ppermute | solution.py:803
  136.3 24.5 %collective-permute-start.20 = (bf16[512,512]{1,0:T(8,128)(2,1)}, bf16[512,512]{1,0:T(8,128)(2,1)S(1)}, u32[]{:S(2)}, u32[]{:S(2)}) collective-permute-start(bf16[512,512]{1,0:T(8,128)(2,1)} %copy-done.103), channel_id=1, source_target_pairs={{0,8},{4,12},{8,0},{12,4},{1,9},{5,13},{9,1},{13,5},{2,10},{6,14},... | collective-permute-start | bytes 1572872 | tf_op jit(solution)/shard_map/ppermute | solution.py:798
  136.8 24.7 %collective-permute-start.21 = (bf16[512,512]{1,0:T(8,128)(2,1)}, bf16[512,512]{1,0:T(8,128)(2,1)S(1)}, u32[]{:S(2)}, u32[]{:S(2)}) collective-permute-start(bf16[512,512]{1,0:T(8,128)(2,1)} %copy-done.30), channel_id=1, source_target_pairs={{0,8},{4,12},{8,0},{12,4},{1,9},{5,13},{9,1},{13,5},{2,10},{6,14},... | collective-permute-start | bytes 1572872 | tf_op jit(solution)/shard_map/ppermute | solution.py:798
  170.2 15.1 %collective-permute-start.22 = (bf16[512,1024]{1,0:T(8,128)(2,1)S(1)}, bf16[512,1024]{1,0:T(8,128)(2,1)S(1)}, u32[]{:S(2)}, u32[]{:S(2)}) collective-permute-start(bf16[512,1024]{1,0:T(8,128)(2,1)S(1)} %get-tuple-element.103.refs_0_.refs_1_), channel_id=1, source_target_pairs={{0,4},{4,0},{8,12},{12,8},{1,5},{5,1},{9,13},{13,9},{2,6},{6,2},{1... | collective-permute-start | bytes 3145736 | tf_op jit(solution)/shard_map/ppermute | solution.py:798
  170.3 15.0 %collective-permute-start.23 = (bf16[512,512]{1,0:T(8,128)(2,1)}, bf16[512,512]{1,0:T(8,128)(2,1)S(1)}, u32[]{:S(2)}, u32[]{:S(2)}) collective-permute-start(bf16[512,512]{1,0:T(8,128)(2,1)} %copy-done.116), channel_id=1, source_target_pairs={{0,8},{4,12},{8,0},{12,4},{1,9},{5,13},{9,1},{13,5},{2,10},{6,14},... | collective-permute-start | bytes 1572872 | tf_op jit(solution)/shard_map/ppermute | solution.py:798
  170.8 26.4 %collective-permute-start.24 = (bf16[512,512]{1,0:T(8,128)(2,1)}, bf16[512,512]{1,0:T(8,128)(2,1)S(1)}, u32[]{:S(2)}, u32[]{:S(2)}) collective-permute-start(bf16[512,512]{1,0:T(8,128)(2,1)} %copy-done.34), channel_id=1, source_target_pairs={{0,8},{4,12},{8,0},{12,4},{1,9},{5,13},{9,1},{13,5},{2,10},{6,14},... | collective-permute-start | bytes 1572872 | tf_op jit(solution)/shard_map/ppermute | solution.py:798
  201.8 2.7 collective-permute-start.25
  207.9 25.8 %collective-permute-start.26 = (bf16[512,1024]{1,0:T(8,128)(2,1)S(1)}, bf16[512,1024]{1,0:T(8,128)(2,1)S(1)}, u32[]{:S(2)}, u32[]{:S(2)}) collective-permute-start(bf16[512,1024]{1,0:T(8,128)(2,1)S(1)} %get-tuple-element.132), channel_id=1, source_target_pairs={{0,16},{1,17},{2,18},{3,19},{4,20},{5,21},{6,22},{7,23},{8,24},{9,... | collective-permute-start | bytes 3145736 | tf_op jit(solution)/shard_map/ppermute | solution.py:28
  236.9 2.7 collective-permute-start.27
  260.0 2.7 collective-permute-start.28
  269.1 2.7 collective-permute-start.29
  286.1 2.7 collective-permute-start.30
  295.9 2.7 collective-permute-start.31
  310.4 2.7 collective-permute-start.32
  319.9 2.7 collective-permute-start.33
  355.9 2.7 collective-permute-start.34
  362.3 27.2 %collective-permute-start.35 = (bf16[512,1024]{1,0:T(8,128)(2,1)S(1)}, bf16[512,1024]{1,0:T(8,128)(2,1)S(1)}, u32[]{:S(2)}, u32[]{:S(2)}) collective-permute-start(bf16[512,1024]{1,0:T(8,128)(2,1)S(1)} %get-tuple-element.131.refs_2_), channel_id=1, source_target_pairs={{16,0},{17,1},{18,2},{19,3},{20,4},{21,5},{22,6},{23,7},{24,8},{25... | collective-permute-start | bytes 3145736 | tf_op jit(solution)/shard_map/ppermute | solution.py:28
  365.1 31.3 %all-to-all-start.1 = ((bf16[4,128,1024]{2,1,0:T(8,128)(2,1)}), bf16[4,128,1024]{2,1,0:T(8,128)(2,1)}, u32[]{:S(2)}, u32[]{:S(2)}) async-start(bf16[4,128,1024]{2,1,0:T(8,128)(2,1)} %bitcast.41), calls=%async_computation.1 | async-start | bytes 2097152 | tf_op jit(solution)/shard_map/all_to_all | solution.py:1224
  395.1 2.7 collective-permute-start.36
  420.3 2.7 collective-permute-start.37
  420.5 26.0 %collective-permute-start.41 = (bf16[1024,512]{1,0:T(8,128)(2,1)S(1)}, bf16[1024,512]{1,0:T(8,128)(2,1)S(1)}, u32[]{:S(2)}, u32[]{:S(2)}) collective-permute-start(bf16[1024,512]{1,0:T(8,128)(2,1)S(1)} %get-tuple-element.149), channel_id=1, source_target_pairs={{0,8},{4,12},{8,0},{12,4},{1,9},{5,13},{9,1},{13,5},{2,10},{6,14},... | collective-permute-start | bytes 3145736 | tf_op jit(solution)/shard_map/ppermute | solution.py:798
  430.7 31.9 %collective-permute-start.39 = (bf16[512,1024]{1,0:T(8,128)(2,1)}, bf16[512,1024]{1,0:T(8,128)(2,1)S(1)}, u32[]{:S(2)}, u32[]{:S(2)}) collective-permute-start(bf16[512,1024]{1,0:T(8,128)(2,1)} %get-tuple-element.141.refs_2_.refs_3_.refs_5_), channel_id=1, source_target_pairs={{0,4},{4,0},{8,12},{12,8},{1,5},{5,1},{9,13},{13,9},{2,6},{6,2},{1... | collective-permute-start | bytes 3145736 | tf_op jit(solution)/shard_map/ppermute | solution.py:798
  432.2 2.0 collective-permute-start.38
  432.7 44.1 %collective-permute-start.40 = (bf16[1024,512]{1,0:T(8,128)(2,1)S(1)}, bf16[1024,512]{1,0:T(8,128)(2,1)S(1)}, u32[]{:S(2)}, u32[]{:S(2)}) collective-permute-start(bf16[1024,512]{1,0:T(8,128)(2,1)S(1)} %get-tuple-element.148), channel_id=1, source_target_pairs={{0,8},{4,12},{8,0},{12,4},{1,9},{5,13},{9,1},{13,5},{2,10},{6,14},... | collective-permute-start | bytes 3145736 | tf_op jit(solution)/shard_map/ppermute | solution.py:798
  447.1 29.7 %collective-permute-start.42 = (bf16[1024,512]{1,0:T(8,128)(2,1)S(1)}, bf16[1024,512]{1,0:T(8,128)(2,1)S(1)}, u32[]{:S(2)}, u32[]{:S(2)}) collective-permute-start(bf16[1024,512]{1,0:T(8,128)(2,1)S(1)} %moved.6.refs_13_), channel_id=1, source_target_pairs={{0,3},{1,0},{2,1},{3,2},{4,7},{5,4},{6,5},{7,6},{8,11},{9,8},{10,9... | collective-permute-start | bytes 3145736 | tf_op jit(solution)/shard_map/ppermute | solution.py:803
  460.6 41.4 %collective-permute-start.44 = (bf16[1024,512]{1,0:T(8,128)(2,1)S(1)}, bf16[1024,512]{1,0:T(8,128)(2,1)S(1)}, u32[]{:S(2)}, u32[]{:S(2)}) collective-permute-start(bf16[1024,512]{1,0:T(8,128)(2,1)S(1)} %get-tuple-element.154), channel_id=1, source_target_pairs={{0,8},{4,12},{8,0},{12,4},{1,9},{5,13},{9,1},{13,5},{2,10},{6,14},... | collective-permute-start | bytes 3145736 | tf_op jit(solution)/shard_map/ppermute | solution.py:798
  461.1 64.6 %collective-permute-start.47 = (bf16[1024,512]{1,0:T(8,128)(2,1)S(1)}, bf16[1024,512]{1,0:T(8,128)(2,1)S(1)}, u32[]{:S(2)}, u32[]{:S(2)}) collective-permute-start(bf16[1024,512]{1,0:T(8,128)(2,1)S(1)} %get-tuple-element.156), channel_id=1, source_target_pairs={{0,8},{4,12},{8,0},{12,4},{1,9},{5,13},{9,1},{13,5},{2,10},{6,14},... | collective-permute-start | bytes 3145736 | tf_op jit(solution)/shard_map/ppermute | solution.py:798
  478.1 23.8 %collective-permute-start.45 = (bf16[1024,512]{1,0:T(8,128)(2,1)S(1)}, bf16[1024,512]{1,0:T(8,128)(2,1)S(1)}, u32[]{:S(2)}, u32[]{:S(2)}) collective-permute-start(bf16[1024,512]{1,0:T(8,128)(2,1)S(1)} %moved.7.refs_13_), channel_id=1, source_target_pairs={{0,3},{1,0},{2,1},{3,2},{4,7},{5,4},{6,5},{7,6},{8,11},{9,8},{10,9... | collective-permute-start | bytes 3145736 | tf_op jit(solution)/shard_map/ppermute | solution.py:803
  502.7 23.5 %collective-permute-start.46 = (bf16[1024,512]{1,0:T(8,128)(2,1)S(1)}, bf16[1024,512]{1,0:T(8,128)(2,1)S(1)}, u32[]{:S(2)}, u32[]{:S(2)}) collective-permute-start(bf16[1024,512]{1,0:T(8,128)(2,1)S(1)} %moved.8.refs_13_), channel_id=1, source_target_pairs={{0,3},{1,0},{2,1},{3,2},{4,7},{5,4},{6,5},{7,6},{8,11},{9,8},{10,9... | collective-permute-start | bytes 3145736 | tf_op jit(solution)/shard_map/ppermute | solution.py:803
  506.0 18.5 %collective-permute-start.43 = (bf16[512,512]{1,0:T(8,128)(2,1)S(1)}, bf16[512,512]{1,0:T(8,128)(2,1)S(1)}, u32[]{:S(2)}, u32[]{:S(2)}) collective-permute-start(bf16[512,512]{1,0:T(8,128)(2,1)S(1)} %get-tuple-element.153), channel_id=1, source_target_pairs={{0,8},{4,12},{8,0},{12,4},{1,9},{5,13},{9,1},{13,5},{2,10},{6,14},... | collective-permute-start | bytes 1572872 | tf_op jit(solution)/shard_map/ppermute | solution.py:798
  532.7 14.9 %collective-permute-start.48 = (bf16[512,1024]{1,0:T(8,128)(2,1)S(1)}, bf16[512,1024]{1,0:T(8,128)(2,1)S(1)}, u32[]{:S(2)}, u32[]{:S(2)}) collective-permute-start(bf16[512,1024]{1,0:T(8,128)(2,1)S(1)} %get-tuple-element.158), channel_id=1, source_target_pairs={{0,4},{4,0},{8,12},{12,8},{1,5},{5,1},{9,13},{13,9},{2,6},{6,2},{1... | collective-permute-start | bytes 3145736 | tf_op jit(solution)/shard_map/ppermute | solution.py:798
  532.8 14.8 %collective-permute-start.49 = (bf16[512,512]{1,0:T(8,128)(2,1)S(1)}, bf16[512,512]{1,0:T(8,128)(2,1)S(1)}, u32[]{:S(2)}, u32[]{:S(2)}) collective-permute-start(bf16[512,512]{1,0:T(8,128)(2,1)S(1)} %get-tuple-element.160), channel_id=1, source_target_pairs={{0,8},{4,12},{8,0},{12,4},{1,9},{5,13},{9,1},{13,5},{2,10},{6,14},... | collective-permute-start | bytes 1572872 | tf_op jit(solution)/shard_map/ppermute | solution.py:798
  533.4 18.7 %collective-permute-start.50 = (bf16[512,512]{1,0:T(8,128)(2,1)S(1)}, bf16[512,512]{1,0:T(8,128)(2,1)S(1)}, u32[]{:S(2)}, u32[]{:S(2)}) collective-permute-start(bf16[512,512]{1,0:T(8,128)(2,1)S(1)} %copy-done.127), channel_id=1, source_target_pairs={{0,3},{1,0},{2,1},{3,2},{4,7},{5,4},{6,5},{7,6},{8,11},{9,8},{10,9... | collective-permute-start | bytes 1572872 | tf_op jit(solution)/shard_map/ppermute | solution.py:803
  537.2 21.2 %collective-permute-start.51 = (bf16[512,512]{1,0:T(8,128)(2,1)S(1)}, bf16[512,512]{1,0:T(8,128)(2,1)S(1)}, u32[]{:S(2)}, u32[]{:S(2)}) collective-permute-start(bf16[512,512]{1,0:T(8,128)(2,1)S(1)} %get-tuple-element.162), channel_id=1, source_target_pairs={{0,8},{4,12},{8,0},{12,4},{1,9},{5,13},{9,1},{13,5},{2,10},{6,14},... | collective-permute-start | bytes 1572872 | tf_op jit(solution)/shard_map/ppermute | solution.py:798
  560.8 36.3 %all-to-all-start.2 = ((bf16[4,128,1024]{2,1,0:T(8,128)(2,1)}), bf16[4,128,1024]{2,1,0:T(8,128)(2,1)S(1)}, u32[]{:S(2)}, u32[]{:S(2)}) async-start(bf16[4,128,1024]{2,1,0:T(8,128)(2,1)} %bitcast.16), calls=%async_computation.2 | async-start | bytes 2097152 | tf_op jit(solution)/shard_map/all_to_all | solution.py:1305
  568.8 5.6 collective-permute-start.53
  568.9 5.5 collective-permute-start.54
  569.5 13.8 %collective-permute-start.55 = (bf16[512,512]{1,0:T(8,128)(2,1)S(1)}, bf16[512,512]{1,0:T(8,128)(2,1)S(1)}, u32[]{:S(2)}, u32[]{:S(2)}) collective-permute-start(bf16[512,512]{1,0:T(8,128)(2,1)S(1)} %copy-done.134), channel_id=1, source_target_pairs={{0,8},{4,12},{8,0},{12,4},{1,9},{5,13},{9,1},{13,5},{2,10},{6,14},... | collective-permute-start | bytes 1572872 | tf_op jit(solution)/shard_map/ppermute | solution.py:798
  570.5 25.8 %collective-permute-start.52 = (bf16[512,512]{1,0:T(8,128)(2,1)S(1)}, bf16[512,512]{1,0:T(8,128)(2,1)S(1)}, u32[]{:S(2)}, u32[]{:S(2)}) collective-permute-start(bf16[512,512]{1,0:T(8,128)(2,1)S(1)} %moved.10), channel_id=1, source_target_pairs={{0,3},{1,0},{2,1},{3,2},{4,7},{5,4},{6,5},{7,6},{8,11},{9,8},{10,9... | collective-permute-start | bytes 1572872 | tf_op jit(solution)/shard_map/ppermute | solution.py:803
  602.3 25.0 %collective-permute-start.56 = (bf16[2,128,1024]{2,1,0:T(8,128)(2,1)}, bf16[2,128,1024]{2,1,0:T(8,128)(2,1)S(1)}, u32[]{:S(2)}, u32[]{:S(2)}) collective-permute-start(bf16[2,128,1024]{2,1,0:T(8,128)(2,1)} %get-tuple-element.172), channel_id=1, source_target_pairs={{0,4},{4,0},{8,12},{12,8},{1,5},{5,1},{9,13},{13,9},{2,6},{6,2},{1... | collective-permute-start | bytes 1572872 | tf_op jit(solution)/shard_map/ppermute | solution.py:798
  602.3 26.0 %collective-permute-start.57 = (bf16[512,512]{1,0:T(8,128)(2,1)}, bf16[512,512]{1,0:T(8,128)(2,1)S(1)}, u32[]{:S(2)}, u32[]{:S(2)}) collective-permute-start(bf16[512,512]{1,0:T(8,128)(2,1)} %copy-done.38), channel_id=1, source_target_pairs={{0,3},{1,0},{2,1},{3,2},{4,7},{5,4},{6,5},{7,6},{8,11},{9,8},{10,9... | collective-permute-start | bytes 1572872 | tf_op jit(solution)/shard_map/ppermute | solution.py:803
  628.5 2.0 collective-permute-start.58
  (141 other events, 1521.5 us)
